TPU v7x, 32 devices: a whole 2x2x4 slice. The times are simulated.
32 devices in a mesh: dp: 16 (over z, x, core), tensor: 2 (over y).
Axes of the slice: x: 2, y: 2, z: 4, core: 2. Of those that a mesh axis runs over, the one named last changes fastest.
Arguments:
- inputs: bfloat16 [5120, 2048], P('dp'), may hold values from -6 to 6
- attn_gain: bfloat16 [2048], P('dp'), may hold values from 0.5 to 1.5
- w_query: bfloat16 [2048, 2048], P('dp', 'tensor'), may hold values from -0.125 to 0.125
- w_key: bfloat16 [2048, 2048], P('dp', 'tensor'), may hold values from -0.125 to 0.125
- w_value: bfloat16 [2048, 2048], P('dp', 'tensor'), may hold values from -0.125 to 0.125
- query_gain: bfloat16 [2048], P('dp'), may hold values from 0.796875 to 2
- key_gain: bfloat16 [2048], P('dp'), may hold values from 0.59765625 to 1.3984375
- w_out: bfloat16 [2048, 2048], P('tensor', 'dp'), may hold values from -0.75 to 0.75
- moe_gain: bfloat16 [2048], P('dp'), may hold values from 0.5 to 1.5
- w_gate: bfloat16 [16, 2048, 1024], P('dp', None, 'tensor'), may hold values from -0.125 to 0.125
- w_up: bfloat16 [16, 2048, 1024], P('dp', None, 'tensor'), may hold values from -0.125 to 0.125
- w_down: bfloat16 [16, 1024, 2048], P('dp', 'tensor'), may hold values from -0.1875 to 0.1875
- experts: int32 [5120, 8], P('dp'), may hold values from 0 to 15, all different within a row; in each aligned block of 320 rows (0 to 319, 320 to 639, ...) at most 288 rows name the same one
- gates: float32 [5120, 8], P('dp'), may hold values from 0.25 to 1
- segments: int32 [16, 192], P('dp'), may hold values from 0 to 1, never falling along the last dimension, each value on 1 to 128 neighbouring positions
- gaps: int32 [16, 2], P('dp'), may hold values from 0 to 512
- cotangent: float32 [5120, 2048], P('dp'), may hold values from -6 to 6
Outputs:
- output: float32 [5120, 2048], P('dp')
- input_grad: float32 [5120, 2048], P('dp')
- attn_gain_grad: float32 [2048], P('dp')
- w_query_grad: float32 [2048, 2048], P('dp', 'tensor')
- w_key_grad: float32 [2048, 2048], P('dp', 'tensor')
- w_value_grad: float32 [2048, 2048], P('dp', 'tensor')
- query_gain_grad: float32 [2048], P('dp')
- key_gain_grad: float32 [2048], P('dp')
- w_out_grad: float32 [2048, 2048], P('tensor', 'dp')
- moe_gain_grad: float32 [2048], P('dp')
- w_gate_grad: float32 [16, 2048, 1024], P('dp', None, 'tensor')
- w_up_grad: float32 [16, 2048, 1024], P('dp', None, 'tensor')
- w_down_grad: float32 [16, 1024, 2048], P('dp', 'tensor')
Inputs may be any that keep to these rules, and one draw needn't show every extreme that they name: Each row names 8 different experts. In the rows of one dp index at most 288 name the same expert, and some dp index reaches 288. `segments`: in each row the numbers never fall; each continuation has 1 to 128 tokens.
All inputs are finite; a program needn't handle non-finite values.
Results may differ from a plain program's by a relative error of at most 0.018.
Values may be sent and summed in bfloat16 or wider, within the bound.
No kernel may reach another device: no remote copies, remote signals or barrier semaphores. Data moves between devices by JAX's collectives and lax.ppermute only.
A program may use at most 384 MiB of HBM per device.

v0:
```python
import jax
import jax.numpy as jnp
from jax import lax
from jax.sharding import PartitionSpec as P

HEADS = 16
HEAD = 128
GROUP = 8
PR_DEV = 128


EPSILON = 1e-05


def from_partner(block, axis, distance):
    count = lax.axis_size(axis)
    route = []
    for low in range(count):
        high = low | 1 << distance
        if high != low and high < count:
            route += [(low, high), (high, low)]
    return lax.ppermute(block, axis, route)


def carried_in(value, axis, join, neutral):
    count, mine = (lax.axis_size(axis), lax.axis_index(axis))
    pieces = lax.all_gather(value, axis)
    running = jnp.full_like(value, 0) + jnp.asarray(neutral, value.dtype)

    def step(position, running):
        longer = join(running, pieces[position])
        return jnp.where(position < mine, longer, running)

    return lax.fori_loop(0, count - 1, step, running)


def rms_norm(values, gain):
    return values * lax.rsqrt(jnp.mean(values * values, axis=-1, keepdims=True) + EPSILON) * gain


def rope_tables(positions, head_size):
    half_size = head_size // 2
    inverse = 10000.0 ** (-(jnp.arange(half_size, dtype=jnp.float32) * 2.0) / head_size)
    angles = positions.astype(jnp.float32)[:, None] * inverse[None, :]
    cosine = jnp.concatenate([jnp.cos(angles), jnp.cos(angles)], axis=-1)
    sine = jnp.concatenate([jnp.sin(angles), jnp.sin(angles)], axis=-1)
    return (cosine, sine)


def rotate(values, cosine, sine):
    half_size = values.shape[-1] // 2
    turned = jnp.concatenate([-values[..., half_size:], values[..., :half_size]], axis=-1)
    return values * cosine[:, None, :] + turned * sine[:, None, :]


def cont_positions(segment_row, gap_row, prompt_length):
    order = jnp.arange(segment_row.shape[0], dtype=jnp.int32)
    same = segment_row[:, None] == segment_row[None, :]
    earlier = order[None, :] < order[:, None]
    offset = jnp.sum((same & earlier).astype(jnp.int32), axis=1)
    labels = jnp.arange(gap_row.shape[0], dtype=jnp.int32)
    shifted = jnp.sum(
        jnp.where(segment_row[:, None] == labels[None, :], gap_row[None, :], 0), axis=1
    )
    return prompt_length + shifted + offset


def rows_product(left, right):
    return lax.dot_general(
        left, right, (((0,), (0,)), ((), ())), preferred_element_type=jnp.float32
    )


def transposed_product(left, right):
    return lax.dot_general(
        left, right, (((1,), (1,)), ((), ())), preferred_element_type=jnp.float32
    )


def collect_prompt(own_block):
    dp_index = lax.axis_index("dp")
    collected = own_block
    for bit_index in range(GROUP.bit_length() - 1):
        partner = from_partner(collected, "dp", bit_index)
        upper_side = dp_index >> bit_index & 1 == 1
        collected = jnp.where(
            upper_side,
            jnp.concatenate([partner, collected], axis=1),
            jnp.concatenate([collected, partner], axis=1),
        )
    return collected


def return_prompt(grads):
    dp_index = lax.axis_index("dp")
    for bit_index in reversed(range(GROUP.bit_length() - 1)):
        half_rows = grads.shape[1] // 2
        first_part = grads[:, :half_rows]
        second_part = grads[:, half_rows:]
        upper_side = dp_index >> bit_index & 1 == 1
        kept_part = jnp.where(upper_side, second_part, first_part)
        sent_part = jnp.where(upper_side, first_part, second_part)
        grads = kept_part + from_partner(sent_part.astype(jnp.bfloat16), "dp", bit_index).astype(
            sent_part.dtype
        )
    return grads


def to_experts(rows):
    arrived = lax.all_to_all(rows, "dp", split_axis=0, concat_axis=0, tiled=True)
    return arrived


def from_experts(rows):
    return lax.all_to_all(rows, "dp", split_axis=0, concat_axis=0, tiled=True)


def masked_scores(queries, keyset, allowed):
    scores = jnp.einsum(
        "qhd,khd->hqk", queries, keyset, preferred_element_type=jnp.float32
    ) * HEAD ** (-0.5)
    return jnp.where(allowed[None], scores, -1e30)


def body(
    inputs,
    attn_gain,
    w_query,
    w_key,
    w_value,
    query_gain,
    key_gain,
    w_out,
    moe_gain,
    w_gate,
    w_up,
    w_down,
    experts,
    gates,
    segments,
    gaps,
    cotangent,
):
    dp_count = lax.axis_size("dp")
    dp_index = lax.axis_index("dp")
    token_count = inputs.shape[0]
    model_width = inputs.shape[1]
    top_count = experts.shape[1]
    expert_count = w_gate.shape[0] * dp_count
    slot_count = max(2, token_count * top_count * 9 // (5 * expert_count))
    capacity = token_count * top_count * dp_count * 9 // (8 * expert_count)
    prompt_length = PR_DEV * GROUP
    column_total = HEADS * HEAD
    tokens_f = inputs.astype(jnp.float32)
    full_q, full_k, full_v, full_o, gain_attn, gain_moe, gain_qfull, gain_kfull = (
        lax.all_gather(w_query, "dp", axis=0, tiled=True),
        lax.all_gather(w_key, "dp", axis=0, tiled=True),
        lax.all_gather(w_value, "dp", axis=0, tiled=True),
        lax.all_gather(w_out, "dp", axis=1, tiled=True),
        lax.all_gather(attn_gain, "dp", axis=0, tiled=True),
        lax.all_gather(moe_gain, "dp", axis=0, tiled=True),
        lax.all_gather(query_gain, "dp", axis=0, tiled=True),
        lax.all_gather(key_gain, "dp", axis=0, tiled=True),
    )
    gain_one = gain_attn.astype(jnp.float32)
    gain_two = gain_moe.astype(jnp.float32)
    local_width = full_q.shape[1]
    local_heads = local_width // HEAD
    column_begin = lax.axis_index("tensor") * local_width
    gain_query_local = lax.dynamic_slice_in_dim(gain_qfull, column_begin, local_width).astype(
        jnp.float32
    )
    gain_key_local = lax.dynamic_slice_in_dim(gain_kfull, column_begin, local_width).astype(
        jnp.float32
    )
    prompt_pos = dp_index % GROUP * PR_DEV + jnp.arange(PR_DEV, dtype=jnp.int32)
    later_pos = cont_positions(segments[0], gaps[0], prompt_length)
    positions = jnp.concatenate([prompt_pos, later_pos], axis=0)
    cosine, sine = rope_tables(positions, HEAD)
    normed_b = rms_norm(tokens_f, gain_one).astype(jnp.bfloat16)
    query_flat = jnp.dot(normed_b, full_q, preferred_element_type=jnp.float32)
    key_flat = jnp.dot(normed_b, full_k, preferred_element_type=jnp.float32)
    value_pre = jnp.dot(normed_b, full_v, preferred_element_type=jnp.float32).reshape(
        token_count, local_heads, HEAD
    )
    query_sq, key_sq = lax.psum(
        (jnp.sum(query_flat * query_flat, axis=1), jnp.sum(key_flat * key_flat, axis=1)), "tensor"
    )
    query_scale = lax.rsqrt(query_sq / column_total + EPSILON)[:, None]
    key_scale = lax.rsqrt(key_sq / column_total + EPSILON)[:, None]
    query_normed = (query_flat * query_scale * gain_query_local).reshape(
        token_count, local_heads, HEAD
    )
    key_normed = (key_flat * key_scale * gain_key_local).reshape(token_count, local_heads, HEAD)
    queries_b = rotate(query_normed, cosine, sine).astype(jnp.bfloat16)
    keys_b = rotate(key_normed, cosine, sine).astype(jnp.bfloat16)
    values_b = value_pre.astype(jnp.bfloat16)
    own_prompt = jnp.stack([keys_b[:PR_DEV], values_b[:PR_DEV]], axis=0)
    group_prompt = collect_prompt(own_prompt)
    keyset = jnp.concatenate([group_prompt[0], keys_b[PR_DEV:]], axis=0)
    valueset = jnp.concatenate([group_prompt[1], values_b[PR_DEV:]], axis=0)
    prompt_query = jnp.arange(token_count, dtype=jnp.int32) < PR_DEV
    prompt_keypos = jnp.arange(prompt_length, dtype=jnp.int32)
    allowed_prompt = (~prompt_query)[:, None] | (prompt_keypos[None, :] <= positions[:, None])
    query_segment = jnp.concatenate([jnp.full((PR_DEV,), -1, jnp.int32), segments[0]], axis=0)
    allowed_cont = (query_segment[:, None] == segments[0][None, :]) & (
        later_pos[None, :] <= positions[:, None]
    )
    allowed = jnp.concatenate([allowed_prompt, allowed_cont], axis=1)
    scores = masked_scores(queries_b, keyset, allowed)
    peak = jnp.max(scores, axis=-1, keepdims=True)
    expo = jnp.exp(scores - peak)
    total = jnp.sum(expo, axis=-1, keepdims=True)
    log_total = peak + jnp.log(total)
    probs_b = (expo / total).astype(jnp.bfloat16)
    context = jnp.einsum("hqk,khd->qhd", probs_b, valueset, preferred_element_type=jnp.float32)
    context_b = context.reshape(token_count, local_heads * HEAD).astype(jnp.bfloat16)
    attn_part = jnp.dot(context_b, full_o, preferred_element_type=jnp.float32)
    attn = lax.psum(attn_part, "tensor")
    hidden_state = tokens_f + attn
    normed_two_b = rms_norm(hidden_state, gain_two).astype(jnp.bfloat16)
    expert_ids = jnp.arange(expert_count, dtype=jnp.int32)
    chosen = experts[:, :, None] == expert_ids[None, None, :]
    selected = jnp.any(chosen, axis=1).astype(jnp.int32)
    counts = jnp.sum(selected, axis=0)
    before = jnp.cumsum(selected, axis=0) - selected
    prefix = carried_in(
        counts, "dp", lambda earlier, later: earlier + later, jnp.zeros_like(counts)
    )
    local_rank = jnp.sum(jnp.where(chosen, before[:, None, :], 0), axis=-1)
    global_start = jnp.sum(jnp.where(chosen, prefix[None, None, :], 0), axis=-1)
    kept = global_start + local_rank < capacity
    flat_slot = jnp.where(kept, experts * slot_count + local_rank, expert_count * slot_count)
    pair_token = jnp.repeat(jnp.arange(token_count, dtype=jnp.int32), top_count)
    owner = (
        jnp.full((expert_count * slot_count,), token_count, jnp.int32)
        .at[flat_slot.reshape(-1)]
        .set(pair_token, mode="drop")
    )
    slot_gate = (
        jnp.zeros((expert_count * slot_count,), jnp.float32)
        .at[flat_slot.reshape(-1)]
        .set(gates.reshape(-1), mode="drop")
    )
    pick_slot = jnp.where(kept, flat_slot, 0)
    pair_weight = jnp.where(kept, gates, 0.0)
    kept_f = kept.astype(jnp.float32)
    padded_rows = jnp.concatenate([normed_two_b, jnp.zeros((1, model_width), jnp.bfloat16)], axis=0)
    send_rows = padded_rows[owner].reshape(expert_count, slot_count, model_width)
    expert_in = to_experts(send_rows).reshape(-1, model_width)
    gate_mat = w_gate[0]
    up_mat = w_up[0]
    down_mat = w_down[0]
    gate_pre = jnp.dot(expert_in, gate_mat, preferred_element_type=jnp.float32)
    up_pre = jnp.dot(expert_in, up_mat, preferred_element_type=jnp.float32)
    sigmoid_gate = jax.nn.sigmoid(gate_pre)
    activated = gate_pre * sigmoid_gate
    hidden_b = (activated * up_pre).astype(jnp.bfloat16)
    expert_part = jnp.dot(hidden_b, down_mat, preferred_element_type=jnp.float32).astype(
        jnp.bfloat16
    )
    returned = from_experts(expert_part.reshape(dp_count, -1, model_width)).reshape(-1, model_width)
    picked = returned[pick_slot]
    mixed_part = jnp.sum(picked.astype(jnp.float32) * pair_weight[:, :, None], axis=1)
    mixed = lax.psum(mixed_part.astype(jnp.bfloat16), "tensor").astype(jnp.float32)
    output = hidden_state + mixed
    padded_grad = jnp.concatenate([cotangent, jnp.zeros((1, model_width), jnp.float32)], axis=0)
    send_grads = (
        (slot_gate[:, None] * padded_grad[owner])
        .astype(jnp.bfloat16)
        .reshape(expert_count, slot_count, model_width)
    )
    expert_grad = to_experts(send_grads).reshape(-1, model_width)
    down_grad = rows_product(hidden_b, expert_grad)
    hidden_grad = transposed_product(expert_grad, down_mat)
    act_slope = sigmoid_gate * (1.0 + gate_pre * (1.0 - sigmoid_gate))
    gate_grad_b = (hidden_grad * up_pre * act_slope).astype(jnp.bfloat16)
    up_grad_b = (hidden_grad * activated).astype(jnp.bfloat16)
    gate_w_grad = rows_product(expert_in, gate_grad_b)
    up_w_grad = rows_product(expert_in, up_grad_b)
    row_grad_b = (
        transposed_product(gate_grad_b, gate_mat) + transposed_product(up_grad_b, up_mat)
    ).astype(jnp.bfloat16)
    row_back = from_experts(row_grad_b.reshape(dp_count, -1, model_width)).reshape(-1, model_width)
    normed_two_part = jnp.sum(row_back[pick_slot].astype(jnp.float32) * kept_f[:, :, None], axis=1)
    normed_two_grad = lax.psum(normed_two_part, "tensor")
    unused_two, norm_two_back = jax.vjp(rms_norm, hidden_state, gain_two)
    state_part, gain_two_grad = norm_two_back(normed_two_grad)
    state_grad = cotangent + state_part
    attn_grad_b = state_grad.astype(jnp.bfloat16)
    out_w_grad = rows_product(context_b, attn_grad_b)
    context_grad_b = (
        transposed_product(attn_grad_b, full_o)
        .astype(jnp.bfloat16)
        .reshape(token_count, local_heads, HEAD)
    )
    again = masked_scores(queries_b, keyset, allowed)
    probs = jnp.exp(again - log_total)
    prob_grad = jnp.einsum(
        "qhd,khd->hqk", context_grad_b, valueset, preferred_element_type=jnp.float32
    )
    value_grad = jnp.einsum(
        "hqk,qhd->khd", probs_b, context_grad_b, preferred_element_type=jnp.float32
    )
    row_dot = jnp.sum(probs * prob_grad, axis=-1, keepdims=True)
    score_grad_b = (probs * (prob_grad - row_dot)).astype(jnp.bfloat16)
    query_grad = jnp.einsum(
        "hqk,khd->qhd", score_grad_b, keyset, preferred_element_type=jnp.float32
    ) * HEAD ** (-0.5)
    key_grad = jnp.einsum(
        "hqk,qhd->khd", score_grad_b, queries_b, preferred_element_type=jnp.float32
    ) * HEAD ** (-0.5)
    prompt_grads = return_prompt(
        jnp.stack([key_grad[:prompt_length], value_grad[:prompt_length]], axis=0)
    )
    key_local = jnp.concatenate([prompt_grads[0], key_grad[prompt_length:]], axis=0)
    value_local = jnp.concatenate([prompt_grads[1], value_grad[prompt_length:]], axis=0)
    unused_q, unrotate_q = jax.vjp(lambda values: rotate(values, cosine, sine), query_normed)
    unused_k, unrotate_k = jax.vjp(lambda values: rotate(values, cosine, sine), key_normed)
    query_normed_grad = unrotate_q(query_grad)[0].reshape(token_count, -1)
    key_normed_grad = unrotate_k(key_local)[0].reshape(token_count, -1)
    query_inner, key_inner = lax.psum(
        (
            jnp.sum(query_flat * gain_query_local * query_normed_grad, axis=1),
            jnp.sum(key_flat * gain_key_local * key_normed_grad, axis=1),
        ),
        "tensor",
    )
    query_cube = query_scale * query_scale * query_scale
    key_cube = key_scale * key_scale * key_scale
    query_pre_grad = (
        query_scale * gain_query_local * query_normed_grad
        - query_flat * query_cube * (query_inner / column_total)[:, None]
    ).astype(jnp.bfloat16)
    key_pre_grad = (
        key_scale * gain_key_local * key_normed_grad
        - key_flat * key_cube * (key_inner / column_total)[:, None]
    ).astype(jnp.bfloat16)
    query_gain_part = jnp.sum(query_normed_grad * query_flat * query_scale, axis=0)
    key_gain_part = jnp.sum(key_normed_grad * key_flat * key_scale, axis=0)
    query_gain_wide = lax.dynamic_update_slice_in_dim(
        jnp.zeros((column_total,), jnp.float32), query_gain_part, column_begin, 0
    )
    key_gain_wide = lax.dynamic_update_slice_in_dim(
        jnp.zeros((column_total,), jnp.float32), key_gain_part, column_begin, 0
    )
    value_pre_grad = value_local.reshape(token_count, -1).astype(jnp.bfloat16)
    query_w_grad = rows_product(normed_b, query_pre_grad)
    key_w_grad = rows_product(normed_b, key_pre_grad)
    value_w_grad = rows_product(normed_b, value_pre_grad)
    normed_part = (
        transposed_product(query_pre_grad, full_q)
        + transposed_product(key_pre_grad, full_k)
        + transposed_product(value_pre_grad, full_v)
    )
    normed_grad, query_gain_both, key_gain_both = lax.psum(
        (normed_part, query_gain_wide, key_gain_wide), "tensor"
    )
    unused_one, norm_one_back = jax.vjp(rms_norm, tokens_f, gain_one)
    input_part, gain_one_grad = norm_one_back(normed_grad)
    input_grad = state_grad + input_part
    (
        query_sum,
        key_sum,
        value_sum,
        out_sum,
        gain_one_sum,
        gain_two_sum,
        query_gain_sum,
        key_gain_sum,
    ) = (
        lax.psum_scatter(query_w_grad, "dp", scatter_dimension=0, tiled=True),
        lax.psum_scatter(key_w_grad, "dp", scatter_dimension=0, tiled=True),
        lax.psum_scatter(value_w_grad, "dp", scatter_dimension=0, tiled=True),
        lax.psum_scatter(out_w_grad, "dp", scatter_dimension=1, tiled=True),
        lax.psum_scatter(gain_one_grad, "dp", scatter_dimension=0, tiled=True),
        lax.psum_scatter(gain_two_grad, "dp", scatter_dimension=0, tiled=True),
        lax.psum_scatter(query_gain_both, "dp", scatter_dimension=0, tiled=True),
        lax.psum_scatter(key_gain_both, "dp", scatter_dimension=0, tiled=True),
    )
    return (
        output,
        input_grad,
        gain_one_sum,
        query_sum,
        key_sum,
        value_sum,
        query_gain_sum,
        key_gain_sum,
        out_sum,
        gain_two_sum,
        gate_w_grad[None],
        up_w_grad[None],
        down_grad[None],
    )


def solution(mesh):
    return jax.shard_map(
        body,
        mesh=mesh,
        in_specs=(
            P("dp", None),
            P("dp"),
            P("dp", "tensor"),
            P("dp", "tensor"),
            P("dp", "tensor"),
            P("dp"),
            P("dp"),
            P("tensor", "dp"),
            P("dp"),
            P("dp", None, "tensor"),
            P("dp", None, "tensor"),
            P("dp", "tensor", None),
            P("dp", None),
            P("dp", None),
            P("dp", None),
            P("dp", None),
            P("dp", None),
        ),
        out_specs=(
            P("dp", None),
            P("dp", None),
            P("dp"),
            P("dp", "tensor"),
            P("dp", "tensor"),
            P("dp", "tensor"),
            P("dp"),
            P("dp"),
            P("tensor", "dp"),
            P("dp"),
            P("dp", None, "tensor"),
            P("dp", None, "tensor"),
            P("dp", "tensor", None),
        ),
        check_vma=False,
    )
```

profile of v0, /device:TPU:0, one launch (start us, length us, event | category | flops | bytes accessed | tf_op | source)
XLA Modules:
  0.0 2886.3 jit_solution(17976755886035803237)
XLA Ops:
  9.5 23.1 all-gather.1
  32.7 17.6 all-gather.3
  50.3 19.0 all-gather.2
  74.4 3.8 convolution_convert_fusion.2
  79.7 35.1 %all-gather.14.cloned.1.call-done = bf16[2048,1024]{1,0:T(8,128)(2,1)} async-done(((bf16[128,1024]{1,0:T(8,128)(2,1)}), bf16[2048,1024]{1,0:T(8,128)(2,1)}) %all-gather.14.cloned.1.call-update) | async-done | bytes 4194320 | tf_op jit(solution)/shard_map/all_gather | solution.py:156
  114.8 4.8 multiply_reduce_fusion.4
  119.7 46.4 %all-gather.10.cloned.1.call-done = bf16[2048,1024]{1,0:T(8,128)(2,1)} async-done(((bf16[128,1024]{1,0:T(8,128)(2,1)}), bf16[2048,1024]{1,0:T(8,128)(2,1)}) %all-gather.10.cloned.1.call-update) | async-done | bytes 4194320 | tf_op jit(solution)/shard_map/all_gather | solution.py:157
  166.1 4.9 multiply_reduce_fusion.5
  171.0 4.9 all-reduce.16
  190.7 27.7 collective-permute-done.1
  218.4 4.1 maximum_select_fusion.1
  226.9 62.6 %all-reduce.8 = s32[256]{0:T(256)S(1)} all-reduce(s32[256]{0:T(256)S(1)} %dynamic-update-slice), channel_id=2, replica_groups=mesh['dp'=16,'tensor'=2] {'dp'}, use_global_device_ids=true, to_apply=%add.8 | all-reduce | flops 256 | bytes 2048
  292.4 4.7 maximum_select_fusion
  298.1 7.6 fusion.92
  305.8 6.7 fusion.2
  312.5 6.3 divide_convert_fusion
  324.3 5.4 fusion.48
  330.4 18.4 all-gather.4
  353.8 10.2 scatter_custom_fusion
  363.9 38.4 %all-reduce.22.cloned.1.call-done = f32[320,2048]{1,0:T(8,128)} async-done(((f32[320,2048]{1,0:T(8,128)}), f32[320,2048]{1,0:T(8,128)}) %all-reduce.22.cloned.1.call-update) | async-done | bytes 2621456 | tf_op jit(solution)/shard_map/psum | solution.py:219
  406.4 18.2 gather_fusion
  424.6 5.8 all-to-all-start
  430.7 9.9 scatter_custom_fusion.1
  444.3 35.7 %gather_fusion.2 = f32[4608,2048]{1,0:T(8,128)} fusion(f32[321,2048]{1,0:T(8,128)} %concatenate.83, s32[5120]{0:T(1024)S(1)} %pad_clamp_fusion), kind=kCustom, calls=%fused_computation.2 | custom fusion | bytes 75515904 | tf_op jit(solution)/shard_map/gather | solution.py:269
  480.0 20.6 multiply_convert_fusion
  500.6 263.2 %all-to-all-done = bf16[16,288,2048]{2,1,0:T(8,128)(2,1)} async-done(((bf16[16,288,2048]{2,1,0:T(8,128)(2,1)}), bf16[16,288,2048]{2,1,0:T(8,128)(2,1)}, u32[]{:S(2)}, u32[]{:S(2)}) %all-to-all-start) | async-done | bytes 18874400 | tf_op jit(solution)/shard_map/all_to_all | solution.py:110
  763.7 78.9 %all-to-all-start.2 = ((bf16[16,288,2048]{2,1,0:T(8,128)(2,1)}), bf16[16,288,2048]{2,1,0:T(8,128)(2,1)}, u32[]{:S(2)}, u32[]{:S(2)}) async-start(bf16[16,288,2048]{2,1,0:T(8,128)(2,1)} %multiply_convert_fusion), calls=%async_computation.2 | async-start | bytes 37748736 | tf_op jit(solution)/shard_map/all_to_all | solution.py:110
  842.7 16.7 fusion.17
  859.4 16.0 fusion.21
  875.4 300.5 %all-to-all-done.2 = bf16[16,288,2048]{2,1,0:T(8,128)(2,1)} async-done(((bf16[16,288,2048]{2,1,0:T(8,128)(2,1)}), bf16[16,288,2048]{2,1,0:T(8,128)(2,1)}, u32[]{:S(2)}, u32[]{:S(2)}) %all-to-all-start.2) | async-done | bytes 18874400 | tf_op jit(solution)/shard_map/all_to_all | solution.py:110
  1175.9 24.6 multiply_convert_fusion.2
  1200.5 17.6 fusion.19
  1218.1 24.9 add_convert_fusion
  1243.0 78.8 %all-to-all-start.3 = ((bf16[16,288,2048]{2,1,0:T(8,128)(2,1)}), bf16[16,288,2048]{2,1,0:T(8,128)(2,1)}, u32[]{:S(2)}, u32[]{:S(2)}) async-start(bf16[16,288,2048]{2,1,0:T(8,128)(2,1)} %bitcast.206), calls=%async_computation.3 | async-start | bytes 37748736 | tf_op jit(solution)/shard_map/all_to_all | solution.py:115
  1321.8 15.0 convolution_convert_fusion
  1336.8 318.2 %all-to-all-done.3 = bf16[16,288,2048]{2,1,0:T(8,128)(2,1)} async-done(((bf16[16,288,2048]{2,1,0:T(8,128)(2,1)}), bf16[16,288,2048]{2,1,0:T(8,128)(2,1)}, u32[]{:S(2)}, u32[]{:S(2)}) %all-to-all-start.3) | async-done | bytes 18874400 | tf_op jit(solution)/shard_map/all_to_all | solution.py:115
  1655.1 78.8 %all-to-all-start.1 = ((bf16[16,288,2048]{2,1,0:T(8,128)(2,1)}), bf16[16,288,2048]{2,1,0:T(8,128)(2,1)}, u32[]{:S(2)}, u32[]{:S(2)}) async-start(bf16[16,288,2048]{2,1,0:T(8,128)(2,1)} %bitcast.205), calls=%async_computation.1 | async-start | bytes 37748736 | tf_op jit(solution)/shard_map/all_to_all | solution.py:115
  1734.4 29.0 %gather_fusion.3 = bf16[2560,2048]{1,0:T(8,128)(2,1)} fusion(bf16[4608,2048]{1,0:T(8,128)(2,1)} %bitcast.26, s32[3072]{0:T(1024)S(1)} %pad_clamp_fusion.1), kind=kCustom, calls=%fused_computation.3 | custom fusion | bytes 20981760 | tf_op jit(solution)/shard_map/gather | solution.py:285
  1763.3 11.3 fusion
  1775.5 291.7 %all-to-all-done.1 = bf16[16,288,2048]{2,1,0:T(8,128)(2,1)} async-done(((bf16[16,288,2048]{2,1,0:T(8,128)(2,1)}), bf16[16,288,2048]{2,1,0:T(8,128)(2,1)}, u32[]{:S(2)}, u32[]{:S(2)}) %all-to-all-start.1) | async-done | bytes 18874400 | tf_op jit(solution)/shard_map/all_to_all | solution.py:115
  2067.2 29.0 %gather_fusion.1 = bf16[2560,2048]{1,0:T(8,128)(2,1)} fusion(bf16[4608,2048]{1,0:T(8,128)(2,1)} %bitcast.21, s32[3072]{0:T(1024)S(1)} %pad_clamp_fusion.1), kind=kCustom, calls=%fused_computation.1 | custom fusion | bytes 20981760 | tf_op jit(solution)/shard_map/gather | solution.py:263
  2096.2 11.0 fusion.1
  2111.0 115.2 %all-reduce.24.cloned.1.call-done = bf16[320,2048]{1,0:T(8,128)(2,1)} async-done(((bf16[320,2048]{1,0:T(8,128)(2,1)}), bf16[320,2048]{1,0:T(8,128)(2,1)}) %all-reduce.24.cloned.1.call-update) | async-done | bytes 1310736 | tf_op jit(solution)/shard_map/psum | solution.py:265
  2226.2 6.0 fusion.9
  2233.8 5.9 convolution_bitcast_fusion
  2244.2 7.7 multiply_reduce_fusion
  2251.9 6.6 multiply_convert_fusion.1
  2265.1 45.9 %collective-permute-done.3 = bf16[2,512,8,128]{3,1,2,0:T(8,128)(2,1)S(1)} collective-permute-done((bf16[2,512,8,128]{3,1,2,0:T(8,128)(2,1)S(1)}, bf16[2,512,8,128]{3,1,2,0:T(8,128)(2,1)S(1)}, u32[]{:S(2)}, u32[]{:S(2)}) %collective-permute-start.3) | collective-permute-done | bytes 2097184 | tf_op jit(solution)/shard_map/ppermute | solution.py:22
  2316.0 20.1 collective-permute-done.4
  2348.8 5.0 all-reduce.15
  2368.7 7.4 fusion.46
  2377.5 6.9 fusion.58
  2384.4 7.0 fusion.79
  2391.4 6.9 fusion.81
  2399.0 16.9 convolution_bitcast_fusion.2
  2415.9 16.5 convolution_bitcast_fusion.3
  2432.4 15.1 convolution_bitcast_fusion.1
  2450.7 63.6 %all-reduce.13 = (f32[2048]{0:T(1024)S(1)}, f32[2048]{0:T(1024)S(1)}, f32[2048]{0:T(1024)S(1)}, f32[2048]{0:T(1024)S(1)}) all-reduce(f32[2048]{0:T(1024)S(1)} %get-tuple-element.110, f32[2048]{0:T(1024)S(1)} %dynamic_update_slice.6, f32[2048]{0:T(1024)S(1)} %dynamic_update_slice.7, ...), channel_id=3, replica_groups=mesh['dp'=16,'tensor'=2] {'dp'}, use_global_device_ids=true, to_apply=%region_34.35.clone | all-reduce | flops 8192 | bytes 65536
  2515.5 5.4 all-reduce.14
  2521.0 4.7 fusion.10
  2525.7 26.4 reduce-scatter.11.cloned.1.call-done
  2552.1 108.9 %reduce-scatter.9.cloned.1.call-done = f32[128,1024]{1,0:T(8,128)} async-done(((f32[2048,1024]{1,0:T(8,128)}), f32[128,1024]{1,0:T(8,128)}) %reduce-scatter.9.cloned.1.call-update) | async-done | bytes 524304 | tf_op jit(solution)/shard_map/reduce_scatter | solution.py:374
  2661.0 109.1 %reduce-scatter.7.cloned.1.call-done = f32[128,1024]{1,0:T(8,128)} async-done(((f32[2048,1024]{1,0:T(8,128)}), f32[128,1024]{1,0:T(8,128)}) %reduce-scatter.7.cloned.1.call-update) | async-done | bytes 524304 | tf_op jit(solution)/shard_map/reduce_scatter | solution.py:373
  2770.1 108.9 %reduce-scatter.5.cloned.1.call-done = f32[128,1024]{1,0:T(8,128)} async-done(((f32[2048,1024]{1,0:T(8,128)}), f32[128,1024]{1,0:T(8,128)}) %reduce-scatter.5.cloned.1.call-update) | async-done | bytes 524304 | tf_op jit(solution)/shard_map/reduce_scatter | solution.py:372
  (363 shorter events, 106.1 us)
Async XLA Ops:
  7.2 1168.8 %copy-start = (bf16[1,512,2048]{2,1,0:T(8,128)(2,1)S(1)}, bf16[1,512,2048]{2,1,0:T(8,128)(2,1)}, u32[]{:S(2)}) copy-start(bf16[1,512,2048]{2,1,0:T(8,128)(2,1)} %param.30) | copy-start | bytes 6291460
  7.2 66.2 %copy-start.1 = (bf16[320,2048]{1,0:T(8,128)(2,1)S(1)}, bf16[320,2048]{1,0:T(8,128)(2,1)}, u32[]{:S(2)}) copy-start(bf16[320,2048]{1,0:T(8,128)(2,1)} %param.19) | copy-start | bytes 3932164
  7.2 67.2 %all-gather.12.cloned.1.call-start = ((), (), s32[]{:S(2)}) async-start(), calls=%async_computation.9 | async-start | bytes 4456448 | tf_op jit(solution)/shard_map/all_gather | solution.py:158
  7.9 106.9 %all-gather.14.cloned.1.call-start = ((), (), s32[]{:S(2)}) async-start(), calls=%async_computation.10 | async-start | bytes 4456448 | tf_op jit(solution)/shard_map/all_gather | solution.py:156
  8.7 157.4 %all-gather.10.cloned.1.call-start = ((), (), s32[]{:S(2)}) async-start(), calls=%async_computation.8 | async-start | bytes 4456448 | tf_op jit(solution)/shard_map/all_gather | solution.py:157
  9.4 314.9 %all-gather.16.cloned.1.call-start = ((), (), s32[]{:S(2)}) async-start(), calls=%async_computation.11 | async-start | bytes 4456448 | tf_op jit(solution)/shard_map/all_gather | solution.py:159
  32.6 133.5 %copy-start.42 = (f32[16,1,128]{2,1,0:T(1,128)}, f32[16,1,128]{2,1,0:T(1,128)S(1)}, u32[]{:S(2)}) copy-start(f32[16,1,128]{2,1,0:T(1,128)S(1)} %convert_element_type.174) | copy-start | bytes 24580
  71.1 109.5 %copy-start.59 = (f32[1024]{0:T(1024)}, f32[1024]{0:T(1024)S(1)}, u32[]{:S(2)}) copy-start(f32[1024]{0:T(1024)S(1)} %get-tuple-element.186) | copy-start | bytes 12292
  71.1 109.5 %copy-start.61 = (f32[1024]{0:T(1024)}, f32[1024]{0:T(1024)S(1)}, u32[]{:S(2)}) copy-start(f32[1024]{0:T(1024)S(1)} %get-tuple-element.185) | copy-start | bytes 12292
  74.4 91.7 %copy-start.49 = (f32[320]{0:T(512)}, f32[320]{0:T(512)S(1)}, u32[]{:S(2)}) copy-start(f32[320]{0:T(512)S(1)} %fusion.69) | copy-start | bytes 3844
  185.0 2.3 collective-permute-start
  190.0 34.0 %copy-start.75 = (s32[1,192]{1,0:T(1,128)S(1)}, s32[1,192]{1,0:T(1,128)}, u32[]{:S(2)}) copy-start(s32[1,192]{1,0:T(1,128)} %param.33) | copy-start | bytes 2308
  190.0 34.0 %copy-start.54 = (s32[320,8]{0,1:T(8,128)S(1)}, s32[320,8]{0,1:T(8,128)}, u32[]{:S(2)}) copy-start(s32[320,8]{0,1:T(8,128)} %param.31) | copy-start | bytes 30724
  190.0 35.2 %copy-start.82 = (u32[32]{0:T(128)S(1)}, u32[32]{0:T(128)}, u32[]{:S(2)}) copy-start(u32[32]{0:T(128)} %constant.143) | copy-start | bytes 388
  190.0 28.4 collective-permute-start.1
  190.7 211.7 %all-reduce.22.cloned.1.call-start = ((), (), s32[]{:S(2)}) async-start(), calls=%async_computation.12 | async-start | bytes 5242880 | tf_op jit(solution)/shard_map/psum | solution.py:219
  222.5 69.9 %collective-permute-start.2 = (bf16[2,512,8,128]{3,1,2,0:T(8,128)(2,1)}, bf16[2,512,8,128]{3,1,2,0:T(8,128)(2,1)}, u32[]{:S(2)}, u32[]{:S(2)}) collective-permute-start(bf16[2,512,8,128]{3,1,2,0:T(8,128)(2,1)} %maximum_select_fusion.1), channel_id=1, source_target_pairs={{0,8},{8,0},{2,10},{10,2},{4,12},{12,4},{6,14},{14,6},{16,24},{24,... | collective-permute-start | bytes 6291464 | tf_op jit(solution)/shard_map/ppermute | solution.py:22
  291.2 6.2 copy-start.47
  292.4 26.5 copy-start.38
  297.4 8.4 copy-start.36
  297.4 21.5 copy-start.24
  305.8 6.7 copy-start.55
  312.5 6.3 copy-start.57
  348.8 55.8 %copy-start.52 = (f32[16,1,128]{2,1,0:T(1,128)}, f32[16,1,128]{2,1,0:T(1,128)S(1)}, u32[]{:S(2)}) copy-start(f32[16,1,128]{2,1,0:T(1,128)S(1)} %convert_element_type.175) | copy-start | bytes 24580
  349.5 4.2 copy-start.73
  424.6 5.8 copy-start.67
  424.6 339.1 %all-to-all-start = ((bf16[16,288,2048]{2,1,0:T(8,128)(2,1)}), bf16[16,288,2048]{2,1,0:T(8,128)(2,1)}, u32[]{:S(2)}, u32[]{:S(2)}) async-start(bf16[16,288,2048]{2,1,0:T(8,128)(2,1)} %bitcast.204), calls=%async_computation | async-start | bytes 37748736 | tf_op jit(solution)/shard_map/all_to_all | solution.py:110
  763.7 412.2 %all-to-all-start.2 = ((bf16[16,288,2048]{2,1,0:T(8,128)(2,1)}), bf16[16,288,2048]{2,1,0:T(8,128)(2,1)}, u32[]{:S(2)}, u32[]{:S(2)}) async-start(bf16[16,288,2048]{2,1,0:T(8,128)(2,1)} %multiply_convert_fusion), calls=%async_computation.2 | async-start | bytes 37748736 | tf_op jit(solution)/shard_map/all_to_all | solution.py:110
  842.7 16.8 copy-start.88
  1175.9 24.6 copy-start.89
  1243.0 412.1 %all-to-all-start.3 = ((bf16[16,288,2048]{2,1,0:T(8,128)(2,1)}), bf16[16,288,2048]{2,1,0:T(8,128)(2,1)}, u32[]{:S(2)}, u32[]{:S(2)}) async-start(bf16[16,288,2048]{2,1,0:T(8,128)(2,1)} %bitcast.206), calls=%async_computation.3 | async-start | bytes 37748736 | tf_op jit(solution)/shard_map/all_to_all | solution.py:115
  1655.1 78.9 %copy-start.70 = (s32[320,8]{0,1:T(8,128)S(1)}, s32[320,8]{0,1:T(8,128)}, u32[]{:S(2)}) copy-start(s32[320,8]{0,1:T(8,128)} %get-tuple-element.138) | copy-start | bytes 30724
  1655.1 79.1 %copy-start.69 = (f32[320,8]{0,1:T(8,128)S(1)}, f32[320,8]{0,1:T(8,128)}, u32[]{:S(2)}) copy-start(f32[320,8]{0,1:T(8,128)} %get-tuple-element.136) | copy-start | bytes 30724
  1655.1 412.1 %all-to-all-start.1 = ((bf16[16,288,2048]{2,1,0:T(8,128)(2,1)}), bf16[16,288,2048]{2,1,0:T(8,128)(2,1)}, u32[]{:S(2)}, u32[]{:S(2)}) async-start(bf16[16,288,2048]{2,1,0:T(8,128)(2,1)} %bitcast.205), calls=%async_computation.1 | async-start | bytes 37748736 | tf_op jit(solution)/shard_map/all_to_all | solution.py:115
  1733.9 373.9 %all-reduce.26.cloned.1.call-start = ((), (), s32[]{:S(2)}) async-start(), calls=%async_computation.14 | async-start | bytes 5242880 | tf_op jit(solution)/shard_map/psum | solution.py:286
  1774.7 451.5 %all-reduce.24.cloned.1.call-start = ((), (), s32[]{:S(2)}) async-start(), calls=%async_computation.13 | async-start | bytes 2621440 | tf_op jit(solution)/shard_map/psum | solution.py:265
  2096.2 11.5 copy-start.56
  2096.2 11.5 copy-start.58
  2096.2 11.6 copy-start.53
  2096.2 11.6 copy-start.72
  2107.2 340.8 %all-reduce.28.cloned.1.call-start = ((), (), s32[]{:S(2)}) async-start(), calls=%async_computation.15 | async-start | bytes 5242880 | tf_op jit(solution)/shard_map/psum | solution.py:356
  2226.2 6.0 copy-start.87
  2232.2 12.0 slice-start
  2232.2 12.0 slice-start.1
  2233.8 10.4 slice-start.2
  2251.9 6.6 copy-start.27
  2263.6 47.4 %collective-permute-start.3 = (bf16[2,512,8,128]{3,1,2,0:T(8,128)(2,1)S(1)}, bf16[2,512,8,128]{3,1,2,0:T(8,128)(2,1)S(1)}, u32[]{:S(2)}, u32[]{:S(2)}) collective-permute-start(bf16[2,512,8,128]{3,1,2,0:T(8,128)(2,1)S(1)} %select_convert_fusion), channel_id=1, source_target_pairs={{0,8},{8,0},{2,10},{10,2},{4,12},{12,4},{6,14},{14,6},{16,24},{24,... | collective-permute-start | bytes 6291464 | tf_op jit(solution)/shard_map/ppermute | solution.py:22
  2312.0 24.1 collective-permute-start.4
  2313.5 30.8 %copy-start.12 = (f32[192,8,128]{2,0,1:T(8,128)}, f32[192,8,128]{2,0,1:T(8,128)S(1)}, u32[]{:S(2)}) copy-start(f32[192,8,128]{2,0,1:T(8,128)S(1)} %slice.136) | copy-start | bytes 2359300
  2315.5 23.1 copy-start.25
  2315.9 22.7 copy-start.15
  2315.9 22.7 copy-start.16
  2315.9 22.7 copy-start.40
  2315.9 22.7 copy-start.62
  2316.0 22.7 copy-start.66
  2336.5 3.1 collective-permute-start.5
  2347.8 5.9 copy-start.81
  2367.7 184.4 %reduce-scatter.11.cloned.1.call-start = ((), (), s32[]{:S(2)}) async-start(), calls=%async_computation.19 | async-start | bytes 8912896 | tf_op jit(solution)/shard_map/reduce_scatter | solution.py:375
  2376.2 284.8 %reduce-scatter.9.cloned.1.call-start = ((), (), s32[]{:S(2)}) async-start(), calls=%async_computation.18 | async-start | bytes 8912896 | tf_op jit(solution)/shard_map/reduce_scatter | solution.py:374
  2384.4 385.7 %reduce-scatter.7.cloned.1.call-start = ((), (), s32[]{:S(2)}) async-start(), calls=%async_computation.17 | async-start | bytes 8912896 | tf_op jit(solution)/shard_map/reduce_scatter | solution.py:373
  2391.4 487.6 %reduce-scatter.5.cloned.1.call-start = ((), (), s32[]{:S(2)}) async-start(), calls=%async_computation.16 | async-start | bytes 8912896 | tf_op jit(solution)/shard_map/reduce_scatter | solution.py:372
  2399.0 33.4 %slice-start.4 = ((s8[4718592]{0:T(1024)(128)(4,1)}), s8[4194304]{0:T(1024)(128)(4,1)S(1)}, s32[]{:S(2)}) async-start(s8[4718592]{0:T(1024)(128)(4,1)} %bitcast.233), calls=%async_computation.24 | async-start | bytes 8388608
  2415.9 16.5 slice-start.5
  2447.5 73.4 %copy-start.77 = (f32[320]{0:T(512)S(1)}, f32[320]{0:T(512)}, u32[]{:S(2)}) copy-start(f32[320]{0:T(512)} %copy-done.76) | copy-start | bytes 3844
  (54 other events, 110.4 us)
Sparse Core Ops, SparseCore 0:
  10.2 53.3 all-gather.11
  65.7 49.0 all-gather.13
  117.0 49.0 all-gather.9
  190.8 64.7 all-gather.15
  329.9 72.4 all-reduce.21
  1774.8 74.6 all-reduce.25
  2107.4 118.7 all-reduce.23
  2367.8 74.3 all-reduce.27
  2446.8 105.1 reduce-scatter.10
  2556.5 104.4 reduce-scatter.8
  2665.6 104.4 reduce-scatter.6
  2774.6 104.4 reduce-scatter.4
where the time goes:
time: 2900 us; the launch traced here: 2890 us
  waiting for transfers between devices  1860 us (64%)
  starting transfers between devices  249 us (9%)
  matrix products  246 us (8%)
  blocking collectives  220 us (8%)
  local copies, waits for them, and re-layouts  176 us (6%)
  other arithmetic  117 us (4%)
    all_to_all x2, waiting for transfers between devices, from_experts(): return lax.all_to_all(rows, 'dp', split_axis=0, concat_axis=0, tiled=True)  610 us
    all_to_all x2, waiting for transfers between devices, to_experts(): lax.all_to_all(rows, 'dp', split_axis=0, concat_axis=0, tiled=True)  564 us
    all_to_all x2, starting transfers between devices, from_experts(): return lax.all_to_all(rows, 'dp', split_axis=0, concat_axis=0, tiled=True)  158 us
    unnamed x2, blocking collectives  126 us
    psum x1, waiting for transfers between devices, body(): lax.psum(mixed_part.astype(jnp.bfloat16), 'tensor').astype(jnp.float32)  115 us
    reduce_scatter x1, waiting for transfers between devices, body(): lax.psum_scatter(key_w_grad, 'dp', scatter_dimension=0, tiled=True)  109 us
    reduce_scatter x1, waiting for transfers between devices, body(): lax.psum_scatter(query_w_grad, 'dp', scatter_dimension=0, tiled=True)  109 us
    reduce_scatter x1, waiting for transfers between devices, body(): lax.psum_scatter(value_w_grad, 'dp', scatter_dimension=0, tiled=True)  109 us
  transfers between devices with their start and end apart: 22, of which 16 were waited for; matrix products, arithmetic and copies ran while one was open for 12% of the time, Pallas kernels for 0%

commit v1 on v0

v1 whole, which is shorter than its diff:
```python
import jax
import jax.numpy as jnp
from jax import lax
from jax.experimental import pallas as pl
from jax.experimental.pallas import tpu as pltpu
from jax.sharding import PartitionSpec as P

HEADS = 16
HEAD = 128
GROUP = 8
PR_DEV = 128


EPSILON = 1e-05
LOW = jnp.bfloat16
FULL = jnp.float32


def swap_bit(block, axis, bit):
    count = lax.axis_size(axis)
    return lax.ppermute(block, axis, [(i, i ^ (1 << bit)) for i in range(count)])


def swap_tensor(block):
    return lax.ppermute(block, "tensor", [(0, 1), (1, 0)])


def rms_norm(values, gain):
    return values * lax.rsqrt(jnp.mean(values * values, axis=-1, keepdims=True) + EPSILON) * gain


def rope_tables(positions, head_size):
    half_size = head_size // 2
    inverse = 10000.0 ** (-(jnp.arange(half_size, dtype=FULL) * 2.0) / head_size)
    angles = positions.astype(FULL)[:, None] * inverse[None, :]
    cosine = jnp.concatenate([jnp.cos(angles), jnp.cos(angles)], axis=-1)
    sine = jnp.concatenate([jnp.sin(angles), jnp.sin(angles)], axis=-1)
    return (cosine, sine)


def rotate(values, cosine, sine):
    half_size = values.shape[-1] // 2
    turned = jnp.concatenate([-values[..., half_size:], values[..., :half_size]], axis=-1)
    return values * cosine[:, None, :] + turned * sine[:, None, :]


def rotate_back(values, cosine, sine):
    half_size = values.shape[-1] // 2
    scaled = values * sine[:, None, :]
    turned = jnp.concatenate([scaled[..., half_size:], -scaled[..., :half_size]], axis=-1)
    return values * cosine[:, None, :] + turned


def cont_positions(segment_row, gap_row, prompt_length):
    order = jnp.arange(segment_row.shape[0], dtype=jnp.int32)
    same = segment_row[:, None] == segment_row[None, :]
    earlier = order[None, :] < order[:, None]
    offset = jnp.sum((same & earlier).astype(jnp.int32), axis=1)
    labels = jnp.arange(gap_row.shape[0], dtype=jnp.int32)
    shifted = jnp.sum(
        jnp.where(segment_row[:, None] == labels[None, :], gap_row[None, :], 0), axis=1
    )
    return prompt_length + shifted + offset


def dot_nn(left, right):
    return jnp.dot(left, right, preferred_element_type=FULL)


def dot_tn(left, right):
    return lax.dot_general(left, right, (((0,), (0,)), ((), ())), preferred_element_type=FULL)


def dot_nt(left, right):
    return lax.dot_general(left, right, (((1,), (1,)), ((), ())), preferred_element_type=FULL)


def collect_prompt(keys, values):
    own = jnp.stack([keys, values], axis=0)
    near = swap_bit(own, "dp", 1)
    far = swap_bit(own, "dp", 2)
    last_keys = swap_bit(far[0], "dp", 1)
    last_values = swap_bit(near[1], "dp", 2)
    blocks = [None] * GROUP
    for at, piece in ((0, own), (2, near), (4, far)):
        blocks[at] = piece
        blocks[at + 1] = swap_bit(piece, "dp", 0)
    last = jnp.stack([last_keys, last_values], axis=0)
    blocks[6] = last
    blocks[7] = swap_bit(last, "dp", 0)
    return [b[0] for b in blocks], [b[1] for b in blocks]


def return_prompt(grads, order):
    parts = {j: grads[j] for j in range(GROUP)}
    for bit in order:
        gone = [j for j in sorted(parts) if j >> bit & 1]
        sent = jnp.stack([parts[j] for j in gone], axis=0).astype(LOW)
        got = swap_bit(sent, "dp", bit)
        for at, j in enumerate(gone):
            stay = j ^ (1 << bit)
            parts[stay] = parts[stay] + got[at].astype(FULL)
            del parts[j]
    return parts[0]


def masked_scores(queries, keyset, allowed):
    scores = jnp.einsum("qhd,khd->hqk", queries, keyset, preferred_element_type=FULL) * HEAD ** (
        -0.5
    )
    return jnp.where(allowed[None], scores, -1e30)


def expert_kernel(
    rows_ref, back_ref, gate_ref, wg0, wg1, wu0, wu1, wd0, wd1, grad_ref, h0, h1, g0, g1, u0, u1
):
    rows = rows_ref[...]
    back = back_ref[...]
    gate = gate_ref[...]
    total = None
    for wg, wu, wd, h, g, u in ((wg0, wu0, wd0, h0, g0, u0), (wg1, wu1, wd1, h1, g1, u1)):
        gate_pre = dot_nn(rows, wg[...])
        up_pre = dot_nn(rows, wu[...])
        hidden_grad = gate * dot_nt(back, wd[...])
        sig = 1.0 / (1.0 + jnp.exp(-gate_pre))
        act = gate_pre * sig
        h[...] = (gate * (act * up_pre)).astype(LOW)
        gate_grad = (hidden_grad * up_pre * (sig * (1.0 + gate_pre * (1.0 - sig)))).astype(LOW)
        up_grad = (hidden_grad * act).astype(LOW)
        g[...] = gate_grad
        u[...] = up_grad
        part = dot_nt(gate_grad, wg[...]) + dot_nt(up_grad, wu[...])
        total = part if total is None else total + part
    grad_ref[...] = total.astype(LOW)


def expert_pass(rows, back, gate, gate_mats, up_mats, down_mats):
    count, width = rows.shape
    hidden = gate_mats[0].shape[1]
    tile = 256
    whole = lambda array: pl.BlockSpec(
        array.shape, lambda i: (0, 0), pipeline_mode=pl.Buffered(1)
    )
    tall = lambda columns: pl.BlockSpec((tile, columns), lambda i: (i, 0))
    mats = [*gate_mats, *up_mats, *down_mats]
    flops = 2 * 5 * count * width * hidden * 2
    return pl.pallas_call(
        expert_kernel,
        grid=(count // tile,),
        in_specs=[tall(width), tall(width), tall(1)] + [whole(m) for m in mats],
        out_specs=[tall(width)] + [tall(hidden)] * 6,
        out_shape=[jax.ShapeDtypeStruct((count, width), LOW)]
        + [jax.ShapeDtypeStruct((count, hidden), LOW)] * 6,
        compiler_params=pltpu.CompilerParams(vmem_limit_bytes=58 * 1024 * 1024),
        cost_estimate=pl.CostEstimate(
            flops=flops,
            bytes_accessed=2 * (3 * count * width + 6 * count * hidden + 6 * width * hidden),
            transcendentals=2 * count * hidden,
        ),
    )(rows, back, gate, *mats)


def body(
    inputs,
    attn_gain,
    w_query,
    w_key,
    w_value,
    query_gain,
    key_gain,
    w_out,
    moe_gain,
    w_gate,
    w_up,
    w_down,
    experts,
    gates,
    segments,
    gaps,
    cotangent,
):
    dp_count = lax.axis_size("dp")
    dp_index = lax.axis_index("dp")
    side = lax.axis_index("tensor")
    token_count, model_width = inputs.shape
    half_count = token_count // 2
    top_count = experts.shape[1]
    expert_count = w_gate.shape[0] * dp_count
    capacity = token_count * top_count * dp_count * 9 // (8 * expert_count)
    prompt_length = PR_DEV * GROUP
    column_total = HEADS * HEAD
    block = w_query.shape[0]
    local_width = w_query.shape[1]
    local_heads = local_width // HEAD

    def own_half(array):
        return lax.dynamic_slice_in_dim(array, side * half_count, half_count, axis=0)

    def other_half(array):
        return lax.dynamic_slice_in_dim(array, (1 - side) * half_count, half_count, axis=0)

    def both_halves(own, other):
        first = side == 0
        return jnp.concatenate(
            [jnp.where(first, own, other), jnp.where(first, other, own)], axis=0
        )

    gate_mats = (w_gate[0], swap_tensor(w_gate[0]))
    up_mats = (w_up[0], swap_tensor(w_up[0]))
    down_mats = (w_down[0], swap_tensor(w_down[0]))

    gates_high = gates.astype(LOW)
    gates_low = (gates - gates_high.astype(FULL)).astype(LOW)
    routing = jnp.concatenate([experts.astype(LOW).T, gates_high.T, gates_low.T], axis=1)
    routing = jnp.pad(routing, ((0, 0), (0, local_width - 3 * token_count)))
    gains = jnp.concatenate([attn_gain, moe_gain, query_gain, key_gain])
    gains = jnp.pad(gains[None], ((0, 7), (0, local_width - 4 * block)))
    packed = jnp.concatenate([w_query, w_key, w_value, w_out.T, gains, routing], axis=0)
    gathered = lax.all_gather(packed, "dp", axis=0, tiled=False)
    full_q = gathered[:, :block].reshape(model_width, local_width)
    full_k = gathered[:, block : 2 * block].reshape(model_width, local_width)
    full_v = gathered[:, 2 * block : 3 * block].reshape(model_width, local_width)
    full_o = gathered[:, 3 * block : 4 * block].reshape(model_width, local_width)
    gain_rows = gathered[:, 4 * block].astype(FULL)
    gain_one, gain_two, gain_q, gain_k = (
        gain_rows[:, j * block : (j + 1) * block].reshape(-1) for j in range(4)
    )
    gain_query_local = lax.dynamic_slice_in_dim(gain_q, side * local_width, local_width)
    gain_key_local = lax.dynamic_slice_in_dim(gain_k, side * local_width, local_width)

    names = gathered[:, 4 * block + 8 :, :token_count]
    weights = gathered[:, 4 * block + 8 :, token_count : 2 * token_count].astype(
        FULL
    ) + gathered[:, 4 * block + 8 :, 2 * token_count : 3 * token_count].astype(FULL)
    named = names == dp_index.astype(LOW)
    picked = jnp.sum(named.astype(FULL), axis=1)
    weight = jnp.sum(jnp.where(named, weights, 0.0), axis=1)
    order = jnp.arange(token_count, dtype=jnp.int32)
    earlier = (order[:, None] < order[None, :]).astype(LOW)
    within = dot_nn(picked.astype(LOW), earlier)
    per_row = jnp.sum(picked, axis=1)
    rows_order = jnp.arange(dp_count, dtype=jnp.int32)
    ahead = jnp.sum(
        jnp.where(rows_order[None, :] < rows_order[:, None], per_row[None, :], 0.0), axis=1
    )
    kept = (picked > 0.0) & (within + ahead[:, None] < capacity)
    weight = jnp.where(kept, weight, 0.0)
    weight = lax.dynamic_slice_in_dim(weight, side * half_count, half_count, axis=1)
    weight = weight.reshape(-1, 1)

    cotangent_half = own_half(cotangent)
    back_rows = lax.all_gather(cotangent_half.astype(LOW), "dp", axis=0, tiled=True)

    tokens_f = inputs.astype(FULL)
    prompt_pos = dp_index % GROUP * PR_DEV + jnp.arange(PR_DEV, dtype=jnp.int32)
    later_pos = cont_positions(segments[0], gaps[0], prompt_length)
    positions = jnp.concatenate([prompt_pos, later_pos], axis=0)
    cosine, sine = rope_tables(positions, HEAD)
    normed_b = rms_norm(tokens_f, gain_one).astype(LOW)
    query_flat = dot_nn(normed_b, full_q)
    key_flat = dot_nn(normed_b, full_k)
    values_b = dot_nn(normed_b, full_v).astype(LOW)
    query_sq, key_sq = lax.psum(
        (jnp.sum(query_flat * query_flat, axis=1), jnp.sum(key_flat * key_flat, axis=1)), "tensor"
    )
    query_scale = lax.rsqrt(query_sq / column_total + EPSILON)[:, None]
    key_scale = lax.rsqrt(key_sq / column_total + EPSILON)[:, None]
    by_head = (token_count, local_heads, HEAD)
    queries_b = rotate(
        (query_flat * query_scale * gain_query_local).reshape(by_head), cosine, sine
    ).astype(LOW)
    keys_b = rotate(
        (key_flat * key_scale * gain_key_local).reshape(by_head), cosine, sine
    ).astype(LOW)
    key_blocks, value_blocks = collect_prompt(
        keys_b[:PR_DEV].reshape(PR_DEV, local_width), values_b[:PR_DEV]
    )
    keyset = jnp.concatenate(
        key_blocks + [keys_b[PR_DEV:].reshape(-1, local_width)], axis=0
    ).reshape(-1, local_heads, HEAD)
    valueset = jnp.concatenate(value_blocks + [values_b[PR_DEV:]], axis=0).reshape(
        -1, local_heads, HEAD
    )
    prompt_query = jnp.arange(token_count, dtype=jnp.int32) < PR_DEV
    prompt_at = jnp.arange(prompt_length, dtype=jnp.int32)
    prompt_keypos = ((dp_index % GROUP) ^ (prompt_at // PR_DEV)) * PR_DEV + prompt_at % PR_DEV
    allowed_prompt = (~prompt_query)[:, None] | (prompt_keypos[None, :] <= positions[:, None])
    query_segment = jnp.concatenate([jnp.full((PR_DEV,), -1, jnp.int32), segments[0]], axis=0)
    allowed_cont = (query_segment[:, None] == segments[0][None, :]) & (
        later_pos[None, :] <= positions[:, None]
    )
    allowed = jnp.concatenate([allowed_prompt, allowed_cont], axis=1)
    scores = masked_scores(queries_b, keyset, allowed)
    peak = jnp.max(scores, axis=-1, keepdims=True)
    expo = jnp.exp(scores - peak)
    total = jnp.sum(expo, axis=-1, keepdims=True)
    log_total = peak + jnp.log(total)
    probs_b = (expo / total).astype(LOW)
    context = jnp.einsum("hqk,khd->qhd", probs_b, valueset, preferred_element_type=FULL)
    context_b = context.reshape(token_count, local_width).astype(LOW)
    attn_part = dot_nt(context_b, full_o)
    attn_other = swap_tensor(other_half(attn_part).astype(LOW))
    hidden_state = (
        own_half(tokens_f) + own_half(attn_part) + attn_other.astype(FULL)
    )
    normed_two_b = rms_norm(hidden_state, gain_two).astype(LOW)

    expert_in = lax.all_gather(normed_two_b, "dp", axis=0, tiled=True)
    grad_rows, h0, h1, g0, g1, u0, u1 = expert_pass(
        expert_in, back_rows, weight, gate_mats, up_mats, down_mats
    )
    normed_two_grad = lax.psum_scatter(grad_rows, "dp", scatter_dimension=0, tiled=True).astype(
        FULL
    )
    mixed_rows = (dot_nn(h0, down_mats[0]) + dot_nn(h1, down_mats[1])).astype(LOW)
    mixed = lax.psum_scatter(mixed_rows, "dp", scatter_dimension=0, tiled=True).astype(FULL)
    output_half = hidden_state + mixed
    output = both_halves(output_half, swap_tensor(output_half))
    gate_w_grad = dot_tn(expert_in, g0) + swap_tensor(
        dot_tn(expert_in, g1).astype(LOW)
    ).astype(FULL)
    up_w_grad = dot_tn(expert_in, u0) + swap_tensor(dot_tn(expert_in, u1).astype(LOW)).astype(
        FULL
    )
    down_grad = dot_tn(h0, back_rows) + swap_tensor(dot_tn(h1, back_rows).astype(LOW)).astype(
        FULL
    )

    unused_two, norm_two_back = jax.vjp(rms_norm, hidden_state, gain_two)
    state_part, gain_two_grad = norm_two_back(normed_two_grad)
    state_half = cotangent_half + state_part
    attn_grad_half = state_half.astype(LOW)
    attn_grad_b = both_halves(attn_grad_half, swap_tensor(attn_grad_half))
    out_w_grad = dot_tn(attn_grad_b, context_b).astype(LOW)
    out_sum = lax.psum_scatter(out_w_grad, "dp", scatter_dimension=0, tiled=True)
    context_grad_b = dot_nn(attn_grad_b, full_o).astype(LOW).reshape(by_head)
    again = masked_scores(queries_b, keyset, allowed)
    probs = jnp.exp(again - log_total)
    prob_grad = jnp.einsum(
        "qhd,khd->hqk", context_grad_b, valueset, preferred_element_type=FULL
    )
    value_grad = jnp.einsum("hqk,qhd->khd", probs_b, context_grad_b, preferred_element_type=FULL)
    row_dot = jnp.sum(probs * prob_grad, axis=-1, keepdims=True)
    score_grad_b = (probs * (prob_grad - row_dot)).astype(LOW)
    query_grad = jnp.einsum(
        "hqk,khd->qhd", score_grad_b, keyset, preferred_element_type=FULL
    ) * HEAD ** (-0.5)
    key_grad = jnp.einsum(
        "hqk,qhd->khd", score_grad_b, queries_b, preferred_element_type=FULL
    ) * HEAD ** (-0.5)
    key_grad = key_grad.reshape(-1, local_width)
    value_grad = value_grad.reshape(-1, local_width)
    blocks_of = lambda array: [array[j * PR_DEV : (j + 1) * PR_DEV] for j in range(GROUP)]
    key_own = return_prompt(blocks_of(key_grad), (0, 1, 2))
    value_own = return_prompt(blocks_of(value_grad), (0, 2, 1))
    key_local = jnp.concatenate([key_own, key_grad[prompt_length:]], axis=0)
    value_local = jnp.concatenate([value_own, value_grad[prompt_length:]], axis=0)
    query_normed_grad = rotate_back(query_grad, cosine, sine).reshape(token_count, -1)
    key_normed_grad = rotate_back(key_local.reshape(by_head), cosine, sine).reshape(
        token_count, -1
    )
    query_inner, key_inner = lax.psum(
        (
            jnp.sum(query_flat * gain_query_local * query_normed_grad, axis=1),
            jnp.sum(key_flat * gain_key_local * key_normed_grad, axis=1),
        ),
        "tensor",
    )
    query_cube = query_scale * query_scale * query_scale
    key_cube = key_scale * key_scale * key_scale
    query_pre_grad = (
        query_scale * gain_query_local * query_normed_grad
        - query_flat * query_cube * (query_inner / column_total)[:, None]
    ).astype(LOW)
    key_pre_grad = (
        key_scale * gain_key_local * key_normed_grad
        - key_flat * key_cube * (key_inner / column_total)[:, None]
    ).astype(LOW)
    query_gain_part = jnp.sum(query_normed_grad * query_flat * query_scale, axis=0)
    key_gain_part = jnp.sum(key_normed_grad * key_flat * key_scale, axis=0)
    wide = lambda part: lax.dynamic_update_slice_in_dim(
        jnp.zeros((column_total,), FULL), part, side * local_width, 0
    )
    value_pre_grad = value_local.astype(LOW)
    w_grads = jnp.stack(
        [
            dot_tn(normed_b, query_pre_grad).astype(LOW).reshape(dp_count, block, local_width),
            dot_tn(normed_b, key_pre_grad).astype(LOW).reshape(dp_count, block, local_width),
            dot_tn(normed_b, value_pre_grad).astype(LOW).reshape(dp_count, block, local_width),
        ],
        axis=1,
    ).reshape(dp_count * 3 * block, local_width)
    w_sum = lax.psum_scatter(w_grads, "dp", scatter_dimension=0, tiled=True).astype(FULL)
    normed_part = (
        dot_nt(query_pre_grad, full_q)
        + dot_nt(key_pre_grad, full_k)
        + dot_nt(value_pre_grad, full_v)
    )
    normed_other = swap_tensor(other_half(normed_part).astype(LOW))
    normed_grad = own_half(normed_part) + normed_other.astype(FULL)
    unused_one, norm_one_back = jax.vjp(rms_norm, own_half(tokens_f), gain_one)
    input_part, gain_one_grad = norm_one_back(normed_grad)
    input_half = state_half + input_part
    input_grad = both_halves(input_half, swap_tensor(input_half))
    gain_grads = jnp.stack(
        [gain_one_grad, gain_two_grad, wide(query_gain_part), wide(key_gain_part)]
    ).reshape(4, dp_count, block)
    gain_sums = lax.psum_scatter(gain_grads, "dp", scatter_dimension=1, tiled=True)
    gain_sums = lax.psum(gain_sums.reshape(4, block), "tensor")
    return (
        output,
        input_grad,
        gain_sums[0],
        w_sum[:block],
        w_sum[block : 2 * block],
        w_sum[2 * block :],
        gain_sums[2],
        gain_sums[3],
        out_sum.astype(FULL).T,
        gain_sums[1],
        gate_w_grad[None],
        up_w_grad[None],
        down_grad[None],
    )


def solution(mesh):
    return jax.shard_map(
        body,
        mesh=mesh,
        in_specs=(
            P("dp", None),
            P("dp"),
            P("dp", "tensor"),
            P("dp", "tensor"),
            P("dp", "tensor"),
            P("dp"),
            P("dp"),
            P("tensor", "dp"),
            P("dp"),
            P("dp", None, "tensor"),
            P("dp", None, "tensor"),
            P("dp", "tensor", None),
            P("dp", None),
            P("dp", None),
            P("dp", None),
            P("dp", None),
            P("dp", None),
        ),
        out_specs=(
            P("dp", None),
            P("dp", None),
            P("dp"),
            P("dp", "tensor"),
            P("dp", "tensor"),
            P("dp", "tensor"),
            P("dp"),
            P("dp"),
            P("tensor", "dp"),
            P("dp"),
            P("dp", None, "tensor"),
            P("dp", None, "tensor"),
            P("dp", "tensor", None),
        ),
        check_vma=False,
    )
```

time: 2900 us -> 990 us (0.34)
  waiting for transfers between devices: 1860 us -> 502 us
  starting transfers between devices: 249 us -> 26.2 us
  blocking collectives: 220 us -> 74.2 us
  matrix products: 246 us -> 151 us
  local copies, waits for them, and re-layouts: 176 us -> 82.7 us
  Pallas kernels: 0 us -> 66.7 us
  other arithmetic: 117 us -> 65.7 us
    all_to_all x4 -> x0, waiting for transfers between devices: 1170 us -> none  [the longest x2 610 us: from_experts(): return lax.all_to_all(rows, 'dp', split_axis=0, concat_axis=0, tiled=True)]
    reduce_scatter x4, waiting for transfers between devices: 353 us -> 90.4 us  [the longest x1 90.4 us: body(): lax.psum_scatter(grad_rows, 'dp', scatter_dimension=0, tiled=True)]
    all_to_all x4 -> x0, starting transfers between devices: 242 us -> none  [the longest x2 158 us: from_experts(): return lax.all_to_all(rows, 'dp', split_axis=0, concat_axis=0, tiled=True)]
    ppermute x6 -> x25, waiting for transfers between devices: 95.9 us -> 323 us  [the longest x11 263 us: swap_tensor(): return lax.ppermute(block, 'tensor', [(0, 1), (1, 0)])]
    psum x4 -> x0, waiting for transfers between devices: 154 us -> none  [the longest x1 115 us: body(): lax.psum(mixed_part.astype(jnp.bfloat16), 'tensor').astype(jnp.float32)]
    gather x4 -> x0, local copies, waits for them, and re-layouts: 112 us -> none  [the longest x1 35.7 us: body(): padded_grad[owner]]
    dot_general x24, matrix products: 230 us -> 125 us  [the longest x10 65.1 us: dot_tn(): lax.dot_general(left, right, (((0,), (0,)), ((), ())), preferred_element_...]
    all_gather x4 -> x0, blocking collectives: 78.1 us -> none  [the longest x1 23.1 us: body(): lax.all_gather(attn_gain, 'dp', axis=0, tiled=True)]
  transfers between devices with their start and end apart: 22 -> 32, of which waited for: 16 -> 16; matrix products, arithmetic and copies ran while one was open for 12% -> 27% of each run, Pallas kernels for 0% -> 0%
where the time goes in v1:
time: 990 us; the launch traced here: 984 us
  waiting for transfers between devices  502 us (51%)
  matrix products  151 us (15%)
  local copies, waits for them, and re-layouts  82.7 us (8%)
  blocking collectives  74.2 us (7%)
  Pallas kernels  66.7 us (7%)
  other arithmetic  65.7 us (7%)
  starting transfers between devices  26.2 us (3%)
  between operations  16.2 us (2%)
    ppermute x11, waiting for transfers between devices, swap_tensor(): return lax.ppermute(block, 'tensor', [(0, 1), (1, 0)])  263 us
    reduce_scatter x1, waiting for transfers between devices, body(): lax.psum_scatter(grad_rows, 'dp', scatter_dimension=0, tiled=True)  90.4 us
    all_gather x1, waiting for transfers between devices, body(): gathered = lax.all_gather(packed, 'dp', axis=0, tiled=False)  87.5 us
    pallas_call x1, Pallas kernels, expert_pass(): pl.pallas_call(expert_kernel, grid=(count // tile,), in_specs=[tall(width...  66.7 us
    dot_general x10, matrix products, dot_tn(): lax.dot_general(left, right, (((0,), (0,)), ((), ())), preferred_element_...  65.1 us
    ppermute x14, waiting for transfers between devices, swap_bit(): return lax.ppermute(block, axis, [(i, i ^ 1 << bit) for i in range(count)])  60.3 us
    unnamed x1, blocking collectives  58.6 us
    dot_general x7, matrix products, dot_nn(): return jnp.dot(left, right, preferred_element_type=FULL)  41.1 us
  transfers between devices with their start and end apart: 32, of which 16 were waited for; matrix products, arithmetic and copies ran while one was open for 27% of the time, Pallas kernels for 0%

profile of v1, /device:TPU:0, one launch (start us, length us, event | category | flops | bytes accessed | tf_op | source)
XLA Modules:
  0.0 983.8 jit_solution(13058109171528730856)
XLA Ops:
  14.7 2.2 dynamic-slice_convert_fusion.2
  21.5 87.5 %all-gather.9.cloned.1.call-done = bf16[8448,1024]{1,0:T(8,128)(2,1)} async-done(((bf16[528,1024]{1,0:T(8,128)(2,1)}), bf16[8448,1024]{1,0:T(8,128)(2,1)}) %all-gather.9.cloned.1.call-update) | async-done | bytes 17301520 | tf_op jit(solution)/shard_map/all_gather | solution.py:219
  110.1 9.5 fusion.76
  124.7 5.2 all-reduce.5
  135.2 4.2 convolution_convert_fusion.9
  145.4 13.9 %collective-permute-done.1 = bf16[2,128,1024]{2,1,0:T(8,128)(2,1)} collective-permute-done((bf16[2,128,1024]{2,1,0:T(8,128)(2,1)}, bf16[2,128,1024]{2,1,0:T(8,128)(2,1)}, u32[]{:S(2)}, u32[]{:S(2)}) %collective-permute-start.1) | collective-permute-done | bytes 524320 | tf_op jit(solution)/shard_map/ppermute | solution.py:21
  162.1 12.4 %collective-permute-done.3 = bf16[2,128,1024]{2,1,0:T(8,128)(2,1)S(1)} collective-permute-done((bf16[2,128,1024]{2,1,0:T(8,128)(2,1)}, bf16[2,128,1024]{2,1,0:T(8,128)(2,1)S(1)}, u32[]{:S(2)}, u32[]{:S(2)}) %collective-permute-start.3) | collective-permute-done | bytes 524320 | tf_op jit(solution)/shard_map/ppermute | solution.py:21
  175.8 12.7 %collective-permute-done.5 = bf16[128,1024]{1,0:T(8,128)(2,1)S(1)} collective-permute-done((bf16[128,1024]{1,0:T(8,128)(2,1)S(1)}, bf16[128,1024]{1,0:T(8,128)(2,1)S(1)}, u32[]{:S(2)}, u32[]{:S(2)}) %collective-permute-start.5) | collective-permute-done | bytes 262176 | tf_op jit(solution)/shard_map/ppermute | solution.py:21
  193.8 4.5 fusion.85
  198.3 2.0 fusion
  200.3 2.7 copy-done
  203.0 2.4 divide_convert_fusion
  205.4 1.9 fusion.19
  213.8 15.2 %collective-permute-done.8 = bf16[160,2048]{1,0:T(8,128)(2,1)S(1)} collective-permute-done((bf16[160,2048]{1,0:T(8,128)(2,1)S(1)}, bf16[160,2048]{1,0:T(8,128)(2,1)S(1)}, u32[]{:S(2)}, u32[]{:S(2)}) %collective-permute-start.8) | collective-permute-done | bytes 655392 | tf_op jit(solution)/shard_map/ppermute | solution.py:25
  236.4 2.3 reshape.333.gate_ref
  238.7 41.5 %collective-permute-done.11.wd1 = bf16[512,2048]{1,0:T(8,128)(2,1)} collective-permute-done((bf16[512,2048]{1,0:T(8,128)(2,1)}, bf16[512,2048]{1,0:T(8,128)(2,1)}, u32[]{:S(2)}, u32[]{:S(2)}) %collective-permute-start.11) | collective-permute-done | bytes 2097184 | tf_op jit(solution)/shard_map/ppermute | solution.py:25
  280.2 44.9 %collective-permute-done.10.wu1 = bf16[2048,512]{1,0:T(8,128)(2,1)} collective-permute-done((bf16[2048,512]{1,0:T(8,128)(2,1)}, bf16[2048,512]{1,0:T(8,128)(2,1)}, u32[]{:S(2)}, u32[]{:S(2)}) %collective-permute-start.10) | collective-permute-done | bytes 2097184 | tf_op jit(solution)/shard_map/ppermute | solution.py:25
  325.1 43.5 %collective-permute-done.9.wg1 = bf16[2048,512]{1,0:T(8,128)(2,1)} collective-permute-done((bf16[2048,512]{1,0:T(8,128)(2,1)}, bf16[2048,512]{1,0:T(8,128)(2,1)}, u32[]{:S(2)}, u32[]{:S(2)}) %collective-permute-start.9) | collective-permute-done | bytes 2097184 | tf_op jit(solution)/shard_map/ppermute | solution.py:25
  368.6 66.7 %shard_map.264 = (bf16[2560,2048]{1,0:T(8,128)(2,1)}, bf16[2560,512]{1,0:T(8,128)(2,1)}, bf16[2560,512]{1,0:T(8,128)(2,1)}, bf16[2560,512]{1,0:T(8,128)(2,1)}, b...) custom-call(bf16[2560,2048]{1,0:T(8,128)(2,1)} %all-gather.5.cloned.1.call-done.rows_ref, ...), custom_call_target="tpu_custom_call" | custom-call | flops 53687091200 | bytes 59768832 | tf_op jit(solution)/shard_map/pallas_call | solution.py:147
  435.3 14.2 %fusion.88 = f32[2560,2048]{1,0:T(8,128)} fusion(bf16[2560,512]{1,0:T(8,128)(2,1)} %get-tuple-element.21, bf16[512,2048]{1,0:T(8,128)(2,1)} %collective-permute-done.11.wd1), kind=kOutput, calls=%fused_computation.290 | convolution fusion | flops 5368709120 | bytes 25690112 | tf_op jit(solution)/shard_map/dot_general | solution.py:67
  449.5 15.0 %add_convert_fusion = bf16[2560,2048]{1,0:T(8,128)(2,1)} fusion(f32[2560,2048]{1,0:T(8,128)} %fusion.88, bf16[2560,512]{1,0:T(8,128)(2,1)S(1)} %copy-done.93, bf16[1,512,2048]{2,1,0:T(8,128)(2,1)S(1)} %copy-done.91), kind=kOutput, calls=%fused_computation | convolution fusion | flops 5379194880 | bytes 36175872 | tf_op jit(solution)/shard_map/dot_general | solution.py:67
  464.7 90.4 %reduce-scatter.7.cloned.1.call-done = bf16[160,2048]{1,0:T(8,128)(2,1)} async-done(((bf16[2560,2048]{1,0:T(8,128)(2,1)}), bf16[160,2048]{1,0:T(8,128)(2,1)}) %reduce-scatter.7.cloned.1.call-update) | async-done | bytes 655376 | tf_op jit(solution)/shard_map/reduce_scatter | solution.py:312
  555.1 2.2 fusion.4
  560.6 14.9 %collective-permute-done.13 = bf16[160,2048]{1,0:T(8,128)(2,1)S(1)} collective-permute-done((bf16[160,2048]{1,0:T(8,128)(2,1)S(1)}, bf16[160,2048]{1,0:T(8,128)(2,1)S(1)}, u32[]{:S(2)}, u32[]{:S(2)}) %collective-permute-start.13) | collective-permute-done | bytes 655392 | tf_op jit(solution)/shard_map/ppermute | solution.py:25
  576.4 4.2 fusion.18
  580.6 7.8 fusion.87
  591.7 13.0 %multiply_reduce_fusion = (f32[8,320]{1,0:T(8,128)S(1)}, f32[8,320,1216]{2,1,0:T(8,128)}) fusion(f32[8,320,1216]{2,1,0:T(8,128)} %copy-done, f32[8,320]{1,0:T(8,128)S(1)} %log_add_fusion, bf16[1216,8,128]{2,0,1:T(8,128)(2,1)} %copy-done.32, bf16[40,8,8,128]{3,2,1,0:T(8,128)(2,1)S(1)} %fusion.18), kind=kOutput, calls=%fused_computation.2 | convolution fusion | flops 806254080 | bytes 28069888 | tf_op jit(solution)/shard_map/qhd,khd->hqk/dot_general | solution.py:339
  605.5 6.5 multiply_convert_fusion
  612.1 4.3 fusion.86
  618.4 4.4 convolution_convert_fusion
  622.8 6.6 broadcast_multiply_fusion
  629.4 2.9 fusion.77
  633.7 2.0 copy.224
  635.7 2.1 copy.225
  645.9 2.2 collective-permute-start.18
  651.6 2.2 slice_bitcast_fusion.28
  655.1 17.6 %collective-permute-done.18 = bf16[2,128,1024]{1,2,0:T(8,128)(2,1)} collective-permute-done((bf16[2,128,1024]{1,2,0:T(8,128)(2,1)}, bf16[2,128,1024]{1,2,0:T(8,128)(2,1)}, u32[]{:S(2)}, u32[]{:S(2)}) %collective-permute-start.18) | collective-permute-done | bytes 524320 | tf_op jit(solution)/shard_map/ppermute | solution.py:21
  672.7 1.9 fusion.34
  674.6 2.9 collective-permute-start.19
  679.2 2.0 copy.219
  683.6 2.0 fusion.38
  689.6 2.7 collective-permute-done.16
  692.2 2.0 copy.213
  697.5 2.0 multiply_reduce_fusion.2
  699.6 5.5 all-reduce.4
  705.1 1.9 subtract_convert_fusion
  707.4 2.4 fusion.9
  709.9 2.5 convolution_convert_fusion.1
  712.4 2.5 convolution_convert_fusion.2
  714.9 2.5 convolution_convert_fusion.3
  719.0 5.2 copy.229
  725.6 9.3 convolution_convert_fusion.5
  736.4 8.6 convolution_convert_fusion.6
  745.6 6.9 convolution_convert_fusion.4
  754.0 29.5 %collective-permute-done.23 = bf16[2048,512]{1,0:T(8,128)(2,1)S(1)} collective-permute-done((bf16[2048,512]{1,0:T(8,128)(2,1)S(1)}, bf16[2048,512]{1,0:T(8,128)(2,1)S(1)}, u32[]{:S(2)}, u32[]{:S(2)}) %collective-permute-start.23) | collective-permute-done | bytes 2097184 | tf_op jit(solution)/shard_map/ppermute | solution.py:25
  783.5 9.9 %add_bitcast_fusion.1 = f32[1,2048,512]{2,1,0:T(8,128)} fusion(bf16[2048,512]{1,0:T(8,128)(2,1)S(1)} %collective-permute-done.23, bf16[2560,2048]{1,0:T(8,128)(2,1)S(1)} %bitcast.373, bf16[2560,512]{1,0:T(8,128)(2,1)} %get-tuple-element.25), kind=kOutput, calls=%fused_computation.12 | convolution fusion | flops 5370806272 | bytes 19398656 | tf_op jit(solution)/shard_map/dot_general | solution.py:71
  801.1 27.4 %collective-permute-done.22 = bf16[2048,512]{1,0:T(8,128)(2,1)S(1)} collective-permute-done((bf16[2048,512]{1,0:T(8,128)(2,1)S(1)}, bf16[2048,512]{1,0:T(8,128)(2,1)S(1)}, u32[]{:S(2)}, u32[]{:S(2)}) %collective-permute-start.22) | collective-permute-done | bytes 2097184 | tf_op jit(solution)/shard_map/ppermute | solution.py:25
  828.4 7.1 add_bitcast_fusion.2
  835.6 46.3 %collective-permute-done.20 = bf16[160,2048]{1,0:T(8,128)(2,1)S(1)} collective-permute-done((bf16[160,2048]{1,0:T(8,128)(2,1)S(1)}, bf16[160,2048]{1,0:T(8,128)(2,1)S(1)}, u32[]{:S(2)}, u32[]{:S(2)}) %collective-permute-start.20) | collective-permute-done | bytes 655392 | tf_op jit(solution)/shard_map/ppermute | solution.py:25
  882.9 4.6 fusion.6
  889.0 11.6 %add_bitcast_fusion = f32[1,512,2048]{2,1,0:T(8,128)} fusion(bf16[512,2048]{1,0:T(8,128)(2,1)} %collective-permute-done.24, bf16[2560,512]{1,0:T(8,128)(2,1)S(1)} %copy-done.94, bf16[2560,2048]{1,0:T(8,128)(2,1)} %all-gather.7.cloned.1.call-done.back_ref), kind=kOutput, calls=%fused_computation.11 | convolution fusion | flops 5370806272 | bytes 19398656 | tf_op jit(solution)/shard_map/dot_general | solution.py:71
  901.2 58.6 %all-reduce.3 = f32[4,16,128]{2,0,1:T(4,128)S(1)} all-reduce(f32[4,16,128]{2,0,1:T(4,128)S(1)} %pad_maximum_fusion.17), channel_id=5, replica_groups=mesh['dp'=16,'tensor'=2] {'dp'}, use_global_device_ids=true, to_apply=%region_28.29.clone | all-reduce | flops 8192 | bytes 65536
  960.5 4.9 psum.39
  974.4 2.3 fusion.83
  (431 shorter events, 115.3 us)
Async XLA Ops:
  7.2 101.8 %all-gather.9.cloned.1.call-start = ((), (), s32[]{:S(2)}) async-start(), calls=%async_computation.10 | async-start | bytes 18382848 | tf_op jit(solution)/shard_map/all_gather | solution.py:219
  14.6 354.0 %all-gather.7.cloned.1.call-start = ((), (), s32[]{:S(2)}) async-start(), calls=%async_computation.5 | async-start | bytes 11141120 | tf_op jit(solution)/shard_map/all_gather | solution.py:252
  16.9 351.6 %all-gather.5.cloned.1.call-start = ((), (), s32[]{:S(2)}) async-start(), calls=%async_computation.4 | async-start | bytes 11141120 | tf_op jit(solution)/shard_map/all_gather | solution.py:308
  18.5 101.1 %copy-start.78 = (s32[320]{0:T(512)}, s32[320]{0:T(512)S(1)}, u32[]{:S(2)}) copy-start(s32[320]{0:T(512)S(1)} %get-tuple-element.182) | copy-start | bytes 3844
  20.1 111.6 %copy-start.46 = (f32[320,128]{1,0:T(8,128)}, f32[320,128]{1,0:T(8,128)S(1)}, u32[]{:S(2)}) copy-start(f32[320,128]{1,0:T(8,128)S(1)} %get-tuple-element.200) | copy-start | bytes 491524
  20.5 101.2 %copy-start.88 = (f32[320]{0:T(512)}, f32[320]{0:T(512)S(1)}, u32[]{:S(2)}) copy-start(f32[320]{0:T(512)S(1)} %add_rsqrt_fusion.2) | copy-start | bytes 3844
  110.0 25.1 %copy-start.67 = (f32[2048]{0:T(1024)}, f32[2048]{0:T(1024)S(1)}, u32[]{:S(2)}) copy-start(f32[2048]{0:T(1024)S(1)} %get-tuple-element.169) | copy-start | bytes 24580
  110.1 447.3 %copy-start.61 = (f32[2048]{0:T(1024)}, f32[2048]{0:T(1024)S(1)}, u32[]{:S(2)}) copy-start(f32[2048]{0:T(1024)S(1)} %get-tuple-element.166) | copy-start | bytes 24580
  110.1 21.7 %copy-start.65 = (f32[1024]{0:T(1024)}, f32[1024]{0:T(1024)S(1)}, u32[]{:S(2)}) copy-start(f32[1024]{0:T(1024)S(1)} %dynamic_slice.30) | copy-start | bytes 12292
  110.1 21.6 %copy-start.63 = (f32[1024]{0:T(1024)}, f32[1024]{0:T(1024)S(1)}, u32[]{:S(2)}) copy-start(f32[1024]{0:T(1024)S(1)} %dynamic_slice.29) | copy-start | bytes 12292
  121.6 10.1 %copy-start.7 = (f32[320,1024]{1,0:T(8,128)}, f32[320,1024]{1,0:T(8,128)S(1)}, u32[]{:S(2)}) copy-start(f32[320,1024]{1,0:T(8,128)S(1)} %get-tuple-element.185) | copy-start | bytes 3932164
  140.4 3.9 collective-permute-start
  140.6 18.8 %collective-permute-start.1 = (bf16[2,128,1024]{2,1,0:T(8,128)(2,1)}, bf16[2,128,1024]{2,1,0:T(8,128)(2,1)}, u32[]{:S(2)}, u32[]{:S(2)}) collective-permute-start(bf16[2,128,1024]{2,1,0:T(8,128)(2,1)} %pad_maximum_fusion.9), channel_id=1, source_target_pairs={{0,4},{2,6},{4,0},{6,2},{8,12},{10,14},{12,8},{14,10},{16,20},{18,... | collective-permute-start | bytes 1572872 | tf_op jit(solution)/shard_map/ppermute | solution.py:21
  142.8 31.7 %collective-permute-start.3 = (bf16[2,128,1024]{2,1,0:T(8,128)(2,1)}, bf16[2,128,1024]{2,1,0:T(8,128)(2,1)S(1)}, u32[]{:S(2)}, u32[]{:S(2)}) collective-permute-start(bf16[2,128,1024]{2,1,0:T(8,128)(2,1)} %pad_maximum_fusion.9), channel_id=1, source_target_pairs={{0,8},{2,10},{4,12},{6,14},{8,0},{10,2},{12,4},{14,6},{16,24},{18,... | collective-permute-start | bytes 1572872 | tf_op jit(solution)/shard_map/ppermute | solution.py:21
  160.6 28.0 %collective-permute-start.5 = (bf16[128,1024]{1,0:T(8,128)(2,1)S(1)}, bf16[128,1024]{1,0:T(8,128)(2,1)S(1)}, u32[]{:S(2)}, u32[]{:S(2)}) collective-permute-start(bf16[128,1024]{1,0:T(8,128)(2,1)S(1)} %get-tuple-element.156), channel_id=1, source_target_pairs={{0,8},{2,10},{4,12},{6,14},{8,0},{10,2},{12,4},{14,6},{16,24},{18,... | collective-permute-start | bytes 786440 | tf_op jit(solution)/shard_map/ppermute | solution.py:21
  174.6 13.9 %collective-permute-start.6 = (bf16[128,1024]{1,0:T(8,128)(2,1)S(1)}, bf16[128,1024]{1,0:T(8,128)(2,1)S(1)}, u32[]{:S(2)}, u32[]{:S(2)}) collective-permute-start(bf16[128,1024]{1,0:T(8,128)(2,1)S(1)} %get-tuple-element.152), channel_id=1, source_target_pairs={{0,4},{2,6},{4,0},{6,2},{8,12},{10,14},{12,8},{14,10},{16,20},{18,... | collective-permute-start | bytes 786440 | tf_op jit(solution)/shard_map/ppermute | solution.py:21
  174.7 13.9 %collective-permute-start.2 = (bf16[2,128,1024]{2,1,0:T(8,128)(2,1)}, bf16[2,128,1024]{2,1,0:T(8,128)(2,1)S(1)}, u32[]{:S(2)}, u32[]{:S(2)}) collective-permute-start(bf16[2,128,1024]{2,1,0:T(8,128)(2,1)} %collective-permute-done.1), channel_id=1, source_target_pairs={{0,2},{2,0},{4,6},{6,4},{8,10},{10,8},{12,14},{14,12},{16,18},{18,... | collective-permute-start | bytes 1572872 | tf_op jit(solution)/shard_map/ppermute | solution.py:21
  175.2 13.6 %collective-permute-start.4 = (bf16[2,128,1024]{2,1,0:T(8,128)(2,1)S(1)}, bf16[2,128,1024]{2,1,0:T(8,128)(2,1)S(1)}, u32[]{:S(2)}, u32[]{:S(2)}) collective-permute-start(bf16[2,128,1024]{2,1,0:T(8,128)(2,1)S(1)} %collective-permute-done.3), channel_id=1, source_target_pairs={{0,2},{2,0},{4,6},{6,4},{8,10},{10,8},{12,14},{14,12},{16,18},{18,... | collective-permute-start | bytes 1572872 | tf_op jit(solution)/shard_map/ppermute | solution.py:21
  188.6 2.0 collective-permute-start.7
  211.9 17.0 %collective-permute-start.8 = (bf16[160,2048]{1,0:T(8,128)(2,1)S(1)}, bf16[160,2048]{1,0:T(8,128)(2,1)S(1)}, u32[]{:S(2)}, u32[]{:S(2)}) collective-permute-start(bf16[160,2048]{1,0:T(8,128)(2,1)S(1)} %dynamic-slice_convert_fusion.1), channel_id=1, source_target_pairs={{0,1},{1,0},{2,3},{3,2},{4,5},{5,4},{6,7},{7,6},{8,9},{9,8},{10,11... | collective-permute-start | bytes 1966088 | tf_op jit(solution)/shard_map/ppermute | solution.py:25
  213.8 16.2 %copy-start.9 = (f32[320,2048]{1,0:T(8,128)}, f32[320,2048]{1,0:T(8,128)S(1)}, u32[]{:S(2)}) copy-start(f32[320,2048]{1,0:T(8,128)S(1)} %convert_element_type.239) | copy-start | bytes 7864324
  230.0 327.4 %copy-start.2 = (f32[160,2048]{1,0:T(8,128)}, f32[160,2048]{1,0:T(8,128)S(1)}, u32[]{:S(2)}) copy-start(f32[160,2048]{1,0:T(8,128)S(1)} %get-tuple-element.96) | copy-start | bytes 3932164
  230.0 327.4 %copy-start.76 = (f32[160]{0:T(256)}, f32[160]{0:T(256)S(1)}, u32[]{:S(2)}) copy-start(f32[160]{0:T(256)S(1)} %fusion.64) | copy-start | bytes 1924
  231.2 323.9 %reduce-scatter.7.cloned.1.call-start = ((), (), s32[]{:S(2)}) async-start(), calls=%async_computation.7 | async-start | bytes 11141120 | tf_op jit(solution)/shard_map/reduce_scatter | solution.py:312
  231.2 48.9 %collective-permute-start.11 = (bf16[512,2048]{1,0:T(8,128)(2,1)}, bf16[512,2048]{1,0:T(8,128)(2,1)}, u32[]{:S(2)}, u32[]{:S(2)}) collective-permute-start(bf16[512,2048]{1,0:T(8,128)(2,1)} %bitcast.378), channel_id=1, source_target_pairs={{0,1},{1,0},{2,3},{3,2},{4,5},{5,4},{6,7},{7,6},{8,9},{9,8},{10,11... | collective-permute-start | bytes 6291464 | tf_op jit(solution)/shard_map/ppermute | solution.py:25
  232.8 92.3 %collective-permute-start.10 = (bf16[2048,512]{1,0:T(8,128)(2,1)}, bf16[2048,512]{1,0:T(8,128)(2,1)}, u32[]{:S(2)}, u32[]{:S(2)}) collective-permute-start(bf16[2048,512]{1,0:T(8,128)(2,1)} %bitcast.376), channel_id=1, source_target_pairs={{0,1},{1,0},{2,3},{3,2},{4,5},{5,4},{6,7},{7,6},{8,9},{9,8},{10,11... | collective-permute-start | bytes 6291464 | tf_op jit(solution)/shard_map/ppermute | solution.py:25
  233.3 135.2 %collective-permute-start.9 = (bf16[2048,512]{1,0:T(8,128)(2,1)}, bf16[2048,512]{1,0:T(8,128)(2,1)}, u32[]{:S(2)}, u32[]{:S(2)}) collective-permute-start(bf16[2048,512]{1,0:T(8,128)(2,1)} %bitcast.374), channel_id=1, source_target_pairs={{0,1},{1,0},{2,3},{3,2},{4,5},{5,4},{6,7},{7,6},{8,9},{9,8},{10,11... | collective-permute-start | bytes 6291464 | tf_op jit(solution)/shard_map/ppermute | solution.py:25
  435.3 447.6 %reduce-scatter.5.cloned.1.call-start = ((), (), s32[]{:S(2)}) async-start(), calls=%async_computation.6 | async-start | bytes 11141120 | tf_op jit(solution)/shard_map/reduce_scatter | solution.py:316
  435.3 14.2 %copy-start.91 = (bf16[1,512,2048]{2,1,0:T(8,128)(2,1)S(1)}, bf16[1,512,2048]{2,1,0:T(8,128)(2,1)}, u32[]{:S(2)}) copy-start(bf16[1,512,2048]{2,1,0:T(8,128)(2,1)} %param.28) | copy-start | bytes 6291460
  435.3 14.2 %copy-start.93 = (bf16[2560,512]{1,0:T(8,128)(2,1)S(1)}, bf16[2560,512]{1,0:T(8,128)(2,1)}, u32[]{:S(2)}) copy-start(bf16[2560,512]{1,0:T(8,128)(2,1)} %get-tuple-element.20) | copy-start | bytes 7864324
  464.5 507.9 %reduce-scatter.11.cloned.1.call-start = ((), (), s32[]{:S(2)}) async-start(), calls=%async_computation.9 | async-start | bytes 4456448 | tf_op jit(solution)/shard_map/reduce_scatter | solution.py:335
  559.1 16.4 %collective-permute-start.13 = (bf16[160,2048]{1,0:T(8,128)(2,1)S(1)}, bf16[160,2048]{1,0:T(8,128)(2,1)S(1)}, u32[]{:S(2)}, u32[]{:S(2)}) collective-permute-start(bf16[160,2048]{1,0:T(8,128)(2,1)S(1)} %fusion.72), channel_id=1, source_target_pairs={{0,1},{1,0},{2,3},{3,2},{4,5},{5,4},{6,7},{7,6},{8,9},{9,8},{10,11... | collective-permute-start | bytes 1966088 | tf_op jit(solution)/shard_map/ppermute | solution.py:25
  589.8 14.9 %slice-start = ((s8[13107200]{0:T(1024)(128)(4,1)}), s8[524288]{0:T(1024)(128)(4,1)S(1)}, s32[]{:S(2)}) async-start(s8[13107200]{0:T(1024)(128)(4,1)} %bitcast.315), calls=%async_computation.11 | async-start | bytes 1048576
  591.7 13.0 %slice-start.1 = ((s8[13107200]{0:T(1024)(128)(4,1)}), s8[4194304]{0:T(1024)(128)(4,1)S(1)}, s32[]{:S(2)}) async-start(s8[13107200]{0:T(1024)(128)(4,1)} %bitcast.315), calls=%async_computation.12 | async-start | bytes 8388608
  591.7 13.0 %slice-start.2 = ((s8[13107200]{0:T(1024)(128)(4,1)}), s8[4194304]{0:T(1024)(128)(4,1)S(1)}, s32[]{:S(2)}) async-start(s8[13107200]{0:T(1024)(128)(4,1)} %bitcast.315), calls=%async_computation.13 | async-start | bytes 8388608
  591.7 13.8 %slice-start.3 = ((s8[13107200]{0:T(1024)(128)(4,1)}), s8[4194304]{0:T(1024)(128)(4,1)S(1)}, s32[]{:S(2)}) async-start(s8[13107200]{0:T(1024)(128)(4,1)} %bitcast.315), calls=%async_computation.14 | async-start | bytes 8388608
  591.7 51.9 %collective-permute-start.17 = (bf16[4,128,1024]{1,2,0:T(8,128)(2,1)}, bf16[4,128,1024]{1,2,0:T(8,128)(2,1)}, u32[]{:S(2)}, u32[]{:S(2)}) collective-permute-start(bf16[4,128,1024]{1,2,0:T(8,128)(2,1)} %pad_maximum_fusion.5), channel_id=1, source_target_pairs={{0,2},{2,0},{4,6},{6,4},{8,10},{10,8},{12,14},{14,12},{16,18},{18,... | collective-permute-start | bytes 3145736 | tf_op jit(solution)/shard_map/ppermute | solution.py:21
  618.4 29.7 %collective-permute-start.14 = (bf16[4,128,1024]{1,2,0:T(8,128)(2,1)}, bf16[4,128,1024]{1,2,0:T(8,128)(2,1)}, u32[]{:S(2)}, u32[]{:S(2)}) collective-permute-start(bf16[4,128,1024]{1,2,0:T(8,128)(2,1)} %pad_maximum_fusion.4), channel_id=1, source_target_pairs={{0,2},{2,0},{4,6},{6,4},{8,10},{10,8},{12,14},{14,12},{16,18},{18,... | collective-permute-start | bytes 3145736 | tf_op jit(solution)/shard_map/ppermute | solution.py:21
  639.8 334.6 %reduce-scatter.9.cloned.1.call-start = ((), (), s32[]{:S(2)}) async-start(), calls=%async_computation.8 | async-start | bytes 13369344 | tf_op jit(solution)/shard_map/reduce_scatter | solution.py:393
  645.9 26.7 %collective-permute-start.18 = (bf16[2,128,1024]{1,2,0:T(8,128)(2,1)}, bf16[2,128,1024]{1,2,0:T(8,128)(2,1)}, u32[]{:S(2)}, u32[]{:S(2)}) collective-permute-start(bf16[2,128,1024]{1,2,0:T(8,128)(2,1)} %pad_maximum_fusion.12), channel_id=1, source_target_pairs={{0,8},{2,10},{4,12},{6,14},{8,0},{10,2},{12,4},{14,6},{16,24},{18,... | collective-permute-start | bytes 1572872 | tf_op jit(solution)/shard_map/ppermute | solution.py:21
  650.1 33.4 %collective-permute-start.15 = (bf16[2,128,1024]{1,2,0:T(8,128)(2,1)}, bf16[2,128,1024]{1,2,0:T(8,128)(2,1)}, u32[]{:S(2)}, u32[]{:S(2)}) collective-permute-start(bf16[2,128,1024]{1,2,0:T(8,128)(2,1)} %pad_maximum_fusion.11), channel_id=1, source_target_pairs={{0,4},{2,6},{4,0},{6,2},{8,12},{10,14},{12,8},{14,10},{16,20},{18,... | collective-permute-start | bytes 1572872 | tf_op jit(solution)/shard_map/ppermute | solution.py:21
  674.6 12.9 %collective-permute-start.19 = (bf16[1,128,1024]{1,2,0:T(8,128)(2,1)}, bf16[1,128,1024]{1,2,0:T(8,128)(2,1)}, u32[]{:S(2)}, u32[]{:S(2)}) collective-permute-start(bf16[1,128,1024]{1,2,0:T(8,128)(2,1)} %fusion.34), channel_id=1, source_target_pairs={{0,4},{2,6},{4,0},{6,2},{8,12},{10,14},{12,8},{14,10},{16,20},{18,... | collective-permute-start | bytes 786440 | tf_op jit(solution)/shard_map/ppermute | solution.py:21
  685.6 6.7 collective-permute-start.16
  725.5 10.9 %copy-start.99 = (bf16[2560,512]{1,0:T(8,128)(2,1)S(1)}, bf16[2560,512]{1,0:T(8,128)(2,1)}, u32[]{:S(2)}) copy-start(bf16[2560,512]{1,0:T(8,128)(2,1)} %get-tuple-element.24) | copy-start | bytes 7864324
  725.5 20.1 %slice-start.4 = ((s8[10485760]{0:T(1024)(128)(4,1)}), s8[4194304]{0:T(1024)(128)(4,1)S(1)}, s32[]{:S(2)}) async-start(s8[10485760]{0:T(1024)(128)(4,1)} %bitcast.370), calls=%async_computation.15 | async-start | bytes 8388608
  725.5 20.1 %slice-start.5 = ((s8[10485760]{0:T(1024)(128)(4,1)}), s8[4194304]{0:T(1024)(128)(4,1)S(1)}, s32[]{:S(2)}) async-start(s8[10485760]{0:T(1024)(128)(4,1)} %bitcast.370), calls=%async_computation.16 | async-start | bytes 8388608
  734.9 48.6 %collective-permute-start.23 = (bf16[2048,512]{1,0:T(8,128)(2,1)S(1)}, bf16[2048,512]{1,0:T(8,128)(2,1)S(1)}, u32[]{:S(2)}, u32[]{:S(2)}) collective-permute-start(bf16[2048,512]{1,0:T(8,128)(2,1)S(1)} %convolution_convert_fusion.5), channel_id=1, source_target_pairs={{0,1},{1,0},{2,3},{3,2},{4,5},{5,4},{6,7},{7,6},{8,9},{9,8},{10,11... | collective-permute-start | bytes 6291464 | tf_op jit(solution)/shard_map/ppermute | solution.py:25
  736.4 47.1 %slice-start.7 = ((s8[10485760]{0:T(1024)(128)(4,1)}), s8[4194304]{0:T(1024)(128)(4,1)S(1)}, s32[]{:S(2)}) async-start(s8[10485760]{0:T(1024)(128)(4,1)} %bitcast.372), calls=%async_computation.18 | async-start | bytes 8388608
  736.4 47.1 %slice-start.8 = ((s8[10485760]{0:T(1024)(128)(4,1)}), s8[4194304]{0:T(1024)(128)(4,1)S(1)}, s32[]{:S(2)}) async-start(s8[10485760]{0:T(1024)(128)(4,1)} %bitcast.372), calls=%async_computation.19 | async-start | bytes 8388608
  745.0 38.5 %slice-start.9 = ((s8[10485760]{0:T(1024)(128)(4,1)}), s8[2097152]{0:T(1024)(128)(4,1)S(1)}, s32[]{:S(2)}) async-start(s8[10485760]{0:T(1024)(128)(4,1)} %bitcast.372), calls=%async_computation.20 | async-start | bytes 4194304
  745.0 83.5 %collective-permute-start.22 = (bf16[2048,512]{1,0:T(8,128)(2,1)S(1)}, bf16[2048,512]{1,0:T(8,128)(2,1)S(1)}, u32[]{:S(2)}, u32[]{:S(2)}) collective-permute-start(bf16[2048,512]{1,0:T(8,128)(2,1)S(1)} %convolution_convert_fusion.6), channel_id=1, source_target_pairs={{0,1},{1,0},{2,3},{3,2},{4,5},{5,4},{6,7},{7,6},{8,9},{9,8},{10,11... | collective-permute-start | bytes 6291464 | tf_op jit(solution)/shard_map/ppermute | solution.py:25
  752.5 136.5 %collective-permute-start.24 = (bf16[512,2048]{1,0:T(8,128)(2,1)}, bf16[512,2048]{1,0:T(8,128)(2,1)}, u32[]{:S(2)}, u32[]{:S(2)}) collective-permute-start(bf16[512,2048]{1,0:T(8,128)(2,1)} %convolution_convert_fusion.4), channel_id=1, source_target_pairs={{0,1},{1,0},{2,3},{3,2},{4,5},{5,4},{6,7},{7,6},{8,9},{9,8},{10,11... | collective-permute-start | bytes 6291464 | tf_op jit(solution)/shard_map/ppermute | solution.py:25
  797.8 30.6 %copy-start.98 = (bf16[2560,512]{1,0:T(8,128)(2,1)S(1)}, bf16[2560,512]{1,0:T(8,128)(2,1)}, u32[]{:S(2)}) copy-start(bf16[2560,512]{1,0:T(8,128)(2,1)} %get-tuple-element.23) | copy-start | bytes 7864324
  799.5 82.5 %copy-start.30 = (f32[320,2048]{1,0:T(8,128)}, f32[320,2048]{1,0:T(8,128)S(1)}, u32[]{:S(2)}) copy-start(f32[320,2048]{1,0:T(8,128)S(1)} %convolution_add_fusion) | copy-start | bytes 7864324
  799.6 82.4 %collective-permute-start.20 = (bf16[160,2048]{1,0:T(8,128)(2,1)S(1)}, bf16[160,2048]{1,0:T(8,128)(2,1)S(1)}, u32[]{:S(2)}, u32[]{:S(2)}) collective-permute-start(bf16[160,2048]{1,0:T(8,128)(2,1)S(1)} %dynamic-slice_convert_fusion), channel_id=1, source_target_pairs={{0,1},{1,0},{2,3},{3,2},{4,5},{5,4},{6,7},{7,6},{8,9},{9,8},{10,11... | collective-permute-start | bytes 1966088 | tf_op jit(solution)/shard_map/ppermute | solution.py:25
  828.4 53.5 %copy-start.10 = (f32[320,2048]{1,0:T(8,128)S(1)}, f32[320,2048]{1,0:T(8,128)}, u32[]{:S(2)}) copy-start(f32[320,2048]{1,0:T(8,128)} %copy-done.9) | copy-start | bytes 7864324
  835.6 47.3 %copy-start.3 = (f32[160,2048]{1,0:T(8,128)S(1)}, f32[160,2048]{1,0:T(8,128)}, u32[]{:S(2)}) copy-start(f32[160,2048]{1,0:T(8,128)} %copy-done.2) | copy-start | bytes 3932164
  835.6 47.3 %copy-start.19 = (bf16[160,2048]{1,0:T(8,128)(2,1)S(1)}, bf16[160,2048]{1,0:T(8,128)(2,1)}, u32[]{:S(2)}) copy-start(bf16[160,2048]{1,0:T(8,128)(2,1)} %reduce-scatter.7.cloned.1.call-done) | copy-start | bytes 1966084
  835.6 47.3 %copy-start.62 = (f32[2048]{0:T(1024)S(1)}, f32[2048]{0:T(1024)}, u32[]{:S(2)}) copy-start(f32[2048]{0:T(1024)} %copy-done.61) | copy-start | bytes 24580
  835.6 47.3 %copy-start.77 = (f32[160]{0:T(256)S(1)}, f32[160]{0:T(256)}, u32[]{:S(2)}) copy-start(f32[160]{0:T(256)} %copy-done.76) | copy-start | bytes 1924
  835.6 47.3 %copy-start.84 = (f32[160]{0:T(256)S(1)}, f32[160]{0:T(256)}, u32[]{:S(2)}) copy-start(f32[160]{0:T(256)} %copy-done.83) | copy-start | bytes 1924
  887.5 13.7 %copy-start.73 = (f32[2048]{0:T(1024)S(1)}, f32[2048]{0:T(1024)}, u32[]{:S(2)}) copy-start(f32[2048]{0:T(1024)} %get-tuple-element.85) | copy-start | bytes 24580
  887.5 78.5 %collective-permute-start.21 = (f32[160,2048]{1,0:T(8,128)}, f32[160,2048]{1,0:T(8,128)S(1)}, u32[]{:S(2)}, u32[]{:S(2)}) collective-permute-start(f32[160,2048]{1,0:T(8,128)} %get-tuple-element.123), channel_id=1, source_target_pairs={{0,1},{1,0},{2,3},{3,2},{4,5},{5,4},{6,7},{7,6},{8,9},{9,8},{10,11... | collective-permute-start | bytes 3932168 | tf_op jit(solution)/shard_map/ppermute | solution.py:25
  900.6 68.5 %collective-permute-start.12 = (f32[160,2048]{1,0:T(8,128)S(1)}, f32[160,2048]{1,0:T(8,128)}, u32[]{:S(2)}, u32[]{:S(2)}) collective-permute-start(f32[160,2048]{1,0:T(8,128)S(1)} %get-tuple-element.124), channel_id=1, source_target_pairs={{0,1},{1,0},{2,3},{3,2},{4,5},{5,4},{6,7},{7,6},{8,9},{9,8},{10,11... | collective-permute-start | bytes 3932168 | tf_op jit(solution)/shard_map/ppermute | solution.py:25
  (78 other events, 248.1 us)
Sparse Core Ops, SparseCore 0:
  14.7 94.2 all-gather.8
  111.3 97.6 all-gather.6
  231.3 88.5 all-gather.4
  435.4 119.7 reduce-scatter.6
  559.0 124.1 reduce-scatter.4
  687.0 73.0 reduce-scatter.10
  764.7 133.7 reduce-scatter.8

commit v2 on v1

--- a/solution.py
+++ b/solution.py
@@ -23,6 +23,77 @@
 
 def swap_tensor(block):
     return lax.ppermute(block, "tensor", [(0, 1), (1, 0)])
+
+
+RING = (0, 2, 4, 6, 7, 5, 3, 1)
+AHEAD = [
+    (RING[p] * 2 + c, RING[(p + 1) % len(RING)] * 2 + c) for p in range(len(RING)) for c in range(2)
+]
+BEHIND = [(to, at) for at, to in AHEAD]
+
+
+def ahead(block):
+    return lax.ppermute(block, "dp", AHEAD)
+
+
+def behind(block):
+    return lax.ppermute(block, "dp", BEHIND)
+
+
+def ring_blocks(dp_index):
+    chip, core = dp_index // 2, dp_index % 2
+    place = jnp.where(chip % 2 == 0, chip // 2, 7 - chip // 2)
+    steps, cross = [], []
+    for hop in (1, 2, 3):
+        steps += [-hop, hop, -hop, hop]
+        cross += [0, 0, 1, 1]
+    steps += [0, 0, 4, 4]
+    cross += [0, 1, 0, 1]
+    there = (place + jnp.array(steps, jnp.int32)) % 8
+    chips = jnp.where(there < 4, 2 * there, 2 * (7 - there) + 1)
+    return 2 * chips + (core ^ jnp.array(cross, jnp.int32))
+
+
+def add_low(*parts):
+    total = parts[0].astype(FULL)
+    for part in parts[1:]:
+        total = total + part.astype(FULL)
+    return total.astype(LOW)
+
+
+def together(value, *others):
+    return lax.optimization_barrier((value, *others))
+
+
+def ring_sum(same, cross, fillers):
+    both = {hop: add_low(same[hop], swap_bit(cross[hop], "dp", 0)) for hop in (4, 3, 2, 1, 0)}
+    rows = both[0].shape[0]
+    cut = rows // 2
+    done = []
+
+    def fill(gate):
+        for work, *operands in fillers[len(done)]:
+            gate, *operands = together(gate, *operands)
+            done_here.append(work(*operands))
+        done.append(list(done_here))
+        done_here.clear()
+        return gate
+
+    done_here = []
+    right, left = ahead(both[4][:cut]), behind(both[4][cut:])
+    left = fill(left)
+    outward, inward = both[3][rows:], both[3][:rows]
+    right = jnp.concatenate([add_low(outward[:cut], right), outward[cut:]], axis=0)
+    left = jnp.concatenate([inward[:cut], add_low(inward[cut:], left)], axis=0)
+    right, left = ahead(right), behind(left)
+    left = fill(left)
+    for hop in (2, 1):
+        right = ahead(add_low(both[hop][rows:], right))
+        left = behind(add_low(both[hop][:rows], left))
+        if hop == 2:
+            left = fill(left)
+    total = both[0].astype(FULL) + right.astype(FULL) + left.astype(FULL)
+    return total, [out for outs in done for out in outs]
 
 
 def rms_norm(values, gain):
@@ -158,6 +229,134 @@
             transcendentals=2 * count * hidden,
         ),
     )(rows, back, gate, *mats)
+
+
+def chunk_kernel(pieces, first, *refs):
+    piece_refs, refs = refs[:pieces], refs[pieces:]
+    back_ref, gate_ref, wg0, wg1, wu0, wu1, wd0, wd1, vg0, vg1, vu0, vu1 = refs[:12]
+    same_ref, cross_ref, rows_ref, h0, h1, g0, g1, u0, u1, kept_g, kept_u = refs[
+        12 if first else 19 :
+    ]
+    step = pl.program_id(0)
+
+    @pl.when(step == 0)
+    def _():
+        at = 0
+        for piece in piece_refs:
+            rows_ref[at : at + piece.shape[0]] = piece[...]
+            at += piece.shape[0]
+
+    def work(wg, wu, wd, h, g, u):
+        rows = rows_ref[...]
+        gate = gate_ref[...]
+        gate_pre = dot_nn(rows, wg[...])
+        up_pre = dot_nn(rows, wu[...])
+        hidden_grad = gate * dot_nt(back_ref[...], wd[...])
+        sig = 1.0 / (1.0 + jnp.exp(-gate_pre))
+        act = gate_pre * sig
+        h[...] = (gate * (act * up_pre)).astype(LOW)
+        gate_grad = (hidden_grad * up_pre * (sig * (1.0 + gate_pre * (1.0 - sig)))).astype(LOW)
+        up_grad = (hidden_grad * act).astype(LOW)
+        g[...] = gate_grad
+        u[...] = up_grad
+        kept_g[step] = gate_grad
+        kept_u[step] = up_grad
+
+    @pl.when(step < 2)
+    def _():
+        work(wg0, wu0, wd0, h0, g0, u0)
+
+    @pl.when((step >= 2) & (step < 4))
+    def _():
+        work(wg1, wu1, wd1, h1, g1, u1)
+
+    @pl.when(step >= 4)
+    def _():
+        total = None
+        for kept, first_half, second_half in ((kept_g, vg0, vg1), (kept_u, vu0, vu1)):
+            for at, mat in ((0, first_half), (2, second_half)):
+                left = jnp.concatenate([kept[at], kept[at + 1]], axis=1)
+                part = dot_nt(left, mat[...])
+                total = part if total is None else total + part
+        half = same_ref.shape[0]
+        same_ref[...] = total[:half].astype(LOW)
+        cross_ref[...] = total[half:].astype(LOW)
+
+
+def expert_chunk(pieces, back, gate, mats, at, held):
+    width = back.shape[1]
+    hidden = mats[0].shape[1]
+    part = hidden // 2
+    slab = width // 4
+    count = sum(piece.shape[0] for piece in pieces)
+    all_rows = back.shape[0]
+    own = lambda j: jnp.minimum(j, 1)
+    other = lambda j: jnp.clip(j - 2, 0, 1)
+    late = lambda j: jnp.maximum(j - 4, 0)
+    once = pl.Buffered(1)
+    fixed = lambda array: pl.BlockSpec(array.shape, lambda j: (0, 0), pipeline_mode=once)
+    chunk = lambda columns, **mode: pl.BlockSpec((count, columns), lambda j: (at, 0), **mode)
+    tall = lambda pick: pl.BlockSpec((width, part), lambda j: (0, pick(j)))
+    flat = lambda pick: pl.BlockSpec((part, width), lambda j: (pick(j), 0))
+    narrow = lambda pick: pl.BlockSpec((count, part), lambda j: (at, pick(j)))
+    again = lambda: pl.BlockSpec((slab, hidden), lambda j: (late(j), 0))
+    whole = lambda: pl.BlockSpec((count // 2, slab), lambda j: (0, late(j)))
+    held_specs = [] if held is None else [pl.BlockSpec(memory_space=pl.ANY)] * 7
+    held_args = [] if held is None else list(held)
+    base = len(pieces) + 12
+    wide = jax.ShapeDtypeStruct((all_rows, hidden), LOW)
+    out = pl.pallas_call(
+        lambda *refs: chunk_kernel(len(pieces), held is None, *refs),
+        grid=(8,),
+        in_specs=[fixed(piece) for piece in pieces]
+        + [chunk(width, pipeline_mode=once), chunk(1, pipeline_mode=once)]
+        + [tall(own), tall(other), tall(own), tall(other), flat(own), flat(other)]
+        + [again(), again(), again(), again()]
+        + held_specs,
+        out_specs=[whole(), whole(), chunk(width)] + [narrow(own), narrow(other)] * 3,
+        out_shape=[jax.ShapeDtypeStruct((count // 2, width), LOW)] * 2
+        + [jax.ShapeDtypeStruct((all_rows, width), LOW)]
+        + [wide] * 6,
+        scratch_shapes=[pltpu.VMEM((4, count, part), LOW)] * 2,
+        input_output_aliases={} if held is None else {base + k: 2 + k for k in range(7)},
+        compiler_params=pltpu.CompilerParams(vmem_limit_bytes=58 * 1024 * 1024),
+        cost_estimate=pl.CostEstimate(
+            flops=2 * 5 * count * width * hidden * 2,
+            bytes_accessed=2 * (3 * count * width + 6 * count * hidden + 6 * width * hidden),
+            transcendentals=2 * count * hidden,
+        ),
+    )(*pieces, back, gate, *mats, *mats[:4], *held_args)
+    return out[0], out[1], out[2:]
+
+
+def expert_ring(rows, back, gate, mats):
+    cut = rows.shape[0] // 2
+    same, cross = {}, {}
+    left, right = ahead(rows), behind(rows)
+    swap = lambda block: swap_bit(block, "dp", 0)
+    same[0], cross[0], held = expert_chunk([rows, swap(rows)], back, gate, mats, 6, None)
+    for hop in (1, 2, 3):
+        pieces = [left, right, swap(left), swap(right)]
+        if hop < 3:
+            left, right = ahead(left), behind(right)
+        else:
+            left, right = ahead(left[:cut]), behind(right[cut:])
+        same[hop], cross[hop], held = expert_chunk(pieces, back, gate, mats, hop - 1, held)
+    pieces = [left, right, swap(left), swap(right)]
+    same[4], cross[4], held = expert_chunk(pieces, back, gate, mats, 7, held)
+    return same, cross, held
+
+
+def halving_sum(parts):
+    bits = parts.shape[0].bit_length() - 1
+    index = lax.axis_index("dp")
+    for bit in reversed(range(bits)):
+        rows = parts.shape[0] // 2
+        upper = index >> bit & 1
+        kept = lax.dynamic_slice_in_dim(parts, upper * rows, rows, axis=0)
+        sent = lax.dynamic_slice_in_dim(parts, (1 - upper) * rows, rows, axis=0)
+        parts = kept + swap_bit(sent, "dp", bit)
+    return parts[0]
 
 
 def body(
@@ -207,7 +406,8 @@
 
     gate_mats = (w_gate[0], swap_tensor(w_gate[0]))
     up_mats = (w_up[0], swap_tensor(w_up[0]))
-    down_mats = (w_down[0], swap_tensor(w_down[0]))
+
+    ring = dp_count == 2 * len(RING)
 
     gates_high = gates.astype(LOW)
     gates_low = (gates - gates_high.astype(FULL)).astype(LOW)
@@ -217,6 +417,8 @@
     gains = jnp.pad(gains[None], ((0, 7), (0, local_width - 4 * block)))
     packed = jnp.concatenate([w_query, w_key, w_value, w_out.T, gains, routing], axis=0)
     gathered = lax.all_gather(packed, "dp", axis=0, tiled=False)
+    gathered, *early = lax.optimization_barrier((gathered, gate_mats[1], up_mats[1]))
+    gate_mats, up_mats = (gate_mats[0], early[0]), (up_mats[0], early[1])
     full_q = gathered[:, :block].reshape(model_width, local_width)
     full_k = gathered[:, block : 2 * block].reshape(model_width, local_width)
     full_v = gathered[:, 2 * block : 3 * block].reshape(model_width, local_width)
@@ -246,10 +448,14 @@
     kept = (picked > 0.0) & (within + ahead[:, None] < capacity)
     weight = jnp.where(kept, weight, 0.0)
     weight = lax.dynamic_slice_in_dim(weight, side * half_count, half_count, axis=1)
+    if ring:
+        blocks = ring_blocks(dp_index)
+        weight = weight[blocks]
     weight = weight.reshape(-1, 1)
 
     cotangent_half = own_half(cotangent)
-    back_rows = lax.all_gather(cotangent_half.astype(LOW), "dp", axis=0, tiled=True)
+    back_rows = lax.all_gather(cotangent_half.astype(LOW), "dp", axis=0, tiled=False)
+    back_rows = (back_rows[blocks] if ring else back_rows).reshape(-1, model_width)
 
     tokens_f = inputs.astype(FULL)
     prompt_pos = dp_index % GROUP * PR_DEV + jnp.arange(PR_DEV, dtype=jnp.int32)
@@ -263,6 +469,8 @@
     query_sq, key_sq = lax.psum(
         (jnp.sum(query_flat * query_flat, axis=1), jnp.sum(key_flat * key_flat, axis=1)), "tensor"
     )
+    query_sq, down_mat = lax.optimization_barrier((query_sq, w_down[0]))
+    down_mats = (down_mat, swap_tensor(down_mat))
     query_scale = lax.rsqrt(query_sq / column_total + EPSILON)[:, None]
     key_scale = lax.rsqrt(key_sq / column_total + EPSILON)[:, None]
     by_head = (token_count, local_heads, HEAD)
@@ -299,40 +507,67 @@
     context = jnp.einsum("hqk,khd->qhd", probs_b, valueset, preferred_element_type=FULL)
     context_b = context.reshape(token_count, local_width).astype(LOW)
     attn_part = dot_nt(context_b, full_o)
+    attn_part, late = lax.optimization_barrier((attn_part, down_mats[1]))
+    down_mats = (down_mats[0], late)
+    mats = (*gate_mats, *up_mats, *down_mats)
     attn_other = swap_tensor(other_half(attn_part).astype(LOW))
     hidden_state = (
         own_half(tokens_f) + own_half(attn_part) + attn_other.astype(FULL)
     )
     normed_two_b = rms_norm(hidden_state, gain_two).astype(LOW)
 
-    expert_in = lax.all_gather(normed_two_b, "dp", axis=0, tiled=True)
-    grad_rows, h0, h1, g0, g1, u0, u1 = expert_pass(
-        expert_in, back_rows, weight, gate_mats, up_mats, down_mats
-    )
-    normed_two_grad = lax.psum_scatter(grad_rows, "dp", scatter_dimension=0, tiled=True).astype(
-        FULL
-    )
-    mixed_rows = (dot_nn(h0, down_mats[0]) + dot_nn(h1, down_mats[1])).astype(LOW)
+    low_tn = lambda left, right: dot_tn(left, right).astype(LOW)
+    if ring:
+        same, cross, held = expert_ring(normed_two_b, back_rows, weight, mats)
+        expert_in, h0, h1, g0, g1, u0, u1 = held
+        down_sent = low_tn(h1, back_rows)
+        down_got = swap_tensor(down_sent)
+        normed_two_grad, outs = ring_sum(
+            same,
+            cross,
+            [
+                [(low_tn, expert_in, g1), (low_tn, expert_in, u1)],
+                [(lambda a, b: dot_nn(a, down_mats[0]) + dot_nn(b, down_mats[1]), h0, h1)],
+                [(dot_tn, h0, back_rows), (dot_tn, expert_in, g0), (dot_tn, expert_in, u0)],
+            ],
+        )
+        gate_sent, up_sent, mixed_rows, down_grad, gate_w_grad, up_w_grad = outs
+        mixed_rows = mixed_rows.astype(LOW)
+        gate_got = swap_tensor(gate_sent)
+    else:
+        expert_in = lax.all_gather(normed_two_b, "dp", axis=0, tiled=True)
+        grad_rows, h0, h1, g0, g1, u0, u1 = expert_pass(
+            expert_in, back_rows, weight, gate_mats, up_mats, down_mats
+        )
+        normed_two_grad = lax.psum_scatter(
+            grad_rows, "dp", scatter_dimension=0, tiled=True
+        ).astype(FULL)
+        mixed_rows = (dot_nn(h0, down_mats[0]) + dot_nn(h1, down_mats[1])).astype(LOW)
+        down_got = swap_tensor(low_tn(h1, back_rows))
+        gate_got = swap_tensor(low_tn(expert_in, g1))
+        up_sent = low_tn(expert_in, u1)
+        down_grad = dot_tn(h0, back_rows)
+        gate_w_grad = dot_tn(expert_in, g0)
+        up_w_grad = dot_tn(expert_in, u0)
+    normed_two_grad, down_got, gate_got, mixed_rows, down_grad, gate_w_grad, up_w_grad = together(
+        normed_two_grad, down_got, gate_got, mixed_rows, down_grad, gate_w_grad, up_w_grad
+    )
+    if ring:
+        back_to = jnp.argsort(blocks)
+        mixed_rows = mixed_rows.reshape(dp_count, half_count, model_width)[back_to].reshape(
+            -1, model_width
+        )
     mixed = lax.psum_scatter(mixed_rows, "dp", scatter_dimension=0, tiled=True).astype(FULL)
     output_half = hidden_state + mixed
-    output = both_halves(output_half, swap_tensor(output_half))
-    gate_w_grad = dot_tn(expert_in, g0) + swap_tensor(
-        dot_tn(expert_in, g1).astype(LOW)
-    ).astype(FULL)
-    up_w_grad = dot_tn(expert_in, u0) + swap_tensor(dot_tn(expert_in, u1).astype(LOW)).astype(
-        FULL
-    )
-    down_grad = dot_tn(h0, back_rows) + swap_tensor(dot_tn(h1, back_rows).astype(LOW)).astype(
-        FULL
-    )
 
     unused_two, norm_two_back = jax.vjp(rms_norm, hidden_state, gain_two)
     state_part, gain_two_grad = norm_two_back(normed_two_grad)
     state_half = cotangent_half + state_part
     attn_grad_half = state_half.astype(LOW)
     attn_grad_b = both_halves(attn_grad_half, swap_tensor(attn_grad_half))
+    attn_grad_b, up_sent = together(attn_grad_b, up_sent)
+    up_got = swap_tensor(up_sent)
     out_w_grad = dot_tn(attn_grad_b, context_b).astype(LOW)
-    out_sum = lax.psum_scatter(out_w_grad, "dp", scatter_dimension=0, tiled=True)
     context_grad_b = dot_nn(attn_grad_b, full_o).astype(LOW).reshape(by_head)
     again = masked_scores(queries_b, keyset, allowed)
     probs = jnp.exp(again - log_total)
@@ -359,6 +594,9 @@
     key_normed_grad = rotate_back(key_local.reshape(by_head), cosine, sine).reshape(
         token_count, -1
     )
+    query_normed_grad, key_normed_grad, up_got = together(
+        query_normed_grad, key_normed_grad, up_got
+    )
     query_inner, key_inner = lax.psum(
         (
             jnp.sum(query_flat * gain_query_local * query_normed_grad, axis=1),
@@ -387,9 +625,14 @@
             dot_tn(normed_b, query_pre_grad).astype(LOW).reshape(dp_count, block, local_width),
             dot_tn(normed_b, key_pre_grad).astype(LOW).reshape(dp_count, block, local_width),
             dot_tn(normed_b, value_pre_grad).astype(LOW).reshape(dp_count, block, local_width),
+            out_w_grad.reshape(dp_count, block, local_width),
         ],
         axis=1,
-    ).reshape(dp_count * 3 * block, local_width)
+    ).reshape(dp_count * 4 * block, local_width)
+    down_grad = down_grad + down_got.astype(FULL)
+    gate_w_grad = gate_w_grad + gate_got.astype(FULL)
+    up_w_grad = up_w_grad + up_got.astype(FULL)
+    output = both_halves(output_half, swap_tensor(output_half))
     w_sum = lax.psum_scatter(w_grads, "dp", scatter_dimension=0, tiled=True).astype(FULL)
     normed_part = (
         dot_nt(query_pre_grad, full_q)
@@ -405,18 +648,18 @@
     gain_grads = jnp.stack(
         [gain_one_grad, gain_two_grad, wide(query_gain_part), wide(key_gain_part)]
     ).reshape(4, dp_count, block)
-    gain_sums = lax.psum_scatter(gain_grads, "dp", scatter_dimension=1, tiled=True)
-    gain_sums = lax.psum(gain_sums.reshape(4, block), "tensor")
+    gain_sums = halving_sum(jnp.swapaxes(gain_grads, 0, 1))
+    gain_sums = gain_sums + swap_tensor(gain_sums)
     return (
         output,
         input_grad,
         gain_sums[0],
         w_sum[:block],
         w_sum[block : 2 * block],
-        w_sum[2 * block :],
+        w_sum[2 * block : 3 * block],
         gain_sums[2],
         gain_sums[3],
-        out_sum.astype(FULL).T,
+        w_sum[3 * block :].T,
         gain_sums[1],
         gate_w_grad[None],
         up_w_grad[None],

time: 990 us -> 1020 us (1.030)
  local copies, waits for them, and re-layouts: 82.7 us -> 174 us
  waiting for transfers between devices: 502 us -> 438 us
  blocking collectives: 74.2 us -> 10.4 us
  Pallas kernels: 66.7 us -> 106 us
  starting transfers between devices: 26.2 us -> 46.9 us
  other arithmetic: 65.7 us -> 85.8 us
  matrix products: 151 us -> 136 us
    reduce_scatter x1, waiting for transfers between devices: 0.01 us -> 119 us  [body(): lax.psum_scatter(mixed_rows, 'dp', scatter_dimension=0, tiled=True)]
    ppermute x11 -> x12, waiting for transfers between devices: 263 us -> 149 us  [swap_tensor(): return lax.ppermute(block, 'tensor', [(0, 1), (1, 0)])]
    reduce_scatter x2 -> x0, waiting for transfers between devices: 90.4 us -> none  [the longest x1 90.4 us: body(): lax.psum_scatter(grad_rows, 'dp', scatter_dimension=0, tiled=True)]
    reduce_scatter x1, waiting for transfers between devices: 0.01 us -> 88.8 us  [body(): lax.psum_scatter(w_grads, 'dp', scatter_dimension=0, tiled=True)]
    all_gather x1, waiting for transfers between devices: 87.5 us -> 0.63 us  [body(): gathered = lax.all_gather(packed, 'dp', axis=0, tiled=False)]
    unnamed x1 -> x0, blocking collectives: 58.6 us -> none
    pallas_call x1 -> x5, Pallas kernels: 66.7 us -> 106 us  [expert_chunk(): pl.pallas_call(lambda *refs: chunk_kernel(len(pieces), held is None, *ref...]
    reshape x1, local copies, waits for them, and re-layouts: 0.65 us -> 27.7 us  [body(): w_grads = jnp.stack([dot_tn(normed_b, query_pre_grad).astype(LOW).reshape...]
  transfers between devices with their start and end apart: 32 -> 64, of which waited for: 16 -> 23; matrix products, arithmetic and copies ran while one was open for 27% -> 23% of each run, Pallas kernels for 0% -> 10%
where the time goes in v2:
time: 1020 us; the launch traced here: 1010 us
  waiting for transfers between devices  438 us (43%)
  local copies, waits for them, and re-layouts  174 us (17%)
  matrix products  136 us (13%)
  Pallas kernels  106 us (10%)
  other arithmetic  85.8 us (8%)
  starting transfers between devices  46.9 us (5%)
  between operations  16.6 us (2%)
  blocking collectives  10.4 us (1%)
    ppermute x12, waiting for transfers between devices, swap_tensor(): return lax.ppermute(block, 'tensor', [(0, 1), (1, 0)])  149 us
    reduce_scatter x1, waiting for transfers between devices, body(): lax.psum_scatter(mixed_rows, 'dp', scatter_dimension=0, tiled=True)  119 us
    pallas_call x5, Pallas kernels, expert_chunk(): pl.pallas_call(lambda *refs: chunk_kernel(len(pieces), held is None, *ref...  106 us
    reduce_scatter x1, waiting for transfers between devices, body(): lax.psum_scatter(w_grads, 'dp', scatter_dimension=0, tiled=True)  88.8 us
    dot_general x10, matrix products, dot_tn(): lax.dot_general(left, right, (((0,), (0,)), ((), ())), preferred_element_...  67.6 us
    ppermute x32, waiting for transfers between devices, swap_bit(): return lax.ppermute(block, axis, [(i, i ^ 1 << bit) for i in range(count)])  61.1 us
    unnamed x337, local copies, waits for them, and re-layouts  40.8 us
    dot_general x7, matrix products, dot_nn(): return jnp.dot(left, right, preferred_element_type=FULL)  34.2 us
  transfers between devices with their start and end apart: 64, of which 23 were waited for; matrix products, arithmetic and copies ran while one was open for 23% of the time, Pallas kernels for 10%

profile of v2, /device:TPU:0, one launch (start us, length us, event | category | flops | bytes accessed | tf_op | source)
XLA Modules:
  0.0 1013.1 jit_solution(9719744045730070763)
XLA Ops:
  14.8 3.0 collective-permute-start
  17.9 2.3 dynamic-slice_convert_fusion.2
  24.3 40.1 %collective-permute-done.refs_5_.refs_11_.refs_7_.refs_13_ = bf16[2048,512]{1,0:T(8,128)(2,1)} collective-permute-done((bf16[2048,512]{1,0:T(8,128)(2,1)S(1)}, bf16[2048,512]{1,0:T(8,128)(2,1)}, u32[]{:S(2)}, u32[]{:S(2)}) %collective-permute-start) | collective-permute-done | bytes 2097184 | tf_op jit(solution)/shard_map/ppermute | solution.py:25
  64.4 44.1 %collective-permute-done.1.refs_7_.refs_13_.refs_9_.refs_15_ = bf16[2048,512]{1,0:T(8,128)(2,1)} collective-permute-done((bf16[2048,512]{1,0:T(8,128)(2,1)}, bf16[2048,512]{1,0:T(8,128)(2,1)}, u32[]{:S(2)}, u32[]{:S(2)}) %collective-permute-start.1) | collective-permute-done | bytes 2097184 | tf_op jit(solution)/shard_map/ppermute | solution.py:25
  110.8 9.6 fusion.71
  125.5 5.5 all-reduce.4
  136.4 4.2 convolution_convert_fusion.9
  148.2 13.4 %collective-permute-done.3 = bf16[2,128,1024]{2,1,0:T(8,128)(2,1)} collective-permute-done((bf16[2,128,1024]{2,1,0:T(8,128)(2,1)}, bf16[2,128,1024]{2,1,0:T(8,128)(2,1)}, u32[]{:S(2)}, u32[]{:S(2)}) %collective-permute-start.3) | collective-permute-done | bytes 524320 | tf_op jit(solution)/shard_map/ppermute | solution.py:21
  162.9 15.1 %collective-permute-done.5 = bf16[2,128,1024]{2,1,0:T(8,128)(2,1)S(1)} collective-permute-done((bf16[2,128,1024]{2,1,0:T(8,128)(2,1)}, bf16[2,128,1024]{2,1,0:T(8,128)(2,1)S(1)}, u32[]{:S(2)}, u32[]{:S(2)}) %collective-permute-start.5) | collective-permute-done | bytes 524320 | tf_op jit(solution)/shard_map/ppermute | solution.py:21
  179.4 10.7 %collective-permute-done.8 = bf16[128,1024]{1,0:T(8,128)(2,1)S(1)} collective-permute-done((bf16[128,1024]{1,0:T(8,128)(2,1)S(1)}, bf16[128,1024]{1,0:T(8,128)(2,1)S(1)}, u32[]{:S(2)}, u32[]{:S(2)}) %collective-permute-start.8) | collective-permute-done | bytes 262176 | tf_op jit(solution)/shard_map/ppermute | solution.py:21
  195.9 4.4 fusion.82
  202.3 2.7 copy-done
  205.1 2.4 divide_convert_fusion
  219.5 14.3 %collective-permute-done.11 = bf16[160,2048]{1,0:T(8,128)(2,1)S(1)} collective-permute-done((bf16[160,2048]{1,0:T(8,128)(2,1)}, bf16[160,2048]{1,0:T(8,128)(2,1)S(1)}, u32[]{:S(2)}, u32[]{:S(2)}) %collective-permute-start.11) | collective-permute-done | bytes 655392 | tf_op jit(solution)/shard_map/ppermute | solution.py:25
  233.8 2.2 multiply_reduce_fusion.11
  239.9 9.7 gather_fusion
  251.1 2.6 collective-permute-done.14.refs_0_
  256.7 2.3 reshape.369.refs_3_.refs_5_
  259.0 16.9 %shard_map.282 = (bf16[160,2048]{1,0:T(8,128)(2,1)}, bf16[160,2048]{1,0:T(8,128)(2,1)}, bf16[2560,2048]{1,0:T(8,128)(2,1)}, bf16[2560,512]{1,0:T(8,128)(2,1)}, b...) custom-call(bf16[160,2048]{1,0:T(8,128)(2,1)} %copy-done.52, ...), custom_call_target="tpu_custom_call" | custom-call | flops 6710886400 | bytes 18481152 | tf_op jit(solution)/shard_map/pallas_call | solution.py:308
  278.5 24.0 %shard_map.283 = (bf16[320,2048]{1,0:T(8,128)(2,1)}, bf16[320,2048]{1,0:T(8,128)(2,1)}, bf16[2560,2048]{1,0:T(8,128)(2,1)}, bf16[2560,512]{1,0:T(8,128)(2,1)}, b...) custom-call(bf16[160,2048]{1,0:T(8,128)(2,1)} %copy-done.77, ...), custom_call_target="tpu_custom_call", output_to_operand_aliasing={{2}: (16, {}), {3}: (17, {}), {4}: (18, {}), {5}: (19, {}),... | custom-call | flops 13421772800 | bytes 24379392 | tf_op jit(solution)/shard_map/pallas_call | solution.py:308
  306.6 24.4 %shard_map.284 = (bf16[320,2048]{1,0:T(8,128)(2,1)}, bf16[320,2048]{1,0:T(8,128)(2,1)}, bf16[2560,2048]{1,0:T(8,128)(2,1)}, bf16[2560,512]{1,0:T(8,128)(2,1)}, b...) custom-call(bf16[160,2048]{1,0:T(8,128)(2,1)} %copy-done.75, ...), custom_call_target="tpu_custom_call", output_to_operand_aliasing={{2}: (16, {}), {3}: (17, {}), {4}: (18, {}), {5}: (19, {}),... | custom-call | flops 13421772800 | bytes 24379392 | tf_op jit(solution)/shard_map/pallas_call | solution.py:308
  332.8 24.0 %shard_map.285 = (bf16[320,2048]{1,0:T(8,128)(2,1)}, bf16[320,2048]{1,0:T(8,128)(2,1)}, bf16[2560,2048]{1,0:T(8,128)(2,1)}, bf16[2560,512]{1,0:T(8,128)(2,1)}, b...) custom-call(bf16[160,2048]{1,0:T(8,128)(2,1)} %copy-done.60, ...), custom_call_target="tpu_custom_call", output_to_operand_aliasing={{2}: (16, {}), {3}: (17, {}), {4}: (18, {}), {5}: (19, {}),... | custom-call | flops 13421772800 | bytes 24379392 | tf_op jit(solution)/shard_map/pallas_call | solution.py:308
  357.9 16.9 %shard_map.286 = (bf16[160,2048]{1,0:T(8,128)(2,1)}, bf16[160,2048]{1,0:T(8,128)(2,1)}, bf16[2560,2048]{1,0:T(8,128)(2,1)}, bf16[2560,512]{1,0:T(8,128)(2,1)}, b...) custom-call(bf16[80,2048]{1,0:T(8,128)(2,1)} %copy-done.91, ...), custom_call_target="tpu_custom_call", output_to_operand_aliasing={{2}: (16, {}), {3}: (17, {}), {4}: (18, {}), {5}: (19, {}),... | custom-call | flops 6710886400 | bytes 18481152 | tf_op jit(solution)/shard_map/pallas_call | solution.py:308
  375.1 10.3 %convolution_convert_fusion.6 = bf16[512,2048]{1,0:T(8,128)(2,1)} fusion(bf16[2560,512]{1,0:T(8,128)(2,1)} %get-tuple-element.157, bf16[2560,2048]{1,0:T(8,128)(2,1)} %bitcast.315), kind=kOutput, calls=%fused_computation.23 | convolution fusion | flops 5369757696 | bytes 15204352 | tf_op jit(solution)/shard_map/dot_general | solution.py:142
  390.4 8.9 collective-permute-done.38
  402.3 6.8 convolution_convert_fusion.5
  410.0 7.3 collective-permute-done.39
  419.9 12.0 %fusion.85 = f32[2560,2048]{1,0:T(8,128)} fusion(bf16[2560,512]{1,0:T(8,128)(2,1)S(1)} %copy-done.4, bf16[512,2048]{1,0:T(8,128)(2,1)} %collective-permute-done.10.refs_9_.refs_11_), kind=kOutput, calls=%fused_computation.319 | convolution fusion | flops 5368709120 | bytes 25690112 | tf_op jit(solution)/shard_map/dot_general | solution.py:138
  431.9 12.9 %add_convert_fusion = bf16[2560,2048]{1,0:T(8,128)(2,1)} fusion(f32[2560,2048]{1,0:T(8,128)} %fusion.85, bf16[2560,512]{1,0:T(8,128)(2,1)S(1)} %copy-done.3, bf16[512,2048]{1,0:T(8,128)(2,1)} %bitcast.19.refs_8_.refs_10_), kind=kOutput, calls=%fused_computation.3 | convolution fusion | flops 5379194880 | bytes 36175872 | tf_op jit(solution)/shard_map/dot_general | solution.py:138
  447.4 10.4 %fusion.87 = f32[2048,512]{1,0:T(8,128)} fusion(bf16[2560,2048]{1,0:T(8,128)(2,1)} %get-tuple-element.167, bf16[2560,512]{1,0:T(8,128)(2,1)S(1)} %copy-done.5), kind=kOutput, calls=%fused_computation.321 | convolution fusion | flops 5368709120 | bytes 17301504 | tf_op jit(solution)/shard_map/dot_general | solution.py:142
  457.8 7.2 fusion.88
  465.0 7.2 fusion.86
  473.8 4.6 collective-permute-done.43
  478.4 9.8 gather_fusion.2
  490.0 118.8 %reduce-scatter.3.cloned.1.call-done = bf16[160,2048]{1,0:T(8,128)(2,1)} async-done(((bf16[2560,2048]{1,0:T(8,128)(2,1)}), bf16[160,2048]{1,0:T(8,128)(2,1)}) %reduce-scatter.3.cloned.1.call-update) | async-done | bytes 655376 | tf_op jit(solution)/shard_map/reduce_scatter | solution.py:560
  608.8 4.2 fusion.68
  614.5 12.0 %convolution_convert_fusion.4 = bf16[2048,512]{1,0:T(8,128)(2,1)} fusion(bf16[2560,2048]{1,0:T(8,128)(2,1)} %get-tuple-element.167, bf16[2560,512]{1,0:T(8,128)(2,1)S(1)} %copy-done.8), kind=kOutput, calls=%fused_computation.21 | convolution fusion | flops 5369757696 | bytes 15204352 | tf_op jit(solution)/shard_map/dot_general | solution.py:142
  626.4 2.9 collective-permute-done.45
  632.7 4.2 fusion.84
  636.9 8.4 multiply_reduce_fusion
  645.3 6.8 multiply_convert_fusion
  652.1 3.9 fusion.83
  656.0 2.3 copy-done.18
  672.0 2.3 pad_maximum_fusion.4
  676.8 2.7 fusion.72
  689.7 2.4 pad_maximum_fusion.5
  694.6 4.7 broadcast_multiply_fusion
  700.8 4.4 convolution_convert_fusion
  712.4 8.3 collective-permute-done.47
  739.9 4.5 convolution_convert_fusion.1
  746.1 4.9 all-reduce.3
  752.8 2.5 convolution_convert_fusion.2
  755.7 2.5 convolution_convert_fusion.3
  759.1 7.2 pad_maximum_fusion
  766.3 28.6 %copy.216 = bf16[16,4,128,1024]{2,1,0,3:T(4,128)(2,1)} copy(bf16[16,4,128,1024]{3,2,0,1:T(8,128)(2,1)} %pad_maximum_fusion) | data formatting | bytes 33554432 | tf_op jit(solution)/shard_map/stack | solution.py:623
  794.9 27.7 %reshape.332 = bf16[8192,1024]{0,1:T(8,128)(2,1)} reshape(bf16[16,4,128,1024]{2,1,0,3:T(4,128)(2,1)} %copy.216) | data formatting | bytes 33554432 | tf_op jit(solution)/shard_map/reshape | solution.py:631
  823.2 5.7 add_bitcast_fusion.2
  838.2 5.2 add_bitcast_fusion
  843.4 28.1 %collective-permute-done.53 = bf16[160,2048]{1,0:T(8,128)(2,1)S(1)} collective-permute-done((bf16[160,2048]{1,0:T(8,128)(2,1)S(1)}, bf16[160,2048]{1,0:T(8,128)(2,1)S(1)}, u32[]{:S(2)}, u32[]{:S(2)}) %collective-permute-start.53) | collective-permute-done | bytes 655392 | tf_op jit(solution)/shard_map/ppermute | solution.py:25
  874.0 4.8 collective-permute-done.55
  878.8 4.1 collective-permute-done.56
  889.8 4.4 add_bitcast_fusion.1
  894.2 15.3 %collective-permute-done.59 = f32[4,128]{1,0:T(4,128)S(1)} collective-permute-done((f32[4,128]{1,0:T(4,128)S(1)}, f32[4,128]{1,0:T(4,128)S(1)}, u32[]{:S(2)}, u32[]{:S(2)}) %collective-permute-start.59) | collective-permute-done | bytes 2080 | tf_op jit(solution)/shard_map/ppermute | solution.py:25
  912.0 88.8 %reduce-scatter.5.cloned.1.call-done = bf16[512,1024]{0,1:T(8,128)(2,1)} async-done(((bf16[8192,1024]{0,1:T(8,128)(2,1)}), bf16[512,1024]{0,1:T(8,128)(2,1)}) %reduce-scatter.5.cloned.1.call-update) | async-done | bytes 1048592 | tf_op jit(solution)/shard_map/reduce_scatter | solution.py:636
  (609 shorter events, 182.0 us)
Async XLA Ops:
  7.2 102.0 %all-gather.5.cloned.1.call-start = ((), (), s32[]{:S(2)}) async-start(), calls=%async_computation.4 | async-start | bytes 18382848 | tf_op jit(solution)/shard_map/all_gather | solution.py:419
  14.8 225.2 %all-gather.7.cloned.1.call-start = ((), (), s32[]{:S(2)}) async-start(), calls=%async_computation.5 | async-start | bytes 11141120 | tf_op jit(solution)/shard_map/all_gather | solution.py:457
  14.8 49.6 %collective-permute-start = (bf16[2048,512]{1,0:T(8,128)(2,1)S(1)}, bf16[2048,512]{1,0:T(8,128)(2,1)}, u32[]{:S(2)}, u32[]{:S(2)}) collective-permute-start(bf16[2048,512]{1,0:T(8,128)(2,1)S(1)} %bitcast.331), channel_id=1, source_target_pairs={{0,1},{1,0},{2,3},{3,2},{4,5},{5,4},{6,7},{7,6},{8,9},{9,8},{10,11... | collective-permute-start | bytes 6291464 | tf_op jit(solution)/shard_map/ppermute | solution.py:25
  17.9 90.7 %collective-permute-start.1 = (bf16[2048,512]{1,0:T(8,128)(2,1)}, bf16[2048,512]{1,0:T(8,128)(2,1)}, u32[]{:S(2)}, u32[]{:S(2)}) collective-permute-start(bf16[2048,512]{1,0:T(8,128)(2,1)} %bitcast.332), channel_id=1, source_target_pairs={{0,1},{1,0},{2,3},{3,2},{4,5},{5,4},{6,7},{7,6},{8,9},{9,8},{10,11... | collective-permute-start | bytes 6291464 | tf_op jit(solution)/shard_map/ppermute | solution.py:25
  20.2 588.6 %reduce-scatter.3.cloned.1.call-start = ((), (), s32[]{:S(2)}) async-start(), calls=%async_computation.2 | async-start | bytes 11141120 | tf_op jit(solution)/shard_map/reduce_scatter | solution.py:560
  141.7 5.5 collective-permute-start.2
  141.8 19.9 %collective-permute-start.3 = (bf16[2,128,1024]{2,1,0:T(8,128)(2,1)}, bf16[2,128,1024]{2,1,0:T(8,128)(2,1)}, u32[]{:S(2)}, u32[]{:S(2)}) collective-permute-start(bf16[2,128,1024]{2,1,0:T(8,128)(2,1)} %pad_maximum_fusion.9), channel_id=1, source_target_pairs={{0,4},{2,6},{4,0},{6,2},{8,12},{10,14},{12,8},{14,10},{16,20},{18,... | collective-permute-start | bytes 1572872 | tf_op jit(solution)/shard_map/ppermute | solution.py:21
  144.0 34.0 %collective-permute-start.5 = (bf16[2,128,1024]{2,1,0:T(8,128)(2,1)}, bf16[2,128,1024]{2,1,0:T(8,128)(2,1)S(1)}, u32[]{:S(2)}, u32[]{:S(2)}) collective-permute-start(bf16[2,128,1024]{2,1,0:T(8,128)(2,1)} %pad_maximum_fusion.9), channel_id=1, source_target_pairs={{0,8},{2,10},{4,12},{6,14},{8,0},{10,2},{12,4},{14,6},{16,24},{18,... | collective-permute-start | bytes 1572872 | tf_op jit(solution)/shard_map/ppermute | solution.py:21
  145.6 69.1 %collective-permute-start.10 = (bf16[512,2048]{1,0:T(8,128)(2,1)}, bf16[512,2048]{1,0:T(8,128)(2,1)}, u32[]{:S(2)}, u32[]{:S(2)}) collective-permute-start(bf16[512,2048]{1,0:T(8,128)(2,1)} %bitcast.19.refs_8_.refs_10_), channel_id=1, source_target_pairs={{0,1},{1,0},{2,3},{3,2},{4,5},{5,4},{6,7},{7,6},{8,9},{9,8},{10,11... | collective-permute-start | bytes 6291464 | tf_op jit(solution)/shard_map/ppermute | solution.py:25
  178.1 12.0 %collective-permute-start.8 = (bf16[128,1024]{1,0:T(8,128)(2,1)S(1)}, bf16[128,1024]{1,0:T(8,128)(2,1)S(1)}, u32[]{:S(2)}, u32[]{:S(2)}) collective-permute-start(bf16[128,1024]{1,0:T(8,128)(2,1)S(1)} %get-tuple-element.303), channel_id=1, source_target_pairs={{0,4},{2,6},{4,0},{6,2},{8,12},{10,14},{12,8},{14,10},{16,20},{18,... | collective-permute-start | bytes 786440 | tf_op jit(solution)/shard_map/ppermute | solution.py:21
  178.2 13.8 %collective-permute-start.7 = (bf16[128,1024]{1,0:T(8,128)(2,1)S(1)}, bf16[128,1024]{1,0:T(8,128)(2,1)S(1)}, u32[]{:S(2)}, u32[]{:S(2)}) collective-permute-start(bf16[128,1024]{1,0:T(8,128)(2,1)S(1)} %get-tuple-element.307), channel_id=1, source_target_pairs={{0,8},{2,10},{4,12},{6,14},{8,0},{10,2},{12,4},{14,6},{16,24},{18,... | collective-permute-start | bytes 786440 | tf_op jit(solution)/shard_map/ppermute | solution.py:21
  178.3 13.8 %collective-permute-start.4 = (bf16[2,128,1024]{2,1,0:T(8,128)(2,1)}, bf16[2,128,1024]{2,1,0:T(8,128)(2,1)S(1)}, u32[]{:S(2)}, u32[]{:S(2)}) collective-permute-start(bf16[2,128,1024]{2,1,0:T(8,128)(2,1)} %collective-permute-done.3), channel_id=1, source_target_pairs={{0,2},{2,0},{4,6},{6,4},{8,10},{10,8},{12,14},{14,12},{16,18},{18,... | collective-permute-start | bytes 1572872 | tf_op jit(solution)/shard_map/ppermute | solution.py:21
  178.8 13.5 %collective-permute-start.6 = (bf16[2,128,1024]{2,1,0:T(8,128)(2,1)S(1)}, bf16[2,128,1024]{2,1,0:T(8,128)(2,1)S(1)}, u32[]{:S(2)}, u32[]{:S(2)}) collective-permute-start(bf16[2,128,1024]{2,1,0:T(8,128)(2,1)S(1)} %collective-permute-done.5), channel_id=1, source_target_pairs={{0,2},{2,0},{4,6},{6,4},{8,10},{10,8},{12,14},{14,12},{16,18},{18,... | collective-permute-start | bytes 1572872 | tf_op jit(solution)/shard_map/ppermute | solution.py:21
  192.1 2.0 collective-permute-start.9
  216.3 17.4 %collective-permute-start.11 = (bf16[160,2048]{1,0:T(8,128)(2,1)}, bf16[160,2048]{1,0:T(8,128)(2,1)S(1)}, u32[]{:S(2)}, u32[]{:S(2)}) collective-permute-start(bf16[160,2048]{1,0:T(8,128)(2,1)} %dynamic-slice_convert_fusion.1), channel_id=1, source_target_pairs={{0,1},{1,0},{2,3},{3,2},{4,5},{5,4},{6,7},{7,6},{8,9},{9,8},{10,11... | collective-permute-start | bytes 1966088 | tf_op jit(solution)/shard_map/ppermute | solution.py:25
  237.3 16.5 %collective-permute-start.14 = (bf16[160,2048]{1,0:T(8,128)(2,1)S(1)}, bf16[160,2048]{1,0:T(8,128)(2,1)S(1)}, u32[]{:S(2)}, u32[]{:S(2)}) collective-permute-start(bf16[160,2048]{1,0:T(8,128)(2,1)S(1)} %multiply_convert_fusion.2.refs_0_), channel_id=1, source_target_pairs={{0,8},{2,10},{8,16},{10,18},{16,24},{18,26},{24,28},{26,30},{28,20... | collective-permute-start | bytes 1966088 | tf_op jit(solution)/shard_map/ppermute | solution.py:36
  237.3 17.7 %collective-permute-start.15 = (bf16[160,2048]{1,0:T(8,128)(2,1)S(1)}, bf16[160,2048]{1,0:T(8,128)(2,1)S(1)}, u32[]{:S(2)}, u32[]{:S(2)}) collective-permute-start(bf16[160,2048]{1,0:T(8,128)(2,1)S(1)} %multiply_convert_fusion.2.refs_0_), channel_id=1, source_target_pairs={{8,0},{10,2},{16,8},{18,10},{24,16},{26,18},{28,24},{30,26},{20,28... | collective-permute-start | bytes 1966088 | tf_op jit(solution)/shard_map/ppermute | solution.py:40
  249.6 9.3 collective-permute-start.12
  253.8 22.5 %collective-permute-start.19 = (bf16[160,2048]{1,0:T(8,128)(2,1)S(1)}, bf16[160,2048]{1,0:T(8,128)(2,1)S(1)}, u32[]{:S(2)}, u32[]{:S(2)}) collective-permute-start(bf16[160,2048]{1,0:T(8,128)(2,1)S(1)} %collective-permute-done.14.refs_0_), channel_id=1, source_target_pairs={{0,8},{2,10},{8,16},{10,18},{16,24},{18,26},{24,28},{26,30},{28,20... | collective-permute-start | bytes 1966088 | tf_op jit(solution)/shard_map/ppermute | solution.py:36
  254.6 23.2 %collective-permute-start.16 = (bf16[160,2048]{1,0:T(8,128)(2,1)S(1)}, bf16[160,2048]{1,0:T(8,128)(2,1)}, u32[]{:S(2)}, u32[]{:S(2)}) collective-permute-start(bf16[160,2048]{1,0:T(8,128)(2,1)S(1)} %collective-permute-done.14.refs_0_), channel_id=1, source_target_pairs={{0,2},{2,0},{4,6},{6,4},{8,10},{10,8},{12,14},{14,12},{16,18},{18,... | collective-permute-start | bytes 1966088 | tf_op jit(solution)/shard_map/ppermute | solution.py:21
  255.1 22.7 %collective-permute-start.20 = (bf16[160,2048]{1,0:T(8,128)(2,1)S(1)}, bf16[160,2048]{1,0:T(8,128)(2,1)S(1)}, u32[]{:S(2)}, u32[]{:S(2)}) collective-permute-start(bf16[160,2048]{1,0:T(8,128)(2,1)S(1)} %collective-permute-done.15.refs_1_), channel_id=1, source_target_pairs={{8,0},{10,2},{16,8},{18,10},{24,16},{26,18},{28,24},{30,26},{20,28... | collective-permute-start | bytes 1966088 | tf_op jit(solution)/shard_map/ppermute | solution.py:40
  255.9 22.5 %collective-permute-start.17 = (bf16[160,2048]{1,0:T(8,128)(2,1)S(1)}, bf16[160,2048]{1,0:T(8,128)(2,1)}, u32[]{:S(2)}, u32[]{:S(2)}) collective-permute-start(bf16[160,2048]{1,0:T(8,128)(2,1)S(1)} %collective-permute-done.15.refs_1_), channel_id=1, source_target_pairs={{0,2},{2,0},{4,6},{6,4},{8,10},{10,8},{12,14},{14,12},{16,18},{18,... | collective-permute-start | bytes 1966088 | tf_op jit(solution)/shard_map/ppermute | solution.py:21
  275.9 196.4 %collective-permute-start.13 = (bf16[160,2048]{1,0:T(8,128)(2,1)}, bf16[160,2048]{1,0:T(8,128)(2,1)}, u32[]{:S(2)}, u32[]{:S(2)}) collective-permute-start(bf16[160,2048]{1,0:T(8,128)(2,1)} %get-tuple-element.104), channel_id=1, source_target_pairs={{0,2},{2,0},{4,6},{6,4},{8,10},{10,8},{12,14},{14,12},{16,18},{18,... | collective-permute-start | bytes 1966088 | tf_op jit(solution)/shard_map/ppermute | solution.py:21
  276.3 26.3 %collective-permute-start.24 = (bf16[160,2048]{1,0:T(8,128)(2,1)S(1)}, bf16[160,2048]{1,0:T(8,128)(2,1)S(1)}, u32[]{:S(2)}, u32[]{:S(2)}) collective-permute-start(bf16[160,2048]{1,0:T(8,128)(2,1)S(1)} %collective-permute-done.19.refs_0_), channel_id=1, source_target_pairs={{0,8},{2,10},{8,16},{10,18},{16,24},{18,26},{24,28},{26,30},{28,20... | collective-permute-start | bytes 1966088 | tf_op jit(solution)/shard_map/ppermute | solution.py:36
  277.8 27.7 %collective-permute-start.21 = (bf16[160,2048]{1,0:T(8,128)(2,1)S(1)}, bf16[160,2048]{1,0:T(8,128)(2,1)S(1)}, u32[]{:S(2)}, u32[]{:S(2)}) collective-permute-start(bf16[160,2048]{1,0:T(8,128)(2,1)S(1)} %collective-permute-done.19.refs_0_), channel_id=1, source_target_pairs={{0,2},{2,0},{4,6},{6,4},{8,10},{10,8},{12,14},{14,12},{16,18},{18,... | collective-permute-start | bytes 1966088 | tf_op jit(solution)/shard_map/ppermute | solution.py:21
  277.8 26.8 %collective-permute-start.25 = (bf16[160,2048]{1,0:T(8,128)(2,1)S(1)}, bf16[160,2048]{1,0:T(8,128)(2,1)S(1)}, u32[]{:S(2)}, u32[]{:S(2)}) collective-permute-start(bf16[160,2048]{1,0:T(8,128)(2,1)S(1)} %collective-permute-done.20.refs_1_), channel_id=1, source_target_pairs={{8,0},{10,2},{16,8},{18,10},{24,16},{26,18},{28,24},{30,26},{20,28... | collective-permute-start | bytes 1966088 | tf_op jit(solution)/shard_map/ppermute | solution.py:40
  278.4 27.2 %collective-permute-start.22 = (bf16[160,2048]{1,0:T(8,128)(2,1)S(1)}, bf16[160,2048]{1,0:T(8,128)(2,1)S(1)}, u32[]{:S(2)}, u32[]{:S(2)}) collective-permute-start(bf16[160,2048]{1,0:T(8,128)(2,1)S(1)} %collective-permute-done.20.refs_1_), channel_id=1, source_target_pairs={{0,2},{2,0},{4,6},{6,4},{8,10},{10,8},{12,14},{14,12},{16,18},{18,... | collective-permute-start | bytes 1966088 | tf_op jit(solution)/shard_map/ppermute | solution.py:21
  302.6 28.4 %collective-permute-start.29 = (bf16[80,2048]{1,0:T(8,128)(2,1)S(1)}, bf16[80,2048]{1,0:T(8,128)(2,1)S(1)}, u32[]{:S(2)}, u32[]{:S(2)}) collective-permute-start(bf16[80,2048]{1,0:T(8,128)(2,1)S(1)} %slice.436), channel_id=1, source_target_pairs={{0,8},{2,10},{8,16},{10,18},{16,24},{18,26},{24,28},{26,30},{28,20... | collective-permute-start | bytes 983048 | tf_op jit(solution)/shard_map/ppermute | solution.py:36
  305.4 25.9 %collective-permute-start.30 = (bf16[80,2048]{1,0:T(8,128)(2,1)}, bf16[80,2048]{1,0:T(8,128)(2,1)S(1)}, u32[]{:S(2)}, u32[]{:S(2)}) collective-permute-start(bf16[80,2048]{1,0:T(8,128)(2,1)} %slice.437), channel_id=1, source_target_pairs={{8,0},{10,2},{16,8},{18,10},{24,16},{26,18},{28,24},{30,26},{20,28... | collective-permute-start | bytes 983048 | tf_op jit(solution)/shard_map/ppermute | solution.py:40
  305.5 26.1 %collective-permute-start.26 = (bf16[160,2048]{1,0:T(8,128)(2,1)S(1)}, bf16[160,2048]{1,0:T(8,128)(2,1)S(1)}, u32[]{:S(2)}, u32[]{:S(2)}) collective-permute-start(bf16[160,2048]{1,0:T(8,128)(2,1)S(1)} %collective-permute-done.24.refs_0_), channel_id=1, source_target_pairs={{0,2},{2,0},{4,6},{6,4},{8,10},{10,8},{12,14},{14,12},{16,18},{18,... | collective-permute-start | bytes 1966088 | tf_op jit(solution)/shard_map/ppermute | solution.py:21
  305.5 26.4 %collective-permute-start.27 = (bf16[160,2048]{1,0:T(8,128)(2,1)S(1)}, bf16[160,2048]{1,0:T(8,128)(2,1)S(1)}, u32[]{:S(2)}, u32[]{:S(2)}) collective-permute-start(bf16[160,2048]{1,0:T(8,128)(2,1)S(1)} %collective-permute-done.25.refs_1_), channel_id=1, source_target_pairs={{0,2},{2,0},{4,6},{6,4},{8,10},{10,8},{12,14},{14,12},{16,18},{18,... | collective-permute-start | bytes 1966088 | tf_op jit(solution)/shard_map/ppermute | solution.py:21
  331.0 54.3 %collective-permute-start.18 = (bf16[320,2048]{1,0:T(8,128)(2,1)}, bf16[320,2048]{1,0:T(8,128)(2,1)S(1)}, u32[]{:S(2)}, u32[]{:S(2)}) collective-permute-start(bf16[320,2048]{1,0:T(8,128)(2,1)} %get-tuple-element.113), channel_id=1, source_target_pairs={{0,2},{2,0},{4,6},{6,4},{8,10},{10,8},{12,14},{14,12},{16,18},{18,... | collective-permute-start | bytes 3932168 | tf_op jit(solution)/shard_map/ppermute | solution.py:21
  331.4 58.4 %collective-permute-start.23 = (bf16[320,2048]{1,0:T(8,128)(2,1)}, bf16[320,2048]{1,0:T(8,128)(2,1)S(1)}, u32[]{:S(2)}, u32[]{:S(2)}) collective-permute-start(bf16[320,2048]{1,0:T(8,128)(2,1)} %get-tuple-element.122), channel_id=1, source_target_pairs={{0,2},{2,0},{4,6},{6,4},{8,10},{10,8},{12,14},{14,12},{16,18},{18,... | collective-permute-start | bytes 3932168 | tf_op jit(solution)/shard_map/ppermute | solution.py:21
  331.6 25.2 %collective-permute-start.31 = (bf16[80,2048]{1,0:T(8,128)(2,1)S(1)}, bf16[80,2048]{1,0:T(8,128)(2,1)S(1)}, u32[]{:S(2)}, u32[]{:S(2)}) collective-permute-start(bf16[80,2048]{1,0:T(8,128)(2,1)S(1)} %collective-permute-done.29.refs_0_), channel_id=1, source_target_pairs={{0,2},{2,0},{4,6},{6,4},{8,10},{10,8},{12,14},{14,12},{16,18},{18,... | collective-permute-start | bytes 983048 | tf_op jit(solution)/shard_map/ppermute | solution.py:21
  331.9 25.3 %collective-permute-start.32 = (bf16[80,2048]{1,0:T(8,128)(2,1)S(1)}, bf16[80,2048]{1,0:T(8,128)(2,1)S(1)}, u32[]{:S(2)}, u32[]{:S(2)}) collective-permute-start(bf16[80,2048]{1,0:T(8,128)(2,1)S(1)} %collective-permute-done.30.refs_1_), channel_id=1, source_target_pairs={{0,2},{2,0},{4,6},{6,4},{8,10},{10,8},{12,14},{14,12},{16,18},{18,... | collective-permute-start | bytes 983048 | tf_op jit(solution)/shard_map/ppermute | solution.py:21
  356.8 42.5 %collective-permute-start.28 = (bf16[320,2048]{1,0:T(8,128)(2,1)}, bf16[320,2048]{1,0:T(8,128)(2,1)S(1)}, u32[]{:S(2)}, u32[]{:S(2)}) collective-permute-start(bf16[320,2048]{1,0:T(8,128)(2,1)} %get-tuple-element.131), channel_id=1, source_target_pairs={{0,2},{2,0},{4,6},{6,4},{8,10},{10,8},{12,14},{14,12},{16,18},{18,... | collective-permute-start | bytes 3932168 | tf_op jit(solution)/shard_map/ppermute | solution.py:21
  374.8 12.7 %collective-permute-start.33 = (bf16[160,2048]{1,0:T(8,128)(2,1)}, bf16[160,2048]{1,0:T(8,128)(2,1)S(1)}, u32[]{:S(2)}, u32[]{:S(2)}) collective-permute-start(bf16[160,2048]{1,0:T(8,128)(2,1)} %get-tuple-element.140), channel_id=1, source_target_pairs={{0,2},{2,0},{4,6},{6,4},{8,10},{10,8},{12,14},{14,12},{16,18},{18,... | collective-permute-start | bytes 1966088 | tf_op jit(solution)/shard_map/ppermute | solution.py:21
  385.4 88.4 %collective-permute-start.42 = (bf16[512,2048]{1,0:T(8,128)(2,1)}, bf16[512,2048]{1,0:T(8,128)(2,1)}, u32[]{:S(2)}, u32[]{:S(2)}) collective-permute-start(bf16[512,2048]{1,0:T(8,128)(2,1)} %convolution_convert_fusion.6), channel_id=1, source_target_pairs={{0,1},{1,0},{2,3},{3,2},{4,5},{5,4},{6,7},{7,6},{8,9},{9,8},{10,11... | collective-permute-start | bytes 6291464 | tf_op jit(solution)/shard_map/ppermute | solution.py:25
  387.8 12.1 %collective-permute-start.34 = (bf16[80,2048]{1,0:T(8,128)(2,1)S(1)}, bf16[80,2048]{1,0:T(8,128)(2,1)S(1)}, u32[]{:S(2)}, u32[]{:S(2)}) collective-permute-start(bf16[80,2048]{1,0:T(8,128)(2,1)S(1)} %get-tuple-element.291), channel_id=1, source_target_pairs={{0,8},{2,10},{8,16},{10,18},{16,24},{18,26},{24,28},{26,30},{28,20... | collective-permute-start | bytes 983048 | tf_op jit(solution)/shard_map/ppermute | solution.py:36
  389.8 9.5 collective-permute-start.38
  400.1 17.2 %collective-permute-start.35 = (bf16[160,2048]{1,0:T(8,128)(2,1)S(1)}, bf16[160,2048]{1,0:T(8,128)(2,1)S(1)}, u32[]{:S(2)}, u32[]{:S(2)}) collective-permute-start(bf16[160,2048]{1,0:T(8,128)(2,1)S(1)} %pad_maximum_fusion.6), channel_id=1, source_target_pairs={{0,8},{2,10},{8,16},{10,18},{16,24},{18,26},{24,28},{26,30},{28,20... | collective-permute-start | bytes 1966088 | tf_op jit(solution)/shard_map/ppermute | solution.py:36
  402.0 15.3 %collective-permute-start.39 = (bf16[160,2048]{1,0:T(8,128)(2,1)S(1)}, bf16[160,2048]{1,0:T(8,128)(2,1)S(1)}, u32[]{:S(2)}, u32[]{:S(2)}) collective-permute-start(bf16[160,2048]{1,0:T(8,128)(2,1)S(1)} %pad_maximum_fusion.7), channel_id=1, source_target_pairs={{8,0},{10,2},{16,8},{18,10},{24,16},{26,18},{28,24},{30,26},{20,28... | collective-permute-start | bytes 1966088 | tf_op jit(solution)/shard_map/ppermute | solution.py:40
  409.2 69.2 %collective-permute-start.43 = (bf16[2048,512]{1,0:T(8,128)(2,1)}, bf16[2048,512]{1,0:T(8,128)(2,1)}, u32[]{:S(2)}, u32[]{:S(2)}) collective-permute-start(bf16[2048,512]{1,0:T(8,128)(2,1)} %convolution_convert_fusion.5), channel_id=1, source_target_pairs={{0,1},{1,0},{2,3},{3,2},{4,5},{5,4},{6,7},{7,6},{8,9},{9,8},{10,11... | collective-permute-start | bytes 6291464 | tf_op jit(solution)/shard_map/ppermute | solution.py:25
  417.8 27.0 %collective-permute-start.36 = (bf16[160,2048]{1,0:T(8,128)(2,1)S(1)}, bf16[160,2048]{1,0:T(8,128)(2,1)S(1)}, u32[]{:S(2)}, u32[]{:S(2)}) collective-permute-start(bf16[160,2048]{1,0:T(8,128)(2,1)S(1)} %get-tuple-element.274), channel_id=1, source_target_pairs={{0,8},{2,10},{8,16},{10,18},{16,24},{18,26},{24,28},{26,30},{28,20... | collective-permute-start | bytes 1966088 | tf_op jit(solution)/shard_map/ppermute | solution.py:36
  419.5 25.3 %collective-permute-start.40 = (bf16[160,2048]{1,0:T(8,128)(2,1)S(1)}, bf16[160,2048]{1,0:T(8,128)(2,1)S(1)}, u32[]{:S(2)}, u32[]{:S(2)}) collective-permute-start(bf16[160,2048]{1,0:T(8,128)(2,1)S(1)} %get-tuple-element.275), channel_id=1, source_target_pairs={{8,0},{10,2},{16,8},{18,10},{24,16},{26,18},{28,24},{30,26},{20,28... | collective-permute-start | bytes 1966088 | tf_op jit(solution)/shard_map/ppermute | solution.py:40
  445.3 26.9 %collective-permute-start.41 = (bf16[160,2048]{1,0:T(8,128)(2,1)S(1)}, bf16[160,2048]{1,0:T(8,128)(2,1)S(1)}, u32[]{:S(2)}, u32[]{:S(2)}) collective-permute-start(bf16[160,2048]{1,0:T(8,128)(2,1)S(1)} %get-tuple-element.273), channel_id=1, source_target_pairs={{8,0},{10,2},{16,8},{18,10},{24,16},{26,18},{28,24},{30,26},{20,28... | collective-permute-start | bytes 1966088 | tf_op jit(solution)/shard_map/ppermute | solution.py:40
  445.7 26.5 %collective-permute-start.37 = (bf16[160,2048]{1,0:T(8,128)(2,1)S(1)}, bf16[160,2048]{1,0:T(8,128)(2,1)S(1)}, u32[]{:S(2)}, u32[]{:S(2)}) collective-permute-start(bf16[160,2048]{1,0:T(8,128)(2,1)S(1)} %get-tuple-element.272), channel_id=1, source_target_pairs={{0,8},{2,10},{8,16},{10,18},{16,24},{18,26},{24,28},{26,30},{28,20... | collective-permute-start | bytes 1966088 | tf_op jit(solution)/shard_map/ppermute | solution.py:36
  488.3 512.5 %reduce-scatter.5.cloned.1.call-start = ((), (), s32[]{:S(2)}) async-start(), calls=%async_computation.3 | async-start | bytes 17825792 | tf_op jit(solution)/shard_map/reduce_scatter | solution.py:636
  613.0 16.3 %collective-permute-start.45 = (bf16[160,2048]{1,0:T(8,128)(2,1)S(1)}, bf16[160,2048]{1,0:T(8,128)(2,1)S(1)}, u32[]{:S(2)}, u32[]{:S(2)}) collective-permute-start(bf16[160,2048]{1,0:T(8,128)(2,1)S(1)} %get-tuple-element.233), channel_id=1, source_target_pairs={{0,1},{1,0},{2,3},{3,2},{4,5},{5,4},{6,7},{7,6},{8,9},{9,8},{10,11... | collective-permute-start | bytes 1966088 | tf_op jit(solution)/shard_map/ppermute | solution.py:25
  674.3 30.9 %collective-permute-start.46 = (bf16[4,128,1024]{1,2,0:T(8,128)(2,1)}, bf16[4,128,1024]{1,2,0:T(8,128)(2,1)}, u32[]{:S(2)}, u32[]{:S(2)}) collective-permute-start(bf16[4,128,1024]{1,2,0:T(8,128)(2,1)} %pad_maximum_fusion.4), channel_id=1, source_target_pairs={{0,2},{2,0},{4,6},{6,4},{8,10},{10,8},{12,14},{14,12},{16,18},{18,... | collective-permute-start | bytes 3145736 | tf_op jit(solution)/shard_map/ppermute | solution.py:21
  675.3 69.1 %collective-permute-start.49 = (bf16[2048,512]{1,0:T(8,128)(2,1)}, bf16[2048,512]{1,0:T(8,128)(2,1)}, u32[]{:S(2)}, u32[]{:S(2)}) collective-permute-start(bf16[2048,512]{1,0:T(8,128)(2,1)} %convolution_convert_fusion.4), channel_id=1, source_target_pairs={{0,1},{1,0},{2,3},{3,2},{4,5},{5,4},{6,7},{7,6},{8,9},{9,8},{10,11... | collective-permute-start | bytes 6291464 | tf_op jit(solution)/shard_map/ppermute | solution.py:25
  692.2 16.0 %collective-permute-start.50 = (bf16[4,128,1024]{1,2,0:T(8,128)(2,1)}, bf16[4,128,1024]{1,2,0:T(8,128)(2,1)}, u32[]{:S(2)}, u32[]{:S(2)}) collective-permute-start(bf16[4,128,1024]{1,2,0:T(8,128)(2,1)} %pad_maximum_fusion.5), channel_id=1, source_target_pairs={{0,2},{2,0},{4,6},{6,4},{8,10},{10,8},{12,14},{14,12},{16,18},{18,... | collective-permute-start | bytes 3145736 | tf_op jit(solution)/shard_map/ppermute | solution.py:21
  706.6 14.2 %collective-permute-start.47 = (bf16[2,128,1024]{1,2,0:T(8,128)(2,1)S(1)}, bf16[2,128,1024]{1,2,0:T(8,128)(2,1)S(1)}, u32[]{:S(2)}, u32[]{:S(2)}) collective-permute-start(bf16[2,128,1024]{1,2,0:T(8,128)(2,1)S(1)} %pad_maximum_fusion.11), channel_id=1, source_target_pairs={{0,4},{2,6},{4,0},{6,2},{8,12},{10,14},{12,8},{14,10},{16,20},{18,... | collective-permute-start | bytes 1572872 | tf_op jit(solution)/shard_map/ppermute | solution.py:21
  709.4 14.8 %collective-permute-start.51 = (bf16[2,128,1024]{1,2,0:T(8,128)(2,1)S(1)}, bf16[2,128,1024]{1,2,0:T(8,128)(2,1)S(1)}, u32[]{:S(2)}, u32[]{:S(2)}) collective-permute-start(bf16[2,128,1024]{1,2,0:T(8,128)(2,1)S(1)} %pad_maximum_fusion.12), channel_id=1, source_target_pairs={{0,8},{2,10},{4,12},{6,14},{8,0},{10,2},{12,4},{14,6},{16,24},{18,... | collective-permute-start | bytes 1572872 | tf_op jit(solution)/shard_map/ppermute | solution.py:21
  722.7 9.6 collective-permute-start.48
  726.2 8.1 collective-permute-start.52
  828.9 44.9 %collective-permute-start.44 = (f32[160,2048]{1,0:T(8,128)S(1)}, f32[160,2048]{1,0:T(8,128)S(1)}, u32[]{:S(2)}, u32[]{:S(2)}) collective-permute-start(f32[160,2048]{1,0:T(8,128)S(1)} %copy-done.35), channel_id=1, source_target_pairs={{0,1},{1,0},{2,3},{3,2},{4,5},{5,4},{6,7},{7,6},{8,9},{9,8},{10,11... | collective-permute-start | bytes 3932168 | tf_op jit(solution)/shard_map/ppermute | solution.py:25
  836.9 34.6 %collective-permute-start.53 = (bf16[160,2048]{1,0:T(8,128)(2,1)S(1)}, bf16[160,2048]{1,0:T(8,128)(2,1)S(1)}, u32[]{:S(2)}, u32[]{:S(2)}) collective-permute-start(bf16[160,2048]{1,0:T(8,128)(2,1)S(1)} %dynamic-slice_convert_fusion), channel_id=1, source_target_pairs={{0,1},{1,0},{2,3},{3,2},{4,5},{5,4},{6,7},{7,6},{8,9},{9,8},{10,11... | collective-permute-start | bytes 1966088 | tf_op jit(solution)/shard_map/ppermute | solution.py:25
  872.1 6.6 collective-permute-start.55
  878.7 4.2 collective-permute-start.56
  882.9 3.6 collective-permute-start.57
  884.3 25.8 %collective-permute-start.54 = (f32[160,2048]{1,0:T(8,128)S(1)}, f32[160,2048]{1,0:T(8,128)S(1)}, u32[]{:S(2)}, u32[]{:S(2)}) collective-permute-start(f32[160,2048]{1,0:T(8,128)S(1)} %fusion.2), channel_id=1, source_target_pairs={{0,1},{1,0},{2,3},{3,2},{4,5},{5,4},{6,7},{7,6},{8,9},{9,8},{10,11... | collective-permute-start | bytes 3932168 | tf_op jit(solution)/shard_map/ppermute | solution.py:25
  886.5 1.7 collective-permute-start.58
  888.2 21.4 %collective-permute-start.59 = (f32[4,128]{1,0:T(4,128)S(1)}, f32[4,128]{1,0:T(4,128)S(1)}, u32[]{:S(2)}, u32[]{:S(2)}) collective-permute-start(f32[4,128]{1,0:T(4,128)S(1)} %fusion.56), channel_id=1, source_target_pairs={{0,1},{1,0},{2,3},{3,2},{4,5},{5,4},{6,7},{7,6},{8,9},{9,8},{10,11... | collective-permute-start | bytes 6152 | tf_op jit(solution)/shard_map/ppermute | solution.py:25
  (147 other events, 1425.4 us)
Sparse Core Ops, SparseCore 0:
  14.9 94.2 all-gather.4
  111.4 97.8 all-gather.6
  488.4 120.3 reduce-scatter.2
  822.7 177.9 reduce-scatter.4

commit v3 on v2

--- a/solution.py
+++ b/solution.py
@@ -109,19 +109,6 @@
     return (cosine, sine)
 
 
-def rotate(values, cosine, sine):
-    half_size = values.shape[-1] // 2
-    turned = jnp.concatenate([-values[..., half_size:], values[..., :half_size]], axis=-1)
-    return values * cosine[:, None, :] + turned * sine[:, None, :]
-
-
-def rotate_back(values, cosine, sine):
-    half_size = values.shape[-1] // 2
-    scaled = values * sine[:, None, :]
-    turned = jnp.concatenate([scaled[..., half_size:], -scaled[..., :half_size]], axis=-1)
-    return values * cosine[:, None, :] + turned
-
-
 def cont_positions(segment_row, gap_row, prompt_length):
     order = jnp.arange(segment_row.shape[0], dtype=jnp.int32)
     same = segment_row[:, None] == segment_row[None, :]
@@ -146,40 +133,234 @@
     return lax.dot_general(left, right, (((1,), (1,)), ((), ())), preferred_element_type=FULL)
 
 
-def collect_prompt(keys, values):
-    own = jnp.stack([keys, values], axis=0)
+def collect_prompt(own):
     near = swap_bit(own, "dp", 1)
     far = swap_bit(own, "dp", 2)
-    last_keys = swap_bit(far[0], "dp", 1)
-    last_values = swap_bit(near[1], "dp", 2)
-    blocks = [None] * GROUP
-    for at, piece in ((0, own), (2, near), (4, far)):
-        blocks[at] = piece
-        blocks[at + 1] = swap_bit(piece, "dp", 0)
-    last = jnp.stack([last_keys, last_values], axis=0)
-    blocks[6] = last
-    blocks[7] = swap_bit(last, "dp", 0)
-    return [b[0] for b in blocks], [b[1] for b in blocks]
-
-
-def return_prompt(grads, order):
-    parts = {j: grads[j] for j in range(GROUP)}
-    for bit in order:
-        gone = [j for j in sorted(parts) if j >> bit & 1]
-        sent = jnp.stack([parts[j] for j in gone], axis=0).astype(LOW)
-        got = swap_bit(sent, "dp", bit)
-        for at, j in enumerate(gone):
-            stay = j ^ (1 << bit)
-            parts[stay] = parts[stay] + got[at].astype(FULL)
-            del parts[j]
-    return parts[0]
-
-
-def masked_scores(queries, keyset, allowed):
-    scores = jnp.einsum("qhd,khd->hqk", queries, keyset, preferred_element_type=FULL) * HEAD ** (
-        -0.5
-    )
-    return jnp.where(allowed[None], scores, -1e30)
+    last = jnp.stack([swap_bit(far[0], "dp", 1), swap_bit(near[1], "dp", 2)], axis=0)
+    others = [swap_bit(piece, "dp", 0) for piece in (own, near, far, last)]
+    return [others[0], near, others[1], far, others[2], last, others[3]]
+
+
+def return_prompt(odd, even):
+    got = swap_bit(odd, "dp", 0)
+    near, far, last = (add_low(even[i], got[i + 1]) for i in range(3))
+    keys = swap_bit(jnp.stack([near[0], last[0]], axis=0), "dp", 1)
+    values = swap_bit(jnp.stack([far[1], last[1]], axis=0), "dp", 2)
+    last_keys = swap_bit(add_low(far[0], keys[1]), "dp", 2)
+    last_values = swap_bit(add_low(near[1], values[1]), "dp", 1)
+    return (got[0, 0], keys[0], last_keys), (got[0, 1], values[0], last_values)
+
+
+def turn(values):
+    return pltpu.roll(values, HEAD // 2, 1)
+
+
+def rope_kernel(q_ref, k_ref, gq_ref, gk_ref, sq_ref, sk_ref, cos_ref, sin_ref, qo_ref, ko_ref):
+    for pre, gain, scale, out in (
+        (q_ref, gq_ref, sq_ref, qo_ref),
+        (k_ref, gk_ref, sk_ref, ko_ref),
+    ):
+        normed = pre[...] * scale[...] * gain[...]
+        out[...] = (normed * cos_ref[...] + turn(normed) * sin_ref[...]).astype(LOW)
+
+
+def head_spec(rows):
+    return pl.BlockSpec((rows, HEAD), lambda h: (0, h))
+
+
+def kept_spec(array):
+    zeros = (0,) * array.ndim
+    return pl.BlockSpec(array.shape, lambda h: zeros, pipeline_mode=pl.Buffered(1))
+
+
+def piece_spec(count):
+    return pl.BlockSpec((count, 2, PR_DEV, HEAD), lambda h: (0, 0, 0, h))
+
+
+def rope_pass(query_flat, key_flat, gain_q, gain_k, scale_q, scale_k, cosine, sine):
+    rows, width = query_flat.shape
+    return pl.pallas_call(
+        rope_kernel,
+        grid=(width // HEAD,),
+        in_specs=[head_spec(rows)] * 2
+        + [head_spec(1)] * 2
+        + [kept_spec(a) for a in (scale_q, scale_k, cosine, sine)],
+        out_specs=[head_spec(rows)] * 2,
+        out_shape=[jax.ShapeDtypeStruct((rows, width), LOW)] * 2,
+    )(query_flat, key_flat, gain_q, gain_k, scale_q, scale_k, cosine, sine)
+
+
+def all_keys(own_ref, pieces, which):
+    return jnp.concatenate(
+        [own_ref[:PR_DEV]] + [piece[0, which] for piece in pieces] + [own_ref[PR_DEV:]], axis=0
+    )
+
+
+def softmax_rows(query, keys, bias):
+    scores = dot_nt(query, keys) * HEAD ** (-0.5) + bias
+    weights = jnp.exp(scores - jnp.max(scores, axis=1, keepdims=True))
+    return weights * (1.0 / jnp.sum(weights, axis=1, keepdims=True))
+
+
+def attend_kernel(q_ref, k_ref, v_ref, bias_ref, *refs):
+    pieces, out_ref = refs[:-1], refs[-1]
+    probs = softmax_rows(
+        q_ref[...], all_keys(k_ref, pieces, 0), bias_ref[...].astype(FULL)
+    ).astype(LOW)
+    out_ref[...] = dot_nn(probs, all_keys(v_ref, pieces, 1)).astype(LOW)
+
+
+def attend(queries, keys, values, bias, pieces):
+    rows, width = queries.shape
+    pieces = [piece[None] for piece in pieces]
+    return pl.pallas_call(
+        attend_kernel,
+        grid=(width // HEAD,),
+        in_specs=[head_spec(rows)] * 3 + [kept_spec(bias)] + [piece_spec(1)] * len(pieces),
+        out_specs=head_spec(rows),
+        out_shape=jax.ShapeDtypeStruct((rows, width), LOW),
+        compiler_params=pltpu.CompilerParams(vmem_limit_bytes=40 * 1024 * 1024),
+    )(queries, keys, values, bias, *pieces)
+
+
+def norm_parts(step, grad, flat_ref, gain_ref, scale_ref, inner_ref, gain_grad_ref):
+    product = flat_ref[...] * grad
+    inner = jnp.sum(product * gain_ref[...], axis=1, keepdims=True)
+    gain_grad_ref[...] = jnp.sum(product * scale_ref[...], axis=0, keepdims=True)
+
+    @pl.when(step == 0)
+    def _():
+        inner_ref[...] = inner
+
+    @pl.when(step > 0)
+    def _():
+        inner_ref[...] += inner
+
+
+def attend_back_kernel(*refs):
+    q_ref, k_ref, v_ref, bias_ref, back_ref, flat_ref, gain_ref, scale_ref, cos_ref, sin_ref = (
+        refs[:10]
+    )
+    pieces = refs[10 : 10 + GROUP - 1]
+    qg_ref, inner_ref, gain_grad_ref, kg_ref, vg_ref, odd_ref, even_ref = refs[10 + GROUP - 1 :]
+    step = pl.program_id(0)
+    query, keys, values = q_ref[...], all_keys(k_ref, pieces, 0), all_keys(v_ref, pieces, 1)
+    back = back_ref[...]
+    probs = softmax_rows(query, keys, bias_ref[...].astype(FULL))
+    prob_grad = dot_nt(back, values)
+    value_grad = dot_tn(probs.astype(LOW), back)
+    row_dot = jnp.sum(probs * prob_grad, axis=1, keepdims=True)
+    score_grad = (probs * (prob_grad - row_dot)).astype(LOW)
+    query_grad = dot_nn(score_grad, keys) * HEAD ** (-0.5)
+    key_grad = dot_tn(score_grad, query) * HEAD ** (-0.5)
+    query_grad = query_grad * cos_ref[...] - turn(query_grad) * sin_ref[...]
+    qg_ref[...] = query_grad
+    norm_parts(step, query_grad, flat_ref, gain_ref, scale_ref, inner_ref, gain_grad_ref)
+    prompt = PR_DEV * GROUP
+    for which, grad, own_ref in ((0, key_grad, kg_ref), (1, value_grad, vg_ref)):
+        own_ref[:PR_DEV] = grad[:PR_DEV]
+        own_ref[PR_DEV:] = grad[prompt:]
+        for j in range(1, GROUP):
+            to = odd_ref if j % 2 else even_ref
+            to[(j - 1) // 2, which] = grad[j * PR_DEV : (j + 1) * PR_DEV].astype(LOW)
+
+
+def attend_back(queries, keys, values, bias, back, flat, gain, scale, cosine, sine, pieces):
+    rows, width = queries.shape
+    pieces = [piece[None] for piece in pieces]
+    wide = jax.ShapeDtypeStruct((rows, width), FULL)
+    return pl.pallas_call(
+        attend_back_kernel,
+        grid=(width // HEAD,),
+        in_specs=[head_spec(rows)] * 3
+        + [kept_spec(bias), head_spec(rows), head_spec(rows), head_spec(1)]
+        + [kept_spec(a) for a in (scale, cosine, sine)]
+        + [piece_spec(1)] * len(pieces),
+        out_specs=[
+            head_spec(rows),
+            pl.BlockSpec((rows, 1), lambda h: (0, 0)),
+            head_spec(1),
+            head_spec(rows),
+            head_spec(rows),
+            piece_spec(4),
+            piece_spec(3),
+        ],
+        out_shape=[
+            wide,
+            jax.ShapeDtypeStruct((rows, 1), FULL),
+            jax.ShapeDtypeStruct((1, width), FULL),
+            wide,
+            wide,
+            jax.ShapeDtypeStruct((4, 2, PR_DEV, width), LOW),
+            jax.ShapeDtypeStruct((3, 2, PR_DEV, width), LOW),
+        ],
+        compiler_params=pltpu.CompilerParams(vmem_limit_bytes=58 * 1024 * 1024),
+    )(queries, keys, values, bias, back, flat, gain, scale, cosine, sine, *pieces)
+
+
+def key_back_kernel(*refs):
+    kg_ref, vg_ref, flat_ref, gain_ref, scale_ref, cos_ref, sin_ref = refs[:7]
+    key_parts, value_parts = refs[7:10], refs[10:13]
+    out_ref, inner_ref, gain_grad_ref, value_ref = refs[13:]
+    step = pl.program_id(0)
+    grads = []
+    for own_ref, parts in ((kg_ref, key_parts), (vg_ref, value_parts)):
+        first = own_ref[:PR_DEV]
+        for part in parts:
+            first = first + part[...].astype(FULL)
+        grads.append(jnp.concatenate([first, own_ref[PR_DEV:]], axis=0))
+    key_grad = grads[0] * cos_ref[...] - turn(grads[0]) * sin_ref[...]
+    out_ref[...] = key_grad
+    norm_parts(step, key_grad, flat_ref, gain_ref, scale_ref, inner_ref, gain_grad_ref)
+    value_ref[...] = grads[1].astype(LOW)
+
+
+def key_back(key_grad, value_grad, flat, gain, scale, cosine, sine, key_parts, value_parts):
+    rows, width = flat.shape
+    return pl.pallas_call(
+        key_back_kernel,
+        grid=(width // HEAD,),
+        in_specs=[head_spec(rows)] * 3
+        + [head_spec(1)]
+        + [kept_spec(a) for a in (scale, cosine, sine)]
+        + [head_spec(PR_DEV)] * 6,
+        out_specs=[
+            head_spec(rows),
+            pl.BlockSpec((rows, 1), lambda h: (0, 0)),
+            head_spec(1),
+            head_spec(rows),
+        ],
+        out_shape=[
+            jax.ShapeDtypeStruct((rows, width), FULL),
+            jax.ShapeDtypeStruct((rows, 1), FULL),
+            jax.ShapeDtypeStruct((1, width), FULL),
+            jax.ShapeDtypeStruct((rows, width), LOW),
+        ],
+    )(key_grad, value_grad, flat, gain, scale, cosine, sine, *key_parts, *value_parts)
+
+
+def ring_weights(first, second):
+    rows = first.shape[0] // len(RING)
+    cut = (first.shape[1] + second.shape[1]) // 2
+    chip = lax.axis_index("dp") // 2
+    place = jnp.where(chip % 2 == 0, chip // 2, 7 - chip // 2)
+
+    def part(hop):
+        there = (place + hop) % len(RING)
+        at = jnp.where(there < 4, 2 * there, 2 * (7 - there) + 1) * rows
+        return jnp.concatenate(
+            [lax.dynamic_slice_in_dim(a, at, rows, axis=0) for a in (first, second)], axis=1
+        )
+
+    far = part(4)
+    right, left = ahead(far[:, :cut]), behind(far[:, cut:])
+    outward, inward = part(3), part(-3)
+    right = jnp.concatenate([add_low(outward[:, :cut], right), outward[:, cut:]], axis=1)
+    left = jnp.concatenate([inward[:, :cut], add_low(inward[:, cut:], left)], axis=1)
+    right, left = ahead(right), behind(left)
+    for hop in (2, 1):
+        right, left = ahead(add_low(part(hop), right)), behind(add_low(part(-hop), left))
+    return part(0).astype(FULL) + right.astype(FULL) + left.astype(FULL)
 
 
 def expert_kernel(
@@ -457,38 +638,13 @@
     back_rows = lax.all_gather(cotangent_half.astype(LOW), "dp", axis=0, tiled=False)
     back_rows = (back_rows[blocks] if ring else back_rows).reshape(-1, model_width)
 
+    core = dp_index % 2
     tokens_f = inputs.astype(FULL)
     prompt_pos = dp_index % GROUP * PR_DEV + jnp.arange(PR_DEV, dtype=jnp.int32)
     later_pos = cont_positions(segments[0], gaps[0], prompt_length)
     positions = jnp.concatenate([prompt_pos, later_pos], axis=0)
     cosine, sine = rope_tables(positions, HEAD)
-    normed_b = rms_norm(tokens_f, gain_one).astype(LOW)
-    query_flat = dot_nn(normed_b, full_q)
-    key_flat = dot_nn(normed_b, full_k)
-    values_b = dot_nn(normed_b, full_v).astype(LOW)
-    query_sq, key_sq = lax.psum(
-        (jnp.sum(query_flat * query_flat, axis=1), jnp.sum(key_flat * key_flat, axis=1)), "tensor"
-    )
-    query_sq, down_mat = lax.optimization_barrier((query_sq, w_down[0]))
-    down_mats = (down_mat, swap_tensor(down_mat))
-    query_scale = lax.rsqrt(query_sq / column_total + EPSILON)[:, None]
-    key_scale = lax.rsqrt(key_sq / column_total + EPSILON)[:, None]
-    by_head = (token_count, local_heads, HEAD)
-    queries_b = rotate(
-        (query_flat * query_scale * gain_query_local).reshape(by_head), cosine, sine
-    ).astype(LOW)
-    keys_b = rotate(
-        (key_flat * key_scale * gain_key_local).reshape(by_head), cosine, sine
-    ).astype(LOW)
-    key_blocks, value_blocks = collect_prompt(
-        keys_b[:PR_DEV].reshape(PR_DEV, local_width), values_b[:PR_DEV]
-    )
-    keyset = jnp.concatenate(
-        key_blocks + [keys_b[PR_DEV:].reshape(-1, local_width)], axis=0
-    ).reshape(-1, local_heads, HEAD)
-    valueset = jnp.concatenate(value_blocks + [values_b[PR_DEV:]], axis=0).reshape(
-        -1, local_heads, HEAD
-    )
+    sine = jnp.where(jnp.arange(HEAD) < HEAD // 2, -sine, sine)
     prompt_query = jnp.arange(token_count, dtype=jnp.int32) < PR_DEV
     prompt_at = jnp.arange(prompt_length, dtype=jnp.int32)
     prompt_keypos = ((dp_index % GROUP) ^ (prompt_at // PR_DEV)) * PR_DEV + prompt_at % PR_DEV
@@ -498,14 +654,30 @@
         later_pos[None, :] <= positions[:, None]
     )
     allowed = jnp.concatenate([allowed_prompt, allowed_cont], axis=1)
-    scores = masked_scores(queries_b, keyset, allowed)
-    peak = jnp.max(scores, axis=-1, keepdims=True)
-    expo = jnp.exp(scores - peak)
-    total = jnp.sum(expo, axis=-1, keepdims=True)
-    log_total = peak + jnp.log(total)
-    probs_b = (expo / total).astype(LOW)
-    context = jnp.einsum("hqk,khd->qhd", probs_b, valueset, preferred_element_type=FULL)
-    context_b = context.reshape(token_count, local_width).astype(LOW)
+    bias = jnp.where(allowed, 0.0, -1e30).astype(LOW)
+    normed_b = rms_norm(tokens_f, gain_one).astype(LOW)
+    query_flat = dot_nn(normed_b, full_q)
+    key_flat = dot_nn(normed_b, full_k)
+    values_b = dot_nn(normed_b, full_v).astype(LOW)
+    query_sq, key_sq = lax.psum(
+        (jnp.sum(query_flat * query_flat, axis=1), jnp.sum(key_flat * key_flat, axis=1)), "tensor"
+    )
+    query_sq, down_mat = lax.optimization_barrier((query_sq, w_down[0]))
+    down_mats = (down_mat, swap_tensor(down_mat))
+    query_scale = lax.rsqrt(query_sq / column_total + EPSILON)[:, None]
+    key_scale = lax.rsqrt(key_sq / column_total + EPSILON)[:, None]
+    queries_b, keys_b = rope_pass(
+        query_flat,
+        key_flat,
+        gain_query_local[None],
+        gain_key_local[None],
+        query_scale,
+        key_scale,
+        cosine,
+        sine,
+    )
+    pieces = collect_prompt(jnp.stack([keys_b[:PR_DEV], values_b[:PR_DEV]], axis=0))
+    context_b = attend(queries_b, keys_b, values_b, bias, pieces)
     attn_part = dot_nt(context_b, full_o)
     attn_part, late = lax.optimization_barrier((attn_part, down_mats[1]))
     down_mats = (down_mats[0], late)
@@ -567,43 +739,34 @@
     attn_grad_b = both_halves(attn_grad_half, swap_tensor(attn_grad_half))
     attn_grad_b, up_sent = together(attn_grad_b, up_sent)
     up_got = swap_tensor(up_sent)
-    out_w_grad = dot_tn(attn_grad_b, context_b).astype(LOW)
-    context_grad_b = dot_nn(attn_grad_b, full_o).astype(LOW).reshape(by_head)
-    again = masked_scores(queries_b, keyset, allowed)
-    probs = jnp.exp(again - log_total)
-    prob_grad = jnp.einsum(
-        "qhd,khd->hqk", context_grad_b, valueset, preferred_element_type=FULL
-    )
-    value_grad = jnp.einsum("hqk,qhd->khd", probs_b, context_grad_b, preferred_element_type=FULL)
-    row_dot = jnp.sum(probs * prob_grad, axis=-1, keepdims=True)
-    score_grad_b = (probs * (prob_grad - row_dot)).astype(LOW)
-    query_grad = jnp.einsum(
-        "hqk,khd->qhd", score_grad_b, keyset, preferred_element_type=FULL
-    ) * HEAD ** (-0.5)
-    key_grad = jnp.einsum(
-        "hqk,qhd->khd", score_grad_b, queries_b, preferred_element_type=FULL
-    ) * HEAD ** (-0.5)
-    key_grad = key_grad.reshape(-1, local_width)
-    value_grad = value_grad.reshape(-1, local_width)
-    blocks_of = lambda array: [array[j * PR_DEV : (j + 1) * PR_DEV] for j in range(GROUP)]
-    key_own = return_prompt(blocks_of(key_grad), (0, 1, 2))
-    value_own = return_prompt(blocks_of(value_grad), (0, 2, 1))
-    key_local = jnp.concatenate([key_own, key_grad[prompt_length:]], axis=0)
-    value_local = jnp.concatenate([value_own, value_grad[prompt_length:]], axis=0)
-    query_normed_grad = rotate_back(query_grad, cosine, sine).reshape(token_count, -1)
-    key_normed_grad = rotate_back(key_local.reshape(by_head), cosine, sine).reshape(
-        token_count, -1
-    )
-    query_normed_grad, key_normed_grad, up_got = together(
-        query_normed_grad, key_normed_grad, up_got
-    )
-    query_inner, key_inner = lax.psum(
-        (
-            jnp.sum(query_flat * gain_query_local * query_normed_grad, axis=1),
-            jnp.sum(key_flat * gain_key_local * key_normed_grad, axis=1),
-        ),
-        "tensor",
-    )
+    context_grad_b = dot_nn(attn_grad_b, full_o).astype(LOW)
+    query_normed_grad, query_inner, query_gain_part, key_grad, value_grad, odd, even = attend_back(
+        queries_b,
+        keys_b,
+        values_b,
+        bias,
+        context_grad_b,
+        query_flat,
+        gain_query_local[None],
+        query_scale,
+        cosine,
+        sine,
+        pieces,
+    )
+    key_parts, value_parts = return_prompt(odd, even)
+    key_normed_grad, key_inner, key_gain_part, value_pre_grad = key_back(
+        key_grad,
+        value_grad,
+        key_flat,
+        gain_key_local[None],
+        key_scale,
+        cosine,
+        sine,
+        key_parts,
+        value_parts,
+    )
+    query_inner, key_inner, up_got = together(query_inner, key_inner, up_got)
+    query_inner, key_inner = lax.psum((query_inner[:, 0], key_inner[:, 0]), "tensor")
     query_cube = query_scale * query_scale * query_scale
     key_cube = key_scale * key_scale * key_scale
     query_pre_grad = (
@@ -614,26 +777,40 @@
         key_scale * gain_key_local * key_normed_grad
         - key_flat * key_cube * (key_inner / column_total)[:, None]
     ).astype(LOW)
-    query_gain_part = jnp.sum(query_normed_grad * query_flat * query_scale, axis=0)
-    key_gain_part = jnp.sum(key_normed_grad * key_flat * key_scale, axis=0)
     wide = lambda part: lax.dynamic_update_slice_in_dim(
         jnp.zeros((column_total,), FULL), part, side * local_width, 0
     )
-    value_pre_grad = value_local.astype(LOW)
-    w_grads = jnp.stack(
-        [
-            dot_tn(normed_b, query_pre_grad).astype(LOW).reshape(dp_count, block, local_width),
-            dot_tn(normed_b, key_pre_grad).astype(LOW).reshape(dp_count, block, local_width),
-            dot_tn(normed_b, value_pre_grad).astype(LOW).reshape(dp_count, block, local_width),
-            out_w_grad.reshape(dp_count, block, local_width),
-        ],
-        axis=1,
-    ).reshape(dp_count * 4 * block, local_width)
+    pre_grads = (query_pre_grad, key_pre_grad, value_pre_grad)
+    if ring:
+        columns = local_width // 2
+        mine = lambda a: lax.dynamic_slice_in_dim(a, core * columns, columns, axis=1)
+        theirs = lambda a: lax.dynamic_slice_in_dim(a, (1 - core) * columns, columns, axis=1)
+        pair = lambda own, sent: jnp.concatenate([own, swap_bit(sent, "dp", 0)], axis=0)
+        normed_pair = pair(normed_b, normed_b)
+        attn_grad_pair = pair(attn_grad_b, attn_grad_b)
+        context_pair = pair(mine(context_b), theirs(context_b))
+        grad_pair = pair(
+            jnp.concatenate([mine(g) for g in pre_grads], axis=1),
+            jnp.concatenate([theirs(g) for g in pre_grads], axis=1),
+        )
+        w_half = ring_weights(low_tn(normed_pair, grad_pair), low_tn(attn_grad_pair, context_pair))
+        own_w = lax.dynamic_slice_in_dim(w_half, core * block, block, axis=0)
+        got_w = swap_bit(lax.dynamic_slice_in_dim(w_half, (1 - core) * block, block, axis=0), "dp", 0)
+        left_w, right_w = jnp.where(core == 0, own_w, got_w), jnp.where(core == 0, got_w, own_w)
+        w_sums = [
+            jnp.concatenate([w[:, j * columns : (j + 1) * columns] for w in (left_w, right_w)], axis=1)
+            for j in range(4)
+        ]
+    else:
+        w_grads = jnp.concatenate(
+            [low_tn(normed_b, g) for g in pre_grads] + [low_tn(attn_grad_b, context_b)], axis=1
+        )
+        w_sum = lax.psum_scatter(w_grads, "dp", scatter_dimension=0, tiled=True).astype(FULL)
+        w_sums = [w_sum[:, j * local_width : (j + 1) * local_width] for j in range(4)]
     down_grad = down_grad + down_got.astype(FULL)
     gate_w_grad = gate_w_grad + gate_got.astype(FULL)
     up_w_grad = up_w_grad + up_got.astype(FULL)
     output = both_halves(output_half, swap_tensor(output_half))
-    w_sum = lax.psum_scatter(w_grads, "dp", scatter_dimension=0, tiled=True).astype(FULL)
     normed_part = (
         dot_nt(query_pre_grad, full_q)
         + dot_nt(key_pre_grad, full_k)
@@ -646,7 +823,7 @@
     input_half = state_half + input_part
     input_grad = both_halves(input_half, swap_tensor(input_half))
     gain_grads = jnp.stack(
-        [gain_one_grad, gain_two_grad, wide(query_gain_part), wide(key_gain_part)]
+        [gain_one_grad, gain_two_grad, wide(query_gain_part[0]), wide(key_gain_part[0])]
     ).reshape(4, dp_count, block)
     gain_sums = halving_sum(jnp.swapaxes(gain_grads, 0, 1))
     gain_sums = gain_sums + swap_tensor(gain_sums)
@@ -654,12 +831,12 @@
         output,
         input_grad,
         gain_sums[0],
-        w_sum[:block],
-        w_sum[block : 2 * block],
-        w_sum[2 * block : 3 * block],
+        w_sums[0],
+        w_sums[1],
+        w_sums[2],
         gain_sums[2],
         gain_sums[3],
-        w_sum[3 * block :].T,
+        w_sums[3].T,
         gain_sums[1],
         gate_w_grad[None],
         up_w_grad[None],

time: 1020 us -> 890 us (0.87)
  local copies, waits for them, and re-layouts: 174 us -> 66.5 us
  Pallas kernels: 106 us -> 154 us
  waiting for transfers between devices: 438 us -> 391 us
  other arithmetic: 85.8 us -> 57.2 us
  starting transfers between devices: 46.9 us -> 68 us
  matrix products: 136 us -> 120 us
    reduce_scatter x1 -> x0, waiting for transfers between devices: 88.8 us -> none  [body(): lax.psum_scatter(w_grads, 'dp', scatter_dimension=0, tiled=True)]
    pallas_call x0 -> x4, Pallas kernels: none -> 48.4 us  [the longest x1 20 us: attend_back(): pl.pallas_call(attend_back_kernel, grid=(width // HEAD,), in_specs=[head_...]
    slice x27 -> x7, local copies, waits for them, and re-layouts: 43.9 us -> 10.9 us  [the longest x1 10.5 us: body(): full_o = gathered[:, 3 * block:4 * block].reshape(model_width, local_width)]
    another operation x5 -> x4, local copies, waits for them, and re-layouts: 29.5 us -> 0.05 us  [the longest x2 0.04 us: body(): jnp.stack([keys_b[:PR_DEV], values_b[:PR_DEV]], axis=0)]
    reshape x1 -> x0, local copies, waits for them, and re-layouts: 27.7 us -> none  [body(): w_grads = jnp.stack([dot_tn(normed_b, query_pre_grad).astype(LOW).reshape...]
    dot_general x6 -> x0, matrix products: 27.4 us -> none  [the longest x1 8.38 us: body(): jnp.einsum('qhd,khd->hqk', context_grad_b, valueset, preferred_element_ty...]
    ppermute x8 -> x12, waiting for transfers between devices: 2.66 us -> 26.2 us  [ahead(): return lax.ppermute(block, 'dp', AHEAD)]
    ppermute x8 -> x12, waiting for transfers between devices: 16.7 us -> 37.8 us  [behind(): return lax.ppermute(block, 'dp', BEHIND)]
  transfers between devices with their start and end apart: 64 -> 75, of which waited for: 23 -> 25; matrix products, arithmetic and copies ran while one was open for 23% -> 23% of each run, Pallas kernels for 10% -> 15%
where the time goes in v3:
time: 890 us; the launch traced here: 883 us
  waiting for transfers between devices  391 us (44%)
  Pallas kernels  154 us (17%)
  matrix products  120 us (13%)
  starting transfers between devices  68 us (8%)
  local copies, waits for them, and re-layouts  66.5 us (7%)
  other arithmetic  57.2 us (6%)
  between operations  16 us (2%)
  blocking collectives  10.6 us (1%)
    ppermute x12, waiting for transfers between devices, swap_tensor(): return lax.ppermute(block, 'tensor', [(0, 1), (1, 0)])  162 us
    reduce_scatter x1, waiting for transfers between devices, body(): lax.psum_scatter(mixed_rows, 'dp', scatter_dimension=0, tiled=True)  118 us
    pallas_call x5, Pallas kernels, expert_chunk(): pl.pallas_call(lambda *refs: chunk_kernel(len(pieces), held is None, *ref...  106 us
    dot_general x8, matrix products, dot_tn(): lax.dot_general(left, right, (((0,), (0,)), ((), ())), preferred_element_...  68.5 us
    ppermute x36, waiting for transfers between devices, swap_bit(): return lax.ppermute(block, axis, [(i, i ^ 1 << bit) for i in range(count)])  47 us
    dot_general x7, matrix products, dot_nn(): return jnp.dot(left, right, preferred_element_type=FULL)  43 us
    ppermute x12, waiting for transfers between devices, behind(): return lax.ppermute(block, 'dp', BEHIND)  37.8 us
    ppermute x12, waiting for transfers between devices, ahead(): return lax.ppermute(block, 'dp', AHEAD)  26.2 us
  transfers between devices with their start and end apart: 75, of which 25 were waited for; matrix products, arithmetic and copies ran while one was open for 23% of the time, Pallas kernels for 15%

profile of v3, /device:TPU:0, one launch (start us, length us, event | category | flops | bytes accessed | tf_op | source)
XLA Modules:
  0.0 883.1 jit_solution(6769998474061881794)
XLA Ops:
  19.4 2.2 dynamic-slice_convert_fusion.2
  21.8 3.0 collective-permute-start
  27.1 44.2 %collective-permute-done.refs_5_.refs_11_.refs_7_.refs_13_ = bf16[2048,512]{1,0:T(8,128)(2,1)} collective-permute-done((bf16[2048,512]{1,0:T(8,128)(2,1)S(1)}, bf16[2048,512]{1,0:T(8,128)(2,1)}, u32[]{:S(2)}, u32[]{:S(2)}) %collective-permute-start) | collective-permute-done | bytes 2097184 | tf_op jit(solution)/shard_map/ppermute | solution.py:25
  71.4 44.1 %collective-permute-done.1.refs_7_.refs_13_.refs_9_.refs_15_ = bf16[2048,512]{1,0:T(8,128)(2,1)} collective-permute-done((bf16[2048,512]{1,0:T(8,128)(2,1)}, bf16[2048,512]{1,0:T(8,128)(2,1)}, u32[]{:S(2)}, u32[]{:S(2)}) %collective-permute-start.1) | collective-permute-done | bytes 2097184 | tf_op jit(solution)/shard_map/ppermute | solution.py:25
  119.2 10.5 %fusion.65 = (bf16[16,128,1024]{2,1,0:T(8,128)(2,1)}, bf16[16,128,1024]{2,1,0:T(8,128)(2,1)}, bf16[16,128,1024]{2,1,0:T(8,128)(2,1)S(1)}, bf16[16,128,1024]{2,1,0:T(8,128)(2,1)S(1)}) fusion(bf16[16,528,1024]{2,1,0:T(8,128)(2,1)} %bitcast.182), kind=kLoop, calls=%fused_computation.271 | loop fusion | bytes 33554432 | tf_op jit(solution)/shard_map/slice | solution.py:606
  129.8 4.9 multiply_reduce_fusion.8
  134.7 4.0 multiply_reduce_fusion.7
  138.6 5.4 all-reduce.4
  146.8 7.0 shard_map.282
  153.8 5.5 convolution_convert_fusion.6.v_ref.refs_2_
  165.1 19.9 %collective-permute-done.3 = bf16[2,128,1024]{2,1,0:T(8,128)(2,1)S(1)} collective-permute-done((bf16[2,128,1024]{2,1,0:T(8,128)(2,1)}, bf16[2,128,1024]{2,1,0:T(8,128)(2,1)S(1)}, u32[]{:S(2)}, u32[]{:S(2)}) %collective-permute-start.3) | collective-permute-done | bytes 524320 | tf_op jit(solution)/shard_map/ppermute | solution.py:21
  186.6 9.6 %collective-permute-done.5 = bf16[2,128,1024]{2,1,0:T(8,128)(2,1)S(1)} collective-permute-done((bf16[2,128,1024]{2,1,0:T(8,128)(2,1)}, bf16[2,128,1024]{2,1,0:T(8,128)(2,1)S(1)}, u32[]{:S(2)}, u32[]{:S(2)}) %collective-permute-start.5) | collective-permute-done | bytes 524320 | tf_op jit(solution)/shard_map/ppermute | solution.py:21
  199.6 8.7 collective-permute-done.8
  212.4 13.6 %shard_map.283 = bf16[320,1024]{1,0:T(8,128)(2,1)S(1)} custom-call(bf16[320,1024]{1,0:T(8,128)(2,1)S(1)} %copy-done.8, bf16[320,1024]{1,0:T(8,128)(2,1)S(1)} %copy-done.2, bf16[320,1024]{1,0:T(8,128)(2,1)S(1)} %convolution_convert_fusion.6.v_ref.refs_2_, bf16[320,1216]{1,0:T(8,128)(2,1)S(1)} %select_convert_fusion.bias_ref.refs_3_, ...), custom_call_target="tpu_custom_call" | custom-call | tf_op jit(solution)/shard_map/pallas_call | solution.py:216
  231.9 14.3 %collective-permute-done.11 = bf16[160,2048]{1,0:T(8,128)(2,1)S(1)} collective-permute-done((bf16[160,2048]{1,0:T(8,128)(2,1)}, bf16[160,2048]{1,0:T(8,128)(2,1)S(1)}, u32[]{:S(2)}, u32[]{:S(2)}) %collective-permute-start.11) | collective-permute-done | bytes 655392 | tf_op jit(solution)/shard_map/ppermute | solution.py:25
  246.2 2.2 multiply_reduce_fusion.6
  249.8 5.9 collective-permute-start.15
  256.3 9.6 %gather_fusion = bf16[16,160,2048]{2,1,0:T(8,128)(2,1)} fusion(bf16[16,160,2048]{2,1,0:T(8,128)(2,1)} %bitcast.184, s32[1024]{0:T(1024)S(1)} %pad_clamp_fusion.1), kind=kCustom, calls=%fused_computation | custom fusion | bytes 20971584 | tf_op jit(solution)/shard_map/gather | solution.py:639
  267.4 2.3 collective-permute-done.14.refs_0_
  269.7 2.2 collective-permute-start.20
  272.8 2.2 reshape.263.refs_3_.refs_5_
  275.1 16.6 %shard_map.284 = (bf16[160,2048]{1,0:T(8,128)(2,1)}, bf16[160,2048]{1,0:T(8,128)(2,1)}, bf16[2560,2048]{1,0:T(8,128)(2,1)}, bf16[2560,512]{1,0:T(8,128)(2,1)}, b...) custom-call(bf16[160,2048]{1,0:T(8,128)(2,1)} %copy-done.35, ...), custom_call_target="tpu_custom_call" | custom-call | flops 6710886400 | bytes 18481152 | tf_op jit(solution)/shard_map/pallas_call | solution.py:489
  294.4 24.1 %shard_map.285 = (bf16[320,2048]{1,0:T(8,128)(2,1)}, bf16[320,2048]{1,0:T(8,128)(2,1)}, bf16[2560,2048]{1,0:T(8,128)(2,1)}, bf16[2560,512]{1,0:T(8,128)(2,1)}, b...) custom-call(bf16[160,2048]{1,0:T(8,128)(2,1)} %copy-done.46, ...), custom_call_target="tpu_custom_call", output_to_operand_aliasing={{2}: (16, {}), {3}: (17, {}), {4}: (18, {}), {5}: (19, {}),... | custom-call | flops 13421772800 | bytes 24379392 | tf_op jit(solution)/shard_map/pallas_call | solution.py:489
  319.5 2.3 collective-permute-start.30
  323.0 24.0 %shard_map.286 = (bf16[320,2048]{1,0:T(8,128)(2,1)}, bf16[320,2048]{1,0:T(8,128)(2,1)}, bf16[2560,2048]{1,0:T(8,128)(2,1)}, bf16[2560,512]{1,0:T(8,128)(2,1)}, b...) custom-call(bf16[160,2048]{1,0:T(8,128)(2,1)} %copy-done.44, ...), custom_call_target="tpu_custom_call", output_to_operand_aliasing={{2}: (16, {}), {3}: (17, {}), {4}: (18, {}), {5}: (19, {}),... | custom-call | flops 13421772800 | bytes 24379392 | tf_op jit(solution)/shard_map/pallas_call | solution.py:489
  348.7 24.0 %shard_map.287 = (bf16[320,2048]{1,0:T(8,128)(2,1)}, bf16[320,2048]{1,0:T(8,128)(2,1)}, bf16[2560,2048]{1,0:T(8,128)(2,1)}, bf16[2560,512]{1,0:T(8,128)(2,1)}, b...) custom-call(bf16[160,2048]{1,0:T(8,128)(2,1)} %copy-done.37, ...), custom_call_target="tpu_custom_call", output_to_operand_aliasing={{2}: (16, {}), {3}: (17, {}), {4}: (18, {}), {5}: (19, {}),... | custom-call | flops 13421772800 | bytes 24379392 | tf_op jit(solution)/shard_map/pallas_call | solution.py:489
  373.8 16.8 %shard_map.288 = (bf16[160,2048]{1,0:T(8,128)(2,1)}, bf16[160,2048]{1,0:T(8,128)(2,1)}, bf16[2560,2048]{1,0:T(8,128)(2,1)}, bf16[2560,512]{1,0:T(8,128)(2,1)}, b...) custom-call(bf16[80,2048]{1,0:T(8,128)(2,1)} %copy-done.55, ...), custom_call_target="tpu_custom_call", output_to_operand_aliasing={{2}: (16, {}), {3}: (17, {}), {4}: (18, {}), {5}: (19, {}),... | custom-call | flops 6710886400 | bytes 18481152 | tf_op jit(solution)/shard_map/pallas_call | solution.py:489
  391.0 10.3 %convolution_convert_fusion.4 = bf16[512,2048]{1,0:T(8,128)(2,1)} fusion(bf16[2560,512]{1,0:T(8,128)(2,1)} %get-tuple-element.172, bf16[2560,2048]{1,0:T(8,128)(2,1)} %bitcast.150), kind=kOutput, calls=%fused_computation.11 | convolution fusion | flops 5369757696 | bytes 15204352 | tf_op jit(solution)/shard_map/dot_general | solution.py:129
  405.3 7.6 collective-permute-done.38
  415.9 6.9 convolution_convert_fusion.3
  423.6 7.6 collective-permute-done.39
  433.8 11.8 %fusion.71 = f32[2560,2048]{1,0:T(8,128)} fusion(bf16[2560,512]{1,0:T(8,128)(2,1)S(1)} %copy-done.11, bf16[512,2048]{1,0:T(8,128)(2,1)} %collective-permute-done.10.refs_9_.refs_11_), kind=kOutput, calls=%fused_computation.277 | convolution fusion | flops 5368709120 | bytes 25690112 | tf_op jit(solution)/shard_map/dot_general | solution.py:125
  445.6 13.0 %add_convert_fusion = bf16[2560,2048]{1,0:T(8,128)(2,1)} fusion(f32[2560,2048]{1,0:T(8,128)} %fusion.71, bf16[2560,512]{1,0:T(8,128)(2,1)S(1)} %copy-done.10, bf16[512,2048]{1,0:T(8,128)(2,1)} %bitcast.14.refs_8_.refs_10_), kind=kOutput, calls=%fused_computation.3 | convolution fusion | flops 5379194880 | bytes 36175872 | tf_op jit(solution)/shard_map/dot_general | solution.py:125
  461.3 10.7 %fusion.73 = f32[2048,512]{1,0:T(8,128)} fusion(bf16[2560,2048]{1,0:T(8,128)(2,1)} %get-tuple-element.182, bf16[2560,512]{1,0:T(8,128)(2,1)S(1)} %copy-done.12), kind=kOutput, calls=%fused_computation.279 | convolution fusion | flops 5368709120 | bytes 17301504 | tf_op jit(solution)/shard_map/dot_general | solution.py:129
  472.0 7.1 fusion.74
  479.2 7.2 fusion.72
  487.9 6.3 collective-permute-done.43
  494.2 9.7 %gather_fusion.2 = bf16[16,160,2048]{2,1,0:T(8,128)(2,1)} fusion(bf16[16,160,2048]{2,1,0:T(8,128)(2,1)} %bitcast.185, s32[1024]{0:T(1024)} %pad_clamp_fusion), kind=kCustom, calls=%fused_computation.2 | custom fusion | bytes 20971584 | tf_op jit(solution)/shard_map/gather | solution.py:729
  505.7 117.9 %reduce-scatter.2.cloned.1.call-done = bf16[160,2048]{1,0:T(8,128)(2,1)} async-done(((bf16[2560,2048]{1,0:T(8,128)(2,1)}), bf16[160,2048]{1,0:T(8,128)(2,1)}) %reduce-scatter.2.cloned.1.call-update) | async-done | bytes 655376 | tf_op jit(solution)/shard_map/reduce_scatter | solution.py:732
  623.6 4.2 fusion.62
  629.3 11.6 %convolution_convert_fusion.2 = bf16[2048,512]{1,0:T(8,128)(2,1)} fusion(bf16[2560,2048]{1,0:T(8,128)(2,1)} %get-tuple-element.182, bf16[2560,512]{1,0:T(8,128)(2,1)S(1)} %copy-done.15), kind=kOutput, calls=%fused_computation.9 | convolution fusion | flops 5369757696 | bytes 15204352 | tf_op jit(solution)/shard_map/dot_general | solution.py:129
  640.9 3.2 collective-permute-done.45
  645.4 3.8 convolution_convert_fusion.5.refs_4_
  649.2 20.0 %shard_map.289 = (f32[320,1024]{1,0:T(8,128)}, f32[320,1]{1,0:T(8,128)}, f32[1,1024]{1,0:T(1,128)}, f32[320,1024]{1,0:T(8,128)}, f32[320,1024]{1,0:T(8,128)}, /*...) custom-call(bf16[320,1024]{1,0:T(8,128)(2,1)} %get-tuple-element.111.q_ref.refs_0_, ...), custom_call_target="tpu_custom_call" | custom-call | tf_op jit(solution)/shard_map/pallas_call | solution.py:272
  671.0 5.6 add_bitcast_fusion.2
  683.4 4.3 add_bitcast_fusion
  689.6 4.4 collective-permute-done.47
  698.7 2.7 collective-permute-done.48.refs_9_
  703.5 7.8 shard_map.290
  711.3 13.2 %collective-permute-done.51 = bf16[2048,512]{1,0:T(8,128)(2,1)S(1)} collective-permute-done((bf16[2048,512]{1,0:T(8,128)(2,1)}, bf16[2048,512]{1,0:T(8,128)(2,1)S(1)}, u32[]{:S(2)}, u32[]{:S(2)}) %collective-permute-start.51) | collective-permute-done | bytes 2097184 | tf_op jit(solution)/shard_map/ppermute | solution.py:25
  726.7 5.1 all-reduce.3
  733.5 3.9 fusion.75
  745.4 3.6 convolution_convert_fusion.1
  749.6 10.0 %collective-permute-done.52 = bf16[160,2048]{1,0:T(8,128)(2,1)S(1)} collective-permute-done((bf16[160,2048]{1,0:T(8,128)(2,1)S(1)}, bf16[160,2048]{1,0:T(8,128)(2,1)S(1)}, u32[]{:S(2)}, u32[]{:S(2)}) %collective-permute-start.52) | collective-permute-done | bytes 655392 | tf_op jit(solution)/shard_map/ppermute | solution.py:25
  760.2 2.4 collective-permute-start.54
  762.6 11.2 %convolution_convert_fusion = bf16[2048,1536]{0,1:T(8,128)(2,1)S(1)} fusion(bf16[320,2048]{1,0:T(8,128)(2,1)} %collective-permute-done.59, bf16[320,2048]{1,0:T(8,128)(2,1)} %multiply_convert_fusion, bf16[320,1536]{1,0:T(8,128)(2,1)S(1)} %collective-permute-done.60, bf16[320,512]{1,0:T(8,128)(2,1)S(1)} %get-tuple-element.318, ...), kind=kOutput, calls=%fused_computation.4 | convolution fusion | flops 4042784768 | bytes 10878976 | tf_op jit(solution)/shard_map/dot_general | solution.py:129
  776.3 8.6 collective-permute-done.44
  789.1 8.0 collective-permute-done.63
  801.2 10.3 %collective-permute-done.68 = bf16[256,2048]{0,1:T(8,128)(2,1)S(1)} collective-permute-done((bf16[256,2048]{0,1:T(8,128)(2,1)S(1)}, bf16[256,2048]{0,1:T(8,128)(2,1)S(1)}, u32[]{:S(2)}, u32[]{:S(2)}) %collective-permute-start.68) | collective-permute-done | bytes 1048608 | tf_op jit(solution)/shard_map/ppermute | solution.py:40
  812.5 7.9 collective-permute-done.64
  822.5 12.3 %collective-permute-done.69 = bf16[256,2048]{0,1:T(8,128)(2,1)S(1)} collective-permute-done((bf16[256,2048]{0,1:T(8,128)(2,1)S(1)}, bf16[256,2048]{0,1:T(8,128)(2,1)S(1)}, u32[]{:S(2)}, u32[]{:S(2)}) %collective-permute-start.69) | collective-permute-done | bytes 1048608 | tf_op jit(solution)/shard_map/ppermute | solution.py:40
  835.9 7.9 collective-permute-done.65
  848.3 2.8 add_bitcast_fusion.1
  851.1 17.9 %collective-permute-done.58 = f32[4,128]{1,0:T(4,128)S(1)} collective-permute-done((f32[4,128]{1,0:T(4,128)S(1)}, f32[4,128]{1,0:T(4,128)S(1)}, u32[]{:S(2)}, u32[]{:S(2)}) %collective-permute-start.58) | collective-permute-done | bytes 2080 | tf_op jit(solution)/shard_map/ppermute | solution.py:25
  (466 shorter events, 128.9 us)
Async XLA Ops:
  7.2 108.3 %all-gather.5.cloned.1.call-start = ((), (), s32[]{:S(2)}) async-start(), calls=%async_computation.2 | async-start | bytes 18382848 | tf_op jit(solution)/shard_map/all_gather | solution.py:600
  19.4 236.9 %all-gather.7.cloned.1.call-start = ((), (), s32[]{:S(2)}) async-start(), calls=%async_computation.3 | async-start | bytes 11141120 | tf_op jit(solution)/shard_map/all_gather | solution.py:638
  21.7 601.9 %reduce-scatter.2.cloned.1.call-start = ((), (), s32[]{:S(2)}) async-start(), calls=%async_computation.1 | async-start | bytes 11141120 | tf_op jit(solution)/shard_map/reduce_scatter | solution.py:732
  21.8 49.6 %collective-permute-start = (bf16[2048,512]{1,0:T(8,128)(2,1)S(1)}, bf16[2048,512]{1,0:T(8,128)(2,1)}, u32[]{:S(2)}, u32[]{:S(2)}) collective-permute-start(bf16[2048,512]{1,0:T(8,128)(2,1)S(1)} %bitcast.164), channel_id=1, source_target_pairs={{0,1},{1,0},{2,3},{3,2},{4,5},{5,4},{6,7},{7,6},{8,9},{9,8},{10,11... | collective-permute-start | bytes 6291464 | tf_op jit(solution)/shard_map/ppermute | solution.py:25
  24.8 90.7 %collective-permute-start.1 = (bf16[2048,512]{1,0:T(8,128)(2,1)}, bf16[2048,512]{1,0:T(8,128)(2,1)}, u32[]{:S(2)}, u32[]{:S(2)}) collective-permute-start(bf16[2048,512]{1,0:T(8,128)(2,1)} %bitcast.165), channel_id=1, source_target_pairs={{0,1},{1,0},{2,3},{3,2},{4,5},{5,4},{6,7},{7,6},{8,9},{9,8},{10,11... | collective-permute-start | bytes 6291464 | tf_op jit(solution)/shard_map/ppermute | solution.py:25
  160.3 24.7 %collective-permute-start.3 = (bf16[2,128,1024]{2,1,0:T(8,128)(2,1)}, bf16[2,128,1024]{2,1,0:T(8,128)(2,1)S(1)}, u32[]{:S(2)}, u32[]{:S(2)}) collective-permute-start(bf16[2,128,1024]{2,1,0:T(8,128)(2,1)} %pad_maximum_fusion.9), channel_id=1, source_target_pairs={{0,4},{2,6},{4,0},{6,2},{8,12},{10,14},{12,8},{14,10},{16,20},{18,... | collective-permute-start | bytes 1572872 | tf_op jit(solution)/shard_map/ppermute | solution.py:21
  161.9 34.2 %collective-permute-start.5 = (bf16[2,128,1024]{2,1,0:T(8,128)(2,1)}, bf16[2,128,1024]{2,1,0:T(8,128)(2,1)S(1)}, u32[]{:S(2)}, u32[]{:S(2)}) collective-permute-start(bf16[2,128,1024]{2,1,0:T(8,128)(2,1)} %pad_maximum_fusion.9), channel_id=1, source_target_pairs={{0,8},{2,10},{4,12},{6,14},{8,0},{10,2},{12,4},{14,6},{16,24},{18,... | collective-permute-start | bytes 1572872 | tf_op jit(solution)/shard_map/ppermute | solution.py:21
  163.6 64.1 %collective-permute-start.10 = (bf16[512,2048]{1,0:T(8,128)(2,1)}, bf16[512,2048]{1,0:T(8,128)(2,1)}, u32[]{:S(2)}, u32[]{:S(2)}) collective-permute-start(bf16[512,2048]{1,0:T(8,128)(2,1)} %bitcast.14.refs_8_.refs_10_), channel_id=1, source_target_pairs={{0,1},{1,0},{2,3},{3,2},{4,5},{5,4},{6,7},{7,6},{8,9},{9,8},{10,11... | collective-permute-start | bytes 6291464 | tf_op jit(solution)/shard_map/ppermute | solution.py:25
  185.0 23.4 %collective-permute-start.8 = (bf16[128,1024]{1,0:T(8,128)(2,1)S(1)}, bf16[128,1024]{1,0:T(8,128)(2,1)S(1)}, u32[]{:S(2)}, u32[]{:S(2)}) collective-permute-start(bf16[128,1024]{1,0:T(8,128)(2,1)S(1)} %slice_bitcast_fusion.10), channel_id=1, source_target_pairs={{0,8},{2,10},{4,12},{6,14},{8,0},{10,2},{12,4},{14,6},{16,24},{18,... | collective-permute-start | bytes 786440 | tf_op jit(solution)/shard_map/ppermute | solution.py:21
  196.2 12.2 %collective-permute-start.7 = (bf16[128,1024]{1,0:T(8,128)(2,1)S(1)}, bf16[128,1024]{1,0:T(8,128)(2,1)S(1)}, u32[]{:S(2)}, u32[]{:S(2)}) collective-permute-start(bf16[128,1024]{1,0:T(8,128)(2,1)S(1)} %slice_bitcast_fusion.11), channel_id=1, source_target_pairs={{0,4},{2,6},{4,0},{6,2},{8,12},{10,14},{12,8},{14,10},{16,20},{18,... | collective-permute-start | bytes 786440 | tf_op jit(solution)/shard_map/ppermute | solution.py:21
  199.1 13.2 %collective-permute-start.2 = (bf16[2,128,1024]{2,1,0:T(8,128)(2,1)}, bf16[2,128,1024]{2,1,0:T(8,128)(2,1)}, u32[]{:S(2)}, u32[]{:S(2)}) collective-permute-start(bf16[2,128,1024]{2,1,0:T(8,128)(2,1)} %pad_maximum_fusion.9), channel_id=1, source_target_pairs={{0,2},{2,0},{4,6},{6,4},{8,10},{10,8},{12,14},{14,12},{16,18},{18,... | collective-permute-start | bytes 1572872 | tf_op jit(solution)/shard_map/ppermute | solution.py:21
  199.1 13.2 %collective-permute-start.4 = (bf16[2,128,1024]{2,1,0:T(8,128)(2,1)S(1)}, bf16[2,128,1024]{2,1,0:T(8,128)(2,1)}, u32[]{:S(2)}, u32[]{:S(2)}) collective-permute-start(bf16[2,128,1024]{2,1,0:T(8,128)(2,1)S(1)} %collective-permute-done.3), channel_id=1, source_target_pairs={{0,2},{2,0},{4,6},{6,4},{8,10},{10,8},{12,14},{14,12},{16,18},{18,... | collective-permute-start | bytes 1572872 | tf_op jit(solution)/shard_map/ppermute | solution.py:21
  229.3 16.9 %collective-permute-start.11 = (bf16[160,2048]{1,0:T(8,128)(2,1)}, bf16[160,2048]{1,0:T(8,128)(2,1)S(1)}, u32[]{:S(2)}, u32[]{:S(2)}) collective-permute-start(bf16[160,2048]{1,0:T(8,128)(2,1)} %dynamic-slice_convert_fusion.1), channel_id=1, source_target_pairs={{0,1},{1,0},{2,3},{3,2},{4,5},{5,4},{6,7},{7,6},{8,9},{9,8},{10,11... | collective-permute-start | bytes 1966088 | tf_op jit(solution)/shard_map/ppermute | solution.py:25
  249.7 20.0 %collective-permute-start.14 = (bf16[160,2048]{1,0:T(8,128)(2,1)S(1)}, bf16[160,2048]{1,0:T(8,128)(2,1)S(1)}, u32[]{:S(2)}, u32[]{:S(2)}) collective-permute-start(bf16[160,2048]{1,0:T(8,128)(2,1)S(1)} %multiply_convert_fusion.1.refs_0_), channel_id=1, source_target_pairs={{0,8},{2,10},{8,16},{10,18},{16,24},{18,26},{24,28},{26,30},{28,20... | collective-permute-start | bytes 1966088 | tf_op jit(solution)/shard_map/ppermute | solution.py:36
  249.8 20.0 %collective-permute-start.15 = (bf16[160,2048]{1,0:T(8,128)(2,1)S(1)}, bf16[160,2048]{1,0:T(8,128)(2,1)S(1)}, u32[]{:S(2)}, u32[]{:S(2)}) collective-permute-start(bf16[160,2048]{1,0:T(8,128)(2,1)S(1)} %multiply_convert_fusion.1.refs_0_), channel_id=1, source_target_pairs={{8,0},{10,2},{16,8},{18,10},{24,16},{26,18},{28,24},{30,26},{20,28... | collective-permute-start | bytes 1966088 | tf_op jit(solution)/shard_map/ppermute | solution.py:40
  269.7 22.4 %collective-permute-start.19 = (bf16[160,2048]{1,0:T(8,128)(2,1)S(1)}, bf16[160,2048]{1,0:T(8,128)(2,1)S(1)}, u32[]{:S(2)}, u32[]{:S(2)}) collective-permute-start(bf16[160,2048]{1,0:T(8,128)(2,1)S(1)} %collective-permute-done.14.refs_0_), channel_id=1, source_target_pairs={{0,8},{2,10},{8,16},{10,18},{16,24},{18,26},{24,28},{26,30},{28,20... | collective-permute-start | bytes 1966088 | tf_op jit(solution)/shard_map/ppermute | solution.py:36
  269.7 22.7 %collective-permute-start.16 = (bf16[160,2048]{1,0:T(8,128)(2,1)S(1)}, bf16[160,2048]{1,0:T(8,128)(2,1)}, u32[]{:S(2)}, u32[]{:S(2)}) collective-permute-start(bf16[160,2048]{1,0:T(8,128)(2,1)S(1)} %collective-permute-done.14.refs_0_), channel_id=1, source_target_pairs={{0,2},{2,0},{4,6},{6,4},{8,10},{10,8},{12,14},{14,12},{16,18},{18,... | collective-permute-start | bytes 1966088 | tf_op jit(solution)/shard_map/ppermute | solution.py:21
  269.7 22.4 %collective-permute-start.20 = (bf16[160,2048]{1,0:T(8,128)(2,1)S(1)}, bf16[160,2048]{1,0:T(8,128)(2,1)S(1)}, u32[]{:S(2)}, u32[]{:S(2)}) collective-permute-start(bf16[160,2048]{1,0:T(8,128)(2,1)S(1)} %collective-permute-done.15.refs_1_), channel_id=1, source_target_pairs={{8,0},{10,2},{16,8},{18,10},{24,16},{26,18},{28,24},{30,26},{20,28... | collective-permute-start | bytes 1966088 | tf_op jit(solution)/shard_map/ppermute | solution.py:40
  272.0 22.3 %collective-permute-start.17 = (bf16[160,2048]{1,0:T(8,128)(2,1)S(1)}, bf16[160,2048]{1,0:T(8,128)(2,1)}, u32[]{:S(2)}, u32[]{:S(2)}) collective-permute-start(bf16[160,2048]{1,0:T(8,128)(2,1)S(1)} %collective-permute-done.15.refs_1_), channel_id=1, source_target_pairs={{0,2},{2,0},{4,6},{6,4},{8,10},{10,8},{12,14},{14,12},{16,18},{18,... | collective-permute-start | bytes 1966088 | tf_op jit(solution)/shard_map/ppermute | solution.py:21
  291.7 194.6 %collective-permute-start.13 = (bf16[160,2048]{1,0:T(8,128)(2,1)}, bf16[160,2048]{1,0:T(8,128)(2,1)}, u32[]{:S(2)}, u32[]{:S(2)}) collective-permute-start(bf16[160,2048]{1,0:T(8,128)(2,1)} %get-tuple-element.119), channel_id=1, source_target_pairs={{0,2},{2,0},{4,6},{6,4},{8,10},{10,8},{12,14},{14,12},{16,18},{18,... | collective-permute-start | bytes 1966088 | tf_op jit(solution)/shard_map/ppermute | solution.py:21
  292.1 26.4 %collective-permute-start.24 = (bf16[160,2048]{1,0:T(8,128)(2,1)S(1)}, bf16[160,2048]{1,0:T(8,128)(2,1)S(1)}, u32[]{:S(2)}, u32[]{:S(2)}) collective-permute-start(bf16[160,2048]{1,0:T(8,128)(2,1)S(1)} %collective-permute-done.19.refs_0_), channel_id=1, source_target_pairs={{0,8},{2,10},{8,16},{10,18},{16,24},{18,26},{24,28},{26,30},{28,20... | collective-permute-start | bytes 1966088 | tf_op jit(solution)/shard_map/ppermute | solution.py:36
  292.2 29.7 %collective-permute-start.21 = (bf16[160,2048]{1,0:T(8,128)(2,1)S(1)}, bf16[160,2048]{1,0:T(8,128)(2,1)S(1)}, u32[]{:S(2)}, u32[]{:S(2)}) collective-permute-start(bf16[160,2048]{1,0:T(8,128)(2,1)S(1)} %collective-permute-done.19.refs_0_), channel_id=1, source_target_pairs={{0,2},{2,0},{4,6},{6,4},{8,10},{10,8},{12,14},{14,12},{16,18},{18,... | collective-permute-start | bytes 1966088 | tf_op jit(solution)/shard_map/ppermute | solution.py:21
  292.4 26.3 %collective-permute-start.25 = (bf16[160,2048]{1,0:T(8,128)(2,1)S(1)}, bf16[160,2048]{1,0:T(8,128)(2,1)S(1)}, u32[]{:S(2)}, u32[]{:S(2)}) collective-permute-start(bf16[160,2048]{1,0:T(8,128)(2,1)S(1)} %collective-permute-done.20.refs_1_), channel_id=1, source_target_pairs={{8,0},{10,2},{16,8},{18,10},{24,16},{26,18},{28,24},{30,26},{20,28... | collective-permute-start | bytes 1966088 | tf_op jit(solution)/shard_map/ppermute | solution.py:40
  294.3 27.6 %collective-permute-start.22 = (bf16[160,2048]{1,0:T(8,128)(2,1)S(1)}, bf16[160,2048]{1,0:T(8,128)(2,1)S(1)}, u32[]{:S(2)}, u32[]{:S(2)}) collective-permute-start(bf16[160,2048]{1,0:T(8,128)(2,1)S(1)} %collective-permute-done.20.refs_1_), channel_id=1, source_target_pairs={{0,2},{2,0},{4,6},{6,4},{8,10},{10,8},{12,14},{14,12},{16,18},{18,... | collective-permute-start | bytes 1966088 | tf_op jit(solution)/shard_map/ppermute | solution.py:21
  318.6 28.4 %collective-permute-start.29 = (bf16[80,2048]{1,0:T(8,128)(2,1)S(1)}, bf16[80,2048]{1,0:T(8,128)(2,1)S(1)}, u32[]{:S(2)}, u32[]{:S(2)}) collective-permute-start(bf16[80,2048]{1,0:T(8,128)(2,1)S(1)} %slice.296), channel_id=1, source_target_pairs={{0,8},{2,10},{8,16},{10,18},{16,24},{18,26},{24,28},{26,30},{28,20... | collective-permute-start | bytes 983048 | tf_op jit(solution)/shard_map/ppermute | solution.py:36
  319.5 27.7 %collective-permute-start.30 = (bf16[80,2048]{1,0:T(8,128)(2,1)}, bf16[80,2048]{1,0:T(8,128)(2,1)S(1)}, u32[]{:S(2)}, u32[]{:S(2)}) collective-permute-start(bf16[80,2048]{1,0:T(8,128)(2,1)} %slice.297), channel_id=1, source_target_pairs={{8,0},{10,2},{16,8},{18,10},{24,16},{26,18},{28,24},{30,26},{20,28... | collective-permute-start | bytes 983048 | tf_op jit(solution)/shard_map/ppermute | solution.py:40
  321.8 25.7 %collective-permute-start.26 = (bf16[160,2048]{1,0:T(8,128)(2,1)S(1)}, bf16[160,2048]{1,0:T(8,128)(2,1)S(1)}, u32[]{:S(2)}, u32[]{:S(2)}) collective-permute-start(bf16[160,2048]{1,0:T(8,128)(2,1)S(1)} %collective-permute-done.24.refs_0_), channel_id=1, source_target_pairs={{0,2},{2,0},{4,6},{6,4},{8,10},{10,8},{12,14},{14,12},{16,18},{18,... | collective-permute-start | bytes 1966088 | tf_op jit(solution)/shard_map/ppermute | solution.py:21
  321.9 25.9 %collective-permute-start.27 = (bf16[160,2048]{1,0:T(8,128)(2,1)S(1)}, bf16[160,2048]{1,0:T(8,128)(2,1)S(1)}, u32[]{:S(2)}, u32[]{:S(2)}) collective-permute-start(bf16[160,2048]{1,0:T(8,128)(2,1)S(1)} %collective-permute-done.25.refs_1_), channel_id=1, source_target_pairs={{0,2},{2,0},{4,6},{6,4},{8,10},{10,8},{12,14},{14,12},{16,18},{18,... | collective-permute-start | bytes 1966088 | tf_op jit(solution)/shard_map/ppermute | solution.py:21
  347.0 54.2 %collective-permute-start.18 = (bf16[320,2048]{1,0:T(8,128)(2,1)}, bf16[320,2048]{1,0:T(8,128)(2,1)S(1)}, u32[]{:S(2)}, u32[]{:S(2)}) collective-permute-start(bf16[320,2048]{1,0:T(8,128)(2,1)} %get-tuple-element.128), channel_id=1, source_target_pairs={{0,2},{2,0},{4,6},{6,4},{8,10},{10,8},{12,14},{14,12},{16,18},{18,... | collective-permute-start | bytes 3932168 | tf_op jit(solution)/shard_map/ppermute | solution.py:21
  347.3 56.1 %collective-permute-start.23 = (bf16[320,2048]{1,0:T(8,128)(2,1)}, bf16[320,2048]{1,0:T(8,128)(2,1)S(1)}, u32[]{:S(2)}, u32[]{:S(2)}) collective-permute-start(bf16[320,2048]{1,0:T(8,128)(2,1)} %get-tuple-element.137), channel_id=1, source_target_pairs={{0,2},{2,0},{4,6},{6,4},{8,10},{10,8},{12,14},{14,12},{16,18},{18,... | collective-permute-start | bytes 3932168 | tf_op jit(solution)/shard_map/ppermute | solution.py:21
  347.6 25.1 %collective-permute-start.31 = (bf16[80,2048]{1,0:T(8,128)(2,1)S(1)}, bf16[80,2048]{1,0:T(8,128)(2,1)S(1)}, u32[]{:S(2)}, u32[]{:S(2)}) collective-permute-start(bf16[80,2048]{1,0:T(8,128)(2,1)S(1)} %collective-permute-done.29.refs_0_), channel_id=1, source_target_pairs={{0,2},{2,0},{4,6},{6,4},{8,10},{10,8},{12,14},{14,12},{16,18},{18,... | collective-permute-start | bytes 983048 | tf_op jit(solution)/shard_map/ppermute | solution.py:21
  347.8 25.2 %collective-permute-start.32 = (bf16[80,2048]{1,0:T(8,128)(2,1)S(1)}, bf16[80,2048]{1,0:T(8,128)(2,1)S(1)}, u32[]{:S(2)}, u32[]{:S(2)}) collective-permute-start(bf16[80,2048]{1,0:T(8,128)(2,1)S(1)} %collective-permute-done.30.refs_1_), channel_id=1, source_target_pairs={{0,2},{2,0},{4,6},{6,4},{8,10},{10,8},{12,14},{14,12},{16,18},{18,... | collective-permute-start | bytes 983048 | tf_op jit(solution)/shard_map/ppermute | solution.py:21
  372.7 40.1 %collective-permute-start.28 = (bf16[320,2048]{1,0:T(8,128)(2,1)}, bf16[320,2048]{1,0:T(8,128)(2,1)S(1)}, u32[]{:S(2)}, u32[]{:S(2)}) collective-permute-start(bf16[320,2048]{1,0:T(8,128)(2,1)} %get-tuple-element.146), channel_id=1, source_target_pairs={{0,2},{2,0},{4,6},{6,4},{8,10},{10,8},{12,14},{14,12},{16,18},{18,... | collective-permute-start | bytes 3932168 | tf_op jit(solution)/shard_map/ppermute | solution.py:21
  401.2 86.7 %collective-permute-start.42 = (bf16[512,2048]{1,0:T(8,128)(2,1)}, bf16[512,2048]{1,0:T(8,128)(2,1)}, u32[]{:S(2)}, u32[]{:S(2)}) collective-permute-start(bf16[512,2048]{1,0:T(8,128)(2,1)} %convolution_convert_fusion.4), channel_id=1, source_target_pairs={{0,1},{1,0},{2,3},{3,2},{4,5},{5,4},{6,7},{7,6},{8,9},{9,8},{10,11... | collective-permute-start | bytes 6291464 | tf_op jit(solution)/shard_map/ppermute | solution.py:25
  413.7 17.6 %collective-permute-start.35 = (bf16[160,2048]{1,0:T(8,128)(2,1)S(1)}, bf16[160,2048]{1,0:T(8,128)(2,1)S(1)}, u32[]{:S(2)}, u32[]{:S(2)}) collective-permute-start(bf16[160,2048]{1,0:T(8,128)(2,1)S(1)} %pad_maximum_fusion.5), channel_id=1, source_target_pairs={{0,8},{2,10},{8,16},{10,18},{16,24},{18,26},{24,28},{26,30},{28,20... | collective-permute-start | bytes 1966088 | tf_op jit(solution)/shard_map/ppermute | solution.py:36
  415.7 15.5 %collective-permute-start.39 = (bf16[160,2048]{1,0:T(8,128)(2,1)S(1)}, bf16[160,2048]{1,0:T(8,128)(2,1)S(1)}, u32[]{:S(2)}, u32[]{:S(2)}) collective-permute-start(bf16[160,2048]{1,0:T(8,128)(2,1)S(1)} %pad_maximum_fusion.6), channel_id=1, source_target_pairs={{8,0},{10,2},{16,8},{18,10},{24,16},{26,18},{28,24},{30,26},{20,28... | collective-permute-start | bytes 1966088 | tf_op jit(solution)/shard_map/ppermute | solution.py:40
  422.7 71.5 %collective-permute-start.43 = (bf16[2048,512]{1,0:T(8,128)(2,1)}, bf16[2048,512]{1,0:T(8,128)(2,1)}, u32[]{:S(2)}, u32[]{:S(2)}) collective-permute-start(bf16[2048,512]{1,0:T(8,128)(2,1)} %convolution_convert_fusion.3), channel_id=1, source_target_pairs={{0,1},{1,0},{2,3},{3,2},{4,5},{5,4},{6,7},{7,6},{8,9},{9,8},{10,11... | collective-permute-start | bytes 6291464 | tf_op jit(solution)/shard_map/ppermute | solution.py:25
  431.7 26.9 %collective-permute-start.36 = (bf16[160,2048]{1,0:T(8,128)(2,1)S(1)}, bf16[160,2048]{1,0:T(8,128)(2,1)S(1)}, u32[]{:S(2)}, u32[]{:S(2)}) collective-permute-start(bf16[160,2048]{1,0:T(8,128)(2,1)S(1)} %get-tuple-element.300), channel_id=1, source_target_pairs={{0,8},{2,10},{8,16},{10,18},{16,24},{18,26},{24,28},{26,30},{28,20... | collective-permute-start | bytes 1966088 | tf_op jit(solution)/shard_map/ppermute | solution.py:36
  433.3 25.3 %collective-permute-start.40 = (bf16[160,2048]{1,0:T(8,128)(2,1)S(1)}, bf16[160,2048]{1,0:T(8,128)(2,1)S(1)}, u32[]{:S(2)}, u32[]{:S(2)}) collective-permute-start(bf16[160,2048]{1,0:T(8,128)(2,1)S(1)} %get-tuple-element.301), channel_id=1, source_target_pairs={{8,0},{10,2},{16,8},{18,10},{24,16},{26,18},{28,24},{30,26},{20,28... | collective-permute-start | bytes 1966088 | tf_op jit(solution)/shard_map/ppermute | solution.py:40
  459.2 27.2 %collective-permute-start.41 = (bf16[160,2048]{1,0:T(8,128)(2,1)S(1)}, bf16[160,2048]{1,0:T(8,128)(2,1)S(1)}, u32[]{:S(2)}, u32[]{:S(2)}) collective-permute-start(bf16[160,2048]{1,0:T(8,128)(2,1)S(1)} %get-tuple-element.299), channel_id=1, source_target_pairs={{8,0},{10,2},{16,8},{18,10},{24,16},{26,18},{28,24},{30,26},{20,28... | collective-permute-start | bytes 1966088 | tf_op jit(solution)/shard_map/ppermute | solution.py:40
  459.4 27.0 %collective-permute-start.37 = (bf16[160,2048]{1,0:T(8,128)(2,1)S(1)}, bf16[160,2048]{1,0:T(8,128)(2,1)S(1)}, u32[]{:S(2)}, u32[]{:S(2)}) collective-permute-start(bf16[160,2048]{1,0:T(8,128)(2,1)S(1)} %get-tuple-element.298), channel_id=1, source_target_pairs={{0,8},{2,10},{8,16},{10,18},{16,24},{18,26},{24,28},{26,30},{28,20... | collective-permute-start | bytes 1966088 | tf_op jit(solution)/shard_map/ppermute | solution.py:36
  627.8 16.3 %collective-permute-start.45 = (bf16[160,2048]{1,0:T(8,128)(2,1)S(1)}, bf16[160,2048]{1,0:T(8,128)(2,1)S(1)}, u32[]{:S(2)}, u32[]{:S(2)}) collective-permute-start(bf16[160,2048]{1,0:T(8,128)(2,1)S(1)} %get-tuple-element.255), channel_id=1, source_target_pairs={{0,1},{1,0},{2,3},{3,2},{4,5},{5,4},{6,7},{7,6},{8,9},{9,8},{10,11... | collective-permute-start | bytes 1966088 | tf_op jit(solution)/shard_map/ppermute | solution.py:25
  669.5 93.1 %collective-permute-start.59 = (bf16[320,2048]{1,0:T(8,128)(2,1)}, bf16[320,2048]{1,0:T(8,128)(2,1)}, u32[]{:S(2)}, u32[]{:S(2)}) collective-permute-start(bf16[320,2048]{1,0:T(8,128)(2,1)} %multiply_convert_fusion), channel_id=1, source_target_pairs={{0,2},{2,0},{4,6},{6,4},{8,10},{10,8},{12,14},{14,12},{16,18},{18,... | collective-permute-start | bytes 3932168 | tf_op jit(solution)/shard_map/ppermute | solution.py:21
  670.6 73.5 %collective-permute-start.62 = (bf16[320,512]{1,0:T(8,128)(2,1)}, bf16[320,512]{1,0:T(8,128)(2,1)}, u32[]{:S(2)}, u32[]{:S(2)}) collective-permute-start(bf16[320,512]{1,0:T(8,128)(2,1)} %get-tuple-element.321), channel_id=1, source_target_pairs={{0,2},{2,0},{4,6},{6,4},{8,10},{10,8},{12,14},{14,12},{16,18},{18,... | collective-permute-start | bytes 983048 | tf_op jit(solution)/shard_map/ppermute | solution.py:21
  676.6 47.9 %collective-permute-start.51 = (bf16[2048,512]{1,0:T(8,128)(2,1)}, bf16[2048,512]{1,0:T(8,128)(2,1)S(1)}, u32[]{:S(2)}, u32[]{:S(2)}) collective-permute-start(bf16[2048,512]{1,0:T(8,128)(2,1)} %convolution_convert_fusion.2), channel_id=1, source_target_pairs={{0,1},{1,0},{2,3},{3,2},{4,5},{5,4},{6,7},{7,6},{8,9},{9,8},{10,11... | collective-permute-start | bytes 6291464 | tf_op jit(solution)/shard_map/ppermute | solution.py:25
  680.2 13.8 %collective-permute-start.47 = (bf16[2,128,1024]{2,1,0:T(8,128)(2,1)S(1)}, bf16[2,128,1024]{2,1,0:T(8,128)(2,1)S(1)}, u32[]{:S(2)}, u32[]{:S(2)}) collective-permute-start(bf16[2,128,1024]{2,1,0:T(8,128)(2,1)S(1)} %pad_maximum_fusion.11), channel_id=1, source_target_pairs={{0,4},{2,6},{4,0},{6,2},{8,12},{10,14},{12,8},{14,10},{16,20},{18,... | collective-permute-start | bytes 1572872 | tf_op jit(solution)/shard_map/ppermute | solution.py:21
  681.9 13.8 %collective-permute-start.49 = (bf16[2,128,1024]{2,1,0:T(8,128)(2,1)S(1)}, bf16[2,128,1024]{2,1,0:T(8,128)(2,1)S(1)}, u32[]{:S(2)}, u32[]{:S(2)}) collective-permute-start(bf16[2,128,1024]{2,1,0:T(8,128)(2,1)S(1)} %pad_maximum_fusion.12), channel_id=1, source_target_pairs={{0,8},{2,10},{4,12},{6,14},{8,0},{10,2},{12,4},{14,6},{16,24},{18,... | collective-permute-start | bytes 1572872 | tf_op jit(solution)/shard_map/ppermute | solution.py:21
  701.4 43.9 %collective-permute-start.61 = (bf16[320,2048]{1,0:T(8,128)(2,1)}, bf16[320,2048]{1,0:T(8,128)(2,1)}, u32[]{:S(2)}, u32[]{:S(2)}) collective-permute-start(bf16[320,2048]{1,0:T(8,128)(2,1)} %pad_maximum_fusion.2), channel_id=1, source_target_pairs={{0,2},{2,0},{4,6},{6,4},{8,10},{10,8},{12,14},{14,12},{16,18},{18,... | collective-permute-start | bytes 3932168 | tf_op jit(solution)/shard_map/ppermute | solution.py:21
  741.9 17.7 %collective-permute-start.52 = (bf16[160,2048]{1,0:T(8,128)(2,1)S(1)}, bf16[160,2048]{1,0:T(8,128)(2,1)S(1)}, u32[]{:S(2)}, u32[]{:S(2)}) collective-permute-start(bf16[160,2048]{1,0:T(8,128)(2,1)S(1)} %dynamic-slice_convert_fusion), channel_id=1, source_target_pairs={{0,1},{1,0},{2,3},{3,2},{4,5},{5,4},{6,7},{7,6},{8,9},{9,8},{10,11... | collective-permute-start | bytes 1966088 | tf_op jit(solution)/shard_map/ppermute | solution.py:25
  743.7 18.9 %collective-permute-start.60 = (bf16[320,1536]{1,0:T(8,128)(2,1)S(1)}, bf16[320,1536]{1,0:T(8,128)(2,1)S(1)}, u32[]{:S(2)}, u32[]{:S(2)}) collective-permute-start(bf16[320,1536]{1,0:T(8,128)(2,1)S(1)} %pad_maximum_fusion.4), channel_id=1, source_target_pairs={{0,2},{2,0},{4,6},{6,4},{8,10},{10,8},{12,14},{14,12},{16,18},{18,... | collective-permute-start | bytes 2949128 | tf_op jit(solution)/shard_map/ppermute | solution.py:21
  744.8 40.1 %collective-permute-start.44 = (f32[160,2048]{1,0:T(8,128)S(1)}, f32[160,2048]{1,0:T(8,128)S(1)}, u32[]{:S(2)}, u32[]{:S(2)}) collective-permute-start(f32[160,2048]{1,0:T(8,128)S(1)} %copy-done.26), channel_id=1, source_target_pairs={{0,1},{1,0},{2,3},{3,2},{4,5},{5,4},{6,7},{7,6},{8,9},{9,8},{10,11... | collective-permute-start | bytes 3932168 | tf_op jit(solution)/shard_map/ppermute | solution.py:25
  760.2 24.9 %collective-permute-start.54 = (f32[8,4,128]{2,1,0:T(4,128)S(1)}, f32[8,4,128]{2,1,0:T(4,128)S(1)}, u32[]{:S(2)}, u32[]{:S(2)}) collective-permute-start(f32[8,4,128]{2,1,0:T(4,128)S(1)} %dynamic-slice_bitcast_fusion), channel_id=1, source_target_pairs={{0,16},{2,18},{4,20},{6,22},{8,24},{10,26},{12,28},{14,30},{16,0},... | collective-permute-start | bytes 49160 | tf_op jit(solution)/shard_map/ppermute | solution.py:21
  774.7 13.5 %collective-permute-start.67 = (bf16[256,1024]{0,1:T(8,128)(2,1)S(1)}, bf16[256,1024]{0,1:T(8,128)(2,1)S(1)}, u32[]{:S(2)}, u32[]{:S(2)}) collective-permute-start(bf16[256,1024]{0,1:T(8,128)(2,1)S(1)} %pad_maximum_fusion.7), channel_id=1, source_target_pairs={{8,0},{10,2},{16,8},{18,10},{24,16},{26,18},{28,24},{30,26},{20,28... | collective-permute-start | bytes 1572872 | tf_op jit(solution)/shard_map/ppermute | solution.py:40
  786.8 13.9 %collective-permute-start.55 = (f32[4,4,128]{2,1,0:T(4,128)S(1)}, f32[4,4,128]{2,1,0:T(4,128)S(1)}, u32[]{:S(2)}, u32[]{:S(2)}) collective-permute-start(f32[4,4,128]{2,1,0:T(4,128)S(1)} %constant_dynamic-slice_fusion.31), channel_id=1, source_target_pairs={{0,8},{2,10},{4,12},{6,14},{8,0},{10,2},{12,4},{14,6},{16,24},{18,... | collective-permute-start | bytes 24584 | tf_op jit(solution)/shard_map/ppermute | solution.py:21
  788.5 23.0 %collective-permute-start.68 = (bf16[256,2048]{0,1:T(8,128)(2,1)S(1)}, bf16[256,2048]{0,1:T(8,128)(2,1)S(1)}, u32[]{:S(2)}, u32[]{:S(2)}) collective-permute-start(bf16[256,2048]{0,1:T(8,128)(2,1)S(1)} %pad_maximum_fusion.3), channel_id=1, source_target_pairs={{8,0},{10,2},{16,8},{18,10},{24,16},{26,18},{28,24},{30,26},{20,28... | collective-permute-start | bytes 3145736 | tf_op jit(solution)/shard_map/ppermute | solution.py:40
  797.3 23.1 %collective-permute-start.64 = (bf16[256,2048]{0,1:T(8,128)(2,1)S(1)}, bf16[256,2048]{0,1:T(8,128)(2,1)S(1)}, u32[]{:S(2)}, u32[]{:S(2)}) collective-permute-start(bf16[256,2048]{0,1:T(8,128)(2,1)S(1)} %fusion.17), channel_id=1, source_target_pairs={{0,8},{2,10},{8,16},{10,18},{16,24},{18,26},{24,28},{26,30},{28,20... | collective-permute-start | bytes 3145736 | tf_op jit(solution)/shard_map/ppermute | solution.py:36
  800.8 21.7 %collective-permute-start.56 = (f32[2,4,128]{2,1,0:T(4,128)S(1)}, f32[2,4,128]{2,1,0:T(4,128)S(1)}, u32[]{:S(2)}, u32[]{:S(2)}) collective-permute-start(f32[2,4,128]{2,1,0:T(4,128)S(1)} %constant_dynamic-slice_fusion.29), channel_id=1, source_target_pairs={{0,4},{2,6},{4,0},{6,2},{8,12},{10,14},{12,8},{14,10},{16,20},{18,... | collective-permute-start | bytes 12296 | tf_op jit(solution)/shard_map/ppermute | solution.py:21
  811.8 23.0 %collective-permute-start.69 = (bf16[256,2048]{0,1:T(8,128)(2,1)S(1)}, bf16[256,2048]{0,1:T(8,128)(2,1)S(1)}, u32[]{:S(2)}, u32[]{:S(2)}) collective-permute-start(bf16[256,2048]{0,1:T(8,128)(2,1)S(1)} %add_convert_fusion.5), channel_id=1, source_target_pairs={{8,0},{10,2},{16,8},{18,10},{24,16},{26,18},{28,24},{30,26},{20,28... | collective-permute-start | bytes 3145736 | tf_op jit(solution)/shard_map/ppermute | solution.py:40
  820.8 23.0 %collective-permute-start.65 = (bf16[256,2048]{0,1:T(8,128)(2,1)S(1)}, bf16[256,2048]{0,1:T(8,128)(2,1)S(1)}, u32[]{:S(2)}, u32[]{:S(2)}) collective-permute-start(bf16[256,2048]{0,1:T(8,128)(2,1)S(1)} %add_convert_fusion.7), channel_id=1, source_target_pairs={{0,8},{2,10},{8,16},{10,18},{16,24},{18,26},{24,28},{26,30},{28,20... | collective-permute-start | bytes 3145736 | tf_op jit(solution)/shard_map/ppermute | solution.py:36
  822.5 25.3 %collective-permute-start.57 = (f32[1,4,128]{2,1,0:T(4,128)S(1)}, f32[1,4,128]{2,1,0:T(4,128)S(1)}, u32[]{:S(2)}, u32[]{:S(2)}) collective-permute-start(f32[1,4,128]{2,1,0:T(4,128)S(1)} %constant_dynamic-slice_fusion.27), channel_id=1, source_target_pairs={{0,2},{2,0},{4,6},{6,4},{8,10},{10,8},{12,14},{14,12},{16,18},{18,... | collective-permute-start | bytes 6152 | tf_op jit(solution)/shard_map/ppermute | solution.py:21
  835.1 33.8 %collective-permute-start.70 = (bf16[256,2048]{0,1:T(8,128)(2,1)S(1)}, bf16[256,2048]{0,1:T(8,128)(2,1)S(1)}, u32[]{:S(2)}, u32[]{:S(2)}) collective-permute-start(bf16[256,2048]{0,1:T(8,128)(2,1)S(1)} %add_convert_fusion.4), channel_id=1, source_target_pairs={{8,0},{10,2},{16,8},{18,10},{24,16},{26,18},{28,24},{30,26},{20,28... | collective-permute-start | bytes 3145736 | tf_op jit(solution)/shard_map/ppermute | solution.py:40
  844.1 24.9 %collective-permute-start.66 = (bf16[256,2048]{0,1:T(8,128)(2,1)S(1)}, bf16[256,2048]{0,1:T(8,128)(2,1)S(1)}, u32[]{:S(2)}, u32[]{:S(2)}) collective-permute-start(bf16[256,2048]{0,1:T(8,128)(2,1)S(1)} %add_convert_fusion.6), channel_id=1, source_target_pairs={{0,8},{2,10},{8,16},{10,18},{16,24},{18,26},{24,28},{26,30},{28,20... | collective-permute-start | bytes 3145736 | tf_op jit(solution)/shard_map/ppermute | solution.py:36
  846.2 23.9 %collective-permute-start.53 = (f32[160,2048]{1,0:T(8,128)S(1)}, f32[160,2048]{1,0:T(8,128)S(1)}, u32[]{:S(2)}, u32[]{:S(2)}) collective-permute-start(f32[160,2048]{1,0:T(8,128)S(1)} %fusion.15), channel_id=1, source_target_pairs={{0,1},{1,0},{2,3},{3,2},{4,5},{5,4},{6,7},{7,6},{8,9},{9,8},{10,11... | collective-permute-start | bytes 3932168 | tf_op jit(solution)/shard_map/ppermute | solution.py:25
  847.7 21.2 %collective-permute-start.58 = (f32[4,128]{1,0:T(4,128)S(1)}, f32[4,128]{1,0:T(4,128)S(1)}, u32[]{:S(2)}, u32[]{:S(2)}) collective-permute-start(f32[4,128]{1,0:T(4,128)S(1)} %fusion.51), channel_id=1, source_target_pairs={{0,1},{1,0},{2,3},{3,2},{4,5},{5,4},{6,7},{7,6},{8,9},{9,8},{10,11... | collective-permute-start | bytes 6152 | tf_op jit(solution)/shard_map/ppermute | solution.py:25
  (105 other events, 1368.0 us)
Sparse Core Ops, SparseCore 0:
  19.5 94.2 all-gather.4
  116.6 101.1 all-gather.6
  504.1 119.4 reduce-scatter.1

commit v4 on v3

--- a/solution.py
+++ b/solution.py
@@ -30,6 +30,7 @@
     (RING[p] * 2 + c, RING[(p + 1) % len(RING)] * 2 + c) for p in range(len(RING)) for c in range(2)
 ]
 BEHIND = [(to, at) for at, to in AHEAD]
+HOPS = (-1, 1, -2, 2, -3, 3, 0, 4)
 
 
 def ahead(block):
@@ -44,11 +45,9 @@
     chip, core = dp_index // 2, dp_index % 2
     place = jnp.where(chip % 2 == 0, chip // 2, 7 - chip // 2)
     steps, cross = [], []
-    for hop in (1, 2, 3):
-        steps += [-hop, hop, -hop, hop]
-        cross += [0, 0, 1, 1]
-    steps += [0, 0, 4, 4]
-    cross += [0, 1, 0, 1]
+    for hop in HOPS:
+        steps += [hop, hop]
+        cross += [0, 1]
     there = (place + jnp.array(steps, jnp.int32)) % 8
     chips = jnp.where(there < 4, 2 * there, 2 * (7 - there) + 1)
     return 2 * chips + (core ^ jnp.array(cross, jnp.int32))
@@ -65,35 +64,34 @@
     return lax.optimization_barrier((value, *others))
 
 
+class Fillers:
+    def __init__(self, stages):
+        self.stages = list(stages)
+        self.outs = []
+
+    def next(self, gate):
+        for work, *operands in self.stages.pop(0) if self.stages else ():
+            gate, *operands = together(gate, *operands)
+            self.outs.append(work(*operands))
+        return gate
+
+
 def ring_sum(same, cross, fillers):
     both = {hop: add_low(same[hop], swap_bit(cross[hop], "dp", 0)) for hop in (4, 3, 2, 1, 0)}
     rows = both[0].shape[0]
     cut = rows // 2
-    done = []
-
-    def fill(gate):
-        for work, *operands in fillers[len(done)]:
-            gate, *operands = together(gate, *operands)
-            done_here.append(work(*operands))
-        done.append(list(done_here))
-        done_here.clear()
-        return gate
-
-    done_here = []
     right, left = ahead(both[4][:cut]), behind(both[4][cut:])
-    left = fill(left)
+    left = fillers.next(left)
     outward, inward = both[3][rows:], both[3][:rows]
     right = jnp.concatenate([add_low(outward[:cut], right), outward[cut:]], axis=0)
     left = jnp.concatenate([inward[:cut], add_low(inward[cut:], left)], axis=0)
     right, left = ahead(right), behind(left)
-    left = fill(left)
+    left = fillers.next(left)
     for hop in (2, 1):
         right = ahead(add_low(both[hop][rows:], right))
         left = behind(add_low(both[hop][:rows], left))
-        if hop == 2:
-            left = fill(left)
-    total = both[0].astype(FULL) + right.astype(FULL) + left.astype(FULL)
-    return total, [out for outs in done for out in outs]
+        left = fillers.next(left)
+    return both[0].astype(FULL) + right.astype(FULL) + left.astype(FULL)
 
 
 def rms_norm(values, gain):
@@ -133,12 +131,11 @@
     return lax.dot_general(left, right, (((1,), (1,)), ((), ())), preferred_element_type=FULL)
 
 
-def collect_prompt(own):
-    near = swap_bit(own, "dp", 1)
-    far = swap_bit(own, "dp", 2)
-    last = jnp.stack([swap_bit(far[0], "dp", 1), swap_bit(near[1], "dp", 2)], axis=0)
-    others = [swap_bit(piece, "dp", 0) for piece in (own, near, far, last)]
-    return [others[0], near, others[1], far, others[2], last, others[3]]
+def collect_prompt(own, first, second):
+    near, far = swap_bit(own, "dp", 1), swap_bit(own, "dp", 2)
+    last = swap_bit(near if first == 1 else far, "dp", second)
+    stay = jnp.stack([own, near, far, last], axis=0)
+    return stay, swap_bit(stay, "dp", 0)
 
 
 def return_prompt(odd, even):
@@ -155,17 +152,32 @@
     return pltpu.roll(values, HEAD // 2, 1)
 
 
-def rope_kernel(q_ref, k_ref, gq_ref, gk_ref, sq_ref, sk_ref, cos_ref, sin_ref, qo_ref, ko_ref):
-    for pre, gain, scale, out in (
-        (q_ref, gq_ref, sq_ref, qo_ref),
-        (k_ref, gk_ref, sk_ref, ko_ref),
-    ):
-        normed = pre[...] * scale[...] * gain[...]
-        out[...] = (normed * cos_ref[...] + turn(normed) * sin_ref[...]).astype(LOW)
+def rope_kernel(pre_ref, gain_ref, scale_ref, cos_ref, sin_ref, out_ref):
+    scale, cosine, sine = scale_ref[...], cos_ref[...], sin_ref[...]
+    for at in range(0, pre_ref.shape[1], HEAD):
+        span = slice(at, at + HEAD)
+        normed = pre_ref[:, span] * scale * gain_ref[:, span]
+        out_ref[:, span] = (normed * cosine + turn(normed) * sine).astype(LOW)
+
+
+def rope_pass(flat, gain, scale, cosine, sine):
+    rows, width = flat.shape
+    part = width // 2
+    wide = lambda rows: pl.BlockSpec((rows, part), lambda h: (0, h))
+    return pl.pallas_call(
+        rope_kernel,
+        grid=(2,),
+        in_specs=[wide(rows), wide(1)] + [kept_spec(a) for a in (scale, cosine, sine)],
+        out_specs=wide(rows),
+        out_shape=jax.ShapeDtypeStruct((rows, width), LOW),
+    )(flat, gain, scale, cosine, sine)
+
+
+PAIR = 2
 
 
 def head_spec(rows):
-    return pl.BlockSpec((rows, HEAD), lambda h: (0, h))
+    return pl.BlockSpec((rows, PAIR * HEAD), lambda h: (0, h))
 
 
 def kept_spec(array):
@@ -174,26 +186,14 @@
 
 
 def piece_spec(count):
-    return pl.BlockSpec((count, 2, PR_DEV, HEAD), lambda h: (0, 0, 0, h))
-
-
-def rope_pass(query_flat, key_flat, gain_q, gain_k, scale_q, scale_k, cosine, sine):
-    rows, width = query_flat.shape
-    return pl.pallas_call(
-        rope_kernel,
-        grid=(width // HEAD,),
-        in_specs=[head_spec(rows)] * 2
-        + [head_spec(1)] * 2
-        + [kept_spec(a) for a in (scale_q, scale_k, cosine, sine)],
-        out_specs=[head_spec(rows)] * 2,
-        out_shape=[jax.ShapeDtypeStruct((rows, width), LOW)] * 2,
-    )(query_flat, key_flat, gain_q, gain_k, scale_q, scale_k, cosine, sine)
-
-
-def all_keys(own_ref, pieces, which):
-    return jnp.concatenate(
-        [own_ref[:PR_DEV]] + [piece[0, which] for piece in pieces] + [own_ref[PR_DEV:]], axis=0
-    )
+    return pl.BlockSpec((count, PR_DEV, PAIR * HEAD), lambda h: (0, 0, h))
+
+
+def all_keys(own_ref, stay_ref, cross_ref, span):
+    blocks = []
+    for j in range(GROUP // 2):
+        blocks += [stay_ref[j, :, span], cross_ref[j, :, span]]
+    return jnp.concatenate(blocks + [own_ref[PR_DEV:, span]], axis=0)
 
 
 def softmax_rows(query, keys, bias):
@@ -202,88 +202,108 @@
     return weights * (1.0 / jnp.sum(weights, axis=1, keepdims=True))
 
 
-def attend_kernel(q_ref, k_ref, v_ref, bias_ref, *refs):
-    pieces, out_ref = refs[:-1], refs[-1]
-    probs = softmax_rows(
-        q_ref[...], all_keys(k_ref, pieces, 0), bias_ref[...].astype(FULL)
-    ).astype(LOW)
-    out_ref[...] = dot_nn(probs, all_keys(v_ref, pieces, 1)).astype(LOW)
+def attend_kernel(q_ref, k_ref, v_ref, bias_ref, k_stay, k_cross, v_stay, v_cross, out_ref):
+    bias = bias_ref[...].astype(FULL)
+    for at in range(0, PAIR * HEAD, HEAD):
+        span = slice(at, at + HEAD)
+        probs = softmax_rows(q_ref[:, span], all_keys(k_ref, k_stay, k_cross, span), bias)
+        out_ref[:, span] = dot_nn(
+            probs.astype(LOW), all_keys(v_ref, v_stay, v_cross, span)
+        ).astype(LOW)
 
 
 def attend(queries, keys, values, bias, pieces):
     rows, width = queries.shape
-    pieces = [piece[None] for piece in pieces]
     return pl.pallas_call(
         attend_kernel,
-        grid=(width // HEAD,),
-        in_specs=[head_spec(rows)] * 3 + [kept_spec(bias)] + [piece_spec(1)] * len(pieces),
+        grid=(width // HEAD // PAIR,),
+        in_specs=[head_spec(rows)] * 3 + [kept_spec(bias)] + [piece_spec(GROUP // 2)] * 4,
         out_specs=head_spec(rows),
         out_shape=jax.ShapeDtypeStruct((rows, width), LOW),
         compiler_params=pltpu.CompilerParams(vmem_limit_bytes=40 * 1024 * 1024),
     )(queries, keys, values, bias, *pieces)
 
 
-def norm_parts(step, grad, flat_ref, gain_ref, scale_ref, inner_ref, gain_grad_ref):
-    product = flat_ref[...] * grad
-    inner = jnp.sum(product * gain_ref[...], axis=1, keepdims=True)
-    gain_grad_ref[...] = jnp.sum(product * scale_ref[...], axis=0, keepdims=True)
-
-    @pl.when(step == 0)
-    def _():
-        inner_ref[...] = inner
-
-    @pl.when(step > 0)
-    def _():
+def norm_parts(step, at, grad, flat_ref, gain_ref, scale_ref, inner_ref, gain_grad_ref):
+    span = slice(at, at + HEAD)
+    product = flat_ref[:, span] * grad
+    inner = jnp.sum(product * gain_ref[:, span], axis=1, keepdims=True)
+    gain_grad_ref[:, span] = jnp.sum(product * scale_ref[...], axis=0, keepdims=True)
+    if at:
         inner_ref[...] += inner
-
-
-def attend_back_kernel(*refs):
-    q_ref, k_ref, v_ref, bias_ref, back_ref, flat_ref, gain_ref, scale_ref, cos_ref, sin_ref = (
-        refs[:10]
-    )
-    pieces = refs[10 : 10 + GROUP - 1]
-    qg_ref, inner_ref, gain_grad_ref, kg_ref, vg_ref, odd_ref, even_ref = refs[10 + GROUP - 1 :]
+    else:
+        inner_ref[...] = jnp.where(step == 0, 0.0, inner_ref[...]) + inner
+
+
+def attend_back_kernel(
+    q_ref,
+    k_ref,
+    v_ref,
+    bias_ref,
+    back_ref,
+    flat_ref,
+    gain_ref,
+    scale_ref,
+    cos_ref,
+    sin_ref,
+    k_stay,
+    k_cross,
+    v_stay,
+    v_cross,
+    qg_ref,
+    inner_ref,
+    gain_grad_ref,
+    kg_ref,
+    vg_ref,
+    odd_ref,
+    even_ref,
+):
     step = pl.program_id(0)
-    query, keys, values = q_ref[...], all_keys(k_ref, pieces, 0), all_keys(v_ref, pieces, 1)
-    back = back_ref[...]
-    probs = softmax_rows(query, keys, bias_ref[...].astype(FULL))
-    prob_grad = dot_nt(back, values)
-    value_grad = dot_tn(probs.astype(LOW), back)
-    row_dot = jnp.sum(probs * prob_grad, axis=1, keepdims=True)
-    score_grad = (probs * (prob_grad - row_dot)).astype(LOW)
-    query_grad = dot_nn(score_grad, keys) * HEAD ** (-0.5)
-    key_grad = dot_tn(score_grad, query) * HEAD ** (-0.5)
-    query_grad = query_grad * cos_ref[...] - turn(query_grad) * sin_ref[...]
-    qg_ref[...] = query_grad
-    norm_parts(step, query_grad, flat_ref, gain_ref, scale_ref, inner_ref, gain_grad_ref)
+    bias = bias_ref[...].astype(FULL)
+    cosine, sine = cos_ref[...], sin_ref[...]
     prompt = PR_DEV * GROUP
-    for which, grad, own_ref in ((0, key_grad, kg_ref), (1, value_grad, vg_ref)):
-        own_ref[:PR_DEV] = grad[:PR_DEV]
-        own_ref[PR_DEV:] = grad[prompt:]
-        for j in range(1, GROUP):
-            to = odd_ref if j % 2 else even_ref
-            to[(j - 1) // 2, which] = grad[j * PR_DEV : (j + 1) * PR_DEV].astype(LOW)
+    for at in range(0, PAIR * HEAD, HEAD):
+        span = slice(at, at + HEAD)
+        query, back = q_ref[:, span], back_ref[:, span]
+        keys = all_keys(k_ref, k_stay, k_cross, span)
+        values = all_keys(v_ref, v_stay, v_cross, span)
+        probs = softmax_rows(query, keys, bias)
+        prob_grad = dot_nt(back, values)
+        value_grad = dot_tn(probs.astype(LOW), back)
+        row_dot = jnp.sum(probs * prob_grad, axis=1, keepdims=True)
+        score_grad = (probs * (prob_grad - row_dot)).astype(LOW)
+        query_grad = dot_nn(score_grad, keys) * HEAD ** (-0.5)
+        key_grad = dot_tn(score_grad, query) * HEAD ** (-0.5)
+        query_grad = query_grad * cosine - turn(query_grad) * sine
+        qg_ref[:, span] = query_grad
+        norm_parts(step, at, query_grad, flat_ref, gain_ref, scale_ref, inner_ref, gain_grad_ref)
+        for which, grad, own_ref in ((0, key_grad, kg_ref), (1, value_grad, vg_ref)):
+            own_ref[:PR_DEV, span] = grad[:PR_DEV]
+            own_ref[PR_DEV:, span] = grad[prompt:]
+            for j in range(1, GROUP):
+                to = odd_ref if j % 2 else even_ref
+                to[(j - 1) // 2, which, :, span] = grad[j * PR_DEV : (j + 1) * PR_DEV].astype(LOW)
 
 
 def attend_back(queries, keys, values, bias, back, flat, gain, scale, cosine, sine, pieces):
     rows, width = queries.shape
-    pieces = [piece[None] for piece in pieces]
     wide = jax.ShapeDtypeStruct((rows, width), FULL)
+    both = lambda count: pl.BlockSpec((count, 2, PR_DEV, PAIR * HEAD), lambda h: (0, 0, 0, h))
     return pl.pallas_call(
         attend_back_kernel,
-        grid=(width // HEAD,),
+        grid=(width // HEAD // PAIR,),
         in_specs=[head_spec(rows)] * 3
         + [kept_spec(bias), head_spec(rows), head_spec(rows), head_spec(1)]
         + [kept_spec(a) for a in (scale, cosine, sine)]
-        + [piece_spec(1)] * len(pieces),
+        + [piece_spec(GROUP // 2)] * 4,
         out_specs=[
             head_spec(rows),
             pl.BlockSpec((rows, 1), lambda h: (0, 0)),
             head_spec(1),
             head_spec(rows),
             head_spec(rows),
-            piece_spec(4),
-            piece_spec(3),
+            both(4),
+            both(3),
         ],
         out_shape=[
             wide,
@@ -303,23 +323,25 @@
     key_parts, value_parts = refs[7:10], refs[10:13]
     out_ref, inner_ref, gain_grad_ref, value_ref = refs[13:]
     step = pl.program_id(0)
-    grads = []
-    for own_ref, parts in ((kg_ref, key_parts), (vg_ref, value_parts)):
-        first = own_ref[:PR_DEV]
-        for part in parts:
-            first = first + part[...].astype(FULL)
-        grads.append(jnp.concatenate([first, own_ref[PR_DEV:]], axis=0))
-    key_grad = grads[0] * cos_ref[...] - turn(grads[0]) * sin_ref[...]
-    out_ref[...] = key_grad
-    norm_parts(step, key_grad, flat_ref, gain_ref, scale_ref, inner_ref, gain_grad_ref)
-    value_ref[...] = grads[1].astype(LOW)
+    for at in range(0, PAIR * HEAD, HEAD):
+        span = slice(at, at + HEAD)
+        grads = []
+        for own_ref, parts in ((kg_ref, key_parts), (vg_ref, value_parts)):
+            first = own_ref[:PR_DEV, span]
+            for part in parts:
+                first = first + part[:, span].astype(FULL)
+            grads.append(jnp.concatenate([first, own_ref[PR_DEV:, span]], axis=0))
+        key_grad = grads[0] * cos_ref[...] - turn(grads[0]) * sin_ref[...]
+        out_ref[:, span] = key_grad
+        norm_parts(step, at, key_grad, flat_ref, gain_ref, scale_ref, inner_ref, gain_grad_ref)
+        value_ref[:, span] = grads[1].astype(LOW)
 
 
 def key_back(key_grad, value_grad, flat, gain, scale, cosine, sine, key_parts, value_parts):
     rows, width = flat.shape
     return pl.pallas_call(
         key_back_kernel,
-        grid=(width // HEAD,),
+        grid=(width // HEAD // PAIR,),
         in_specs=[head_spec(rows)] * 3
         + [head_spec(1)]
         + [kept_spec(a) for a in (scale, cosine, sine)]
@@ -339,7 +361,104 @@
     )(key_grad, value_grad, flat, gain, scale, cosine, sine, *key_parts, *value_parts)
 
 
-def ring_weights(first, second):
+def pack_kernel(query, key, value, out, rest, packed):
+    at = 0
+    for ref in (query, key, value):
+        packed[at : at + ref.shape[0]] = ref[...]
+        at += ref.shape[0]
+    packed[at : at + out.shape[1]] = out[...].T
+    packed[at + out.shape[1] :] = rest[...]
+
+
+def pack_weights(w_query, w_key, w_value, w_out, rest):
+    rows = 4 * w_query.shape[0] + rest.shape[0]
+    return pl.pallas_call(
+        pack_kernel, out_shape=jax.ShapeDtypeStruct((rows, w_query.shape[1]), LOW)
+    )(w_query, w_key, w_value, w_out, rest)
+
+
+def pack_specs(gathered, places, steps, at):
+    count, width = gathered.shape[0] // steps, gathered.shape[2]
+    block = at
+    return [
+        pl.BlockSpec((count, block, width), lambda i, place=place: (i, place, 0))
+        for place in places
+    ]
+
+
+def project_kernel(mats, roundings, rows_ref, *refs):
+    mat_refs, out_refs, totals = refs[:mats], refs[mats : 2 * mats], refs[2 * mats :]
+    step = pl.program_id(0)
+    rows = rows_ref[...]
+    for mat, out, total, rounding in zip(mat_refs, out_refs, totals, roundings):
+        flat = mat[...].reshape(-1, mat.shape[2])
+        part = dot_nn(rows, flat)
+
+        @pl.when(step == 0)
+        def _():
+            total[...] = part
+
+        @pl.when(step > 0)
+        def _():
+            total[...] += part
+
+        @pl.when(step == pl.num_programs(0) - 1)
+        def _():
+            out[...] = total[...].astype(rounding)
+
+
+def project(rows, gathered, block, places, roundings):
+    count, width = rows.shape
+    columns = gathered.shape[2]
+    steps = 4
+    outs = [jax.ShapeDtypeStruct((count, columns), rounding) for rounding in roundings]
+    return pl.pallas_call(
+        lambda *refs: project_kernel(len(places), roundings, *refs),
+        grid=(steps,),
+        in_specs=[pl.BlockSpec((count, width // steps), lambda i: (0, i))]
+        + pack_specs(gathered, places, steps, block),
+        out_specs=[pl.BlockSpec((count, columns), lambda i: (0, 0)) for _ in outs],
+        out_shape=outs,
+        scratch_shapes=[pltpu.VMEM((count, columns), FULL)] * len(outs),
+        compiler_params=pltpu.CompilerParams(vmem_limit_bytes=40 * 1024 * 1024),
+        cost_estimate=pl.CostEstimate(
+            flops=2 * count * width * columns * len(places),
+            bytes_accessed=2 * width * columns * len(places) + 8 * count * columns,
+            transcendentals=0,
+        ),
+    )(rows, *[gathered] * len(places))
+
+
+def project_back_kernel(mats, *refs):
+    out = refs[-1]
+    total = None
+    for rows_ref, mat in zip(refs[:mats], refs[mats:-1]):
+        part = dot_nt(rows_ref[...], mat[...].reshape(-1, mat.shape[2]))
+        total = part if total is None else total + part
+    out[...] = total
+
+
+def project_back(rows, gathered, block, places):
+    count, columns = rows[0].shape
+    width = gathered.shape[0] * block
+    steps = 4
+    fixed = pl.BlockSpec((count, columns), lambda i: (0, 0), pipeline_mode=pl.Buffered(1))
+    return pl.pallas_call(
+        lambda *refs: project_back_kernel(len(places), *refs),
+        grid=(steps,),
+        in_specs=[fixed] * len(rows) + pack_specs(gathered, places, steps, block),
+        out_specs=pl.BlockSpec((count, width // steps), lambda i: (0, i)),
+        out_shape=jax.ShapeDtypeStruct((count, width), FULL),
+        compiler_params=pltpu.CompilerParams(vmem_limit_bytes=40 * 1024 * 1024),
+        cost_estimate=pl.CostEstimate(
+            flops=2 * count * width * columns * len(places),
+            bytes_accessed=2 * width * columns * len(places) + 4 * count * width,
+            transcendentals=0,
+        ),
+    )(*rows, *[gathered] * len(places))
+
+
+def ring_weights(first, second, fillers):
     rows = first.shape[0] // len(RING)
     cut = (first.shape[1] + second.shape[1]) // 2
     chip = lax.axis_index("dp") // 2
@@ -354,12 +473,15 @@
 
     far = part(4)
     right, left = ahead(far[:, :cut]), behind(far[:, cut:])
+    left = fillers.next(left)
     outward, inward = part(3), part(-3)
     right = jnp.concatenate([add_low(outward[:, :cut], right), outward[:, cut:]], axis=1)
     left = jnp.concatenate([inward[:, :cut], add_low(inward[:, cut:], left)], axis=1)
     right, left = ahead(right), behind(left)
+    left = fillers.next(left)
     for hop in (2, 1):
         right, left = ahead(add_low(part(hop), right)), behind(add_low(part(-hop), left))
+        left = fillers.next(left)
     return part(0).astype(FULL) + right.astype(FULL) + left.astype(FULL)
 
 
@@ -412,119 +534,177 @@
     )(rows, back, gate, *mats)
 
 
-def chunk_kernel(pieces, first, *refs):
+def chunk_kernel(pieces, held, at, size, gate_ref, *refs):
     piece_refs, refs = refs[:pieces], refs[pieces:]
-    back_ref, gate_ref, wg0, wg1, wu0, wu1, wd0, wd1, vg0, vg1, vu0, vu1 = refs[:12]
-    same_ref, cross_ref, rows_ref, h0, h1, g0, g1, u0, u1, kept_g, kept_u = refs[
-        12 if first else 19 :
+    back_ref, mats, refs = refs[0], refs[1:7], refs[7 + held :]
+    same_ref, cross_ref, rows_out, hidden_out, gate_out, up_out = refs[:6]
+    rows, back, wg, wu, wd, hidden, gate_grad, up_grad, grads, sems = refs[6:]
+    count = rows.shape[0]
+    part = wg.shape[2]
+    slab = wg.shape[1] // 4
+    place = pl.ds(at * count, count)
+    copy = pltpu.make_async_copy
+    load_rows, start = [], 0
+    for piece in piece_refs:
+        span = pl.ds(start, piece.shape[0])
+        load_rows.append(copy(piece, rows.at[span], sems.at[len(load_rows)]))
+        start += piece.shape[0]
+    load_back = copy(back_ref.at[place], back, sems.at[4])
+    loads = [
+        [copy(mats[2 * k + half], to.at[half], sems.at[5 + 3 * half + k]) for k, to in enumerate((wg, wu, wd))]
+        for half in range(2)
     ]
-    step = pl.program_id(0)
-
-    @pl.when(step == 0)
-    def _():
-        at = 0
-        for piece in piece_refs:
-            rows_ref[at : at + piece.shape[0]] = piece[...]
-            at += piece.shape[0]
-
-    def work(wg, wu, wd, h, g, u):
-        rows = rows_ref[...]
-        gate = gate_ref[...]
-        gate_pre = dot_nn(rows, wg[...])
-        up_pre = dot_nn(rows, wu[...])
-        hidden_grad = gate * dot_nt(back_ref[...], wd[...])
+    for one in load_rows + loads[0][:2] + [load_back] + loads[0][2:] + loads[1]:
+        one.start()
+    gate = gate_ref[...]
+    for one in load_rows:
+        one.wait()
+    stores = [copy(rows, rows_out.at[place], sems.at[11])]
+    stores[0].start()
+    for half in range(2):
+        columns = pl.ds(half * part, part)
+        loads[half][0].wait()
+        gate_pre = dot_nn(rows[...], wg[half])
+        loads[half][1].wait()
+        up_pre = dot_nn(rows[...], wu[half])
+        if half == 0:
+            load_back.wait()
+        loads[half][2].wait()
+        hidden_grad = gate * dot_nt(back[...], wd[half])
         sig = 1.0 / (1.0 + jnp.exp(-gate_pre))
         act = gate_pre * sig
-        h[...] = (gate * (act * up_pre)).astype(LOW)
-        gate_grad = (hidden_grad * up_pre * (sig * (1.0 + gate_pre * (1.0 - sig)))).astype(LOW)
-        up_grad = (hidden_grad * act).astype(LOW)
-        g[...] = gate_grad
-        u[...] = up_grad
-        kept_g[step] = gate_grad
-        kept_u[step] = up_grad
-
-    @pl.when(step < 2)
-    def _():
-        work(wg0, wu0, wd0, h0, g0, u0)
-
-    @pl.when((step >= 2) & (step < 4))
-    def _():
-        work(wg1, wu1, wd1, h1, g1, u1)
-
-    @pl.when(step >= 4)
-    def _():
+        hidden[:, columns] = (gate * (act * up_pre)).astype(LOW)
+        gate_grad[:, columns] = (
+            hidden_grad * up_pre * (sig * (1.0 + gate_pre * (1.0 - sig)))
+        ).astype(LOW)
+        up_grad[:, columns] = (hidden_grad * act).astype(LOW)
+        for k, (held_in, out) in enumerate(
+            ((hidden, hidden_out), (gate_grad, gate_out), (up_grad, up_out))
+        ):
+            stores.append(
+                copy(held_in.at[:, columns], out.at[place, columns], sems.at[12 + 3 * half + k])
+            )
+            stores[-1].start()
+
+    @pl.loop(0, 4)
+    def _(j):
+        span = pl.ds(pl.multiple_of(j * slab, slab), slab)
         total = None
-        for kept, first_half, second_half in ((kept_g, vg0, vg1), (kept_u, vu0, vu1)):
-            for at, mat in ((0, first_half), (2, second_half)):
-                left = jnp.concatenate([kept[at], kept[at + 1]], axis=1)
-                part = dot_nt(left, mat[...])
-                total = part if total is None else total + part
-        half = same_ref.shape[0]
-        same_ref[...] = total[:half].astype(LOW)
-        cross_ref[...] = total[half:].astype(LOW)
-
-
-def expert_chunk(pieces, back, gate, mats, at, held):
-    width = back.shape[1]
-    hidden = mats[0].shape[1]
-    part = hidden // 2
-    slab = width // 4
+        for grad, mat in ((gate_grad, wg), (up_grad, wu)):
+            for half in range(2):
+                piece = dot_nt(grad[:, half * part : (half + 1) * part], mat[half, span])
+                total = piece if total is None else total + piece
+        grads[:, span] = total.astype(LOW)
+
+    for k in range(count // size):
+        to = cross_ref if k % 2 else same_ref
+        stores.append(
+            copy(
+                grads.at[pl.ds(k * size, size)],
+                to.at[pl.ds(k // 2 * size, size)],
+                sems.at[18 + k],
+            )
+        )
+        stores[-1].start()
+    for one in stores:
+        one.wait()
+
+
+def expert_chunk(pieces, back, gate, mats, at, held, size):
+    all_rows, width = back.shape
+    part = mats[0].shape[1]
+    hidden = 2 * part
     count = sum(piece.shape[0] for piece in pieces)
-    all_rows = back.shape[0]
-    own = lambda j: jnp.minimum(j, 1)
-    other = lambda j: jnp.clip(j - 2, 0, 1)
-    late = lambda j: jnp.maximum(j - 4, 0)
-    once = pl.Buffered(1)
-    fixed = lambda array: pl.BlockSpec(array.shape, lambda j: (0, 0), pipeline_mode=once)
-    chunk = lambda columns, **mode: pl.BlockSpec((count, columns), lambda j: (at, 0), **mode)
-    tall = lambda pick: pl.BlockSpec((width, part), lambda j: (0, pick(j)))
-    flat = lambda pick: pl.BlockSpec((part, width), lambda j: (pick(j), 0))
-    narrow = lambda pick: pl.BlockSpec((count, part), lambda j: (at, pick(j)))
-    again = lambda: pl.BlockSpec((slab, hidden), lambda j: (late(j), 0))
-    whole = lambda: pl.BlockSpec((count // 2, slab), lambda j: (0, late(j)))
-    held_specs = [] if held is None else [pl.BlockSpec(memory_space=pl.ANY)] * 7
-    held_args = [] if held is None else list(held)
-    base = len(pieces) + 12
-    wide = jax.ShapeDtypeStruct((all_rows, hidden), LOW)
+    anywhere = pl.BlockSpec(memory_space=pl.ANY)
+    held = [] if held is None else list(held)
+    args = [gate, *pieces, back, *mats, *held]
     out = pl.pallas_call(
-        lambda *refs: chunk_kernel(len(pieces), held is None, *refs),
-        grid=(8,),
-        in_specs=[fixed(piece) for piece in pieces]
-        + [chunk(width, pipeline_mode=once), chunk(1, pipeline_mode=once)]
-        + [tall(own), tall(other), tall(own), tall(other), flat(own), flat(other)]
-        + [again(), again(), again(), again()]
-        + held_specs,
-        out_specs=[whole(), whole(), chunk(width)] + [narrow(own), narrow(other)] * 3,
+        lambda *refs: chunk_kernel(len(pieces), len(held), at, size, *refs),
+        grid=(1,),
+        in_specs=[pl.BlockSpec((count, 1), lambda j: (at, 0))] + [anywhere] * (len(args) - 1),
+        out_specs=[anywhere] * 6,
         out_shape=[jax.ShapeDtypeStruct((count // 2, width), LOW)] * 2
         + [jax.ShapeDtypeStruct((all_rows, width), LOW)]
-        + [wide] * 6,
-        scratch_shapes=[pltpu.VMEM((4, count, part), LOW)] * 2,
-        input_output_aliases={} if held is None else {base + k: 2 + k for k in range(7)},
-        compiler_params=pltpu.CompilerParams(vmem_limit_bytes=58 * 1024 * 1024),
+        + [jax.ShapeDtypeStruct((all_rows, hidden), LOW)] * 3,
+        scratch_shapes=[
+            pltpu.VMEM((count, width), LOW),
+            pltpu.VMEM((count, width), LOW),
+            pltpu.VMEM((2, width, part), LOW),
+            pltpu.VMEM((2, width, part), LOW),
+            pltpu.VMEM((2, part, width), LOW),
+            pltpu.VMEM((count, hidden), LOW),
+            pltpu.VMEM((count, hidden), LOW),
+            pltpu.VMEM((count, hidden), LOW),
+            pltpu.VMEM((count, width), LOW),
+            pltpu.SemaphoreType.DMA((22,)),
+        ],
+        input_output_aliases={len(args) - len(held) + k: 2 + k for k in range(len(held))},
+        compiler_params=pltpu.CompilerParams(vmem_limit_bytes=50 * 1024 * 1024),
         cost_estimate=pl.CostEstimate(
-            flops=2 * 5 * count * width * hidden * 2,
-            bytes_accessed=2 * (3 * count * width + 6 * count * hidden + 6 * width * hidden),
-            transcendentals=2 * count * hidden,
+            flops=2 * 5 * count * width * hidden,
+            bytes_accessed=2 * (4 * count * width + 3 * count * hidden + 3 * width * hidden),
+            transcendentals=count * hidden,
         ),
-    )(*pieces, back, gate, *mats, *mats[:4], *held_args)
+    )(*args)
     return out[0], out[1], out[2:]
 
 
+def mixed_kernel(chip_ref, core_ref, hidden_ref, first_ref, second_ref, out_ref):
+    part = first_ref.shape[0]
+    rows = out_ref.shape[2]
+    result = dot_nn(hidden_ref[:, :part], first_ref[...]) + dot_nn(
+        hidden_ref[:, part:], second_ref[...]
+    )
+    result = result.astype(LOW)
+    out_ref[0, core_ref[0]] = result[:rows]
+    out_ref[0, 1 - core_ref[0]] = result[rows:]
+
+
+def mixed_pass(hidden, down_mats, blocks):
+    count, columns = hidden.shape
+    width = down_mats[0].shape[1]
+    chips = blocks.shape[0] // 2
+    rows = count // chips
+    once = pl.Buffered(1)
+    fixed = lambda m: pl.BlockSpec(m.shape, lambda i, a, b: (0, 0), pipeline_mode=once)
+    out = pl.pallas_call(
+        mixed_kernel,
+        grid_spec=pltpu.PrefetchScalarGridSpec(
+            num_scalar_prefetch=2,
+            grid=(chips,),
+            in_specs=[pl.BlockSpec((rows, columns), lambda i, a, b: (i, 0))]
+            + [fixed(m) for m in down_mats],
+            out_specs=pl.BlockSpec(
+                (1, 2, rows // 2, width), lambda i, chip, core: (chip[i], 0, 0, 0)
+            ),
+        ),
+        out_shape=jax.ShapeDtypeStruct((chips, 2, rows // 2, width), LOW),
+        compiler_params=pltpu.CompilerParams(vmem_limit_bytes=40 * 1024 * 1024),
+        cost_estimate=pl.CostEstimate(
+            flops=2 * count * columns * width,
+            bytes_accessed=2 * (count * (columns + width) + columns * width),
+            transcendentals=0,
+        ),
+    )(blocks[::2] // 2, blocks[:1] % 2, hidden, *down_mats)
+    return out.reshape(count, width)
+
+
 def expert_ring(rows, back, gate, mats):
-    cut = rows.shape[0] // 2
+    size = rows.shape[0]
+    cut = size // 2
     same, cross = {}, {}
     left, right = ahead(rows), behind(rows)
     swap = lambda block: swap_bit(block, "dp", 0)
-    same[0], cross[0], held = expert_chunk([rows, swap(rows)], back, gate, mats, 6, None)
+    same[0], cross[0], held = expert_chunk([rows, swap(rows)], back, gate, mats, 6, None, size)
     for hop in (1, 2, 3):
-        pieces = [left, right, swap(left), swap(right)]
+        pieces = [left, swap(left), right, swap(right)]
         if hop < 3:
             left, right = ahead(left), behind(right)
         else:
             left, right = ahead(left[:cut]), behind(right[cut:])
-        same[hop], cross[hop], held = expert_chunk(pieces, back, gate, mats, hop - 1, held)
+        same[hop], cross[hop], held = expert_chunk(pieces, back, gate, mats, hop - 1, held, size)
     pieces = [left, right, swap(left), swap(right)]
-    same[4], cross[4], held = expert_chunk(pieces, back, gate, mats, 7, held)
+    same[4], cross[4], held = expert_chunk(pieces, back, gate, mats, 7, held, size)
     return same, cross, held
 
 
@@ -596,14 +776,12 @@
     routing = jnp.pad(routing, ((0, 0), (0, local_width - 3 * token_count)))
     gains = jnp.concatenate([attn_gain, moe_gain, query_gain, key_gain])
     gains = jnp.pad(gains[None], ((0, 7), (0, local_width - 4 * block)))
-    packed = jnp.concatenate([w_query, w_key, w_value, w_out.T, gains, routing], axis=0)
+    packed = pack_weights(
+        w_query, w_key, w_value, w_out, jnp.concatenate([gains, routing], axis=0)
+    )
     gathered = lax.all_gather(packed, "dp", axis=0, tiled=False)
     gathered, *early = lax.optimization_barrier((gathered, gate_mats[1], up_mats[1]))
     gate_mats, up_mats = (gate_mats[0], early[0]), (up_mats[0], early[1])
-    full_q = gathered[:, :block].reshape(model_width, local_width)
-    full_k = gathered[:, block : 2 * block].reshape(model_width, local_width)
-    full_v = gathered[:, 2 * block : 3 * block].reshape(model_width, local_width)
-    full_o = gathered[:, 3 * block : 4 * block].reshape(model_width, local_width)
     gain_rows = gathered[:, 4 * block].astype(FULL)
     gain_one, gain_two, gain_q, gain_k = (
         gain_rows[:, j * block : (j + 1) * block].reshape(-1) for j in range(4)
@@ -656,9 +834,10 @@
     allowed = jnp.concatenate([allowed_prompt, allowed_cont], axis=1)
     bias = jnp.where(allowed, 0.0, -1e30).astype(LOW)
     normed_b = rms_norm(tokens_f, gain_one).astype(LOW)
-    query_flat = dot_nn(normed_b, full_q)
-    key_flat = dot_nn(normed_b, full_k)
-    values_b = dot_nn(normed_b, full_v).astype(LOW)
+    query_flat, key_flat, values_b = project(
+        normed_b, gathered, block, (0, 1, 2), (FULL, FULL, LOW)
+    )
+    value_pieces = collect_prompt(values_b[:PR_DEV], 1, 2)
     query_sq, key_sq = lax.psum(
         (jnp.sum(query_flat * query_flat, axis=1), jnp.sum(key_flat * key_flat, axis=1)), "tensor"
     )
@@ -666,23 +845,16 @@
     down_mats = (down_mat, swap_tensor(down_mat))
     query_scale = lax.rsqrt(query_sq / column_total + EPSILON)[:, None]
     key_scale = lax.rsqrt(key_sq / column_total + EPSILON)[:, None]
-    queries_b, keys_b = rope_pass(
-        query_flat,
-        key_flat,
-        gain_query_local[None],
-        gain_key_local[None],
-        query_scale,
-        key_scale,
-        cosine,
-        sine,
-    )
-    pieces = collect_prompt(jnp.stack([keys_b[:PR_DEV], values_b[:PR_DEV]], axis=0))
+    keys_b = rope_pass(key_flat, gain_key_local[None], key_scale, cosine, sine)
+    pieces = (*collect_prompt(keys_b[:PR_DEV], 2, 1), *value_pieces)
+    queries_b = rope_pass(query_flat, gain_query_local[None], query_scale, cosine, sine)
     context_b = attend(queries_b, keys_b, values_b, bias, pieces)
-    attn_part = dot_nt(context_b, full_o)
+    attn_part = project_back([context_b], gathered, block, (3,))
     attn_part, late = lax.optimization_barrier((attn_part, down_mats[1]))
     down_mats = (down_mats[0], late)
     mats = (*gate_mats, *up_mats, *down_mats)
     attn_other = swap_tensor(other_half(attn_part).astype(LOW))
+    attn_other, back_rows, weight = together(attn_other, back_rows, weight)
     hidden_state = (
         own_half(tokens_f) + own_half(attn_part) + attn_other.astype(FULL)
     )
@@ -691,20 +863,21 @@
     low_tn = lambda left, right: dot_tn(left, right).astype(LOW)
     if ring:
         same, cross, held = expert_ring(normed_two_b, back_rows, weight, mats)
-        expert_in, h0, h1, g0, g1, u0, u1 = held
-        down_sent = low_tn(h1, back_rows)
-        down_got = swap_tensor(down_sent)
-        normed_two_grad, outs = ring_sum(
-            same,
-            cross,
+        expert_in, hidden, gate_grad, up_grad = held
+        part = down_mats[0].shape[0]
+        h0, h1 = hidden[:, :part], hidden[:, part:]
+        g0, g1 = gate_grad[:, :part], gate_grad[:, part:]
+        u0, u1 = up_grad[:, :part], up_grad[:, part:]
+        down_got = swap_tensor(low_tn(h1, back_rows))
+        fillers = Fillers(
             [
-                [(low_tn, expert_in, g1), (low_tn, expert_in, u1)],
-                [(lambda a, b: dot_nn(a, down_mats[0]) + dot_nn(b, down_mats[1]), h0, h1)],
-                [(dot_tn, h0, back_rows), (dot_tn, expert_in, g0), (dot_tn, expert_in, u0)],
-            ],
+                [(low_tn, expert_in, g1)],
+                [(low_tn, expert_in, u1)],
+                [(lambda h: mixed_pass(h, down_mats, blocks), hidden)],
+            ]
         )
-        gate_sent, up_sent, mixed_rows, down_grad, gate_w_grad, up_w_grad = outs
-        mixed_rows = mixed_rows.astype(LOW)
+        normed_two_grad = ring_sum(same, cross, fillers)
+        gate_sent, up_sent, mixed_rows = fillers.outs
         gate_got = swap_tensor(gate_sent)
     else:
         expert_in = lax.all_gather(normed_two_b, "dp", axis=0, tiled=True)
@@ -718,19 +891,10 @@
         down_got = swap_tensor(low_tn(h1, back_rows))
         gate_got = swap_tensor(low_tn(expert_in, g1))
         up_sent = low_tn(expert_in, u1)
-        down_grad = dot_tn(h0, back_rows)
-        gate_w_grad = dot_tn(expert_in, g0)
-        up_w_grad = dot_tn(expert_in, u0)
-    normed_two_grad, down_got, gate_got, mixed_rows, down_grad, gate_w_grad, up_w_grad = together(
-        normed_two_grad, down_got, gate_got, mixed_rows, down_grad, gate_w_grad, up_w_grad
-    )
-    if ring:
-        back_to = jnp.argsort(blocks)
-        mixed_rows = mixed_rows.reshape(dp_count, half_count, model_width)[back_to].reshape(
-            -1, model_width
-        )
-    mixed = lax.psum_scatter(mixed_rows, "dp", scatter_dimension=0, tiled=True).astype(FULL)
-    output_half = hidden_state + mixed
+    normed_two_grad, down_got, gate_got, mixed_rows = together(
+        normed_two_grad, down_got, gate_got, mixed_rows
+    )
+    mixed = lax.psum_scatter(mixed_rows, "dp", scatter_dimension=0, tiled=True)
 
     unused_two, norm_two_back = jax.vjp(rms_norm, hidden_state, gain_two)
     state_part, gain_two_grad = norm_two_back(normed_two_grad)
@@ -739,7 +903,7 @@
     attn_grad_b = both_halves(attn_grad_half, swap_tensor(attn_grad_half))
     attn_grad_b, up_sent = together(attn_grad_b, up_sent)
     up_got = swap_tensor(up_sent)
-    context_grad_b = dot_nn(attn_grad_b, full_o).astype(LOW)
+    (context_grad_b,) = project(attn_grad_b, gathered, block, (3,), (LOW,))
     query_normed_grad, query_inner, query_gain_part, key_grad, value_grad, odd, even = attend_back(
         queries_b,
         keys_b,
@@ -753,6 +917,7 @@
         sine,
         pieces,
     )
+    odd, up_got = together(odd, up_got)
     key_parts, value_parts = return_prompt(odd, even)
     key_normed_grad, key_inner, key_gain_part, value_pre_grad = key_back(
         key_grad,
@@ -765,8 +930,9 @@
         key_parts,
         value_parts,
     )
-    query_inner, key_inner, up_got = together(query_inner, key_inner, up_got)
     query_inner, key_inner = lax.psum((query_inner[:, 0], key_inner[:, 0]), "tensor")
+    query_inner, key_inner, mixed = together(query_inner, key_inner, mixed)
+    output_half = hidden_state + mixed.astype(FULL)
     query_cube = query_scale * query_scale * query_scale
     key_cube = key_scale * key_scale * key_scale
     query_pre_grad = (
@@ -781,6 +947,8 @@
         jnp.zeros((column_total,), FULL), part, side * local_width, 0
     )
     pre_grads = (query_pre_grad, key_pre_grad, value_pre_grad)
+    grad_sum = lambda left, right, got: dot_tn(left, right) + got.astype(FULL)
+    down, gate, up = (h0, back_rows, down_got), (expert_in, g0, gate_got), (expert_in, u0, up_got)
     if ring:
         columns = local_width // 2
         mine = lambda a: lax.dynamic_slice_in_dim(a, core * columns, columns, axis=1)
@@ -793,7 +961,16 @@
             jnp.concatenate([mine(g) for g in pre_grads], axis=1),
             jnp.concatenate([theirs(g) for g in pre_grads], axis=1),
         )
-        w_half = ring_weights(low_tn(normed_pair, grad_pair), low_tn(attn_grad_pair, context_pair))
+        normed_pair, attn_grad_pair, context_pair = together(
+            normed_pair, attn_grad_pair, context_pair
+        )
+        out_half = low_tn(attn_grad_pair, context_pair)
+        normed_pair, grad_pair = together(normed_pair, grad_pair)
+        first_half = low_tn(normed_pair, grad_pair)
+        first_half, *pre_grads = together(first_half, *pre_grads)
+        fillers = Fillers([[(grad_sum, *down)], [(grad_sum, *gate)], [(grad_sum, *up)]])
+        w_half = ring_weights(first_half, out_half, fillers)
+        down_grad, gate_w_grad, up_w_grad = fillers.outs
         own_w = lax.dynamic_slice_in_dim(w_half, core * block, block, axis=0)
         got_w = swap_bit(lax.dynamic_slice_in_dim(w_half, (1 - core) * block, block, axis=0), "dp", 0)
         left_w, right_w = jnp.where(core == 0, own_w, got_w), jnp.where(core == 0, got_w, own_w)
@@ -807,15 +984,9 @@
         )
         w_sum = lax.psum_scatter(w_grads, "dp", scatter_dimension=0, tiled=True).astype(FULL)
         w_sums = [w_sum[:, j * local_width : (j + 1) * local_width] for j in range(4)]
-    down_grad = down_grad + down_got.astype(FULL)
-    gate_w_grad = gate_w_grad + gate_got.astype(FULL)
-    up_w_grad = up_w_grad + up_got.astype(FULL)
+        down_grad, gate_w_grad, up_w_grad = grad_sum(*down), grad_sum(*gate), grad_sum(*up)
     output = both_halves(output_half, swap_tensor(output_half))
-    normed_part = (
-        dot_nt(query_pre_grad, full_q)
-        + dot_nt(key_pre_grad, full_k)
-        + dot_nt(value_pre_grad, full_v)
-    )
+    normed_part = project_back(pre_grads, gathered, block, (0, 1, 2))
     normed_other = swap_tensor(other_half(normed_part).astype(LOW))
     normed_grad = own_half(normed_part) + normed_other.astype(FULL)
     unused_one, norm_one_back = jax.vjp(rms_norm, own_half(tokens_f), gain_one)

time: 890 us -> 801 us (0.900)
  matrix products: 120 us -> 61.5 us
  waiting for transfers between devices: 391 us -> 360 us
  Pallas kernels: 154 us -> 176 us
  local copies, waits for them, and re-layouts: 66.5 us -> 56.8 us
    reduce_scatter x1, waiting for transfers between devices: 118 us -> 0.02 us  [body(): mixed = lax.psum_scatter(mixed_rows, 'dp', scatter_dimension=0, tiled=True)]
    ppermute x36, waiting for transfers between devices: 47 us -> 91.1 us  [swap_bit(): return lax.ppermute(block, axis, [(i, i ^ 1 << bit) for i in range(count)])]
    dot_general x7 -> x1, matrix products: 43 us -> 0.13 us  [dot_nn(): return jnp.dot(left, right, preferred_element_type=FULL)]
    pallas_call x9 -> x16, Pallas kernels: 154 us -> 176 us  [the longest x5 90.4 us: expert_chunk(): pl.pallas_call(lambda *refs: chunk_kernel(len(pieces), len(held), at, siz...]
    ppermute x12, waiting for transfers between devices: 162 us -> 182 us  [swap_tensor(): return lax.ppermute(block, 'tensor', [(0, 1), (1, 0)])]
    all_gather x1, waiting for transfers between devices: 0.01 us -> 16.3 us  [body(): lax.all_gather(cotangent_half.astype(LOW), 'dp', axis=0, tiled=False)]
    ppermute x12, waiting for transfers between devices: 37.8 us -> 51.1 us  [behind(): return lax.ppermute(block, 'dp', BEHIND)]
    broadcast_in_dim x3 -> x0, other arithmetic: 12.8 us -> none  [the longest x1 5.65 us: body(): gate_w_grad[None]]
  transfers between devices with their start and end apart: 75 -> 75, of which waited for: 25 -> 32; matrix products, arithmetic and copies ran while one was open for 23% -> 18% of each run, Pallas kernels for 15% -> 22%
where the time goes in v4:
time: 801 us; the launch traced here: 796 us
  waiting for transfers between devices  360 us (45%)
  Pallas kernels  176 us (22%)
  matrix products  61.5 us (8%)
  starting transfers between devices  59.4 us (7%)
  local copies, waits for them, and re-layouts  56.8 us (7%)
  other arithmetic  55.7 us (7%)
  between operations  15.6 us (2%)
  blocking collectives  10.2 us (1%)
    ppermute x12, waiting for transfers between devices, swap_tensor(): return lax.ppermute(block, 'tensor', [(0, 1), (1, 0)])  182 us
    ppermute x36, waiting for transfers between devices, swap_bit(): return lax.ppermute(block, axis, [(i, i ^ 1 << bit) for i in range(count)])  91.1 us
    pallas_call x5, Pallas kernels, expert_chunk(): pl.pallas_call(lambda *refs: chunk_kernel(len(pieces), len(held), at, siz...  90.4 us
    dot_general x8, matrix products, dot_tn(): lax.dot_general(left, right, (((0,), (0,)), ((), ())), preferred_element_...  61.3 us
    ppermute x12, waiting for transfers between devices, behind(): return lax.ppermute(block, 'dp', BEHIND)  51.1 us
    unnamed x152, local copies, waits for them, and re-layouts  21.8 us
    pallas_call x1, Pallas kernels, attend_back(): pl.pallas_call(attend_back_kernel, grid=(width // HEAD // PAIR,), in_spec...  19.9 us
    ppermute x12, waiting for transfers between devices, ahead(): return lax.ppermute(block, 'dp', AHEAD)  19.8 us
  transfers between devices with their start and end apart: 75, of which 32 were waited for; matrix products, arithmetic and copies ran while one was open for 18% of the time, Pallas kernels for 22%

profile of v4, /device:TPU:0, one launch (start us, length us, event | category | flops | bytes accessed | tf_op | source)
XLA Modules:
  0.0 795.8 jit_solution(7386451156860012368)
XLA Ops:
  10.2 2.4 shard_map.282
  12.7 2.3 dynamic-slice_convert_fusion.2
  15.1 3.0 collective-permute-start
  21.2 43.5 %collective-permute-done.refs_5_.refs_7_ = bf16[2048,512]{1,0:T(8,128)(2,1)} collective-permute-done((bf16[2048,512]{1,0:T(8,128)(2,1)S(1)}, bf16[2048,512]{1,0:T(8,128)(2,1)}, u32[]{:S(2)}, u32[]{:S(2)}) %collective-permute-start) | collective-permute-done | bytes 2097184 | tf_op jit(solution)/shard_map/ppermute | solution.py:25
  64.7 44.1 %collective-permute-done.1.refs_7_.refs_9_ = bf16[2048,512]{1,0:T(8,128)(2,1)} collective-permute-done((bf16[2048,512]{1,0:T(8,128)(2,1)}, bf16[2048,512]{1,0:T(8,128)(2,1)}, u32[]{:S(2)}, u32[]{:S(2)}) %collective-permute-start.1) | collective-permute-done | bytes 2097184 | tf_op jit(solution)/shard_map/ppermute | solution.py:25
  110.8 10.2 %shard_map.283 = (f32[320,1024]{1,0:T(8,128)S(1)}, f32[320,1024]{1,0:T(8,128)S(1)}, bf16[320,1024]{1,0:T(8,128)(2,1)S(1)}) custom-call(bf16[320,2048]{1,0:T(8,128)(2,1)S(1)} %multiply_convert_fusion.refs_0_, bf16[16,528,1024]{2,1,0:T(8,128)(2,1)} %bitcast.120, bf16[16,528,1024]{2,1,0:T(8,128)(2,1)} %bitcast.121, bf16[16,528,1024]{2,1,0:T(8,128)(2,1)} %bitcast.122), custom_call_target="tpu_custom_call" | custom-call | flops 4026531840 | bytes 15204352 | tf_op jit(solution)/shard_map/pallas_call | solution.py:415
  123.2 5.2 all-reduce.4
  131.0 2.6 shard_map.285.k_ref
  142.7 5.1 collective-permute-done.3
  151.5 2.1 convert_element_type.352
  154.2 9.2 %collective-permute-done.4 = bf16[128,1024]{1,0:T(8,128)(2,1)} collective-permute-done((bf16[128,1024]{1,0:T(8,128)(2,1)}, bf16[128,1024]{1,0:T(8,128)(2,1)}, u32[]{:S(2)}, u32[]{:S(2)}) %collective-permute-start.4) | collective-permute-done | bytes 262176 | tf_op jit(solution)/shard_map/ppermute | solution.py:21
  164.8 7.5 collective-permute-done.7
  172.4 14.6 %collective-permute-done.8 = bf16[128,1024]{1,0:T(8,128)(2,1)} collective-permute-done((bf16[128,1024]{1,0:T(8,128)(2,1)}, bf16[128,1024]{1,0:T(8,128)(2,1)}, u32[]{:S(2)}, u32[]{:S(2)}) %collective-permute-start.8) | collective-permute-done | bytes 262176 | tf_op jit(solution)/shard_map/ppermute | solution.py:21
  187.0 2.3 pad_maximum_fusion.7.v_stay
  190.9 16.3 %all-gather.7.cloned.1.call-done = bf16[2560,2048]{1,0:T(8,128)(2,1)} async-done(((bf16[160,2048]{1,0:T(8,128)(2,1)}), bf16[2560,2048]{1,0:T(8,128)(2,1)}) %all-gather.7.cloned.1.call-update) | async-done | bytes 10485776 | tf_op jit(solution)/shard_map/all_gather | solution.py:816
  207.2 9.6 %gather_fusion = bf16[16,160,2048]{2,1,0:T(8,128)(2,1)} fusion(bf16[16,160,2048]{2,1,0:T(8,128)(2,1)} %bitcast.157, s32[1024]{0:T(1024)S(1)} %pad_clamp_fusion), kind=kCustom, calls=%fused_computation | custom fusion | bytes 20971584 | tf_op jit(solution)/shard_map/gather | solution.py:817
  218.8 2.6 shard_map.284.q_ref
  225.8 9.8 %shard_map.286.refs_0_ = bf16[320,1024]{1,0:T(8,128)(2,1)S(1)} custom-call(bf16[320,1024]{1,0:T(8,128)(2,1)S(1)} %copy-done.16, bf16[320,1024]{1,0:T(8,128)(2,1)S(1)} %copy-done.12, bf16[320,1024]{1,0:T(8,128)(2,1)S(1)} %copy-done.18, bf16[320,1216]{1,0:T(8,128)(2,1)S(1)} %copy-done.13, bf16[4,128,1024]{2,1,0:T(8,128)(2,1)S(1)} %pad_maximum_fusion.6.k_stay, ...), custom_call_target="tpu_custom_call" | custom-call | tf_op jit(solution)/shard_map/pallas_call | solution.py:217
  235.6 4.5 shard_map.287
  245.5 13.2 %collective-permute-done.11 = bf16[160,2048]{1,0:T(8,128)(2,1)S(1)} collective-permute-done((bf16[160,2048]{1,0:T(8,128)(2,1)S(1)}, bf16[160,2048]{1,0:T(8,128)(2,1)S(1)}, u32[]{:S(2)}, u32[]{:S(2)}) %collective-permute-start.11) | collective-permute-done | bytes 655392 | tf_op jit(solution)/shard_map/ppermute | solution.py:25
  258.7 2.1 multiply_reduce_fusion.6
  263.2 14.1 %collective-permute-done.14.refs_1_ = bf16[160,2048]{1,0:T(8,128)(2,1)} collective-permute-done((bf16[160,2048]{1,0:T(8,128)(2,1)S(1)}, bf16[160,2048]{1,0:T(8,128)(2,1)}, u32[]{:S(2)}, u32[]{:S(2)}) %collective-permute-start.14) | collective-permute-done | bytes 655392 | tf_op jit(solution)/shard_map/ppermute | solution.py:37
  280.3 12.8 %shard_map.288 = (bf16[160,2048]{1,0:T(8,128)(2,1)S(1)}, bf16[160,2048]{1,0:T(8,128)(2,1)}, bf16[2560,2048]{1,0:T(8,128)(2,1)}, bf16[2560,1024]{1,0:T(8,128)(2,1...) custom-call(f32[2560,1]{1,0:T(8,128)S(1)} %copy.63.refs_0_, ...), custom_call_target="tpu_custom_call" | custom-call | flops 6710886400 | bytes 19791872 | tf_op jit(solution)/shard_map/pallas_call | solution.py:621
  297.4 21.2 %shard_map.289 = (bf16[320,2048]{1,0:T(8,128)(2,1)S(1)}, bf16[320,2048]{1,0:T(8,128)(2,1)}, bf16[2560,2048]{1,0:T(8,128)(2,1)}, bf16[2560,1024]{1,0:T(8,128)(2,1...) custom-call(f32[2560,1]{1,0:T(8,128)} %copy-done.2, ...), custom_call_target="tpu_custom_call", output_to_operand_aliasing={{2}: (12, {}), {3}: (13, {}), {4}: (14, {}), {5}: (15, {})} | custom-call | flops 13421772800 | bytes 27000832 | tf_op jit(solution)/shard_map/pallas_call | solution.py:621
  321.8 21.3 %shard_map.290 = (bf16[320,2048]{1,0:T(8,128)(2,1)S(1)}, bf16[320,2048]{1,0:T(8,128)(2,1)}, bf16[2560,2048]{1,0:T(8,128)(2,1)}, bf16[2560,1024]{1,0:T(8,128)(2,1...) custom-call(f32[2560,1]{1,0:T(8,128)} %copy-done.2, ...), custom_call_target="tpu_custom_call", output_to_operand_aliasing={{2}: (12, {}), {3}: (13, {}), {4}: (14, {}), {5}: (15, {})} | custom-call | flops 13421772800 | bytes 27000832 | tf_op jit(solution)/shard_map/pallas_call | solution.py:621
  344.2 22.6 %shard_map.291 = (bf16[320,2048]{1,0:T(8,128)(2,1)S(1)}, bf16[320,2048]{1,0:T(8,128)(2,1)}, bf16[2560,2048]{1,0:T(8,128)(2,1)}, bf16[2560,1024]{1,0:T(8,128)(2,1...) custom-call(f32[2560,1]{1,0:T(8,128)} %copy-done.2, ...), custom_call_target="tpu_custom_call", output_to_operand_aliasing={{2}: (12, {}), {3}: (13, {}), {4}: (14, {}), {5}: (15, {})} | custom-call | flops 13421772800 | bytes 27000832 | tf_op jit(solution)/shard_map/pallas_call | solution.py:621
  367.0 12.4 %shard_map.292 = (bf16[160,2048]{1,0:T(8,128)(2,1)S(1)}, bf16[160,2048]{1,0:T(8,128)(2,1)S(1)}, bf16[2560,2048]{1,0:T(8,128)(2,1)}, bf16[2560,1024]{1,0:T(8,128)...) custom-call(f32[2560,1]{1,0:T(8,128)S(1)} %copy-done.3, ...), custom_call_target="tpu_custom_call", output_to_operand_aliasing={{2}: (12, {}), {3}: (13, {}), {4}: (14, {}), {5}: (15, {})} | custom-call | flops 6710886400 | bytes 19791872 | tf_op jit(solution)/shard_map/pallas_call | solution.py:621
  379.9 9.3 %convolution_convert_fusion.4 = bf16[512,2048]{1,0:T(8,128)(2,1)S(1)} fusion(bf16[2560,2048]{1,0:T(8,128)(2,1)} %bitcast.134, bf16[2560,1024]{1,0:T(8,128)(2,1)} %get-tuple-element.155.hidden_ref), kind=kOutput, calls=%fused_computation.9 | convolution fusion | flops 5369757696 | bytes 15204352 | tf_op jit(solution)/shard_map/dot_general | solution.py:127
  392.0 7.2 collective-permute-done.38
  403.0 5.0 collective-permute-done.34
  410.5 2.7 fusion.48
  416.5 7.5 collective-permute-done.39
  426.6 8.3 %convolution_convert_fusion.3 = bf16[2048,512]{1,0:T(8,128)(2,1)S(1)} fusion(bf16[2560,2048]{1,0:T(8,128)(2,1)} %get-tuple-element.195, bf16[2560,512]{1,0:T(8,128)(2,1)S(1)} %get-tuple-element.154), kind=kOutput, calls=%fused_computation.8 | convolution fusion | flops 5369757696 | bytes 15204352 | tf_op jit(solution)/shard_map/dot_general | solution.py:127
  438.4 2.1 collective-permute-done.40
  443.1 16.0 %shard_map.293 = bf16[8,2,160,2048]{3,2,1,0:T(8,128)(2,1)} custom-call(s32[8]{0:T(128)S(1)} %and_select_fusion.chip_ref, s32[1]{0:T(128)S(6)} %select_n.316.core_ref, bf16[2560,1024]{1,0:T(8,128)(2,1)S(1)} %bitcast.111, bf16[512,2048]{1,0:T(8,128)(2,1)S(1)} %bitcast.118, bf16[512,2048]{1,0:T(8,128)(2,1)} %collective-permute-done.10.refs_9_.refs_11_.second_ref), custom_call_target="tpu_custom_call" | custom-call | flops 10737418240 | bytes 19922944 | tf_op jit(solution)/shard_map/pallas_call | solution.py:670
  461.9 41.7 %collective-permute-done.43 = bf16[2048,512]{1,0:T(8,128)(2,1)} collective-permute-done((bf16[2048,512]{1,0:T(8,128)(2,1)S(1)}, bf16[2048,512]{1,0:T(8,128)(2,1)}, u32[]{:S(2)}, u32[]{:S(2)}) %collective-permute-start.43) | collective-permute-done | bytes 2097184 | tf_op jit(solution)/shard_map/ppermute | solution.py:25
  509.6 12.5 %convolution_convert_fusion.2 = bf16[2048,512]{1,0:T(8,128)(2,1)} fusion(bf16[2560,2048]{1,0:T(8,128)(2,1)} %get-tuple-element.195, bf16[2560,512]{1,0:T(8,128)(2,1)S(1)} %copy-done.31), kind=kOutput, calls=%fused_computation.7 | convolution fusion | flops 5369757696 | bytes 15204352 | tf_op jit(solution)/shard_map/dot_general | solution.py:127
  524.3 4.7 shard_map.294.back_ref
  529.8 19.9 %shard_map.295 = (f32[320,1024]{1,0:T(8,128)}, f32[320,1]{1,0:T(8,128)}, f32[1,1024]{1,0:T(1,128)}, f32[320,1024]{1,0:T(8,128)}, f32[320,1024]{1,0:T(8,128)}, /*...) custom-call(bf16[320,1024]{1,0:T(8,128)(2,1)} %shard_map.284.q_ref, ...), custom_call_target="tpu_custom_call" | custom-call | tf_op jit(solution)/shard_map/pallas_call | solution.py:292
  549.7 16.8 %collective-permute-done.45 = bf16[2048,512]{1,0:T(8,128)(2,1)S(1)} collective-permute-done((bf16[2048,512]{1,0:T(8,128)(2,1)}, bf16[2048,512]{1,0:T(8,128)(2,1)S(1)}, u32[]{:S(2)}, u32[]{:S(2)}) %collective-permute-start.45) | collective-permute-done | bytes 2097184 | tf_op jit(solution)/shard_map/ppermute | solution.py:25
  569.3 4.8 collective-permute-done.52
  574.1 3.1 pad_maximum_fusion.1
  578.1 3.5 slice.274
  582.4 2.1 add_convert_fusion.15
  586.3 3.1 pad_maximum_fusion.2
  591.2 8.2 %collective-permute-done.47 = bf16[2,128,1024]{2,1,0:T(8,128)(2,1)S(1)} collective-permute-done((bf16[2,128,1024]{2,1,0:T(8,128)(2,1)S(1)}, bf16[2,128,1024]{2,1,0:T(8,128)(2,1)S(1)}, u32[]{:S(2)}, u32[]{:S(2)}) %collective-permute-start.47) | collective-permute-done | bytes 524320 | tf_op jit(solution)/shard_map/ppermute | solution.py:21
  602.0 19.7 %collective-permute-done.48.refs_9_ = bf16[128,1024]{1,0:T(8,128)(2,1)S(1)} collective-permute-done((bf16[128,1024]{1,0:T(8,128)(2,1)S(1)}, bf16[128,1024]{1,0:T(8,128)(2,1)S(1)}, u32[]{:S(2)}, u32[]{:S(2)}) %collective-permute-start.48) | collective-permute-done | bytes 262176 | tf_op jit(solution)/shard_map/ppermute | solution.py:21
  622.5 5.4 shard_map.296
  629.1 4.9 all-reduce.3
  635.3 2.3 subtract_convert_fusion
  644.8 5.3 convolution_convert_fusion
  650.1 7.7 shard_map.297
  660.0 2.0 collective-permute-start.63
  662.1 12.7 %collective-permute-done.51 = f32[160,2048]{1,0:T(8,128)S(1)} collective-permute-done((f32[160,2048]{1,0:T(8,128)S(1)}, f32[160,2048]{1,0:T(8,128)S(1)}, u32[]{:S(2)}, u32[]{:S(2)}) %collective-permute-start.51) | collective-permute-done | bytes 1310752 | tf_op jit(solution)/shard_map/ppermute | solution.py:25
  678.2 8.6 %collective-permute-done.56 = bf16[160,2048]{1,0:T(8,128)(2,1)S(1)} collective-permute-done((bf16[160,2048]{1,0:T(8,128)(2,1)S(1)}, bf16[160,2048]{1,0:T(8,128)(2,1)S(1)}, u32[]{:S(2)}, u32[]{:S(2)}) %collective-permute-start.56) | collective-permute-done | bytes 655392 | tf_op jit(solution)/shard_map/ppermute | solution.py:25
  687.7 10.1 %collective-permute-done.58 = f32[8,4,128]{2,1,0:T(4,128)S(1)} collective-permute-done((f32[8,4,128]{2,1,0:T(4,128)S(1)}, f32[8,4,128]{2,1,0:T(4,128)S(1)}, u32[]{:S(2)}, u32[]{:S(2)}) %collective-permute-start.58) | collective-permute-done | bytes 16416 | tf_op jit(solution)/shard_map/ppermute | solution.py:21
  697.8 3.1 collective-permute-start.59
  704.2 8.5 %add_bitcast_fusion = f32[1,512,2048]{2,1,0:T(8,128)} fusion(bf16[512,2048]{1,0:T(8,128)(2,1)} %collective-permute-done.42, bf16[2560,512]{1,0:T(8,128)(2,1)S(1)} %copy-done.32, bf16[2560,2048]{1,0:T(8,128)(2,1)S(1)} %bitcast.137), kind=kOutput, calls=%fused_computation.3 | convolution fusion | flops 5370806272 | bytes 19398656 | tf_op jit(solution)/shard_map/dot_general | solution.py:127
  712.7 9.3 %collective-permute-done.60 = f32[2,4,128]{2,1,0:T(4,128)S(1)} collective-permute-done((f32[2,4,128]{2,1,0:T(4,128)S(1)}, f32[2,4,128]{2,1,0:T(4,128)S(1)}, u32[]{:S(2)}, u32[]{:S(2)}) %collective-permute-start.60) | collective-permute-done | bytes 4128 | tf_op jit(solution)/shard_map/ppermute | solution.py:21
  725.6 2.0 collective-permute-start.65
  729.1 21.1 %collective-permute-done.69 = bf16[256,2048]{1,0:T(8,128)(2,1)S(1)} collective-permute-done((bf16[256,2048]{1,0:T(8,128)(2,1)S(1)}, bf16[256,2048]{1,0:T(8,128)(2,1)S(1)}, u32[]{:S(2)}, u32[]{:S(2)}) %collective-permute-start.69) | collective-permute-done | bytes 1048608 | tf_op jit(solution)/shard_map/ppermute | solution.py:41
  753.1 8.4 %add_bitcast_fusion.2 = f32[1,2048,512]{2,1,0:T(8,128)} fusion(bf16[2048,512]{1,0:T(8,128)(2,1)} %collective-permute-done.43, bf16[2560,2048]{1,0:T(8,128)(2,1)S(1)} %bitcast.139, bf16[2560,512]{1,0:T(8,128)(2,1)S(1)} %copy-done.29), kind=kOutput, calls=%fused_computation.5 | convolution fusion | flops 5370806272 | bytes 19398656 | tf_op jit(solution)/shard_map/dot_general | solution.py:127
  763.3 11.4 %collective-permute-done.70 = bf16[256,2048]{1,0:T(8,128)(2,1)S(1)} collective-permute-done((bf16[256,2048]{1,0:T(8,128)(2,1)S(1)}, bf16[256,2048]{1,0:T(8,128)(2,1)S(1)}, u32[]{:S(2)}, u32[]{:S(2)}) %collective-permute-start.70) | collective-permute-done | bytes 1048608 | tf_op jit(solution)/shard_map/ppermute | solution.py:41
  777.9 7.2 add_bitcast_fusion.1
  (422 shorter events, 134.9 us)
Async XLA Ops:
  7.2 101.6 %all-gather.5.cloned.1.call-start = ((), (), s32[]{:S(2)}) async-start(), calls=%async_computation.2 | async-start | bytes 18382848 | tf_op jit(solution)/shard_map/all_gather | solution.py:782
  12.6 194.6 %all-gather.7.cloned.1.call-start = ((), (), s32[]{:S(2)}) async-start(), calls=%async_computation.3 | async-start | bytes 11141120 | tf_op jit(solution)/shard_map/all_gather | solution.py:816
  15.0 620.2 %reduce-scatter.2.cloned.1.call-start = ((), (), s32[]{:S(2)}) async-start(), calls=%async_computation.1 | async-start | bytes 11141120 | tf_op jit(solution)/shard_map/reduce_scatter | solution.py:897
  15.1 49.6 %collective-permute-start = (bf16[2048,512]{1,0:T(8,128)(2,1)S(1)}, bf16[2048,512]{1,0:T(8,128)(2,1)}, u32[]{:S(2)}, u32[]{:S(2)}) collective-permute-start(bf16[2048,512]{1,0:T(8,128)(2,1)S(1)} %bitcast.149), channel_id=1, source_target_pairs={{0,1},{1,0},{2,3},{3,2},{4,5},{5,4},{6,7},{7,6},{8,9},{9,8},{10,11... | collective-permute-start | bytes 6291464 | tf_op jit(solution)/shard_map/ppermute | solution.py:25
  18.1 90.7 %collective-permute-start.1 = (bf16[2048,512]{1,0:T(8,128)(2,1)}, bf16[2048,512]{1,0:T(8,128)(2,1)}, u32[]{:S(2)}, u32[]{:S(2)}) collective-permute-start(bf16[2048,512]{1,0:T(8,128)(2,1)} %bitcast.150), channel_id=1, source_target_pairs={{0,1},{1,0},{2,3},{3,2},{4,5},{5,4},{6,7},{7,6},{8,9},{9,8},{10,11... | collective-permute-start | bytes 6291464 | tf_op jit(solution)/shard_map/ppermute | solution.py:25
  135.6 12.3 %collective-permute-start.3 = (bf16[128,1024]{1,0:T(8,128)(2,1)}, bf16[128,1024]{1,0:T(8,128)(2,1)}, u32[]{:S(2)}, u32[]{:S(2)}) collective-permute-start(bf16[128,1024]{1,0:T(8,128)(2,1)} %get-tuple-element.322), channel_id=1, source_target_pairs={{0,8},{2,10},{4,12},{6,14},{8,0},{10,2},{12,4},{14,6},{16,24},{18,... | collective-permute-start | bytes 786440 | tf_op jit(solution)/shard_map/ppermute | solution.py:21
  137.4 102.8 %collective-permute-start.10 = (bf16[512,2048]{1,0:T(8,128)(2,1)S(1)}, bf16[512,2048]{1,0:T(8,128)(2,1)}, u32[]{:S(2)}, u32[]{:S(2)}) collective-permute-start(bf16[512,2048]{1,0:T(8,128)(2,1)S(1)} %bitcast.117), channel_id=1, source_target_pairs={{0,1},{1,0},{2,3},{3,2},{4,5},{5,4},{6,7},{7,6},{8,9},{9,8},{10,11... | collective-permute-start | bytes 6291464 | tf_op jit(solution)/shard_map/ppermute | solution.py:25
  142.2 12.0 %collective-permute-start.2 = (bf16[128,1024]{1,0:T(8,128)(2,1)}, bf16[128,1024]{1,0:T(8,128)(2,1)}, u32[]{:S(2)}, u32[]{:S(2)}) collective-permute-start(bf16[128,1024]{1,0:T(8,128)(2,1)} %get-tuple-element.322), channel_id=1, source_target_pairs={{0,4},{2,6},{4,0},{6,2},{8,12},{10,14},{12,8},{14,10},{16,20},{18,... | collective-permute-start | bytes 786440 | tf_op jit(solution)/shard_map/ppermute | solution.py:21
  147.9 15.5 %collective-permute-start.4 = (bf16[128,1024]{1,0:T(8,128)(2,1)}, bf16[128,1024]{1,0:T(8,128)(2,1)}, u32[]{:S(2)}, u32[]{:S(2)}) collective-permute-start(bf16[128,1024]{1,0:T(8,128)(2,1)} %collective-permute-done.3), channel_id=1, source_target_pairs={{0,4},{2,6},{4,0},{6,2},{8,12},{10,14},{12,8},{14,10},{16,20},{18,... | collective-permute-start | bytes 786440 | tf_op jit(solution)/shard_map/ppermute | solution.py:21
  149.4 23.0 %collective-permute-start.7 = (bf16[128,1024]{1,0:T(8,128)(2,1)}, bf16[128,1024]{1,0:T(8,128)(2,1)}, u32[]{:S(2)}, u32[]{:S(2)}) collective-permute-start(bf16[128,1024]{1,0:T(8,128)(2,1)} %get-tuple-element.320), channel_id=1, source_target_pairs={{0,8},{2,10},{4,12},{6,14},{8,0},{10,2},{12,4},{14,6},{16,24},{18,... | collective-permute-start | bytes 786440 | tf_op jit(solution)/shard_map/ppermute | solution.py:21
  150.0 37.0 %collective-permute-start.8 = (bf16[128,1024]{1,0:T(8,128)(2,1)}, bf16[128,1024]{1,0:T(8,128)(2,1)}, u32[]{:S(2)}, u32[]{:S(2)}) collective-permute-start(bf16[128,1024]{1,0:T(8,128)(2,1)} %collective-permute-done.6), channel_id=1, source_target_pairs={{0,8},{2,10},{4,12},{6,14},{8,0},{10,2},{12,4},{14,6},{16,24},{18,... | collective-permute-start | bytes 786440 | tf_op jit(solution)/shard_map/ppermute | solution.py:21
  164.7 56.6 %collective-permute-start.5 = (bf16[4,128,1024]{2,1,0:T(8,128)(2,1)S(1)}, bf16[4,128,1024]{2,1,0:T(8,128)(2,1)}, u32[]{:S(2)}, u32[]{:S(2)}) collective-permute-start(bf16[4,128,1024]{2,1,0:T(8,128)(2,1)S(1)} %pad_maximum_fusion.6.k_stay), channel_id=1, source_target_pairs={{0,2},{2,0},{4,6},{6,4},{8,10},{10,8},{12,14},{14,12},{16,18},{18,... | collective-permute-start | bytes 3145736 | tf_op jit(solution)/shard_map/ppermute | solution.py:21
  189.3 32.1 %collective-permute-start.9 = (bf16[4,128,1024]{2,1,0:T(8,128)(2,1)}, bf16[4,128,1024]{2,1,0:T(8,128)(2,1)}, u32[]{:S(2)}, u32[]{:S(2)}) collective-permute-start(bf16[4,128,1024]{2,1,0:T(8,128)(2,1)} %pad_maximum_fusion.7.v_stay), channel_id=1, source_target_pairs={{0,2},{2,0},{4,6},{6,4},{8,10},{10,8},{12,14},{14,12},{16,18},{18,... | collective-permute-start | bytes 3145736 | tf_op jit(solution)/shard_map/ppermute | solution.py:21
  241.7 17.0 %collective-permute-start.11 = (bf16[160,2048]{1,0:T(8,128)(2,1)S(1)}, bf16[160,2048]{1,0:T(8,128)(2,1)S(1)}, u32[]{:S(2)}, u32[]{:S(2)}) collective-permute-start(bf16[160,2048]{1,0:T(8,128)(2,1)S(1)} %dynamic-slice_convert_fusion.1), channel_id=1, source_target_pairs={{0,1},{1,0},{2,3},{3,2},{4,5},{5,4},{6,7},{7,6},{8,9},{9,8},{10,11... | collective-permute-start | bytes 1966088 | tf_op jit(solution)/shard_map/ppermute | solution.py:25
  261.0 16.2 %collective-permute-start.14 = (bf16[160,2048]{1,0:T(8,128)(2,1)S(1)}, bf16[160,2048]{1,0:T(8,128)(2,1)}, u32[]{:S(2)}, u32[]{:S(2)}) collective-permute-start(bf16[160,2048]{1,0:T(8,128)(2,1)S(1)} %multiply_convert_fusion.1.refs_1_), channel_id=1, source_target_pairs={{0,8},{2,10},{8,16},{10,18},{16,24},{18,26},{24,28},{26,30},{28,20... | collective-permute-start | bytes 1966088 | tf_op jit(solution)/shard_map/ppermute | solution.py:37
  261.8 16.2 %collective-permute-start.16 = (bf16[160,2048]{1,0:T(8,128)(2,1)S(1)}, bf16[160,2048]{1,0:T(8,128)(2,1)}, u32[]{:S(2)}, u32[]{:S(2)}) collective-permute-start(bf16[160,2048]{1,0:T(8,128)(2,1)S(1)} %multiply_convert_fusion.1.refs_1_), channel_id=1, source_target_pairs={{8,0},{10,2},{16,8},{18,10},{24,16},{26,18},{28,24},{30,26},{20,28... | collective-permute-start | bytes 1966088 | tf_op jit(solution)/shard_map/ppermute | solution.py:41
  263.1 17.2 %collective-permute-start.12 = (bf16[160,2048]{1,0:T(8,128)(2,1)S(1)}, bf16[160,2048]{1,0:T(8,128)(2,1)S(1)}, u32[]{:S(2)}, u32[]{:S(2)}) collective-permute-start(bf16[160,2048]{1,0:T(8,128)(2,1)S(1)} %multiply_convert_fusion.1.refs_1_), channel_id=1, source_target_pairs={{0,2},{2,0},{4,6},{6,4},{8,10},{10,8},{12,14},{14,12},{16,18},{18,... | collective-permute-start | bytes 1966088 | tf_op jit(solution)/shard_map/ppermute | solution.py:21
  277.2 16.2 %collective-permute-start.19 = (bf16[160,2048]{1,0:T(8,128)(2,1)}, bf16[160,2048]{1,0:T(8,128)(2,1)S(1)}, u32[]{:S(2)}, u32[]{:S(2)}) collective-permute-start(bf16[160,2048]{1,0:T(8,128)(2,1)} %collective-permute-done.14.refs_1_), channel_id=1, source_target_pairs={{0,8},{2,10},{8,16},{10,18},{16,24},{18,26},{24,28},{26,30},{28,20... | collective-permute-start | bytes 1966088 | tf_op jit(solution)/shard_map/ppermute | solution.py:37
  277.6 18.1 %collective-permute-start.15 = (bf16[160,2048]{1,0:T(8,128)(2,1)}, bf16[160,2048]{1,0:T(8,128)(2,1)}, u32[]{:S(2)}, u32[]{:S(2)}) collective-permute-start(bf16[160,2048]{1,0:T(8,128)(2,1)} %collective-permute-done.14.refs_1_), channel_id=1, source_target_pairs={{0,2},{2,0},{4,6},{6,4},{8,10},{10,8},{12,14},{14,12},{16,18},{18,... | collective-permute-start | bytes 1966088 | tf_op jit(solution)/shard_map/ppermute | solution.py:21
  278.0 17.7 %collective-permute-start.21 = (bf16[160,2048]{1,0:T(8,128)(2,1)}, bf16[160,2048]{1,0:T(8,128)(2,1)}, u32[]{:S(2)}, u32[]{:S(2)}) collective-permute-start(bf16[160,2048]{1,0:T(8,128)(2,1)} %collective-permute-done.16.refs_3_), channel_id=1, source_target_pairs={{8,0},{10,2},{16,8},{18,10},{24,16},{26,18},{28,24},{30,26},{20,28... | collective-permute-start | bytes 1966088 | tf_op jit(solution)/shard_map/ppermute | solution.py:41
  279.4 17.7 %collective-permute-start.17 = (bf16[160,2048]{1,0:T(8,128)(2,1)}, bf16[160,2048]{1,0:T(8,128)(2,1)}, u32[]{:S(2)}, u32[]{:S(2)}) collective-permute-start(bf16[160,2048]{1,0:T(8,128)(2,1)} %collective-permute-done.16.refs_3_), channel_id=1, source_target_pairs={{0,2},{2,0},{4,6},{6,4},{8,10},{10,8},{12,14},{14,12},{16,18},{18,... | collective-permute-start | bytes 1966088 | tf_op jit(solution)/shard_map/ppermute | solution.py:21
  293.1 166.0 %collective-permute-start.13 = (bf16[160,2048]{1,0:T(8,128)(2,1)}, bf16[160,2048]{1,0:T(8,128)(2,1)}, u32[]{:S(2)}, u32[]{:S(2)}) collective-permute-start(bf16[160,2048]{1,0:T(8,128)(2,1)} %get-tuple-element.121), channel_id=1, source_target_pairs={{0,2},{2,0},{4,6},{6,4},{8,10},{10,8},{12,14},{14,12},{16,18},{18,... | collective-permute-start | bytes 1966088 | tf_op jit(solution)/shard_map/ppermute | solution.py:21
  293.5 25.2 %collective-permute-start.24 = (bf16[160,2048]{1,0:T(8,128)(2,1)S(1)}, bf16[160,2048]{1,0:T(8,128)(2,1)S(1)}, u32[]{:S(2)}, u32[]{:S(2)}) collective-permute-start(bf16[160,2048]{1,0:T(8,128)(2,1)S(1)} %collective-permute-done.19.refs_1_), channel_id=1, source_target_pairs={{0,8},{2,10},{8,16},{10,18},{16,24},{18,26},{24,28},{26,30},{28,20... | collective-permute-start | bytes 1966088 | tf_op jit(solution)/shard_map/ppermute | solution.py:37
  295.7 25.6 %collective-permute-start.20 = (bf16[160,2048]{1,0:T(8,128)(2,1)S(1)}, bf16[160,2048]{1,0:T(8,128)(2,1)S(1)}, u32[]{:S(2)}, u32[]{:S(2)}) collective-permute-start(bf16[160,2048]{1,0:T(8,128)(2,1)S(1)} %collective-permute-done.19.refs_1_), channel_id=1, source_target_pairs={{0,2},{2,0},{4,6},{6,4},{8,10},{10,8},{12,14},{14,12},{16,18},{18,... | collective-permute-start | bytes 1966088 | tf_op jit(solution)/shard_map/ppermute | solution.py:21
  295.7 23.9 %collective-permute-start.26 = (bf16[160,2048]{1,0:T(8,128)(2,1)}, bf16[160,2048]{1,0:T(8,128)(2,1)S(1)}, u32[]{:S(2)}, u32[]{:S(2)}) collective-permute-start(bf16[160,2048]{1,0:T(8,128)(2,1)} %collective-permute-done.21.refs_3_), channel_id=1, source_target_pairs={{8,0},{10,2},{16,8},{18,10},{24,16},{26,18},{28,24},{30,26},{20,28... | collective-permute-start | bytes 1966088 | tf_op jit(solution)/shard_map/ppermute | solution.py:41
  297.1 24.1 %collective-permute-start.22 = (bf16[160,2048]{1,0:T(8,128)(2,1)}, bf16[160,2048]{1,0:T(8,128)(2,1)S(1)}, u32[]{:S(2)}, u32[]{:S(2)}) collective-permute-start(bf16[160,2048]{1,0:T(8,128)(2,1)} %collective-permute-done.21.refs_3_), channel_id=1, source_target_pairs={{0,2},{2,0},{4,6},{6,4},{8,10},{10,8},{12,14},{14,12},{16,18},{18,... | collective-permute-start | bytes 1966088 | tf_op jit(solution)/shard_map/ppermute | solution.py:21
  318.7 24.4 %collective-permute-start.29 = (bf16[80,2048]{1,0:T(8,128)(2,1)S(1)}, bf16[80,2048]{1,0:T(8,128)(2,1)S(1)}, u32[]{:S(2)}, u32[]{:S(2)}) collective-permute-start(bf16[80,2048]{1,0:T(8,128)(2,1)S(1)} %slice.300), channel_id=1, source_target_pairs={{0,8},{2,10},{8,16},{10,18},{16,24},{18,26},{24,28},{26,30},{28,20... | collective-permute-start | bytes 983048 | tf_op jit(solution)/shard_map/ppermute | solution.py:37
  319.6 23.6 %collective-permute-start.30 = (bf16[80,2048]{1,0:T(8,128)(2,1)S(1)}, bf16[80,2048]{1,0:T(8,128)(2,1)S(1)}, u32[]{:S(2)}, u32[]{:S(2)}) collective-permute-start(bf16[80,2048]{1,0:T(8,128)(2,1)S(1)} %slice.301), channel_id=1, source_target_pairs={{8,0},{10,2},{16,8},{18,10},{24,16},{26,18},{28,24},{30,26},{20,28... | collective-permute-start | bytes 983048 | tf_op jit(solution)/shard_map/ppermute | solution.py:41
  321.3 22.4 %collective-permute-start.25 = (bf16[160,2048]{1,0:T(8,128)(2,1)S(1)}, bf16[160,2048]{1,0:T(8,128)(2,1)S(1)}, u32[]{:S(2)}, u32[]{:S(2)}) collective-permute-start(bf16[160,2048]{1,0:T(8,128)(2,1)S(1)} %collective-permute-done.24.refs_1_), channel_id=1, source_target_pairs={{0,2},{2,0},{4,6},{6,4},{8,10},{10,8},{12,14},{14,12},{16,18},{18,... | collective-permute-start | bytes 1966088 | tf_op jit(solution)/shard_map/ppermute | solution.py:21
  321.3 22.5 %collective-permute-start.27 = (bf16[160,2048]{1,0:T(8,128)(2,1)S(1)}, bf16[160,2048]{1,0:T(8,128)(2,1)S(1)}, u32[]{:S(2)}, u32[]{:S(2)}) collective-permute-start(bf16[160,2048]{1,0:T(8,128)(2,1)S(1)} %collective-permute-done.26.refs_3_), channel_id=1, source_target_pairs={{0,2},{2,0},{4,6},{6,4},{8,10},{10,8},{12,14},{14,12},{16,18},{18,... | collective-permute-start | bytes 1966088 | tf_op jit(solution)/shard_map/ppermute | solution.py:21
  343.1 91.8 %collective-permute-start.18 = (bf16[320,2048]{1,0:T(8,128)(2,1)}, bf16[320,2048]{1,0:T(8,128)(2,1)}, u32[]{:S(2)}, u32[]{:S(2)}) collective-permute-start(bf16[320,2048]{1,0:T(8,128)(2,1)} %get-tuple-element.127), channel_id=1, source_target_pairs={{0,2},{2,0},{4,6},{6,4},{8,10},{10,8},{12,14},{14,12},{16,18},{18,... | collective-permute-start | bytes 3932168 | tf_op jit(solution)/shard_map/ppermute | solution.py:21
  343.2 70.0 %collective-permute-start.23 = (bf16[320,2048]{1,0:T(8,128)(2,1)}, bf16[320,2048]{1,0:T(8,128)(2,1)}, u32[]{:S(2)}, u32[]{:S(2)}) collective-permute-start(bf16[320,2048]{1,0:T(8,128)(2,1)} %get-tuple-element.133), channel_id=1, source_target_pairs={{0,2},{2,0},{4,6},{6,4},{8,10},{10,8},{12,14},{14,12},{16,18},{18,... | collective-permute-start | bytes 3932168 | tf_op jit(solution)/shard_map/ppermute | solution.py:21
  343.7 23.1 %collective-permute-start.31 = (bf16[80,2048]{1,0:T(8,128)(2,1)S(1)}, bf16[80,2048]{1,0:T(8,128)(2,1)S(1)}, u32[]{:S(2)}, u32[]{:S(2)}) collective-permute-start(bf16[80,2048]{1,0:T(8,128)(2,1)S(1)} %collective-permute-done.29.refs_1_), channel_id=1, source_target_pairs={{0,2},{2,0},{4,6},{6,4},{8,10},{10,8},{12,14},{14,12},{16,18},{18,... | collective-permute-start | bytes 983048 | tf_op jit(solution)/shard_map/ppermute | solution.py:21
  343.8 23.2 %collective-permute-start.32 = (bf16[80,2048]{1,0:T(8,128)(2,1)S(1)}, bf16[80,2048]{1,0:T(8,128)(2,1)S(1)}, u32[]{:S(2)}, u32[]{:S(2)}) collective-permute-start(bf16[80,2048]{1,0:T(8,128)(2,1)S(1)} %collective-permute-done.30.refs_2_), channel_id=1, source_target_pairs={{0,2},{2,0},{4,6},{6,4},{8,10},{10,8},{12,14},{14,12},{16,18},{18,... | collective-permute-start | bytes 983048 | tf_op jit(solution)/shard_map/ppermute | solution.py:21
  366.8 33.3 %collective-permute-start.28 = (bf16[320,2048]{1,0:T(8,128)(2,1)}, bf16[320,2048]{1,0:T(8,128)(2,1)S(1)}, u32[]{:S(2)}, u32[]{:S(2)}) collective-permute-start(bf16[320,2048]{1,0:T(8,128)(2,1)} %get-tuple-element.139), channel_id=1, source_target_pairs={{0,2},{2,0},{4,6},{6,4},{8,10},{10,8},{12,14},{14,12},{16,18},{18,... | collective-permute-start | bytes 3932168 | tf_op jit(solution)/shard_map/ppermute | solution.py:21
  379.4 9.8 %collective-permute-start.33 = (bf16[160,2048]{1,0:T(8,128)(2,1)S(1)}, bf16[160,2048]{1,0:T(8,128)(2,1)S(1)}, u32[]{:S(2)}, u32[]{:S(2)}) collective-permute-start(bf16[160,2048]{1,0:T(8,128)(2,1)S(1)} %get-tuple-element.145), channel_id=1, source_target_pairs={{0,2},{2,0},{4,6},{6,4},{8,10},{10,8},{12,14},{14,12},{16,18},{18,... | collective-permute-start | bytes 1966088 | tf_op jit(solution)/shard_map/ppermute | solution.py:21
  408.3 15.7 %collective-permute-start.35 = (bf16[160,2048]{1,0:T(8,128)(2,1)S(1)}, bf16[160,2048]{1,0:T(8,128)(2,1)S(1)}, u32[]{:S(2)}, u32[]{:S(2)}) collective-permute-start(bf16[160,2048]{1,0:T(8,128)(2,1)S(1)} %pad_maximum_fusion.10), channel_id=1, source_target_pairs={{0,8},{2,10},{8,16},{10,18},{16,24},{18,26},{24,28},{26,30},{28,20... | collective-permute-start | bytes 1966088 | tf_op jit(solution)/shard_map/ppermute | solution.py:37
  409.3 14.7 %collective-permute-start.39 = (bf16[160,2048]{1,0:T(8,128)(2,1)S(1)}, bf16[160,2048]{1,0:T(8,128)(2,1)S(1)}, u32[]{:S(2)}, u32[]{:S(2)}) collective-permute-start(bf16[160,2048]{1,0:T(8,128)(2,1)S(1)} %pad_maximum_fusion.11), channel_id=1, source_target_pairs={{8,0},{10,2},{16,8},{18,10},{24,16},{26,18},{28,24},{30,26},{20,28... | collective-permute-start | bytes 1966088 | tf_op jit(solution)/shard_map/ppermute | solution.py:41
  413.2 48.7 %collective-permute-start.42 = (bf16[512,2048]{1,0:T(8,128)(2,1)S(1)}, bf16[512,2048]{1,0:T(8,128)(2,1)}, u32[]{:S(2)}, u32[]{:S(2)}) collective-permute-start(bf16[512,2048]{1,0:T(8,128)(2,1)S(1)} %convolution_convert_fusion.4), channel_id=1, source_target_pairs={{0,1},{1,0},{2,3},{3,2},{4,5},{5,4},{6,7},{7,6},{8,9},{9,8},{10,11... | collective-permute-start | bytes 6291464 | tf_op jit(solution)/shard_map/ppermute | solution.py:25
  424.5 15.9 %collective-permute-start.36 = (bf16[160,2048]{1,0:T(8,128)(2,1)S(1)}, bf16[160,2048]{1,0:T(8,128)(2,1)S(1)}, u32[]{:S(2)}, u32[]{:S(2)}) collective-permute-start(bf16[160,2048]{1,0:T(8,128)(2,1)S(1)} %get-tuple-element.295), channel_id=1, source_target_pairs={{0,8},{2,10},{8,16},{10,18},{16,24},{18,26},{24,28},{26,30},{28,20... | collective-permute-start | bytes 1966088 | tf_op jit(solution)/shard_map/ppermute | solution.py:37
  426.2 14.2 %collective-permute-start.40 = (bf16[160,2048]{1,0:T(8,128)(2,1)S(1)}, bf16[160,2048]{1,0:T(8,128)(2,1)S(1)}, u32[]{:S(2)}, u32[]{:S(2)}) collective-permute-start(bf16[160,2048]{1,0:T(8,128)(2,1)S(1)} %get-tuple-element.296), channel_id=1, source_target_pairs={{8,0},{10,2},{16,8},{18,10},{24,16},{26,18},{28,24},{30,26},{20,28... | collective-permute-start | bytes 1966088 | tf_op jit(solution)/shard_map/ppermute | solution.py:41
  434.9 68.6 %collective-permute-start.43 = (bf16[2048,512]{1,0:T(8,128)(2,1)S(1)}, bf16[2048,512]{1,0:T(8,128)(2,1)}, u32[]{:S(2)}, u32[]{:S(2)}) collective-permute-start(bf16[2048,512]{1,0:T(8,128)(2,1)S(1)} %convolution_convert_fusion.3), channel_id=1, source_target_pairs={{0,1},{1,0},{2,3},{3,2},{4,5},{5,4},{6,7},{7,6},{8,9},{9,8},{10,11... | collective-permute-start | bytes 6291464 | tf_op jit(solution)/shard_map/ppermute | solution.py:25
  441.0 18.1 %collective-permute-start.41 = (bf16[160,2048]{1,0:T(8,128)(2,1)S(1)}, bf16[160,2048]{1,0:T(8,128)(2,1)S(1)}, u32[]{:S(2)}, u32[]{:S(2)}) collective-permute-start(bf16[160,2048]{1,0:T(8,128)(2,1)S(1)} %get-tuple-element.294), channel_id=1, source_target_pairs={{8,0},{10,2},{16,8},{18,10},{24,16},{26,18},{28,24},{30,26},{20,28... | collective-permute-start | bytes 1966088 | tf_op jit(solution)/shard_map/ppermute | solution.py:41
  441.4 17.7 %collective-permute-start.37 = (bf16[160,2048]{1,0:T(8,128)(2,1)S(1)}, bf16[160,2048]{1,0:T(8,128)(2,1)S(1)}, u32[]{:S(2)}, u32[]{:S(2)}) collective-permute-start(bf16[160,2048]{1,0:T(8,128)(2,1)S(1)} %get-tuple-element.293), channel_id=1, source_target_pairs={{0,8},{2,10},{8,16},{10,18},{16,24},{18,26},{24,28},{26,30},{28,20... | collective-permute-start | bytes 1966088 | tf_op jit(solution)/shard_map/ppermute | solution.py:37
  508.1 14.1 %collective-permute-start.44 = (bf16[160,2048]{1,0:T(8,128)(2,1)S(1)}, bf16[160,2048]{1,0:T(8,128)(2,1)S(1)}, u32[]{:S(2)}, u32[]{:S(2)}) collective-permute-start(bf16[160,2048]{1,0:T(8,128)(2,1)S(1)} %get-tuple-element.251), channel_id=1, source_target_pairs={{0,1},{1,0},{2,3},{3,2},{4,5},{5,4},{6,7},{7,6},{8,9},{9,8},{10,11... | collective-permute-start | bytes 1966088 | tf_op jit(solution)/shard_map/ppermute | solution.py:25
  522.4 44.1 %collective-permute-start.45 = (bf16[2048,512]{1,0:T(8,128)(2,1)}, bf16[2048,512]{1,0:T(8,128)(2,1)S(1)}, u32[]{:S(2)}, u32[]{:S(2)}) collective-permute-start(bf16[2048,512]{1,0:T(8,128)(2,1)} %convolution_convert_fusion.2), channel_id=1, source_target_pairs={{0,1},{1,0},{2,3},{3,2},{4,5},{5,4},{6,7},{7,6},{8,9},{9,8},{10,11... | collective-permute-start | bytes 6291464 | tf_op jit(solution)/shard_map/ppermute | solution.py:25
  567.8 14.5 %collective-permute-start.46 = (bf16[4,2,128,1024]{3,2,1,0:T(8,128)(2,1)}, bf16[4,2,128,1024]{3,2,1,0:T(8,128)(2,1)}, u32[]{:S(2)}, u32[]{:S(2)}) collective-permute-start(bf16[4,2,128,1024]{3,2,1,0:T(8,128)(2,1)} %get-tuple-element.165), channel_id=1, source_target_pairs={{0,2},{2,0},{4,6},{6,4},{8,10},{10,8},{12,14},{14,12},{16,18},{18,... | collective-permute-start | bytes 6291464 | tf_op jit(solution)/shard_map/ppermute | solution.py:21
  584.6 14.8 %collective-permute-start.47 = (bf16[2,128,1024]{2,1,0:T(8,128)(2,1)S(1)}, bf16[2,128,1024]{2,1,0:T(8,128)(2,1)S(1)}, u32[]{:S(2)}, u32[]{:S(2)}) collective-permute-start(bf16[2,128,1024]{2,1,0:T(8,128)(2,1)S(1)} %pad_maximum_fusion.15), channel_id=1, source_target_pairs={{0,4},{2,6},{4,0},{6,2},{8,12},{10,14},{12,8},{14,10},{16,20},{18,... | collective-permute-start | bytes 1572872 | tf_op jit(solution)/shard_map/ppermute | solution.py:21
  585.2 14.4 %collective-permute-start.49 = (bf16[2,128,1024]{2,1,0:T(8,128)(2,1)S(1)}, bf16[2,128,1024]{2,1,0:T(8,128)(2,1)S(1)}, u32[]{:S(2)}, u32[]{:S(2)}) collective-permute-start(bf16[2,128,1024]{2,1,0:T(8,128)(2,1)S(1)} %pad_maximum_fusion.16), channel_id=1, source_target_pairs={{0,8},{2,10},{4,12},{6,14},{8,0},{10,2},{12,4},{14,6},{16,24},{18,... | collective-permute-start | bytes 1572872 | tf_op jit(solution)/shard_map/ppermute | solution.py:21
  599.5 22.2 %collective-permute-start.48 = (bf16[128,1024]{1,0:T(8,128)(2,1)S(1)}, bf16[128,1024]{1,0:T(8,128)(2,1)S(1)}, u32[]{:S(2)}, u32[]{:S(2)}) collective-permute-start(bf16[128,1024]{1,0:T(8,128)(2,1)S(1)} %fusion.9), channel_id=1, source_target_pairs={{0,8},{2,10},{4,12},{6,14},{8,0},{10,2},{12,4},{14,6},{16,24},{18,... | collective-permute-start | bytes 786440 | tf_op jit(solution)/shard_map/ppermute | solution.py:21
  599.7 22.0 %collective-permute-start.50 = (bf16[128,1024]{1,0:T(8,128)(2,1)S(1)}, bf16[128,1024]{1,0:T(8,128)(2,1)S(1)}, u32[]{:S(2)}, u32[]{:S(2)}) collective-permute-start(bf16[128,1024]{1,0:T(8,128)(2,1)S(1)} %fusion.10), channel_id=1, source_target_pairs={{0,4},{2,6},{4,0},{6,2},{8,12},{10,14},{12,8},{14,10},{16,20},{18,... | collective-permute-start | bytes 786440 | tf_op jit(solution)/shard_map/ppermute | solution.py:21
  643.0 31.8 %collective-permute-start.51 = (f32[160,2048]{1,0:T(8,128)S(1)}, f32[160,2048]{1,0:T(8,128)S(1)}, u32[]{:S(2)}, u32[]{:S(2)}) collective-permute-start(f32[160,2048]{1,0:T(8,128)S(1)} %convert_add_fusion.2), channel_id=1, source_target_pairs={{0,1},{1,0},{2,3},{3,2},{4,5},{5,4},{6,7},{7,6},{8,9},{9,8},{10,11... | collective-permute-start | bytes 3932168 | tf_op jit(solution)/shard_map/ppermute | solution.py:25
  657.9 28.9 %collective-permute-start.56 = (bf16[160,2048]{1,0:T(8,128)(2,1)S(1)}, bf16[160,2048]{1,0:T(8,128)(2,1)S(1)}, u32[]{:S(2)}, u32[]{:S(2)}) collective-permute-start(bf16[160,2048]{1,0:T(8,128)(2,1)S(1)} %dynamic-slice_convert_fusion), channel_id=1, source_target_pairs={{0,1},{1,0},{2,3},{3,2},{4,5},{5,4},{6,7},{7,6},{8,9},{9,8},{10,11... | collective-permute-start | bytes 1966088 | tf_op jit(solution)/shard_map/ppermute | solution.py:25
  659.9 16.9 %collective-permute-start.67 = (bf16[256,1024]{1,0:T(8,128)(2,1)S(1)}, bf16[256,1024]{1,0:T(8,128)(2,1)S(1)}, u32[]{:S(2)}, u32[]{:S(2)}) collective-permute-start(bf16[256,1024]{1,0:T(8,128)(2,1)S(1)} %pad_maximum_fusion.13), channel_id=1, source_target_pairs={{8,0},{10,2},{16,8},{18,10},{24,16},{26,18},{28,24},{30,26},{20,28... | collective-permute-start | bytes 1572872 | tf_op jit(solution)/shard_map/ppermute | solution.py:41
  660.0 27.5 %collective-permute-start.63 = (bf16[256,1024]{1,0:T(8,128)(2,1)S(1)}, bf16[256,1024]{1,0:T(8,128)(2,1)S(1)}, u32[]{:S(2)}, u32[]{:S(2)}) collective-permute-start(bf16[256,1024]{1,0:T(8,128)(2,1)S(1)} %get-tuple-element.265), channel_id=1, source_target_pairs={{0,8},{2,10},{8,16},{10,18},{16,24},{18,26},{24,28},{26,30},{28,20... | collective-permute-start | bytes 1572872 | tf_op jit(solution)/shard_map/ppermute | solution.py:37
  678.0 46.8 %collective-permute-start.68 = (bf16[256,2048]{1,0:T(8,128)(2,1)}, bf16[256,2048]{1,0:T(8,128)(2,1)S(1)}, u32[]{:S(2)}, u32[]{:S(2)}) collective-permute-start(bf16[256,2048]{1,0:T(8,128)(2,1)} %pad_maximum_fusion.8), channel_id=1, source_target_pairs={{8,0},{10,2},{16,8},{18,10},{24,16},{26,18},{28,24},{30,26},{20,28... | collective-permute-start | bytes 3145736 | tf_op jit(solution)/shard_map/ppermute | solution.py:41
  687.4 10.4 %collective-permute-start.58 = (f32[8,4,128]{2,1,0:T(4,128)S(1)}, f32[8,4,128]{2,1,0:T(4,128)S(1)}, u32[]{:S(2)}, u32[]{:S(2)}) collective-permute-start(f32[8,4,128]{2,1,0:T(4,128)S(1)} %dynamic-slice_bitcast_fusion), channel_id=1, source_target_pairs={{0,16},{2,18},{4,20},{6,22},{8,24},{10,26},{12,28},{14,30},{16,0},... | collective-permute-start | bytes 49160 | tf_op jit(solution)/shard_map/ppermute | solution.py:21
  702.0 23.2 %collective-permute-start.64 = (bf16[256,2048]{1,0:T(8,128)(2,1)}, bf16[256,2048]{1,0:T(8,128)(2,1)S(1)}, u32[]{:S(2)}, u32[]{:S(2)}) collective-permute-start(bf16[256,2048]{1,0:T(8,128)(2,1)} %fusion.5), channel_id=1, source_target_pairs={{0,8},{2,10},{8,16},{10,18},{16,24},{18,26},{24,28},{26,30},{28,20... | collective-permute-start | bytes 3145736 | tf_op jit(solution)/shard_map/ppermute | solution.py:37
  702.6 19.5 %collective-permute-start.60 = (f32[2,4,128]{2,1,0:T(4,128)S(1)}, f32[2,4,128]{2,1,0:T(4,128)S(1)}, u32[]{:S(2)}, u32[]{:S(2)}) collective-permute-start(f32[2,4,128]{2,1,0:T(4,128)S(1)} %constant_dynamic-slice_fusion.21), channel_id=1, source_target_pairs={{0,4},{2,6},{4,0},{6,2},{8,12},{10,14},{12,8},{14,10},{16,20},{18,... | collective-permute-start | bytes 12296 | tf_op jit(solution)/shard_map/ppermute | solution.py:21
  725.2 25.0 %collective-permute-start.69 = (bf16[256,2048]{1,0:T(8,128)(2,1)S(1)}, bf16[256,2048]{1,0:T(8,128)(2,1)S(1)}, u32[]{:S(2)}, u32[]{:S(2)}) collective-permute-start(bf16[256,2048]{1,0:T(8,128)(2,1)S(1)} %add_convert_fusion.4), channel_id=1, source_target_pairs={{8,0},{10,2},{16,8},{18,10},{24,16},{26,18},{28,24},{30,26},{20,28... | collective-permute-start | bytes 3145736 | tf_op jit(solution)/shard_map/ppermute | solution.py:41
  725.6 25.3 %collective-permute-start.65 = (bf16[256,2048]{1,0:T(8,128)(2,1)S(1)}, bf16[256,2048]{1,0:T(8,128)(2,1)S(1)}, u32[]{:S(2)}, u32[]{:S(2)}) collective-permute-start(bf16[256,2048]{1,0:T(8,128)(2,1)S(1)} %add_convert_fusion.6), channel_id=1, source_target_pairs={{0,8},{2,10},{8,16},{10,18},{16,24},{18,26},{24,28},{26,30},{28,20... | collective-permute-start | bytes 3145736 | tf_op jit(solution)/shard_map/ppermute | solution.py:37
  728.1 33.4 %collective-permute-start.57 = (f32[160,2048]{1,0:T(8,128)S(1)}, f32[160,2048]{1,0:T(8,128)S(1)}, u32[]{:S(2)}, u32[]{:S(2)}) collective-permute-start(f32[160,2048]{1,0:T(8,128)S(1)} %fusion.3), channel_id=1, source_target_pairs={{0,1},{1,0},{2,3},{3,2},{4,5},{5,4},{6,7},{7,6},{8,9},{9,8},{10,11... | collective-permute-start | bytes 3932168 | tf_op jit(solution)/shard_map/ppermute | solution.py:25
  750.5 24.1 %collective-permute-start.70 = (bf16[256,2048]{1,0:T(8,128)(2,1)S(1)}, bf16[256,2048]{1,0:T(8,128)(2,1)S(1)}, u32[]{:S(2)}, u32[]{:S(2)}) collective-permute-start(bf16[256,2048]{1,0:T(8,128)(2,1)S(1)} %add_convert_fusion.3), channel_id=1, source_target_pairs={{8,0},{10,2},{16,8},{18,10},{24,16},{26,18},{28,24},{30,26},{20,28... | collective-permute-start | bytes 3145736 | tf_op jit(solution)/shard_map/ppermute | solution.py:41
  751.2 24.2 %collective-permute-start.66 = (bf16[256,2048]{1,0:T(8,128)(2,1)S(1)}, bf16[256,2048]{1,0:T(8,128)(2,1)S(1)}, u32[]{:S(2)}, u32[]{:S(2)}) collective-permute-start(bf16[256,2048]{1,0:T(8,128)(2,1)S(1)} %add_convert_fusion.5), channel_id=1, source_target_pairs={{0,8},{2,10},{8,16},{10,18},{16,24},{18,26},{24,28},{26,30},{28,20... | collective-permute-start | bytes 3145736 | tf_op jit(solution)/shard_map/ppermute | solution.py:37
  (86 other events, 921.0 us)
Sparse Core Ops, SparseCore 0:
  12.7 94.2 all-gather.4
  109.9 97.2 all-gather.6
  503.7 123.9 reduce-scatter.1

commit v5 on v4

--- a/solution.py
+++ b/solution.py
@@ -138,14 +138,23 @@
     return stay, swap_bit(stay, "dp", 0)
 
 
+def merge_kernel(even_ref, got_ref, keys_ref, values_ref, far_ref, near_ref):
+    near, far, last = 0, 1, 2
+    add = lambda j, which: add_low(even_ref[j, which], got_ref[j + 1, which])
+    keys_ref[0], keys_ref[1] = add(near, 0), add(last, 0)
+    values_ref[0], values_ref[1] = add(far, 1), add(last, 1)
+    far_ref[...], near_ref[...] = add(far, 0), add(near, 1)
+
+
 def return_prompt(odd, even):
     got = swap_bit(odd, "dp", 0)
-    near, far, last = (add_low(even[i], got[i + 1]) for i in range(3))
-    keys = swap_bit(jnp.stack([near[0], last[0]], axis=0), "dp", 1)
-    values = swap_bit(jnp.stack([far[1], last[1]], axis=0), "dp", 2)
-    last_keys = swap_bit(add_low(far[0], keys[1]), "dp", 2)
-    last_values = swap_bit(add_low(near[1], values[1]), "dp", 1)
-    return (got[0, 0], keys[0], last_keys), (got[0, 1], values[0], last_values)
+    one = jax.ShapeDtypeStruct(even.shape[2:], LOW)
+    two = jax.ShapeDtypeStruct(even.shape[1:], LOW)
+    keys, values, far, near = pl.pallas_call(merge_kernel, out_shape=[two, two, one, one])(even, got)
+    keys, values = swap_bit(keys, "dp", 1), swap_bit(values, "dp", 2)
+    last_keys = swap_bit(add_low(far, keys[1]), "dp", 2)
+    last_values = swap_bit(add_low(near, values[1]), "dp", 1)
+    return got, keys, values, last_keys, last_values
 
 
 def turn(values):
@@ -320,16 +329,15 @@
 
 def key_back_kernel(*refs):
     kg_ref, vg_ref, flat_ref, gain_ref, scale_ref, cos_ref, sin_ref = refs[:7]
-    key_parts, value_parts = refs[7:10], refs[10:13]
-    out_ref, inner_ref, gain_grad_ref, value_ref = refs[13:]
+    got, keys, values, last_keys, last_values = refs[7:12]
+    out_ref, inner_ref, gain_grad_ref, value_ref = refs[12:]
     step = pl.program_id(0)
     for at in range(0, PAIR * HEAD, HEAD):
         span = slice(at, at + HEAD)
         grads = []
-        for own_ref, parts in ((kg_ref, key_parts), (vg_ref, value_parts)):
-            first = own_ref[:PR_DEV, span]
-            for part in parts:
-                first = first + part[:, span].astype(FULL)
+        for which, own_ref, near, last in ((0, kg_ref, keys, last_keys), (1, vg_ref, values, last_values)):
+            first = own_ref[:PR_DEV, span] + got[0, which, :, span].astype(FULL)
+            first = first + near[0, :, span].astype(FULL) + last[:, span].astype(FULL)
             grads.append(jnp.concatenate([first, own_ref[PR_DEV:, span]], axis=0))
         key_grad = grads[0] * cos_ref[...] - turn(grads[0]) * sin_ref[...]
         out_ref[:, span] = key_grad
@@ -337,15 +345,18 @@
         value_ref[:, span] = grads[1].astype(LOW)
 
 
-def key_back(key_grad, value_grad, flat, gain, scale, cosine, sine, key_parts, value_parts):
+def key_back(key_grad, value_grad, flat, gain, scale, cosine, sine, returned):
     rows, width = flat.shape
+    columns = PAIR * HEAD
     return pl.pallas_call(
         key_back_kernel,
-        grid=(width // HEAD // PAIR,),
+        grid=(width // columns,),
         in_specs=[head_spec(rows)] * 3
         + [head_spec(1)]
         + [kept_spec(a) for a in (scale, cosine, sine)]
-        + [head_spec(PR_DEV)] * 6,
+        + [pl.BlockSpec((1, 2, PR_DEV, columns), lambda h: (0, 0, 0, h))]
+        + [pl.BlockSpec((1, PR_DEV, columns), lambda h: (0, 0, h))] * 2
+        + [head_spec(PR_DEV)] * 2,
         out_specs=[
             head_spec(rows),
             pl.BlockSpec((rows, 1), lambda h: (0, 0)),
@@ -358,23 +369,60 @@
             jax.ShapeDtypeStruct((1, width), FULL),
             jax.ShapeDtypeStruct((rows, width), LOW),
         ],
-    )(key_grad, value_grad, flat, gain, scale, cosine, sine, *key_parts, *value_parts)
-
-
-def pack_kernel(query, key, value, out, rest, packed):
+    )(key_grad, value_grad, flat, gain, scale, cosine, sine, *returned)
+
+
+def pack_kernel(query, key, value, rest, *refs):
+    packed = refs[-1]
     at = 0
-    for ref in (query, key, value):
+    for ref in (query, key, value, rest):
         packed[at : at + ref.shape[0]] = ref[...]
         at += ref.shape[0]
-    packed[at : at + out.shape[1]] = out[...].T
-    packed[at + out.shape[1] :] = rest[...]
-
-
-def pack_weights(w_query, w_key, w_value, w_out, rest):
-    rows = 4 * w_query.shape[0] + rest.shape[0]
+    for back in refs[:-1]:
+        width = packed.shape[1]
+        for start in range(0, back.shape[1], width):
+            packed[at : at + back.shape[0]] = back[:, start : start + width].astype(LOW)
+            at += back.shape[0]
+
+
+def pack_weights(w_query, w_key, w_value, rest, back):
+    width = w_query.shape[1]
+    rows = 3 * w_query.shape[0] + rest.shape[0] + sum(b.size // width for b in back)
+    return pl.pallas_call(pack_kernel, out_shape=jax.ShapeDtypeStruct((rows, width), LOW))(
+        w_query, w_key, w_value, rest, *back
+    )
+
+
+def unpack_kernel(first, blocks_ref, packed, out, sems):
+    width = packed.shape[2]
+    parts = out.shape[1] // width
+    rows = (packed.shape[1] - first) // parts
+    copies = [
+        pltpu.make_async_copy(
+            packed.at[blocks_ref[i], pl.ds(first + j * rows, rows)],
+            out.at[pl.ds(i * rows, rows), pl.ds(j * width, width)],
+            sems.at[i * parts + j],
+        )
+        for i in range(packed.shape[0])
+        for j in range(parts)
+    ]
+    for one in copies:
+        one.start()
+    for one in copies:
+        one.wait()
+
+
+def unpack_rows(packed, blocks, first, width):
+    count = packed.shape[0]
+    parts = width // packed.shape[2]
+    rows = (packed.shape[1] - first) // parts
     return pl.pallas_call(
-        pack_kernel, out_shape=jax.ShapeDtypeStruct((rows, w_query.shape[1]), LOW)
-    )(w_query, w_key, w_value, w_out, rest)
+        lambda *refs: unpack_kernel(first, *refs),
+        in_specs=[pl.BlockSpec(memory_space=pltpu.SMEM), pl.BlockSpec(memory_space=pl.ANY)],
+        out_specs=pl.BlockSpec(memory_space=pl.ANY),
+        out_shape=jax.ShapeDtypeStruct((count * rows, width), LOW),
+        scratch_shapes=[pltpu.SemaphoreType.DMA((count * parts,))],
+    )(blocks, packed)
 
 
 def pack_specs(gathered, places, steps, at):
@@ -471,7 +519,7 @@
             [lax.dynamic_slice_in_dim(a, at, rows, axis=0) for a in (first, second)], axis=1
         )
 
-    far = part(4)
+    far = fillers.next(part(4))
     right, left = ahead(far[:, :cut]), behind(far[:, cut:])
     left = fillers.next(left)
     outward, inward = part(3), part(-3)
@@ -537,8 +585,9 @@
 def chunk_kernel(pieces, held, at, size, gate_ref, *refs):
     piece_refs, refs = refs[:pieces], refs[pieces:]
     back_ref, mats, refs = refs[0], refs[1:7], refs[7 + held :]
-    same_ref, cross_ref, rows_out, hidden_out, gate_out, up_out = refs[:6]
-    rows, back, wg, wu, wd, hidden, gate_grad, up_grad, grads, sems = refs[6:]
+    same_ref, cross_ref, rows_out = refs[:3]
+    outs = refs[3:9]
+    rows, back, wg, wu, wd, hidden, gate_grad, up_grad, grads, sems = refs[9:]
     count = rows.shape[0]
     part = wg.shape[2]
     slab = wg.shape[1] // 4
@@ -578,11 +627,11 @@
             hidden_grad * up_pre * (sig * (1.0 + gate_pre * (1.0 - sig)))
         ).astype(LOW)
         up_grad[:, columns] = (hidden_grad * act).astype(LOW)
-        for k, (held_in, out) in enumerate(
-            ((hidden, hidden_out), (gate_grad, gate_out), (up_grad, up_out))
-        ):
+        for k, held_in in enumerate((hidden, gate_grad, up_grad)):
             stores.append(
-                copy(held_in.at[:, columns], out.at[place, columns], sems.at[12 + 3 * half + k])
+                copy(
+                    held_in.at[:, columns], outs[2 * k + half].at[place], sems.at[12 + 3 * half + k]
+                )
             )
             stores[-1].start()
 
@@ -622,10 +671,10 @@
         lambda *refs: chunk_kernel(len(pieces), len(held), at, size, *refs),
         grid=(1,),
         in_specs=[pl.BlockSpec((count, 1), lambda j: (at, 0))] + [anywhere] * (len(args) - 1),
-        out_specs=[anywhere] * 6,
+        out_specs=[anywhere] * 9,
         out_shape=[jax.ShapeDtypeStruct((count // 2, width), LOW)] * 2
         + [jax.ShapeDtypeStruct((all_rows, width), LOW)]
-        + [jax.ShapeDtypeStruct((all_rows, hidden), LOW)] * 3,
+        + [jax.ShapeDtypeStruct((all_rows, part), LOW)] * 6,
         scratch_shapes=[
             pltpu.VMEM((count, width), LOW),
             pltpu.VMEM((count, width), LOW),
@@ -649,19 +698,16 @@
     return out[0], out[1], out[2:]
 
 
-def mixed_kernel(chip_ref, core_ref, hidden_ref, first_ref, second_ref, out_ref):
-    part = first_ref.shape[0]
+def mixed_kernel(chip_ref, core_ref, h0_ref, h1_ref, first_ref, second_ref, out_ref):
     rows = out_ref.shape[2]
-    result = dot_nn(hidden_ref[:, :part], first_ref[...]) + dot_nn(
-        hidden_ref[:, part:], second_ref[...]
-    )
+    result = dot_nn(h0_ref[...], first_ref[...]) + dot_nn(h1_ref[...], second_ref[...])
     result = result.astype(LOW)
     out_ref[0, core_ref[0]] = result[:rows]
     out_ref[0, 1 - core_ref[0]] = result[rows:]
 
 
-def mixed_pass(hidden, down_mats, blocks):
-    count, columns = hidden.shape
+def mixed_pass(h0, h1, down_mats, blocks):
+    count, columns = h0.shape
     width = down_mats[0].shape[1]
     chips = blocks.shape[0] // 2
     rows = count // chips
@@ -672,7 +718,7 @@
         grid_spec=pltpu.PrefetchScalarGridSpec(
             num_scalar_prefetch=2,
             grid=(chips,),
-            in_specs=[pl.BlockSpec((rows, columns), lambda i, a, b: (i, 0))]
+            in_specs=[pl.BlockSpec((rows, columns), lambda i, a, b: (i, 0))] * 2
             + [fixed(m) for m in down_mats],
             out_specs=pl.BlockSpec(
                 (1, 2, rows // 2, width), lambda i, chip, core: (chip[i], 0, 0, 0)
@@ -681,31 +727,33 @@
         out_shape=jax.ShapeDtypeStruct((chips, 2, rows // 2, width), LOW),
         compiler_params=pltpu.CompilerParams(vmem_limit_bytes=40 * 1024 * 1024),
         cost_estimate=pl.CostEstimate(
-            flops=2 * count * columns * width,
-            bytes_accessed=2 * (count * (columns + width) + columns * width),
+            flops=4 * count * columns * width,
+            bytes_accessed=2 * (count * (2 * columns + width) + 2 * columns * width),
             transcendentals=0,
         ),
-    )(blocks[::2] // 2, blocks[:1] % 2, hidden, *down_mats)
+    )(blocks[::2] // 2, blocks[:1] % 2, h0, h1, *down_mats)
     return out.reshape(count, width)
 
 
-def expert_ring(rows, back, gate, mats):
+def expert_ring(rows, back, gate, mats, waiting):
     size = rows.shape[0]
     cut = size // 2
     same, cross = {}, {}
+    swap = lambda block: swap_bit(block, "dp", 0)
+    rows, pair = together(rows, swap(rows))
     left, right = ahead(rows), behind(rows)
-    swap = lambda block: swap_bit(block, "dp", 0)
-    same[0], cross[0], held = expert_chunk([rows, swap(rows)], back, gate, mats, 6, None, size)
+    same[0], cross[0], held = expert_chunk([rows, pair], back, gate, mats, 6, None, size)
     for hop in (1, 2, 3):
         pieces = [left, swap(left), right, swap(right)]
         if hop < 3:
             left, right = ahead(left), behind(right)
         else:
             left, right = ahead(left[:cut]), behind(right[cut:])
+            pieces[0], waiting = together(pieces[0], waiting)
         same[hop], cross[hop], held = expert_chunk(pieces, back, gate, mats, hop - 1, held, size)
     pieces = [left, right, swap(left), swap(right)]
     same[4], cross[4], held = expert_chunk(pieces, back, gate, mats, 7, held, size)
-    return same, cross, held
+    return same, cross, held, waiting
 
 
 def halving_sum(parts):
@@ -776,23 +824,30 @@
     routing = jnp.pad(routing, ((0, 0), (0, local_width - 3 * token_count)))
     gains = jnp.concatenate([attn_gain, moe_gain, query_gain, key_gain])
     gains = jnp.pad(gains[None], ((0, 7), (0, local_width - 4 * block)))
+    cotangent_half = own_half(cotangent)
     packed = pack_weights(
-        w_query, w_key, w_value, w_out, jnp.concatenate([gains, routing], axis=0)
+        w_query,
+        w_key,
+        w_value,
+        jnp.concatenate([gains, routing], axis=0),
+        [cotangent_half] if ring else [],
     )
     gathered = lax.all_gather(packed, "dp", axis=0, tiled=False)
+    gathered_out = lax.all_gather(w_out.T, "dp", axis=0, tiled=False)
     gathered, *early = lax.optimization_barrier((gathered, gate_mats[1], up_mats[1]))
     gate_mats, up_mats = (gate_mats[0], early[0]), (up_mats[0], early[1])
-    gain_rows = gathered[:, 4 * block].astype(FULL)
+    rest = gathered[:, 3 * block : 3 * block + 16]
+    gain_rows = rest[:, 0].astype(FULL)
     gain_one, gain_two, gain_q, gain_k = (
         gain_rows[:, j * block : (j + 1) * block].reshape(-1) for j in range(4)
     )
     gain_query_local = lax.dynamic_slice_in_dim(gain_q, side * local_width, local_width)
     gain_key_local = lax.dynamic_slice_in_dim(gain_k, side * local_width, local_width)
 
-    names = gathered[:, 4 * block + 8 :, :token_count]
-    weights = gathered[:, 4 * block + 8 :, token_count : 2 * token_count].astype(
-        FULL
-    ) + gathered[:, 4 * block + 8 :, 2 * token_count : 3 * token_count].astype(FULL)
+    names, *parts = (
+        rest[:, 8:, j * token_count : (j + 1) * token_count] for j in range(3)
+    )
+    weights = parts[0].astype(FULL) + parts[1].astype(FULL)
     named = names == dp_index.astype(LOW)
     picked = jnp.sum(named.astype(FULL), axis=1)
     weight = jnp.sum(jnp.where(named, weights, 0.0), axis=1)
@@ -811,10 +866,6 @@
         blocks = ring_blocks(dp_index)
         weight = weight[blocks]
     weight = weight.reshape(-1, 1)
-
-    cotangent_half = own_half(cotangent)
-    back_rows = lax.all_gather(cotangent_half.astype(LOW), "dp", axis=0, tiled=False)
-    back_rows = (back_rows[blocks] if ring else back_rows).reshape(-1, model_width)
 
     core = dp_index % 2
     tokens_f = inputs.astype(FULL)
@@ -837,9 +888,11 @@
     query_flat, key_flat, values_b = project(
         normed_b, gathered, block, (0, 1, 2), (FULL, FULL, LOW)
     )
-    value_pieces = collect_prompt(values_b[:PR_DEV], 1, 2)
+    key_sq = jnp.sum(key_flat * key_flat, axis=1)
+    key_sq, value_prompt = together(key_sq, values_b[:PR_DEV])
+    value_pieces = collect_prompt(value_prompt, 1, 2)
     query_sq, key_sq = lax.psum(
-        (jnp.sum(query_flat * query_flat, axis=1), jnp.sum(key_flat * key_flat, axis=1)), "tensor"
+        (jnp.sum(query_flat * query_flat, axis=1), key_sq), "tensor"
     )
     query_sq, down_mat = lax.optimization_barrier((query_sq, w_down[0]))
     down_mats = (down_mat, swap_tensor(down_mat))
@@ -849,36 +902,39 @@
     pieces = (*collect_prompt(keys_b[:PR_DEV], 2, 1), *value_pieces)
     queries_b = rope_pass(query_flat, gain_query_local[None], query_scale, cosine, sine)
     context_b = attend(queries_b, keys_b, values_b, bias, pieces)
-    attn_part = project_back([context_b], gathered, block, (3,))
-    attn_part, late = lax.optimization_barrier((attn_part, down_mats[1]))
+    attn_part = project_back([context_b], gathered_out, block, (0,))
+    attn_part, late, weight = together(attn_part, down_mats[1], weight)
     down_mats = (down_mats[0], late)
     mats = (*gate_mats, *up_mats, *down_mats)
     attn_other = swap_tensor(other_half(attn_part).astype(LOW))
+    if ring:
+        gathered, attn_part = together(gathered, attn_part)
+        back_rows = unpack_rows(gathered, blocks, 3 * block + 16, model_width)
+    else:
+        back_rows = lax.all_gather(cotangent_half.astype(LOW), "dp", axis=0, tiled=True)
     attn_other, back_rows, weight = together(attn_other, back_rows, weight)
-    hidden_state = (
-        own_half(tokens_f) + own_half(attn_part) + attn_other.astype(FULL)
-    )
+    hidden_state = own_half(tokens_f) + own_half(attn_part) + attn_other.astype(FULL)
     normed_two_b = rms_norm(hidden_state, gain_two).astype(LOW)
 
     low_tn = lambda left, right: dot_tn(left, right).astype(LOW)
+    upper = lambda array: array[: array.shape[0] // 2]
+    lower = lambda array: array[array.shape[0] // 2 :]
+    hidden_other = swap_tensor(hidden_state)
     if ring:
-        same, cross, held = expert_ring(normed_two_b, back_rows, weight, mats)
-        expert_in, hidden, gate_grad, up_grad = held
-        part = down_mats[0].shape[0]
-        h0, h1 = hidden[:, :part], hidden[:, part:]
-        g0, g1 = gate_grad[:, :part], gate_grad[:, part:]
-        u0, u1 = up_grad[:, :part], up_grad[:, part:]
+        same, cross, held, hidden_other = expert_ring(
+            normed_two_b, back_rows, weight, mats, hidden_other
+        )
+        expert_in, h0, h1, g0, g1, u0, u1 = held
         down_got = swap_tensor(low_tn(h1, back_rows))
         fillers = Fillers(
             [
                 [(low_tn, expert_in, g1)],
                 [(low_tn, expert_in, u1)],
-                [(lambda h: mixed_pass(h, down_mats, blocks), hidden)],
+                [(lambda *h: mixed_pass(*h, down_mats, blocks), h0, h1)],
             ]
         )
         normed_two_grad = ring_sum(same, cross, fillers)
         gate_sent, up_sent, mixed_rows = fillers.outs
-        gate_got = swap_tensor(gate_sent)
     else:
         expert_in = lax.all_gather(normed_two_b, "dp", axis=0, tiled=True)
         grad_rows, h0, h1, g0, g1, u0, u1 = expert_pass(
@@ -889,10 +945,11 @@
         ).astype(FULL)
         mixed_rows = (dot_nn(h0, down_mats[0]) + dot_nn(h1, down_mats[1])).astype(LOW)
         down_got = swap_tensor(low_tn(h1, back_rows))
-        gate_got = swap_tensor(low_tn(expert_in, g1))
+        gate_sent = low_tn(expert_in, g1)
         up_sent = low_tn(expert_in, u1)
-    normed_two_grad, down_got, gate_got, mixed_rows = together(
-        normed_two_grad, down_got, gate_got, mixed_rows
+    gate_first = swap_tensor(upper(gate_sent))
+    normed_two_grad, down_got, gate_first, mixed_rows = together(
+        normed_two_grad, down_got, gate_first, mixed_rows
     )
     mixed = lax.psum_scatter(mixed_rows, "dp", scatter_dimension=0, tiled=True)
 
@@ -901,9 +958,9 @@
     state_half = cotangent_half + state_part
     attn_grad_half = state_half.astype(LOW)
     attn_grad_b = both_halves(attn_grad_half, swap_tensor(attn_grad_half))
-    attn_grad_b, up_sent = together(attn_grad_b, up_sent)
-    up_got = swap_tensor(up_sent)
-    (context_grad_b,) = project(attn_grad_b, gathered, block, (3,), (LOW,))
+    attn_grad_b, gate_sent = together(attn_grad_b, gate_sent)
+    gate_second = swap_tensor(lower(gate_sent))
+    (context_grad_b,) = project(attn_grad_b, gathered_out, block, (0,), (LOW,))
     query_normed_grad, query_inner, query_gain_part, key_grad, value_grad, odd, even = attend_back(
         queries_b,
         keys_b,
@@ -917,66 +974,77 @@
         sine,
         pieces,
     )
-    odd, up_got = together(odd, up_got)
-    key_parts, value_parts = return_prompt(odd, even)
-    key_normed_grad, key_inner, key_gain_part, value_pre_grad = key_back(
-        key_grad,
-        value_grad,
-        key_flat,
-        gain_key_local[None],
-        key_scale,
-        cosine,
-        sine,
-        key_parts,
-        value_parts,
-    )
-    query_inner, key_inner = lax.psum((query_inner[:, 0], key_inner[:, 0]), "tensor")
-    query_inner, key_inner, mixed = together(query_inner, key_inner, mixed)
-    output_half = hidden_state + mixed.astype(FULL)
-    query_cube = query_scale * query_scale * query_scale
-    key_cube = key_scale * key_scale * key_scale
+    query_inner, gate_second = together(query_inner, gate_second)
+    query_inner = lax.psum(query_inner[:, 0], "tensor")
+    query_inner, up_sent = together(query_inner, up_sent)
+    up_first = swap_tensor(upper(up_sent))
     query_pre_grad = (
         query_scale * gain_query_local * query_normed_grad
-        - query_flat * query_cube * (query_inner / column_total)[:, None]
+        - query_flat * (query_scale * query_scale * query_scale) * (query_inner / column_total)[:, None]
     ).astype(LOW)
-    key_pre_grad = (
-        key_scale * gain_key_local * key_normed_grad
-        - key_flat * key_cube * (key_inner / column_total)[:, None]
-    ).astype(LOW)
-    wide = lambda part: lax.dynamic_update_slice_in_dim(
-        jnp.zeros((column_total,), FULL), part, side * local_width, 0
-    )
-    pre_grads = (query_pre_grad, key_pre_grad, value_pre_grad)
-    grad_sum = lambda left, right, got: dot_tn(left, right) + got.astype(FULL)
-    down, gate, up = (h0, back_rows, down_got), (expert_in, g0, gate_got), (expert_in, u0, up_got)
     if ring:
         columns = local_width // 2
         mine = lambda a: lax.dynamic_slice_in_dim(a, core * columns, columns, axis=1)
         theirs = lambda a: lax.dynamic_slice_in_dim(a, (1 - core) * columns, columns, axis=1)
         pair = lambda own, sent: jnp.concatenate([own, swap_bit(sent, "dp", 0)], axis=0)
-        normed_pair = pair(normed_b, normed_b)
-        attn_grad_pair = pair(attn_grad_b, attn_grad_b)
-        context_pair = pair(mine(context_b), theirs(context_b))
-        grad_pair = pair(
-            jnp.concatenate([mine(g) for g in pre_grads], axis=1),
-            jnp.concatenate([theirs(g) for g in pre_grads], axis=1),
-        )
-        normed_pair, attn_grad_pair, context_pair = together(
-            normed_pair, attn_grad_pair, context_pair
-        )
-        out_half = low_tn(attn_grad_pair, context_pair)
-        normed_pair, grad_pair = together(normed_pair, grad_pair)
-        first_half = low_tn(normed_pair, grad_pair)
-        first_half, *pre_grads = together(first_half, *pre_grads)
-        fillers = Fillers([[(grad_sum, *down)], [(grad_sum, *gate)], [(grad_sum, *up)]])
-        w_half = ring_weights(first_half, out_half, fillers)
-        down_grad, gate_w_grad, up_w_grad = fillers.outs
+        half = lambda a: pair(mine(a), theirs(a))
+        normed_pair, attn_grad_pair = pair(normed_b, normed_b), pair(attn_grad_b, attn_grad_b)
+        normed_pair, attn_grad_pair, context_half = together(
+            normed_pair, attn_grad_pair, half(context_b)
+        )
+        normed_pair, query_half = together(normed_pair, half(query_pre_grad))
+        first_halves = ring_weights(
+            low_tn(normed_pair, query_half), low_tn(attn_grad_pair, context_half), Fillers([])
+        )
+    returned = return_prompt(odd, even)
+    key_normed_grad, key_inner, key_gain_part, value_pre_grad = key_back(
+        key_grad, value_grad, key_flat, gain_key_local[None], key_scale, cosine, sine, returned
+    )
+    key_inner, up_first = together(key_inner, up_first)
+    key_inner = lax.psum(key_inner[:, 0], "tensor")
+    key_inner, mixed, up_sent = together(key_inner, mixed, up_sent)
+    up_second = swap_tensor(lower(up_sent))
+    mixed_other = swap_tensor(mixed)
+    key_pre_grad = (
+        key_scale * gain_key_local * key_normed_grad
+        - key_flat * (key_scale * key_scale * key_scale) * (key_inner / column_total)[:, None]
+    ).astype(LOW)
+    output = both_halves(
+        hidden_state + mixed.astype(FULL), hidden_other + mixed_other.astype(FULL)
+    )
+    wide = lambda part: lax.dynamic_update_slice_in_dim(
+        jnp.zeros((column_total,), FULL), part, side * local_width, 0
+    )
+    gate_got = jnp.concatenate([gate_first, gate_second], axis=0)
+    up_got = jnp.concatenate([up_first, up_second], axis=0)
+    pre_grads = (query_pre_grad, key_pre_grad, value_pre_grad)
+    grad_sum = lambda left, right, got: dot_tn(left, right) + got.astype(FULL)
+    down, gate, up = (h0, back_rows, down_got), (expert_in, g0, gate_got), (expert_in, u0, up_got)
+    back_all = lambda *grads: project_back(grads, gathered, block, (0, 1, 2))
+    if ring:
+        fillers = Fillers(
+            [
+                [(back_all, *pre_grads)],
+                [(grad_sum, *down)],
+                [(grad_sum, *gate)],
+                [(grad_sum, *up)],
+            ]
+        )
+        second_halves = ring_weights(
+            low_tn(normed_pair, half(key_pre_grad)),
+            low_tn(normed_pair, half(value_pre_grad)),
+            fillers,
+        )
+        normed_part, down_grad, gate_w_grad, up_w_grad = fillers.outs
+        w_half = jnp.concatenate([first_halves, second_halves], axis=1)
         own_w = lax.dynamic_slice_in_dim(w_half, core * block, block, axis=0)
-        got_w = swap_bit(lax.dynamic_slice_in_dim(w_half, (1 - core) * block, block, axis=0), "dp", 0)
+        got_w = swap_bit(
+            lax.dynamic_slice_in_dim(w_half, (1 - core) * block, block, axis=0), "dp", 0
+        )
         left_w, right_w = jnp.where(core == 0, own_w, got_w), jnp.where(core == 0, got_w, own_w)
         w_sums = [
             jnp.concatenate([w[:, j * columns : (j + 1) * columns] for w in (left_w, right_w)], axis=1)
-            for j in range(4)
+            for j in (0, 2, 3, 1)
         ]
     else:
         w_grads = jnp.concatenate(
@@ -985,8 +1053,7 @@
         w_sum = lax.psum_scatter(w_grads, "dp", scatter_dimension=0, tiled=True).astype(FULL)
         w_sums = [w_sum[:, j * local_width : (j + 1) * local_width] for j in range(4)]
         down_grad, gate_w_grad, up_w_grad = grad_sum(*down), grad_sum(*gate), grad_sum(*up)
-    output = both_halves(output_half, swap_tensor(output_half))
-    normed_part = project_back(pre_grads, gathered, block, (0, 1, 2))
+        normed_part = back_all(*pre_grads)
     normed_other = swap_tensor(other_half(normed_part).astype(LOW))
     normed_grad = own_half(normed_part) + normed_other.astype(FULL)
     unused_one, norm_one_back = jax.vjp(rms_norm, own_half(tokens_f), gain_one)

time: 801 us -> 1090 us (1.36)
  Pallas kernels: 176 us -> 498 us
  waiting for transfers between devices: 360 us -> 301 us
  other arithmetic: 55.7 us -> 74.4 us
    pallas_call x2 -> x4, Pallas kernels: 7.89 us -> 331 us  [the longest x1 320 us: unpack_rows(): pl.pallas_call(lambda *refs: unpack_kernel(first, *refs), in_specs=[pl.Bl...]
    ppermute x12 -> x15, waiting for transfers between devices: 182 us -> 135 us  [swap_tensor(): return lax.ppermute(block, 'tensor', [(0, 1), (1, 0)])]
    ppermute x36 -> x38, waiting for transfers between devices: 91.1 us -> 51.2 us  [swap_bit(): return lax.ppermute(block, axis, [(i, i ^ 1 << bit) for i in range(count)])]
    all_gather x1, waiting for transfers between devices: 0.01 us -> 29.5 us  [body(): gathered = lax.all_gather(packed, 'dp', axis=0, tiled=False)]
    ppermute x12 -> x16, waiting for transfers between devices: 19.8 us -> 28 us  [ahead(): return lax.ppermute(block, 'dp', AHEAD)]
    dot_general x8 -> x10, matrix products: 61.3 us -> 58.1 us  [dot_tn(): lax.dot_general(left, right, (((0,), (0,)), ((), ())), preferred_element_...]
    unnamed x152 -> x210, local copies, waits for them, and re-layouts: 21.8 us -> 24.2 us
    ppermute x12 -> x16, waiting for transfers between devices: 51.1 us -> 50.3 us  [behind(): return lax.ppermute(block, 'dp', BEHIND)]
  transfers between devices with their start and end apart: 75 -> 88, of which waited for: 32 -> 33; matrix products, arithmetic and copies ran while one was open for 18% -> 14% of each run, Pallas kernels for 22% -> 45%
where the time goes in v5:
time: 1090 us; the launch traced here: 1080 us
  Pallas kernels  498 us (46%)
  waiting for transfers between devices  301 us (28%)
  other arithmetic  74.4 us (7%)
  starting transfers between devices  66.7 us (6%)
  matrix products  58.2 us (5%)
  local copies, waits for them, and re-layouts  52 us (5%)
  between operations  16 us (1%)
  blocking collectives  15.9 us (1%)
    pallas_call x1, Pallas kernels, unpack_rows(): pl.pallas_call(lambda *refs: unpack_kernel(first, *refs), in_specs=[pl.Bl...  320 us
    ppermute x15, waiting for transfers between devices, swap_tensor(): return lax.ppermute(block, 'tensor', [(0, 1), (1, 0)])  135 us
    pallas_call x5, Pallas kernels, expert_chunk(): pl.pallas_call(lambda *refs: chunk_kernel(len(pieces), len(held), at, siz...  90.7 us
    dot_general x10, matrix products, dot_tn(): lax.dot_general(left, right, (((0,), (0,)), ((), ())), preferred_element_...  58.1 us
    ppermute x38, waiting for transfers between devices, swap_bit(): return lax.ppermute(block, axis, [(i, i ^ 1 << bit) for i in range(count)])  51.2 us
    ppermute x16, waiting for transfers between devices, behind(): return lax.ppermute(block, 'dp', BEHIND)  50.3 us
    all_gather x1, waiting for transfers between devices, body(): gathered = lax.all_gather(packed, 'dp', axis=0, tiled=False)  29.5 us
    ppermute x16, waiting for transfers between devices, ahead(): return lax.ppermute(block, 'dp', AHEAD)  28 us
  transfers between devices with their start and end apart: 88, of which 33 were waited for; matrix products, arithmetic and copies ran while one was open for 14% of the time, Pallas kernels for 45%

profile of v5, /device:TPU:0, one launch (start us, length us, event | category | flops | bytes accessed | tf_op | source)
XLA Modules:
  0.0 1081.8 jit_solution(17778672498621761899)
XLA Ops:
  10.2 2.5 constant_dynamic-slice_fusion.42.refs_0_
  12.7 2.9 shard_map.282
  16.4 3.0 collective-permute-start
  21.8 44.2 %collective-permute-done.refs_5_.refs_7_ = bf16[2048,512]{1,0:T(8,128)(2,1)} collective-permute-done((bf16[2048,512]{1,0:T(8,128)(2,1)S(1)}, bf16[2048,512]{1,0:T(8,128)(2,1)}, u32[]{:S(2)}, u32[]{:S(2)}) %collective-permute-start) | collective-permute-done | bytes 2097184 | tf_op jit(solution)/shard_map/ppermute | solution.py:25
  66.0 44.1 %collective-permute-done.1.refs_7_.refs_9_ = bf16[2048,512]{1,0:T(8,128)(2,1)} collective-permute-done((bf16[2048,512]{1,0:T(8,128)(2,1)}, bf16[2048,512]{1,0:T(8,128)(2,1)}, u32[]{:S(2)}, u32[]{:S(2)}) %collective-permute-start.1) | collective-permute-done | bytes 2097184 | tf_op jit(solution)/shard_map/ppermute | solution.py:25
  110.2 29.5 %all-gather.5.cloned.1.call-done = bf16[11520,1024]{1,0:T(8,128)(2,1)} async-done(((bf16[720,1024]{1,0:T(8,128)(2,1)}), bf16[11520,1024]{1,0:T(8,128)(2,1)}) %all-gather.5.cloned.1.call-update) | async-done | bytes 23592976 | tf_op jit(solution)/shard_map/all_gather | solution.py:835
  141.7 10.1 shard_map.283
  153.2 5.1 all-reduce.3
  160.2 2.7 shard_map.285.k_ref
  169.3 2.5 collective-permute-done.3
  174.3 3.0 collective-permute-done.6
  178.4 10.0 collective-permute-done.2
  188.4 6.8 collective-permute-done.4
  196.7 2.6 pad_maximum_fusion.8.v_stay
  200.0 5.8 all-gather.7.cloned.1.call-done
  205.8 6.4 copy.79
  215.9 2.7 shard_map.284.q_ref
  223.3 9.8 shard_map.286.refs_0_
  233.1 2.3 shard_map.287
  239.7 319.8 %shard_map.288.refs_3_.refs_5_ = bf16[2560,2048]{1,0:T(8,128)(2,1)} custom-call(s32[16]{0:T(128)} %get-tuple-element.320.refs_0_, bf16[16,720,1024]{2,1,0:T(8,128)(2,1)} %bitcast.106), custom_call_target="tpu_custom_call" | custom-call | tf_op jit(solution)/shard_map/pallas_call | solution.py:419
  559.6 2.7 multiply_reduce_fusion.6
  565.9 2.2 collective-permute-start.16
  568.1 14.7 %collective-permute-done.14.refs_1_ = bf16[160,2048]{1,0:T(8,128)(2,1)} collective-permute-done((bf16[160,2048]{1,0:T(8,128)(2,1)S(1)}, bf16[160,2048]{1,0:T(8,128)(2,1)}, u32[]{:S(2)}, u32[]{:S(2)}) %collective-permute-start.14) | collective-permute-done | bytes 655392 | tf_op jit(solution)/shard_map/ppermute | solution.py:37
  587.2 12.3 %shard_map.289 = (bf16[160,2048]{1,0:T(8,128)(2,1)S(1)}, bf16[160,2048]{1,0:T(8,128)(2,1)S(1)}, bf16[2560,2048]{1,0:T(8,128)(2,1)}, bf16[2560,512]{1,0:T(8,128)(...) custom-call(f32[2560,1]{1,0:T(8,128)S(1)} %copy.80.refs_0_, ...), custom_call_target="tpu_custom_call" | custom-call | flops 6710886400 | bytes 19791872 | tf_op jit(solution)/shard_map/pallas_call | solution.py:670
  603.5 21.3 %shard_map.290 = (bf16[320,2048]{1,0:T(8,128)(2,1)S(1)}, bf16[320,2048]{1,0:T(8,128)(2,1)}, bf16[2560,2048]{1,0:T(8,128)(2,1)}, bf16[2560,512]{1,0:T(8,128)(2,1)...) custom-call(f32[2560,1]{1,0:T(8,128)} %copy-done.2, ...), custom_call_target="tpu_custom_call", output_to_operand_aliasing={{2}: (12, {}), {3}: (13, {}), {4}: (14, {}), {5}: (15, {}),... | custom-call | flops 13421772800 | bytes 27000832 | tf_op jit(solution)/shard_map/pallas_call | solution.py:670
  629.0 21.3 %shard_map.291 = (bf16[320,2048]{1,0:T(8,128)(2,1)S(1)}, bf16[320,2048]{1,0:T(8,128)(2,1)}, bf16[2560,2048]{1,0:T(8,128)(2,1)}, bf16[2560,512]{1,0:T(8,128)(2,1)...) custom-call(f32[2560,1]{1,0:T(8,128)} %copy-done.2, ...), custom_call_target="tpu_custom_call", output_to_operand_aliasing={{2}: (12, {}), {3}: (13, {}), {4}: (14, {}), {5}: (15, {}),... | custom-call | flops 13421772800 | bytes 27000832 | tf_op jit(solution)/shard_map/pallas_call | solution.py:670
  652.0 22.6 %shard_map.292 = (bf16[320,2048]{1,0:T(8,128)(2,1)S(1)}, bf16[320,2048]{1,0:T(8,128)(2,1)}, bf16[2560,2048]{1,0:T(8,128)(2,1)}, bf16[2560,512]{1,0:T(8,128)(2,1)...) custom-call(f32[2560,1]{1,0:T(8,128)} %copy-done.2, ...), custom_call_target="tpu_custom_call", output_to_operand_aliasing={{2}: (12, {}), {3}: (13, {}), {4}: (14, {}), {5}: (15, {}),... | custom-call | flops 13421772800 | bytes 27000832 | tf_op jit(solution)/shard_map/pallas_call | solution.py:670
  675.7 13.1 %shard_map.293 = (bf16[160,2048]{1,0:T(8,128)(2,1)S(1)}, bf16[160,2048]{1,0:T(8,128)(2,1)}, bf16[2560,2048]{1,0:T(8,128)(2,1)}, bf16[2560,512]{1,0:T(8,128)(2,1)...) custom-call(f32[2560,1]{1,0:T(8,128)S(1)} %copy-done.3, ...), custom_call_target="tpu_custom_call", output_to_operand_aliasing={{2}: (12, {}), {3}: (13, {}), {4}: (14, {}), {5}: (15, {}),... | custom-call | flops 6710886400 | bytes 19791872 | tf_op jit(solution)/shard_map/pallas_call | solution.py:670
  693.4 8.4 convolution_convert_fusion.6
  704.3 7.4 collective-permute-done.35
  715.3 13.3 %collective-permute-done.40 = bf16[160,2048]{1,0:T(8,128)(2,1)S(1)} collective-permute-done((bf16[160,2048]{1,0:T(8,128)(2,1)S(1)}, bf16[160,2048]{1,0:T(8,128)(2,1)S(1)}, u32[]{:S(2)}, u32[]{:S(2)}) %collective-permute-start.40) | collective-permute-done | bytes 655392 | tf_op jit(solution)/shard_map/ppermute | solution.py:41
  731.1 5.9 convolution_convert_fusion.5
  738.7 5.1 collective-permute-done.41
  746.3 16.0 %shard_map.294 = bf16[8,2,160,2048]{3,2,1,0:T(8,128)(2,1)} custom-call(s32[8]{0:T(128)S(1)} %and_select_fusion.chip_ref, s32[1]{0:T(128)S(6)} %select_n.361.core_ref, bf16[2560,512]{1,0:T(8,128)(2,1)S(1)} %copy-done.4, bf16[2560,512]{1,0:T(8,128)(2,1)S(1)} %copy-done.6, bf16[512,2048]{1,0:T(8,128)(2,1)S(1)} %bitcast.98, ...), custom_call_target="tpu_custom_call" | custom-call | flops 10737418240 | bytes 19922944 | tf_op jit(solution)/shard_map/pallas_call | solution.py:716
  763.9 8.0 collective-permute-done.44
  776.5 3.8 fusion.51
  781.6 3.9 pad_maximum_fusion.1
  786.4 11.1 %collective-permute-done.45 = bf16[160,2048]{1,0:T(8,128)(2,1)} collective-permute-done((bf16[160,2048]{1,0:T(8,128)(2,1)}, bf16[160,2048]{1,0:T(8,128)(2,1)}, u32[]{:S(2)}, u32[]{:S(2)}) %collective-permute-start.45) | collective-permute-done | bytes 655392 | tf_op jit(solution)/shard_map/ppermute | solution.py:25
  801.1 11.8 %convolution_convert_fusion.4 = bf16[2048,512]{1,0:T(8,128)(2,1)} fusion(bf16[2560,2048]{1,0:T(8,128)(2,1)} %get-tuple-element.261, bf16[2560,512]{1,0:T(8,128)(2,1)S(1)} %copy-done.38), kind=kOutput, calls=%fused_computation.8 | convolution fusion | flops 5369757696 | bytes 15204352 | tf_op jit(solution)/shard_map/dot_general | solution.py:127
  812.9 3.9 shard_map.295.back_ref
  817.7 19.6 %shard_map.296 = (f32[320,1024]{1,0:T(8,128)}, f32[320,1]{1,0:T(8,128)}, f32[1,1024]{1,0:T(1,128)}, f32[320,1024]{1,0:T(8,128)}, f32[320,1024]{1,0:T(8,128)}, /*...) custom-call(bf16[320,1024]{1,0:T(8,128)(2,1)} %shard_map.284.q_ref, ...), custom_call_target="tpu_custom_call" | custom-call | tf_op jit(solution)/shard_map/pallas_call | solution.py:301
  839.4 5.1 psum.30
  857.3 3.7 collective-permute-done.71
  861.9 2.5 collective-permute-start.72
  867.3 3.3 shard_map.297
  873.0 2.3 slice.171
  876.8 11.5 %collective-permute-done.72 = bf16[256,1024]{0,1:T(8,128)(2,1)} collective-permute-done((bf16[256,1024]{0,1:T(8,128)(2,1)}, bf16[256,1024]{0,1:T(8,128)(2,1)}, u32[]{:S(2)}, u32[]{:S(2)}) %collective-permute-start.72) | collective-permute-done | bytes 524320 | tf_op jit(solution)/shard_map/ppermute | solution.py:41
  893.7 5.3 collective-permute-done.47.refs_8_
  900.0 11.6 %collective-permute-done.48.refs_9_ = bf16[2,128,1024]{2,1,0:T(8,128)(2,1)S(1)} collective-permute-done((bf16[2,128,1024]{2,1,0:T(8,128)(2,1)S(1)}, bf16[2,128,1024]{2,1,0:T(8,128)(2,1)S(1)}, u32[]{:S(2)}, u32[]{:S(2)}) %collective-permute-start.48) | collective-permute-done | bytes 524320 | tf_op jit(solution)/shard_map/ppermute | solution.py:21
  915.7 4.7 collective-permute-done.73
  921.4 5.5 collective-permute-done.49.refs_10_
  926.9 5.3 shard_map.298
  936.3 2.6 collective-permute-start.70
  940.0 5.7 psum.31
  946.3 5.0 convolution_convert_fusion.2
  963.7 8.7 shard_map.299
  977.2 4.7 collective-permute-done.75
  984.3 26.7 %collective-permute-done.60 = bf16[160,2048]{1,0:T(8,128)(2,1)S(1)} collective-permute-done((bf16[160,2048]{1,0:T(8,128)(2,1)S(1)}, bf16[160,2048]{1,0:T(8,128)(2,1)S(1)}, u32[]{:S(2)}, u32[]{:S(2)}) %collective-permute-start.60) | collective-permute-done | bytes 655392 | tf_op jit(solution)/shard_map/ppermute | solution.py:25
  1013.5 7.1 add_bitcast_fusion
  1020.8 2.6 fusion.5
  1037.6 8.8 collective-permute-done.81
  1049.0 7.2 add_bitcast_fusion.2
  1056.2 2.5 collective-permute-done.83
  1061.4 7.1 add_bitcast_fusion.1
  (510 shorter events, 172.0 us)
Async XLA Ops:
  7.2 132.5 %all-gather.5.cloned.1.call-start = ((), (), s32[]{:S(2)}) async-start(), calls=%async_computation.2 | async-start | bytes 25067520 | tf_op jit(solution)/shard_map/all_gather | solution.py:835
  15.6 190.2 %all-gather.7.cloned.1.call-start = ((), (), s32[]{:S(2)}) async-start(), calls=%async_computation.3 | async-start | bytes 4456448 | tf_op jit(solution)/shard_map/all_gather | solution.py:836
  16.4 935.0 %reduce-scatter.2.cloned.1.call-start = ((), (), s32[]{:S(2)}) async-start(), calls=%async_computation.1 | async-start | bytes 11141120 | tf_op jit(solution)/shard_map/reduce_scatter | solution.py:954
  16.4 49.6 %collective-permute-start = (bf16[2048,512]{1,0:T(8,128)(2,1)S(1)}, bf16[2048,512]{1,0:T(8,128)(2,1)}, u32[]{:S(2)}, u32[]{:S(2)}) collective-permute-start(bf16[2048,512]{1,0:T(8,128)(2,1)S(1)} %bitcast.119), channel_id=1, source_target_pairs={{0,1},{1,0},{2,3},{3,2},{4,5},{5,4},{6,7},{7,6},{8,9},{9,8},{10,11... | collective-permute-start | bytes 6291464 | tf_op jit(solution)/shard_map/ppermute | solution.py:25
  19.5 90.7 %collective-permute-start.1 = (bf16[2048,512]{1,0:T(8,128)(2,1)}, bf16[2048,512]{1,0:T(8,128)(2,1)}, u32[]{:S(2)}, u32[]{:S(2)}) collective-permute-start(bf16[2048,512]{1,0:T(8,128)(2,1)} %bitcast.120), channel_id=1, source_target_pairs={{0,1},{1,0},{2,3},{3,2},{4,5},{5,4},{6,7},{7,6},{8,9},{9,8},{10,11... | collective-permute-start | bytes 6291464 | tf_op jit(solution)/shard_map/ppermute | solution.py:25
  166.9 21.5 %collective-permute-start.2 = (bf16[128,1024]{1,0:T(8,128)(2,1)S(1)}, bf16[128,1024]{1,0:T(8,128)(2,1)S(1)}, u32[]{:S(2)}, u32[]{:S(2)}) collective-permute-start(bf16[128,1024]{1,0:T(8,128)(2,1)S(1)} %get-tuple-element.385), channel_id=1, source_target_pairs={{0,4},{2,6},{4,0},{6,2},{8,12},{10,14},{12,8},{14,10},{16,20},{18,... | collective-permute-start | bytes 786440 | tf_op jit(solution)/shard_map/ppermute | solution.py:21
  167.8 67.7 %collective-permute-start.10 = (bf16[512,2048]{1,0:T(8,128)(2,1)S(1)}, bf16[512,2048]{1,0:T(8,128)(2,1)}, u32[]{:S(2)}, u32[]{:S(2)}) collective-permute-start(bf16[512,2048]{1,0:T(8,128)(2,1)S(1)} %bitcast.97), channel_id=1, source_target_pairs={{0,1},{1,0},{2,3},{3,2},{4,5},{5,4},{6,7},{7,6},{8,9},{9,8},{10,11... | collective-permute-start | bytes 6291464 | tf_op jit(solution)/shard_map/ppermute | solution.py:25
  171.9 23.4 %collective-permute-start.4 = (bf16[128,1024]{1,0:T(8,128)(2,1)S(1)}, bf16[128,1024]{1,0:T(8,128)(2,1)}, u32[]{:S(2)}, u32[]{:S(2)}) collective-permute-start(bf16[128,1024]{1,0:T(8,128)(2,1)S(1)} %collective-permute-done.3), channel_id=1, source_target_pairs={{0,4},{2,6},{4,0},{6,2},{8,12},{10,14},{12,8},{14,10},{16,20},{18,... | collective-permute-start | bytes 786440 | tf_op jit(solution)/shard_map/ppermute | solution.py:21
  172.6 24.0 %collective-permute-start.7 = (bf16[128,1024]{1,0:T(8,128)(2,1)}, bf16[128,1024]{1,0:T(8,128)(2,1)}, u32[]{:S(2)}, u32[]{:S(2)}) collective-permute-start(bf16[128,1024]{1,0:T(8,128)(2,1)} %slice.147), channel_id=1, source_target_pairs={{0,8},{2,10},{4,12},{6,14},{8,0},{10,2},{12,4},{14,6},{16,24},{18,... | collective-permute-start | bytes 786440 | tf_op jit(solution)/shard_map/ppermute | solution.py:21
  177.3 19.3 %collective-permute-start.8 = (bf16[128,1024]{1,0:T(8,128)(2,1)}, bf16[128,1024]{1,0:T(8,128)(2,1)}, u32[]{:S(2)}, u32[]{:S(2)}) collective-permute-start(bf16[128,1024]{1,0:T(8,128)(2,1)} %collective-permute-done.6), channel_id=1, source_target_pairs={{0,8},{2,10},{4,12},{6,14},{8,0},{10,2},{12,4},{14,6},{16,24},{18,... | collective-permute-start | bytes 786440 | tf_op jit(solution)/shard_map/ppermute | solution.py:21
  196.6 22.0 %collective-permute-start.5 = (bf16[4,128,1024]{2,1,0:T(8,128)(2,1)S(1)}, bf16[4,128,1024]{2,1,0:T(8,128)(2,1)}, u32[]{:S(2)}, u32[]{:S(2)}) collective-permute-start(bf16[4,128,1024]{2,1,0:T(8,128)(2,1)S(1)} %pad_maximum_fusion.7.k_stay), channel_id=1, source_target_pairs={{0,2},{2,0},{4,6},{6,4},{8,10},{10,8},{12,14},{14,12},{16,18},{18,... | collective-permute-start | bytes 3145736 | tf_op jit(solution)/shard_map/ppermute | solution.py:21
  199.2 19.3 %collective-permute-start.9 = (bf16[4,128,1024]{2,1,0:T(8,128)(2,1)}, bf16[4,128,1024]{2,1,0:T(8,128)(2,1)}, u32[]{:S(2)}, u32[]{:S(2)}) collective-permute-start(bf16[4,128,1024]{2,1,0:T(8,128)(2,1)} %pad_maximum_fusion.8.v_stay), channel_id=1, source_target_pairs={{0,2},{2,0},{4,6},{6,4},{8,10},{10,8},{12,14},{14,12},{16,18},{18,... | collective-permute-start | bytes 3145736 | tf_op jit(solution)/shard_map/ppermute | solution.py:21
  236.4 323.1 %collective-permute-start.11 = (bf16[160,2048]{1,0:T(8,128)(2,1)}, bf16[160,2048]{1,0:T(8,128)(2,1)S(1)}, u32[]{:S(2)}, u32[]{:S(2)}) collective-permute-start(bf16[160,2048]{1,0:T(8,128)(2,1)} %dynamic-slice_convert_fusion.1), channel_id=1, source_target_pairs={{0,1},{1,0},{2,3},{3,2},{4,5},{5,4},{6,7},{7,6},{8,9},{9,8},{10,11... | collective-permute-start | bytes 1966088 | tf_op jit(solution)/shard_map/ppermute | solution.py:25
  565.9 16.9 %collective-permute-start.14 = (bf16[160,2048]{1,0:T(8,128)(2,1)S(1)}, bf16[160,2048]{1,0:T(8,128)(2,1)}, u32[]{:S(2)}, u32[]{:S(2)}) collective-permute-start(bf16[160,2048]{1,0:T(8,128)(2,1)S(1)} %multiply_convert_fusion.1.refs_1_), channel_id=1, source_target_pairs={{0,8},{2,10},{8,16},{10,18},{16,24},{18,26},{24,28},{26,30},{28,20... | collective-permute-start | bytes 1966088 | tf_op jit(solution)/shard_map/ppermute | solution.py:37
  565.9 17.2 %collective-permute-start.16 = (bf16[160,2048]{1,0:T(8,128)(2,1)S(1)}, bf16[160,2048]{1,0:T(8,128)(2,1)}, u32[]{:S(2)}, u32[]{:S(2)}) collective-permute-start(bf16[160,2048]{1,0:T(8,128)(2,1)S(1)} %multiply_convert_fusion.1.refs_1_), channel_id=1, source_target_pairs={{8,0},{10,2},{16,8},{18,10},{24,16},{26,18},{28,24},{30,26},{20,28... | collective-permute-start | bytes 1966088 | tf_op jit(solution)/shard_map/ppermute | solution.py:41
  582.8 18.5 %collective-permute-start.19 = (bf16[160,2048]{1,0:T(8,128)(2,1)}, bf16[160,2048]{1,0:T(8,128)(2,1)S(1)}, u32[]{:S(2)}, u32[]{:S(2)}) collective-permute-start(bf16[160,2048]{1,0:T(8,128)(2,1)} %collective-permute-done.14.refs_1_), channel_id=1, source_target_pairs={{0,8},{2,10},{8,16},{10,18},{16,24},{18,26},{24,28},{26,30},{28,20... | collective-permute-start | bytes 1966088 | tf_op jit(solution)/shard_map/ppermute | solution.py:37
  583.1 18.5 %collective-permute-start.21 = (bf16[160,2048]{1,0:T(8,128)(2,1)}, bf16[160,2048]{1,0:T(8,128)(2,1)}, u32[]{:S(2)}, u32[]{:S(2)}) collective-permute-start(bf16[160,2048]{1,0:T(8,128)(2,1)} %collective-permute-done.16.refs_3_), channel_id=1, source_target_pairs={{8,0},{10,2},{16,8},{18,10},{24,16},{26,18},{28,24},{30,26},{20,28... | collective-permute-start | bytes 1966088 | tf_op jit(solution)/shard_map/ppermute | solution.py:41
  584.8 16.7 %collective-permute-start.15 = (bf16[160,2048]{1,0:T(8,128)(2,1)}, bf16[160,2048]{1,0:T(8,128)(2,1)}, u32[]{:S(2)}, u32[]{:S(2)}) collective-permute-start(bf16[160,2048]{1,0:T(8,128)(2,1)} %collective-permute-done.14.refs_1_), channel_id=1, source_target_pairs={{0,2},{2,0},{4,6},{6,4},{8,10},{10,8},{12,14},{14,12},{16,18},{18,... | collective-permute-start | bytes 1966088 | tf_op jit(solution)/shard_map/ppermute | solution.py:21
  584.8 18.5 %collective-permute-start.17 = (bf16[160,2048]{1,0:T(8,128)(2,1)}, bf16[160,2048]{1,0:T(8,128)(2,1)}, u32[]{:S(2)}, u32[]{:S(2)}) collective-permute-start(bf16[160,2048]{1,0:T(8,128)(2,1)} %collective-permute-done.16.refs_3_), channel_id=1, source_target_pairs={{0,2},{2,0},{4,6},{6,4},{8,10},{10,8},{12,14},{14,12},{16,18},{18,... | collective-permute-start | bytes 1966088 | tf_op jit(solution)/shard_map/ppermute | solution.py:21
  585.3 66.1 %collective-permute-start.25 = (f32[160,2048]{1,0:T(8,128)}, f32[160,2048]{1,0:T(8,128)}, u32[]{:S(2)}, u32[]{:S(2)}) collective-permute-start(f32[160,2048]{1,0:T(8,128)} %get-tuple-element.318), channel_id=1, source_target_pairs={{0,1},{1,0},{2,3},{3,2},{4,5},{5,4},{6,7},{7,6},{8,9},{9,8},{10,11... | collective-permute-start | bytes 3932168 | tf_op jit(solution)/shard_map/ppermute | solution.py:25
  601.3 24.7 %collective-permute-start.24 = (bf16[160,2048]{1,0:T(8,128)(2,1)S(1)}, bf16[160,2048]{1,0:T(8,128)(2,1)S(1)}, u32[]{:S(2)}, u32[]{:S(2)}) collective-permute-start(bf16[160,2048]{1,0:T(8,128)(2,1)S(1)} %collective-permute-done.19.refs_1_), channel_id=1, source_target_pairs={{0,8},{2,10},{8,16},{10,18},{16,24},{18,26},{24,28},{26,30},{28,20... | collective-permute-start | bytes 1966088 | tf_op jit(solution)/shard_map/ppermute | solution.py:37
  601.5 27.0 %collective-permute-start.20 = (bf16[160,2048]{1,0:T(8,128)(2,1)S(1)}, bf16[160,2048]{1,0:T(8,128)(2,1)S(1)}, u32[]{:S(2)}, u32[]{:S(2)}) collective-permute-start(bf16[160,2048]{1,0:T(8,128)(2,1)S(1)} %collective-permute-done.19.refs_1_), channel_id=1, source_target_pairs={{0,2},{2,0},{4,6},{6,4},{8,10},{10,8},{12,14},{14,12},{16,18},{18,... | collective-permute-start | bytes 1966088 | tf_op jit(solution)/shard_map/ppermute | solution.py:21
  601.6 24.7 %collective-permute-start.27 = (bf16[160,2048]{1,0:T(8,128)(2,1)}, bf16[160,2048]{1,0:T(8,128)(2,1)S(1)}, u32[]{:S(2)}, u32[]{:S(2)}) collective-permute-start(bf16[160,2048]{1,0:T(8,128)(2,1)} %collective-permute-done.21.refs_3_), channel_id=1, source_target_pairs={{8,0},{10,2},{16,8},{18,10},{24,16},{26,18},{28,24},{30,26},{20,28... | collective-permute-start | bytes 1966088 | tf_op jit(solution)/shard_map/ppermute | solution.py:41
  603.4 25.2 %collective-permute-start.22 = (bf16[160,2048]{1,0:T(8,128)(2,1)}, bf16[160,2048]{1,0:T(8,128)(2,1)S(1)}, u32[]{:S(2)}, u32[]{:S(2)}) collective-permute-start(bf16[160,2048]{1,0:T(8,128)(2,1)} %collective-permute-done.21.refs_3_), channel_id=1, source_target_pairs={{0,2},{2,0},{4,6},{6,4},{8,10},{10,8},{12,14},{14,12},{16,18},{18,... | collective-permute-start | bytes 1966088 | tf_op jit(solution)/shard_map/ppermute | solution.py:21
  626.0 25.5 %collective-permute-start.30 = (bf16[80,2048]{1,0:T(8,128)(2,1)S(1)}, bf16[80,2048]{1,0:T(8,128)(2,1)S(1)}, u32[]{:S(2)}, u32[]{:S(2)}) collective-permute-start(bf16[80,2048]{1,0:T(8,128)(2,1)S(1)} %slice.197), channel_id=1, source_target_pairs={{0,8},{2,10},{8,16},{10,18},{16,24},{18,26},{24,28},{26,30},{28,20... | collective-permute-start | bytes 983048 | tf_op jit(solution)/shard_map/ppermute | solution.py:37
  626.3 25.2 %collective-permute-start.31 = (bf16[80,2048]{1,0:T(8,128)(2,1)S(1)}, bf16[80,2048]{1,0:T(8,128)(2,1)S(1)}, u32[]{:S(2)}, u32[]{:S(2)}) collective-permute-start(bf16[80,2048]{1,0:T(8,128)(2,1)S(1)} %slice.198), channel_id=1, source_target_pairs={{8,0},{10,2},{16,8},{18,10},{24,16},{26,18},{28,24},{30,26},{20,28... | collective-permute-start | bytes 983048 | tf_op jit(solution)/shard_map/ppermute | solution.py:41
  628.5 23.4 %collective-permute-start.26 = (bf16[160,2048]{1,0:T(8,128)(2,1)S(1)}, bf16[160,2048]{1,0:T(8,128)(2,1)S(1)}, u32[]{:S(2)}, u32[]{:S(2)}) collective-permute-start(bf16[160,2048]{1,0:T(8,128)(2,1)S(1)} %collective-permute-done.24.refs_1_), channel_id=1, source_target_pairs={{0,2},{2,0},{4,6},{6,4},{8,10},{10,8},{12,14},{14,12},{16,18},{18,... | collective-permute-start | bytes 1966088 | tf_op jit(solution)/shard_map/ppermute | solution.py:21
  628.5 23.4 %collective-permute-start.28 = (bf16[160,2048]{1,0:T(8,128)(2,1)S(1)}, bf16[160,2048]{1,0:T(8,128)(2,1)S(1)}, u32[]{:S(2)}, u32[]{:S(2)}) collective-permute-start(bf16[160,2048]{1,0:T(8,128)(2,1)S(1)} %collective-permute-done.27.refs_3_), channel_id=1, source_target_pairs={{0,2},{2,0},{4,6},{6,4},{8,10},{10,8},{12,14},{14,12},{16,18},{18,... | collective-permute-start | bytes 1966088 | tf_op jit(solution)/shard_map/ppermute | solution.py:21
  651.5 24.2 %collective-permute-start.32 = (bf16[80,2048]{1,0:T(8,128)(2,1)S(1)}, bf16[80,2048]{1,0:T(8,128)(2,1)S(1)}, u32[]{:S(2)}, u32[]{:S(2)}) collective-permute-start(bf16[80,2048]{1,0:T(8,128)(2,1)S(1)} %collective-permute-done.30.refs_1_), channel_id=1, source_target_pairs={{0,2},{2,0},{4,6},{6,4},{8,10},{10,8},{12,14},{14,12},{16,18},{18,... | collective-permute-start | bytes 983048 | tf_op jit(solution)/shard_map/ppermute | solution.py:21
  651.5 24.2 %collective-permute-start.33 = (bf16[80,2048]{1,0:T(8,128)(2,1)S(1)}, bf16[80,2048]{1,0:T(8,128)(2,1)S(1)}, u32[]{:S(2)}, u32[]{:S(2)}) collective-permute-start(bf16[80,2048]{1,0:T(8,128)(2,1)S(1)} %collective-permute-done.31.refs_2_), channel_id=1, source_target_pairs={{0,2},{2,0},{4,6},{6,4},{8,10},{10,8},{12,14},{14,12},{16,18},{18,... | collective-permute-start | bytes 983048 | tf_op jit(solution)/shard_map/ppermute | solution.py:21
  689.2 73.1 %collective-permute-start.13 = (bf16[160,2048]{1,0:T(8,128)(2,1)}, bf16[160,2048]{1,0:T(8,128)(2,1)S(1)}, u32[]{:S(2)}, u32[]{:S(2)}) collective-permute-start(bf16[160,2048]{1,0:T(8,128)(2,1)} %copy-done.32), channel_id=1, source_target_pairs={{0,2},{2,0},{4,6},{6,4},{8,10},{10,8},{12,14},{14,12},{16,18},{18,... | collective-permute-start | bytes 1966088 | tf_op jit(solution)/shard_map/ppermute | solution.py:21
  689.7 23.8 %collective-permute-start.18 = (bf16[320,2048]{1,0:T(8,128)(2,1)}, bf16[320,2048]{1,0:T(8,128)(2,1)S(1)}, u32[]{:S(2)}, u32[]{:S(2)}) collective-permute-start(bf16[320,2048]{1,0:T(8,128)(2,1)} %get-tuple-element.170), channel_id=1, source_target_pairs={{0,2},{2,0},{4,6},{6,4},{8,10},{10,8},{12,14},{14,12},{16,18},{18,... | collective-permute-start | bytes 3932168 | tf_op jit(solution)/shard_map/ppermute | solution.py:21
  689.8 25.0 %collective-permute-start.23 = (bf16[320,2048]{1,0:T(8,128)(2,1)}, bf16[320,2048]{1,0:T(8,128)(2,1)S(1)}, u32[]{:S(2)}, u32[]{:S(2)}) collective-permute-start(bf16[320,2048]{1,0:T(8,128)(2,1)} %get-tuple-element.179), channel_id=1, source_target_pairs={{0,2},{2,0},{4,6},{6,4},{8,10},{10,8},{12,14},{14,12},{16,18},{18,... | collective-permute-start | bytes 3932168 | tf_op jit(solution)/shard_map/ppermute | solution.py:21
  702.5 70.3 %collective-permute-start.43 = (bf16[512,2048]{1,0:T(8,128)(2,1)S(1)}, bf16[512,2048]{1,0:T(8,128)(2,1)S(1)}, u32[]{:S(2)}, u32[]{:S(2)}) collective-permute-start(bf16[512,2048]{1,0:T(8,128)(2,1)S(1)} %convolution_convert_fusion.6), channel_id=1, source_target_pairs={{0,1},{1,0},{2,3},{3,2},{4,5},{5,4},{6,7},{7,6},{8,9},{9,8},{10,11... | collective-permute-start | bytes 6291464 | tf_op jit(solution)/shard_map/ppermute | solution.py:25
  712.1 16.5 %collective-permute-start.36 = (bf16[160,2048]{1,0:T(8,128)(2,1)S(1)}, bf16[160,2048]{1,0:T(8,128)(2,1)S(1)}, u32[]{:S(2)}, u32[]{:S(2)}) collective-permute-start(bf16[160,2048]{1,0:T(8,128)(2,1)S(1)} %pad_maximum_fusion.9), channel_id=1, source_target_pairs={{0,8},{2,10},{8,16},{10,18},{16,24},{18,26},{24,28},{26,30},{28,20... | collective-permute-start | bytes 1966088 | tf_op jit(solution)/shard_map/ppermute | solution.py:37
  713.5 15.1 %collective-permute-start.40 = (bf16[160,2048]{1,0:T(8,128)(2,1)S(1)}, bf16[160,2048]{1,0:T(8,128)(2,1)S(1)}, u32[]{:S(2)}, u32[]{:S(2)}) collective-permute-start(bf16[160,2048]{1,0:T(8,128)(2,1)S(1)} %pad_maximum_fusion.10), channel_id=1, source_target_pairs={{8,0},{10,2},{16,8},{18,10},{24,16},{26,18},{28,24},{30,26},{20,28... | collective-permute-start | bytes 1966088 | tf_op jit(solution)/shard_map/ppermute | solution.py:41
  729.1 14.7 %collective-permute-start.37 = (bf16[160,2048]{1,0:T(8,128)(2,1)S(1)}, bf16[160,2048]{1,0:T(8,128)(2,1)S(1)}, u32[]{:S(2)}, u32[]{:S(2)}) collective-permute-start(bf16[160,2048]{1,0:T(8,128)(2,1)S(1)} %get-tuple-element.360), channel_id=1, source_target_pairs={{0,8},{2,10},{8,16},{10,18},{16,24},{18,26},{24,28},{26,30},{28,20... | collective-permute-start | bytes 1966088 | tf_op jit(solution)/shard_map/ppermute | solution.py:37
  729.4 14.3 %collective-permute-start.41 = (bf16[160,2048]{1,0:T(8,128)(2,1)S(1)}, bf16[160,2048]{1,0:T(8,128)(2,1)S(1)}, u32[]{:S(2)}, u32[]{:S(2)}) collective-permute-start(bf16[160,2048]{1,0:T(8,128)(2,1)S(1)} %get-tuple-element.361), channel_id=1, source_target_pairs={{8,0},{10,2},{16,8},{18,10},{24,16},{26,18},{28,24},{30,26},{20,28... | collective-permute-start | bytes 1966088 | tf_op jit(solution)/shard_map/ppermute | solution.py:41
  737.1 34.7 %collective-permute-start.44 = (bf16[1024,512]{1,0:T(8,128)(2,1)S(1)}, bf16[1024,512]{1,0:T(8,128)(2,1)S(1)}, u32[]{:S(2)}, u32[]{:S(2)}) collective-permute-start(bf16[1024,512]{1,0:T(8,128)(2,1)S(1)} %slice.206), channel_id=1, source_target_pairs={{0,1},{1,0},{2,3},{3,2},{4,5},{5,4},{6,7},{7,6},{8,9},{9,8},{10,11... | collective-permute-start | bytes 3145736 | tf_op jit(solution)/shard_map/ppermute | solution.py:25
  744.3 18.1 %collective-permute-start.42 = (bf16[160,2048]{1,0:T(8,128)(2,1)S(1)}, bf16[160,2048]{1,0:T(8,128)(2,1)S(1)}, u32[]{:S(2)}, u32[]{:S(2)}) collective-permute-start(bf16[160,2048]{1,0:T(8,128)(2,1)S(1)} %get-tuple-element.359), channel_id=1, source_target_pairs={{8,0},{10,2},{16,8},{18,10},{24,16},{26,18},{28,24},{30,26},{20,28... | collective-permute-start | bytes 1966088 | tf_op jit(solution)/shard_map/ppermute | solution.py:41
  746.0 16.3 %collective-permute-start.38 = (bf16[160,2048]{1,0:T(8,128)(2,1)S(1)}, bf16[160,2048]{1,0:T(8,128)(2,1)S(1)}, u32[]{:S(2)}, u32[]{:S(2)}) collective-permute-start(bf16[160,2048]{1,0:T(8,128)(2,1)S(1)} %get-tuple-element.358), channel_id=1, source_target_pairs={{0,8},{2,10},{8,16},{10,18},{16,24},{18,26},{24,28},{26,30},{28,20... | collective-permute-start | bytes 1966088 | tf_op jit(solution)/shard_map/ppermute | solution.py:37
  780.2 17.3 %collective-permute-start.45 = (bf16[160,2048]{1,0:T(8,128)(2,1)}, bf16[160,2048]{1,0:T(8,128)(2,1)}, u32[]{:S(2)}, u32[]{:S(2)}) collective-permute-start(bf16[160,2048]{1,0:T(8,128)(2,1)} %get-tuple-element.315), channel_id=1, source_target_pairs={{0,1},{1,0},{2,3},{3,2},{4,5},{5,4},{6,7},{7,6},{8,9},{9,8},{10,11... | collective-permute-start | bytes 1966088 | tf_op jit(solution)/shard_map/ppermute | solution.py:25
  800.2 37.2 %collective-permute-start.51 = (bf16[1024,512]{1,0:T(8,128)(2,1)S(1)}, bf16[1024,512]{1,0:T(8,128)(2,1)S(1)}, u32[]{:S(2)}, u32[]{:S(2)}) collective-permute-start(bf16[1024,512]{1,0:T(8,128)(2,1)S(1)} %slice.170), channel_id=1, source_target_pairs={{0,1},{1,0},{2,3},{3,2},{4,5},{5,4},{6,7},{7,6},{8,9},{9,8},{10,11... | collective-permute-start | bytes 3145736 | tf_op jit(solution)/shard_map/ppermute | solution.py:25
  800.7 46.2 %collective-permute-start.55 = (bf16[320,2048]{1,0:T(8,128)(2,1)}, bf16[320,2048]{1,0:T(8,128)(2,1)}, u32[]{:S(2)}, u32[]{:S(2)}) collective-permute-start(bf16[320,2048]{1,0:T(8,128)(2,1)} %pad_maximum_fusion.6.refs_0_), channel_id=1, source_target_pairs={{0,2},{2,0},{4,6},{6,4},{8,10},{10,8},{12,14},{14,12},{16,18},{18,... | collective-permute-start | bytes 3932168 | tf_op jit(solution)/shard_map/ppermute | solution.py:21
  837.3 29.9 %collective-permute-start.46 = (bf16[4,2,128,1024]{3,2,1,0:T(8,128)(2,1)}, bf16[4,2,128,1024]{3,2,1,0:T(8,128)(2,1)}, u32[]{:S(2)}, u32[]{:S(2)}) collective-permute-start(bf16[4,2,128,1024]{3,2,1,0:T(8,128)(2,1)} %get-tuple-element.215), channel_id=1, source_target_pairs={{0,2},{2,0},{4,6},{6,4},{8,10},{10,8},{12,14},{14,12},{16,18},{18,... | collective-permute-start | bytes 6291464 | tf_op jit(solution)/shard_map/ppermute | solution.py:21
  861.9 26.4 %collective-permute-start.72 = (bf16[256,1024]{0,1:T(8,128)(2,1)}, bf16[256,1024]{0,1:T(8,128)(2,1)}, u32[]{:S(2)}, u32[]{:S(2)}) collective-permute-start(bf16[256,1024]{0,1:T(8,128)(2,1)} %pad_maximum_fusion.15), channel_id=1, source_target_pairs={{8,0},{10,2},{16,8},{18,10},{24,16},{26,18},{28,24},{30,26},{20,28... | collective-permute-start | bytes 1572872 | tf_op jit(solution)/shard_map/ppermute | solution.py:41
  865.8 24.0 %collective-permute-start.68 = (bf16[256,1024]{0,1:T(8,128)(2,1)}, bf16[256,1024]{0,1:T(8,128)(2,1)}, u32[]{:S(2)}, u32[]{:S(2)}) collective-permute-start(bf16[256,1024]{0,1:T(8,128)(2,1)} %pad_maximum_fusion.14), channel_id=1, source_target_pairs={{0,8},{2,10},{8,16},{10,18},{16,24},{18,26},{24,28},{26,30},{28,20... | collective-permute-start | bytes 1572872 | tf_op jit(solution)/shard_map/ppermute | solution.py:37
  870.6 28.4 %collective-permute-start.47 = (bf16[2,128,1024]{2,1,0:T(8,128)(2,1)}, bf16[2,128,1024]{2,1,0:T(8,128)(2,1)S(1)}, u32[]{:S(2)}, u32[]{:S(2)}) collective-permute-start(bf16[2,128,1024]{2,1,0:T(8,128)(2,1)} %get-tuple-element.217), channel_id=1, source_target_pairs={{0,4},{2,6},{4,0},{6,2},{8,12},{10,14},{12,8},{14,10},{16,20},{18,... | collective-permute-start | bytes 1572872 | tf_op jit(solution)/shard_map/ppermute | solution.py:21
  875.2 63.7 %collective-permute-start.52 = (bf16[1024,512]{1,0:T(8,128)(2,1)}, bf16[1024,512]{1,0:T(8,128)(2,1)}, u32[]{:S(2)}, u32[]{:S(2)}) collective-permute-start(bf16[1024,512]{1,0:T(8,128)(2,1)} %slice.171), channel_id=1, source_target_pairs={{0,1},{1,0},{2,3},{3,2},{4,5},{5,4},{6,7},{7,6},{8,9},{9,8},{10,11... | collective-permute-start | bytes 3145736 | tf_op jit(solution)/shard_map/ppermute | solution.py:25
  876.4 35.2 %collective-permute-start.48 = (bf16[2,128,1024]{2,1,0:T(8,128)(2,1)S(1)}, bf16[2,128,1024]{2,1,0:T(8,128)(2,1)S(1)}, u32[]{:S(2)}, u32[]{:S(2)}) collective-permute-start(bf16[2,128,1024]{2,1,0:T(8,128)(2,1)S(1)} %copy-done.96), channel_id=1, source_target_pairs={{0,8},{2,10},{4,12},{6,14},{8,0},{10,2},{12,4},{14,6},{16,24},{18,... | collective-permute-start | bytes 1572872 | tf_op jit(solution)/shard_map/ppermute | solution.py:21
  889.7 30.7 %collective-permute-start.73 = (bf16[256,1024]{0,1:T(8,128)(2,1)S(1)}, bf16[256,1024]{0,1:T(8,128)(2,1)S(1)}, u32[]{:S(2)}, u32[]{:S(2)}) collective-permute-start(bf16[256,1024]{0,1:T(8,128)(2,1)S(1)} %add_convert_fusion.14), channel_id=1, source_target_pairs={{8,0},{10,2},{16,8},{18,10},{24,16},{26,18},{28,24},{30,26},{20,28... | collective-permute-start | bytes 1572872 | tf_op jit(solution)/shard_map/ppermute | solution.py:41
  891.7 42.5 %collective-permute-start.69 = (bf16[256,1024]{0,1:T(8,128)(2,1)}, bf16[256,1024]{0,1:T(8,128)(2,1)}, u32[]{:S(2)}, u32[]{:S(2)}) collective-permute-start(bf16[256,1024]{0,1:T(8,128)(2,1)} %add_convert_fusion.16), channel_id=1, source_target_pairs={{0,8},{2,10},{8,16},{10,18},{16,24},{18,26},{24,28},{26,30},{28,20... | collective-permute-start | bytes 1572872 | tf_op jit(solution)/shard_map/ppermute | solution.py:37
  899.9 27.0 %collective-permute-start.49 = (bf16[128,1024]{1,0:T(8,128)(2,1)S(1)}, bf16[128,1024]{1,0:T(8,128)(2,1)}, u32[]{:S(2)}, u32[]{:S(2)}) collective-permute-start(bf16[128,1024]{1,0:T(8,128)(2,1)S(1)} %fusion.13), channel_id=1, source_target_pairs={{0,8},{2,10},{4,12},{6,14},{8,0},{10,2},{12,4},{14,6},{16,24},{18,... | collective-permute-start | bytes 786440 | tf_op jit(solution)/shard_map/ppermute | solution.py:21
  912.5 14.4 %collective-permute-start.50 = (bf16[128,1024]{1,0:T(8,128)(2,1)S(1)}, bf16[128,1024]{1,0:T(8,128)(2,1)}, u32[]{:S(2)}, u32[]{:S(2)}) collective-permute-start(bf16[128,1024]{1,0:T(8,128)(2,1)S(1)} %fusion.12), channel_id=1, source_target_pairs={{0,4},{2,6},{4,0},{6,2},{8,12},{10,14},{12,8},{14,10},{16,20},{18,... | collective-permute-start | bytes 786440 | tf_op jit(solution)/shard_map/ppermute | solution.py:21
  921.4 34.2 %collective-permute-start.74 = (bf16[256,1024]{0,1:T(8,128)(2,1)}, bf16[256,1024]{0,1:T(8,128)(2,1)}, u32[]{:S(2)}, u32[]{:S(2)}) collective-permute-start(bf16[256,1024]{0,1:T(8,128)(2,1)} %add_convert_fusion.13), channel_id=1, source_target_pairs={{8,0},{10,2},{16,8},{18,10},{24,16},{26,18},{28,24},{30,26},{20,28... | collective-permute-start | bytes 1572872 | tf_op jit(solution)/shard_map/ppermute | solution.py:41
  936.3 19.2 %collective-permute-start.70 = (bf16[256,1024]{0,1:T(8,128)(2,1)}, bf16[256,1024]{0,1:T(8,128)(2,1)}, u32[]{:S(2)}, u32[]{:S(2)}) collective-permute-start(bf16[256,1024]{0,1:T(8,128)(2,1)} %add_convert_fusion.15), channel_id=1, source_target_pairs={{0,8},{2,10},{8,16},{10,18},{16,24},{18,26},{24,28},{26,30},{28,20... | collective-permute-start | bytes 1572872 | tf_op jit(solution)/shard_map/ppermute | solution.py:37
  957.1 63.6 %collective-permute-start.53 = (bf16[160,2048]{1,0:T(8,128)(2,1)}, bf16[160,2048]{1,0:T(8,128)(2,1)}, u32[]{:S(2)}, u32[]{:S(2)}) collective-permute-start(bf16[160,2048]{1,0:T(8,128)(2,1)} %reduce-scatter.2.cloned.1.call-done), channel_id=1, source_target_pairs={{0,1},{1,0},{2,3},{3,2},{4,5},{5,4},{6,7},{7,6},{8,9},{9,8},{10,11... | collective-permute-start | bytes 1966088 | tf_op jit(solution)/shard_map/ppermute | solution.py:25
  959.7 76.1 %collective-permute-start.82 = (bf16[1024,512]{1,0:T(8,128)(2,1)}, bf16[1024,512]{1,0:T(8,128)(2,1)}, u32[]{:S(2)}, u32[]{:S(2)}) collective-permute-start(bf16[1024,512]{1,0:T(8,128)(2,1)} %slice.175), channel_id=1, source_target_pairs={{0,1},{1,0},{2,3},{3,2},{4,5},{5,4},{6,7},{7,6},{8,9},{9,8},{10,11... | collective-permute-start | bytes 3145736 | tf_op jit(solution)/shard_map/ppermute | solution.py:25
  972.5 38.5 %collective-permute-start.60 = (bf16[160,2048]{1,0:T(8,128)(2,1)S(1)}, bf16[160,2048]{1,0:T(8,128)(2,1)S(1)}, u32[]{:S(2)}, u32[]{:S(2)}) collective-permute-start(bf16[160,2048]{1,0:T(8,128)(2,1)S(1)} %dynamic-slice_convert_fusion), channel_id=1, source_target_pairs={{0,1},{1,0},{2,3},{3,2},{4,5},{5,4},{6,7},{7,6},{8,9},{9,8},{10,11... | collective-permute-start | bytes 1966088 | tf_op jit(solution)/shard_map/ppermute | solution.py:25
  976.5 56.8 %collective-permute-start.80 = (bf16[256,1024]{0,1:T(8,128)(2,1)S(1)}, bf16[256,1024]{0,1:T(8,128)(2,1)S(1)}, u32[]{:S(2)}, u32[]{:S(2)}) collective-permute-start(bf16[256,1024]{0,1:T(8,128)(2,1)S(1)} %pad_maximum_fusion.17), channel_id=1, source_target_pairs={{8,0},{10,2},{16,8},{18,10},{24,16},{26,18},{28,24},{30,26},{20,28... | collective-permute-start | bytes 1572872 | tf_op jit(solution)/shard_map/ppermute | solution.py:41
  982.9 51.4 %collective-permute-start.76 = (bf16[256,1024]{0,1:T(8,128)(2,1)S(1)}, bf16[256,1024]{0,1:T(8,128)(2,1)S(1)}, u32[]{:S(2)}, u32[]{:S(2)}) collective-permute-start(bf16[256,1024]{0,1:T(8,128)(2,1)S(1)} %pad_maximum_fusion.16), channel_id=1, source_target_pairs={{0,8},{2,10},{8,16},{10,18},{16,24},{18,26},{24,28},{26,30},{28,20... | collective-permute-start | bytes 1572872 | tf_op jit(solution)/shard_map/ppermute | solution.py:37
  1031.0 37.5 %collective-permute-start.61 = (f32[160,2048]{1,0:T(8,128)S(1)}, f32[160,2048]{1,0:T(8,128)S(1)}, u32[]{:S(2)}, u32[]{:S(2)}) collective-permute-start(f32[160,2048]{1,0:T(8,128)S(1)} %fusion.1), channel_id=1, source_target_pairs={{0,1},{1,0},{2,3},{3,2},{4,5},{5,4},{6,7},{7,6},{8,9},{9,8},{10,11... | collective-permute-start | bytes 3932168 | tf_op jit(solution)/shard_map/ppermute | solution.py:25
  1033.4 12.9 %collective-permute-start.81 = (bf16[256,1024]{0,1:T(8,128)(2,1)S(1)}, bf16[256,1024]{0,1:T(8,128)(2,1)S(1)}, u32[]{:S(2)}, u32[]{:S(2)}) collective-permute-start(bf16[256,1024]{0,1:T(8,128)(2,1)S(1)} %add_convert_fusion.10), channel_id=1, source_target_pairs={{8,0},{10,2},{16,8},{18,10},{24,16},{26,18},{28,24},{30,26},{20,28... | collective-permute-start | bytes 1572872 | tf_op jit(solution)/shard_map/ppermute | solution.py:41
  1034.5 13.1 %collective-permute-start.77 = (bf16[256,1024]{0,1:T(8,128)(2,1)S(1)}, bf16[256,1024]{0,1:T(8,128)(2,1)S(1)}, u32[]{:S(2)}, u32[]{:S(2)}) collective-permute-start(bf16[256,1024]{0,1:T(8,128)(2,1)S(1)} %add_convert_fusion.12), channel_id=1, source_target_pairs={{0,8},{2,10},{8,16},{10,18},{16,24},{18,26},{24,28},{26,30},{28,20... | collective-permute-start | bytes 1572872 | tf_op jit(solution)/shard_map/ppermute | solution.py:37
  (127 other events, 1931.4 us)
Sparse Core Ops, SparseCore 0:
  15.8 123.8 all-gather.4
  141.8 63.9 all-gather.6
  774.3 138.5 reduce-scatter.1

commit v6 on v5

--- a/solution.py
+++ b/solution.py
@@ -64,16 +64,19 @@
     return lax.optimization_barrier((value, *others))
 
 
+def after(value, token):
+    return lax.optimization_barrier((value, token))[0]
+
+
 class Fillers:
     def __init__(self, stages):
         self.stages = list(stages)
         self.outs = []
 
-    def next(self, gate):
+    def next(self, token):
         for work, *operands in self.stages.pop(0) if self.stages else ():
-            gate, *operands = together(gate, *operands)
+            operands = [after(operand, token) for operand in operands]
             self.outs.append(work(*operands))
-        return gate
 
 
 def ring_sum(same, cross, fillers):
@@ -81,16 +84,16 @@
     rows = both[0].shape[0]
     cut = rows // 2
     right, left = ahead(both[4][:cut]), behind(both[4][cut:])
-    left = fillers.next(left)
+    fillers.next(left)
     outward, inward = both[3][rows:], both[3][:rows]
     right = jnp.concatenate([add_low(outward[:cut], right), outward[cut:]], axis=0)
     left = jnp.concatenate([inward[:cut], add_low(inward[cut:], left)], axis=0)
     right, left = ahead(right), behind(left)
-    left = fillers.next(left)
+    fillers.next(left)
     for hop in (2, 1):
         right = ahead(add_low(both[hop][rows:], right))
         left = behind(add_low(both[hop][:rows], left))
-        left = fillers.next(left)
+        fillers.next(left)
     return both[0].astype(FULL) + right.astype(FULL) + left.astype(FULL)
 
 
@@ -372,44 +375,59 @@
     )(key_grad, value_grad, flat, gain, scale, cosine, sine, *returned)
 
 
-def pack_kernel(query, key, value, rest, *refs):
-    packed = refs[-1]
+def pack_kernel(query, key, value, rest, out, *refs):
+    packed, turned = refs[-2:]
     at = 0
     for ref in (query, key, value, rest):
         packed[at : at + ref.shape[0]] = ref[...]
         at += ref.shape[0]
-    for back in refs[:-1]:
+    for back in refs[:-2]:
         width = packed.shape[1]
         for start in range(0, back.shape[1], width):
             packed[at : at + back.shape[0]] = back[:, start : start + width].astype(LOW)
             at += back.shape[0]
-
-
-def pack_weights(w_query, w_key, w_value, rest, back):
+    turned[...] = out[...].T
+
+
+def pack_weights(w_query, w_key, w_value, rest, w_out, back):
     width = w_query.shape[1]
     rows = 3 * w_query.shape[0] + rest.shape[0] + sum(b.size // width for b in back)
-    return pl.pallas_call(pack_kernel, out_shape=jax.ShapeDtypeStruct((rows, width), LOW))(
-        w_query, w_key, w_value, rest, *back
-    )
-
-
-def unpack_kernel(first, blocks_ref, packed, out, sems):
+    return pl.pallas_call(
+        pack_kernel,
+        out_shape=[
+            jax.ShapeDtypeStruct((rows, width), LOW),
+            jax.ShapeDtypeStruct(w_out.shape[::-1], LOW),
+        ],
+    )(w_query, w_key, w_value, rest, w_out, *back)
+
+
+def unpack_kernel(first, blocks_ref, packed, out, held, sems):
     width = packed.shape[2]
     parts = out.shape[1] // width
     rows = (packed.shape[1] - first) // parts
-    copies = [
+    count = packed.shape[0]
+    place = lambda i: pl.ds(i * rows, rows)
+    loads = [
         pltpu.make_async_copy(
             packed.at[blocks_ref[i], pl.ds(first + j * rows, rows)],
-            out.at[pl.ds(i * rows, rows), pl.ds(j * width, width)],
+            held.at[place(i), pl.ds(j * width, width)],
             sems.at[i * parts + j],
         )
-        for i in range(packed.shape[0])
+        for i in range(count)
         for j in range(parts)
     ]
-    for one in copies:
+    stores = [
+        pltpu.make_async_copy(held.at[place(i)], out.at[place(i)], sems.at[count * parts + i])
+        for i in range(count)
+    ]
+    for one in loads:
         one.start()
-    for one in copies:
-        one.wait()
+    for i, store in enumerate(stores):
+        for j in range(parts):
+            loads[i * parts + j].wait()
+        store.start()
+    for store in stores:
+        store.wait()
 
 
 def unpack_rows(packed, blocks, first, width):
@@ -421,7 +439,11 @@
         in_specs=[pl.BlockSpec(memory_space=pltpu.SMEM), pl.BlockSpec(memory_space=pl.ANY)],
         out_specs=pl.BlockSpec(memory_space=pl.ANY),
         out_shape=jax.ShapeDtypeStruct((count * rows, width), LOW),
-        scratch_shapes=[pltpu.SemaphoreType.DMA((count * parts,))],
+        scratch_shapes=[
+            pltpu.VMEM((count * rows, width), LOW),
+            pltpu.SemaphoreType.DMA((count * parts + count,)),
+        ],
+        compiler_params=pltpu.CompilerParams(vmem_limit_bytes=24 * 1024 * 1024),
     )(blocks, packed)
 
 
@@ -519,18 +541,20 @@
             [lax.dynamic_slice_in_dim(a, at, rows, axis=0) for a in (first, second)], axis=1
         )
 
-    far = fillers.next(part(4))
+    far = part(4)
     right, left = ahead(far[:, :cut]), behind(far[:, cut:])
-    left = fillers.next(left)
+    fillers.next(left)
     outward, inward = part(3), part(-3)
     right = jnp.concatenate([add_low(outward[:, :cut], right), outward[:, cut:]], axis=1)
     left = jnp.concatenate([inward[:, :cut], add_low(inward[:, cut:], left)], axis=1)
     right, left = ahead(right), behind(left)
-    left = fillers.next(left)
+    fillers.next(left)
+    token = left
     for hop in (2, 1):
         right, left = ahead(add_low(part(hop), right)), behind(add_low(part(-hop), left))
-        left = fillers.next(left)
-    return part(0).astype(FULL) + right.astype(FULL) + left.astype(FULL)
+        fillers.next(left)
+        token = left if hop == 2 else token
+    return part(0).astype(FULL) + right.astype(FULL) + left.astype(FULL), token
 
 
 def expert_kernel(
@@ -587,10 +611,11 @@
     back_ref, mats, refs = refs[0], refs[1:7], refs[7 + held :]
     same_ref, cross_ref, rows_out = refs[:3]
     outs = refs[3:9]
-    rows, back, wg, wu, wd, hidden, gate_grad, up_grad, grads, sems = refs[9:]
+    rows, back, wide, wd, hidden, both_grads, grads, sems = refs[9:]
     count = rows.shape[0]
-    part = wg.shape[2]
-    slab = wg.shape[1] // 4
+    part = wd.shape[1]
+    slab = wide.shape[0] // 4
+    across = lambda k, half: pl.ds((2 * k + half) * part, part)
     place = pl.ds(at * count, count)
     copy = pltpu.make_async_copy
     load_rows, start = [], 0
@@ -599,10 +624,12 @@
         load_rows.append(copy(piece, rows.at[span], sems.at[len(load_rows)]))
         start += piece.shape[0]
     load_back = copy(back_ref.at[place], back, sems.at[4])
-    loads = [
-        [copy(mats[2 * k + half], to.at[half], sems.at[5 + 3 * half + k]) for k, to in enumerate((wg, wu, wd))]
-        for half in range(2)
-    ]
+    loads = []
+    for half in range(2):
+        places = [wide.at[:, across(0, half)], wide.at[:, across(1, half)], wd.at[half]]
+        loads.append(
+            [copy(mats[2 * k + half], to, sems.at[5 + 3 * half + k]) for k, to in enumerate(places)]
+        )
     for one in load_rows + loads[0][:2] + [load_back] + loads[0][2:] + loads[1]:
         one.start()
     gate = gate_ref[...]
@@ -612,38 +639,38 @@
     stores[0].start()
     for half in range(2):
         columns = pl.ds(half * part, part)
-        loads[half][0].wait()
-        gate_pre = dot_nn(rows[...], wg[half])
-        loads[half][1].wait()
-        up_pre = dot_nn(rows[...], wu[half])
+        if half == 0:
+            loads[0][0].wait()
+        gate_pre = dot_nn(rows[...], wide[:, across(0, half)])
+        if half == 0:
+            loads[0][1].wait()
+        up_pre = dot_nn(rows[...], wide[:, across(1, half)])
         if half == 0:
             load_back.wait()
-        loads[half][2].wait()
+            for one in loads[0][2:] + loads[1]:
+                one.wait()
         hidden_grad = gate * dot_nt(back[...], wd[half])
         sig = 1.0 / (1.0 + jnp.exp(-gate_pre))
         act = gate_pre * sig
         hidden[:, columns] = (gate * (act * up_pre)).astype(LOW)
-        gate_grad[:, columns] = (
+        both_grads[:, across(0, half)] = (
             hidden_grad * up_pre * (sig * (1.0 + gate_pre * (1.0 - sig)))
         ).astype(LOW)
-        up_grad[:, columns] = (hidden_grad * act).astype(LOW)
-        for k, held_in in enumerate((hidden, gate_grad, up_grad)):
-            stores.append(
-                copy(
-                    held_in.at[:, columns], outs[2 * k + half].at[place], sems.at[12 + 3 * half + k]
-                )
-            )
+        both_grads[:, across(1, half)] = (hidden_grad * act).astype(LOW)
+    for half in range(2):
+        held_in = (
+            hidden.at[:, pl.ds(half * part, part)],
+            both_grads.at[:, across(0, half)],
+            both_grads.at[:, across(1, half)],
+        )
+        for k, source in enumerate(held_in):
+            stores.append(copy(source, outs[2 * k + half].at[place], sems.at[12 + 3 * half + k]))
             stores[-1].start()
 
     @pl.loop(0, 4)
     def _(j):
         span = pl.ds(pl.multiple_of(j * slab, slab), slab)
-        total = None
-        for grad, mat in ((gate_grad, wg), (up_grad, wu)):
-            for half in range(2):
-                piece = dot_nt(grad[:, half * part : (half + 1) * part], mat[half, span])
-                total = piece if total is None else total + piece
-        grads[:, span] = total.astype(LOW)
+        grads[:, span] = dot_nt(both_grads[...], wide[span]).astype(LOW)
 
     for k in range(count // size):
         to = cross_ref if k % 2 else same_ref
@@ -678,12 +705,10 @@
         scratch_shapes=[
             pltpu.VMEM((count, width), LOW),
             pltpu.VMEM((count, width), LOW),
-            pltpu.VMEM((2, width, part), LOW),
-            pltpu.VMEM((2, width, part), LOW),
+            pltpu.VMEM((width, 2 * hidden), LOW),
             pltpu.VMEM((2, part, width), LOW),
             pltpu.VMEM((count, hidden), LOW),
-            pltpu.VMEM((count, hidden), LOW),
-            pltpu.VMEM((count, hidden), LOW),
+            pltpu.VMEM((count, 2 * hidden), LOW),
             pltpu.VMEM((count, width), LOW),
             pltpu.SemaphoreType.DMA((22,)),
         ],
@@ -742,10 +767,12 @@
     swap = lambda block: swap_bit(block, "dp", 0)
     rows, pair = together(rows, swap(rows))
     left, right = ahead(rows), behind(rows)
+    waiting = swap_tensor(after(waiting, pair))
     same[0], cross[0], held = expert_chunk([rows, pair], back, gate, mats, 6, None, size)
     for hop in (1, 2, 3):
         pieces = [left, swap(left), right, swap(right)]
         if hop < 3:
+            left, right, same[hop - 1] = together(left, right, same[hop - 1])
             left, right = ahead(left), behind(right)
         else:
             left, right = ahead(left[:cut]), behind(right[cut:])
@@ -825,15 +852,16 @@
     gains = jnp.concatenate([attn_gain, moe_gain, query_gain, key_gain])
     gains = jnp.pad(gains[None], ((0, 7), (0, local_width - 4 * block)))
     cotangent_half = own_half(cotangent)
-    packed = pack_weights(
+    packed, turned = pack_weights(
         w_query,
         w_key,
         w_value,
         jnp.concatenate([gains, routing], axis=0),
+        w_out,
         [cotangent_half] if ring else [],
     )
     gathered = lax.all_gather(packed, "dp", axis=0, tiled=False)
-    gathered_out = lax.all_gather(w_out.T, "dp", axis=0, tiled=False)
+    gathered_out = lax.all_gather(turned, "dp", axis=0, tiled=False)
     gathered, *early = lax.optimization_barrier((gathered, gate_mats[1], up_mats[1]))
     gate_mats, up_mats = (gate_mats[0], early[0]), (up_mats[0], early[1])
     rest = gathered[:, 3 * block : 3 * block + 16]
@@ -902,14 +930,16 @@
     pieces = (*collect_prompt(keys_b[:PR_DEV], 2, 1), *value_pieces)
     queries_b = rope_pass(query_flat, gain_query_local[None], query_scale, cosine, sine)
     context_b = attend(queries_b, keys_b, values_b, bias, pieces)
+    gathered_out = after(gathered_out, context_b)
     attn_part = project_back([context_b], gathered_out, block, (0,))
     attn_part, late, weight = together(attn_part, down_mats[1], weight)
     down_mats = (down_mats[0], late)
     mats = (*gate_mats, *up_mats, *down_mats)
     attn_other = swap_tensor(other_half(attn_part).astype(LOW))
     if ring:
-        gathered, attn_part = together(gathered, attn_part)
-        back_rows = unpack_rows(gathered, blocks, 3 * block + 16, model_width)
+        back_rows = unpack_rows(
+            after(gathered, attn_part), blocks, 3 * block + 16, model_width
+        )
     else:
         back_rows = lax.all_gather(cotangent_half.astype(LOW), "dp", axis=0, tiled=True)
     attn_other, back_rows, weight = together(attn_other, back_rows, weight)
@@ -919,10 +949,9 @@
     low_tn = lambda left, right: dot_tn(left, right).astype(LOW)
     upper = lambda array: array[: array.shape[0] // 2]
     lower = lambda array: array[array.shape[0] // 2 :]
-    hidden_other = swap_tensor(hidden_state)
     if ring:
         same, cross, held, hidden_other = expert_ring(
-            normed_two_b, back_rows, weight, mats, hidden_other
+            normed_two_b, back_rows, weight, mats, hidden_state
         )
         expert_in, h0, h1, g0, g1, u0, u1 = held
         down_got = swap_tensor(low_tn(h1, back_rows))
@@ -936,6 +965,7 @@
         normed_two_grad = ring_sum(same, cross, fillers)
         gate_sent, up_sent, mixed_rows = fillers.outs
     else:
+        hidden_other = swap_tensor(hidden_state)
         expert_in = lax.all_gather(normed_two_b, "dp", axis=0, tiled=True)
         grad_rows, h0, h1, g0, g1, u0, u1 = expert_pass(
             expert_in, back_rows, weight, gate_mats, up_mats, down_mats
@@ -948,8 +978,8 @@
         gate_sent = low_tn(expert_in, g1)
         up_sent = low_tn(expert_in, u1)
     gate_first = swap_tensor(upper(gate_sent))
-    normed_two_grad, down_got, gate_first, mixed_rows = together(
-        normed_two_grad, down_got, gate_first, mixed_rows
+    normed_two_grad, down_got, gate_first, mixed_rows, up_sent = together(
+        normed_two_grad, down_got, gate_first, mixed_rows, up_sent
     )
     mixed = lax.psum_scatter(mixed_rows, "dp", scatter_dimension=0, tiled=True)
 
@@ -958,8 +988,8 @@
     state_half = cotangent_half + state_part
     attn_grad_half = state_half.astype(LOW)
     attn_grad_b = both_halves(attn_grad_half, swap_tensor(attn_grad_half))
-    attn_grad_b, gate_sent = together(attn_grad_b, gate_sent)
-    gate_second = swap_tensor(lower(gate_sent))
+    attn_grad_b, gate_sent, up_sent = together(attn_grad_b, gate_sent, up_sent)
+    gate_second, up_got = swap_tensor(lower(gate_sent)), swap_tensor(up_sent)
     (context_grad_b,) = project(attn_grad_b, gathered_out, block, (0,), (LOW,))
     query_normed_grad, query_inner, query_gain_part, key_grad, value_grad, odd, even = attend_back(
         queries_b,
@@ -974,69 +1004,63 @@
         sine,
         pieces,
     )
-    query_inner, gate_second = together(query_inner, gate_second)
-    query_inner = lax.psum(query_inner[:, 0], "tensor")
-    query_inner, up_sent = together(query_inner, up_sent)
-    up_first = swap_tensor(upper(up_sent))
-    query_pre_grad = (
-        query_scale * gain_query_local * query_normed_grad
-        - query_flat * (query_scale * query_scale * query_scale) * (query_inner / column_total)[:, None]
+    returned = return_prompt(odd, even)
+    key_normed_grad, key_inner, key_gain_part, value_pre_grad = key_back(
+        key_grad, value_grad, key_flat, gain_key_local[None], key_scale, cosine, sine, returned
+    )
+    query_inner, key_inner, gate_second, up_got = together(
+        query_inner, key_inner, gate_second, up_got
+    )
+    query_inner, key_inner = lax.psum((query_inner[:, 0], key_inner[:, 0]), "tensor")
+    pre_grad = lambda scale, gain, grad, flat, inner: (
+        scale * gain * grad - flat * (scale * scale * scale) * (inner / column_total)[:, None]
     ).astype(LOW)
+    query_pre_grad = pre_grad(
+        query_scale, gain_query_local, query_normed_grad, query_flat, query_inner
+    )
+    key_pre_grad = pre_grad(key_scale, gain_key_local, key_normed_grad, key_flat, key_inner)
+    mixed = after(mixed, key_pre_grad)
+    gate_got = jnp.concatenate([gate_first, gate_second], axis=0)
+    pre_grads = (query_pre_grad, key_pre_grad, value_pre_grad)
+    grad_sum = lambda left, right, got: dot_tn(left, right) + got.astype(FULL)
+    down, gate, up = (h0, back_rows, down_got), (expert_in, g0, gate_got), (expert_in, u0, up_got)
+    back_all = lambda *grads: project_back(grads, gathered, block, (0, 1, 2))
+
+    def share(part):
+        return own_half(part), swap_tensor(other_half(part).astype(LOW))
+
+    def input_side(own, other):
+        unused_one, norm_one_back = jax.vjp(rms_norm, own_half(tokens_f), gain_one)
+        input_part, gain_one_grad = norm_one_back(own + other.astype(FULL))
+        input_half = state_half + input_part
+        return input_half, swap_tensor(input_half), gain_one_grad
+
     if ring:
         columns = local_width // 2
         mine = lambda a: lax.dynamic_slice_in_dim(a, core * columns, columns, axis=1)
         theirs = lambda a: lax.dynamic_slice_in_dim(a, (1 - core) * columns, columns, axis=1)
         pair = lambda own, sent: jnp.concatenate([own, swap_bit(sent, "dp", 0)], axis=0)
-        half = lambda a: pair(mine(a), theirs(a))
+        half = lambda *a: pair(
+            jnp.concatenate([mine(x) for x in a], axis=1),
+            jnp.concatenate([theirs(x) for x in a], axis=1),
+        )
         normed_pair, attn_grad_pair = pair(normed_b, normed_b), pair(attn_grad_b, attn_grad_b)
         normed_pair, attn_grad_pair, context_half = together(
             normed_pair, attn_grad_pair, half(context_b)
         )
-        normed_pair, query_half = together(normed_pair, half(query_pre_grad))
-        first_halves = ring_weights(
-            low_tn(normed_pair, query_half), low_tn(attn_grad_pair, context_half), Fillers([])
-        )
-    returned = return_prompt(odd, even)
-    key_normed_grad, key_inner, key_gain_part, value_pre_grad = key_back(
-        key_grad, value_grad, key_flat, gain_key_local[None], key_scale, cosine, sine, returned
-    )
-    key_inner, up_first = together(key_inner, up_first)
-    key_inner = lax.psum(key_inner[:, 0], "tensor")
-    key_inner, mixed, up_sent = together(key_inner, mixed, up_sent)
-    up_second = swap_tensor(lower(up_sent))
-    mixed_other = swap_tensor(mixed)
-    key_pre_grad = (
-        key_scale * gain_key_local * key_normed_grad
-        - key_flat * (key_scale * key_scale * key_scale) * (key_inner / column_total)[:, None]
-    ).astype(LOW)
-    output = both_halves(
-        hidden_state + mixed.astype(FULL), hidden_other + mixed_other.astype(FULL)
-    )
-    wide = lambda part: lax.dynamic_update_slice_in_dim(
-        jnp.zeros((column_total,), FULL), part, side * local_width, 0
-    )
-    gate_got = jnp.concatenate([gate_first, gate_second], axis=0)
-    up_got = jnp.concatenate([up_first, up_second], axis=0)
-    pre_grads = (query_pre_grad, key_pre_grad, value_pre_grad)
-    grad_sum = lambda left, right, got: dot_tn(left, right) + got.astype(FULL)
-    down, gate, up = (h0, back_rows, down_got), (expert_in, g0, gate_got), (expert_in, u0, up_got)
-    back_all = lambda *grads: project_back(grads, gathered, block, (0, 1, 2))
-    if ring:
+        out_half = low_tn(attn_grad_pair, context_half)
+        grads_half, out_half = together(half(*pre_grads), out_half)
         fillers = Fillers(
             [
-                [(back_all, *pre_grads)],
-                [(grad_sum, *down)],
+                [(lambda *grads: share(back_all(*grads)), *pre_grads)],
+                [(grad_sum, *down), (swap_tensor, mixed)],
                 [(grad_sum, *gate)],
-                [(grad_sum, *up)],
             ]
         )
-        second_halves = ring_weights(
-            low_tn(normed_pair, half(key_pre_grad)),
-            low_tn(normed_pair, half(value_pre_grad)),
-            fillers,
-        )
-        normed_part, down_grad, gate_w_grad, up_w_grad = fillers.outs
-        w_half = jnp.concatenate([first_halves, second_halves], axis=1)
+        w_half, token = ring_weights(low_tn(normed_pair, grads_half), out_half, fillers)
+        (own_part, other_part), down_grad, mixed_other, gate_w_grad = fillers.outs
+        input_half, input_other, gain_one_grad = input_side(own_part, after(other_part, token))
+        up_w_grad = grad_sum(after(up[0], token), *up[1:])
         own_w = lax.dynamic_slice_in_dim(w_half, core * block, block, axis=0)
         got_w = swap_bit(
             lax.dynamic_slice_in_dim(w_half, (1 - core) * block, block, axis=0), "dp", 0
@@ -1044,8 +1068,9 @@
         left_w, right_w = jnp.where(core == 0, own_w, got_w), jnp.where(core == 0, got_w, own_w)
         w_sums = [
             jnp.concatenate([w[:, j * columns : (j + 1) * columns] for w in (left_w, right_w)], axis=1)
-            for j in (0, 2, 3, 1)
+            for j in range(4)
         ]
+        mixed_other = after(mixed_other, token)
     else:
         w_grads = jnp.concatenate(
             [low_tn(normed_b, g) for g in pre_grads] + [low_tn(attn_grad_b, context_b)], axis=1
@@ -1053,13 +1078,15 @@
         w_sum = lax.psum_scatter(w_grads, "dp", scatter_dimension=0, tiled=True).astype(FULL)
         w_sums = [w_sum[:, j * local_width : (j + 1) * local_width] for j in range(4)]
         down_grad, gate_w_grad, up_w_grad = grad_sum(*down), grad_sum(*gate), grad_sum(*up)
-        normed_part = back_all(*pre_grads)
-    normed_other = swap_tensor(other_half(normed_part).astype(LOW))
-    normed_grad = own_half(normed_part) + normed_other.astype(FULL)
-    unused_one, norm_one_back = jax.vjp(rms_norm, own_half(tokens_f), gain_one)
-    input_part, gain_one_grad = norm_one_back(normed_grad)
-    input_half = state_half + input_part
-    input_grad = both_halves(input_half, swap_tensor(input_half))
+        mixed_other = swap_tensor(mixed)
+        input_half, input_other, gain_one_grad = input_side(*share(back_all(*pre_grads)))
+    input_grad = both_halves(input_half, input_other)
+    output = both_halves(
+        hidden_state + mixed.astype(FULL), hidden_other + mixed_other.astype(FULL)
+    )
+    wide = lambda part: lax.dynamic_update_slice_in_dim(
+        jnp.zeros((column_total,), FULL), part, side * local_width, 0
+    )
     gain_grads = jnp.stack(
         [gain_one_grad, gain_two_grad, wide(query_gain_part[0]), wide(key_gain_part[0])]
     ).reshape(4, dp_count, block)

time: 1090 us -> 842 us (0.77)
  Pallas kernels: 498 us -> 187 us
  waiting for transfers between devices: 301 us -> 352 us
  local copies, waits for them, and re-layouts: 52 us -> 70.1 us
    pallas_call x1, Pallas kernels: 320 us -> 5.73 us  [unpack_rows(): pl.pallas_call(lambda *refs: unpack_kernel(first, *refs), in_specs=[pl.Bl...]
    ppermute x16 -> x12, waiting for transfers between devices: 28 us -> 49.5 us  [ahead(): return lax.ppermute(block, 'dp', AHEAD)]
    ppermute x16 -> x12, starting transfers between devices: 15.6 us -> 31.5 us  [ahead(): return lax.ppermute(block, 'dp', AHEAD)]
    ppermute x15 -> x14, waiting for transfers between devices: 135 us -> 148 us  [swap_tensor(): return lax.ppermute(block, 'tensor', [(0, 1), (1, 0)])]
    dynamic_slice x4 -> x10, local copies, waits for them, and re-layouts: 3.67 us -> 16.4 us  [part(): lax.dynamic_slice_in_dim(a, at, rows, axis=0)]
    unnamed x210 -> x246, local copies, waits for them, and re-layouts: 24.2 us -> 35.8 us
    ppermute x16 -> x12, waiting for transfers between devices: 50.3 us -> 61.9 us  [behind(): return lax.ppermute(block, 'dp', BEHIND)]
    ppermute x38 -> x36, waiting for transfers between devices: 51.2 us -> 62.7 us  [swap_bit(): return lax.ppermute(block, axis, [(i, i ^ 1 << bit) for i in range(count)])]
  transfers between devices with their start and end apart: 88 -> 77, of which waited for: 33 -> 32; matrix products, arithmetic and copies ran while one was open for 14% -> 17% of each run, Pallas kernels for 45% -> 19%
where the time goes in v6:
time: 842 us; the launch traced here: 836 us
  waiting for transfers between devices  352 us (42%)
  Pallas kernels  187 us (22%)
  starting transfers between devices  76.2 us (9%)
  other arithmetic  70.2 us (8%)
  local copies, waits for them, and re-layouts  70.1 us (8%)
  matrix products  54 us (6%)
  between operations  15.7 us (2%)
  blocking collectives  10.4 us (1%)
    ppermute x14, waiting for transfers between devices, swap_tensor(): return lax.ppermute(block, 'tensor', [(0, 1), (1, 0)])  148 us
    pallas_call x5, Pallas kernels, expert_chunk(): pl.pallas_call(lambda *refs: chunk_kernel(len(pieces), len(held), at, siz...  94.9 us
    ppermute x36, waiting for transfers between devices, swap_bit(): return lax.ppermute(block, axis, [(i, i ^ 1 << bit) for i in range(count)])  62.7 us
    ppermute x12, waiting for transfers between devices, behind(): return lax.ppermute(block, 'dp', BEHIND)  61.9 us
    dot_general x8, matrix products, dot_tn(): lax.dot_general(left, right, (((0,), (0,)), ((), ())), preferred_element_...  53.8 us
    ppermute x12, waiting for transfers between devices, ahead(): return lax.ppermute(block, 'dp', AHEAD)  49.5 us
    unnamed x246, local copies, waits for them, and re-layouts  35.8 us
    ppermute x12, starting transfers between devices, ahead(): return lax.ppermute(block, 'dp', AHEAD)  31.5 us
  transfers between devices with their start and end apart: 77, of which 32 were waited for; matrix products, arithmetic and copies ran while one was open for 17% of the time, Pallas kernels for 19%

profile of v6, /device:TPU:0, one launch (start us, length us, event | category | flops | bytes accessed | tf_op | source)
XLA Modules:
  0.0 835.6 jit_solution(7370249116828667857)
XLA Ops:
  10.2 2.5 constant_dynamic-slice_fusion.33.refs_0_
  12.7 3.1 shard_map.282
  16.6 3.0 collective-permute-start
  22.0 44.2 %collective-permute-done.refs_5_.refs_7_ = bf16[2048,512]{1,0:T(8,128)(2,1)} collective-permute-done((bf16[2048,512]{1,0:T(8,128)(2,1)S(1)}, bf16[2048,512]{1,0:T(8,128)(2,1)}, u32[]{:S(2)}, u32[]{:S(2)}) %collective-permute-start) | collective-permute-done | bytes 2097184 | tf_op jit(solution)/shard_map/ppermute | solution.py:25
  66.2 44.1 %collective-permute-done.1.refs_7_.refs_9_ = bf16[2048,512]{1,0:T(8,128)(2,1)} collective-permute-done((bf16[2048,512]{1,0:T(8,128)(2,1)}, bf16[2048,512]{1,0:T(8,128)(2,1)}, u32[]{:S(2)}, u32[]{:S(2)}) %collective-permute-start.1) | collective-permute-done | bytes 2097184 | tf_op jit(solution)/shard_map/ppermute | solution.py:25
  110.3 29.5 %all-gather.5.cloned.1.call-done = bf16[11520,1024]{1,0:T(8,128)(2,1)} async-done(((bf16[720,1024]{1,0:T(8,128)(2,1)}), bf16[11520,1024]{1,0:T(8,128)(2,1)}) %all-gather.5.cloned.1.call-update) | async-done | bytes 23592976 | tf_op jit(solution)/shard_map/all_gather | solution.py:863
  142.9 9.8 %shard_map.283 = (f32[320,1024]{1,0:T(8,128)S(1)}, f32[320,1024]{1,0:T(8,128)S(1)}, bf16[320,1024]{1,0:T(8,128)(2,1)S(1)}) custom-call(bf16[320,2048]{1,0:T(8,128)(2,1)} %multiply_convert_fusion.refs_0_, bf16[16,720,1024]{2,1,0:T(8,128)(2,1)} %bitcast.106, bf16[16,720,1024]{2,1,0:T(8,128)(2,1)} %bitcast.107, bf16[16,720,1024]{2,1,0:T(8,128)(2,1)} %bitcast.108), custom_call_target="tpu_custom_call" | custom-call | flops 4026531840 | bytes 15204352 | tf_op jit(solution)/shard_map/pallas_call | solution.py:485
  154.2 5.1 all-reduce.4
  161.1 2.6 shard_map.285.k_ref
  170.2 8.8 %collective-permute-done.3 = bf16[128,1024]{1,0:T(8,128)(2,1)S(1)} collective-permute-done((bf16[128,1024]{1,0:T(8,128)(2,1)S(1)}, bf16[128,1024]{1,0:T(8,128)(2,1)S(1)}, u32[]{:S(2)}, u32[]{:S(2)}) %collective-permute-start.3) | collective-permute-done | bytes 262176 | tf_op jit(solution)/shard_map/ppermute | solution.py:21
  182.4 9.0 %collective-permute-done.2 = bf16[128,1024]{1,0:T(8,128)(2,1)S(1)} collective-permute-done((bf16[128,1024]{1,0:T(8,128)(2,1)S(1)}, bf16[128,1024]{1,0:T(8,128)(2,1)S(1)}, u32[]{:S(2)}, u32[]{:S(2)}) %collective-permute-start.2) | collective-permute-done | bytes 262176 | tf_op jit(solution)/shard_map/ppermute | solution.py:21
  191.3 5.2 collective-permute-done.4
  197.9 2.6 pad_maximum_fusion.8.v_stay
  205.0 2.6 shard_map.284.q_ref
  212.0 9.8 %shard_map.286.refs_0_ = bf16[320,1024]{1,0:T(8,128)(2,1)S(1)} custom-call(bf16[320,1024]{1,0:T(8,128)(2,1)S(1)} %copy-done.21, bf16[320,1024]{1,0:T(8,128)(2,1)S(1)} %copy-done.14, bf16[320,1024]{1,0:T(8,128)(2,1)S(1)} %copy-done.23, bf16[320,1216]{1,0:T(8,128)(2,1)S(1)} %copy-done.15, bf16[4,128,1024]{2,1,0:T(8,128)(2,1)S(1)} %pad_maximum_fusion.7.k_stay, ...), custom_call_target="tpu_custom_call" | custom-call | tf_op jit(solution)/shard_map/pallas_call | solution.py:229
  230.2 5.7 shard_map.288.refs_3_.refs_5_
  236.0 3.9 copy-done
  239.9 5.5 collective-permute-done.11
  249.1 10.0 %collective-permute-start.13 = (bf16[160,2048]{1,0:T(8,128)(2,1)S(1)}, bf16[160,2048]{1,0:T(8,128)(2,1)}, u32[]{:S(2)}, u32[]{:S(2)}) collective-permute-start(bf16[160,2048]{1,0:T(8,128)(2,1)S(1)} %multiply_convert_fusion.1.refs_1_), channel_id=1, source_target_pairs={{0,8},{2,10},{8,16},{10,18},{16,24},{18,26},{24,28},{26,30},{28,20... | collective-permute-start | bytes 1966088 | tf_op jit(solution)/shard_map/ppermute | solution.py:37
  260.6 14.9 %collective-permute-done.13.refs_1_ = bf16[160,2048]{1,0:T(8,128)(2,1)} collective-permute-done((bf16[160,2048]{1,0:T(8,128)(2,1)S(1)}, bf16[160,2048]{1,0:T(8,128)(2,1)}, u32[]{:S(2)}, u32[]{:S(2)}) %collective-permute-start.13) | collective-permute-done | bytes 655392 | tf_op jit(solution)/shard_map/ppermute | solution.py:37
  276.9 14.1 %shard_map.289 = (bf16[160,2048]{1,0:T(8,128)(2,1)S(1)}, bf16[160,2048]{1,0:T(8,128)(2,1)}, bf16[2560,2048]{1,0:T(8,128)(2,1)}, bf16[2560,512]{1,0:T(8,128)(2,1)...) custom-call(f32[2560,1]{1,0:T(8,128)S(1)} %copy.93.refs_0_, ...), custom_call_target="tpu_custom_call" | custom-call | flops 6710886400 | bytes 19791872 | tf_op jit(solution)/shard_map/pallas_call | solution.py:697
  293.9 22.1 %shard_map.290 = (bf16[320,2048]{1,0:T(8,128)(2,1)S(1)}, bf16[320,2048]{1,0:T(8,128)(2,1)}, bf16[2560,2048]{1,0:T(8,128)(2,1)}, bf16[2560,512]{1,0:T(8,128)(2,1)...) custom-call(f32[2560,1]{1,0:T(8,128)} %copy-done.3, ...), custom_call_target="tpu_custom_call", output_to_operand_aliasing={{2}: (12, {}), {3}: (13, {}), {4}: (14, {}), {5}: (15, {}),... | custom-call | flops 13421772800 | bytes 27000832 | tf_op jit(solution)/shard_map/pallas_call | solution.py:697
  321.8 11.8 %collective-permute-done.24.refs_1_ = bf16[160,2048]{1,0:T(8,128)(2,1)S(1)} collective-permute-done((bf16[160,2048]{1,0:T(8,128)(2,1)S(1)}, bf16[160,2048]{1,0:T(8,128)(2,1)S(1)}, u32[]{:S(2)}, u32[]{:S(2)}) %collective-permute-start.24) | collective-permute-done | bytes 655392 | tf_op jit(solution)/shard_map/ppermute | solution.py:37
  336.6 22.0 %shard_map.291 = (bf16[320,2048]{1,0:T(8,128)(2,1)S(1)}, bf16[320,2048]{1,0:T(8,128)(2,1)}, bf16[2560,2048]{1,0:T(8,128)(2,1)}, bf16[2560,512]{1,0:T(8,128)(2,1)...) custom-call(f32[2560,1]{1,0:T(8,128)} %copy-done.3, ...), custom_call_target="tpu_custom_call", output_to_operand_aliasing={{2}: (12, {}), {3}: (13, {}), {4}: (14, {}), {5}: (15, {}),... | custom-call | flops 13421772800 | bytes 27000832 | tf_op jit(solution)/shard_map/pallas_call | solution.py:697
  360.8 22.9 %shard_map.292 = (bf16[320,2048]{1,0:T(8,128)(2,1)S(1)}, bf16[320,2048]{1,0:T(8,128)(2,1)}, bf16[2560,2048]{1,0:T(8,128)(2,1)}, bf16[2560,512]{1,0:T(8,128)(2,1)...) custom-call(f32[2560,1]{1,0:T(8,128)} %copy-done.3, ...), custom_call_target="tpu_custom_call", output_to_operand_aliasing={{2}: (12, {}), {3}: (13, {}), {4}: (14, {}), {5}: (15, {}),... | custom-call | flops 13421772800 | bytes 27000832 | tf_op jit(solution)/shard_map/pallas_call | solution.py:697
  391.9 13.8 %shard_map.293 = (bf16[160,2048]{1,0:T(8,128)(2,1)S(1)}, bf16[160,2048]{1,0:T(8,128)(2,1)S(1)}, bf16[2560,2048]{1,0:T(8,128)(2,1)}, bf16[2560,512]{1,0:T(8,128)(...) custom-call(f32[2560,1]{1,0:T(8,128)S(1)} %copy-done.4, ...), custom_call_target="tpu_custom_call", output_to_operand_aliasing={{2}: (12, {}), {3}: (13, {}), {4}: (14, {}), {5}: (15, {}),... | custom-call | flops 6710886400 | bytes 19791872 | tf_op jit(solution)/shard_map/pallas_call | solution.py:697
  405.8 8.7 %convolution_convert_fusion.4 = bf16[512,2048]{1,0:T(8,128)(2,1)} fusion(bf16[2560,512]{1,0:T(8,128)(2,1)} %get-tuple-element.215.h1_ref, bf16[2560,2048]{1,0:T(8,128)(2,1)S(1)} %bitcast.90), kind=kOutput, calls=%fused_computation.8 | convolution fusion | flops 5369757696 | bytes 15204352 | tf_op jit(solution)/shard_map/dot_general | solution.py:130
  422.1 7.2 collective-permute-done.39
  433.7 5.8 convolution_convert_fusion.3
  441.5 5.7 collective-permute-done.36
  450.1 6.8 convolution_convert_fusion.2
  457.0 5.6 collective-permute-done.37
  466.3 15.9 %shard_map.294 = bf16[8,2,160,2048]{3,2,1,0:T(8,128)(2,1)} custom-call(s32[8]{0:T(128)S(1)} %copy-done.42, s32[1]{0:T(128)S(6)} %select_n.315.core_ref, bf16[2560,512]{1,0:T(8,128)(2,1)S(1)} %copy-done.5, bf16[2560,512]{1,0:T(8,128)(2,1)S(1)} %copy-done.6, bf16[512,2048]{1,0:T(8,128)(2,1)S(1)} %bitcast.99, ...), custom_call_target="tpu_custom_call" | custom-call | flops 10737418240 | bytes 19922944 | tf_op jit(solution)/shard_map/pallas_call | solution.py:741
  482.1 2.6 convert_add_fusion.4
  489.9 2.9 fusion.44
  494.3 14.9 %collective-permute-done.45 = bf16[160,2048]{1,0:T(8,128)(2,1)} collective-permute-done((bf16[160,2048]{1,0:T(8,128)(2,1)S(1)}, bf16[160,2048]{1,0:T(8,128)(2,1)}, u32[]{:S(2)}, u32[]{:S(2)}) %collective-permute-start.45) | collective-permute-done | bytes 655392 | tf_op jit(solution)/shard_map/ppermute | solution.py:25
  511.6 3.9 shard_map.295.back_ref
  516.4 19.6 %shard_map.296 = (f32[320,1024]{1,0:T(8,128)}, f32[320,1]{1,0:T(8,128)}, f32[1,1024]{1,0:T(1,128)}, f32[320,1024]{1,0:T(8,128)}, f32[320,1024]{1,0:T(8,128)}, /*...) custom-call(bf16[320,1024]{1,0:T(8,128)(2,1)} %shard_map.284.q_ref, ...), custom_call_target="tpu_custom_call" | custom-call | tf_op jit(solution)/shard_map/pallas_call | solution.py:304
  537.8 2.8 collective-permute-done.46.got_ref.refs_7_
  540.6 3.3 shard_map.297
  549.7 8.5 %collective-permute-done.47.refs_8_ = bf16[2,128,1024]{2,1,0:T(8,128)(2,1)} collective-permute-done((bf16[2,128,1024]{2,1,0:T(8,128)(2,1)}, bf16[2,128,1024]{2,1,0:T(8,128)(2,1)}, u32[]{:S(2)}, u32[]{:S(2)}) %collective-permute-start.47) | collective-permute-done | bytes 524320 | tf_op jit(solution)/shard_map/ppermute | solution.py:21
  562.8 3.5 pad_maximum_fusion
  568.1 2.5 collective-permute-done.50.refs_11_
  571.4 5.4 shard_map.298
  576.7 30.2 %collective-permute-done.51 = bf16[1024,512]{1,0:T(8,128)(2,1)} collective-permute-done((bf16[1024,512]{1,0:T(8,128)(2,1)}, bf16[1024,512]{1,0:T(8,128)(2,1)}, u32[]{:S(2)}, u32[]{:S(2)}) %collective-permute-start.51) | collective-permute-done | bytes 1048608 | tf_op jit(solution)/shard_map/ppermute | solution.py:25
  608.2 5.3 all-reduce.3
  626.4 2.6 pad_maximum_fusion.5
  632.1 7.8 convolution_convert_fusion
  639.9 2.5 constant_dynamic-slice_fusion.12
  644.6 3.3 pad_maximum_fusion.4
  663.5 8.3 collective-permute-done.68
  674.2 6.9 collective-permute-start.69
  681.2 7.7 shard_map.299
  690.6 31.9 %collective-permute-done.58 = bf16[256,2048]{0,1:T(8,128)(2,1)S(1)} collective-permute-done((bf16[256,2048]{0,1:T(8,128)(2,1)S(1)}, bf16[256,2048]{0,1:T(8,128)(2,1)S(1)}, u32[]{:S(2)}, u32[]{:S(2)}) %collective-permute-start.58) | collective-permute-done | bytes 1048608 | tf_op jit(solution)/shard_map/ppermute | solution.py:41
  723.8 3.2 collective-permute-done.69
  727.3 2.6 collective-permute-start.70
  730.0 7.3 add_bitcast_fusion
  737.3 20.4 %collective-permute-done.60 = bf16[256,2048]{0,1:T(8,128)(2,1)S(1)} collective-permute-done((bf16[256,2048]{0,1:T(8,128)(2,1)}, bf16[256,2048]{0,1:T(8,128)(2,1)S(1)}, u32[]{:S(2)}, u32[]{:S(2)}) %collective-permute-start.60) | collective-permute-done | bytes 1048608 | tf_op jit(solution)/shard_map/ppermute | solution.py:41
  759.4 4.2 collective-permute-done.63
  768.3 2.8 collective-permute-start.65
  771.5 16.6 %collective-permute-done.65 = f32[2,4,128]{2,1,0:T(4,128)S(1)} collective-permute-done((f32[2,4,128]{2,1,0:T(4,128)S(1)}, f32[2,4,128]{2,1,0:T(4,128)S(1)}, u32[]{:S(2)}, u32[]{:S(2)}) %collective-permute-start.65) | collective-permute-done | bytes 4128 | tf_op jit(solution)/shard_map/ppermute | solution.py:21
  788.2 7.2 add_bitcast_fusion.2
  795.4 8.4 %add_bitcast_fusion.1 = f32[1,2048,512]{2,1,0:T(8,128)} fusion(bf16[2048,512]{1,0:T(8,128)(2,1)} %collective-permute-done.52, bf16[2560,2048]{1,0:T(8,128)(2,1)S(1)} %bitcast.115, bf16[2560,512]{1,0:T(8,128)(2,1)S(1)} %copy-done.47), kind=kOutput, calls=%fused_computation.3 | convolution fusion | flops 5370806272 | bytes 19398656 | tf_op jit(solution)/shard_map/dot_general | solution.py:130
  816.8 8.6 %collective-permute-done.59 = bf16[160,2048]{1,0:T(8,128)(2,1)} collective-permute-done((bf16[160,2048]{1,0:T(8,128)(2,1)}, bf16[160,2048]{1,0:T(8,128)(2,1)}, u32[]{:S(2)}, u32[]{:S(2)}) %collective-permute-start.59) | collective-permute-done | bytes 655392 | tf_op jit(solution)/shard_map/ppermute | solution.py:25
  (516 shorter events, 177.7 us)
Async XLA Ops:
  7.2 132.7 %all-gather.5.cloned.1.call-start = ((), (), s32[]{:S(2)}) async-start(), calls=%async_computation.2 | async-start | bytes 25067520 | tf_op jit(solution)/shard_map/all_gather | solution.py:863
  15.8 206.9 %all-gather.7.cloned.1.call-start = ((), (), s32[]{:S(2)}) async-start(), calls=%async_computation.3 | async-start | bytes 4456448 | tf_op jit(solution)/shard_map/all_gather | solution.py:864
  16.6 791.7 %reduce-scatter.2.cloned.1.call-start = ((), (), s32[]{:S(2)}) async-start(), calls=%async_computation.1 | async-start | bytes 11141120 | tf_op jit(solution)/shard_map/reduce_scatter | solution.py:984
  16.6 49.6 %collective-permute-start = (bf16[2048,512]{1,0:T(8,128)(2,1)S(1)}, bf16[2048,512]{1,0:T(8,128)(2,1)}, u32[]{:S(2)}, u32[]{:S(2)}) collective-permute-start(bf16[2048,512]{1,0:T(8,128)(2,1)S(1)} %bitcast.121), channel_id=1, source_target_pairs={{0,1},{1,0},{2,3},{3,2},{4,5},{5,4},{6,7},{7,6},{8,9},{9,8},{10,11... | collective-permute-start | bytes 6291464 | tf_op jit(solution)/shard_map/ppermute | solution.py:25
  19.7 90.7 %collective-permute-start.1 = (bf16[2048,512]{1,0:T(8,128)(2,1)}, bf16[2048,512]{1,0:T(8,128)(2,1)}, u32[]{:S(2)}, u32[]{:S(2)}) collective-permute-start(bf16[2048,512]{1,0:T(8,128)(2,1)} %bitcast.122), channel_id=1, source_target_pairs={{0,1},{1,0},{2,3},{3,2},{4,5},{5,4},{6,7},{7,6},{8,9},{9,8},{10,11... | collective-permute-start | bytes 6291464 | tf_op jit(solution)/shard_map/ppermute | solution.py:25
  164.8 14.2 %collective-permute-start.3 = (bf16[128,1024]{1,0:T(8,128)(2,1)S(1)}, bf16[128,1024]{1,0:T(8,128)(2,1)S(1)}, u32[]{:S(2)}, u32[]{:S(2)}) collective-permute-start(bf16[128,1024]{1,0:T(8,128)(2,1)S(1)} %get-tuple-element.377), channel_id=1, source_target_pairs={{0,8},{2,10},{4,12},{6,14},{8,0},{10,2},{12,4},{14,6},{16,24},{18,... | collective-permute-start | bytes 786440 | tf_op jit(solution)/shard_map/ppermute | solution.py:21
  166.3 13.9 %collective-permute-start.6 = (bf16[128,1024]{1,0:T(8,128)(2,1)}, bf16[128,1024]{1,0:T(8,128)(2,1)}, u32[]{:S(2)}, u32[]{:S(2)}) collective-permute-start(bf16[128,1024]{1,0:T(8,128)(2,1)} %slice.153), channel_id=1, source_target_pairs={{0,4},{2,6},{4,0},{6,2},{8,12},{10,14},{12,8},{14,10},{16,20},{18,... | collective-permute-start | bytes 786440 | tf_op jit(solution)/shard_map/ppermute | solution.py:21
  167.8 23.6 %collective-permute-start.2 = (bf16[128,1024]{1,0:T(8,128)(2,1)S(1)}, bf16[128,1024]{1,0:T(8,128)(2,1)S(1)}, u32[]{:S(2)}, u32[]{:S(2)}) collective-permute-start(bf16[128,1024]{1,0:T(8,128)(2,1)S(1)} %get-tuple-element.377), channel_id=1, source_target_pairs={{0,4},{2,6},{4,0},{6,2},{8,12},{10,14},{12,8},{14,10},{16,20},{18,... | collective-permute-start | bytes 786440 | tf_op jit(solution)/shard_map/ppermute | solution.py:21
  168.7 59.6 %collective-permute-start.10 = (bf16[512,2048]{1,0:T(8,128)(2,1)S(1)}, bf16[512,2048]{1,0:T(8,128)(2,1)}, u32[]{:S(2)}, u32[]{:S(2)}) collective-permute-start(bf16[512,2048]{1,0:T(8,128)(2,1)S(1)} %bitcast.98), channel_id=1, source_target_pairs={{0,1},{1,0},{2,3},{3,2},{4,5},{5,4},{6,7},{7,6},{8,9},{9,8},{10,11... | collective-permute-start | bytes 6291464 | tf_op jit(solution)/shard_map/ppermute | solution.py:25
  179.0 17.5 %collective-permute-start.4 = (bf16[128,1024]{1,0:T(8,128)(2,1)S(1)}, bf16[128,1024]{1,0:T(8,128)(2,1)}, u32[]{:S(2)}, u32[]{:S(2)}) collective-permute-start(bf16[128,1024]{1,0:T(8,128)(2,1)S(1)} %collective-permute-done.3), channel_id=1, source_target_pairs={{0,4},{2,6},{4,0},{6,2},{8,12},{10,14},{12,8},{14,10},{16,20},{18,... | collective-permute-start | bytes 786440 | tf_op jit(solution)/shard_map/ppermute | solution.py:21
  179.1 18.7 %collective-permute-start.7 = (bf16[128,1024]{1,0:T(8,128)(2,1)}, bf16[128,1024]{1,0:T(8,128)(2,1)}, u32[]{:S(2)}, u32[]{:S(2)}) collective-permute-start(bf16[128,1024]{1,0:T(8,128)(2,1)} %slice.153), channel_id=1, source_target_pairs={{0,8},{2,10},{4,12},{6,14},{8,0},{10,2},{12,4},{14,6},{16,24},{18,... | collective-permute-start | bytes 786440 | tf_op jit(solution)/shard_map/ppermute | solution.py:21
  180.2 17.7 %collective-permute-start.8 = (bf16[128,1024]{1,0:T(8,128)(2,1)}, bf16[128,1024]{1,0:T(8,128)(2,1)}, u32[]{:S(2)}, u32[]{:S(2)}) collective-permute-start(bf16[128,1024]{1,0:T(8,128)(2,1)} %collective-permute-done.6), channel_id=1, source_target_pairs={{0,8},{2,10},{4,12},{6,14},{8,0},{10,2},{12,4},{14,6},{16,24},{18,... | collective-permute-start | bytes 786440 | tf_op jit(solution)/shard_map/ppermute | solution.py:21
  197.8 9.8 %collective-permute-start.5 = (bf16[4,128,1024]{2,1,0:T(8,128)(2,1)S(1)}, bf16[4,128,1024]{2,1,0:T(8,128)(2,1)}, u32[]{:S(2)}, u32[]{:S(2)}) collective-permute-start(bf16[4,128,1024]{2,1,0:T(8,128)(2,1)S(1)} %pad_maximum_fusion.7.k_stay), channel_id=1, source_target_pairs={{0,2},{2,0},{4,6},{6,4},{8,10},{10,8},{12,14},{14,12},{16,18},{18,... | collective-permute-start | bytes 3145736 | tf_op jit(solution)/shard_map/ppermute | solution.py:21
  228.4 17.0 %collective-permute-start.11 = (bf16[160,2048]{1,0:T(8,128)(2,1)S(1)}, bf16[160,2048]{1,0:T(8,128)(2,1)S(1)}, u32[]{:S(2)}, u32[]{:S(2)}) collective-permute-start(bf16[160,2048]{1,0:T(8,128)(2,1)S(1)} %dynamic-slice_convert_fusion.1), channel_id=1, source_target_pairs={{0,1},{1,0},{2,3},{3,2},{4,5},{5,4},{6,7},{7,6},{8,9},{9,8},{10,11... | collective-permute-start | bytes 1966088 | tf_op jit(solution)/shard_map/ppermute | solution.py:25
  249.1 26.3 %collective-permute-start.13 = (bf16[160,2048]{1,0:T(8,128)(2,1)S(1)}, bf16[160,2048]{1,0:T(8,128)(2,1)}, u32[]{:S(2)}, u32[]{:S(2)}) collective-permute-start(bf16[160,2048]{1,0:T(8,128)(2,1)S(1)} %multiply_convert_fusion.1.refs_1_), channel_id=1, source_target_pairs={{0,8},{2,10},{8,16},{10,18},{16,24},{18,26},{24,28},{26,30},{28,20... | collective-permute-start | bytes 1966088 | tf_op jit(solution)/shard_map/ppermute | solution.py:37
  259.2 17.3 %collective-permute-start.14 = (bf16[160,2048]{1,0:T(8,128)(2,1)S(1)}, bf16[160,2048]{1,0:T(8,128)(2,1)}, u32[]{:S(2)}, u32[]{:S(2)}) collective-permute-start(bf16[160,2048]{1,0:T(8,128)(2,1)S(1)} %multiply_convert_fusion.1.refs_1_), channel_id=1, source_target_pairs={{8,0},{10,2},{16,8},{18,10},{24,16},{26,18},{28,24},{30,26},{20,28... | collective-permute-start | bytes 1966088 | tf_op jit(solution)/shard_map/ppermute | solution.py:41
  275.5 18.4 %collective-permute-start.18 = (bf16[160,2048]{1,0:T(8,128)(2,1)}, bf16[160,2048]{1,0:T(8,128)(2,1)}, u32[]{:S(2)}, u32[]{:S(2)}) collective-permute-start(bf16[160,2048]{1,0:T(8,128)(2,1)} %collective-permute-done.13.refs_1_), channel_id=1, source_target_pairs={{0,2},{2,0},{4,6},{6,4},{8,10},{10,8},{12,14},{14,12},{16,18},{18,... | collective-permute-start | bytes 1966088 | tf_op jit(solution)/shard_map/ppermute | solution.py:21
  276.4 17.5 %collective-permute-start.19 = (bf16[160,2048]{1,0:T(8,128)(2,1)}, bf16[160,2048]{1,0:T(8,128)(2,1)}, u32[]{:S(2)}, u32[]{:S(2)}) collective-permute-start(bf16[160,2048]{1,0:T(8,128)(2,1)} %collective-permute-done.14.refs_3_), channel_id=1, source_target_pairs={{0,2},{2,0},{4,6},{6,4},{8,10},{10,8},{12,14},{14,12},{16,18},{18,... | collective-permute-start | bytes 1966088 | tf_op jit(solution)/shard_map/ppermute | solution.py:21
  291.9 25.2 %collective-permute-start.16 = (bf16[160,2048]{1,0:T(8,128)(2,1)}, bf16[160,2048]{1,0:T(8,128)(2,1)S(1)}, u32[]{:S(2)}, u32[]{:S(2)}) collective-permute-start(bf16[160,2048]{1,0:T(8,128)(2,1)} %collective-permute-done.13.refs_1_), channel_id=1, source_target_pairs={{0,8},{2,10},{8,16},{10,18},{16,24},{18,26},{24,28},{26,30},{28,20... | collective-permute-start | bytes 1966088 | tf_op jit(solution)/shard_map/ppermute | solution.py:37
  293.6 23.5 %collective-permute-start.17 = (bf16[160,2048]{1,0:T(8,128)(2,1)}, bf16[160,2048]{1,0:T(8,128)(2,1)S(1)}, u32[]{:S(2)}, u32[]{:S(2)}) collective-permute-start(bf16[160,2048]{1,0:T(8,128)(2,1)} %collective-permute-done.14.refs_3_), channel_id=1, source_target_pairs={{8,0},{10,2},{16,8},{18,10},{24,16},{26,18},{28,24},{30,26},{20,28... | collective-permute-start | bytes 1966088 | tf_op jit(solution)/shard_map/ppermute | solution.py:41
  317.1 16.6 %collective-permute-start.24 = (bf16[160,2048]{1,0:T(8,128)(2,1)S(1)}, bf16[160,2048]{1,0:T(8,128)(2,1)S(1)}, u32[]{:S(2)}, u32[]{:S(2)}) collective-permute-start(bf16[160,2048]{1,0:T(8,128)(2,1)S(1)} %collective-permute-done.16.refs_1_), channel_id=1, source_target_pairs={{0,8},{2,10},{8,16},{10,18},{16,24},{18,26},{24,28},{26,30},{28,20... | collective-permute-start | bytes 1966088 | tf_op jit(solution)/shard_map/ppermute | solution.py:37
  318.8 16.7 %collective-permute-start.27 = (bf16[160,2048]{1,0:T(8,128)(2,1)S(1)}, bf16[160,2048]{1,0:T(8,128)(2,1)S(1)}, u32[]{:S(2)}, u32[]{:S(2)}) collective-permute-start(bf16[160,2048]{1,0:T(8,128)(2,1)S(1)} %collective-permute-done.17.refs_3_), channel_id=1, source_target_pairs={{8,0},{10,2},{16,8},{18,10},{24,16},{26,18},{28,24},{30,26},{20,28... | collective-permute-start | bytes 1966088 | tf_op jit(solution)/shard_map/ppermute | solution.py:41
  319.1 17.0 %collective-permute-start.21 = (bf16[160,2048]{1,0:T(8,128)(2,1)S(1)}, bf16[160,2048]{1,0:T(8,128)(2,1)}, u32[]{:S(2)}, u32[]{:S(2)}) collective-permute-start(bf16[160,2048]{1,0:T(8,128)(2,1)S(1)} %collective-permute-done.16.refs_1_), channel_id=1, source_target_pairs={{0,2},{2,0},{4,6},{6,4},{8,10},{10,8},{12,14},{14,12},{16,18},{18,... | collective-permute-start | bytes 1966088 | tf_op jit(solution)/shard_map/ppermute | solution.py:21
  319.1 17.0 %collective-permute-start.22 = (bf16[160,2048]{1,0:T(8,128)(2,1)S(1)}, bf16[160,2048]{1,0:T(8,128)(2,1)}, u32[]{:S(2)}, u32[]{:S(2)}) collective-permute-start(bf16[160,2048]{1,0:T(8,128)(2,1)S(1)} %collective-permute-done.17.refs_3_), channel_id=1, source_target_pairs={{0,2},{2,0},{4,6},{6,4},{8,10},{10,8},{12,14},{14,12},{16,18},{18,... | collective-permute-start | bytes 1966088 | tf_op jit(solution)/shard_map/ppermute | solution.py:21
  319.7 40.0 %collective-permute-start.25 = (f32[160,2048]{1,0:T(8,128)}, f32[160,2048]{1,0:T(8,128)S(1)}, u32[]{:S(2)}, u32[]{:S(2)}) collective-permute-start(f32[160,2048]{1,0:T(8,128)} %copy-done.49), channel_id=1, source_target_pairs={{0,1},{1,0},{2,3},{3,2},{4,5},{5,4},{6,7},{7,6},{8,9},{9,8},{10,11... | collective-permute-start | bytes 3932168 | tf_op jit(solution)/shard_map/ppermute | solution.py:25
  333.7 26.1 %collective-permute-start.30 = (bf16[80,2048]{1,0:T(8,128)(2,1)S(1)}, bf16[80,2048]{1,0:T(8,128)(2,1)S(1)}, u32[]{:S(2)}, u32[]{:S(2)}) collective-permute-start(bf16[80,2048]{1,0:T(8,128)(2,1)S(1)} %slice.205), channel_id=1, source_target_pairs={{0,8},{2,10},{8,16},{10,18},{16,24},{18,26},{24,28},{26,30},{28,20... | collective-permute-start | bytes 983048 | tf_op jit(solution)/shard_map/ppermute | solution.py:37
  335.5 24.7 %collective-permute-start.31 = (bf16[80,2048]{1,0:T(8,128)(2,1)S(1)}, bf16[80,2048]{1,0:T(8,128)(2,1)S(1)}, u32[]{:S(2)}, u32[]{:S(2)}) collective-permute-start(bf16[80,2048]{1,0:T(8,128)(2,1)S(1)} %slice.206), channel_id=1, source_target_pairs={{8,0},{10,2},{16,8},{18,10},{24,16},{26,18},{28,24},{30,26},{20,28... | collective-permute-start | bytes 983048 | tf_op jit(solution)/shard_map/ppermute | solution.py:41
  336.1 24.2 %collective-permute-start.26 = (bf16[160,2048]{1,0:T(8,128)(2,1)S(1)}, bf16[160,2048]{1,0:T(8,128)(2,1)S(1)}, u32[]{:S(2)}, u32[]{:S(2)}) collective-permute-start(bf16[160,2048]{1,0:T(8,128)(2,1)S(1)} %collective-permute-done.24.refs_1_), channel_id=1, source_target_pairs={{0,2},{2,0},{4,6},{6,4},{8,10},{10,8},{12,14},{14,12},{16,18},{18,... | collective-permute-start | bytes 1966088 | tf_op jit(solution)/shard_map/ppermute | solution.py:21
  336.1 24.7 %collective-permute-start.28 = (bf16[160,2048]{1,0:T(8,128)(2,1)S(1)}, bf16[160,2048]{1,0:T(8,128)(2,1)S(1)}, u32[]{:S(2)}, u32[]{:S(2)}) collective-permute-start(bf16[160,2048]{1,0:T(8,128)(2,1)S(1)} %collective-permute-done.27.refs_3_), channel_id=1, source_target_pairs={{0,2},{2,0},{4,6},{6,4},{8,10},{10,8},{12,14},{14,12},{16,18},{18,... | collective-permute-start | bytes 1966088 | tf_op jit(solution)/shard_map/ppermute | solution.py:21
  359.7 122.4 %collective-permute-start.15 = (bf16[160,2048]{1,0:T(8,128)(2,1)}, bf16[160,2048]{1,0:T(8,128)(2,1)}, u32[]{:S(2)}, u32[]{:S(2)}) collective-permute-start(bf16[160,2048]{1,0:T(8,128)(2,1)} %get-tuple-element.164), channel_id=1, source_target_pairs={{0,2},{2,0},{4,6},{6,4},{8,10},{10,8},{12,14},{14,12},{16,18},{18,... | collective-permute-start | bytes 1966088 | tf_op jit(solution)/shard_map/ppermute | solution.py:21
  359.8 54.7 %collective-permute-start.20 = (bf16[320,2048]{1,0:T(8,128)(2,1)}, bf16[320,2048]{1,0:T(8,128)(2,1)}, u32[]{:S(2)}, u32[]{:S(2)}) collective-permute-start(bf16[320,2048]{1,0:T(8,128)(2,1)} %get-tuple-element.176), channel_id=1, source_target_pairs={{0,2},{2,0},{4,6},{6,4},{8,10},{10,8},{12,14},{14,12},{16,18},{18,... | collective-permute-start | bytes 3932168 | tf_op jit(solution)/shard_map/ppermute | solution.py:21
  360.2 59.6 %collective-permute-start.23 = (bf16[320,2048]{1,0:T(8,128)(2,1)}, bf16[320,2048]{1,0:T(8,128)(2,1)}, u32[]{:S(2)}, u32[]{:S(2)}) collective-permute-start(bf16[320,2048]{1,0:T(8,128)(2,1)} %get-tuple-element.185), channel_id=1, source_target_pairs={{0,2},{2,0},{4,6},{6,4},{8,10},{10,8},{12,14},{14,12},{16,18},{18,... | collective-permute-start | bytes 3932168 | tf_op jit(solution)/shard_map/ppermute | solution.py:21
  360.3 24.5 %collective-permute-start.32 = (bf16[80,2048]{1,0:T(8,128)(2,1)S(1)}, bf16[80,2048]{1,0:T(8,128)(2,1)S(1)}, u32[]{:S(2)}, u32[]{:S(2)}) collective-permute-start(bf16[80,2048]{1,0:T(8,128)(2,1)S(1)} %collective-permute-done.30.refs_1_), channel_id=1, source_target_pairs={{0,2},{2,0},{4,6},{6,4},{8,10},{10,8},{12,14},{14,12},{16,18},{18,... | collective-permute-start | bytes 983048 | tf_op jit(solution)/shard_map/ppermute | solution.py:21
  360.7 25.2 %collective-permute-start.33 = (bf16[80,2048]{1,0:T(8,128)(2,1)S(1)}, bf16[80,2048]{1,0:T(8,128)(2,1)S(1)}, u32[]{:S(2)}, u32[]{:S(2)}) collective-permute-start(bf16[80,2048]{1,0:T(8,128)(2,1)S(1)} %collective-permute-done.31.refs_2_), channel_id=1, source_target_pairs={{0,2},{2,0},{4,6},{6,4},{8,10},{10,8},{12,14},{14,12},{16,18},{18,... | collective-permute-start | bytes 983048 | tf_op jit(solution)/shard_map/ppermute | solution.py:21
  385.5 43.8 %collective-permute-start.29 = (bf16[320,2048]{1,0:T(8,128)(2,1)}, bf16[320,2048]{1,0:T(8,128)(2,1)}, u32[]{:S(2)}, u32[]{:S(2)}) collective-permute-start(bf16[320,2048]{1,0:T(8,128)(2,1)} %get-tuple-element.198), channel_id=1, source_target_pairs={{0,2},{2,0},{4,6},{6,4},{8,10},{10,8},{12,14},{14,12},{16,18},{18,... | collective-permute-start | bytes 3932168 | tf_op jit(solution)/shard_map/ppermute | solution.py:21
  405.7 12.1 %collective-permute-start.34 = (bf16[160,2048]{1,0:T(8,128)(2,1)S(1)}, bf16[160,2048]{1,0:T(8,128)(2,1)S(1)}, u32[]{:S(2)}, u32[]{:S(2)}) collective-permute-start(bf16[160,2048]{1,0:T(8,128)(2,1)S(1)} %get-tuple-element.207), channel_id=1, source_target_pairs={{0,2},{2,0},{4,6},{6,4},{8,10},{10,8},{12,14},{14,12},{16,18},{18,... | collective-permute-start | bytes 1966088 | tf_op jit(solution)/shard_map/ppermute | solution.py:21
  414.5 71.6 %collective-permute-start.43 = (bf16[512,2048]{1,0:T(8,128)(2,1)}, bf16[512,2048]{1,0:T(8,128)(2,1)S(1)}, u32[]{:S(2)}, u32[]{:S(2)}) collective-permute-start(bf16[512,2048]{1,0:T(8,128)(2,1)} %convolution_convert_fusion.4), channel_id=1, source_target_pairs={{0,1},{1,0},{2,3},{3,2},{4,5},{5,4},{6,7},{7,6},{8,9},{9,8},{10,11... | collective-permute-start | bytes 6291464 | tf_op jit(solution)/shard_map/ppermute | solution.py:25
  418.1 13.1 %collective-permute-start.35 = (bf16[80,2048]{1,0:T(8,128)(2,1)S(1)}, bf16[80,2048]{1,0:T(8,128)(2,1)S(1)}, u32[]{:S(2)}, u32[]{:S(2)}) collective-permute-start(bf16[80,2048]{1,0:T(8,128)(2,1)S(1)} %get-tuple-element.374), channel_id=1, source_target_pairs={{0,8},{2,10},{8,16},{10,18},{16,24},{18,26},{24,28},{26,30},{28,20... | collective-permute-start | bytes 983048 | tf_op jit(solution)/shard_map/ppermute | solution.py:37
  431.5 15.7 %collective-permute-start.36 = (bf16[160,2048]{1,0:T(8,128)(2,1)S(1)}, bf16[160,2048]{1,0:T(8,128)(2,1)S(1)}, u32[]{:S(2)}, u32[]{:S(2)}) collective-permute-start(bf16[160,2048]{1,0:T(8,128)(2,1)S(1)} %pad_maximum_fusion.11), channel_id=1, source_target_pairs={{0,8},{2,10},{8,16},{10,18},{16,24},{18,26},{24,28},{26,30},{28,20... | collective-permute-start | bytes 1966088 | tf_op jit(solution)/shard_map/ppermute | solution.py:37
  432.1 15.4 %collective-permute-start.40 = (bf16[160,2048]{1,0:T(8,128)(2,1)S(1)}, bf16[160,2048]{1,0:T(8,128)(2,1)S(1)}, u32[]{:S(2)}, u32[]{:S(2)}) collective-permute-start(bf16[160,2048]{1,0:T(8,128)(2,1)S(1)} %pad_maximum_fusion.12), channel_id=1, source_target_pairs={{8,0},{10,2},{16,8},{18,10},{24,16},{26,18},{28,24},{30,26},{20,28... | collective-permute-start | bytes 1966088 | tf_op jit(solution)/shard_map/ppermute | solution.py:41
  440.9 44.2 %collective-permute-start.44 = (bf16[1024,512]{1,0:T(8,128)(2,1)S(1)}, bf16[1024,512]{1,0:T(8,128)(2,1)S(1)}, u32[]{:S(2)}, u32[]{:S(2)}) collective-permute-start(bf16[1024,512]{1,0:T(8,128)(2,1)S(1)} %slice.214), channel_id=1, source_target_pairs={{0,1},{1,0},{2,3},{3,2},{4,5},{5,4},{6,7},{7,6},{8,9},{9,8},{10,11... | collective-permute-start | bytes 3145736 | tf_op jit(solution)/shard_map/ppermute | solution.py:25
  448.0 14.5 %collective-permute-start.37 = (bf16[160,2048]{1,0:T(8,128)(2,1)S(1)}, bf16[160,2048]{1,0:T(8,128)(2,1)S(1)}, u32[]{:S(2)}, u32[]{:S(2)}) collective-permute-start(bf16[160,2048]{1,0:T(8,128)(2,1)S(1)} %get-tuple-element.352), channel_id=1, source_target_pairs={{0,8},{2,10},{8,16},{10,18},{16,24},{18,26},{24,28},{26,30},{28,20... | collective-permute-start | bytes 1966088 | tf_op jit(solution)/shard_map/ppermute | solution.py:37
  449.3 14.3 %collective-permute-start.41 = (bf16[160,2048]{1,0:T(8,128)(2,1)S(1)}, bf16[160,2048]{1,0:T(8,128)(2,1)S(1)}, u32[]{:S(2)}, u32[]{:S(2)}) collective-permute-start(bf16[160,2048]{1,0:T(8,128)(2,1)S(1)} %get-tuple-element.353), channel_id=1, source_target_pairs={{8,0},{10,2},{16,8},{18,10},{24,16},{26,18},{28,24},{30,26},{20,28... | collective-permute-start | bytes 1966088 | tf_op jit(solution)/shard_map/ppermute | solution.py:41
  464.1 18.0 %collective-permute-start.42 = (bf16[160,2048]{1,0:T(8,128)(2,1)S(1)}, bf16[160,2048]{1,0:T(8,128)(2,1)S(1)}, u32[]{:S(2)}, u32[]{:S(2)}) collective-permute-start(bf16[160,2048]{1,0:T(8,128)(2,1)S(1)} %get-tuple-element.351), channel_id=1, source_target_pairs={{8,0},{10,2},{16,8},{18,10},{24,16},{26,18},{28,24},{30,26},{20,28... | collective-permute-start | bytes 1966088 | tf_op jit(solution)/shard_map/ppermute | solution.py:41
  465.0 17.1 %collective-permute-start.38 = (bf16[160,2048]{1,0:T(8,128)(2,1)S(1)}, bf16[160,2048]{1,0:T(8,128)(2,1)S(1)}, u32[]{:S(2)}, u32[]{:S(2)}) collective-permute-start(bf16[160,2048]{1,0:T(8,128)(2,1)S(1)} %get-tuple-element.350), channel_id=1, source_target_pairs={{0,8},{2,10},{8,16},{10,18},{16,24},{18,26},{24,28},{26,30},{28,20... | collective-permute-start | bytes 1966088 | tf_op jit(solution)/shard_map/ppermute | solution.py:37
  492.8 16.4 %collective-permute-start.45 = (bf16[160,2048]{1,0:T(8,128)(2,1)S(1)}, bf16[160,2048]{1,0:T(8,128)(2,1)}, u32[]{:S(2)}, u32[]{:S(2)}) collective-permute-start(bf16[160,2048]{1,0:T(8,128)(2,1)S(1)} %get-tuple-element.317), channel_id=1, source_target_pairs={{0,1},{1,0},{2,3},{3,2},{4,5},{5,4},{6,7},{7,6},{8,9},{9,8},{10,11... | collective-permute-start | bytes 1966088 | tf_op jit(solution)/shard_map/ppermute | solution.py:25
  536.1 70.8 %collective-permute-start.52 = (bf16[2048,512]{1,0:T(8,128)(2,1)}, bf16[2048,512]{1,0:T(8,128)(2,1)}, u32[]{:S(2)}, u32[]{:S(2)}) collective-permute-start(bf16[2048,512]{1,0:T(8,128)(2,1)} %convolution_convert_fusion.2), channel_id=1, source_target_pairs={{0,1},{1,0},{2,3},{3,2},{4,5},{5,4},{6,7},{7,6},{8,9},{9,8},{10,11... | collective-permute-start | bytes 6291464 | tf_op jit(solution)/shard_map/ppermute | solution.py:25
  537.7 24.5 %collective-permute-start.53 = (bf16[320,2048]{1,0:T(8,128)(2,1)}, bf16[320,2048]{1,0:T(8,128)(2,1)}, u32[]{:S(2)}, u32[]{:S(2)}) collective-permute-start(bf16[320,2048]{1,0:T(8,128)(2,1)} %multiply_convert_fusion.refs_0_), channel_id=1, source_target_pairs={{0,2},{2,0},{4,6},{6,4},{8,10},{10,8},{12,14},{14,12},{16,18},{18,... | collective-permute-start | bytes 3932168 | tf_op jit(solution)/shard_map/ppermute | solution.py:21
  543.9 14.3 %collective-permute-start.47 = (bf16[2,128,1024]{2,1,0:T(8,128)(2,1)}, bf16[2,128,1024]{2,1,0:T(8,128)(2,1)}, u32[]{:S(2)}, u32[]{:S(2)}) collective-permute-start(bf16[2,128,1024]{2,1,0:T(8,128)(2,1)} %get-tuple-element.227), channel_id=1, source_target_pairs={{0,4},{2,6},{4,0},{6,2},{8,12},{10,14},{12,8},{14,10},{16,20},{18,... | collective-permute-start | bytes 1572872 | tf_op jit(solution)/shard_map/ppermute | solution.py:21
  544.7 14.6 %collective-permute-start.48 = (bf16[2,128,1024]{2,1,0:T(8,128)(2,1)}, bf16[2,128,1024]{2,1,0:T(8,128)(2,1)}, u32[]{:S(2)}, u32[]{:S(2)}) collective-permute-start(bf16[2,128,1024]{2,1,0:T(8,128)(2,1)} %get-tuple-element.228), channel_id=1, source_target_pairs={{0,8},{2,10},{4,12},{6,14},{8,0},{10,2},{12,4},{14,6},{16,24},{18,... | collective-permute-start | bytes 1572872 | tf_op jit(solution)/shard_map/ppermute | solution.py:21
  548.2 58.8 %collective-permute-start.51 = (bf16[1024,512]{1,0:T(8,128)(2,1)}, bf16[1024,512]{1,0:T(8,128)(2,1)}, u32[]{:S(2)}, u32[]{:S(2)}) collective-permute-start(bf16[1024,512]{1,0:T(8,128)(2,1)} %slice.176), channel_id=1, source_target_pairs={{0,1},{1,0},{2,3},{3,2},{4,5},{5,4},{6,7},{7,6},{8,9},{9,8},{10,11... | collective-permute-start | bytes 3145736 | tf_op jit(solution)/shard_map/ppermute | solution.py:25
  567.2 55.2 %collective-permute-start.54 = (bf16[320,2048]{1,0:T(8,128)(2,1)}, bf16[320,2048]{1,0:T(8,128)(2,1)}, u32[]{:S(2)}, u32[]{:S(2)}) collective-permute-start(bf16[320,2048]{1,0:T(8,128)(2,1)} %pad_maximum_fusion.6.refs_0_), channel_id=1, source_target_pairs={{0,2},{2,0},{4,6},{6,4},{8,10},{10,8},{12,14},{14,12},{16,18},{18,... | collective-permute-start | bytes 3932168 | tf_op jit(solution)/shard_map/ppermute | solution.py:21
  643.2 18.5 %collective-permute-start.57 = (bf16[256,1024]{0,1:T(8,128)(2,1)}, bf16[256,1024]{0,1:T(8,128)(2,1)}, u32[]{:S(2)}, u32[]{:S(2)}) collective-permute-start(bf16[256,1024]{0,1:T(8,128)(2,1)} %pad_maximum_fusion.14), channel_id=1, source_target_pairs={{8,0},{10,2},{16,8},{18,10},{24,16},{26,18},{28,24},{30,26},{20,28... | collective-permute-start | bytes 1572872 | tf_op jit(solution)/shard_map/ppermute | solution.py:41
  649.0 22.8 %collective-permute-start.68 = (bf16[256,1024]{0,1:T(8,128)(2,1)}, bf16[256,1024]{0,1:T(8,128)(2,1)}, u32[]{:S(2)}, u32[]{:S(2)}) collective-permute-start(bf16[256,1024]{0,1:T(8,128)(2,1)} %get-tuple-element.331), channel_id=1, source_target_pairs={{0,8},{2,10},{8,16},{10,18},{16,24},{18,26},{24,28},{26,30},{28,20... | collective-permute-start | bytes 1572872 | tf_op jit(solution)/shard_map/ppermute | solution.py:37
  663.3 59.2 %collective-permute-start.58 = (bf16[256,2048]{0,1:T(8,128)(2,1)S(1)}, bf16[256,2048]{0,1:T(8,128)(2,1)S(1)}, u32[]{:S(2)}, u32[]{:S(2)}) collective-permute-start(bf16[256,2048]{0,1:T(8,128)(2,1)S(1)} %pad_maximum_fusion.9), channel_id=1, source_target_pairs={{8,0},{10,2},{16,8},{18,10},{24,16},{26,18},{28,24},{30,26},{20,28... | collective-permute-start | bytes 3145736 | tf_op jit(solution)/shard_map/ppermute | solution.py:41
  674.2 52.7 %collective-permute-start.69 = (bf16[256,2048]{0,1:T(8,128)(2,1)}, bf16[256,2048]{0,1:T(8,128)(2,1)S(1)}, u32[]{:S(2)}, u32[]{:S(2)}) collective-permute-start(bf16[256,2048]{0,1:T(8,128)(2,1)} %fusion.4), channel_id=1, source_target_pairs={{0,8},{2,10},{8,16},{10,18},{16,24},{18,26},{24,28},{26,30},{28,20... | collective-permute-start | bytes 3145736 | tf_op jit(solution)/shard_map/ppermute | solution.py:37
  689.0 48.3 %collective-permute-start.61 = (bf16[160,2048]{1,0:T(8,128)(2,1)S(1)}, bf16[160,2048]{1,0:T(8,128)(2,1)S(1)}, u32[]{:S(2)}, u32[]{:S(2)}) collective-permute-start(bf16[160,2048]{1,0:T(8,128)(2,1)S(1)} %dynamic-slice_convert_fusion), channel_id=1, source_target_pairs={{0,1},{1,0},{2,3},{3,2},{4,5},{5,4},{6,7},{7,6},{8,9},{9,8},{10,11... | collective-permute-start | bytes 1966088 | tf_op jit(solution)/shard_map/ppermute | solution.py:25
  723.8 33.9 %collective-permute-start.60 = (bf16[256,2048]{0,1:T(8,128)(2,1)}, bf16[256,2048]{0,1:T(8,128)(2,1)S(1)}, u32[]{:S(2)}, u32[]{:S(2)}) collective-permute-start(bf16[256,2048]{0,1:T(8,128)(2,1)} %add_convert_fusion.6), channel_id=1, source_target_pairs={{8,0},{10,2},{16,8},{18,10},{24,16},{26,18},{28,24},{30,26},{20,28... | collective-permute-start | bytes 3145736 | tf_op jit(solution)/shard_map/ppermute | solution.py:41
  727.3 43.9 %collective-permute-start.70 = (bf16[256,2048]{0,1:T(8,128)(2,1)S(1)}, bf16[256,2048]{0,1:T(8,128)(2,1)S(1)}, u32[]{:S(2)}, u32[]{:S(2)}) collective-permute-start(bf16[256,2048]{0,1:T(8,128)(2,1)S(1)} %add_convert_fusion.5), channel_id=1, source_target_pairs={{0,8},{2,10},{8,16},{10,18},{16,24},{18,26},{24,28},{26,30},{28,20... | collective-permute-start | bytes 3145736 | tf_op jit(solution)/shard_map/ppermute | solution.py:37
  758.8 46.6 %collective-permute-start.62 = (f32[160,2048]{1,0:T(8,128)S(1)}, f32[160,2048]{1,0:T(8,128)S(1)}, u32[]{:S(2)}, u32[]{:S(2)}) collective-permute-start(f32[160,2048]{1,0:T(8,128)S(1)} %fusion.2), channel_id=1, source_target_pairs={{0,1},{1,0},{2,3},{3,2},{4,5},{5,4},{6,7},{7,6},{8,9},{9,8},{10,11... | collective-permute-start | bytes 3932168 | tf_op jit(solution)/shard_map/ppermute | solution.py:25
  765.4 38.5 %collective-permute-start.72 = (bf16[256,2048]{0,1:T(8,128)(2,1)S(1)}, bf16[256,2048]{0,1:T(8,128)(2,1)S(1)}, u32[]{:S(2)}, u32[]{:S(2)}) collective-permute-start(bf16[256,2048]{0,1:T(8,128)(2,1)S(1)} %add_convert_fusion.3), channel_id=1, source_target_pairs={{8,0},{10,2},{16,8},{18,10},{24,16},{26,18},{28,24},{30,26},{20,28... | collective-permute-start | bytes 3145736 | tf_op jit(solution)/shard_map/ppermute | solution.py:41
  768.3 19.8 %collective-permute-start.65 = (f32[2,4,128]{2,1,0:T(4,128)S(1)}, f32[2,4,128]{2,1,0:T(4,128)S(1)}, u32[]{:S(2)}, u32[]{:S(2)}) collective-permute-start(f32[2,4,128]{2,1,0:T(4,128)S(1)} %constant_dynamic-slice_fusion.15), channel_id=1, source_target_pairs={{0,4},{2,6},{4,0},{6,2},{8,12},{10,14},{12,8},{14,10},{16,20},{18,... | collective-permute-start | bytes 12296 | tf_op jit(solution)/shard_map/ppermute | solution.py:21
  771.4 32.4 %collective-permute-start.71 = (bf16[256,2048]{0,1:T(8,128)(2,1)S(1)}, bf16[256,2048]{0,1:T(8,128)(2,1)S(1)}, u32[]{:S(2)}, u32[]{:S(2)}) collective-permute-start(bf16[256,2048]{0,1:T(8,128)(2,1)S(1)} %add_convert_fusion.4), channel_id=1, source_target_pairs={{0,8},{2,10},{8,16},{10,18},{16,24},{18,26},{24,28},{26,30},{28,20... | collective-permute-start | bytes 3145736 | tf_op jit(solution)/shard_map/ppermute | solution.py:37
  808.2 17.2 %collective-permute-start.59 = (bf16[160,2048]{1,0:T(8,128)(2,1)}, bf16[160,2048]{1,0:T(8,128)(2,1)}, u32[]{:S(2)}, u32[]{:S(2)}) collective-permute-start(bf16[160,2048]{1,0:T(8,128)(2,1)} %reduce-scatter.2.cloned.1.call-done), channel_id=1, source_target_pairs={{0,1},{1,0},{2,3},{3,2},{4,5},{5,4},{6,7},{7,6},{8,9},{9,8},{10,11... | collective-permute-start | bytes 1966088 | tf_op jit(solution)/shard_map/ppermute | solution.py:25
  (134 other events, 2040.2 us)
Sparse Core Ops, SparseCore 0:
  15.9 123.8 all-gather.4
  142.6 61.9 all-gather.6
  621.8 154.2 reduce-scatter.1

commit v7 on v6

--- a/solution.py
+++ b/solution.py
@@ -69,14 +69,12 @@
 
 
 class Fillers:
-    def __init__(self, stages):
+    def __init__(self, *stages):
         self.stages = list(stages)
-        self.outs = []
 
     def next(self, token):
-        for work, *operands in self.stages.pop(0) if self.stages else ():
-            operands = [after(operand, token) for operand in operands]
-            self.outs.append(work(*operands))
+        if self.stages:
+            self.stages.pop(0)(lambda value: after(value, token))
 
 
 def ring_sum(same, cross, fillers):
@@ -97,6 +95,17 @@
     return both[0].astype(FULL) + right.astype(FULL) + left.astype(FULL)
 
 
+def swap_in_turn(arrays, pieces, token):
+    whole = []
+    for array in arrays:
+        rows, got = array.shape[0] // pieces, []
+        for i in range(pieces):
+            got.append(swap_tensor(after(array[i * rows : (i + 1) * rows], token)))
+            token = got[-1]
+        whole.append(jnp.concatenate(got, axis=0))
+    return whole
+
+
 def rms_norm(values, gain):
     return values * lax.rsqrt(jnp.mean(values * values, axis=-1, keepdims=True) + EPSILON) * gain
 
@@ -137,27 +146,35 @@
 def collect_prompt(own, first, second):
     near, far = swap_bit(own, "dp", 1), swap_bit(own, "dp", 2)
     last = swap_bit(near if first == 1 else far, "dp", second)
-    stay = jnp.stack([own, near, far, last], axis=0)
-    return stay, swap_bit(stay, "dp", 0)
-
-
-def merge_kernel(even_ref, got_ref, keys_ref, values_ref, far_ref, near_ref):
+    blocks = []
+    for block in (own, near, far, last):
+        blocks += [block, swap_bit(block, "dp", 0)]
+    return blocks[1:]
+
+
+SMALL = pl.CostEstimate(flops=1, bytes_accessed=1, transcendentals=0)
+
+
+def merge_kernel(even_ref, *refs):
+    got, (keys_ref, values_ref, far_ref, near_ref) = refs[:3], refs[3:]
     near, far, last = 0, 1, 2
-    add = lambda j, which: add_low(even_ref[j, which], got_ref[j + 1, which])
+    add = lambda j, which: add_low(even_ref[j, which], got[j][which])
     keys_ref[0], keys_ref[1] = add(near, 0), add(last, 0)
     values_ref[0], values_ref[1] = add(far, 1), add(last, 1)
     far_ref[...], near_ref[...] = add(far, 0), add(near, 1)
 
 
 def return_prompt(odd, even):
-    got = swap_bit(odd, "dp", 0)
+    got = [swap_bit(block, "dp", 0) for block in odd]
     one = jax.ShapeDtypeStruct(even.shape[2:], LOW)
     two = jax.ShapeDtypeStruct(even.shape[1:], LOW)
-    keys, values, far, near = pl.pallas_call(merge_kernel, out_shape=[two, two, one, one])(even, got)
+    keys, values, far, near = pl.pallas_call(
+        merge_kernel, out_shape=[two, two, one, one], cost_estimate=SMALL
+    )(even, *got[1:])
     keys, values = swap_bit(keys, "dp", 1), swap_bit(values, "dp", 2)
     last_keys = swap_bit(add_low(far, keys[1]), "dp", 2)
     last_values = swap_bit(add_low(near, values[1]), "dp", 1)
-    return got, keys, values, last_keys, last_values
+    return got[0], keys, values, last_keys, last_values
 
 
 def turn(values):
@@ -197,15 +214,15 @@
     return pl.BlockSpec(array.shape, lambda h: zeros, pipeline_mode=pl.Buffered(1))
 
 
-def piece_spec(count):
-    return pl.BlockSpec((count, PR_DEV, PAIR * HEAD), lambda h: (0, 0, h))
-
-
-def all_keys(own_ref, stay_ref, cross_ref, span):
-    blocks = []
-    for j in range(GROUP // 2):
-        blocks += [stay_ref[j, :, span], cross_ref[j, :, span]]
-    return jnp.concatenate(blocks + [own_ref[PR_DEV:, span]], axis=0)
+def all_keys(own_ref, pieces, span):
+    return jnp.concatenate(
+        [own_ref[:PR_DEV, span]] + [p[:, span] for p in pieces] + [own_ref[PR_DEV:, span]], axis=0
+    )
+
+
+def turned_query(flat_ref, gain_ref, scale, cosine, sine, span):
+    normed = flat_ref[:, span] * scale * gain_ref[:, span]
+    return (normed * cosine + turn(normed) * sine).astype(LOW)
 
 
 def softmax_rows(query, keys, bias):
@@ -214,26 +231,40 @@
     return weights * (1.0 / jnp.sum(weights, axis=1, keepdims=True))
 
 
-def attend_kernel(q_ref, k_ref, v_ref, bias_ref, k_stay, k_cross, v_stay, v_cross, out_ref):
+PIECES = GROUP - 1
+
+
+def attend_kernel(flat_ref, gain_ref, scale_ref, cos_ref, sin_ref, bias_ref, k_ref, v_ref, *refs):
+    out_ref = refs[-1]
     bias = bias_ref[...].astype(FULL)
+    scale, cosine, sine = scale_ref[...], cos_ref[...], sin_ref[...]
     for at in range(0, PAIR * HEAD, HEAD):
         span = slice(at, at + HEAD)
-        probs = softmax_rows(q_ref[:, span], all_keys(k_ref, k_stay, k_cross, span), bias)
-        out_ref[:, span] = dot_nn(
-            probs.astype(LOW), all_keys(v_ref, v_stay, v_cross, span)
-        ).astype(LOW)
-
-
-def attend(queries, keys, values, bias, pieces):
-    rows, width = queries.shape
+        query = turned_query(flat_ref, gain_ref, scale, cosine, sine, span)
+        probs = softmax_rows(query, all_keys(k_ref, refs[:PIECES], span), bias)
+        values = all_keys(v_ref, refs[PIECES : 2 * PIECES], span)
+        out_ref[:, span] = dot_nn(probs.astype(LOW), values).astype(LOW)
+
+
+def attend_specs(rows, scale, cosine, sine, bias):
+    return (
+        [head_spec(rows), head_spec(1)]
+        + [kept_spec(a) for a in (scale, cosine, sine, bias)]
+        + [head_spec(rows)] * 2
+        + [head_spec(PR_DEV)] * (2 * PIECES)
+    )
+
+
+def attend(flat, gain, scale, cosine, sine, bias, keys, values, pieces):
+    rows, width = flat.shape
     return pl.pallas_call(
         attend_kernel,
         grid=(width // HEAD // PAIR,),
-        in_specs=[head_spec(rows)] * 3 + [kept_spec(bias)] + [piece_spec(GROUP // 2)] * 4,
+        in_specs=attend_specs(rows, scale, cosine, sine, bias),
         out_specs=head_spec(rows),
         out_shape=jax.ShapeDtypeStruct((rows, width), LOW),
         compiler_params=pltpu.CompilerParams(vmem_limit_bytes=40 * 1024 * 1024),
-    )(queries, keys, values, bias, *pieces)
+    )(flat, gain, scale, cosine, sine, bias, keys, values, *pieces)
 
 
 def norm_parts(step, at, grad, flat_ref, gain_ref, scale_ref, inner_ref, gain_grad_ref):
@@ -248,37 +279,21 @@
 
 
 def attend_back_kernel(
-    q_ref,
-    k_ref,
-    v_ref,
-    bias_ref,
-    back_ref,
-    flat_ref,
-    gain_ref,
-    scale_ref,
-    cos_ref,
-    sin_ref,
-    k_stay,
-    k_cross,
-    v_stay,
-    v_cross,
-    qg_ref,
-    inner_ref,
-    gain_grad_ref,
-    kg_ref,
-    vg_ref,
-    odd_ref,
-    even_ref,
+    flat_ref, gain_ref, scale_ref, cos_ref, sin_ref, bias_ref, k_ref, v_ref, *refs
 ):
+    back_ref = refs[2 * PIECES]
+    qg_ref, inner_ref, gain_grad_ref, kg_ref, vg_ref, even_ref = refs[2 * PIECES + 1 : -4]
+    odd_refs = refs[-4:]
     step = pl.program_id(0)
     bias = bias_ref[...].astype(FULL)
-    cosine, sine = cos_ref[...], sin_ref[...]
+    scale, cosine, sine = scale_ref[...], cos_ref[...], sin_ref[...]
     prompt = PR_DEV * GROUP
     for at in range(0, PAIR * HEAD, HEAD):
         span = slice(at, at + HEAD)
-        query, back = q_ref[:, span], back_ref[:, span]
-        keys = all_keys(k_ref, k_stay, k_cross, span)
-        values = all_keys(v_ref, v_stay, v_cross, span)
+        query = turned_query(flat_ref, gain_ref, scale, cosine, sine, span)
+        back = back_ref[:, span]
+        keys = all_keys(k_ref, refs[:PIECES], span)
+        values = all_keys(v_ref, refs[PIECES : 2 * PIECES], span)
         probs = softmax_rows(query, keys, bias)
         prob_grad = dot_nt(back, values)
         value_grad = dot_tn(probs.astype(LOW), back)
@@ -293,41 +308,41 @@
             own_ref[:PR_DEV, span] = grad[:PR_DEV]
             own_ref[PR_DEV:, span] = grad[prompt:]
             for j in range(1, GROUP):
-                to = odd_ref if j % 2 else even_ref
-                to[(j - 1) // 2, which, :, span] = grad[j * PR_DEV : (j + 1) * PR_DEV].astype(LOW)
-
-
-def attend_back(queries, keys, values, bias, back, flat, gain, scale, cosine, sine, pieces):
-    rows, width = queries.shape
+                to = odd_refs[j // 2] if j % 2 else even_ref.at[j // 2 - 1]
+                to[which, :, span] = grad[j * PR_DEV : (j + 1) * PR_DEV].astype(LOW)
+
+
+def attend_back(flat, gain, scale, cosine, sine, bias, keys, values, pieces, back):
+    rows, width = flat.shape
     wide = jax.ShapeDtypeStruct((rows, width), FULL)
-    both = lambda count: pl.BlockSpec((count, 2, PR_DEV, PAIR * HEAD), lambda h: (0, 0, 0, h))
+    both = pl.BlockSpec((3, 2, PR_DEV, PAIR * HEAD), lambda h: (0, 0, 0, h))
     return pl.pallas_call(
         attend_back_kernel,
         grid=(width // HEAD // PAIR,),
-        in_specs=[head_spec(rows)] * 3
-        + [kept_spec(bias), head_spec(rows), head_spec(rows), head_spec(1)]
-        + [kept_spec(a) for a in (scale, cosine, sine)]
-        + [piece_spec(GROUP // 2)] * 4,
+        in_specs=attend_specs(rows, scale, cosine, sine, bias) + [head_spec(rows)],
         out_specs=[
             head_spec(rows),
             pl.BlockSpec((rows, 1), lambda h: (0, 0)),
             head_spec(1),
             head_spec(rows),
             head_spec(rows),
-            both(4),
-            both(3),
-        ],
+            both,
+        ]
+        + [pl.BlockSpec((2, PR_DEV, PAIR * HEAD), lambda h: (0, 0, h))] * 4,
         out_shape=[
             wide,
             jax.ShapeDtypeStruct((rows, 1), FULL),
             jax.ShapeDtypeStruct((1, width), FULL),
             wide,
             wide,
-            jax.ShapeDtypeStruct((4, 2, PR_DEV, width), LOW),
             jax.ShapeDtypeStruct((3, 2, PR_DEV, width), LOW),
-        ],
+        ]
+        + [jax.ShapeDtypeStruct((2, PR_DEV, width), LOW)] * 4,
         compiler_params=pltpu.CompilerParams(vmem_limit_bytes=58 * 1024 * 1024),
-    )(queries, keys, values, bias, back, flat, gain, scale, cosine, sine, *pieces)
+        cost_estimate=pl.CostEstimate(
+            flops=20 * 10**9, bytes_accessed=40 * 10**6, transcendentals=4 * 10**6
+        ),
+    )(flat, gain, scale, cosine, sine, bias, keys, values, *pieces, back)
 
 
 def key_back_kernel(*refs):
@@ -339,7 +354,7 @@
         span = slice(at, at + HEAD)
         grads = []
         for which, own_ref, near, last in ((0, kg_ref, keys, last_keys), (1, vg_ref, values, last_values)):
-            first = own_ref[:PR_DEV, span] + got[0, which, :, span].astype(FULL)
+            first = own_ref[:PR_DEV, span] + got[which, :, span].astype(FULL)
             first = first + near[0, :, span].astype(FULL) + last[:, span].astype(FULL)
             grads.append(jnp.concatenate([first, own_ref[PR_DEV:, span]], axis=0))
         key_grad = grads[0] * cos_ref[...] - turn(grads[0]) * sin_ref[...]
@@ -357,7 +372,7 @@
         in_specs=[head_spec(rows)] * 3
         + [head_spec(1)]
         + [kept_spec(a) for a in (scale, cosine, sine)]
-        + [pl.BlockSpec((1, 2, PR_DEV, columns), lambda h: (0, 0, 0, h))]
+        + [pl.BlockSpec((2, PR_DEV, columns), lambda h: (0, 0, h))]
         + [pl.BlockSpec((1, PR_DEV, columns), lambda h: (0, 0, h))] * 2
         + [head_spec(PR_DEV)] * 2,
         out_specs=[
@@ -372,6 +387,7 @@
             jax.ShapeDtypeStruct((1, width), FULL),
             jax.ShapeDtypeStruct((rows, width), LOW),
         ],
+        cost_estimate=SMALL,
     )(key_grad, value_grad, flat, gain, scale, cosine, sine, *returned)
 
 
@@ -528,21 +544,95 @@
     )(*rows, *[gathered] * len(places))
 
 
-def ring_weights(first, second, fillers):
-    rows = first.shape[0] // len(RING)
-    cut = (first.shape[1] + second.shape[1]) // 2
-    chip = lax.axis_index("dp") // 2
-    place = jnp.where(chip % 2 == 0, chip // 2, 7 - chip // 2)
-
-    def part(hop):
-        there = (place + hop) % len(RING)
-        at = jnp.where(there < 4, 2 * there, 2 * (7 - there) + 1) * rows
-        return jnp.concatenate(
-            [lax.dynamic_slice_in_dim(a, at, rows, axis=0) for a in (first, second)], axis=1
+def pre_kernel(core_ref, *refs):
+    inputs, outs = refs[:11], refs[11:]
+    step = pl.program_id(0)
+    columns = inputs[0].shape[1]
+    parts = []
+    for flat, grad, gain, scale, inner in (inputs[:5], inputs[5:10]):
+        scaled = scale[...]
+        mean = inner[...] * (1.0 / (HEADS * HEAD))
+        parts.append(
+            (
+                scaled * gain[...] * grad[...] - flat[...] * (scaled * scaled * scaled) * mean
+            ).astype(LOW)
         )
-
-    far = part(4)
-    right, left = ahead(far[:, :cut]), behind(far[:, cut:])
+    outs[0][...], outs[1][...] = parts
+
+    @pl.when(step != core_ref[0])
+    def _():
+        for j, part in enumerate((*parts, inputs[10][...])):
+            outs[2][:, j * columns : (j + 1) * columns] = part
+
+
+def pre_grads_pass(core, query, key, value):
+    rows, width = value.shape
+    columns = width // 2
+    half = lambda rows: pl.BlockSpec((rows, columns), lambda h: (0, h))
+    side = [half(rows), half(rows), half(1)] + [pl.BlockSpec((rows, 1), lambda h: (0, 0))] * 2
+    return pl.pallas_call(
+        pre_kernel,
+        grid=(2,),
+        in_specs=[pl.BlockSpec(memory_space=pltpu.SMEM)] + side + side + [half(rows)],
+        out_specs=[half(rows), half(rows), pl.BlockSpec((rows, 3 * columns), lambda h: (0, 0))],
+        out_shape=[jax.ShapeDtypeStruct((rows, width), LOW)] * 2
+        + [jax.ShapeDtypeStruct((rows, 3 * columns), LOW)],
+    )(core, *query, *key, value)
+
+
+def weight_kernel(chip_ref, core_ref, *refs):
+    normed, normed_got, back, back_got, query, key, value, got, context, context_got = refs[:10]
+    out_ref, pre_both, context_both = refs[10:]
+    rows, columns = query.shape
+
+    @pl.when(pl.program_id(0) == 0)
+    def _():
+        for j, part in enumerate((query, key, value)):
+            pre_both[:rows, j * columns : (j + 1) * columns] = part[...]
+        pre_both[rows:] = got[...]
+        context_both[:rows] = context[...]
+        context_both[rows:] = context_got[...]
+
+    left = jnp.concatenate([normed[...], normed_got[...]], axis=0)
+    out_ref[0, :, : 3 * columns] = dot_tn(left, pre_both[...]).astype(LOW)
+    left = jnp.concatenate([back[...], back_got[...]], axis=0)
+    out_ref[0, :, 3 * columns :] = dot_tn(left, context_both[...]).astype(LOW)
+
+
+def weight_grads(chips, core, normed, back, pre_grads, got, context, context_got):
+    rows, width = normed[0].shape
+    columns = context_got.shape[1]
+    count = chips.shape[0]
+    block = width // count
+    tall = pl.BlockSpec((rows, block), lambda i, chip, core: (0, chip[i]))
+    mine = pl.BlockSpec((rows, columns), lambda i, chip, core: (0, core[0]))
+    fixed = lambda a: pl.BlockSpec(a.shape, lambda i, chip, core: (0, 0))
+    return pl.pallas_call(
+        weight_kernel,
+        grid_spec=pltpu.PrefetchScalarGridSpec(
+            num_scalar_prefetch=2,
+            grid=(count,),
+            in_specs=[tall] * 4 + [mine] * 3 + [fixed(got), mine, fixed(context_got)],
+            out_specs=pl.BlockSpec((1, block, 4 * columns), lambda i, chip, core: (i, 0, 0)),
+            scratch_shapes=[
+                pltpu.VMEM((2 * rows, 3 * columns), LOW),
+                pltpu.VMEM((2 * rows, columns), LOW),
+            ],
+        ),
+        out_shape=jax.ShapeDtypeStruct((count, block, 4 * columns), LOW),
+        compiler_params=pltpu.CompilerParams(vmem_limit_bytes=40 * 1024 * 1024),
+        cost_estimate=pl.CostEstimate(
+            flops=16 * rows * width * columns,
+            bytes_accessed=2 * (4 * rows * width + 8 * rows * columns + 4 * width * columns),
+            transcendentals=0,
+        ),
+    )(chips, core, *normed, *back, *pre_grads, got, context, context_got)
+
+
+def ring_weights(blocks, fillers):
+    part = lambda hop: blocks[HOPS.index(hop)]
+    cut = blocks.shape[2] // 2
+    right, left = ahead(part(4)[:, :cut]), behind(part(4)[:, cut:])
     fillers.next(left)
     outward, inward = part(3), part(-3)
     right = jnp.concatenate([add_low(outward[:, :cut], right), outward[:, cut:]], axis=1)
@@ -639,16 +729,13 @@
     stores[0].start()
     for half in range(2):
         columns = pl.ds(half * part, part)
-        if half == 0:
-            loads[0][0].wait()
+        loads[half][0].wait()
         gate_pre = dot_nn(rows[...], wide[:, across(0, half)])
-        if half == 0:
-            loads[0][1].wait()
+        loads[half][1].wait()
         up_pre = dot_nn(rows[...], wide[:, across(1, half)])
         if half == 0:
             load_back.wait()
-            for one in loads[0][2:] + loads[1]:
-                one.wait()
+        loads[half][2].wait()
         hidden_grad = gate * dot_nt(back[...], wd[half])
         sig = 1.0 / (1.0 + jnp.exp(-gate_pre))
         act = gate_pre * sig
@@ -770,9 +857,9 @@
     waiting = swap_tensor(after(waiting, pair))
     same[0], cross[0], held = expert_chunk([rows, pair], back, gate, mats, 6, None, size)
     for hop in (1, 2, 3):
+        left, right, same[hop - 1] = together(left, right, same[hop - 1])
         pieces = [left, swap(left), right, swap(right)]
         if hop < 3:
-            left, right, same[hop - 1] = together(left, right, same[hop - 1])
             left, right = ahead(left), behind(right)
         else:
             left, right = ahead(left[:cut]), behind(right[cut:])
@@ -928,8 +1015,8 @@
     key_scale = lax.rsqrt(key_sq / column_total + EPSILON)[:, None]
     keys_b = rope_pass(key_flat, gain_key_local[None], key_scale, cosine, sine)
     pieces = (*collect_prompt(keys_b[:PR_DEV], 2, 1), *value_pieces)
-    queries_b = rope_pass(query_flat, gain_query_local[None], query_scale, cosine, sine)
-    context_b = attend(queries_b, keys_b, values_b, bias, pieces)
+    turned_by = (gain_query_local[None], query_scale, cosine, sine, bias)
+    context_b = attend(query_flat, *turned_by, keys_b, values_b, pieces)
     gathered_out = after(gathered_out, context_b)
     attn_part = project_back([context_b], gathered_out, block, (0,))
     attn_part, late, weight = together(attn_part, down_mats[1], weight)
@@ -955,15 +1042,20 @@
         )
         expert_in, h0, h1, g0, g1, u0, u1 = held
         down_got = swap_tensor(low_tn(h1, back_rows))
-        fillers = Fillers(
-            [
-                [(low_tn, expert_in, g1)],
-                [(low_tn, expert_in, u1)],
-                [(lambda *h: mixed_pass(*h, down_mats, blocks), h0, h1)],
-            ]
-        )
+        late = {}
+
+        def gate_stage(gated):
+            late["gate"] = low_tn(gated(expert_in), g1)
+
+        def up_stage(gated):
+            late["up"] = low_tn(gated(expert_in), u1)
+
+        def mixed_stage(gated):
+            late["mixed"] = mixed_pass(gated(h0), h1, down_mats, blocks)
+
+        fillers = Fillers(gate_stage, up_stage, mixed_stage)
         normed_two_grad = ring_sum(same, cross, fillers)
-        gate_sent, up_sent, mixed_rows = fillers.outs
+        gate_sent, up_sent, mixed_rows = late["gate"], late["up"], late["mixed"]
     else:
         hidden_other = swap_tensor(hidden_state)
         expert_in = lax.all_gather(normed_two_b, "dp", axis=0, tiled=True)
@@ -989,41 +1081,40 @@
     attn_grad_half = state_half.astype(LOW)
     attn_grad_b = both_halves(attn_grad_half, swap_tensor(attn_grad_half))
     attn_grad_b, gate_sent, up_sent = together(attn_grad_b, gate_sent, up_sent)
-    gate_second, up_got = swap_tensor(lower(gate_sent)), swap_tensor(up_sent)
     (context_grad_b,) = project(attn_grad_b, gathered_out, block, (0,), (LOW,))
-    query_normed_grad, query_inner, query_gain_part, key_grad, value_grad, odd, even = attend_back(
-        queries_b,
-        keys_b,
-        values_b,
-        bias,
-        context_grad_b,
-        query_flat,
-        gain_query_local[None],
-        query_scale,
-        cosine,
-        sine,
-        pieces,
+    gate_second, up_first = swap_in_turn([lower(gate_sent), upper(up_sent)], 2, context_grad_b)
+    if ring:
+        pair = lambda own: (own, swap_bit(own, "dp", 0))
+        columns = local_width // 2
+        context_sent = lax.dynamic_slice_in_dim(context_b, (1 - core) * columns, columns, axis=1)
+        normed_pair, attn_grad_pair = pair(normed_b), pair(attn_grad_b)
+        context_got = swap_bit(context_sent, "dp", 0)
+    query_normed_grad, query_inner, query_gain_part, key_grad, value_grad, even, *odd = attend_back(
+        query_flat, *turned_by, keys_b, values_b, pieces, context_grad_b
     )
     returned = return_prompt(odd, even)
     key_normed_grad, key_inner, key_gain_part, value_pre_grad = key_back(
         key_grad, value_grad, key_flat, gain_key_local[None], key_scale, cosine, sine, returned
     )
-    query_inner, key_inner, gate_second, up_got = together(
-        query_inner, key_inner, gate_second, up_got
-    )
+    query_inner, gate_second, up_first = together(query_inner, gate_second, up_first)
     query_inner, key_inner = lax.psum((query_inner[:, 0], key_inner[:, 0]), "tensor")
-    pre_grad = lambda scale, gain, grad, flat, inner: (
-        scale * gain * grad - flat * (scale * scale * scale) * (inner / column_total)[:, None]
-    ).astype(LOW)
-    query_pre_grad = pre_grad(
-        query_scale, gain_query_local, query_normed_grad, query_flat, query_inner
-    )
-    key_pre_grad = pre_grad(key_scale, gain_key_local, key_normed_grad, key_flat, key_inner)
-    mixed = after(mixed, key_pre_grad)
+    (up_second,) = swap_in_turn([lower(up_sent)], 2, query_inner)
+    query_pre_grad, key_pre_grad, pre_sent = pre_grads_pass(
+        core[None],
+        (
+            query_flat,
+            query_normed_grad,
+            gain_query_local[None],
+            query_scale,
+            query_inner[:, None],
+        ),
+        (key_flat, key_normed_grad, gain_key_local[None], key_scale, key_inner[:, None]),
+        value_pre_grad,
+    )
+    up_got = jnp.concatenate([up_first, up_second], axis=0)
     gate_got = jnp.concatenate([gate_first, gate_second], axis=0)
     pre_grads = (query_pre_grad, key_pre_grad, value_pre_grad)
     grad_sum = lambda left, right, got: dot_tn(left, right) + got.astype(FULL)
-    down, gate, up = (h0, back_rows, down_got), (expert_in, g0, gate_got), (expert_in, u0, up_got)
     back_all = lambda *grads: project_back(grads, gathered, block, (0, 1, 2))
 
     def share(part):
@@ -1036,31 +1127,36 @@
         return input_half, swap_tensor(input_half), gain_one_grad
 
     if ring:
-        columns = local_width // 2
-        mine = lambda a: lax.dynamic_slice_in_dim(a, core * columns, columns, axis=1)
-        theirs = lambda a: lax.dynamic_slice_in_dim(a, (1 - core) * columns, columns, axis=1)
-        pair = lambda own, sent: jnp.concatenate([own, swap_bit(sent, "dp", 0)], axis=0)
-        half = lambda *a: pair(
-            jnp.concatenate([mine(x) for x in a], axis=1),
-            jnp.concatenate([theirs(x) for x in a], axis=1),
+        pre_got = swap_bit(pre_sent, "dp", 0)
+        w_blocks = weight_grads(
+            blocks[::2] // 2,
+            core[None],
+            normed_pair,
+            attn_grad_pair,
+            pre_grads,
+            pre_got,
+            context_b,
+            context_got,
         )
-        normed_pair, attn_grad_pair = pair(normed_b, normed_b), pair(attn_grad_b, attn_grad_b)
-        normed_pair, attn_grad_pair, context_half = together(
-            normed_pair, attn_grad_pair, half(context_b)
-        )
-        out_half = low_tn(attn_grad_pair, context_half)
-        grads_half, out_half = together(half(*pre_grads), out_half)
-        fillers = Fillers(
-            [
-                [(lambda *grads: share(back_all(*grads)), *pre_grads)],
-                [(grad_sum, *down), (swap_tensor, mixed)],
-                [(grad_sum, *gate)],
-            ]
-        )
-        w_half, token = ring_weights(low_tn(normed_pair, grads_half), out_half, fillers)
-        (own_part, other_part), down_grad, mixed_other, gate_w_grad = fillers.outs
-        input_half, input_other, gain_one_grad = input_side(own_part, after(other_part, token))
-        up_w_grad = grad_sum(after(up[0], token), *up[1:])
+        w_blocks, mixed = together(w_blocks, mixed)
+        mixed_other = swap_tensor(mixed)
+        late = {}
+
+        def normed_stage(gated):
+            late["normed"] = share(back_all(*[gated(grad) for grad in pre_grads]))
+
+        def expert_stage(gated):
+            late["down"] = grad_sum(gated(h0), back_rows, down_got)
+            late["up"] = grad_sum(gated(expert_in), u0, up_got)
+
+        def input_stage(gated):
+            late["input"] = input_side(late["normed"][0], gated(late["normed"][1]))
+
+        fillers = Fillers(normed_stage, expert_stage, input_stage)
+        w_half, token = ring_weights(w_blocks, fillers)
+        input_half, input_other, gain_one_grad = late["input"]
+        down_grad, up_w_grad = late["down"], late["up"]
+        gate_w_grad = grad_sum(after(expert_in, token), g0, gate_got)
         own_w = lax.dynamic_slice_in_dim(w_half, core * block, block, axis=0)
         got_w = swap_bit(
             lax.dynamic_slice_in_dim(w_half, (1 - core) * block, block, axis=0), "dp", 0
@@ -1077,7 +1173,9 @@
         )
         w_sum = lax.psum_scatter(w_grads, "dp", scatter_dimension=0, tiled=True).astype(FULL)
         w_sums = [w_sum[:, j * local_width : (j + 1) * local_width] for j in range(4)]
-        down_grad, gate_w_grad, up_w_grad = grad_sum(*down), grad_sum(*gate), grad_sum(*up)
+        down_grad = grad_sum(h0, back_rows, down_got)
+        gate_w_grad = grad_sum(expert_in, g0, gate_got)
+        up_w_grad = grad_sum(expert_in, u0, up_got)
         mixed_other = swap_tensor(mixed)
         input_half, input_other, gain_one_grad = input_side(*share(back_all(*pre_grads)))
     input_grad = both_halves(input_half, input_other)

time: 842 us -> 765 us (0.909)
  waiting for transfers between devices: 352 us -> 287 us
  other arithmetic: 70.2 us -> 58.3 us
  Pallas kernels: 187 us -> 198 us
    ppermute x12, waiting for transfers between devices: 49.5 us -> 8.27 us  [ahead(): return lax.ppermute(block, 'dp', AHEAD)]
    dynamic_slice x14 -> x1, local copies, waits for them, and re-layouts: 20 us -> 0.03 us  [body(): lax.dynamic_slice_in_dim(context_b, (1 - core) * columns, columns, axis=1)]
    ppermute x12, waiting for transfers between devices: 61.9 us -> 43.3 us  [behind(): return lax.ppermute(block, 'dp', BEHIND)]
    pallas_call x2 -> x4, Pallas kernels: 13.1 us -> 31.1 us  [the longest x1 12.6 us: weight_grads(): pl.pallas_call(weight_kernel, grid_spec=pltpu.PrefetchScalarGridSpec(num_...]
    ppermute x12, starting transfers between devices: 31.5 us -> 16.9 us  [ahead(): return lax.ppermute(block, 'dp', AHEAD)]
    ppermute x14 -> x18, waiting for transfers between devices: 148 us -> 135 us  [swap_tensor(): return lax.ppermute(block, 'tensor', [(0, 1), (1, 0)])]
    concatenate x7 -> x2, other arithmetic: 14.3 us -> 4.58 us  [swap_in_turn(): whole.append(jnp.concatenate(got, axis=0))]
    ppermute x36 -> x45, waiting for transfers between devices: 62.7 us -> 69.9 us  [swap_bit(): return lax.ppermute(block, axis, [(i, i ^ 1 << bit) for i in range(count)])]
  transfers between devices with their start and end apart: 77 -> 90, of which waited for: 32 -> 42; matrix products, arithmetic and copies ran while one was open for 17% -> 15% of each run, Pallas kernels for 19% -> 26%
where the time goes in v7:
time: 765 us; the launch traced here: 758 us
  waiting for transfers between devices  287 us (38%)
  Pallas kernels  198 us (26%)
  starting transfers between devices  71.8 us (9%)
  local copies, waits for them, and re-layouts  62.1 us (8%)
  other arithmetic  58.3 us (8%)
  matrix products  49.9 us (7%)
  between operations  15.7 us (2%)
  blocking collectives  15.1 us (2%)
    ppermute x18, waiting for transfers between devices, swap_tensor(): return lax.ppermute(block, 'tensor', [(0, 1), (1, 0)])  135 us
    pallas_call x5, Pallas kernels, expert_chunk(): pl.pallas_call(lambda *refs: chunk_kernel(len(pieces), len(held), at, siz...  91.4 us
    ppermute x45, waiting for transfers between devices, swap_bit(): return lax.ppermute(block, axis, [(i, i ^ 1 << bit) for i in range(count)])  69.9 us
    dot_general x6, matrix products, dot_tn(): lax.dot_general(left, right, (((0,), (0,)), ((), ())), preferred_element_...  49.8 us
    ppermute x12, waiting for transfers between devices, behind(): return lax.ppermute(block, 'dp', BEHIND)  43.3 us
    unnamed x226, local copies, waits for them, and re-layouts  42.6 us
    all_gather x1, waiting for transfers between devices, body(): gathered = lax.all_gather(packed, 'dp', axis=0, tiled=False)  29.5 us
    ppermute x18, starting transfers between devices, swap_tensor(): return lax.ppermute(block, 'tensor', [(0, 1), (1, 0)])  24 us
  transfers between devices with their start and end apart: 90, of which 42 were waited for; matrix products, arithmetic and copies ran while one was open for 15% of the time, Pallas kernels for 26%

profile of v7, /device:TPU:0, one launch (start us, length us, event | category | flops | bytes accessed | tf_op | source)
XLA Modules:
  0.0 757.9 jit_solution(4467224352177061809)
XLA Ops:
  9.4 2.5 constant_dynamic-slice_fusion.7.refs_0_
  12.7 3.1 shard_map.282
  16.6 3.0 collective-permute-start
  22.8 43.4 %collective-permute-done.refs_5_.refs_7_ = bf16[2048,512]{1,0:T(8,128)(2,1)} collective-permute-done((bf16[2048,512]{1,0:T(8,128)(2,1)S(1)}, bf16[2048,512]{1,0:T(8,128)(2,1)}, u32[]{:S(2)}, u32[]{:S(2)}) %collective-permute-start) | collective-permute-done | bytes 2097184 | tf_op jit(solution)/shard_map/ppermute | solution.py:25
  66.2 44.1 %collective-permute-done.1.refs_7_.refs_9_ = bf16[2048,512]{1,0:T(8,128)(2,1)} collective-permute-done((bf16[2048,512]{1,0:T(8,128)(2,1)}, bf16[2048,512]{1,0:T(8,128)(2,1)}, u32[]{:S(2)}, u32[]{:S(2)}) %collective-permute-start.1) | collective-permute-done | bytes 2097184 | tf_op jit(solution)/shard_map/ppermute | solution.py:25
  110.3 29.5 %all-gather.5.cloned.1.call-done = bf16[11520,1024]{1,0:T(8,128)(2,1)} async-done(((bf16[720,1024]{1,0:T(8,128)(2,1)}), bf16[11520,1024]{1,0:T(8,128)(2,1)}) %all-gather.5.cloned.1.call-update) | async-done | bytes 23592976 | tf_op jit(solution)/shard_map/all_gather | solution.py:950
  141.8 10.1 %shard_map.283 = (f32[320,1024]{1,0:T(8,128)S(1)}, f32[320,1024]{1,0:T(8,128)S(1)}, bf16[320,1024]{1,0:T(8,128)(2,1)S(1)}) custom-call(bf16[320,2048]{1,0:T(8,128)(2,1)S(1)} %multiply_convert_fusion.refs_0_, bf16[16,720,1024]{2,1,0:T(8,128)(2,1)} %bitcast.118, bf16[16,720,1024]{2,1,0:T(8,128)(2,1)} %bitcast.119, bf16[16,720,1024]{2,1,0:T(8,128)(2,1)} %bitcast.120), custom_call_target="tpu_custom_call" | custom-call | flops 4026531840 | bytes 15204352 | tf_op jit(solution)/shard_map/pallas_call | solution.py:501
  153.9 5.4 all-reduce.4
  164.3 2.6 shard_map.284.k_ref
  174.5 10.4 %collective-permute-done.5.refs_3_ = bf16[128,1024]{1,0:T(8,128)(2,1)} collective-permute-done((bf16[128,1024]{1,0:T(8,128)(2,1)}, bf16[128,1024]{1,0:T(8,128)(2,1)}, u32[]{:S(2)}, u32[]{:S(2)}) %collective-permute-start.5) | collective-permute-done | bytes 262176 | tf_op jit(solution)/shard_map/ppermute | solution.py:21
  188.6 6.1 collective-permute-done.10.refs_8_
  196.6 2.8 collective-permute-done.7.refs_5_
  201.4 6.0 collective-permute-done.14.refs_12_
  216.4 10.6 %shard_map.285.refs_0_.refs_8_ = bf16[320,1024]{1,0:T(8,128)(2,1)S(1)} custom-call(f32[320,1024]{1,0:T(8,128)S(1)} %copy-done.11, f32[1,1024]{1,0:T(1,128)S(1)} %bitcast.111, f32[320,1]{1,0:T(8,128)S(1)} %broadcast_in_dim.136.scale_ref.refs_3_, f32[320,128]{1,0:T(8,128)S(1)} %copy-done.24, f32[320,128]{1,0:T(8,128)S(1)} %copy-done.23, ...), custom_call_target="tpu_custom_call" | custom-call | tf_op jit(solution)/shard_map/pallas_call | solution.py:260
  232.4 2.3 shard_map.286
  236.4 5.7 shard_map.287.refs_3_.refs_5_
  242.1 3.9 copy-done
  246.0 5.6 collective-permute-done.17
  260.0 12.3 %shard_map.288 = (bf16[160,2048]{1,0:T(8,128)(2,1)S(1)}, bf16[160,2048]{1,0:T(8,128)(2,1)S(1)}, bf16[2560,2048]{1,0:T(8,128)(2,1)}, bf16[2560,512]{1,0:T(8,128)(...) custom-call(f32[2560,1]{1,0:T(8,128)S(1)} %copy.76.refs_0_, ...), custom_call_target="tpu_custom_call" | custom-call | flops 6710886400 | bytes 19791872 | tf_op jit(solution)/shard_map/pallas_call | solution.py:784
  274.1 2.8 collective-permute-done.21.refs_3_
  280.1 21.3 %shard_map.289 = (bf16[320,2048]{1,0:T(8,128)(2,1)S(1)}, bf16[320,2048]{1,0:T(8,128)(2,1)}, bf16[2560,2048]{1,0:T(8,128)(2,1)}, bf16[2560,512]{1,0:T(8,128)(2,1)...) custom-call(f32[2560,1]{1,0:T(8,128)} %copy-done.3, ...), custom_call_target="tpu_custom_call", output_to_operand_aliasing={{2}: (12, {}), {3}: (13, {}), {4}: (14, {}), {5}: (15, {}),... | custom-call | flops 13421772800 | bytes 27000832 | tf_op jit(solution)/shard_map/pallas_call | solution.py:784
  305.7 22.4 %shard_map.290 = (bf16[320,2048]{1,0:T(8,128)(2,1)S(1)}, bf16[320,2048]{1,0:T(8,128)(2,1)}, bf16[2560,2048]{1,0:T(8,128)(2,1)}, bf16[2560,512]{1,0:T(8,128)(2,1)...) custom-call(f32[2560,1]{1,0:T(8,128)} %copy-done.3, ...), custom_call_target="tpu_custom_call", output_to_operand_aliasing={{2}: (12, {}), {3}: (13, {}), {4}: (14, {}), {5}: (15, {}),... | custom-call | flops 13421772800 | bytes 27000832 | tf_op jit(solution)/shard_map/pallas_call | solution.py:784
  334.4 5.9 collective-permute-done.37.refs_1_
  340.3 2.6 collective-permute-done.38.refs_2_
  343.6 23.0 %shard_map.291 = (bf16[320,2048]{1,0:T(8,128)(2,1)S(1)}, bf16[320,2048]{1,0:T(8,128)(2,1)}, bf16[2560,2048]{1,0:T(8,128)(2,1)}, bf16[2560,512]{1,0:T(8,128)(2,1)...) custom-call(f32[2560,1]{1,0:T(8,128)} %copy-done.3, ...), custom_call_target="tpu_custom_call", output_to_operand_aliasing={{2}: (12, {}), {3}: (13, {}), {4}: (14, {}), {5}: (15, {}),... | custom-call | flops 13421772800 | bytes 27000832 | tf_op jit(solution)/shard_map/pallas_call | solution.py:784
  374.3 12.4 %shard_map.292 = (bf16[160,2048]{1,0:T(8,128)(2,1)S(1)}, bf16[160,2048]{1,0:T(8,128)(2,1)S(1)}, bf16[2560,2048]{1,0:T(8,128)(2,1)}, bf16[2560,512]{1,0:T(8,128)(...) custom-call(f32[2560,1]{1,0:T(8,128)S(1)} %copy-done.4, ...), custom_call_target="tpu_custom_call", output_to_operand_aliasing={{2}: (12, {}), {3}: (13, {}), {4}: (14, {}), {5}: (15, {}),... | custom-call | flops 6710886400 | bytes 19791872 | tf_op jit(solution)/shard_map/pallas_call | solution.py:784
  387.3 8.6 %convolution_convert_fusion.2 = bf16[512,2048]{1,0:T(8,128)(2,1)} fusion(bf16[2560,512]{1,0:T(8,128)(2,1)} %get-tuple-element.214.h1_ref, bf16[2560,2048]{1,0:T(8,128)(2,1)S(1)} %bitcast.99), kind=kOutput, calls=%fused_computation.6 | convolution fusion | flops 5369757696 | bytes 15204352 | tf_op jit(solution)/shard_map/dot_general | solution.py:139
  403.8 7.2 collective-permute-done.46
  414.1 6.0 convolution_convert_fusion.1
  421.9 5.8 collective-permute-done.47
  430.4 6.9 convolution_convert_fusion
  437.3 5.9 collective-permute-done.48
  445.9 16.0 %shard_map.293 = bf16[8,2,160,2048]{3,2,1,0:T(8,128)(2,1)} custom-call(s32[8]{0:T(128)S(1)} %copy-done.57, s32[1]{0:T(128)S(6)} %select_n.213.core_ref, bf16[2560,512]{1,0:T(8,128)(2,1)S(1)} %copy-done.5, bf16[2560,512]{1,0:T(8,128)(2,1)S(1)} %copy-done.6, bf16[512,2048]{1,0:T(8,128)(2,1)S(1)} %bitcast.108, ...), custom_call_target="tpu_custom_call" | custom-call | flops 10737418240 | bytes 19922944 | tf_op jit(solution)/shard_map/pallas_call | solution.py:828
  461.9 2.6 convert_add_fusion.8
  470.5 3.6 fusion.45
  475.7 14.4 %collective-permute-done.52 = bf16[160,2048]{1,0:T(8,128)(2,1)} collective-permute-done((bf16[160,2048]{1,0:T(8,128)(2,1)S(1)}, bf16[160,2048]{1,0:T(8,128)(2,1)}, u32[]{:S(2)}, u32[]{:S(2)}) %collective-permute-start.52) | collective-permute-done | bytes 655392 | tf_op jit(solution)/shard_map/ppermute | solution.py:25
  491.7 2.7 shard_map.294.refs_14_
  497.0 10.6 %collective-permute-done.54 = bf16[512,512]{1,0:T(8,128)(2,1)S(1)} collective-permute-done((bf16[512,512]{1,0:T(8,128)(2,1)S(1)}, bf16[512,512]{1,0:T(8,128)(2,1)S(1)}, u32[]{:S(2)}, u32[]{:S(2)}) %collective-permute-start.54) | collective-permute-done | bytes 524320 | tf_op jit(solution)/shard_map/ppermute | solution.py:25
  509.3 19.8 %shard_map.295 = (f32[320,1024]{1,0:T(8,128)}, f32[320,1]{1,0:T(8,128)}, f32[1,1024]{1,0:T(1,128)}, f32[320,1024]{1,0:T(8,128)}, f32[320,1024]{1,0:T(8,128)}, /*...) custom-call(f32[320,1024]{1,0:T(8,128)} %copy-done.10, ...), custom_call_target="tpu_custom_call" | custom-call | flops 20000000000 | bytes 40000000 | tf_op jit(solution)/shard_map/pallas_call | solution.py:319
  532.9 3.1 shard_map.296
  537.9 7.7 %collective-permute-done.56 = bf16[512,512]{1,0:T(8,128)(2,1)} collective-permute-done((bf16[512,512]{1,0:T(8,128)(2,1)}, bf16[512,512]{1,0:T(8,128)(2,1)}, u32[]{:S(2)}, u32[]{:S(2)}) %collective-permute-start.56) | collective-permute-done | bytes 524320 | tf_op jit(solution)/shard_map/ppermute | solution.py:25
  546.3 8.6 %collective-permute-done.63.refs_9_ = bf16[2,128,1024]{2,1,0:T(8,128)(2,1)S(1)} collective-permute-done((bf16[2,128,1024]{2,1,0:T(8,128)(2,1)}, bf16[2,128,1024]{2,1,0:T(8,128)(2,1)S(1)}, u32[]{:S(2)}, u32[]{:S(2)}) %collective-permute-start.63) | collective-permute-done | bytes 524320 | tf_op jit(solution)/shard_map/ppermute | solution.py:21
  557.6 5.5 collective-permute-done.62.refs_8_
  565.6 2.3 pad_maximum_fusion.3
  568.4 4.4 collective-permute-done.64.refs_10_
  572.8 5.7 shard_map.297
  578.6 2.3 pad_maximum_fusion.4
  581.0 9.6 %all-reduce.3 = (f32[320]{0:T(512)S(1)}, f32[320,1]{1,0:T(8,128)}) all-reduce(f32[320]{0:T(512)S(1)} %reduce.1, f32[320,1]{1,0:T(8,128)S(1)} %copy-done.85), channel_id=1, replica_groups=mesh['dp'=16,'tensor'=2] {'tensor'}, use_global_device_ids=true, to_apply=%region_13.14 | all-reduce | flops 640 | bytes 5120 | tf_op jit(solution)/shard_map/psum | solution.py:1100
  591.4 4.8 shard_map.298
  596.9 2.4 collective-permute-done.67.refs_9_
  605.2 12.6 %shard_map.299 = bf16[8,256,2048]{2,1,0:T(8,128)(2,1)} custom-call(s32[8]{0:T(128)S(1)} %copy-done.57, s32[1]{0:T(128)} %bitcast.15.core_ref, bf16[320,2048]{1,0:T(8,128)(2,1)S(1)} %copy-done.15, bf16[320,2048]{1,0:T(8,128)(2,1)} %collective-permute-done.18.refs_1_, bf16[320,2048]{1,0:T(8,128)(2,1)S(1)} %copy-done.13, ...), custom_call_target="tpu_custom_call" | custom-call | flops 5368709120 | bytes 16252928 | tf_op jit(solution)/shard_map/pallas_call | solution.py:610
  617.8 3.6 slice_bitcast_fusion
  628.8 7.9 %collective-permute-done.69 = bf16[256,1024]{1,0:T(8,128)(2,1)} collective-permute-done((bf16[256,1024]{1,0:T(8,128)(2,1)}, bf16[256,1024]{1,0:T(8,128)(2,1)}, u32[]{:S(2)}, u32[]{:S(2)}) %collective-permute-start.69) | collective-permute-done | bytes 524320 | tf_op jit(solution)/shard_map/ppermute | solution.py:41
  642.9 7.7 %shard_map.300 = f32[320,2048]{1,0:T(8,128)S(1)} custom-call(bf16[320,1024]{1,0:T(8,128)(2,1)S(1)} %copy-done.35, bf16[320,1024]{1,0:T(8,128)(2,1)S(1)} %copy-done.37, bf16[320,1024]{1,0:T(8,128)(2,1)S(1)} %copy-done.22, bf16[16,720,1024]{2,1,0:T(8,128)(2,1)} %bitcast.123, bf16[16,720,1024]{2,1,0:T(8,128)(2,1)} %bitcast.124, bf16[16,720,1024]{2,1,0:T(8,128)(2,1)} %bitcast.125), custom_call_target="tpu_custom_call" | custom-call | flops 4026531840 | bytes 15204352 | tf_op jit(solution)/shard_map/pallas_call | solution.py:532
  652.7 9.8 %collective-permute-done.70 = bf16[256,2048]{1,0:T(8,128)(2,1)S(1)} collective-permute-done((bf16[256,2048]{1,0:T(8,128)(2,1)S(1)}, bf16[256,2048]{1,0:T(8,128)(2,1)S(1)}, u32[]{:S(2)}, u32[]{:S(2)}) %collective-permute-start.70) | collective-permute-done | bytes 1048608 | tf_op jit(solution)/shard_map/ppermute | solution.py:41
  664.0 2.5 fusion.1
  668.7 11.4 %add_bitcast_fusion.1 = f32[1,2048,512]{2,1,0:T(8,128)} fusion(bf16[2560,2048]{1,0:T(8,128)(2,1)} %get-tuple-element.266, bf16[2560,512]{1,0:T(8,128)(2,1)S(1)} %copy-done.62, bf16[512,512]{1,0:T(8,128)(2,1)S(1)} %collective-permute-done.86, bf16[512,512]{1,0:T(8,128)(2,1)S(1)} %collective-permute-done.85, bf16[1024,512]{1,0:T(8,128)(2,1)S(1)} %copy-done.79), kind=kOutput, calls=%fused_computation.2 | convolution fusion | flops 5376049152 | bytes 19398656 | tf_op jit(solution)/shard_map/dot_general | solution.py:139
  680.1 8.5 %add_bitcast_fusion = f32[1,512,2048]{2,1,0:T(8,128)} fusion(bf16[512,2048]{1,0:T(8,128)(2,1)} %collective-permute-done.50, bf16[2560,512]{1,0:T(8,128)(2,1)S(1)} %copy-done.5, bf16[2560,2048]{1,0:T(8,128)(2,1)S(1)} %bitcast.101), kind=kOutput, calls=%fused_computation.1 | convolution fusion | flops 5370806272 | bytes 19398656 | tf_op jit(solution)/shard_map/dot_general | solution.py:139
  690.4 2.6 fusion.2
  698.0 16.6 %collective-permute-done.74 = f32[8,4,128]{2,1,0:T(4,128)S(1)} collective-permute-done((f32[8,4,128]{2,1,0:T(4,128)S(1)}, f32[8,4,128]{2,1,0:T(4,128)S(1)}, u32[]{:S(2)}, u32[]{:S(2)}) %collective-permute-start.74) | collective-permute-done | bytes 16416 | tf_op jit(solution)/shard_map/ppermute | solution.py:21
  719.1 2.8 collective-permute-start.76
  721.9 8.3 %add_bitcast_fusion.2 = f32[1,2048,512]{2,1,0:T(8,128)} fusion(bf16[2560,2048]{1,0:T(8,128)(2,1)S(1)} %bitcast.127, bf16[2560,512]{1,0:T(8,128)(2,1)S(1)} %copy-done.60, bf16[1024,512]{1,0:T(8,128)(2,1)S(1)} %copy-done.78, bf16[1024,512]{1,0:T(8,128)(2,1)S(1)} %copy-done.102), kind=kOutput, calls=%fused_computation.3 | convolution fusion | flops 5373952000 | bytes 19398656 | tf_op jit(solution)/shard_map/dot_general | solution.py:139
  730.4 2.4 fusion.8
  735.5 7.1 collective-permute-done.78
  (499 shorter events, 171.8 us)
Async XLA Ops:
  7.2 132.6 %all-gather.5.cloned.1.call-start = ((), (), s32[]{:S(2)}) async-start(), calls=%async_computation.2 | async-start | bytes 25067520 | tf_op jit(solution)/shard_map/all_gather | solution.py:950
  15.8 213.3 %all-gather.7.cloned.1.call-start = ((), (), s32[]{:S(2)}) async-start(), calls=%async_computation.3 | async-start | bytes 4456448 | tf_op jit(solution)/shard_map/all_gather | solution.py:951
  16.5 601.3 %reduce-scatter.2.cloned.1.call-start = ((), (), s32[]{:S(2)}) async-start(), calls=%async_computation.1 | async-start | bytes 11141120 | tf_op jit(solution)/shard_map/reduce_scatter | solution.py:1076
  16.6 49.6 %collective-permute-start = (bf16[2048,512]{1,0:T(8,128)(2,1)S(1)}, bf16[2048,512]{1,0:T(8,128)(2,1)}, u32[]{:S(2)}, u32[]{:S(2)}) collective-permute-start(bf16[2048,512]{1,0:T(8,128)(2,1)S(1)} %bitcast.133), channel_id=1, source_target_pairs={{0,1},{1,0},{2,3},{3,2},{4,5},{5,4},{6,7},{7,6},{8,9},{9,8},{10,11... | collective-permute-start | bytes 6291464 | tf_op jit(solution)/shard_map/ppermute | solution.py:25
  19.6 90.7 %collective-permute-start.1 = (bf16[2048,512]{1,0:T(8,128)(2,1)}, bf16[2048,512]{1,0:T(8,128)(2,1)}, u32[]{:S(2)}, u32[]{:S(2)}) collective-permute-start(bf16[2048,512]{1,0:T(8,128)(2,1)} %bitcast.134), channel_id=1, source_target_pairs={{0,1},{1,0},{2,3},{3,2},{4,5},{5,4},{6,7},{7,6},{8,9},{9,8},{10,11... | collective-permute-start | bytes 6291464 | tf_op jit(solution)/shard_map/ppermute | solution.py:25
  159.4 75.3 %collective-permute-start.16 = (bf16[512,2048]{1,0:T(8,128)(2,1)S(1)}, bf16[512,2048]{1,0:T(8,128)(2,1)}, u32[]{:S(2)}, u32[]{:S(2)}) collective-permute-start(bf16[512,2048]{1,0:T(8,128)(2,1)S(1)} %bitcast.107), channel_id=1, source_target_pairs={{0,1},{1,0},{2,3},{3,2},{4,5},{5,4},{6,7},{7,6},{8,9},{9,8},{10,11... | collective-permute-start | bytes 6291464 | tf_op jit(solution)/shard_map/ppermute | solution.py:25
  168.7 16.2 %collective-permute-start.5 = (bf16[128,1024]{1,0:T(8,128)(2,1)}, bf16[128,1024]{1,0:T(8,128)(2,1)}, u32[]{:S(2)}, u32[]{:S(2)}) collective-permute-start(bf16[128,1024]{1,0:T(8,128)(2,1)} %slice.263), channel_id=1, source_target_pairs={{0,8},{2,10},{4,12},{6,14},{8,0},{10,2},{12,4},{14,6},{16,24},{18,... | collective-permute-start | bytes 786440 | tf_op jit(solution)/shard_map/ppermute | solution.py:21
  170.2 15.1 %collective-permute-start.3 = (bf16[128,1024]{1,0:T(8,128)(2,1)}, bf16[128,1024]{1,0:T(8,128)(2,1)}, u32[]{:S(2)}, u32[]{:S(2)}) collective-permute-start(bf16[128,1024]{1,0:T(8,128)(2,1)} %slice.263), channel_id=1, source_target_pairs={{0,4},{2,6},{4,0},{6,2},{8,12},{10,14},{12,8},{14,10},{16,20},{18,... | collective-permute-start | bytes 786440 | tf_op jit(solution)/shard_map/ppermute | solution.py:21
  173.7 12.9 %collective-permute-start.2 = (bf16[128,1024]{1,0:T(8,128)(2,1)}, bf16[128,1024]{1,0:T(8,128)(2,1)}, u32[]{:S(2)}, u32[]{:S(2)}) collective-permute-start(bf16[128,1024]{1,0:T(8,128)(2,1)} %slice.263), channel_id=1, source_target_pairs={{0,2},{2,0},{4,6},{6,4},{8,10},{10,8},{12,14},{14,12},{16,18},{18,... | collective-permute-start | bytes 786440 | tf_op jit(solution)/shard_map/ppermute | solution.py:21
  173.7 21.0 %collective-permute-start.10 = (bf16[128,1024]{1,0:T(8,128)(2,1)}, bf16[128,1024]{1,0:T(8,128)(2,1)}, u32[]{:S(2)}, u32[]{:S(2)}) collective-permute-start(bf16[128,1024]{1,0:T(8,128)(2,1)} %slice.203), channel_id=1, source_target_pairs={{0,4},{2,6},{4,0},{6,2},{8,12},{10,14},{12,8},{14,10},{16,20},{18,... | collective-permute-start | bytes 786440 | tf_op jit(solution)/shard_map/ppermute | solution.py:21
  186.6 12.9 %collective-permute-start.7 = (bf16[128,1024]{1,0:T(8,128)(2,1)}, bf16[128,1024]{1,0:T(8,128)(2,1)}, u32[]{:S(2)}, u32[]{:S(2)}) collective-permute-start(bf16[128,1024]{1,0:T(8,128)(2,1)} %collective-permute-done.5.refs_3_), channel_id=1, source_target_pairs={{0,4},{2,6},{4,0},{6,2},{8,12},{10,14},{12,8},{14,10},{16,20},{18,... | collective-permute-start | bytes 786440 | tf_op jit(solution)/shard_map/ppermute | solution.py:21
  195.2 12.2 %collective-permute-start.14 = (bf16[128,1024]{1,0:T(8,128)(2,1)}, bf16[128,1024]{1,0:T(8,128)(2,1)}, u32[]{:S(2)}, u32[]{:S(2)}) collective-permute-start(bf16[128,1024]{1,0:T(8,128)(2,1)} %collective-permute-done.10.refs_8_), channel_id=1, source_target_pairs={{0,8},{2,10},{4,12},{6,14},{8,0},{10,2},{12,4},{14,6},{16,24},{18,... | collective-permute-start | bytes 786440 | tf_op jit(solution)/shard_map/ppermute | solution.py:21
  234.8 16.8 %collective-permute-start.17 = (bf16[160,2048]{1,0:T(8,128)(2,1)S(1)}, bf16[160,2048]{1,0:T(8,128)(2,1)S(1)}, u32[]{:S(2)}, u32[]{:S(2)}) collective-permute-start(bf16[160,2048]{1,0:T(8,128)(2,1)S(1)} %dynamic-slice_convert_fusion.1), channel_id=1, source_target_pairs={{0,1},{1,0},{2,3},{3,2},{4,5},{5,4},{6,7},{7,6},{8,9},{9,8},{10,11... | collective-permute-start | bytes 1966088 | tf_op jit(solution)/shard_map/ppermute | solution.py:25
  257.3 16.8 %collective-permute-start.20 = (bf16[160,2048]{1,0:T(8,128)(2,1)S(1)}, bf16[160,2048]{1,0:T(8,128)(2,1)S(1)}, u32[]{:S(2)}, u32[]{:S(2)}) collective-permute-start(bf16[160,2048]{1,0:T(8,128)(2,1)S(1)} %multiply_convert_fusion.1.refs_1_), channel_id=1, source_target_pairs={{0,8},{2,10},{8,16},{10,18},{16,24},{18,26},{24,28},{26,30},{28,20... | collective-permute-start | bytes 1966088 | tf_op jit(solution)/shard_map/ppermute | solution.py:37
  257.7 19.2 %collective-permute-start.21 = (bf16[160,2048]{1,0:T(8,128)(2,1)S(1)}, bf16[160,2048]{1,0:T(8,128)(2,1)}, u32[]{:S(2)}, u32[]{:S(2)}) collective-permute-start(bf16[160,2048]{1,0:T(8,128)(2,1)S(1)} %multiply_convert_fusion.1.refs_1_), channel_id=1, source_target_pairs={{8,0},{10,2},{16,8},{18,10},{24,16},{26,18},{28,24},{30,26},{20,28... | collective-permute-start | bytes 1966088 | tf_op jit(solution)/shard_map/ppermute | solution.py:41
  277.4 25.1 %collective-permute-start.23 = (bf16[160,2048]{1,0:T(8,128)(2,1)S(1)}, bf16[160,2048]{1,0:T(8,128)(2,1)S(1)}, u32[]{:S(2)}, u32[]{:S(2)}) collective-permute-start(bf16[160,2048]{1,0:T(8,128)(2,1)S(1)} %collective-permute-done.20.refs_1_), channel_id=1, source_target_pairs={{0,8},{2,10},{8,16},{10,18},{16,24},{18,26},{24,28},{26,30},{28,20... | collective-permute-start | bytes 1966088 | tf_op jit(solution)/shard_map/ppermute | solution.py:37
  279.1 23.4 %collective-permute-start.24 = (bf16[160,2048]{1,0:T(8,128)(2,1)}, bf16[160,2048]{1,0:T(8,128)(2,1)S(1)}, u32[]{:S(2)}, u32[]{:S(2)}) collective-permute-start(bf16[160,2048]{1,0:T(8,128)(2,1)} %collective-permute-done.21.refs_3_), channel_id=1, source_target_pairs={{8,0},{10,2},{16,8},{18,10},{24,16},{26,18},{28,24},{30,26},{20,28... | collective-permute-start | bytes 1966088 | tf_op jit(solution)/shard_map/ppermute | solution.py:41
  303.1 31.3 %collective-permute-start.33 = (f32[160,2048]{1,0:T(8,128)}, f32[160,2048]{1,0:T(8,128)}, u32[]{:S(2)}, u32[]{:S(2)}) collective-permute-start(f32[160,2048]{1,0:T(8,128)} %get-tuple-element.193), channel_id=1, source_target_pairs={{0,1},{1,0},{2,3},{3,2},{4,5},{5,4},{6,7},{7,6},{8,9},{9,8},{10,11... | collective-permute-start | bytes 3932168 | tf_op jit(solution)/shard_map/ppermute | solution.py:25
  303.4 25.7 %collective-permute-start.28 = (bf16[160,2048]{1,0:T(8,128)(2,1)S(1)}, bf16[160,2048]{1,0:T(8,128)(2,1)S(1)}, u32[]{:S(2)}, u32[]{:S(2)}) collective-permute-start(bf16[160,2048]{1,0:T(8,128)(2,1)S(1)} %collective-permute-done.23.refs_1_), channel_id=1, source_target_pairs={{0,8},{2,10},{8,16},{10,18},{16,24},{18,26},{24,28},{26,30},{28,20... | collective-permute-start | bytes 1966088 | tf_op jit(solution)/shard_map/ppermute | solution.py:37
  305.1 24.0 %collective-permute-start.29 = (bf16[160,2048]{1,0:T(8,128)(2,1)S(1)}, bf16[160,2048]{1,0:T(8,128)(2,1)S(1)}, u32[]{:S(2)}, u32[]{:S(2)}) collective-permute-start(bf16[160,2048]{1,0:T(8,128)(2,1)S(1)} %collective-permute-done.24.refs_3_), channel_id=1, source_target_pairs={{8,0},{10,2},{16,8},{18,10},{24,16},{26,18},{28,24},{30,26},{20,28... | collective-permute-start | bytes 1966088 | tf_op jit(solution)/shard_map/ppermute | solution.py:41
  329.2 13.8 %collective-permute-start.34 = (bf16[160,2048]{1,0:T(8,128)(2,1)S(1)}, bf16[160,2048]{1,0:T(8,128)(2,1)S(1)}, u32[]{:S(2)}, u32[]{:S(2)}) collective-permute-start(bf16[160,2048]{1,0:T(8,128)(2,1)S(1)} %collective-permute-done.28.refs_1_), channel_id=1, source_target_pairs={{0,2},{2,0},{4,6},{6,4},{8,10},{10,8},{12,14},{14,12},{16,18},{18,... | collective-permute-start | bytes 1966088 | tf_op jit(solution)/shard_map/ppermute | solution.py:21
  329.2 14.3 %collective-permute-start.35 = (bf16[160,2048]{1,0:T(8,128)(2,1)S(1)}, bf16[160,2048]{1,0:T(8,128)(2,1)S(1)}, u32[]{:S(2)}, u32[]{:S(2)}) collective-permute-start(bf16[160,2048]{1,0:T(8,128)(2,1)S(1)} %collective-permute-done.29.refs_3_), channel_id=1, source_target_pairs={{0,2},{2,0},{4,6},{6,4},{8,10},{10,8},{12,14},{14,12},{16,18},{18,... | collective-permute-start | bytes 1966088 | tf_op jit(solution)/shard_map/ppermute | solution.py:21
  334.4 127.5 %collective-permute-start.22 = (bf16[160,2048]{1,0:T(8,128)(2,1)}, bf16[160,2048]{1,0:T(8,128)(2,1)}, u32[]{:S(2)}, u32[]{:S(2)}) collective-permute-start(bf16[160,2048]{1,0:T(8,128)(2,1)} %copy-done.56), channel_id=1, source_target_pairs={{0,2},{2,0},{4,6},{6,4},{8,10},{10,8},{12,14},{14,12},{16,18},{18,... | collective-permute-start | bytes 1966088 | tf_op jit(solution)/shard_map/ppermute | solution.py:21
  340.3 55.7 %collective-permute-start.27 = (bf16[320,2048]{1,0:T(8,128)(2,1)}, bf16[320,2048]{1,0:T(8,128)(2,1)}, u32[]{:S(2)}, u32[]{:S(2)}) collective-permute-start(bf16[320,2048]{1,0:T(8,128)(2,1)} %get-tuple-element.179), channel_id=1, source_target_pairs={{0,2},{2,0},{4,6},{6,4},{8,10},{10,8},{12,14},{14,12},{16,18},{18,... | collective-permute-start | bytes 3932168 | tf_op jit(solution)/shard_map/ppermute | solution.py:21
  343.0 58.6 %collective-permute-start.32 = (bf16[320,2048]{1,0:T(8,128)(2,1)}, bf16[320,2048]{1,0:T(8,128)(2,1)}, u32[]{:S(2)}, u32[]{:S(2)}) collective-permute-start(bf16[320,2048]{1,0:T(8,128)(2,1)} %get-tuple-element.191), channel_id=1, source_target_pairs={{0,2},{2,0},{4,6},{6,4},{8,10},{10,8},{12,14},{14,12},{16,18},{18,... | collective-permute-start | bytes 3932168 | tf_op jit(solution)/shard_map/ppermute | solution.py:21
  343.0 24.7 %collective-permute-start.39 = (bf16[80,2048]{1,0:T(8,128)(2,1)S(1)}, bf16[80,2048]{1,0:T(8,128)(2,1)S(1)}, u32[]{:S(2)}, u32[]{:S(2)}) collective-permute-start(bf16[80,2048]{1,0:T(8,128)(2,1)S(1)} %collective-permute-done.37.refs_1_), channel_id=1, source_target_pairs={{0,2},{2,0},{4,6},{6,4},{8,10},{10,8},{12,14},{14,12},{16,18},{18,... | collective-permute-start | bytes 983048 | tf_op jit(solution)/shard_map/ppermute | solution.py:21
  343.5 24.9 %collective-permute-start.40 = (bf16[80,2048]{1,0:T(8,128)(2,1)S(1)}, bf16[80,2048]{1,0:T(8,128)(2,1)S(1)}, u32[]{:S(2)}, u32[]{:S(2)}) collective-permute-start(bf16[80,2048]{1,0:T(8,128)(2,1)S(1)} %collective-permute-done.38.refs_2_), channel_id=1, source_target_pairs={{0,2},{2,0},{4,6},{6,4},{8,10},{10,8},{12,14},{14,12},{16,18},{18,... | collective-permute-start | bytes 983048 | tf_op jit(solution)/shard_map/ppermute | solution.py:21
  386.7 12.8 %collective-permute-start.41 = (bf16[160,2048]{1,0:T(8,128)(2,1)S(1)}, bf16[160,2048]{1,0:T(8,128)(2,1)S(1)}, u32[]{:S(2)}, u32[]{:S(2)}) collective-permute-start(bf16[160,2048]{1,0:T(8,128)(2,1)S(1)} %get-tuple-element.213), channel_id=1, source_target_pairs={{0,2},{2,0},{4,6},{6,4},{8,10},{10,8},{12,14},{14,12},{16,18},{18,... | collective-permute-start | bytes 1966088 | tf_op jit(solution)/shard_map/ppermute | solution.py:21
  387.2 23.8 %collective-permute-start.36 = (bf16[320,2048]{1,0:T(8,128)(2,1)}, bf16[320,2048]{1,0:T(8,128)(2,1)S(1)}, u32[]{:S(2)}, u32[]{:S(2)}) collective-permute-start(bf16[320,2048]{1,0:T(8,128)(2,1)} %get-tuple-element.204), channel_id=1, source_target_pairs={{0,2},{2,0},{4,6},{6,4},{8,10},{10,8},{12,14},{14,12},{16,18},{18,... | collective-permute-start | bytes 3932168 | tf_op jit(solution)/shard_map/ppermute | solution.py:21
  396.0 71.6 %collective-permute-start.50 = (bf16[512,2048]{1,0:T(8,128)(2,1)}, bf16[512,2048]{1,0:T(8,128)(2,1)}, u32[]{:S(2)}, u32[]{:S(2)}) collective-permute-start(bf16[512,2048]{1,0:T(8,128)(2,1)} %convolution_convert_fusion.2), channel_id=1, source_target_pairs={{0,1},{1,0},{2,3},{3,2},{4,5},{5,4},{6,7},{7,6},{8,9},{9,8},{10,11... | collective-permute-start | bytes 6291464 | tf_op jit(solution)/shard_map/ppermute | solution.py:25
  399.8 11.8 %collective-permute-start.42 = (bf16[80,2048]{1,0:T(8,128)(2,1)S(1)}, bf16[80,2048]{1,0:T(8,128)(2,1)S(1)}, u32[]{:S(2)}, u32[]{:S(2)}) collective-permute-start(bf16[80,2048]{1,0:T(8,128)(2,1)S(1)} %get-tuple-element.369), channel_id=1, source_target_pairs={{0,8},{2,10},{8,16},{10,18},{16,24},{18,26},{24,28},{26,30},{28,20... | collective-permute-start | bytes 983048 | tf_op jit(solution)/shard_map/ppermute | solution.py:37
  411.9 15.8 %collective-permute-start.47 = (bf16[160,2048]{1,0:T(8,128)(2,1)S(1)}, bf16[160,2048]{1,0:T(8,128)(2,1)S(1)}, u32[]{:S(2)}, u32[]{:S(2)}) collective-permute-start(bf16[160,2048]{1,0:T(8,128)(2,1)S(1)} %pad_maximum_fusion.8), channel_id=1, source_target_pairs={{8,0},{10,2},{16,8},{18,10},{24,16},{26,18},{28,24},{30,26},{20,28... | collective-permute-start | bytes 1966088 | tf_op jit(solution)/shard_map/ppermute | solution.py:41
  412.3 15.5 %collective-permute-start.43 = (bf16[160,2048]{1,0:T(8,128)(2,1)S(1)}, bf16[160,2048]{1,0:T(8,128)(2,1)S(1)}, u32[]{:S(2)}, u32[]{:S(2)}) collective-permute-start(bf16[160,2048]{1,0:T(8,128)(2,1)S(1)} %pad_maximum_fusion.7), channel_id=1, source_target_pairs={{0,8},{2,10},{8,16},{10,18},{16,24},{18,26},{24,28},{26,30},{28,20... | collective-permute-start | bytes 1966088 | tf_op jit(solution)/shard_map/ppermute | solution.py:37
  421.5 45.1 %collective-permute-start.51 = (bf16[1024,512]{1,0:T(8,128)(2,1)S(1)}, bf16[1024,512]{1,0:T(8,128)(2,1)S(1)}, u32[]{:S(2)}, u32[]{:S(2)}) collective-permute-start(bf16[1024,512]{1,0:T(8,128)(2,1)S(1)} %slice.275), channel_id=1, source_target_pairs={{0,1},{1,0},{2,3},{3,2},{4,5},{5,4},{6,7},{7,6},{8,9},{9,8},{10,11... | collective-permute-start | bytes 3145736 | tf_op jit(solution)/shard_map/ppermute | solution.py:25
  428.4 14.9 %collective-permute-start.48 = (bf16[160,2048]{1,0:T(8,128)(2,1)S(1)}, bf16[160,2048]{1,0:T(8,128)(2,1)S(1)}, u32[]{:S(2)}, u32[]{:S(2)}) collective-permute-start(bf16[160,2048]{1,0:T(8,128)(2,1)S(1)} %get-tuple-element.354), channel_id=1, source_target_pairs={{8,0},{10,2},{16,8},{18,10},{24,16},{26,18},{28,24},{30,26},{20,28... | collective-permute-start | bytes 1966088 | tf_op jit(solution)/shard_map/ppermute | solution.py:41
  428.7 14.6 %collective-permute-start.44 = (bf16[160,2048]{1,0:T(8,128)(2,1)S(1)}, bf16[160,2048]{1,0:T(8,128)(2,1)S(1)}, u32[]{:S(2)}, u32[]{:S(2)}) collective-permute-start(bf16[160,2048]{1,0:T(8,128)(2,1)S(1)} %get-tuple-element.353), channel_id=1, source_target_pairs={{0,8},{2,10},{8,16},{10,18},{16,24},{18,26},{24,28},{26,30},{28,20... | collective-permute-start | bytes 1966088 | tf_op jit(solution)/shard_map/ppermute | solution.py:37
  443.8 18.1 %collective-permute-start.45 = (bf16[160,2048]{1,0:T(8,128)(2,1)S(1)}, bf16[160,2048]{1,0:T(8,128)(2,1)S(1)}, u32[]{:S(2)}, u32[]{:S(2)}) collective-permute-start(bf16[160,2048]{1,0:T(8,128)(2,1)S(1)} %get-tuple-element.351), channel_id=1, source_target_pairs={{0,8},{2,10},{8,16},{10,18},{16,24},{18,26},{24,28},{26,30},{28,20... | collective-permute-start | bytes 1966088 | tf_op jit(solution)/shard_map/ppermute | solution.py:37
  445.5 16.4 %collective-permute-start.49 = (bf16[160,2048]{1,0:T(8,128)(2,1)S(1)}, bf16[160,2048]{1,0:T(8,128)(2,1)S(1)}, u32[]{:S(2)}, u32[]{:S(2)}) collective-permute-start(bf16[160,2048]{1,0:T(8,128)(2,1)S(1)} %get-tuple-element.352), channel_id=1, source_target_pairs={{8,0},{10,2},{16,8},{18,10},{24,16},{26,18},{28,24},{30,26},{20,28... | collective-permute-start | bytes 1966088 | tf_op jit(solution)/shard_map/ppermute | solution.py:41
  474.1 16.0 %collective-permute-start.52 = (bf16[160,2048]{1,0:T(8,128)(2,1)S(1)}, bf16[160,2048]{1,0:T(8,128)(2,1)}, u32[]{:S(2)}, u32[]{:S(2)}) collective-permute-start(bf16[160,2048]{1,0:T(8,128)(2,1)S(1)} %get-tuple-element.323), channel_id=1, source_target_pairs={{0,1},{1,0},{2,3},{3,2},{4,5},{5,4},{6,7},{7,6},{8,9},{9,8},{10,11... | collective-permute-start | bytes 1966088 | tf_op jit(solution)/shard_map/ppermute | solution.py:25
  495.3 12.3 %collective-permute-start.54 = (bf16[512,512]{1,0:T(8,128)(2,1)S(1)}, bf16[512,512]{1,0:T(8,128)(2,1)S(1)}, u32[]{:S(2)}, u32[]{:S(2)}) collective-permute-start(bf16[512,512]{1,0:T(8,128)(2,1)S(1)} %get-tuple-element.228), channel_id=1, source_target_pairs={{0,1},{1,0},{2,3},{3,2},{4,5},{5,4},{6,7},{7,6},{8,9},{9,8},{10,11... | collective-permute-start | bytes 1572872 | tf_op jit(solution)/shard_map/ppermute | solution.py:25
  507.5 23.6 %collective-permute-start.55 = (bf16[512,512]{1,0:T(8,128)(2,1)S(1)}, bf16[512,512]{1,0:T(8,128)(2,1)}, u32[]{:S(2)}, u32[]{:S(2)}) collective-permute-start(bf16[512,512]{1,0:T(8,128)(2,1)S(1)} %get-tuple-element.229), channel_id=1, source_target_pairs={{0,1},{1,0},{2,3},{3,2},{4,5},{5,4},{6,7},{7,6},{8,9},{9,8},{10,11... | collective-permute-start | bytes 1572872 | tf_op jit(solution)/shard_map/ppermute | solution.py:25
  531.1 14.6 %collective-permute-start.56 = (bf16[512,512]{1,0:T(8,128)(2,1)}, bf16[512,512]{1,0:T(8,128)(2,1)}, u32[]{:S(2)}, u32[]{:S(2)}) collective-permute-start(bf16[512,512]{1,0:T(8,128)(2,1)} %get-tuple-element.231), channel_id=1, source_target_pairs={{0,1},{1,0},{2,3},{3,2},{4,5},{5,4},{6,7},{7,6},{8,9},{9,8},{10,11... | collective-permute-start | bytes 1572872 | tf_op jit(solution)/shard_map/ppermute | solution.py:25
  536.0 18.9 %collective-permute-start.63 = (bf16[2,128,1024]{2,1,0:T(8,128)(2,1)}, bf16[2,128,1024]{2,1,0:T(8,128)(2,1)S(1)}, u32[]{:S(2)}, u32[]{:S(2)}) collective-permute-start(bf16[2,128,1024]{2,1,0:T(8,128)(2,1)} %get-tuple-element.242), channel_id=1, source_target_pairs={{0,8},{2,10},{4,12},{6,14},{8,0},{10,2},{12,4},{14,6},{16,24},{18,... | collective-permute-start | bytes 1572872 | tf_op jit(solution)/shard_map/ppermute | solution.py:21
  537.9 25.1 %collective-permute-start.62 = (bf16[2,128,1024]{2,1,0:T(8,128)(2,1)}, bf16[2,128,1024]{2,1,0:T(8,128)(2,1)S(1)}, u32[]{:S(2)}, u32[]{:S(2)}) collective-permute-start(bf16[2,128,1024]{2,1,0:T(8,128)(2,1)} %get-tuple-element.241), channel_id=1, source_target_pairs={{0,4},{2,6},{4,0},{6,2},{8,12},{10,14},{12,8},{14,10},{16,20},{18,... | collective-permute-start | bytes 1572872 | tf_op jit(solution)/shard_map/ppermute | solution.py:21
  537.9 27.1 %collective-permute-start.58 = (bf16[2,128,1024]{2,1,0:T(8,128)(2,1)}, bf16[2,128,1024]{2,1,0:T(8,128)(2,1)}, u32[]{:S(2)}, u32[]{:S(2)}) collective-permute-start(bf16[2,128,1024]{2,1,0:T(8,128)(2,1)} %get-tuple-element.236), channel_id=1, source_target_pairs={{0,2},{2,0},{4,6},{6,4},{8,10},{10,8},{12,14},{14,12},{16,18},{18,... | collective-permute-start | bytes 1572872 | tf_op jit(solution)/shard_map/ppermute | solution.py:21
  545.7 32.8 %collective-permute-start.57 = (bf16[512,512]{1,0:T(8,128)(2,1)}, bf16[512,512]{1,0:T(8,128)(2,1)}, u32[]{:S(2)}, u32[]{:S(2)}) collective-permute-start(bf16[512,512]{1,0:T(8,128)(2,1)} %get-tuple-element.232), channel_id=1, source_target_pairs={{0,1},{1,0},{2,3},{3,2},{4,5},{5,4},{6,7},{7,6},{8,9},{9,8},{10,11... | collective-permute-start | bytes 1572872 | tf_op jit(solution)/shard_map/ppermute | solution.py:25
  556.1 12.3 %collective-permute-start.65 = (bf16[128,1024]{1,0:T(8,128)(2,1)S(1)}, bf16[128,1024]{1,0:T(8,128)(2,1)S(1)}, u32[]{:S(2)}, u32[]{:S(2)}) collective-permute-start(bf16[128,1024]{1,0:T(8,128)(2,1)S(1)} %fusion.9), channel_id=1, source_target_pairs={{0,4},{2,6},{4,0},{6,2},{8,12},{10,14},{12,8},{14,10},{16,20},{18,... | collective-permute-start | bytes 786440 | tf_op jit(solution)/shard_map/ppermute | solution.py:21
  565.0 34.3 %collective-permute-start.18 = (bf16[320,2048]{1,0:T(8,128)(2,1)}, bf16[320,2048]{1,0:T(8,128)(2,1)}, u32[]{:S(2)}, u32[]{:S(2)}) collective-permute-start(bf16[320,2048]{1,0:T(8,128)(2,1)} %copy-done.14), channel_id=1, source_target_pairs={{0,2},{2,0},{4,6},{6,4},{8,10},{10,8},{12,14},{14,12},{16,18},{18,... | collective-permute-start | bytes 3932168 | tf_op jit(solution)/shard_map/ppermute | solution.py:21
  565.1 34.3 %collective-permute-start.53 = (bf16[320,2048]{1,0:T(8,128)(2,1)}, bf16[320,2048]{1,0:T(8,128)(2,1)}, u32[]{:S(2)}, u32[]{:S(2)}) collective-permute-start(bf16[320,2048]{1,0:T(8,128)(2,1)} %copy-done.12), channel_id=1, source_target_pairs={{0,2},{2,0},{4,6},{6,4},{8,10},{10,8},{12,14},{14,12},{16,18},{18,... | collective-permute-start | bytes 3932168 | tf_op jit(solution)/shard_map/ppermute | solution.py:21
  622.4 14.3 %collective-permute-start.69 = (bf16[256,1024]{1,0:T(8,128)(2,1)}, bf16[256,1024]{1,0:T(8,128)(2,1)}, u32[]{:S(2)}, u32[]{:S(2)}) collective-permute-start(bf16[256,1024]{1,0:T(8,128)(2,1)} %get-tuple-element.368), channel_id=1, source_target_pairs={{8,0},{10,2},{16,8},{18,10},{24,16},{26,18},{28,24},{30,26},{20,28... | collective-permute-start | bytes 1572872 | tf_op jit(solution)/shard_map/ppermute | solution.py:41
  623.9 15.7 %collective-permute-start.79 = (bf16[256,1024]{1,0:T(8,128)(2,1)}, bf16[256,1024]{1,0:T(8,128)(2,1)S(1)}, u32[]{:S(2)}, u32[]{:S(2)}) collective-permute-start(bf16[256,1024]{1,0:T(8,128)(2,1)} %get-tuple-element.367), channel_id=1, source_target_pairs={{0,8},{2,10},{8,16},{10,18},{16,24},{18,26},{24,28},{26,30},{28,20... | collective-permute-start | bytes 1572872 | tf_op jit(solution)/shard_map/ppermute | solution.py:37
  624.4 16.2 %collective-permute-start.85 = (bf16[512,512]{1,0:T(8,128)(2,1)}, bf16[512,512]{1,0:T(8,128)(2,1)S(1)}, u32[]{:S(2)}, u32[]{:S(2)}) collective-permute-start(bf16[512,512]{1,0:T(8,128)(2,1)} %get-tuple-element.269), channel_id=1, source_target_pairs={{0,1},{1,0},{2,3},{3,2},{4,5},{5,4},{6,7},{7,6},{8,9},{9,8},{10,11... | collective-permute-start | bytes 1572872 | tf_op jit(solution)/shard_map/ppermute | solution.py:25
  638.1 24.4 %collective-permute-start.70 = (bf16[256,2048]{1,0:T(8,128)(2,1)S(1)}, bf16[256,2048]{1,0:T(8,128)(2,1)S(1)}, u32[]{:S(2)}, u32[]{:S(2)}) collective-permute-start(bf16[256,2048]{1,0:T(8,128)(2,1)S(1)} %pad_maximum_fusion.5), channel_id=1, source_target_pairs={{8,0},{10,2},{16,8},{18,10},{24,16},{26,18},{28,24},{30,26},{20,28... | collective-permute-start | bytes 3145736 | tf_op jit(solution)/shard_map/ppermute | solution.py:41
  639.9 24.1 %collective-permute-start.80 = (bf16[256,2048]{1,0:T(8,128)(2,1)S(1)}, bf16[256,2048]{1,0:T(8,128)(2,1)S(1)}, u32[]{:S(2)}, u32[]{:S(2)}) collective-permute-start(bf16[256,2048]{1,0:T(8,128)(2,1)S(1)} %pad_maximum_fusion.6), channel_id=1, source_target_pairs={{0,8},{2,10},{8,16},{10,18},{16,24},{18,26},{24,28},{26,30},{28,20... | collective-permute-start | bytes 3145736 | tf_op jit(solution)/shard_map/ppermute | solution.py:37
  640.6 28.0 %collective-permute-start.86 = (bf16[512,512]{1,0:T(8,128)(2,1)S(1)}, bf16[512,512]{1,0:T(8,128)(2,1)S(1)}, u32[]{:S(2)}, u32[]{:S(2)}) collective-permute-start(bf16[512,512]{1,0:T(8,128)(2,1)S(1)} %copy-done.82), channel_id=1, source_target_pairs={{0,1},{1,0},{2,3},{3,2},{4,5},{5,4},{6,7},{7,6},{8,9},{9,8},{10,11... | collective-permute-start | bytes 1572872 | tf_op jit(solution)/shard_map/ppermute | solution.py:25
  642.8 87.4 %collective-permute-start.68 = (bf16[160,2048]{1,0:T(8,128)(2,1)}, bf16[160,2048]{1,0:T(8,128)(2,1)}, u32[]{:S(2)}, u32[]{:S(2)}) collective-permute-start(bf16[160,2048]{1,0:T(8,128)(2,1)} %reduce-scatter.2.cloned.1.call-done), channel_id=1, source_target_pairs={{0,1},{1,0},{2,3},{3,2},{4,5},{5,4},{6,7},{7,6},{8,9},{9,8},{10,11... | collective-permute-start | bytes 1966088 | tf_op jit(solution)/shard_map/ppermute | solution.py:25
  650.7 43.9 %collective-permute-start.72 = (bf16[160,2048]{1,0:T(8,128)(2,1)S(1)}, bf16[160,2048]{1,0:T(8,128)(2,1)S(1)}, u32[]{:S(2)}, u32[]{:S(2)}) collective-permute-start(bf16[160,2048]{1,0:T(8,128)(2,1)S(1)} %dynamic-slice_convert_fusion), channel_id=1, source_target_pairs={{0,1},{1,0},{2,3},{3,2},{4,5},{5,4},{6,7},{7,6},{8,9},{9,8},{10,11... | collective-permute-start | bytes 1966088 | tf_op jit(solution)/shard_map/ppermute | solution.py:25
  666.5 23.3 %collective-permute-start.71 = (bf16[256,2048]{1,0:T(8,128)(2,1)S(1)}, bf16[256,2048]{1,0:T(8,128)(2,1)S(1)}, u32[]{:S(2)}, u32[]{:S(2)}) collective-permute-start(bf16[256,2048]{1,0:T(8,128)(2,1)S(1)} %get-tuple-element.332), channel_id=1, source_target_pairs={{8,0},{10,2},{16,8},{18,10},{24,16},{26,18},{28,24},{30,26},{20,28... | collective-permute-start | bytes 3145736 | tf_op jit(solution)/shard_map/ppermute | solution.py:41
  667.1 23.3 %collective-permute-start.81 = (bf16[256,2048]{1,0:T(8,128)(2,1)S(1)}, bf16[256,2048]{1,0:T(8,128)(2,1)}, u32[]{:S(2)}, u32[]{:S(2)}) collective-permute-start(bf16[256,2048]{1,0:T(8,128)(2,1)S(1)} %get-tuple-element.331), channel_id=1, source_target_pairs={{0,8},{2,10},{8,16},{10,18},{16,24},{18,26},{24,28},{26,30},{28,20... | collective-permute-start | bytes 3145736 | tf_op jit(solution)/shard_map/ppermute | solution.py:37
  693.0 49.6 %collective-permute-start.82 = (bf16[256,2048]{1,0:T(8,128)(2,1)S(1)}, bf16[256,2048]{1,0:T(8,128)(2,1)S(1)}, u32[]{:S(2)}, u32[]{:S(2)}) collective-permute-start(bf16[256,2048]{1,0:T(8,128)(2,1)S(1)} %get-tuple-element.329), channel_id=1, source_target_pairs={{0,8},{2,10},{8,16},{10,18},{16,24},{18,26},{24,28},{26,30},{28,20... | collective-permute-start | bytes 3145736 | tf_op jit(solution)/shard_map/ppermute | solution.py:37
  695.3 19.4 %collective-permute-start.74 = (f32[8,4,128]{2,1,0:T(4,128)S(1)}, f32[8,4,128]{2,1,0:T(4,128)S(1)}, u32[]{:S(2)}, u32[]{:S(2)}) collective-permute-start(f32[8,4,128]{2,1,0:T(4,128)S(1)} %dynamic-slice_bitcast_fusion), channel_id=1, source_target_pairs={{0,16},{2,18},{4,20},{6,22},{8,24},{10,26},{12,28},{14,30},{16,0},... | collective-permute-start | bytes 49160 | tf_op jit(solution)/shard_map/ppermute | solution.py:21
  696.7 46.0 %collective-permute-start.83 = (bf16[256,2048]{1,0:T(8,128)(2,1)S(1)}, bf16[256,2048]{1,0:T(8,128)(2,1)S(1)}, u32[]{:S(2)}, u32[]{:S(2)}) collective-permute-start(bf16[256,2048]{1,0:T(8,128)(2,1)S(1)} %get-tuple-element.330), channel_id=1, source_target_pairs={{8,0},{10,2},{16,8},{18,10},{24,16},{26,18},{28,24},{30,26},{20,28... | collective-permute-start | bytes 3145736 | tf_op jit(solution)/shard_map/ppermute | solution.py:41
  716.0 29.1 %collective-permute-start.73 = (f32[160,2048]{1,0:T(8,128)S(1)}, f32[160,2048]{1,0:T(8,128)S(1)}, u32[]{:S(2)}, u32[]{:S(2)}) collective-permute-start(f32[160,2048]{1,0:T(8,128)S(1)} %fusion.6), channel_id=1, source_target_pairs={{0,1},{1,0},{2,3},{3,2},{4,5},{5,4},{6,7},{7,6},{8,9},{9,8},{10,11... | collective-permute-start | bytes 3932168 | tf_op jit(solution)/shard_map/ppermute | solution.py:25
  719.1 11.2 %collective-permute-start.76 = (f32[2,4,128]{2,1,0:T(4,128)S(1)}, f32[2,4,128]{2,1,0:T(4,128)S(1)}, u32[]{:S(2)}, u32[]{:S(2)}) collective-permute-start(f32[2,4,128]{2,1,0:T(4,128)S(1)} %constant_dynamic-slice_fusion.3), channel_id=1, source_target_pairs={{0,4},{2,6},{4,0},{6,2},{8,12},{10,14},{12,8},{14,10},{16,20},{18,... | collective-permute-start | bytes 12296 | tf_op jit(solution)/shard_map/ppermute | solution.py:21
  (138 other events, 1265.6 us)
Sparse Core Ops, SparseCore 0:
  15.9 123.8 all-gather.4
  142.5 63.4 all-gather.6
  467.8 130.6 reduce-scatter.1

commit v8 on v7

--- a/solution.py
+++ b/solution.py
@@ -12,6 +12,7 @@
 
 
 EPSILON = 1e-05
+VMEM = 60 * 1024 * 1024
 LOW = jnp.bfloat16
 FULL = jnp.float32
 
@@ -31,6 +32,13 @@
 ]
 BEHIND = [(to, at) for at, to in AHEAD]
 HOPS = (-1, 1, -2, 2, -3, 3, 0, 4)
+LAYOUT = (
+    *((-2, 0), (2, 0), (-1, 1), (1, 1)),
+    *((-3, 0), (3, 0), (-2, 1), (2, 1)),
+    *((4, 0), (4, 1), (-3, 1), (3, 1)),
+    *((0, 0), (0, 1)),
+    *((-1, 0), (1, 0)),
+)
 
 
 def ahead(block):
@@ -41,16 +49,16 @@
     return lax.ppermute(block, "dp", BEHIND)
 
 
+def ring_chips(dp_index, hops):
+    chip = dp_index // 2
+    place = jnp.where(chip % 2 == 0, chip // 2, 7 - chip // 2)
+    there = (place + jnp.array(hops, jnp.int32)) % len(RING)
+    return jnp.where(there < 4, 2 * there, 2 * (7 - there) + 1)
+
+
 def ring_blocks(dp_index):
-    chip, core = dp_index // 2, dp_index % 2
-    place = jnp.where(chip % 2 == 0, chip // 2, 7 - chip // 2)
-    steps, cross = [], []
-    for hop in HOPS:
-        steps += [hop, hop]
-        cross += [0, 1]
-    there = (place + jnp.array(steps, jnp.int32)) % 8
-    chips = jnp.where(there < 4, 2 * there, 2 * (7 - there) + 1)
-    return 2 * chips + (core ^ jnp.array(cross, jnp.int32))
+    chips = ring_chips(dp_index, [hop for hop, _ in LAYOUT])
+    return 2 * chips + (dp_index % 2 ^ jnp.array([cross for _, cross in LAYOUT], jnp.int32))
 
 
 def add_low(*parts):
@@ -74,7 +82,7 @@
 
     def next(self, token):
         if self.stages:
-            self.stages.pop(0)(lambda value: after(value, token))
+            return self.stages.pop(0)(lambda value: after(value, token), token)
 
 
 def ring_sum(same, cross, fillers):
@@ -82,28 +90,31 @@
     rows = both[0].shape[0]
     cut = rows // 2
     right, left = ahead(both[4][:cut]), behind(both[4][cut:])
-    fillers.next(left)
     outward, inward = both[3][rows:], both[3][:rows]
     right = jnp.concatenate([add_low(outward[:cut], right), outward[cut:]], axis=0)
     left = jnp.concatenate([inward[:cut], add_low(inward[cut:], left)], axis=0)
+    right, left = together(right, left)
+    fillers.next((right, left))
     right, left = ahead(right), behind(left)
-    fillers.next(left)
     for hop in (2, 1):
-        right = ahead(add_low(both[hop][rows:], right))
-        left = behind(add_low(both[hop][:rows], left))
-        fillers.next(left)
+        right, left = add_low(both[hop][rows:], right), add_low(both[hop][:rows], left)
+        right, left = together(right, left)
+        fillers.next((right, left))
+        right, left = ahead(right), behind(left)
     return both[0].astype(FULL) + right.astype(FULL) + left.astype(FULL)
 
 
-def swap_in_turn(arrays, pieces, token):
-    whole = []
-    for array in arrays:
-        rows, got = array.shape[0] // pieces, []
-        for i in range(pieces):
-            got.append(swap_tensor(after(array[i * rows : (i + 1) * rows], token)))
-            token = got[-1]
-        whole.append(jnp.concatenate(got, axis=0))
-    return whole
+def swap_in_turn(pieces, token):
+    got = []
+    for piece in pieces:
+        got.append(swap_tensor(after(piece, token)))
+        token = got[-1]
+    return got
+
+
+def cut_rows(array, count):
+    rows = array.shape[0] // count
+    return [array[i * rows : (i + 1) * rows] for i in range(count)]
 
 
 def rms_norm(values, gain):
@@ -263,7 +274,7 @@
         in_specs=attend_specs(rows, scale, cosine, sine, bias),
         out_specs=head_spec(rows),
         out_shape=jax.ShapeDtypeStruct((rows, width), LOW),
-        compiler_params=pltpu.CompilerParams(vmem_limit_bytes=40 * 1024 * 1024),
+        compiler_params=pltpu.CompilerParams(vmem_limit_bytes=VMEM),
     )(flat, gain, scale, cosine, sine, bias, keys, values, *pieces)
 
 
@@ -338,7 +349,7 @@
             jax.ShapeDtypeStruct((3, 2, PR_DEV, width), LOW),
         ]
         + [jax.ShapeDtypeStruct((2, PR_DEV, width), LOW)] * 4,
-        compiler_params=pltpu.CompilerParams(vmem_limit_bytes=58 * 1024 * 1024),
+        compiler_params=pltpu.CompilerParams(vmem_limit_bytes=VMEM),
         cost_estimate=pl.CostEstimate(
             flops=20 * 10**9, bytes_accessed=40 * 10**6, transcendentals=4 * 10**6
         ),
@@ -391,30 +402,20 @@
     )(key_grad, value_grad, flat, gain, scale, cosine, sine, *returned)
 
 
-def pack_kernel(query, key, value, rest, out, *refs):
-    packed, turned = refs[-2:]
+def pack_kernel(query, key, value, out, rest, packed):
     at = 0
-    for ref in (query, key, value, rest):
+    for ref in (query, key, value):
         packed[at : at + ref.shape[0]] = ref[...]
         at += ref.shape[0]
-    for back in refs[:-2]:
-        width = packed.shape[1]
-        for start in range(0, back.shape[1], width):
-            packed[at : at + back.shape[0]] = back[:, start : start + width].astype(LOW)
-            at += back.shape[0]
-    turned[...] = out[...].T
-
-
-def pack_weights(w_query, w_key, w_value, rest, w_out, back):
-    width = w_query.shape[1]
-    rows = 3 * w_query.shape[0] + rest.shape[0] + sum(b.size // width for b in back)
+    packed[at : at + out.shape[1]] = out[...].T
+    packed[at + out.shape[1] :] = rest[...]
+
+
+def pack_weights(w_query, w_key, w_value, w_out, rest):
+    rows = 4 * w_query.shape[0] + rest.shape[0]
     return pl.pallas_call(
-        pack_kernel,
-        out_shape=[
-            jax.ShapeDtypeStruct((rows, width), LOW),
-            jax.ShapeDtypeStruct(w_out.shape[::-1], LOW),
-        ],
-    )(w_query, w_key, w_value, rest, w_out, *back)
+        pack_kernel, out_shape=jax.ShapeDtypeStruct((rows, w_query.shape[1]), LOW)
+    )(w_query, w_key, w_value, w_out, rest)
 
 
 def unpack_kernel(first, blocks_ref, packed, out, held, sems):
@@ -459,7 +460,7 @@
             pltpu.VMEM((count * rows, width), LOW),
             pltpu.SemaphoreType.DMA((count * parts + count,)),
         ],
-        compiler_params=pltpu.CompilerParams(vmem_limit_bytes=24 * 1024 * 1024),
+        compiler_params=pltpu.CompilerParams(vmem_limit_bytes=VMEM),
     )(blocks, packed)
 
 
@@ -506,7 +507,7 @@
         out_specs=[pl.BlockSpec((count, columns), lambda i: (0, 0)) for _ in outs],
         out_shape=outs,
         scratch_shapes=[pltpu.VMEM((count, columns), FULL)] * len(outs),
-        compiler_params=pltpu.CompilerParams(vmem_limit_bytes=40 * 1024 * 1024),
+        compiler_params=pltpu.CompilerParams(vmem_limit_bytes=VMEM),
         cost_estimate=pl.CostEstimate(
             flops=2 * count * width * columns * len(places),
             bytes_accessed=2 * width * columns * len(places) + 8 * count * columns,
@@ -535,7 +536,7 @@
         in_specs=[fixed] * len(rows) + pack_specs(gathered, places, steps, block),
         out_specs=pl.BlockSpec((count, width // steps), lambda i: (0, i)),
         out_shape=jax.ShapeDtypeStruct((count, width), FULL),
-        compiler_params=pltpu.CompilerParams(vmem_limit_bytes=40 * 1024 * 1024),
+        compiler_params=pltpu.CompilerParams(vmem_limit_bytes=VMEM),
         cost_estimate=pl.CostEstimate(
             flops=2 * count * width * columns * len(places),
             bytes_accessed=2 * width * columns * len(places) + 4 * count * width,
@@ -582,7 +583,7 @@
 
 def weight_kernel(chip_ref, core_ref, *refs):
     normed, normed_got, back, back_got, query, key, value, got, context, context_got = refs[:10]
-    out_ref, pre_both, context_both = refs[10:]
+    out_ref, right_ref, left_ref, pre_both, context_both = refs[10:]
     rows, columns = query.shape
 
     @pl.when(pl.program_id(0) == 0)
@@ -597,6 +598,11 @@
     out_ref[0, :, : 3 * columns] = dot_tn(left, pre_both[...]).astype(LOW)
     left = jnp.concatenate([back[...], back_got[...]], axis=0)
     out_ref[0, :, 3 * columns :] = dot_tn(left, context_both[...]).astype(LOW)
+
+    @pl.when(pl.program_id(0) == HOPS.index(4))
+    def _():
+        right_ref[...] = out_ref[0, :, : 2 * columns]
+        left_ref[...] = out_ref[0, :, 2 * columns :]
 
 
 def weight_grads(chips, core, normed, back, pre_grads, got, context, context_got):
@@ -613,14 +619,16 @@
             num_scalar_prefetch=2,
             grid=(count,),
             in_specs=[tall] * 4 + [mine] * 3 + [fixed(got), mine, fixed(context_got)],
-            out_specs=pl.BlockSpec((1, block, 4 * columns), lambda i, chip, core: (i, 0, 0)),
+            out_specs=[pl.BlockSpec((1, block, 4 * columns), lambda i, chip, core: (i, 0, 0))]
+            + [pl.BlockSpec((block, 2 * columns), lambda i, chip, core: (0, 0))] * 2,
             scratch_shapes=[
                 pltpu.VMEM((2 * rows, 3 * columns), LOW),
                 pltpu.VMEM((2 * rows, columns), LOW),
             ],
         ),
-        out_shape=jax.ShapeDtypeStruct((count, block, 4 * columns), LOW),
-        compiler_params=pltpu.CompilerParams(vmem_limit_bytes=40 * 1024 * 1024),
+        out_shape=[jax.ShapeDtypeStruct((count, block, 4 * columns), LOW)]
+        + [jax.ShapeDtypeStruct((block, 2 * columns), LOW)] * 2,
+        compiler_params=pltpu.CompilerParams(vmem_limit_bytes=VMEM),
         cost_estimate=pl.CostEstimate(
             flops=16 * rows * width * columns,
             bytes_accessed=2 * (4 * rows * width + 8 * rows * columns + 4 * width * columns),
@@ -629,21 +637,22 @@
     )(chips, core, *normed, *back, *pre_grads, got, context, context_got)
 
 
-def ring_weights(blocks, fillers):
+def ring_weights(blocks, right, left, fillers):
     part = lambda hop: blocks[HOPS.index(hop)]
     cut = blocks.shape[2] // 2
-    right, left = ahead(part(4)[:, :cut]), behind(part(4)[:, cut:])
-    fillers.next(left)
+    right, left = ahead(right), behind(left)
     outward, inward = part(3), part(-3)
     right = jnp.concatenate([add_low(outward[:, :cut], right), outward[:, cut:]], axis=1)
     left = jnp.concatenate([inward[:, :cut], add_low(inward[:, cut:], left)], axis=1)
+    right, left = together(right, left)
+    fillers.next((right, left))
     right, left = ahead(right), behind(left)
-    fillers.next(left)
-    token = left
     for hop in (2, 1):
-        right, left = ahead(add_low(part(hop), right)), behind(add_low(part(-hop), left))
-        fillers.next(left)
-        token = left if hop == 2 else token
+        right, left = add_low(part(hop), right), add_low(part(-hop), left)
+        right, left = together(right, left)
+        right, left = fillers.next((right, left)) or (right, left)
+        token = right
+        right, left = ahead(right), behind(left)
     return part(0).astype(FULL) + right.astype(FULL) + left.astype(FULL), token
 
 
@@ -687,7 +696,7 @@
         out_specs=[tall(width)] + [tall(hidden)] * 6,
         out_shape=[jax.ShapeDtypeStruct((count, width), LOW)]
         + [jax.ShapeDtypeStruct((count, hidden), LOW)] * 6,
-        compiler_params=pltpu.CompilerParams(vmem_limit_bytes=58 * 1024 * 1024),
+        compiler_params=pltpu.CompilerParams(vmem_limit_bytes=VMEM),
         cost_estimate=pl.CostEstimate(
             flops=flops,
             bytes_accessed=2 * (3 * count * width + 6 * count * hidden + 6 * width * hidden),
@@ -696,12 +705,12 @@
     )(rows, back, gate, *mats)
 
 
-def chunk_kernel(pieces, held, at, size, gate_ref, *refs):
+def chunk_kernel(pieces, held, at, splits, gate_ref, *refs):
     piece_refs, refs = refs[:pieces], refs[pieces:]
     back_ref, mats, refs = refs[0], refs[1:7], refs[7 + held :]
-    same_ref, cross_ref, rows_out = refs[:3]
-    outs = refs[3:9]
-    rows, back, wide, wd, hidden, both_grads, grads, sems = refs[9:]
+    grad_outs, refs = refs[: len(splits)], refs[len(splits) :]
+    rows_out, outs = refs[0], refs[1:7]
+    rows, back, wide, wd, hidden, both_grads, grads, sems = refs[7:]
     count = rows.shape[0]
     part = wd.shape[1]
     slab = wide.shape[0] // 4
@@ -713,19 +722,19 @@
         span = pl.ds(start, piece.shape[0])
         load_rows.append(copy(piece, rows.at[span], sems.at[len(load_rows)]))
         start += piece.shape[0]
-    load_back = copy(back_ref.at[place], back, sems.at[4])
+    load_back = copy(back_ref.at[place], back, sems.at[6])
     loads = []
     for half in range(2):
         places = [wide.at[:, across(0, half)], wide.at[:, across(1, half)], wd.at[half]]
         loads.append(
-            [copy(mats[2 * k + half], to, sems.at[5 + 3 * half + k]) for k, to in enumerate(places)]
+            [copy(mats[2 * k + half], to, sems.at[7 + 3 * half + k]) for k, to in enumerate(places)]
         )
     for one in load_rows + loads[0][:2] + [load_back] + loads[0][2:] + loads[1]:
         one.start()
     gate = gate_ref[...]
     for one in load_rows:
         one.wait()
-    stores = [copy(rows, rows_out.at[place], sems.at[11])]
+    stores = [copy(rows, rows_out.at[place], sems.at[13])]
     stores[0].start()
     for half in range(2):
         columns = pl.ds(half * part, part)
@@ -751,7 +760,7 @@
             both_grads.at[:, across(1, half)],
         )
         for k, source in enumerate(held_in):
-            stores.append(copy(source, outs[2 * k + half].at[place], sems.at[12 + 3 * half + k]))
+            stores.append(copy(source, outs[2 * k + half].at[place], sems.at[14 + 3 * half + k]))
             stores[-1].start()
 
     @pl.loop(0, 4)
@@ -759,21 +768,16 @@
         span = pl.ds(pl.multiple_of(j * slab, slab), slab)
         grads[:, span] = dot_nt(both_grads[...], wide[span]).astype(LOW)
 
-    for k in range(count // size):
-        to = cross_ref if k % 2 else same_ref
-        stores.append(
-            copy(
-                grads.at[pl.ds(k * size, size)],
-                to.at[pl.ds(k // 2 * size, size)],
-                sems.at[18 + k],
-            )
-        )
+    start = 0
+    for k, (split, to) in enumerate(zip(splits, grad_outs)):
+        stores.append(copy(grads.at[pl.ds(start, split)], to, sems.at[20 + k]))
         stores[-1].start()
+        start += split
     for one in stores:
         one.wait()
 
 
-def expert_chunk(pieces, back, gate, mats, at, held, size):
+def expert_chunk(pieces, back, gate, mats, at, held, splits):
     all_rows, width = back.shape
     part = mats[0].shape[1]
     hidden = 2 * part
@@ -782,11 +786,11 @@
     held = [] if held is None else list(held)
     args = [gate, *pieces, back, *mats, *held]
     out = pl.pallas_call(
-        lambda *refs: chunk_kernel(len(pieces), len(held), at, size, *refs),
+        lambda *refs: chunk_kernel(len(pieces), len(held), at, splits, *refs),
         grid=(1,),
         in_specs=[pl.BlockSpec((count, 1), lambda j: (at, 0))] + [anywhere] * (len(args) - 1),
-        out_specs=[anywhere] * 9,
-        out_shape=[jax.ShapeDtypeStruct((count // 2, width), LOW)] * 2
+        out_specs=[anywhere] * (len(splits) + 7),
+        out_shape=[jax.ShapeDtypeStruct((split, width), LOW) for split in splits]
         + [jax.ShapeDtypeStruct((all_rows, width), LOW)]
         + [jax.ShapeDtypeStruct((all_rows, part), LOW)] * 6,
         scratch_shapes=[
@@ -797,76 +801,90 @@
             pltpu.VMEM((count, hidden), LOW),
             pltpu.VMEM((count, 2 * hidden), LOW),
             pltpu.VMEM((count, width), LOW),
-            pltpu.SemaphoreType.DMA((22,)),
+            pltpu.SemaphoreType.DMA((23,)),
         ],
-        input_output_aliases={len(args) - len(held) + k: 2 + k for k in range(len(held))},
-        compiler_params=pltpu.CompilerParams(vmem_limit_bytes=50 * 1024 * 1024),
+        input_output_aliases={
+            len(args) - len(held) + k: len(splits) + k for k in range(len(held))
+        },
+        compiler_params=pltpu.CompilerParams(vmem_limit_bytes=VMEM),
         cost_estimate=pl.CostEstimate(
             flops=2 * 5 * count * width * hidden,
             bytes_accessed=2 * (4 * count * width + 3 * count * hidden + 3 * width * hidden),
             transcendentals=count * hidden,
         ),
     )(*args)
-    return out[0], out[1], out[2:]
-
-
-def mixed_kernel(chip_ref, core_ref, h0_ref, h1_ref, first_ref, second_ref, out_ref):
+    return out[: len(splits)], out[len(splits) :]
+
+
+def mixed_kernel(chip_ref, same_ref, cross_ref, core_ref, *refs):
+    first_ref, second_ref, out_ref = refs[4:]
     rows = out_ref.shape[2]
-    result = dot_nn(h0_ref[...], first_ref[...]) + dot_nn(h1_ref[...], second_ref[...])
-    result = result.astype(LOW)
+    first, second = (
+        jnp.concatenate([refs[k][...], refs[k + 1][...]], axis=0) for k in (0, 2)
+    )
+    result = (dot_nn(first, first_ref[...]) + dot_nn(second, second_ref[...])).astype(LOW)
     out_ref[0, core_ref[0]] = result[:rows]
     out_ref[0, 1 - core_ref[0]] = result[rows:]
 
 
-def mixed_pass(h0, h1, down_mats, blocks):
+def mixed_pass(h0, h1, down_mats, chips, core):
     count, columns = h0.shape
     width = down_mats[0].shape[1]
-    chips = blocks.shape[0] // 2
-    rows = count // chips
+    rows = count // len(LAYOUT)
+    places = [
+        jnp.array([LAYOUT.index((hop, cross)) for hop in HOPS], jnp.int32) for cross in (0, 1)
+    ]
     once = pl.Buffered(1)
-    fixed = lambda m: pl.BlockSpec(m.shape, lambda i, a, b: (0, 0), pipeline_mode=once)
+    fixed = lambda m: pl.BlockSpec(m.shape, lambda i, *tables: (0, 0), pipeline_mode=once)
+    block = lambda k: pl.BlockSpec((rows, columns), lambda i, *tables: (tables[k][i], 0))
     out = pl.pallas_call(
         mixed_kernel,
         grid_spec=pltpu.PrefetchScalarGridSpec(
-            num_scalar_prefetch=2,
-            grid=(chips,),
-            in_specs=[pl.BlockSpec((rows, columns), lambda i, a, b: (i, 0))] * 2
-            + [fixed(m) for m in down_mats],
+            num_scalar_prefetch=4,
+            grid=(len(HOPS),),
+            in_specs=[block(1), block(2), block(1), block(2)] + [fixed(m) for m in down_mats],
             out_specs=pl.BlockSpec(
-                (1, 2, rows // 2, width), lambda i, chip, core: (chip[i], 0, 0, 0)
+                (1, 2, rows, width), lambda i, chip, *tables: (chip[i], 0, 0, 0)
             ),
         ),
-        out_shape=jax.ShapeDtypeStruct((chips, 2, rows // 2, width), LOW),
-        compiler_params=pltpu.CompilerParams(vmem_limit_bytes=40 * 1024 * 1024),
+        out_shape=jax.ShapeDtypeStruct((len(HOPS), 2, rows, width), LOW),
+        compiler_params=pltpu.CompilerParams(vmem_limit_bytes=VMEM),
         cost_estimate=pl.CostEstimate(
             flops=4 * count * columns * width,
             bytes_accessed=2 * (count * (2 * columns + width) + 2 * columns * width),
             transcendentals=0,
         ),
-    )(blocks[::2] // 2, blocks[:1] % 2, h0, h1, *down_mats)
+    )(chips, *places, core, h0, h0, h1, h1, *down_mats)
     return out.reshape(count, width)
 
 
 def expert_ring(rows, back, gate, mats, waiting):
     size = rows.shape[0]
     cut = size // 2
-    same, cross = {}, {}
     swap = lambda block: swap_bit(block, "dp", 0)
+    chunk = lambda pieces, at, held, *splits: expert_chunk(
+        pieces, back, gate, mats, at, held, splits
+    )
     rows, pair = together(rows, swap(rows))
     left, right = ahead(rows), behind(rows)
     waiting = swap_tensor(after(waiting, pair))
-    same[0], cross[0], held = expert_chunk([rows, pair], back, gate, mats, 6, None, size)
-    for hop in (1, 2, 3):
-        left, right, same[hop - 1] = together(left, right, same[hop - 1])
-        pieces = [left, swap(left), right, swap(right)]
-        if hop < 3:
-            left, right = ahead(left), behind(right)
-        else:
-            left, right = ahead(left[:cut]), behind(right[cut:])
-            pieces[0], waiting = together(pieces[0], waiting)
-        same[hop], cross[hop], held = expert_chunk(pieces, back, gate, mats, hop - 1, held, size)
-    pieces = [left, right, swap(left), swap(right)]
-    same[4], cross[4], held = expert_chunk(pieces, back, gate, mats, 7, held, size)
+    same, cross = {}, {}
+    (same[0], cross[0]), held = chunk([rows, pair], 6, None, size, size)
+    left, right, same[0] = together(left, right, same[0])
+    pieces, crossed = [left, right], [swap(left), swap(right)]
+    left, right = ahead(left), behind(right)
+    (same[1],), held = chunk(pieces, 7, held, 2 * size)
+    left, right, same[1] = together(left, right, same[1])
+    pieces, crossed = [left, right, *crossed], [swap(left), swap(right)]
+    left, right = ahead(left), behind(right)
+    (same[2], cross[1]), held = chunk(pieces, 0, held, 2 * size, 2 * size)
+    left, right, waiting, same[2] = together(left, right, waiting, same[2])
+    pieces, crossed = [left, right, *crossed], [swap(left), swap(right)]
+    left, right = ahead(left[:cut]), behind(right[cut:])
+    (same[3], cross[2]), held = chunk(pieces, 1, held, 2 * size, 2 * size)
+    left, right, same[3] = together(left, right, same[3])
+    pieces = [left, right, swap(left), swap(right), *crossed]
+    (same[4], cross[4], cross[3]), held = chunk(pieces, 2, held, size, size, 2 * size)
     return same, cross, held, waiting
 
 
@@ -938,20 +956,15 @@
     routing = jnp.pad(routing, ((0, 0), (0, local_width - 3 * token_count)))
     gains = jnp.concatenate([attn_gain, moe_gain, query_gain, key_gain])
     gains = jnp.pad(gains[None], ((0, 7), (0, local_width - 4 * block)))
+    packed = pack_weights(
+        w_query, w_key, w_value, w_out, jnp.concatenate([gains, routing], axis=0)
+    )
+    gathered = lax.all_gather(packed, "dp", axis=0, tiled=False)
     cotangent_half = own_half(cotangent)
-    packed, turned = pack_weights(
-        w_query,
-        w_key,
-        w_value,
-        jnp.concatenate([gains, routing], axis=0),
-        w_out,
-        [cotangent_half] if ring else [],
-    )
-    gathered = lax.all_gather(packed, "dp", axis=0, tiled=False)
-    gathered_out = lax.all_gather(turned, "dp", axis=0, tiled=False)
+    gathered_back = lax.all_gather(cotangent_half.astype(LOW), "dp", axis=0, tiled=False)
     gathered, *early = lax.optimization_barrier((gathered, gate_mats[1], up_mats[1]))
     gate_mats, up_mats = (gate_mats[0], early[0]), (up_mats[0], early[1])
-    rest = gathered[:, 3 * block : 3 * block + 16]
+    rest = gathered[:, 4 * block : 4 * block + 16]
     gain_rows = rest[:, 0].astype(FULL)
     gain_one, gain_two, gain_q, gain_k = (
         gain_rows[:, j * block : (j + 1) * block].reshape(-1) for j in range(4)
@@ -978,7 +991,7 @@
     weight = jnp.where(kept, weight, 0.0)
     weight = lax.dynamic_slice_in_dim(weight, side * half_count, half_count, axis=1)
     if ring:
-        blocks = ring_blocks(dp_index)
+        blocks, chips = ring_blocks(dp_index), ring_chips(dp_index, HOPS)
         weight = weight[blocks]
     weight = weight.reshape(-1, 1)
 
@@ -1017,18 +1030,16 @@
     pieces = (*collect_prompt(keys_b[:PR_DEV], 2, 1), *value_pieces)
     turned_by = (gain_query_local[None], query_scale, cosine, sine, bias)
     context_b = attend(query_flat, *turned_by, keys_b, values_b, pieces)
-    gathered_out = after(gathered_out, context_b)
-    attn_part = project_back([context_b], gathered_out, block, (0,))
+    attn_part = project_back([context_b], gathered, block, (3,))
     attn_part, late, weight = together(attn_part, down_mats[1], weight)
     down_mats = (down_mats[0], late)
     mats = (*gate_mats, *up_mats, *down_mats)
     attn_other = swap_tensor(other_half(attn_part).astype(LOW))
+    gathered_back = after(gathered_back, attn_part)
     if ring:
-        back_rows = unpack_rows(
-            after(gathered, attn_part), blocks, 3 * block + 16, model_width
-        )
+        back_rows = unpack_rows(gathered_back, blocks, 0, model_width)
     else:
-        back_rows = lax.all_gather(cotangent_half.astype(LOW), "dp", axis=0, tiled=True)
+        back_rows = gathered_back.reshape(-1, model_width)
     attn_other, back_rows, weight = together(attn_other, back_rows, weight)
     hidden_state = own_half(tokens_f) + own_half(attn_part) + attn_other.astype(FULL)
     normed_two_b = rms_norm(hidden_state, gain_two).astype(LOW)
@@ -1044,14 +1055,14 @@
         down_got = swap_tensor(low_tn(h1, back_rows))
         late = {}
 
-        def gate_stage(gated):
+        def gate_stage(gated, token):
             late["gate"] = low_tn(gated(expert_in), g1)
 
-        def up_stage(gated):
+        def up_stage(gated, token):
             late["up"] = low_tn(gated(expert_in), u1)
 
-        def mixed_stage(gated):
-            late["mixed"] = mixed_pass(gated(h0), h1, down_mats, blocks)
+        def mixed_stage(gated, token):
+            late["mixed"] = mixed_pass(gated(h0), h1, down_mats, chips, core[None])
 
         fillers = Fillers(gate_stage, up_stage, mixed_stage)
         normed_two_grad = ring_sum(same, cross, fillers)
@@ -1081,8 +1092,9 @@
     attn_grad_half = state_half.astype(LOW)
     attn_grad_b = both_halves(attn_grad_half, swap_tensor(attn_grad_half))
     attn_grad_b, gate_sent, up_sent = together(attn_grad_b, gate_sent, up_sent)
-    (context_grad_b,) = project(attn_grad_b, gathered_out, block, (0,), (LOW,))
-    gate_second, up_first = swap_in_turn([lower(gate_sent), upper(up_sent)], 2, context_grad_b)
+    (context_grad_b,) = project(attn_grad_b, gathered, block, (3,), (LOW,))
+    gate_pieces, up_pieces = cut_rows(gate_sent, 4), cut_rows(up_sent, 4)
+    soon = swap_in_turn([*gate_pieces[2:], up_pieces[0]], context_grad_b)
     if ring:
         pair = lambda own: (own, swap_bit(own, "dp", 0))
         columns = local_width // 2
@@ -1093,12 +1105,16 @@
         query_flat, *turned_by, keys_b, values_b, pieces, context_grad_b
     )
     returned = return_prompt(odd, even)
+    if ring:
+        key_grad, context_got, *pairs = together(
+            key_grad, context_got, normed_pair[1], attn_grad_pair[1]
+        )
+        normed_pair, attn_grad_pair = (normed_b, pairs[0]), (attn_grad_b, pairs[1])
     key_normed_grad, key_inner, key_gain_part, value_pre_grad = key_back(
         key_grad, value_grad, key_flat, gain_key_local[None], key_scale, cosine, sine, returned
     )
-    query_inner, gate_second, up_first = together(query_inner, gate_second, up_first)
+    query_inner, *soon = together(query_inner, *soon)
     query_inner, key_inner = lax.psum((query_inner[:, 0], key_inner[:, 0]), "tensor")
-    (up_second,) = swap_in_turn([lower(up_sent)], 2, query_inner)
     query_pre_grad, key_pre_grad, pre_sent = pre_grads_pass(
         core[None],
         (
@@ -1111,25 +1127,39 @@
         (key_flat, key_normed_grad, gain_key_local[None], key_scale, key_inner[:, None]),
         value_pre_grad,
     )
-    up_got = jnp.concatenate([up_first, up_second], axis=0)
-    gate_got = jnp.concatenate([gate_first, gate_second], axis=0)
+    gate_got = jnp.concatenate([gate_first, *soon[:2]], axis=0)
     pre_grads = (query_pre_grad, key_pre_grad, value_pre_grad)
     grad_sum = lambda left, right, got: dot_tn(left, right) + got.astype(FULL)
     back_all = lambda *grads: project_back(grads, gathered, block, (0, 1, 2))
 
+    wide = lambda part: lax.dynamic_update_slice_in_dim(
+        jnp.zeros((column_total,), FULL), part, side * local_width, 0
+    )
+
     def share(part):
-        return own_half(part), swap_tensor(other_half(part).astype(LOW))
+        return own_half(part), swap_tensor(other_half(part).astype(LOW)), gain_part(part)
 
     def input_side(own, other):
-        unused_one, norm_one_back = jax.vjp(rms_norm, own_half(tokens_f), gain_one)
-        input_part, gain_one_grad = norm_one_back(own + other.astype(FULL))
-        input_half = state_half + input_part
-        return input_half, swap_tensor(input_half), gain_one_grad
+        unused_one, norm_one_back = jax.vjp(
+            lambda values: rms_norm(values, gain_one), own_half(tokens_f)
+        )
+        input_half = state_half + norm_one_back(own + other.astype(FULL))[0]
+        return input_half, swap_tensor(input_half)
+
+    def gain_part(part):
+        return jnp.sum(part * rms_norm(tokens_f, 1.0), axis=0)
+
+    def gain_side(gain_one_grad):
+        grads = jnp.stack(
+            [gain_one_grad, gain_two_grad, wide(query_gain_part[0]), wide(key_gain_part[0])]
+        ).reshape(4, dp_count, block)
+        sums = halving_sum(jnp.swapaxes(grads, 0, 1))
+        return sums + swap_tensor(sums)
 
     if ring:
         pre_got = swap_bit(pre_sent, "dp", 0)
-        w_blocks = weight_grads(
-            blocks[::2] // 2,
+        w_blocks, *far = weight_grads(
+            chips,
             core[None],
             normed_pair,
             attn_grad_pair,
@@ -1138,25 +1168,30 @@
             context_b,
             context_got,
         )
-        w_blocks, mixed = together(w_blocks, mixed)
+        w_blocks, mixed, *far = together(w_blocks, mixed, *far)
+        up_got = jnp.concatenate([soon[2], *swap_in_turn(up_pieces[1:], far[0])], axis=0)
         mixed_other = swap_tensor(mixed)
         late = {}
 
-        def normed_stage(gated):
+        def normed_stage(gated, token):
             late["normed"] = share(back_all(*[gated(grad) for grad in pre_grads]))
 
-        def expert_stage(gated):
+        def expert_stage(gated, token):
             late["down"] = grad_sum(gated(h0), back_rows, down_got)
-            late["up"] = grad_sum(gated(expert_in), u0, up_got)
-
-        def input_stage(gated):
+            late["gate"] = grad_sum(gated(expert_in), g0, gate_got)
+
+        def input_stage(gated, token):
+            late["down"], late["gate"], *token = together(late["down"], late["gate"], *token)
             late["input"] = input_side(late["normed"][0], gated(late["normed"][1]))
+            late["gains"] = gain_side(gated(late["normed"][2]))
+            return token
 
         fillers = Fillers(normed_stage, expert_stage, input_stage)
-        w_half, token = ring_weights(w_blocks, fillers)
-        input_half, input_other, gain_one_grad = late["input"]
-        down_grad, up_w_grad = late["down"], late["up"]
-        gate_w_grad = grad_sum(after(expert_in, token), g0, gate_got)
+        w_half, token = ring_weights(w_blocks, *far, fillers)
+        input_half, input_other = late["input"]
+        gain_sums, token = together(late["gains"], token)
+        down_grad, gate_w_grad = late["down"], late["gate"]
+        up_w_grad = grad_sum(after(expert_in, token), u0, up_got)
         own_w = lax.dynamic_slice_in_dim(w_half, core * block, block, axis=0)
         got_w = swap_bit(
             lax.dynamic_slice_in_dim(w_half, (1 - core) * block, block, axis=0), "dp", 0
@@ -1175,21 +1210,16 @@
         w_sums = [w_sum[:, j * local_width : (j + 1) * local_width] for j in range(4)]
         down_grad = grad_sum(h0, back_rows, down_got)
         gate_w_grad = grad_sum(expert_in, g0, gate_got)
+        up_got = jnp.concatenate([soon[2], *map(swap_tensor, up_pieces[1:])], axis=0)
         up_w_grad = grad_sum(expert_in, u0, up_got)
         mixed_other = swap_tensor(mixed)
-        input_half, input_other, gain_one_grad = input_side(*share(back_all(*pre_grads)))
+        *normed_parts, gain_one_grad = share(back_all(*pre_grads))
+        gain_sums = gain_side(gain_one_grad)
+        input_half, input_other = input_side(*normed_parts)
     input_grad = both_halves(input_half, input_other)
     output = both_halves(
         hidden_state + mixed.astype(FULL), hidden_other + mixed_other.astype(FULL)
     )
-    wide = lambda part: lax.dynamic_update_slice_in_dim(
-        jnp.zeros((column_total,), FULL), part, side * local_width, 0
-    )
-    gain_grads = jnp.stack(
-        [gain_one_grad, gain_two_grad, wide(query_gain_part[0]), wide(key_gain_part[0])]
-    ).reshape(4, dp_count, block)
-    gain_sums = halving_sum(jnp.swapaxes(gain_grads, 0, 1))
-    gain_sums = gain_sums + swap_tensor(gain_sums)
     return (
         output,
         input_grad,

time: 765 us -> 757 us (0.990)
  local copies, waits for them, and re-layouts: 62.1 us -> 30.9 us
  Pallas kernels: 198 us -> 215 us
    unnamed x226 -> x130, local copies, waits for them, and re-layouts: 42.6 us -> 8.12 us
    all_gather x1, waiting for transfers between devices: 29.5 us -> 0.01 us  [body(): gathered = lax.all_gather(packed, 'dp', axis=0, tiled=False)]
    ppermute x12, waiting for transfers between devices: 8.27 us -> 37.1 us  [ahead(): return lax.ppermute(block, 'dp', AHEAD)]
    ppermute x12, waiting for transfers between devices: 43.3 us -> 15.6 us  [behind(): return lax.ppermute(block, 'dp', BEHIND)]
    ppermute x45, waiting for transfers between devices: 69.9 us -> 90.3 us  [swap_bit(): return lax.ppermute(block, axis, [(i, i ^ 1 << bit) for i in range(count)])]
    ppermute x12, starting transfers between devices: 9.77 us -> 22 us  [behind(): return lax.ppermute(block, 'dp', BEHIND)]
  transfers between devices with their start and end apart: 90 -> 90, of which waited for: 42 -> 34; matrix products, arithmetic and copies ran while one was open for 15% -> 17% of each run, Pallas kernels for 26% -> 28%
where the time goes in v8:
time: 757 us; the launch traced here: 748 us
  waiting for transfers between devices  282 us (37%)
  Pallas kernels  215 us (28%)
  starting transfers between devices  78.9 us (10%)
  other arithmetic  55.4 us (7%)
  matrix products  53.4 us (7%)
  local copies, waits for them, and re-layouts  30.9 us (4%)
  blocking collectives  17.1 us (2%)
  between operations  15.5 us (2%)
    ppermute x18, waiting for transfers between devices, swap_tensor(): return lax.ppermute(block, 'tensor', [(0, 1), (1, 0)])  139 us
    pallas_call x5, Pallas kernels, expert_chunk(): pl.pallas_call(lambda *refs: chunk_kernel(len(pieces), len(held), at, spl...  92.2 us
    ppermute x45, waiting for transfers between devices, swap_bit(): return lax.ppermute(block, axis, [(i, i ^ 1 << bit) for i in range(count)])  90.3 us
    dot_general x6, matrix products, dot_tn(): lax.dot_general(left, right, (((0,), (0,)), ((), ())), preferred_element_...  53.3 us
    ppermute x12, waiting for transfers between devices, ahead(): return lax.ppermute(block, 'dp', AHEAD)  37.1 us
    ppermute x12, starting transfers between devices, behind(): return lax.ppermute(block, 'dp', BEHIND)  22 us
    ppermute x18, starting transfers between devices, swap_tensor(): return lax.ppermute(block, 'tensor', [(0, 1), (1, 0)])  21.1 us
    ppermute x45, starting transfers between devices, swap_bit(): return lax.ppermute(block, axis, [(i, i ^ 1 << bit) for i in range(count)])  20.9 us
  transfers between devices with their start and end apart: 90, of which 34 were waited for; matrix products, arithmetic and copies ran while one was open for 17% of the time, Pallas kernels for 28%

profile of v8, /device:TPU:0, one launch (start us, length us, event | category | flops | bytes accessed | tf_op | source)
XLA Modules:
  0.0 747.8 jit_solution(12214839430963747275)
XLA Ops:
  10.1 2.4 shard_map.309
  12.7 2.3 dynamic-slice_convert_fusion.2
  15.1 3.0 collective-permute-start
  21.3 43.4 %collective-permute-done.refs_5_.refs_7_.refs_9_ = bf16[2048,512]{1,0:T(8,128)(2,1)} collective-permute-done((bf16[2048,512]{1,0:T(8,128)(2,1)S(1)}, bf16[2048,512]{1,0:T(8,128)(2,1)}, u32[]{:S(2)}, u32[]{:S(2)}) %collective-permute-start) | collective-permute-done | bytes 2097184 | tf_op jit(solution)/shard_map/ppermute | solution.py:26
  64.7 44.1 %collective-permute-done.1.refs_7_.refs_9_.refs_11_ = bf16[2048,512]{1,0:T(8,128)(2,1)} collective-permute-done((bf16[2048,512]{1,0:T(8,128)(2,1)}, bf16[2048,512]{1,0:T(8,128)(2,1)}, u32[]{:S(2)}, u32[]{:S(2)}) %collective-permute-start.1) | collective-permute-done | bytes 2097184 | tf_op jit(solution)/shard_map/ppermute | solution.py:26
  111.9 11.7 %shard_map.310 = (f32[320,1024]{1,0:T(8,128)}, f32[320,1024]{1,0:T(8,128)}, bf16[320,1024]{1,0:T(8,128)(2,1)}) custom-call(bf16[320,2048]{1,0:T(8,128)(2,1)} %multiply_convert_fusion.refs_0_, bf16[16,528,1024]{2,1,0:T(8,128)(2,1)} %bitcast.94, bf16[16,528,1024]{2,1,0:T(8,128)(2,1)} %bitcast.95, bf16[16,528,1024]{2,1,0:T(8,128)(2,1)} %bitcast.96), custom_call_target="tpu_custom_call" | custom-call | flops 4026531840 | bytes 15204352 | tf_op jit(solution)/shard_map/pallas_call | solution.py:502
  125.4 2.0 multiply_reduce_fusion.7
  127.4 4.9 all-reduce.4
  134.0 2.0 negate_select_fusion
  137.4 2.7 shard_map.311.k_ref
  145.1 2.1 select_convert_fusion.bias_ref
  153.0 2.5 collective-permute-start.7
  155.6 6.9 collective-permute-done.10.refs_8_
  162.5 10.4 %collective-permute-done.12.refs_10_ = bf16[128,1024]{1,0:T(8,128)(2,1)} collective-permute-done((bf16[128,1024]{1,0:T(8,128)(2,1)}, bf16[128,1024]{1,0:T(8,128)(2,1)}, u32[]{:S(2)}, u32[]{:S(2)}) %collective-permute-start.12) | collective-permute-done | bytes 262176 | tf_op jit(solution)/shard_map/ppermute | solution.py:22
  175.2 14.5 %collective-permute-done.14.refs_12_ = bf16[128,1024]{1,0:T(8,128)(2,1)} collective-permute-done((bf16[128,1024]{1,0:T(8,128)(2,1)}, bf16[128,1024]{1,0:T(8,128)(2,1)}, u32[]{:S(2)}, u32[]{:S(2)}) %collective-permute-start.14) | collective-permute-done | bytes 262176 | tf_op jit(solution)/shard_map/ppermute | solution.py:22
  191.8 11.9 %shard_map.312.refs_0_.refs_8_ = bf16[320,1024]{1,0:T(8,128)(2,1)} custom-call(f32[320,1024]{1,0:T(8,128)} %get-tuple-element.172.flat_ref.refs_0_, f32[1,1024]{1,0:T(1,128)} %bitcast.134, f32[320,1]{1,0:T(8,128)} %broadcast_in_dim.137.scale_ref.refs_3_, f32[320,128]{1,0:T(8,128)} %get-tuple-element.442.cos_ref.refs_5_, ...), custom_call_target="tpu_custom_call" | custom-call | tf_op jit(solution)/shard_map/pallas_call | solution.py:271
  203.7 5.5 shard_map.313
  213.5 8.8 %shard_map.314.refs_3_.refs_5_.refs_7_ = bf16[2560,2048]{1,0:T(8,128)(2,1)} custom-call(s32[16]{0:T(128)} %get-tuple-element.384.refs_0_, bf16[16,160,2048]{2,1,0:T(8,128)(2,1)} %bitcast.128), custom_call_target="tpu_custom_call" | custom-call | tf_op jit(solution)/shard_map/pallas_call | solution.py:454
  222.3 5.6 collective-permute-done.17
  227.9 2.0 multiply_reduce_fusion.6
  230.2 2.1 collective-permute-done.18.refs_2_
  232.3 2.3 collective-permute-start.20
  236.1 13.7 %shard_map.315 = (bf16[160,2048]{1,0:T(8,128)(2,1)}, bf16[160,2048]{1,0:T(8,128)(2,1)}, bf16[2560,2048]{1,0:T(8,128)(2,1)}, bf16[2560,512]{1,0:T(8,128)(2,1)}, b...) custom-call(f32[2560,1]{1,0:T(8,128)} %copy.78.refs_0_, ...), custom_call_target="tpu_custom_call" | custom-call | flops 6710886400 | bytes 19791872 | tf_op jit(solution)/shard_map/pallas_call | solution.py:788
  254.1 13.7 %shard_map.316 = (bf16[320,2048]{1,0:T(8,128)(2,1)}, bf16[2560,2048]{1,0:T(8,128)(2,1)}, bf16[2560,512]{1,0:T(8,128)(2,1)}, bf16[2560,512]{1,0:T(8,128)(2,1)}, b...) custom-call(f32[2560,1]{1,0:T(8,128)} %copy.78.refs_0_, ...), custom_call_target="tpu_custom_call", output_to_operand_aliasing={{1}: (10, {}), {2}: (11, {}), {3}: (12, {}), {4}: (13, {}),... | custom-call | flops 6710886400 | bytes 19791872 | tf_op jit(solution)/shard_map/pallas_call | solution.py:788
  269.0 11.7 %collective-permute-start.28 = (bf16[160,2048]{1,0:T(8,128)(2,1)S(1)}, bf16[160,2048]{1,0:T(8,128)(2,1)S(1)}, u32[]{:S(2)}, u32[]{:S(2)}) collective-permute-start(bf16[160,2048]{1,0:T(8,128)(2,1)S(1)} %collective-permute-done.23.refs_2_), channel_id=1, source_target_pairs={{8,0},{10,2},{16,8},{18,10},{24,16},{26,18},{28,24},{30,26},{20,28... | collective-permute-start | bytes 1966088 | tf_op jit(solution)/shard_map/ppermute | solution.py:49
  280.8 21.5 %shard_map.317 = (bf16[320,2048]{1,0:T(8,128)(2,1)}, bf16[320,2048]{1,0:T(8,128)(2,1)}, bf16[2560,2048]{1,0:T(8,128)(2,1)}, bf16[2560,512]{1,0:T(8,128)(2,1)}, b...) custom-call(f32[2560,1]{1,0:T(8,128)} %copy.78.refs_0_, ...), custom_call_target="tpu_custom_call", output_to_operand_aliasing={{2}: (12, {}), {3}: (13, {}), {4}: (14, {}), {5}: (15, {}),... | custom-call | flops 13421772800 | bytes 27000832 | tf_op jit(solution)/shard_map/pallas_call | solution.py:788
  306.4 21.8 %shard_map.318 = (bf16[320,2048]{1,0:T(8,128)(2,1)}, bf16[320,2048]{1,0:T(8,128)(2,1)}, bf16[2560,2048]{1,0:T(8,128)(2,1)}, bf16[2560,512]{1,0:T(8,128)(2,1)}, b...) custom-call(f32[2560,1]{1,0:T(8,128)} %copy.78.refs_0_, ...), custom_call_target="tpu_custom_call", output_to_operand_aliasing={{2}: (12, {}), {3}: (13, {}), {4}: (14, {}), {5}: (15, {}),... | custom-call | flops 13421772800 | bytes 27000832 | tf_op jit(solution)/shard_map/pallas_call | solution.py:788
  331.3 21.5 %shard_map.319 = (bf16[160,2048]{1,0:T(8,128)(2,1)}, bf16[160,2048]{1,0:T(8,128)(2,1)}, bf16[320,2048]{1,0:T(8,128)(2,1)}, bf16[2560,2048]{1,0:T(8,128)(2,1)}, b...) custom-call(f32[2560,1]{1,0:T(8,128)} %copy.78.refs_0_, ...), custom_call_target="tpu_custom_call", output_to_operand_aliasing={{3}: (14, {}), {4}: (15, {}), {5}: (16, {}), {6}: (17, {}),... | custom-call | flops 13421772800 | bytes 27000832 | tf_op jit(solution)/shard_map/pallas_call | solution.py:788
  353.4 10.6 %convolution_convert_fusion.2 = bf16[512,2048]{1,0:T(8,128)(2,1)} fusion(bf16[2560,512]{1,0:T(8,128)(2,1)} %get-tuple-element.247.refs_2_.refs_3_, bf16[2560,2048]{1,0:T(8,128)(2,1)} %shard_map.314.refs_3_.refs_5_.refs_7_), kind=kOutput, calls=%fused_computation.6 | convolution fusion | flops 5369757696 | bytes 15204352 | tf_op jit(solution)/shard_map/dot_general | solution.py:150
  371.9 5.1 collective-permute-done.41
  380.0 5.8 convolution_convert_fusion.1
  388.1 5.2 collective-permute-done.43
  397.4 6.8 convolution_convert_fusion
  404.2 5.5 collective-permute-done.45
  414.4 17.5 %shard_map.320 = bf16[8,2,160,2048]{3,2,1,0:T(8,128)(2,1)} custom-call(s32[8]{0:T(128)} %compare_select_fusion.6.chip_ref, s32[8]{0:T(128)} %constant.197.clone.same_ref, s32[8]{0:T(128)} %constant.198.clone.cross_ref, s32[1]{0:T(128)} %bitcast.15.core_ref, bf16[2560,512]{1,0:T(8,128)(2,1)} %get-tuple-element.308.refs_0_.refs_1_, ...), custom_call_target="tpu_custom_call" | custom-call | flops 10737418240 | bytes 19922944 | tf_op jit(solution)/shard_map/pallas_call | solution.py:840
  439.1 14.8 %collective-permute-done.51 = bf16[160,2048]{1,0:T(8,128)(2,1)S(1)} collective-permute-done((bf16[160,2048]{1,0:T(8,128)(2,1)S(1)}, bf16[160,2048]{1,0:T(8,128)(2,1)S(1)}, u32[]{:S(2)}, u32[]{:S(2)}) %collective-permute-start.51) | collective-permute-done | bytes 655392 | tf_op jit(solution)/shard_map/ppermute | solution.py:26
  455.1 5.9 shard_map.321.refs_14_
  463.0 19.8 %shard_map.322 = (f32[320,1024]{1,0:T(8,128)}, f32[320,1]{1,0:T(8,128)}, f32[1,1024]{1,0:T(1,128)}, f32[320,1024]{1,0:T(8,128)}, f32[320,1024]{1,0:T(8,128)}, /*...) custom-call(f32[320,1024]{1,0:T(8,128)} %get-tuple-element.172.flat_, ...), custom_call_target="tpu_custom_call" | custom-call | flops 20000000000 | bytes 40000000 | tf_op jit(solution)/shard_map/pallas_call | solution.py:330
  487.4 3.1 shard_map.323
  491.5 1.9 collective-permute-start.62
  493.5 2.8 fusion.49
  496.4 3.1 collective-permute-done.56
  499.4 23.6 %collective-permute-done.63.refs_9_ = bf16[2,128,1024]{2,1,0:T(8,128)(2,1)} collective-permute-done((bf16[2,128,1024]{2,1,0:T(8,128)(2,1)}, bf16[2,128,1024]{2,1,0:T(8,128)(2,1)}, u32[]{:S(2)}, u32[]{:S(2)}) %collective-permute-start.63) | collective-permute-done | bytes 524320 | tf_op jit(solution)/shard_map/ppermute | solution.py:22
  528.2 6.9 collective-permute-done.65.refs_11_
  536.4 5.3 shard_map.324
  541.8 12.2 %all-reduce.3 = (f32[320,1]{1,0:T(8,128)}, f32[320,1]{1,0:T(8,128)}) all-reduce(f32[320,1]{1,0:T(8,128)S(1)} %copy-done.38, f32[320,1]{1,0:T(8,128)} %get-tuple-element.281), channel_id=1, replica_groups=mesh['dp'=16,'tensor'=2] {'tensor'}, use_global_device_ids=true, to_apply=%region_13.14 | all-reduce | flops 640 | bytes 5120 | tf_op jit(solution)/shard_map/psum | solution.py:1117
  554.0 4.7 shard_map.325
  558.7 2.8 collective-permute-done.66.refs_7_
  562.4 14.1 %shard_map.326 = (bf16[8,256,2048]{2,1,0:T(8,128)(2,1)}, bf16[256,1024]{1,0:T(8,128)(2,1)}, bf16[256,1024]{1,0:T(8,128)(2,1)}) custom-call(s32[8]{0:T(128)} %compare_select_fusion.6.chip_ref, s32[1]{0:T(128)} %bitcast.15.core_ref, bf16[320,2048]{1,0:T(8,128)(2,1)} %multiply_convert_fusion.refs_0_, bf16[320,2048]{1,0:T(8,128)(2,1)} %collective-permute-done.53.refs_1_, ...), custom_call_target="tpu_custom_call" | custom-call | flops 5368709120 | bytes 16252928 | tf_op jit(solution)/shard_map/pallas_call | solution.py:616
  581.1 10.4 %collective-permute-done.69 = bf16[256,1024]{1,0:T(8,128)(2,1)S(1)} collective-permute-done((bf16[256,1024]{1,0:T(8,128)(2,1)}, bf16[256,1024]{1,0:T(8,128)(2,1)S(1)}, u32[]{:S(2)}, u32[]{:S(2)}) %collective-permute-start.69) | collective-permute-done | bytes 524320 | tf_op jit(solution)/shard_map/ppermute | solution.py:49
  592.1 2.3 collective-permute-start.70
  595.8 21.4 %collective-permute-done.70 = bf16[256,2048]{1,0:T(8,128)(2,1)} collective-permute-done((bf16[256,2048]{1,0:T(8,128)(2,1)S(1)}, bf16[256,2048]{1,0:T(8,128)(2,1)}, u32[]{:S(2)}, u32[]{:S(2)}) %collective-permute-start.70) | collective-permute-done | bytes 1048608 | tf_op jit(solution)/shard_map/ppermute | solution.py:45
  618.9 4.0 fusion.2
  627.9 9.3 %shard_map.327 = f32[320,2048]{1,0:T(8,128)} custom-call(bf16[320,1024]{1,0:T(8,128)(2,1)} %get-tuple-element.298.refs_4_.refs_0_, bf16[320,1024]{1,0:T(8,128)(2,1)} %get-tuple-element.299.refs_5_.refs_1_, bf16[320,1024]{1,0:T(8,128)(2,1)} %get-tuple-element.300.refs_10_.refs_6_.refs_2_, bf16[16,528,1024]{2,1,0:T(8,128)(2,1)} %bitcast.100, ...), custom_call_target="tpu_custom_call" | custom-call | flops 4026531840 | bytes 15204352 | tf_op jit(solution)/shard_map/pallas_call | solution.py:533
  639.4 2.2 multiply_reduce_fusion
  641.6 12.7 %collective-permute-done.85 = bf16[512,512]{1,0:T(8,128)(2,1)} collective-permute-done((bf16[512,512]{1,0:T(8,128)(2,1)}, bf16[512,512]{1,0:T(8,128)(2,1)}, u32[]{:S(2)}, u32[]{:S(2)}) %collective-permute-start.85) | collective-permute-done | bytes 524320 | tf_op jit(solution)/shard_map/ppermute | solution.py:26
  655.9 3.1 fusion.1
  659.1 2.2 collective-permute-start.74
  661.4 12.1 %convert_add_fusion = f32[2048,512]{1,0:T(8,128)} fusion(bf16[2560,2048]{1,0:T(8,128)(2,1)} %get-tuple-element.322, bf16[2560,512]{1,0:T(8,128)(2,1)S(1)} %copy-done.3, bf16[512,512]{1,0:T(8,128)(2,1)} %collective-permute-done.56, bf16[512,512]{1,0:T(8,128)(2,1)} %collective-permute-done.55, bf16[1024,512]{1,0:T(8,128)(2,1)} %collective-permute-done.50), kind=kOutput, calls=%fused_computation.2 | convolution fusion | flops 5376049152 | bytes 19398656 | tf_op jit(solution)/shard_map/dot_general | solution.py:150
  674.2 8.7 %convert_add_fusion.1 = f32[512,2048]{1,0:T(8,128)} fusion(bf16[512,2048]{1,0:T(8,128)(2,1)} %collective-permute-done.49, bf16[2560,512]{1,0:T(8,128)(2,1)S(1)} %copy-done.2, bf16[2560,2048]{1,0:T(8,128)(2,1)S(1)} %bitcast.104), kind=kOutput, calls=%fused_computation.3 | convolution fusion | flops 5370806272 | bytes 19398656 | tf_op jit(solution)/shard_map/dot_general | solution.py:150
  686.3 14.2 %collective-permute-done.76 = f32[2,4,128]{2,1,0:T(4,128)S(1)} collective-permute-done((f32[2,4,128]{2,1,0:T(4,128)S(1)}, f32[2,4,128]{2,1,0:T(4,128)S(1)}, u32[]{:S(2)}, u32[]{:S(2)}) %collective-permute-start.76) | collective-permute-done | bytes 4128 | tf_op jit(solution)/shard_map/ppermute | solution.py:22
  706.7 9.2 %add_bitcast_fusion = f32[1,2048,512]{2,1,0:T(8,128)} fusion(bf16[2560,2048]{1,0:T(8,128)(2,1)S(1)} %bitcast.108, bf16[2560,512]{1,0:T(8,128)(2,1)S(1)} %copy-done.5, bf16[512,512]{1,0:T(8,128)(2,1)} %collective-permute-done.86, bf16[512,512]{1,0:T(8,128)(2,1)} %collective-permute-done.85, bf16[512,512]{1,0:T(8,128)(2,1)S(1)} %copy-done.51, ...), kind=kOutput, calls=%fused_computation.1 | convolution fusion | flops 5378146304 | bytes 19398656 | tf_op jit(solution)/shard_map/dot_general | solution.py:150
  715.9 2.1 fusion.8
  722.1 13.0 %collective-permute-done.80 = f32[160,2048]{1,0:T(8,128)S(1)} collective-permute-done((f32[160,2048]{1,0:T(8,128)S(1)}, f32[160,2048]{1,0:T(8,128)S(1)}, u32[]{:S(2)}, u32[]{:S(2)}) %collective-permute-start.80) | collective-permute-done | bytes 1310752 | tf_op jit(solution)/shard_map/ppermute | solution.py:26
  (397 shorter events, 130.9 us)
Async XLA Ops:
  7.2 101.6 %all-gather.5.cloned.1.call-start = ((), (), s32[]{:S(2)}) async-start(), calls=%async_computation.2 | async-start | bytes 18382848 | tf_op jit(solution)/shard_map/all_gather | solution.py:962
  12.6 200.9 %all-gather.7.cloned.1.call-start = ((), (), s32[]{:S(2)}) async-start(), calls=%async_computation.3 | async-start | bytes 11141120 | tf_op jit(solution)/shard_map/all_gather | solution.py:964
  15.0 561.5 %reduce-scatter.2.cloned.1.call-start = ((), (), s32[]{:S(2)}) async-start(), calls=%async_computation.1 | async-start | bytes 11141120 | tf_op jit(solution)/shard_map/reduce_scatter | solution.py:1087
  15.1 49.6 %collective-permute-start = (bf16[2048,512]{1,0:T(8,128)(2,1)S(1)}, bf16[2048,512]{1,0:T(8,128)(2,1)}, u32[]{:S(2)}, u32[]{:S(2)}) collective-permute-start(bf16[2048,512]{1,0:T(8,128)(2,1)S(1)} %bitcast.114), channel_id=1, source_target_pairs={{0,1},{1,0},{2,3},{3,2},{4,5},{5,4},{6,7},{7,6},{8,9},{9,8},{10,11... | collective-permute-start | bytes 6291464 | tf_op jit(solution)/shard_map/ppermute | solution.py:26
  18.1 90.7 %collective-permute-start.1 = (bf16[2048,512]{1,0:T(8,128)(2,1)}, bf16[2048,512]{1,0:T(8,128)(2,1)}, u32[]{:S(2)}, u32[]{:S(2)}) collective-permute-start(bf16[2048,512]{1,0:T(8,128)(2,1)} %bitcast.115), channel_id=1, source_target_pairs={{0,1},{1,0},{2,3},{3,2},{4,5},{5,4},{6,7},{7,6},{8,9},{9,8},{10,11... | collective-permute-start | bytes 6291464 | tf_op jit(solution)/shard_map/ppermute | solution.py:26
  132.3 76.9 %collective-permute-start.16 = (bf16[512,2048]{1,0:T(8,128)(2,1)S(1)}, bf16[512,2048]{1,0:T(8,128)(2,1)}, u32[]{:S(2)}, u32[]{:S(2)}) collective-permute-start(bf16[512,2048]{1,0:T(8,128)(2,1)S(1)} %bitcast.127), channel_id=1, source_target_pairs={{0,1},{1,0},{2,3},{3,2},{4,5},{5,4},{6,7},{7,6},{8,9},{9,8},{10,11... | collective-permute-start | bytes 6291464 | tf_op jit(solution)/shard_map/ppermute | solution.py:26
  147.2 15.3 %collective-permute-start.10 = (bf16[128,1024]{1,0:T(8,128)(2,1)}, bf16[128,1024]{1,0:T(8,128)(2,1)}, u32[]{:S(2)}, u32[]{:S(2)}) collective-permute-start(bf16[128,1024]{1,0:T(8,128)(2,1)} %slice.177), channel_id=1, source_target_pairs={{0,4},{2,6},{4,0},{6,2},{8,12},{10,14},{12,8},{14,10},{16,20},{18,... | collective-permute-start | bytes 786440 | tf_op jit(solution)/shard_map/ppermute | solution.py:22
  148.5 24.4 %collective-permute-start.12 = (bf16[128,1024]{1,0:T(8,128)(2,1)}, bf16[128,1024]{1,0:T(8,128)(2,1)}, u32[]{:S(2)}, u32[]{:S(2)}) collective-permute-start(bf16[128,1024]{1,0:T(8,128)(2,1)} %slice.177), channel_id=1, source_target_pairs={{0,8},{2,10},{4,12},{6,14},{8,0},{10,2},{12,4},{14,6},{16,24},{18,... | collective-permute-start | bytes 786440 | tf_op jit(solution)/shard_map/ppermute | solution.py:22
  151.2 21.7 %collective-permute-start.9 = (bf16[128,1024]{1,0:T(8,128)(2,1)}, bf16[128,1024]{1,0:T(8,128)(2,1)}, u32[]{:S(2)}, u32[]{:S(2)}) collective-permute-start(bf16[128,1024]{1,0:T(8,128)(2,1)} %slice.177), channel_id=1, source_target_pairs={{0,2},{2,0},{4,6},{6,4},{8,10},{10,8},{12,14},{14,12},{16,18},{18,... | collective-permute-start | bytes 786440 | tf_op jit(solution)/shard_map/ppermute | solution.py:22
  153.0 20.2 %collective-permute-start.7 = (bf16[128,1024]{1,0:T(8,128)(2,1)}, bf16[128,1024]{1,0:T(8,128)(2,1)}, u32[]{:S(2)}, u32[]{:S(2)}) collective-permute-start(bf16[128,1024]{1,0:T(8,128)(2,1)} %collective-permute-done.5.refs_3_), channel_id=1, source_target_pairs={{0,4},{2,6},{4,0},{6,2},{8,12},{10,14},{12,8},{14,10},{16,20},{18,... | collective-permute-start | bytes 786440 | tf_op jit(solution)/shard_map/ppermute | solution.py:22
  172.9 16.7 %collective-permute-start.14 = (bf16[128,1024]{1,0:T(8,128)(2,1)}, bf16[128,1024]{1,0:T(8,128)(2,1)}, u32[]{:S(2)}, u32[]{:S(2)}) collective-permute-start(bf16[128,1024]{1,0:T(8,128)(2,1)} %collective-permute-done.10.refs_8_), channel_id=1, source_target_pairs={{0,8},{2,10},{4,12},{6,14},{8,0},{10,2},{12,4},{14,6},{16,24},{18,... | collective-permute-start | bytes 786440 | tf_op jit(solution)/shard_map/ppermute | solution.py:22
  173.2 18.6 %collective-permute-start.11 = (bf16[128,1024]{1,0:T(8,128)(2,1)}, bf16[128,1024]{1,0:T(8,128)(2,1)}, u32[]{:S(2)}, u32[]{:S(2)}) collective-permute-start(bf16[128,1024]{1,0:T(8,128)(2,1)} %collective-permute-done.10.refs_8_), channel_id=1, source_target_pairs={{0,2},{2,0},{4,6},{6,4},{8,10},{10,8},{12,14},{14,12},{16,18},{18,... | collective-permute-start | bytes 786440 | tf_op jit(solution)/shard_map/ppermute | solution.py:22
  174.7 17.2 %collective-permute-start.13 = (bf16[128,1024]{1,0:T(8,128)(2,1)}, bf16[128,1024]{1,0:T(8,128)(2,1)}, u32[]{:S(2)}, u32[]{:S(2)}) collective-permute-start(bf16[128,1024]{1,0:T(8,128)(2,1)} %collective-permute-done.12.refs_10_), channel_id=1, source_target_pairs={{0,2},{2,0},{4,6},{6,4},{8,10},{10,8},{12,14},{14,12},{16,18},{18,... | collective-permute-start | bytes 786440 | tf_op jit(solution)/shard_map/ppermute | solution.py:22
  174.8 17.0 %collective-permute-start.8 = (bf16[128,1024]{1,0:T(8,128)(2,1)}, bf16[128,1024]{1,0:T(8,128)(2,1)}, u32[]{:S(2)}, u32[]{:S(2)}) collective-permute-start(bf16[128,1024]{1,0:T(8,128)(2,1)} %collective-permute-done.7.refs_5_), channel_id=1, source_target_pairs={{0,2},{2,0},{4,6},{6,4},{8,10},{10,8},{12,14},{14,12},{16,18},{18,... | collective-permute-start | bytes 786440 | tf_op jit(solution)/shard_map/ppermute | solution.py:22
  210.6 17.3 %collective-permute-start.17 = (bf16[160,2048]{1,0:T(8,128)(2,1)S(1)}, bf16[160,2048]{1,0:T(8,128)(2,1)S(1)}, u32[]{:S(2)}, u32[]{:S(2)}) collective-permute-start(bf16[160,2048]{1,0:T(8,128)(2,1)S(1)} %dynamic-slice_convert_fusion.1), channel_id=1, source_target_pairs={{0,1},{1,0},{2,3},{3,2},{4,5},{5,4},{6,7},{7,6},{8,9},{9,8},{10,11... | collective-permute-start | bytes 1966088 | tf_op jit(solution)/shard_map/ppermute | solution.py:26
  232.3 17.5 %collective-permute-start.19 = (bf16[160,2048]{1,0:T(8,128)(2,1)S(1)}, bf16[160,2048]{1,0:T(8,128)(2,1)}, u32[]{:S(2)}, u32[]{:S(2)}) collective-permute-start(bf16[160,2048]{1,0:T(8,128)(2,1)S(1)} %multiply_convert_fusion.1.refs_1_), channel_id=1, source_target_pairs={{0,8},{2,10},{8,16},{10,18},{16,24},{18,26},{24,28},{26,30},{28,20... | collective-permute-start | bytes 1966088 | tf_op jit(solution)/shard_map/ppermute | solution.py:45
  232.3 17.5 %collective-permute-start.20 = (bf16[160,2048]{1,0:T(8,128)(2,1)S(1)}, bf16[160,2048]{1,0:T(8,128)(2,1)S(1)}, u32[]{:S(2)}, u32[]{:S(2)}) collective-permute-start(bf16[160,2048]{1,0:T(8,128)(2,1)S(1)} %multiply_convert_fusion.1.refs_1_), channel_id=1, source_target_pairs={{8,0},{10,2},{16,8},{18,10},{24,16},{26,18},{28,24},{30,26},{20,28... | collective-permute-start | bytes 1966088 | tf_op jit(solution)/shard_map/ppermute | solution.py:49
  250.6 17.2 %collective-permute-start.22 = (bf16[160,2048]{1,0:T(8,128)(2,1)}, bf16[160,2048]{1,0:T(8,128)(2,1)}, u32[]{:S(2)}, u32[]{:S(2)}) collective-permute-start(bf16[160,2048]{1,0:T(8,128)(2,1)} %collective-permute-done.19.refs_1_), channel_id=1, source_target_pairs={{0,8},{2,10},{8,16},{10,18},{16,24},{18,26},{24,28},{26,30},{28,20... | collective-permute-start | bytes 1966088 | tf_op jit(solution)/shard_map/ppermute | solution.py:45
  251.4 16.4 %collective-permute-start.23 = (bf16[160,2048]{1,0:T(8,128)(2,1)}, bf16[160,2048]{1,0:T(8,128)(2,1)S(1)}, u32[]{:S(2)}, u32[]{:S(2)}) collective-permute-start(bf16[160,2048]{1,0:T(8,128)(2,1)} %copy-done.29), channel_id=1, source_target_pairs={{8,0},{10,2},{16,8},{18,10},{24,16},{26,18},{28,24},{30,26},{20,28... | collective-permute-start | bytes 1966088 | tf_op jit(solution)/shard_map/ppermute | solution.py:49
  252.7 16.3 %collective-permute-start.24 = (bf16[160,2048]{1,0:T(8,128)(2,1)}, bf16[160,2048]{1,0:T(8,128)(2,1)}, u32[]{:S(2)}, u32[]{:S(2)}) collective-permute-start(bf16[160,2048]{1,0:T(8,128)(2,1)} %collective-permute-done.19.refs_1_), channel_id=1, source_target_pairs={{0,2},{2,0},{4,6},{6,4},{8,10},{10,8},{12,14},{14,12},{16,18},{18,... | collective-permute-start | bytes 1966088 | tf_op jit(solution)/shard_map/ppermute | solution.py:22
  252.7 28.0 %collective-permute-start.25 = (bf16[160,2048]{1,0:T(8,128)(2,1)}, bf16[160,2048]{1,0:T(8,128)(2,1)}, u32[]{:S(2)}, u32[]{:S(2)}) collective-permute-start(bf16[160,2048]{1,0:T(8,128)(2,1)} %copy-done.29), channel_id=1, source_target_pairs={{0,2},{2,0},{4,6},{6,4},{8,10},{10,8},{12,14},{14,12},{16,18},{18,... | collective-permute-start | bytes 1966088 | tf_op jit(solution)/shard_map/ppermute | solution.py:22
  253.2 49.1 %collective-permute-start.29 = (f32[160,2048]{1,0:T(8,128)S(1)}, f32[160,2048]{1,0:T(8,128)}, u32[]{:S(2)}, u32[]{:S(2)}) collective-permute-start(f32[160,2048]{1,0:T(8,128)S(1)} %get-tuple-element.214), channel_id=1, source_target_pairs={{0,1},{1,0},{2,3},{3,2},{4,5},{5,4},{6,7},{7,6},{8,9},{9,8},{10,11... | collective-permute-start | bytes 3932168 | tf_op jit(solution)/shard_map/ppermute | solution.py:26
  267.9 34.4 %collective-permute-start.27 = (bf16[160,2048]{1,0:T(8,128)(2,1)}, bf16[160,2048]{1,0:T(8,128)(2,1)S(1)}, u32[]{:S(2)}, u32[]{:S(2)}) collective-permute-start(bf16[160,2048]{1,0:T(8,128)(2,1)} %collective-permute-done.22.refs_1_), channel_id=1, source_target_pairs={{0,8},{2,10},{8,16},{10,18},{16,24},{18,26},{24,28},{26,30},{28,20... | collective-permute-start | bytes 1966088 | tf_op jit(solution)/shard_map/ppermute | solution.py:45
  269.0 36.5 %collective-permute-start.30 = (bf16[160,2048]{1,0:T(8,128)(2,1)}, bf16[160,2048]{1,0:T(8,128)(2,1)}, u32[]{:S(2)}, u32[]{:S(2)}) collective-permute-start(bf16[160,2048]{1,0:T(8,128)(2,1)} %collective-permute-done.22.refs_1_), channel_id=1, source_target_pairs={{0,2},{2,0},{4,6},{6,4},{8,10},{10,8},{12,14},{14,12},{16,18},{18,... | collective-permute-start | bytes 1966088 | tf_op jit(solution)/shard_map/ppermute | solution.py:22
  269.0 33.3 %collective-permute-start.28 = (bf16[160,2048]{1,0:T(8,128)(2,1)S(1)}, bf16[160,2048]{1,0:T(8,128)(2,1)S(1)}, u32[]{:S(2)}, u32[]{:S(2)}) collective-permute-start(bf16[160,2048]{1,0:T(8,128)(2,1)S(1)} %collective-permute-done.23.refs_2_), channel_id=1, source_target_pairs={{8,0},{10,2},{16,8},{18,10},{24,16},{26,18},{28,24},{30,26},{20,28... | collective-permute-start | bytes 1966088 | tf_op jit(solution)/shard_map/ppermute | solution.py:49
  280.7 25.7 %collective-permute-start.31 = (bf16[160,2048]{1,0:T(8,128)(2,1)S(1)}, bf16[160,2048]{1,0:T(8,128)(2,1)}, u32[]{:S(2)}, u32[]{:S(2)}) collective-permute-start(bf16[160,2048]{1,0:T(8,128)(2,1)S(1)} %collective-permute-done.23.refs_2_), channel_id=1, source_target_pairs={{0,2},{2,0},{4,6},{6,4},{8,10},{10,8},{12,14},{14,12},{16,18},{18,... | collective-permute-start | bytes 1966088 | tf_op jit(solution)/shard_map/ppermute | solution.py:22
  303.1 27.6 %collective-permute-start.37 = (bf16[160,2048]{1,0:T(8,128)(2,1)S(1)}, bf16[160,2048]{1,0:T(8,128)(2,1)}, u32[]{:S(2)}, u32[]{:S(2)}) collective-permute-start(bf16[160,2048]{1,0:T(8,128)(2,1)S(1)} %collective-permute-done.27.refs_1_), channel_id=1, source_target_pairs={{0,2},{2,0},{4,6},{6,4},{8,10},{10,8},{12,14},{14,12},{16,18},{18,... | collective-permute-start | bytes 1966088 | tf_op jit(solution)/shard_map/ppermute | solution.py:22
  304.3 26.5 %collective-permute-start.38 = (bf16[160,2048]{1,0:T(8,128)(2,1)S(1)}, bf16[160,2048]{1,0:T(8,128)(2,1)}, u32[]{:S(2)}, u32[]{:S(2)}) collective-permute-start(bf16[160,2048]{1,0:T(8,128)(2,1)S(1)} %collective-permute-done.28.refs_2_), channel_id=1, source_target_pairs={{0,2},{2,0},{4,6},{6,4},{8,10},{10,8},{12,14},{14,12},{16,18},{18,... | collective-permute-start | bytes 1966088 | tf_op jit(solution)/shard_map/ppermute | solution.py:22
  304.4 23.8 %collective-permute-start.33 = (bf16[80,2048]{1,0:T(8,128)(2,1)}, bf16[80,2048]{1,0:T(8,128)(2,1)S(1)}, u32[]{:S(2)}, u32[]{:S(2)}) collective-permute-start(bf16[80,2048]{1,0:T(8,128)(2,1)} %slice.185), channel_id=1, source_target_pairs={{0,8},{2,10},{8,16},{10,18},{16,24},{18,26},{24,28},{26,30},{28,20... | collective-permute-start | bytes 983048 | tf_op jit(solution)/shard_map/ppermute | solution.py:45
  305.5 22.7 %collective-permute-start.34 = (bf16[80,2048]{1,0:T(8,128)(2,1)}, bf16[80,2048]{1,0:T(8,128)(2,1)}, u32[]{:S(2)}, u32[]{:S(2)}) collective-permute-start(bf16[80,2048]{1,0:T(8,128)(2,1)} %slice.186), channel_id=1, source_target_pairs={{8,0},{10,2},{16,8},{18,10},{24,16},{26,18},{28,24},{30,26},{20,28... | collective-permute-start | bytes 983048 | tf_op jit(solution)/shard_map/ppermute | solution.py:49
  329.4 102.6 %collective-permute-start.21 = (bf16[160,2048]{1,0:T(8,128)(2,1)}, bf16[160,2048]{1,0:T(8,128)(2,1)}, u32[]{:S(2)}, u32[]{:S(2)}) collective-permute-start(bf16[160,2048]{1,0:T(8,128)(2,1)} %get-tuple-element.192), channel_id=1, source_target_pairs={{0,2},{2,0},{4,6},{6,4},{8,10},{10,8},{12,14},{14,12},{16,18},{18,... | collective-permute-start | bytes 1966088 | tf_op jit(solution)/shard_map/ppermute | solution.py:22
  329.9 34.1 %collective-permute-start.26 = (bf16[320,2048]{1,0:T(8,128)(2,1)}, bf16[320,2048]{1,0:T(8,128)(2,1)}, u32[]{:S(2)}, u32[]{:S(2)}) collective-permute-start(bf16[320,2048]{1,0:T(8,128)(2,1)} %get-tuple-element.213), channel_id=1, source_target_pairs={{0,2},{2,0},{4,6},{6,4},{8,10},{10,8},{12,14},{14,12},{16,18},{18,... | collective-permute-start | bytes 3932168 | tf_op jit(solution)/shard_map/ppermute | solution.py:22
  330.6 37.7 %collective-permute-start.32 = (bf16[320,2048]{1,0:T(8,128)(2,1)}, bf16[320,2048]{1,0:T(8,128)(2,1)}, u32[]{:S(2)}, u32[]{:S(2)}) collective-permute-start(bf16[320,2048]{1,0:T(8,128)(2,1)} %get-tuple-element.226), channel_id=1, source_target_pairs={{0,2},{2,0},{4,6},{6,4},{8,10},{10,8},{12,14},{14,12},{16,18},{18,... | collective-permute-start | bytes 3932168 | tf_op jit(solution)/shard_map/ppermute | solution.py:22
  353.1 18.2 %collective-permute-start.39 = (bf16[320,2048]{1,0:T(8,128)(2,1)}, bf16[320,2048]{1,0:T(8,128)(2,1)S(1)}, u32[]{:S(2)}, u32[]{:S(2)}) collective-permute-start(bf16[320,2048]{1,0:T(8,128)(2,1)} %get-tuple-element.238), channel_id=1, source_target_pairs={{0,2},{2,0},{4,6},{6,4},{8,10},{10,8},{12,14},{14,12},{16,18},{18,... | collective-permute-start | bytes 3932168 | tf_op jit(solution)/shard_map/ppermute | solution.py:22
  364.1 70.6 %collective-permute-start.49 = (bf16[512,2048]{1,0:T(8,128)(2,1)}, bf16[512,2048]{1,0:T(8,128)(2,1)}, u32[]{:S(2)}, u32[]{:S(2)}) collective-permute-start(bf16[512,2048]{1,0:T(8,128)(2,1)} %convolution_convert_fusion.2), channel_id=1, source_target_pairs={{0,1},{1,0},{2,3},{3,2},{4,5},{5,4},{6,7},{7,6},{8,9},{9,8},{10,11... | collective-permute-start | bytes 6291464 | tf_op jit(solution)/shard_map/ppermute | solution.py:26
  377.9 15.5 %collective-permute-start.43 = (bf16[160,2048]{1,0:T(8,128)(2,1)S(1)}, bf16[160,2048]{1,0:T(8,128)(2,1)S(1)}, u32[]{:S(2)}, u32[]{:S(2)}) collective-permute-start(bf16[160,2048]{1,0:T(8,128)(2,1)S(1)} %pad_maximum_fusion.5), channel_id=1, source_target_pairs={{0,8},{2,10},{8,16},{10,18},{16,24},{18,26},{24,28},{26,30},{28,20... | collective-permute-start | bytes 1966088 | tf_op jit(solution)/shard_map/ppermute | solution.py:45
  379.6 15.1 %collective-permute-start.44 = (bf16[160,2048]{1,0:T(8,128)(2,1)S(1)}, bf16[160,2048]{1,0:T(8,128)(2,1)S(1)}, u32[]{:S(2)}, u32[]{:S(2)}) collective-permute-start(bf16[160,2048]{1,0:T(8,128)(2,1)S(1)} %pad_maximum_fusion.6), channel_id=1, source_target_pairs={{8,0},{10,2},{16,8},{18,10},{24,16},{26,18},{28,24},{30,26},{20,28... | collective-permute-start | bytes 1966088 | tf_op jit(solution)/shard_map/ppermute | solution.py:49
  387.0 47.8 %collective-permute-start.50 = (bf16[1024,512]{1,0:T(8,128)(2,1)}, bf16[1024,512]{1,0:T(8,128)(2,1)}, u32[]{:S(2)}, u32[]{:S(2)}) collective-permute-start(bf16[1024,512]{1,0:T(8,128)(2,1)} %slice.244), channel_id=1, source_target_pairs={{0,1},{1,0},{2,3},{3,2},{4,5},{5,4},{6,7},{7,6},{8,9},{9,8},{10,11... | collective-permute-start | bytes 3145736 | tf_op jit(solution)/shard_map/ppermute | solution.py:26
  412.4 19.6 %collective-permute-start.47 = (bf16[160,2048]{1,0:T(8,128)(2,1)}, bf16[160,2048]{1,0:T(8,128)(2,1)S(1)}, u32[]{:S(2)}, u32[]{:S(2)}) collective-permute-start(bf16[160,2048]{1,0:T(8,128)(2,1)} %get-tuple-element.245), channel_id=1, source_target_pairs={{0,8},{2,10},{8,16},{10,18},{16,24},{18,26},{24,28},{26,30},{28,20... | collective-permute-start | bytes 1966088 | tf_op jit(solution)/shard_map/ppermute | solution.py:45
  413.2 19.7 %collective-permute-start.48 = (bf16[160,2048]{1,0:T(8,128)(2,1)S(1)}, bf16[160,2048]{1,0:T(8,128)(2,1)}, u32[]{:S(2)}, u32[]{:S(2)}) collective-permute-start(bf16[160,2048]{1,0:T(8,128)(2,1)S(1)} %get-tuple-element.246), channel_id=1, source_target_pairs={{8,0},{10,2},{16,8},{18,10},{24,16},{26,18},{28,24},{30,26},{20,28... | collective-permute-start | bytes 1966088 | tf_op jit(solution)/shard_map/ppermute | solution.py:49
  438.0 15.8 %collective-permute-start.51 = (bf16[160,2048]{1,0:T(8,128)(2,1)S(1)}, bf16[160,2048]{1,0:T(8,128)(2,1)S(1)}, u32[]{:S(2)}, u32[]{:S(2)}) collective-permute-start(bf16[160,2048]{1,0:T(8,128)(2,1)S(1)} %get-tuple-element.379), channel_id=1, source_target_pairs={{0,1},{1,0},{2,3},{3,2},{4,5},{5,4},{6,7},{7,6},{8,9},{9,8},{10,11... | collective-permute-start | bytes 1966088 | tf_op jit(solution)/shard_map/ppermute | solution.py:26
  461.9 22.0 %collective-permute-start.55 = (bf16[512,512]{1,0:T(8,128)(2,1)S(1)}, bf16[512,512]{1,0:T(8,128)(2,1)}, u32[]{:S(2)}, u32[]{:S(2)}) collective-permute-start(bf16[512,512]{1,0:T(8,128)(2,1)S(1)} %get-tuple-element.264), channel_id=1, source_target_pairs={{0,1},{1,0},{2,3},{3,2},{4,5},{5,4},{6,7},{7,6},{8,9},{9,8},{10,11... | collective-permute-start | bytes 1572872 | tf_op jit(solution)/shard_map/ppermute | solution.py:26
  483.5 44.7 %collective-permute-start.53 = (bf16[320,2048]{1,0:T(8,128)(2,1)}, bf16[320,2048]{1,0:T(8,128)(2,1)}, u32[]{:S(2)}, u32[]{:S(2)}) collective-permute-start(bf16[320,2048]{1,0:T(8,128)(2,1)} %multiply_convert_fusion.refs_0_), channel_id=1, source_target_pairs={{0,2},{2,0},{4,6},{6,4},{8,10},{10,8},{12,14},{14,12},{16,18},{18,... | collective-permute-start | bytes 3932168 | tf_op jit(solution)/shard_map/ppermute | solution.py:22
  483.9 44.3 %collective-permute-start.54 = (bf16[320,2048]{1,0:T(8,128)(2,1)S(1)}, bf16[320,2048]{1,0:T(8,128)(2,1)}, u32[]{:S(2)}, u32[]{:S(2)}) collective-permute-start(bf16[320,2048]{1,0:T(8,128)(2,1)S(1)} %copy-done.11), channel_id=1, source_target_pairs={{0,2},{2,0},{4,6},{6,4},{8,10},{10,8},{12,14},{14,12},{16,18},{18,... | collective-permute-start | bytes 3932168 | tf_op jit(solution)/shard_map/ppermute | solution.py:22
  490.5 32.5 %collective-permute-start.63 = (bf16[2,128,1024]{2,1,0:T(8,128)(2,1)}, bf16[2,128,1024]{2,1,0:T(8,128)(2,1)}, u32[]{:S(2)}, u32[]{:S(2)}) collective-permute-start(bf16[2,128,1024]{2,1,0:T(8,128)(2,1)} %get-tuple-element.277), channel_id=1, source_target_pairs={{0,8},{2,10},{4,12},{6,14},{8,0},{10,2},{12,4},{14,6},{16,24},{18,... | collective-permute-start | bytes 1572872 | tf_op jit(solution)/shard_map/ppermute | solution.py:22
  491.5 31.5 %collective-permute-start.62 = (bf16[2,128,1024]{2,1,0:T(8,128)(2,1)}, bf16[2,128,1024]{2,1,0:T(8,128)(2,1)}, u32[]{:S(2)}, u32[]{:S(2)}) collective-permute-start(bf16[2,128,1024]{2,1,0:T(8,128)(2,1)} %get-tuple-element.276), channel_id=1, source_target_pairs={{0,4},{2,6},{4,0},{6,2},{8,12},{10,14},{12,8},{14,10},{16,20},{18,... | collective-permute-start | bytes 1572872 | tf_op jit(solution)/shard_map/ppermute | solution.py:22
  499.4 27.2 %collective-permute-start.52 = (bf16[320,512]{1,0:T(8,128)(2,1)S(1)}, bf16[320,512]{1,0:T(8,128)(2,1)S(1)}, u32[]{:S(2)}, u32[]{:S(2)}) collective-permute-start(bf16[320,512]{1,0:T(8,128)(2,1)S(1)} %constant_dynamic-slice_fusion.6), channel_id=1, source_target_pairs={{0,2},{2,0},{4,6},{6,4},{8,10},{10,8},{12,14},{14,12},{16,18},{18,... | collective-permute-start | bytes 983048 | tf_op jit(solution)/shard_map/ppermute | solution.py:22
  523.0 18.7 %collective-permute-start.57 = (bf16[512,512]{1,0:T(8,128)(2,1)S(1)}, bf16[512,512]{1,0:T(8,128)(2,1)}, u32[]{:S(2)}, u32[]{:S(2)}) collective-permute-start(bf16[512,512]{1,0:T(8,128)(2,1)S(1)} %get-tuple-element.267), channel_id=1, source_target_pairs={{0,1},{1,0},{2,3},{3,2},{4,5},{5,4},{6,7},{7,6},{8,9},{9,8},{10,11... | collective-permute-start | bytes 1572872 | tf_op jit(solution)/shard_map/ppermute | solution.py:26
  576.5 15.0 %collective-permute-start.69 = (bf16[256,1024]{1,0:T(8,128)(2,1)}, bf16[256,1024]{1,0:T(8,128)(2,1)S(1)}, u32[]{:S(2)}, u32[]{:S(2)}) collective-permute-start(bf16[256,1024]{1,0:T(8,128)(2,1)} %get-tuple-element.295), channel_id=1, source_target_pairs={{8,0},{10,2},{16,8},{18,10},{24,16},{26,18},{28,24},{30,26},{20,28... | collective-permute-start | bytes 1572872 | tf_op jit(solution)/shard_map/ppermute | solution.py:49
  592.1 25.0 %collective-permute-start.70 = (bf16[256,2048]{1,0:T(8,128)(2,1)S(1)}, bf16[256,2048]{1,0:T(8,128)(2,1)}, u32[]{:S(2)}, u32[]{:S(2)}) collective-permute-start(bf16[256,2048]{1,0:T(8,128)(2,1)S(1)} %pad_maximum_fusion.3), channel_id=1, source_target_pairs={{0,8},{2,10},{8,16},{10,18},{16,24},{18,26},{24,28},{26,30},{28,20... | collective-permute-start | bytes 3145736 | tf_op jit(solution)/shard_map/ppermute | solution.py:45
  594.4 24.5 %collective-permute-start.71 = (bf16[256,2048]{1,0:T(8,128)(2,1)S(1)}, bf16[256,2048]{1,0:T(8,128)(2,1)}, u32[]{:S(2)}, u32[]{:S(2)}) collective-permute-start(bf16[256,2048]{1,0:T(8,128)(2,1)S(1)} %pad_maximum_fusion.4), channel_id=1, source_target_pairs={{8,0},{10,2},{16,8},{18,10},{24,16},{26,18},{28,24},{30,26},{20,28... | collective-permute-start | bytes 3145736 | tf_op jit(solution)/shard_map/ppermute | solution.py:49
  594.5 31.3 %collective-permute-start.84 = (bf16[512,512]{1,0:T(8,128)(2,1)}, bf16[512,512]{1,0:T(8,128)(2,1)S(1)}, u32[]{:S(2)}, u32[]{:S(2)}) collective-permute-start(bf16[512,512]{1,0:T(8,128)(2,1)} %get-tuple-element.325), channel_id=1, source_target_pairs={{0,1},{1,0},{2,3},{3,2},{4,5},{5,4},{6,7},{7,6},{8,9},{9,8},{10,11... | collective-permute-start | bytes 1572872 | tf_op jit(solution)/shard_map/ppermute | solution.py:26
  622.9 32.1 %collective-permute-start.72 = (bf16[256,2048]{1,0:T(8,128)(2,1)}, bf16[256,2048]{1,0:T(8,128)(2,1)S(1)}, u32[]{:S(2)}, u32[]{:S(2)}) collective-permute-start(bf16[256,2048]{1,0:T(8,128)(2,1)} %get-tuple-element.301), channel_id=1, source_target_pairs={{0,8},{2,10},{8,16},{10,18},{16,24},{18,26},{24,28},{26,30},{28,20... | collective-permute-start | bytes 3145736 | tf_op jit(solution)/shard_map/ppermute | solution.py:45
  624.3 31.6 %collective-permute-start.73 = (bf16[256,2048]{1,0:T(8,128)(2,1)S(1)}, bf16[256,2048]{1,0:T(8,128)(2,1)}, u32[]{:S(2)}, u32[]{:S(2)}) collective-permute-start(bf16[256,2048]{1,0:T(8,128)(2,1)S(1)} %get-tuple-element.302), channel_id=1, source_target_pairs={{8,0},{10,2},{16,8},{18,10},{24,16},{26,18},{28,24},{30,26},{20,28... | collective-permute-start | bytes 3145736 | tf_op jit(solution)/shard_map/ppermute | solution.py:49
  625.0 90.9 %collective-permute-start.67 = (bf16[160,2048]{1,0:T(8,128)(2,1)}, bf16[160,2048]{1,0:T(8,128)(2,1)}, u32[]{:S(2)}, u32[]{:S(2)}) collective-permute-start(bf16[160,2048]{1,0:T(8,128)(2,1)} %reduce-scatter.2.cloned.1.call-done), channel_id=1, source_target_pairs={{0,1},{1,0},{2,3},{3,2},{4,5},{5,4},{6,7},{7,6},{8,9},{9,8},{10,11... | collective-permute-start | bytes 1966088 | tf_op jit(solution)/shard_map/ppermute | solution.py:26
  626.5 27.7 %collective-permute-start.85 = (bf16[512,512]{1,0:T(8,128)(2,1)}, bf16[512,512]{1,0:T(8,128)(2,1)}, u32[]{:S(2)}, u32[]{:S(2)}) collective-permute-start(bf16[512,512]{1,0:T(8,128)(2,1)} %get-tuple-element.326), channel_id=1, source_target_pairs={{0,1},{1,0},{2,3},{3,2},{4,5},{5,4},{6,7},{7,6},{8,9},{9,8},{10,11... | collective-permute-start | bytes 1572872 | tf_op jit(solution)/shard_map/ppermute | solution.py:26
  638.6 45.5 %collective-permute-start.79 = (bf16[160,2048]{1,0:T(8,128)(2,1)S(1)}, bf16[160,2048]{1,0:T(8,128)(2,1)S(1)}, u32[]{:S(2)}, u32[]{:S(2)}) collective-permute-start(bf16[160,2048]{1,0:T(8,128)(2,1)S(1)} %dynamic-slice_convert_fusion), channel_id=1, source_target_pairs={{0,1},{1,0},{2,3},{3,2},{4,5},{5,4},{6,7},{7,6},{8,9},{9,8},{10,11... | collective-permute-start | bytes 1966088 | tf_op jit(solution)/shard_map/ppermute | solution.py:26
  654.3 52.4 %collective-permute-start.86 = (bf16[512,512]{1,0:T(8,128)(2,1)}, bf16[512,512]{1,0:T(8,128)(2,1)}, u32[]{:S(2)}, u32[]{:S(2)}) collective-permute-start(bf16[512,512]{1,0:T(8,128)(2,1)} %get-tuple-element.327), channel_id=1, source_target_pairs={{0,1},{1,0},{2,3},{3,2},{4,5},{5,4},{6,7},{7,6},{8,9},{9,8},{10,11... | collective-permute-start | bytes 1572872 | tf_op jit(solution)/shard_map/ppermute | solution.py:26
  659.1 14.4 %collective-permute-start.74 = (f32[8,4,128]{2,1,0:T(4,128)S(1)}, f32[8,4,128]{2,1,0:T(4,128)S(1)}, u32[]{:S(2)}, u32[]{:S(2)}) collective-permute-start(f32[8,4,128]{2,1,0:T(4,128)S(1)} %dynamic-slice_bitcast_fusion), channel_id=1, source_target_pairs={{0,16},{2,18},{4,20},{6,22},{8,24},{10,26},{12,28},{14,30},{16,0},... | collective-permute-start | bytes 49160 | tf_op jit(solution)/shard_map/ppermute | solution.py:22
  683.0 36.7 %collective-permute-start.81 = (bf16[256,2048]{1,0:T(8,128)(2,1)S(1)}, bf16[256,2048]{1,0:T(8,128)(2,1)S(1)}, u32[]{:S(2)}, u32[]{:S(2)}) collective-permute-start(bf16[256,2048]{1,0:T(8,128)(2,1)S(1)} %get-tuple-element.316), channel_id=1, source_target_pairs={{0,8},{2,10},{8,16},{10,18},{16,24},{18,26},{24,28},{26,30},{28,20... | collective-permute-start | bytes 3145736 | tf_op jit(solution)/shard_map/ppermute | solution.py:45
  684.2 35.4 %collective-permute-start.82 = (bf16[256,2048]{1,0:T(8,128)(2,1)S(1)}, bf16[256,2048]{1,0:T(8,128)(2,1)S(1)}, u32[]{:S(2)}, u32[]{:S(2)}) collective-permute-start(bf16[256,2048]{1,0:T(8,128)(2,1)S(1)} %get-tuple-element.320), channel_id=1, source_target_pairs={{8,0},{10,2},{16,8},{18,10},{24,16},{26,18},{28,24},{30,26},{20,28... | collective-permute-start | bytes 3145736 | tf_op jit(solution)/shard_map/ppermute | solution.py:49
  685.3 15.3 %collective-permute-start.76 = (f32[2,4,128]{2,1,0:T(4,128)S(1)}, f32[2,4,128]{2,1,0:T(4,128)S(1)}, u32[]{:S(2)}, u32[]{:S(2)}) collective-permute-start(f32[2,4,128]{2,1,0:T(4,128)S(1)} %constant_dynamic-slice_fusion.3), channel_id=1, source_target_pairs={{0,4},{2,6},{4,0},{6,2},{8,12},{10,14},{12,8},{14,10},{16,20},{18,... | collective-permute-start | bytes 12296 | tf_op jit(solution)/shard_map/ppermute | solution.py:22
  705.3 29.7 %collective-permute-start.80 = (f32[160,2048]{1,0:T(8,128)S(1)}, f32[160,2048]{1,0:T(8,128)S(1)}, u32[]{:S(2)}, u32[]{:S(2)}) collective-permute-start(f32[160,2048]{1,0:T(8,128)S(1)} %fusion.6), channel_id=1, source_target_pairs={{0,1},{1,0},{2,3},{3,2},{4,5},{5,4},{6,7},{7,6},{8,9},{9,8},{10,11... | collective-permute-start | bytes 3932168 | tf_op jit(solution)/shard_map/ppermute | solution.py:26
  721.5 15.4 %collective-permute-start.83 = (f32[128,2048]{1,0:T(8,128)S(1)}, f32[128,2048]{1,0:T(8,128)S(1)}, u32[]{:S(2)}, u32[]{:S(2)}) collective-permute-start(f32[128,2048]{1,0:T(8,128)S(1)} %constant_dynamic-slice_fusion), channel_id=1, source_target_pairs={{0,2},{2,0},{4,6},{6,4},{8,10},{10,8},{12,14},{14,12},{16,18},{18,... | collective-permute-start | bytes 3145736 | tf_op jit(solution)/shard_map/ppermute | solution.py:22
  (90 other events, 1049.3 us)
Sparse Core Ops, SparseCore 0:
  12.7 94.2 all-gather.4
  109.9 99.6 all-gather.6
  434.9 132.7 reduce-scatter.1

commit v9 on v8

--- a/solution.py
+++ b/solution.py
@@ -13,6 +13,7 @@
 
 EPSILON = 1e-05
 VMEM = 60 * 1024 * 1024
+SOME = 32 * 1024 * 1024
 LOW = jnp.bfloat16
 FULL = jnp.float32
 
@@ -82,7 +83,7 @@
 
     def next(self, token):
         if self.stages:
-            return self.stages.pop(0)(lambda value: after(value, token), token)
+            self.stages.pop(0)(lambda value: after(value, token))
 
 
 def ring_sum(same, cross, fillers):
@@ -90,17 +91,16 @@
     rows = both[0].shape[0]
     cut = rows // 2
     right, left = ahead(both[4][:cut]), behind(both[4][cut:])
+    fillers.next(left)
     outward, inward = both[3][rows:], both[3][:rows]
     right = jnp.concatenate([add_low(outward[:cut], right), outward[cut:]], axis=0)
     left = jnp.concatenate([inward[:cut], add_low(inward[cut:], left)], axis=0)
-    right, left = together(right, left)
-    fillers.next((right, left))
     right, left = ahead(right), behind(left)
+    fillers.next(left)
     for hop in (2, 1):
-        right, left = add_low(both[hop][rows:], right), add_low(both[hop][:rows], left)
-        right, left = together(right, left)
-        fillers.next((right, left))
-        right, left = ahead(right), behind(left)
+        right = ahead(add_low(both[hop][rows:], right))
+        left = behind(add_low(both[hop][:rows], left))
+        fillers.next(left)
     return both[0].astype(FULL) + right.astype(FULL) + left.astype(FULL)
 
 
@@ -460,7 +460,7 @@
             pltpu.VMEM((count * rows, width), LOW),
             pltpu.SemaphoreType.DMA((count * parts + count,)),
         ],
-        compiler_params=pltpu.CompilerParams(vmem_limit_bytes=VMEM),
+        compiler_params=pltpu.CompilerParams(vmem_limit_bytes=SOME),
     )(blocks, packed)
 
 
@@ -507,7 +507,7 @@
         out_specs=[pl.BlockSpec((count, columns), lambda i: (0, 0)) for _ in outs],
         out_shape=outs,
         scratch_shapes=[pltpu.VMEM((count, columns), FULL)] * len(outs),
-        compiler_params=pltpu.CompilerParams(vmem_limit_bytes=VMEM),
+        compiler_params=pltpu.CompilerParams(vmem_limit_bytes=SOME),
         cost_estimate=pl.CostEstimate(
             flops=2 * count * width * columns * len(places),
             bytes_accessed=2 * width * columns * len(places) + 8 * count * columns,
@@ -536,7 +536,7 @@
         in_specs=[fixed] * len(rows) + pack_specs(gathered, places, steps, block),
         out_specs=pl.BlockSpec((count, width // steps), lambda i: (0, i)),
         out_shape=jax.ShapeDtypeStruct((count, width), FULL),
-        compiler_params=pltpu.CompilerParams(vmem_limit_bytes=VMEM),
+        compiler_params=pltpu.CompilerParams(vmem_limit_bytes=SOME),
         cost_estimate=pl.CostEstimate(
             flops=2 * count * width * columns * len(places),
             bytes_accessed=2 * width * columns * len(places) + 4 * count * width,
@@ -641,18 +641,17 @@
     part = lambda hop: blocks[HOPS.index(hop)]
     cut = blocks.shape[2] // 2
     right, left = ahead(right), behind(left)
+    fillers.next(left)
     outward, inward = part(3), part(-3)
     right = jnp.concatenate([add_low(outward[:, :cut], right), outward[:, cut:]], axis=1)
     left = jnp.concatenate([inward[:, :cut], add_low(inward[:, cut:], left)], axis=1)
-    right, left = together(right, left)
-    fillers.next((right, left))
     right, left = ahead(right), behind(left)
+    fillers.next(left)
+    token = left
     for hop in (2, 1):
-        right, left = add_low(part(hop), right), add_low(part(-hop), left)
-        right, left = together(right, left)
-        right, left = fillers.next((right, left)) or (right, left)
-        token = right
-        right, left = ahead(right), behind(left)
+        right, left = ahead(add_low(part(hop), right)), behind(add_low(part(-hop), left))
+        fillers.next(left)
+        token = left if hop == 2 else token
     return part(0).astype(FULL) + right.astype(FULL) + left.astype(FULL), token
 
 
@@ -848,7 +847,7 @@
             ),
         ),
         out_shape=jax.ShapeDtypeStruct((len(HOPS), 2, rows, width), LOW),
-        compiler_params=pltpu.CompilerParams(vmem_limit_bytes=VMEM),
+        compiler_params=pltpu.CompilerParams(vmem_limit_bytes=SOME),
         cost_estimate=pl.CostEstimate(
             flops=4 * count * columns * width,
             bytes_accessed=2 * (count * (2 * columns + width) + 2 * columns * width),
@@ -867,37 +866,34 @@
     )
     rows, pair = together(rows, swap(rows))
     left, right = ahead(rows), behind(rows)
-    waiting = swap_tensor(after(waiting, pair))
+    parts, crossed = cut_rows(waiting, 4), []
     same, cross = {}, {}
+    cross_over = lambda token: crossed.append(swap_tensor(after(parts[len(crossed)], token)))
+    cross_over(pair)
     (same[0], cross[0]), held = chunk([rows, pair], 6, None, size, size)
     left, right, same[0] = together(left, right, same[0])
-    pieces, crossed = [left, right], [swap(left), swap(right)]
+    pieces, got = [left, right], [swap(left), swap(right)]
     left, right = ahead(left), behind(right)
+    pieces[0], crossed[0] = together(pieces[0], crossed[0])
+    cross_over(pieces[0])
     (same[1],), held = chunk(pieces, 7, held, 2 * size)
     left, right, same[1] = together(left, right, same[1])
-    pieces, crossed = [left, right, *crossed], [swap(left), swap(right)]
+    pieces, got = [left, right, *got], [swap(left), swap(right)]
     left, right = ahead(left), behind(right)
+    pieces[0], crossed[1] = together(pieces[0], crossed[1])
+    cross_over(pieces[0])
     (same[2], cross[1]), held = chunk(pieces, 0, held, 2 * size, 2 * size)
-    left, right, waiting, same[2] = together(left, right, waiting, same[2])
-    pieces, crossed = [left, right, *crossed], [swap(left), swap(right)]
+    left, right, same[2] = together(left, right, same[2])
+    pieces, got = [left, right, *got], [swap(left), swap(right)]
     left, right = ahead(left[:cut]), behind(right[cut:])
+    pieces[0], crossed[2] = together(pieces[0], crossed[2])
+    cross_over(pieces[0])
     (same[3], cross[2]), held = chunk(pieces, 1, held, 2 * size, 2 * size)
-    left, right, same[3] = together(left, right, same[3])
-    pieces = [left, right, swap(left), swap(right), *crossed]
+    left, right, crossed[3], same[3] = together(left, right, crossed[3], same[3])
+    pieces = [left, right, swap(left), swap(right), *got]
     (same[4], cross[4], cross[3]), held = chunk(pieces, 2, held, size, size, 2 * size)
+    waiting = jnp.concatenate(crossed, axis=0)
     return same, cross, held, waiting
-
-
-def halving_sum(parts):
-    bits = parts.shape[0].bit_length() - 1
-    index = lax.axis_index("dp")
-    for bit in reversed(range(bits)):
-        rows = parts.shape[0] // 2
-        upper = index >> bit & 1
-        kept = lax.dynamic_slice_in_dim(parts, upper * rows, rows, axis=0)
-        sent = lax.dynamic_slice_in_dim(parts, (1 - upper) * rows, rows, axis=0)
-        parts = kept + swap_bit(sent, "dp", bit)
-    return parts[0]
 
 
 def body(
@@ -962,39 +958,6 @@
     gathered = lax.all_gather(packed, "dp", axis=0, tiled=False)
     cotangent_half = own_half(cotangent)
     gathered_back = lax.all_gather(cotangent_half.astype(LOW), "dp", axis=0, tiled=False)
-    gathered, *early = lax.optimization_barrier((gathered, gate_mats[1], up_mats[1]))
-    gate_mats, up_mats = (gate_mats[0], early[0]), (up_mats[0], early[1])
-    rest = gathered[:, 4 * block : 4 * block + 16]
-    gain_rows = rest[:, 0].astype(FULL)
-    gain_one, gain_two, gain_q, gain_k = (
-        gain_rows[:, j * block : (j + 1) * block].reshape(-1) for j in range(4)
-    )
-    gain_query_local = lax.dynamic_slice_in_dim(gain_q, side * local_width, local_width)
-    gain_key_local = lax.dynamic_slice_in_dim(gain_k, side * local_width, local_width)
-
-    names, *parts = (
-        rest[:, 8:, j * token_count : (j + 1) * token_count] for j in range(3)
-    )
-    weights = parts[0].astype(FULL) + parts[1].astype(FULL)
-    named = names == dp_index.astype(LOW)
-    picked = jnp.sum(named.astype(FULL), axis=1)
-    weight = jnp.sum(jnp.where(named, weights, 0.0), axis=1)
-    order = jnp.arange(token_count, dtype=jnp.int32)
-    earlier = (order[:, None] < order[None, :]).astype(LOW)
-    within = dot_nn(picked.astype(LOW), earlier)
-    per_row = jnp.sum(picked, axis=1)
-    rows_order = jnp.arange(dp_count, dtype=jnp.int32)
-    ahead = jnp.sum(
-        jnp.where(rows_order[None, :] < rows_order[:, None], per_row[None, :], 0.0), axis=1
-    )
-    kept = (picked > 0.0) & (within + ahead[:, None] < capacity)
-    weight = jnp.where(kept, weight, 0.0)
-    weight = lax.dynamic_slice_in_dim(weight, side * half_count, half_count, axis=1)
-    if ring:
-        blocks, chips = ring_blocks(dp_index), ring_chips(dp_index, HOPS)
-        weight = weight[blocks]
-    weight = weight.reshape(-1, 1)
-
     core = dp_index % 2
     tokens_f = inputs.astype(FULL)
     prompt_pos = dp_index % GROUP * PR_DEV + jnp.arange(PR_DEV, dtype=jnp.int32)
@@ -1012,6 +975,41 @@
     )
     allowed = jnp.concatenate([allowed_prompt, allowed_cont], axis=1)
     bias = jnp.where(allowed, 0.0, -1e30).astype(LOW)
+    gathered, cosine, sine, bias, *early = together(
+        gathered, cosine, sine, bias, gate_mats[1], up_mats[1]
+    )
+    gate_mats, up_mats = (gate_mats[0], early[0]), (up_mats[0], early[1])
+    rest = gathered[:, 4 * block : 4 * block + 16]
+    gain_rows = rest[:, 0].astype(FULL)
+    gain_one, gain_two, gain_q, gain_k = (
+        gain_rows[:, j * block : (j + 1) * block].reshape(-1) for j in range(4)
+    )
+    gain_query_local = lax.dynamic_slice_in_dim(gain_q, side * local_width, local_width)
+    gain_key_local = lax.dynamic_slice_in_dim(gain_k, side * local_width, local_width)
+
+    names, *parts = (
+        rest[:, 8:, j * token_count : (j + 1) * token_count] for j in range(3)
+    )
+    weights = parts[0].astype(FULL) + parts[1].astype(FULL)
+    named = names == dp_index.astype(LOW)
+    picked = jnp.sum(named.astype(FULL), axis=1)
+    weight = jnp.sum(jnp.where(named, weights, 0.0), axis=1)
+    order = jnp.arange(token_count, dtype=jnp.int32)
+    earlier = (order[:, None] < order[None, :]).astype(LOW)
+    within = dot_nn(picked.astype(LOW), earlier)
+    per_row = jnp.sum(picked, axis=1)
+    rows_order = jnp.arange(dp_count, dtype=jnp.int32)
+    ahead = jnp.sum(
+        jnp.where(rows_order[None, :] < rows_order[:, None], per_row[None, :], 0.0), axis=1
+    )
+    kept = (picked > 0.0) & (within + ahead[:, None] < capacity)
+    weight = jnp.where(kept, weight, 0.0)
+    weight = lax.dynamic_slice_in_dim(weight, side * half_count, half_count, axis=1)
+    if ring:
+        blocks, chips = ring_blocks(dp_index), ring_chips(dp_index, HOPS)
+        weight = weight[blocks]
+    weight = weight.reshape(-1, 1)
+
     normed_b = rms_norm(tokens_f, gain_one).astype(LOW)
     query_flat, key_flat, values_b = project(
         normed_b, gathered, block, (0, 1, 2), (FULL, FULL, LOW)
@@ -1055,13 +1053,13 @@
         down_got = swap_tensor(low_tn(h1, back_rows))
         late = {}
 
-        def gate_stage(gated, token):
+        def gate_stage(gated):
             late["gate"] = low_tn(gated(expert_in), g1)
 
-        def up_stage(gated, token):
+        def up_stage(gated):
             late["up"] = low_tn(gated(expert_in), u1)
 
-        def mixed_stage(gated, token):
+        def mixed_stage(gated):
             late["mixed"] = mixed_pass(gated(h0), h1, down_mats, chips, core[None])
 
         fillers = Fillers(gate_stage, up_stage, mixed_stage)
@@ -1093,8 +1091,7 @@
     attn_grad_b = both_halves(attn_grad_half, swap_tensor(attn_grad_half))
     attn_grad_b, gate_sent, up_sent = together(attn_grad_b, gate_sent, up_sent)
     (context_grad_b,) = project(attn_grad_b, gathered, block, (3,), (LOW,))
-    gate_pieces, up_pieces = cut_rows(gate_sent, 4), cut_rows(up_sent, 4)
-    soon = swap_in_turn([*gate_pieces[2:], up_pieces[0]], context_grad_b)
+    soon = swap_in_turn([lower(gate_sent), upper(up_sent)], context_grad_b)
     if ring:
         pair = lambda own: (own, swap_bit(own, "dp", 0))
         columns = local_width // 2
@@ -1127,7 +1124,7 @@
         (key_flat, key_normed_grad, gain_key_local[None], key_scale, key_inner[:, None]),
         value_pre_grad,
     )
-    gate_got = jnp.concatenate([gate_first, *soon[:2]], axis=0)
+    gate_got = jnp.concatenate([gate_first, soon[0]], axis=0)
     pre_grads = (query_pre_grad, key_pre_grad, value_pre_grad)
     grad_sum = lambda left, right, got: dot_tn(left, right) + got.astype(FULL)
     back_all = lambda *grads: project_back(grads, gathered, block, (0, 1, 2))
@@ -1153,8 +1150,9 @@
         grads = jnp.stack(
             [gain_one_grad, gain_two_grad, wide(query_gain_part[0]), wide(key_gain_part[0])]
         ).reshape(4, dp_count, block)
-        sums = halving_sum(jnp.swapaxes(grads, 0, 1))
-        return sums + swap_tensor(sums)
+        grads = jnp.swapaxes(grads, 0, 1).reshape(dp_count, 4 * block)
+        sums = jnp.sum(lax.all_to_all(grads, "dp", 0, 0, tiled=True), axis=0)
+        return (sums + swap_tensor(sums)).reshape(4, block)
 
     if ring:
         pre_got = swap_bit(pre_sent, "dp", 0)
@@ -1169,27 +1167,27 @@
             context_got,
         )
         w_blocks, mixed, *far = together(w_blocks, mixed, *far)
-        up_got = jnp.concatenate([soon[2], *swap_in_turn(up_pieces[1:], far[0])], axis=0)
+        up_got = jnp.concatenate(
+            [soon[1], *swap_in_turn(cut_rows(lower(up_sent), 2), far[0])], axis=0
+        )
         mixed_other = swap_tensor(mixed)
         late = {}
 
-        def normed_stage(gated, token):
+        def normed_stage(gated):
             late["normed"] = share(back_all(*[gated(grad) for grad in pre_grads]))
 
-        def expert_stage(gated, token):
+        def expert_stage(gated):
             late["down"] = grad_sum(gated(h0), back_rows, down_got)
             late["gate"] = grad_sum(gated(expert_in), g0, gate_got)
 
-        def input_stage(gated, token):
-            late["down"], late["gate"], *token = together(late["down"], late["gate"], *token)
+        def input_stage(gated):
             late["input"] = input_side(late["normed"][0], gated(late["normed"][1]))
             late["gains"] = gain_side(gated(late["normed"][2]))
-            return token
 
         fillers = Fillers(normed_stage, expert_stage, input_stage)
         w_half, token = ring_weights(w_blocks, *far, fillers)
         input_half, input_other = late["input"]
-        gain_sums, token = together(late["gains"], token)
+        gain_sums = late["gains"]
         down_grad, gate_w_grad = late["down"], late["gate"]
         up_w_grad = grad_sum(after(expert_in, token), u0, up_got)
         own_w = lax.dynamic_slice_in_dim(w_half, core * block, block, axis=0)
@@ -1210,7 +1208,7 @@
         w_sums = [w_sum[:, j * local_width : (j + 1) * local_width] for j in range(4)]
         down_grad = grad_sum(h0, back_rows, down_got)
         gate_w_grad = grad_sum(expert_in, g0, gate_got)
-        up_got = jnp.concatenate([soon[2], *map(swap_tensor, up_pieces[1:])], axis=0)
+        up_got = jnp.concatenate([soon[1], swap_tensor(lower(up_sent))], axis=0)
         up_w_grad = grad_sum(expert_in, u0, up_got)
         mixed_other = swap_tensor(mixed)
         *normed_parts, gain_one_grad = share(back_all(*pre_grads))

time: 757 us -> 715 us (0.945)
  waiting for transfers between devices: 282 us -> 226 us
  local copies, waits for them, and re-layouts: 30.9 us -> 69.5 us
  Pallas kernels: 215 us -> 198 us
    unnamed x130 -> x208, local copies, waits for them, and re-layouts: 8.12 us -> 47.7 us
    ppermute x12, waiting for transfers between devices: 37.1 us -> 1.95 us  [ahead(): return lax.ppermute(block, 'dp', AHEAD)]
    ppermute x18 -> x19, waiting for transfers between devices: 139 us -> 115 us  [swap_tensor(): return lax.ppermute(block, 'tensor', [(0, 1), (1, 0)])]
    ppermute x12, waiting for transfers between devices: 15.6 us -> 36.7 us  [behind(): return lax.ppermute(block, 'dp', BEHIND)]
    ppermute x45 -> x41, waiting for transfers between devices: 90.3 us -> 72.5 us  [swap_bit(): return lax.ppermute(block, axis, [(i, i ^ 1 << bit) for i in range(count)])]
    ppermute x45 -> x41, starting transfers between devices: 20.9 us -> 17.7 us  [swap_bit(): return lax.ppermute(block, axis, [(i, i ^ 1 << bit) for i in range(count)])]
    ppermute x18 -> x19, starting transfers between devices: 21.1 us -> 22.5 us  [swap_tensor(): return lax.ppermute(block, 'tensor', [(0, 1), (1, 0)])]
  transfers between devices with their start and end apart: 90 -> 88, of which waited for: 34 -> 29; matrix products, arithmetic and copies ran while one was open for 17% -> 17% of each run, Pallas kernels for 28% -> 28%
where the time goes in v9:
time: 715 us; the launch traced here: 708 us
  waiting for transfers between devices  226 us (32%)
  Pallas kernels  198 us (28%)
  starting transfers between devices  72.7 us (10%)
  local copies, waits for them, and re-layouts  69.5 us (10%)
  matrix products  54.6 us (8%)
  other arithmetic  52.6 us (7%)
  blocking collectives  18.4 us (3%)
  between operations  15.6 us (2%)
    ppermute x19, waiting for transfers between devices, swap_tensor(): return lax.ppermute(block, 'tensor', [(0, 1), (1, 0)])  115 us
    pallas_call x5, Pallas kernels, expert_chunk(): pl.pallas_call(lambda *refs: chunk_kernel(len(pieces), len(held), at, spl...  92.3 us
    ppermute x41, waiting for transfers between devices, swap_bit(): return lax.ppermute(block, axis, [(i, i ^ 1 << bit) for i in range(count)])  72.5 us
    dot_general x6, matrix products, dot_tn(): lax.dot_general(left, right, (((0,), (0,)), ((), ())), preferred_element_...  54.5 us
    unnamed x208, local copies, waits for them, and re-layouts  47.7 us
    ppermute x12, waiting for transfers between devices, behind(): return lax.ppermute(block, 'dp', BEHIND)  36.7 us
    ppermute x19, starting transfers between devices, swap_tensor(): return lax.ppermute(block, 'tensor', [(0, 1), (1, 0)])  22.5 us
    pallas_call x1, Pallas kernels, attend_back(): pl.pallas_call(attend_back_kernel, grid=(width // HEAD // PAIR,), in_spec...  19.8 us
  transfers between devices with their start and end apart: 88, of which 29 were waited for; matrix products, arithmetic and copies ran while one was open for 17% of the time, Pallas kernels for 28%

profile of v9, /device:TPU:0, one launch (start us, length us, event | category | flops | bytes accessed | tf_op | source)
XLA Modules:
  0.0 708.4 jit_solution(4239442915707088893)
XLA Ops:
  10.1 2.4 shard_map.309
  12.7 2.3 dynamic-slice_convert_fusion.2
  15.1 3.0 collective-permute-start
  22.0 42.6 %collective-permute-done.refs_5_.refs_7_.refs_9_ = bf16[2048,512]{1,0:T(8,128)(2,1)} collective-permute-done((bf16[2048,512]{1,0:T(8,128)(2,1)S(1)}, bf16[2048,512]{1,0:T(8,128)(2,1)}, u32[]{:S(2)}, u32[]{:S(2)}) %collective-permute-start) | collective-permute-done | bytes 2097184 | tf_op jit(solution)/shard_map/ppermute | solution.py:27
  64.7 44.1 %collective-permute-done.1.refs_7_.refs_9_.refs_11_ = bf16[2048,512]{1,0:T(8,128)(2,1)} collective-permute-done((bf16[2048,512]{1,0:T(8,128)(2,1)}, bf16[2048,512]{1,0:T(8,128)(2,1)}, u32[]{:S(2)}, u32[]{:S(2)}) %collective-permute-start.1) | collective-permute-done | bytes 2097184 | tf_op jit(solution)/shard_map/ppermute | solution.py:27
  110.8 5.9 copy-done
  116.7 8.6 %shard_map.310 = (f32[320,1024]{1,0:T(8,128)S(1)}, f32[320,1024]{1,0:T(8,128)S(1)}, bf16[320,1024]{1,0:T(8,128)(2,1)S(1)}) custom-call(bf16[320,2048]{1,0:T(8,128)(2,1)S(1)} %multiply_convert_fusion.refs_0_, bf16[16,528,1024]{2,1,0:T(8,128)(2,1)S(1)} %bitcast.86, bf16[16,528,1024]{2,1,0:T(8,128)(2,1)S(1)} %bitcast.87, bf16[16,528,1024]{2,1,0:T(8,128)(2,1)S(1)} %bitcast.88), custom_call_target="tpu_custom_call" | custom-call | flops 4026531840 | bytes 15204352 | tf_op jit(solution)/shard_map/pallas_call | solution.py:502
  127.3 5.5 all-reduce.4
  135.9 2.6 shard_map.311.k_ref
  143.8 4.0 collective-permute-done.5.refs_3_
  148.4 2.7 collective-permute-done.3.refs_1_
  152.5 2.4 collective-permute-start.7
  154.9 6.1 collective-permute-done.10.refs_8_
  161.0 9.7 %collective-permute-done.12.refs_10_ = bf16[128,1024]{1,0:T(8,128)(2,1)S(1)} collective-permute-done((bf16[128,1024]{1,0:T(8,128)(2,1)}, bf16[128,1024]{1,0:T(8,128)(2,1)S(1)}, u32[]{:S(2)}, u32[]{:S(2)}) %collective-permute-start.12) | collective-permute-done | bytes 262176 | tf_op jit(solution)/shard_map/ppermute | solution.py:23
  172.8 15.6 %collective-permute-done.14.refs_12_ = bf16[128,1024]{1,0:T(8,128)(2,1)} collective-permute-done((bf16[128,1024]{1,0:T(8,128)(2,1)S(1)}, bf16[128,1024]{1,0:T(8,128)(2,1)}, u32[]{:S(2)}, u32[]{:S(2)}) %collective-permute-start.14) | collective-permute-done | bytes 262176 | tf_op jit(solution)/shard_map/ppermute | solution.py:23
  190.6 11.9 %shard_map.312.refs_0_.refs_8_ = bf16[320,1024]{1,0:T(8,128)(2,1)} custom-call(f32[320,1024]{1,0:T(8,128)} %copy-done.12, f32[1,1024]{1,0:T(1,128)} %bitcast.123, f32[320,1]{1,0:T(8,128)} %broadcast_in_dim.137.scale_ref.refs_3_, f32[320,128]{1,0:T(8,128)} %get-tuple-element.165.cos_ref.refs_5_, f32[320,128]{1,0:T(8,128)} %get-tuple-element.166.sin_ref.refs_6_, ...), custom_call_target="tpu_custom_call" | custom-call | tf_op jit(solution)/shard_map/pallas_call | solution.py:271
  202.5 6.2 copy-done.1
  209.8 2.6 shard_map.313
  214.0 3.2 collective-permute-start.17
  219.0 4.0 copy-done.13
  222.9 7.4 %shard_map.314.refs_3_.refs_5_.refs_7_ = bf16[2560,2048]{1,0:T(8,128)(2,1)S(1)} custom-call(s32[16]{0:T(128)S(1)} %get-tuple-element.379.refs_0_, bf16[16,160,2048]{2,1,0:T(8,128)(2,1)S(1)} %bitcast.103), custom_call_target="tpu_custom_call" | custom-call | tf_op jit(solution)/shard_map/pallas_call | solution.py:454
  230.4 4.0 copy-done.4
  242.4 13.7 %shard_map.315 = (bf16[160,2048]{1,0:T(8,128)(2,1)}, bf16[160,2048]{1,0:T(8,128)(2,1)}, bf16[2560,2048]{1,0:T(8,128)(2,1)}, bf16[2560,512]{1,0:T(8,128)(2,1)}, b...) custom-call(f32[2560,1]{1,0:T(8,128)} %copy.91.refs_0_, ...), custom_call_target="tpu_custom_call" | custom-call | flops 6710886400 | bytes 19791872 | tf_op jit(solution)/shard_map/pallas_call | solution.py:787
  260.2 13.7 %shard_map.316 = (bf16[320,2048]{1,0:T(8,128)(2,1)}, bf16[2560,2048]{1,0:T(8,128)(2,1)}, bf16[2560,512]{1,0:T(8,128)(2,1)}, bf16[2560,512]{1,0:T(8,128)(2,1)}, b...) custom-call(f32[2560,1]{1,0:T(8,128)} %copy.91.refs_0_, ...), custom_call_target="tpu_custom_call", output_to_operand_aliasing={{1}: (10, {}), {2}: (11, {}), {3}: (12, {}), {4}: (13, {}),... | custom-call | flops 6710886400 | bytes 19791872 | tf_op jit(solution)/shard_map/pallas_call | solution.py:787
  277.8 21.5 %shard_map.317 = (bf16[320,2048]{1,0:T(8,128)(2,1)}, bf16[320,2048]{1,0:T(8,128)(2,1)}, bf16[2560,2048]{1,0:T(8,128)(2,1)}, bf16[2560,512]{1,0:T(8,128)(2,1)}, b...) custom-call(f32[2560,1]{1,0:T(8,128)} %copy.91.refs_0_, ...), custom_call_target="tpu_custom_call", output_to_operand_aliasing={{2}: (12, {}), {3}: (13, {}), {4}: (14, {}), {5}: (15, {}),... | custom-call | flops 13421772800 | bytes 27000832 | tf_op jit(solution)/shard_map/pallas_call | solution.py:787
  304.9 21.9 %shard_map.318 = (bf16[320,2048]{1,0:T(8,128)(2,1)}, bf16[320,2048]{1,0:T(8,128)(2,1)}, bf16[2560,2048]{1,0:T(8,128)(2,1)}, bf16[2560,512]{1,0:T(8,128)(2,1)}, b...) custom-call(f32[2560,1]{1,0:T(8,128)} %copy.91.refs_0_, ...), custom_call_target="tpu_custom_call", output_to_operand_aliasing={{2}: (12, {}), {3}: (13, {}), {4}: (14, {}), {5}: (15, {}),... | custom-call | flops 13421772800 | bytes 27000832 | tf_op jit(solution)/shard_map/pallas_call | solution.py:787
  330.8 21.5 %shard_map.319 = (bf16[160,2048]{1,0:T(8,128)(2,1)}, bf16[160,2048]{1,0:T(8,128)(2,1)}, bf16[320,2048]{1,0:T(8,128)(2,1)}, bf16[2560,2048]{1,0:T(8,128)(2,1)}, b...) custom-call(f32[2560,1]{1,0:T(8,128)} %copy.91.refs_0_, ...), custom_call_target="tpu_custom_call", output_to_operand_aliasing={{3}: (14, {}), {4}: (15, {}), {5}: (16, {}), {6}: (17, {}),... | custom-call | flops 13421772800 | bytes 27000832 | tf_op jit(solution)/shard_map/pallas_call | solution.py:787
  352.9 9.4 %convolution_convert_fusion.2 = bf16[512,2048]{1,0:T(8,128)(2,1)S(1)} fusion(bf16[2560,512]{1,0:T(8,128)(2,1)} %get-tuple-element.241.refs_2_.refs_3_, bf16[2560,2048]{1,0:T(8,128)(2,1)} %copy-done.4), kind=kOutput, calls=%fused_computation.6 | convolution fusion | flops 5369757696 | bytes 15204352 | tf_op jit(solution)/shard_map/dot_general | solution.py:150
  368.0 7.8 %collective-permute-done.48 = bf16[80,2048]{1,0:T(8,128)(2,1)S(1)} collective-permute-done((bf16[80,2048]{1,0:T(8,128)(2,1)S(1)}, bf16[80,2048]{1,0:T(8,128)(2,1)S(1)}, u32[]{:S(2)}, u32[]{:S(2)}) %collective-permute-start.48) | collective-permute-done | bytes 327712 | tf_op jit(solution)/shard_map/ppermute | solution.py:50
  378.9 5.9 convolution_convert_fusion.1
  385.9 6.5 collective-permute-done.49
  396.0 6.9 convolution_convert_fusion
  402.9 5.7 collective-permute-done.50
  412.0 14.7 %shard_map.320 = bf16[8,2,160,2048]{3,2,1,0:T(8,128)(2,1)S(1)} custom-call(s32[8]{0:T(128)S(1)} %compare_select_fusion.6.chip_ref, s32[8]{0:T(128)S(1)} %copy-done.27, s32[8]{0:T(128)S(1)} %copy-done.28, s32[1]{0:T(128)} %bitcast.15.core_ref, bf16[2560,512]{1,0:T(8,128)(2,1)S(1)} %copy-done.7, bf16[2560,512]{1,0:T(8,128)(2,1)S(1)} %copy-done.7, ...), custom_call_target="tpu_custom_call" | custom-call | flops 10737418240 | bytes 19922944 | tf_op jit(solution)/shard_map/pallas_call | solution.py:839
  426.8 3.8 copy-done.14
  430.6 2.6 convert_add_fusion.6
  434.2 2.2 multiply_reduce_fusion.2
  436.7 2.8 fusion.43
  440.8 14.7 %collective-permute-done.54 = bf16[160,2048]{1,0:T(8,128)(2,1)} collective-permute-done((bf16[160,2048]{1,0:T(8,128)(2,1)S(1)}, bf16[160,2048]{1,0:T(8,128)(2,1)}, u32[]{:S(2)}, u32[]{:S(2)}) %collective-permute-start.54) | collective-permute-done | bytes 655392 | tf_op jit(solution)/shard_map/ppermute | solution.py:27
  458.0 5.9 copy-done.2
  464.0 3.0 shard_map.321.refs_14_
  468.7 19.8 %shard_map.322 = (f32[320,1024]{1,0:T(8,128)}, f32[320,1]{1,0:T(8,128)}, f32[1,1024]{1,0:T(1,128)}, f32[320,1024]{1,0:T(8,128)}, f32[320,1024]{1,0:T(8,128)}, /*...) custom-call(f32[320,1024]{1,0:T(8,128)} %copy-done.12, ...), custom_call_target="tpu_custom_call" | custom-call | flops 20000000000 | bytes 40000000 | tf_op jit(solution)/shard_map/pallas_call | solution.py:330
  494.5 3.2 shard_map.323
  499.7 2.3 slice.214
  503.2 18.9 %collective-permute-done.65.refs_9_ = bf16[2,128,1024]{2,1,0:T(8,128)(2,1)} collective-permute-done((bf16[2,128,1024]{2,1,0:T(8,128)(2,1)}, bf16[2,128,1024]{2,1,0:T(8,128)(2,1)}, u32[]{:S(2)}, u32[]{:S(2)}) %collective-permute-start.65) | collective-permute-done | bytes 524320 | tf_op jit(solution)/shard_map/ppermute | solution.py:23
  527.8 5.3 collective-permute-done.67.refs_11_
  534.6 5.3 shard_map.324
  540.0 13.0 %all-reduce.3 = (f32[320,1]{1,0:T(8,128)}, f32[320,1]{1,0:T(8,128)}) all-reduce(f32[320,1]{1,0:T(8,128)} %get-tuple-element.261, f32[320,1]{1,0:T(8,128)} %get-tuple-element.274), channel_id=1, replica_groups=mesh['dp'=16,'tensor'=2] {'tensor'}, use_global_device_ids=true, to_apply=%region_13.14 | all-reduce | flops 640 | bytes 5120 | tf_op jit(solution)/shard_map/psum | solution.py:1114
  552.9 4.6 shard_map.325
  560.5 14.1 %shard_map.326 = (bf16[8,256,2048]{2,1,0:T(8,128)(2,1)}, bf16[256,1024]{1,0:T(8,128)(2,1)}, bf16[256,1024]{1,0:T(8,128)(2,1)}) custom-call(s32[8]{0:T(128)} %copy-done.26, s32[1]{0:T(128)} %bitcast.15.core_ref, bf16[320,2048]{1,0:T(8,128)(2,1)} %copy-done.18, bf16[320,2048]{1,0:T(8,128)(2,1)} %collective-permute-done.56.refs_1_, ...), custom_call_target="tpu_custom_call" | custom-call | flops 5368709120 | bytes 16252928 | tf_op jit(solution)/shard_map/pallas_call | solution.py:616
  579.9 9.1 %collective-permute-done.70 = bf16[256,1024]{1,0:T(8,128)(2,1)S(1)} collective-permute-done((bf16[256,1024]{1,0:T(8,128)(2,1)}, bf16[256,1024]{1,0:T(8,128)(2,1)S(1)}, u32[]{:S(2)}, u32[]{:S(2)}) %collective-permute-start.70) | collective-permute-done | bytes 524320 | tf_op jit(solution)/shard_map/ppermute | solution.py:50
  590.5 2.2 collective-permute-start.77
  594.9 5.9 copy-done.3
  600.8 5.9 shard_map.327
  609.4 5.9 collective-permute-done.71
  615.3 2.6 fusion.1
  620.1 11.9 %add_bitcast_fusion.2 = f32[1,2048,512]{2,1,0:T(8,128)} fusion(bf16[2560,2048]{1,0:T(8,128)(2,1)} %get-tuple-element.304, bf16[2560,512]{1,0:T(8,128)(2,1)S(1)} %copy-done.33, bf16[1024,512]{1,0:T(8,128)(2,1)} %collective-permute-done.58, bf16[1024,512]{1,0:T(8,128)(2,1)S(1)} %copy-done.92), kind=kOutput, calls=%fused_computation.3 | convolution fusion | flops 5373952000 | bytes 19398656 | tf_op jit(solution)/shard_map/dot_general | solution.py:150
  632.1 8.3 %add_bitcast_fusion = f32[1,512,2048]{2,1,0:T(8,128)} fusion(bf16[512,2048]{1,0:T(8,128)(2,1)} %collective-permute-done.52, bf16[2560,512]{1,0:T(8,128)(2,1)S(1)} %copy-done.7, bf16[2560,2048]{1,0:T(8,128)(2,1)S(1)} %bitcast.95), kind=kOutput, calls=%fused_computation.1 | convolution fusion | flops 5370806272 | bytes 19398656 | tf_op jit(solution)/shard_map/dot_general | solution.py:150
  642.3 3.7 fusion.2
  648.7 5.8 all-to-all-start
  656.6 2.9 fusion.6
  659.7 12.0 %add_bitcast_fusion.1 = f32[1,2048,512]{2,1,0:T(8,128)} fusion(bf16[2560,2048]{1,0:T(8,128)(2,1)} %get-tuple-element.304, bf16[2560,512]{1,0:T(8,128)(2,1)S(1)} %copy-done.35, bf16[512,512]{1,0:T(8,128)(2,1)} %collective-permute-done.83, bf16[512,512]{1,0:T(8,128)(2,1)S(1)} %copy-done.94, bf16[1024,512]{1,0:T(8,128)(2,1)} %collective-permute-done.59), kind=kOutput, calls=%fused_computation.2 | convolution fusion | flops 5376049152 | bytes 19398656 | tf_op jit(solution)/shard_map/dot_general | solution.py:150
  677.3 13.8 %collective-permute-done.75 = f32[512]{0:T(512)S(1)} collective-permute-done((f32[512]{0:T(512)S(1)}, f32[512]{0:T(512)S(1)}, u32[]{:S(2)}, u32[]{:S(2)}) %collective-permute-start.75) | collective-permute-done | bytes 2080 | tf_op jit(solution)/shard_map/ppermute | solution.py:27
  691.1 2.4 fusion.3
  (466 shorter events, 132.6 us)
Async XLA Ops:
  7.2 101.6 %all-gather.5.cloned.1.call-start = ((), (), s32[]{:S(2)}) async-start(), calls=%async_computation.3 | async-start | bytes 18382848 | tf_op jit(solution)/shard_map/all_gather | solution.py:958
  12.6 206.3 %all-gather.7.cloned.1.call-start = ((), (), s32[]{:S(2)}) async-start(), calls=%async_computation.4 | async-start | bytes 11141120 | tf_op jit(solution)/shard_map/all_gather | solution.py:960
  15.0 559.7 %reduce-scatter.2.cloned.1.call-start = ((), (), s32[]{:S(2)}) async-start(), calls=%async_computation.2 | async-start | bytes 11141120 | tf_op jit(solution)/shard_map/reduce_scatter | solution.py:1085
  15.1 49.6 %collective-permute-start = (bf16[2048,512]{1,0:T(8,128)(2,1)S(1)}, bf16[2048,512]{1,0:T(8,128)(2,1)}, u32[]{:S(2)}, u32[]{:S(2)}) collective-permute-start(bf16[2048,512]{1,0:T(8,128)(2,1)S(1)} %bitcast.112), channel_id=1, source_target_pairs={{0,1},{1,0},{2,3},{3,2},{4,5},{5,4},{6,7},{7,6},{8,9},{9,8},{10,11... | collective-permute-start | bytes 6291464 | tf_op jit(solution)/shard_map/ppermute | solution.py:27
  18.1 90.7 %collective-permute-start.1 = (bf16[2048,512]{1,0:T(8,128)(2,1)}, bf16[2048,512]{1,0:T(8,128)(2,1)}, u32[]{:S(2)}, u32[]{:S(2)}) collective-permute-start(bf16[2048,512]{1,0:T(8,128)(2,1)} %bitcast.113), channel_id=1, source_target_pairs={{0,1},{1,0},{2,3},{3,2},{4,5},{5,4},{6,7},{7,6},{8,9},{9,8},{10,11... | collective-permute-start | bytes 6291464 | tf_op jit(solution)/shard_map/ppermute | solution.py:27
  132.7 79.7 %collective-permute-start.16 = (bf16[512,2048]{1,0:T(8,128)(2,1)S(1)}, bf16[512,2048]{1,0:T(8,128)(2,1)}, u32[]{:S(2)}, u32[]{:S(2)}) collective-permute-start(bf16[512,2048]{1,0:T(8,128)(2,1)S(1)} %bitcast.101), channel_id=1, source_target_pairs={{0,1},{1,0},{2,3},{3,2},{4,5},{5,4},{6,7},{7,6},{8,9},{9,8},{10,11... | collective-permute-start | bytes 6291464 | tf_op jit(solution)/shard_map/ppermute | solution.py:27
  143.3 17.7 %collective-permute-start.10 = (bf16[128,1024]{1,0:T(8,128)(2,1)}, bf16[128,1024]{1,0:T(8,128)(2,1)S(1)}, u32[]{:S(2)}, u32[]{:S(2)}) collective-permute-start(bf16[128,1024]{1,0:T(8,128)(2,1)} %slice.190), channel_id=1, source_target_pairs={{0,4},{2,6},{4,0},{6,2},{8,12},{10,14},{12,8},{14,10},{16,20},{18,... | collective-permute-start | bytes 786440 | tf_op jit(solution)/shard_map/ppermute | solution.py:23
  147.8 22.9 %collective-permute-start.12 = (bf16[128,1024]{1,0:T(8,128)(2,1)}, bf16[128,1024]{1,0:T(8,128)(2,1)S(1)}, u32[]{:S(2)}, u32[]{:S(2)}) collective-permute-start(bf16[128,1024]{1,0:T(8,128)(2,1)} %slice.190), channel_id=1, source_target_pairs={{0,8},{2,10},{4,12},{6,14},{8,0},{10,2},{12,4},{14,6},{16,24},{18,... | collective-permute-start | bytes 786440 | tf_op jit(solution)/shard_map/ppermute | solution.py:23
  151.1 19.6 %collective-permute-start.9 = (bf16[128,1024]{1,0:T(8,128)(2,1)}, bf16[128,1024]{1,0:T(8,128)(2,1)}, u32[]{:S(2)}, u32[]{:S(2)}) collective-permute-start(bf16[128,1024]{1,0:T(8,128)(2,1)} %slice.190), channel_id=1, source_target_pairs={{0,2},{2,0},{4,6},{6,4},{8,10},{10,8},{12,14},{14,12},{16,18},{18,... | collective-permute-start | bytes 786440 | tf_op jit(solution)/shard_map/ppermute | solution.py:23
  152.5 18.6 %collective-permute-start.7 = (bf16[128,1024]{1,0:T(8,128)(2,1)S(1)}, bf16[128,1024]{1,0:T(8,128)(2,1)}, u32[]{:S(2)}, u32[]{:S(2)}) collective-permute-start(bf16[128,1024]{1,0:T(8,128)(2,1)S(1)} %collective-permute-done.5.refs_3_), channel_id=1, source_target_pairs={{0,4},{2,6},{4,0},{6,2},{8,12},{10,14},{12,8},{14,10},{16,20},{18,... | collective-permute-start | bytes 786440 | tf_op jit(solution)/shard_map/ppermute | solution.py:23
  170.7 17.7 %collective-permute-start.14 = (bf16[128,1024]{1,0:T(8,128)(2,1)S(1)}, bf16[128,1024]{1,0:T(8,128)(2,1)}, u32[]{:S(2)}, u32[]{:S(2)}) collective-permute-start(bf16[128,1024]{1,0:T(8,128)(2,1)S(1)} %collective-permute-done.10.refs_8_), channel_id=1, source_target_pairs={{0,8},{2,10},{4,12},{6,14},{8,0},{10,2},{12,4},{14,6},{16,24},{18,... | collective-permute-start | bytes 786440 | tf_op jit(solution)/shard_map/ppermute | solution.py:23
  171.1 19.5 %collective-permute-start.11 = (bf16[128,1024]{1,0:T(8,128)(2,1)S(1)}, bf16[128,1024]{1,0:T(8,128)(2,1)}, u32[]{:S(2)}, u32[]{:S(2)}) collective-permute-start(bf16[128,1024]{1,0:T(8,128)(2,1)S(1)} %collective-permute-done.10.refs_8_), channel_id=1, source_target_pairs={{0,2},{2,0},{4,6},{6,4},{8,10},{10,8},{12,14},{14,12},{16,18},{18,... | collective-permute-start | bytes 786440 | tf_op jit(solution)/shard_map/ppermute | solution.py:23
  172.3 18.3 %collective-permute-start.13 = (bf16[128,1024]{1,0:T(8,128)(2,1)S(1)}, bf16[128,1024]{1,0:T(8,128)(2,1)}, u32[]{:S(2)}, u32[]{:S(2)}) collective-permute-start(bf16[128,1024]{1,0:T(8,128)(2,1)S(1)} %collective-permute-done.12.refs_10_), channel_id=1, source_target_pairs={{0,2},{2,0},{4,6},{6,4},{8,10},{10,8},{12,14},{14,12},{16,18},{18,... | collective-permute-start | bytes 786440 | tf_op jit(solution)/shard_map/ppermute | solution.py:23
  172.4 18.1 %collective-permute-start.8 = (bf16[128,1024]{1,0:T(8,128)(2,1)}, bf16[128,1024]{1,0:T(8,128)(2,1)}, u32[]{:S(2)}, u32[]{:S(2)}) collective-permute-start(bf16[128,1024]{1,0:T(8,128)(2,1)} %collective-permute-done.7.refs_5_), channel_id=1, source_target_pairs={{0,2},{2,0},{4,6},{6,4},{8,10},{10,8},{12,14},{14,12},{16,18},{18,... | collective-permute-start | bytes 786440 | tf_op jit(solution)/shard_map/ppermute | solution.py:23
  214.0 20.4 %collective-permute-start.17 = (bf16[160,2048]{1,0:T(8,128)(2,1)S(1)}, bf16[160,2048]{1,0:T(8,128)(2,1)S(1)}, u32[]{:S(2)}, u32[]{:S(2)}) collective-permute-start(bf16[160,2048]{1,0:T(8,128)(2,1)S(1)} %dynamic-slice_convert_fusion.1), channel_id=1, source_target_pairs={{0,1},{1,0},{2,3},{3,2},{4,5},{5,4},{6,7},{7,6},{8,9},{9,8},{10,11... | collective-permute-start | bytes 1966088 | tf_op jit(solution)/shard_map/ppermute | solution.py:27
  237.0 19.1 %collective-permute-start.19 = (bf16[160,2048]{1,0:T(8,128)(2,1)S(1)}, bf16[160,2048]{1,0:T(8,128)(2,1)S(1)}, u32[]{:S(2)}, u32[]{:S(2)}) collective-permute-start(bf16[160,2048]{1,0:T(8,128)(2,1)S(1)} %multiply_convert_fusion.1.refs_1_), channel_id=1, source_target_pairs={{0,8},{2,10},{8,16},{10,18},{16,24},{18,26},{24,28},{26,30},{28,20... | collective-permute-start | bytes 1966088 | tf_op jit(solution)/shard_map/ppermute | solution.py:46
  237.0 19.1 %collective-permute-start.20 = (bf16[160,2048]{1,0:T(8,128)(2,1)S(1)}, bf16[160,2048]{1,0:T(8,128)(2,1)S(1)}, u32[]{:S(2)}, u32[]{:S(2)}) collective-permute-start(bf16[160,2048]{1,0:T(8,128)(2,1)S(1)} %multiply_convert_fusion.1.refs_1_), channel_id=1, source_target_pairs={{8,0},{10,2},{16,8},{18,10},{24,16},{26,18},{28,24},{30,26},{20,28... | collective-permute-start | bytes 1966088 | tf_op jit(solution)/shard_map/ppermute | solution.py:50
  241.7 17.3 %collective-permute-start.24 = (f32[40,2048]{1,0:T(8,128)}, f32[40,2048]{1,0:T(8,128)S(1)}, u32[]{:S(2)}, u32[]{:S(2)}) collective-permute-start(f32[40,2048]{1,0:T(8,128)} %get-tuple-element.189), channel_id=1, source_target_pairs={{0,1},{1,0},{2,3},{3,2},{4,5},{5,4},{6,7},{7,6},{8,9},{9,8},{10,11... | collective-permute-start | bytes 983048 | tf_op jit(solution)/shard_map/ppermute | solution.py:27
  256.2 17.8 %collective-permute-start.22 = (bf16[160,2048]{1,0:T(8,128)(2,1)S(1)}, bf16[160,2048]{1,0:T(8,128)(2,1)S(1)}, u32[]{:S(2)}, u32[]{:S(2)}) collective-permute-start(bf16[160,2048]{1,0:T(8,128)(2,1)S(1)} %collective-permute-done.19.refs_1_), channel_id=1, source_target_pairs={{0,8},{2,10},{8,16},{10,18},{16,24},{18,26},{24,28},{26,30},{28,20... | collective-permute-start | bytes 1966088 | tf_op jit(solution)/shard_map/ppermute | solution.py:46
  256.2 17.7 %collective-permute-start.23 = (bf16[160,2048]{1,0:T(8,128)(2,1)S(1)}, bf16[160,2048]{1,0:T(8,128)(2,1)S(1)}, u32[]{:S(2)}, u32[]{:S(2)}) collective-permute-start(bf16[160,2048]{1,0:T(8,128)(2,1)S(1)} %collective-permute-done.20.refs_2_), channel_id=1, source_target_pairs={{8,0},{10,2},{16,8},{18,10},{24,16},{26,18},{28,24},{30,26},{20,28... | collective-permute-start | bytes 1966088 | tf_op jit(solution)/shard_map/ppermute | solution.py:50
  258.4 18.4 %collective-permute-start.26 = (bf16[160,2048]{1,0:T(8,128)(2,1)S(1)}, bf16[160,2048]{1,0:T(8,128)(2,1)}, u32[]{:S(2)}, u32[]{:S(2)}) collective-permute-start(bf16[160,2048]{1,0:T(8,128)(2,1)S(1)} %collective-permute-done.19.refs_1_), channel_id=1, source_target_pairs={{0,2},{2,0},{4,6},{6,4},{8,10},{10,8},{12,14},{14,12},{16,18},{18,... | collective-permute-start | bytes 1966088 | tf_op jit(solution)/shard_map/ppermute | solution.py:23
  258.4 18.6 %collective-permute-start.27 = (bf16[160,2048]{1,0:T(8,128)(2,1)S(1)}, bf16[160,2048]{1,0:T(8,128)(2,1)}, u32[]{:S(2)}, u32[]{:S(2)}) collective-permute-start(bf16[160,2048]{1,0:T(8,128)(2,1)S(1)} %collective-permute-done.20.refs_2_), channel_id=1, source_target_pairs={{0,2},{2,0},{4,6},{6,4},{8,10},{10,8},{12,14},{14,12},{16,18},{18,... | collective-permute-start | bytes 1966088 | tf_op jit(solution)/shard_map/ppermute | solution.py:23
  258.9 15.3 %collective-permute-start.25 = (f32[40,2048]{1,0:T(8,128)}, f32[40,2048]{1,0:T(8,128)S(1)}, u32[]{:S(2)}, u32[]{:S(2)}) collective-permute-start(f32[40,2048]{1,0:T(8,128)} %get-tuple-element.201), channel_id=1, source_target_pairs={{0,1},{1,0},{2,3},{3,2},{4,5},{5,4},{6,7},{7,6},{8,9},{9,8},{10,11... | collective-permute-start | bytes 983048 | tf_op jit(solution)/shard_map/ppermute | solution.py:27
  274.0 25.3 %collective-permute-start.29 = (bf16[160,2048]{1,0:T(8,128)(2,1)S(1)}, bf16[160,2048]{1,0:T(8,128)(2,1)S(1)}, u32[]{:S(2)}, u32[]{:S(2)}) collective-permute-start(bf16[160,2048]{1,0:T(8,128)(2,1)S(1)} %collective-permute-done.22.refs_1_), channel_id=1, source_target_pairs={{0,8},{2,10},{8,16},{10,18},{16,24},{18,26},{24,28},{26,30},{28,20... | collective-permute-start | bytes 1966088 | tf_op jit(solution)/shard_map/ppermute | solution.py:46
  274.2 28.5 %collective-permute-start.32 = (bf16[160,2048]{1,0:T(8,128)(2,1)S(1)}, bf16[160,2048]{1,0:T(8,128)(2,1)}, u32[]{:S(2)}, u32[]{:S(2)}) collective-permute-start(bf16[160,2048]{1,0:T(8,128)(2,1)S(1)} %collective-permute-done.22.refs_1_), channel_id=1, source_target_pairs={{0,2},{2,0},{4,6},{6,4},{8,10},{10,8},{12,14},{14,12},{16,18},{18,... | collective-permute-start | bytes 1966088 | tf_op jit(solution)/shard_map/ppermute | solution.py:23
  275.1 24.2 %collective-permute-start.30 = (bf16[160,2048]{1,0:T(8,128)(2,1)S(1)}, bf16[160,2048]{1,0:T(8,128)(2,1)S(1)}, u32[]{:S(2)}, u32[]{:S(2)}) collective-permute-start(bf16[160,2048]{1,0:T(8,128)(2,1)S(1)} %collective-permute-done.23.refs_2_), channel_id=1, source_target_pairs={{8,0},{10,2},{16,8},{18,10},{24,16},{26,18},{28,24},{30,26},{20,28... | collective-permute-start | bytes 1966088 | tf_op jit(solution)/shard_map/ppermute | solution.py:50
  276.8 26.1 %collective-permute-start.33 = (bf16[160,2048]{1,0:T(8,128)(2,1)S(1)}, bf16[160,2048]{1,0:T(8,128)(2,1)S(1)}, u32[]{:S(2)}, u32[]{:S(2)}) collective-permute-start(bf16[160,2048]{1,0:T(8,128)(2,1)S(1)} %collective-permute-done.23.refs_2_), channel_id=1, source_target_pairs={{0,2},{2,0},{4,6},{6,4},{8,10},{10,8},{12,14},{14,12},{16,18},{18,... | collective-permute-start | bytes 1966088 | tf_op jit(solution)/shard_map/ppermute | solution.py:23
  277.0 24.4 %collective-permute-start.31 = (f32[40,2048]{1,0:T(8,128)}, f32[40,2048]{1,0:T(8,128)}, u32[]{:S(2)}, u32[]{:S(2)}) collective-permute-start(f32[40,2048]{1,0:T(8,128)} %get-tuple-element.215), channel_id=1, source_target_pairs={{0,1},{1,0},{2,3},{3,2},{4,5},{5,4},{6,7},{7,6},{8,9},{9,8},{10,11... | collective-permute-start | bytes 983048 | tf_op jit(solution)/shard_map/ppermute | solution.py:27
  300.2 29.8 %collective-permute-start.40 = (bf16[160,2048]{1,0:T(8,128)(2,1)S(1)}, bf16[160,2048]{1,0:T(8,128)(2,1)S(1)}, u32[]{:S(2)}, u32[]{:S(2)}) collective-permute-start(bf16[160,2048]{1,0:T(8,128)(2,1)S(1)} %collective-permute-done.29.refs_1_), channel_id=1, source_target_pairs={{0,2},{2,0},{4,6},{6,4},{8,10},{10,8},{12,14},{14,12},{16,18},{18,... | collective-permute-start | bytes 1966088 | tf_op jit(solution)/shard_map/ppermute | solution.py:23
  300.9 29.0 %collective-permute-start.41 = (bf16[160,2048]{1,0:T(8,128)(2,1)S(1)}, bf16[160,2048]{1,0:T(8,128)(2,1)}, u32[]{:S(2)}, u32[]{:S(2)}) collective-permute-start(bf16[160,2048]{1,0:T(8,128)(2,1)S(1)} %collective-permute-done.30.refs_2_), channel_id=1, source_target_pairs={{0,2},{2,0},{4,6},{6,4},{8,10},{10,8},{12,14},{14,12},{16,18},{18,... | collective-permute-start | bytes 1966088 | tf_op jit(solution)/shard_map/ppermute | solution.py:23
  301.4 25.4 %collective-permute-start.37 = (f32[40,2048]{1,0:T(8,128)}, f32[40,2048]{1,0:T(8,128)}, u32[]{:S(2)}, u32[]{:S(2)}) collective-permute-start(f32[40,2048]{1,0:T(8,128)} %get-tuple-element.226), channel_id=1, source_target_pairs={{0,1},{1,0},{2,3},{3,2},{4,5},{5,4},{6,7},{7,6},{8,9},{9,8},{10,11... | collective-permute-start | bytes 983048 | tf_op jit(solution)/shard_map/ppermute | solution.py:27
  302.7 24.2 %collective-permute-start.35 = (bf16[80,2048]{1,0:T(8,128)(2,1)}, bf16[80,2048]{1,0:T(8,128)(2,1)S(1)}, u32[]{:S(2)}, u32[]{:S(2)}) collective-permute-start(bf16[80,2048]{1,0:T(8,128)(2,1)} %slice.201), channel_id=1, source_target_pairs={{0,8},{2,10},{8,16},{10,18},{16,24},{18,26},{24,28},{26,30},{28,20... | collective-permute-start | bytes 983048 | tf_op jit(solution)/shard_map/ppermute | solution.py:46
  302.9 24.0 %collective-permute-start.36 = (bf16[80,2048]{1,0:T(8,128)(2,1)}, bf16[80,2048]{1,0:T(8,128)(2,1)S(1)}, u32[]{:S(2)}, u32[]{:S(2)}) collective-permute-start(bf16[80,2048]{1,0:T(8,128)(2,1)} %slice.202), channel_id=1, source_target_pairs={{8,0},{10,2},{16,8},{18,10},{24,16},{26,18},{28,24},{30,26},{20,28... | collective-permute-start | bytes 983048 | tf_op jit(solution)/shard_map/ppermute | solution.py:50
  327.5 103.1 %collective-permute-start.21 = (bf16[160,2048]{1,0:T(8,128)(2,1)}, bf16[160,2048]{1,0:T(8,128)(2,1)}, u32[]{:S(2)}, u32[]{:S(2)}) collective-permute-start(bf16[160,2048]{1,0:T(8,128)(2,1)} %get-tuple-element.186), channel_id=1, source_target_pairs={{0,2},{2,0},{4,6},{6,4},{8,10},{10,8},{12,14},{14,12},{16,18},{18,... | collective-permute-start | bytes 1966088 | tf_op jit(solution)/shard_map/ppermute | solution.py:23
  328.6 33.8 %collective-permute-start.28 = (bf16[320,2048]{1,0:T(8,128)(2,1)}, bf16[320,2048]{1,0:T(8,128)(2,1)}, u32[]{:S(2)}, u32[]{:S(2)}) collective-permute-start(bf16[320,2048]{1,0:T(8,128)(2,1)} %get-tuple-element.211), channel_id=1, source_target_pairs={{0,2},{2,0},{4,6},{6,4},{8,10},{10,8},{12,14},{14,12},{16,18},{18,... | collective-permute-start | bytes 3932168 | tf_op jit(solution)/shard_map/ppermute | solution.py:23
  329.8 36.6 %collective-permute-start.34 = (bf16[320,2048]{1,0:T(8,128)(2,1)}, bf16[320,2048]{1,0:T(8,128)(2,1)S(1)}, u32[]{:S(2)}, u32[]{:S(2)}) collective-permute-start(bf16[320,2048]{1,0:T(8,128)(2,1)} %get-tuple-element.225), channel_id=1, source_target_pairs={{0,2},{2,0},{4,6},{6,4},{8,10},{10,8},{12,14},{14,12},{16,18},{18,... | collective-permute-start | bytes 3932168 | tf_op jit(solution)/shard_map/ppermute | solution.py:23
  352.8 23.0 %collective-permute-start.42 = (bf16[320,2048]{1,0:T(8,128)(2,1)}, bf16[320,2048]{1,0:T(8,128)(2,1)S(1)}, u32[]{:S(2)}, u32[]{:S(2)}) collective-permute-start(bf16[320,2048]{1,0:T(8,128)(2,1)} %get-tuple-element.238), channel_id=1, source_target_pairs={{0,2},{2,0},{4,6},{6,4},{8,10},{10,8},{12,14},{14,12},{16,18},{18,... | collective-permute-start | bytes 3932168 | tf_op jit(solution)/shard_map/ppermute | solution.py:23
  362.4 70.8 %collective-permute-start.52 = (bf16[512,2048]{1,0:T(8,128)(2,1)S(1)}, bf16[512,2048]{1,0:T(8,128)(2,1)}, u32[]{:S(2)}, u32[]{:S(2)}) collective-permute-start(bf16[512,2048]{1,0:T(8,128)(2,1)S(1)} %convolution_convert_fusion.2), channel_id=1, source_target_pairs={{0,1},{1,0},{2,3},{3,2},{4,5},{5,4},{6,7},{7,6},{8,9},{9,8},{10,11... | collective-permute-start | bytes 6291464 | tf_op jit(solution)/shard_map/ppermute | solution.py:27
  376.7 15.7 %collective-permute-start.49 = (bf16[160,2048]{1,0:T(8,128)(2,1)S(1)}, bf16[160,2048]{1,0:T(8,128)(2,1)S(1)}, u32[]{:S(2)}, u32[]{:S(2)}) collective-permute-start(bf16[160,2048]{1,0:T(8,128)(2,1)S(1)} %pad_maximum_fusion.6), channel_id=1, source_target_pairs={{8,0},{10,2},{16,8},{18,10},{24,16},{26,18},{28,24},{30,26},{20,28... | collective-permute-start | bytes 1966088 | tf_op jit(solution)/shard_map/ppermute | solution.py:50
  377.9 15.4 %collective-permute-start.45 = (bf16[160,2048]{1,0:T(8,128)(2,1)S(1)}, bf16[160,2048]{1,0:T(8,128)(2,1)S(1)}, u32[]{:S(2)}, u32[]{:S(2)}) collective-permute-start(bf16[160,2048]{1,0:T(8,128)(2,1)S(1)} %pad_maximum_fusion.5), channel_id=1, source_target_pairs={{0,8},{2,10},{8,16},{10,18},{16,24},{18,26},{24,28},{26,30},{28,20... | collective-permute-start | bytes 1966088 | tf_op jit(solution)/shard_map/ppermute | solution.py:46
  384.9 48.3 %collective-permute-start.53 = (bf16[1024,512]{1,0:T(8,128)(2,1)S(1)}, bf16[1024,512]{1,0:T(8,128)(2,1)S(1)}, u32[]{:S(2)}, u32[]{:S(2)}) collective-permute-start(bf16[1024,512]{1,0:T(8,128)(2,1)S(1)} %slice.263), channel_id=1, source_target_pairs={{0,1},{1,0},{2,3},{3,2},{4,5},{5,4},{6,7},{7,6},{8,9},{9,8},{10,11... | collective-permute-start | bytes 3145736 | tf_op jit(solution)/shard_map/ppermute | solution.py:27
  393.9 14.6 %collective-permute-start.50 = (bf16[160,2048]{1,0:T(8,128)(2,1)S(1)}, bf16[160,2048]{1,0:T(8,128)(2,1)S(1)}, u32[]{:S(2)}, u32[]{:S(2)}) collective-permute-start(bf16[160,2048]{1,0:T(8,128)(2,1)S(1)} %get-tuple-element.399), channel_id=1, source_target_pairs={{8,0},{10,2},{16,8},{18,10},{24,16},{26,18},{28,24},{30,26},{20,28... | collective-permute-start | bytes 1966088 | tf_op jit(solution)/shard_map/ppermute | solution.py:50
  409.9 20.7 %collective-permute-start.47 = (bf16[160,2048]{1,0:T(8,128)(2,1)S(1)}, bf16[160,2048]{1,0:T(8,128)(2,1)S(1)}, u32[]{:S(2)}, u32[]{:S(2)}) collective-permute-start(bf16[160,2048]{1,0:T(8,128)(2,1)S(1)} %get-tuple-element.396), channel_id=1, source_target_pairs={{0,8},{2,10},{8,16},{10,18},{16,24},{18,26},{24,28},{26,30},{28,20... | collective-permute-start | bytes 1966088 | tf_op jit(solution)/shard_map/ppermute | solution.py:46
  410.8 19.8 %collective-permute-start.51 = (bf16[160,2048]{1,0:T(8,128)(2,1)S(1)}, bf16[160,2048]{1,0:T(8,128)(2,1)S(1)}, u32[]{:S(2)}, u32[]{:S(2)}) collective-permute-start(bf16[160,2048]{1,0:T(8,128)(2,1)S(1)} %get-tuple-element.397), channel_id=1, source_target_pairs={{8,0},{10,2},{16,8},{18,10},{24,16},{26,18},{28,24},{30,26},{20,28... | collective-permute-start | bytes 1966088 | tf_op jit(solution)/shard_map/ppermute | solution.py:50
  439.5 16.0 %collective-permute-start.54 = (bf16[160,2048]{1,0:T(8,128)(2,1)S(1)}, bf16[160,2048]{1,0:T(8,128)(2,1)}, u32[]{:S(2)}, u32[]{:S(2)}) collective-permute-start(bf16[160,2048]{1,0:T(8,128)(2,1)S(1)} %get-tuple-element.374), channel_id=1, source_target_pairs={{0,1},{1,0},{2,3},{3,2},{4,5},{5,4},{6,7},{7,6},{8,9},{9,8},{10,11... | collective-permute-start | bytes 1966088 | tf_op jit(solution)/shard_map/ppermute | solution.py:27
  467.8 34.2 %collective-permute-start.58 = (bf16[1024,512]{1,0:T(8,128)(2,1)}, bf16[1024,512]{1,0:T(8,128)(2,1)}, u32[]{:S(2)}, u32[]{:S(2)}) collective-permute-start(bf16[1024,512]{1,0:T(8,128)(2,1)} %slice.213), channel_id=1, source_target_pairs={{0,1},{1,0},{2,3},{3,2},{4,5},{5,4},{6,7},{7,6},{8,9},{9,8},{10,11... | collective-permute-start | bytes 3145736 | tf_op jit(solution)/shard_map/ppermute | solution.py:27
  489.2 37.2 %collective-permute-start.56 = (bf16[320,2048]{1,0:T(8,128)(2,1)}, bf16[320,2048]{1,0:T(8,128)(2,1)}, u32[]{:S(2)}, u32[]{:S(2)}) collective-permute-start(bf16[320,2048]{1,0:T(8,128)(2,1)} %copy-done.18), channel_id=1, source_target_pairs={{0,2},{2,0},{4,6},{6,4},{8,10},{10,8},{12,14},{14,12},{16,18},{18,... | collective-permute-start | bytes 3932168 | tf_op jit(solution)/shard_map/ppermute | solution.py:23
  490.7 37.1 %collective-permute-start.57 = (bf16[320,2048]{1,0:T(8,128)(2,1)}, bf16[320,2048]{1,0:T(8,128)(2,1)}, u32[]{:S(2)}, u32[]{:S(2)}) collective-permute-start(bf16[320,2048]{1,0:T(8,128)(2,1)} %copy-done.17), channel_id=1, source_target_pairs={{0,2},{2,0},{4,6},{6,4},{8,10},{10,8},{12,14},{14,12},{16,18},{18,... | collective-permute-start | bytes 3932168 | tf_op jit(solution)/shard_map/ppermute | solution.py:23
  497.7 24.5 %collective-permute-start.65 = (bf16[2,128,1024]{2,1,0:T(8,128)(2,1)}, bf16[2,128,1024]{2,1,0:T(8,128)(2,1)}, u32[]{:S(2)}, u32[]{:S(2)}) collective-permute-start(bf16[2,128,1024]{2,1,0:T(8,128)(2,1)} %get-tuple-element.270), channel_id=1, source_target_pairs={{0,8},{2,10},{4,12},{6,14},{8,0},{10,2},{12,4},{14,6},{16,24},{18,... | collective-permute-start | bytes 1572872 | tf_op jit(solution)/shard_map/ppermute | solution.py:23
  498.6 23.6 %collective-permute-start.64 = (bf16[2,128,1024]{2,1,0:T(8,128)(2,1)}, bf16[2,128,1024]{2,1,0:T(8,128)(2,1)}, u32[]{:S(2)}, u32[]{:S(2)}) collective-permute-start(bf16[2,128,1024]{2,1,0:T(8,128)(2,1)} %get-tuple-element.269), channel_id=1, source_target_pairs={{0,4},{2,6},{4,0},{6,2},{8,12},{10,14},{12,8},{14,10},{16,20},{18,... | collective-permute-start | bytes 1572872 | tf_op jit(solution)/shard_map/ppermute | solution.py:23
  502.0 38.0 %collective-permute-start.59 = (bf16[1024,512]{1,0:T(8,128)(2,1)}, bf16[1024,512]{1,0:T(8,128)(2,1)}, u32[]{:S(2)}, u32[]{:S(2)}) collective-permute-start(bf16[1024,512]{1,0:T(8,128)(2,1)} %slice.214), channel_id=1, source_target_pairs={{0,1},{1,0},{2,3},{3,2},{4,5},{5,4},{6,7},{7,6},{8,9},{9,8},{10,11... | collective-permute-start | bytes 3145736 | tf_op jit(solution)/shard_map/ppermute | solution.py:27
  575.7 14.5 %collective-permute-start.76 = (bf16[256,1024]{1,0:T(8,128)(2,1)}, bf16[256,1024]{1,0:T(8,128)(2,1)S(1)}, u32[]{:S(2)}, u32[]{:S(2)}) collective-permute-start(bf16[256,1024]{1,0:T(8,128)(2,1)} %get-tuple-element.299), channel_id=1, source_target_pairs={{0,8},{2,10},{8,16},{10,18},{16,24},{18,26},{24,28},{26,30},{28,20... | collective-permute-start | bytes 1572872 | tf_op jit(solution)/shard_map/ppermute | solution.py:46
  589.3 26.0 %collective-permute-start.71 = (bf16[256,2048]{1,0:T(8,128)(2,1)S(1)}, bf16[256,2048]{1,0:T(8,128)(2,1)S(1)}, u32[]{:S(2)}, u32[]{:S(2)}) collective-permute-start(bf16[256,2048]{1,0:T(8,128)(2,1)S(1)} %pad_maximum_fusion.3), channel_id=1, source_target_pairs={{8,0},{10,2},{16,8},{18,10},{24,16},{26,18},{28,24},{30,26},{20,28... | collective-permute-start | bytes 3145736 | tf_op jit(solution)/shard_map/ppermute | solution.py:50
  590.5 24.8 %collective-permute-start.77 = (bf16[256,2048]{1,0:T(8,128)(2,1)S(1)}, bf16[256,2048]{1,0:T(8,128)(2,1)S(1)}, u32[]{:S(2)}, u32[]{:S(2)}) collective-permute-start(bf16[256,2048]{1,0:T(8,128)(2,1)S(1)} %pad_maximum_fusion.4), channel_id=1, source_target_pairs={{0,8},{2,10},{8,16},{10,18},{16,24},{18,26},{24,28},{26,30},{28,20... | collective-permute-start | bytes 3145736 | tf_op jit(solution)/shard_map/ppermute | solution.py:46
  592.8 79.0 %collective-permute-start.69 = (bf16[160,2048]{1,0:T(8,128)(2,1)}, bf16[160,2048]{1,0:T(8,128)(2,1)}, u32[]{:S(2)}, u32[]{:S(2)}) collective-permute-start(bf16[160,2048]{1,0:T(8,128)(2,1)} %reduce-scatter.2.cloned.1.call-done), channel_id=1, source_target_pairs={{0,1},{1,0},{2,3},{3,2},{4,5},{5,4},{6,7},{7,6},{8,9},{9,8},{10,11... | collective-permute-start | bytes 1966088 | tf_op jit(solution)/shard_map/ppermute | solution.py:27
  593.0 66.7 %collective-permute-start.83 = (bf16[512,512]{1,0:T(8,128)(2,1)}, bf16[512,512]{1,0:T(8,128)(2,1)}, u32[]{:S(2)}, u32[]{:S(2)}) collective-permute-start(bf16[512,512]{1,0:T(8,128)(2,1)} %get-tuple-element.308), channel_id=1, source_target_pairs={{0,1},{1,0},{2,3},{3,2},{4,5},{5,4},{6,7},{7,6},{8,9},{9,8},{10,11... | collective-permute-start | bytes 1572872 | tf_op jit(solution)/shard_map/ppermute | solution.py:27
  607.6 46.9 %collective-permute-start.73 = (bf16[160,2048]{1,0:T(8,128)(2,1)}, bf16[160,2048]{1,0:T(8,128)(2,1)S(1)}, u32[]{:S(2)}, u32[]{:S(2)}) collective-permute-start(bf16[160,2048]{1,0:T(8,128)(2,1)} %dynamic-slice_convert_fusion), channel_id=1, source_target_pairs={{0,1},{1,0},{2,3},{3,2},{4,5},{5,4},{6,7},{7,6},{8,9},{9,8},{10,11... | collective-permute-start | bytes 1966088 | tf_op jit(solution)/shard_map/ppermute | solution.py:27
  617.9 24.3 %collective-permute-start.72 = (bf16[256,2048]{1,0:T(8,128)(2,1)S(1)}, bf16[256,2048]{1,0:T(8,128)(2,1)S(1)}, u32[]{:S(2)}, u32[]{:S(2)}) collective-permute-start(bf16[256,2048]{1,0:T(8,128)(2,1)S(1)} %get-tuple-element.383), channel_id=1, source_target_pairs={{8,0},{10,2},{16,8},{18,10},{24,16},{26,18},{28,24},{30,26},{20,28... | collective-permute-start | bytes 3145736 | tf_op jit(solution)/shard_map/ppermute | solution.py:50
  619.1 23.1 %collective-permute-start.78 = (bf16[256,2048]{1,0:T(8,128)(2,1)S(1)}, bf16[256,2048]{1,0:T(8,128)(2,1)S(1)}, u32[]{:S(2)}, u32[]{:S(2)}) collective-permute-start(bf16[256,2048]{1,0:T(8,128)(2,1)S(1)} %get-tuple-element.382), channel_id=1, source_target_pairs={{0,8},{2,10},{8,16},{10,18},{16,24},{18,26},{24,28},{26,30},{28,20... | collective-permute-start | bytes 3145736 | tf_op jit(solution)/shard_map/ppermute | solution.py:46
  646.0 45.1 %collective-permute-start.79 = (bf16[256,2048]{1,0:T(8,128)(2,1)}, bf16[256,2048]{1,0:T(8,128)(2,1)}, u32[]{:S(2)}, u32[]{:S(2)}) collective-permute-start(bf16[256,2048]{1,0:T(8,128)(2,1)} %get-tuple-element.380), channel_id=1, source_target_pairs={{0,8},{2,10},{8,16},{10,18},{16,24},{18,26},{24,28},{26,30},{28,20... | collective-permute-start | bytes 3145736 | tf_op jit(solution)/shard_map/ppermute | solution.py:46
  647.7 43.4 %collective-permute-start.80 = (bf16[256,2048]{1,0:T(8,128)(2,1)}, bf16[256,2048]{1,0:T(8,128)(2,1)}, u32[]{:S(2)}, u32[]{:S(2)}) collective-permute-start(bf16[256,2048]{1,0:T(8,128)(2,1)} %get-tuple-element.381), channel_id=1, source_target_pairs={{8,0},{10,2},{16,8},{18,10},{24,16},{26,18},{28,24},{30,26},{20,28... | collective-permute-start | bytes 3145736 | tf_op jit(solution)/shard_map/ppermute | solution.py:50
  648.7 24.9 %all-to-all-start = ((f32[16,1,512]{2,1,0:T(1,128)}), f32[16,1,512]{2,1,0:T(1,128)S(1)}, u32[]{:S(2)}, u32[]{:S(2)}) async-start(f32[16,1,512]{2,1,0:T(1,128)} %bitcast.27), calls=%async_computation.1 | async-start | bytes 65536 | tf_op jit(solution)/shard_map/all_to_all | solution.py:1154
  659.6 34.7 %collective-permute-start.74 = (f32[160,2048]{1,0:T(8,128)}, f32[160,2048]{1,0:T(8,128)}, u32[]{:S(2)}, u32[]{:S(2)}) collective-permute-start(f32[160,2048]{1,0:T(8,128)} %fusion.6), channel_id=1, source_target_pairs={{0,1},{1,0},{2,3},{3,2},{4,5},{5,4},{6,7},{7,6},{8,9},{9,8},{10,11... | collective-permute-start | bytes 3932168 | tf_op jit(solution)/shard_map/ppermute | solution.py:27
  673.7 17.4 %collective-permute-start.75 = (f32[512]{0:T(512)S(1)}, f32[512]{0:T(512)S(1)}, u32[]{:S(2)}, u32[]{:S(2)}) collective-permute-start(f32[512]{0:T(512)S(1)} %reduce_sum.179), channel_id=1, source_target_pairs={{0,1},{1,0},{2,3},{3,2},{4,5},{5,4},{6,7},{7,6},{8,9},{9,8},{10,11... | collective-permute-start | bytes 6152 | tf_op jit(solution)/shard_map/ppermute | solution.py:27
  (127 other events, 1268.6 us)
Sparse Core Ops, SparseCore 0:
  12.7 94.2 all-gather.4
  109.9 97.7 all-gather.6
  434.3 130.4 reduce-scatter.1

commit v10 on v9

--- a/solution.py
+++ b/solution.py
@@ -13,7 +13,6 @@
 
 EPSILON = 1e-05
 VMEM = 60 * 1024 * 1024
-SOME = 32 * 1024 * 1024
 LOW = jnp.bfloat16
 FULL = jnp.float32
 
@@ -90,6 +89,7 @@
     both = {hop: add_low(same[hop], swap_bit(cross[hop], "dp", 0)) for hop in (4, 3, 2, 1, 0)}
     rows = both[0].shape[0]
     cut = rows // 2
+    fillers.next(both[4])
     right, left = ahead(both[4][:cut]), behind(both[4][cut:])
     fillers.next(left)
     outward, inward = both[3][rows:], both[3][:rows]
@@ -460,7 +460,7 @@
             pltpu.VMEM((count * rows, width), LOW),
             pltpu.SemaphoreType.DMA((count * parts + count,)),
         ],
-        compiler_params=pltpu.CompilerParams(vmem_limit_bytes=SOME),
+        compiler_params=pltpu.CompilerParams(vmem_limit_bytes=VMEM),
     )(blocks, packed)
 
 
@@ -507,7 +507,7 @@
         out_specs=[pl.BlockSpec((count, columns), lambda i: (0, 0)) for _ in outs],
         out_shape=outs,
         scratch_shapes=[pltpu.VMEM((count, columns), FULL)] * len(outs),
-        compiler_params=pltpu.CompilerParams(vmem_limit_bytes=SOME),
+        compiler_params=pltpu.CompilerParams(vmem_limit_bytes=VMEM),
         cost_estimate=pl.CostEstimate(
             flops=2 * count * width * columns * len(places),
             bytes_accessed=2 * width * columns * len(places) + 8 * count * columns,
@@ -536,7 +536,7 @@
         in_specs=[fixed] * len(rows) + pack_specs(gathered, places, steps, block),
         out_specs=pl.BlockSpec((count, width // steps), lambda i: (0, i)),
         out_shape=jax.ShapeDtypeStruct((count, width), FULL),
-        compiler_params=pltpu.CompilerParams(vmem_limit_bytes=SOME),
+        compiler_params=pltpu.CompilerParams(vmem_limit_bytes=VMEM),
         cost_estimate=pl.CostEstimate(
             flops=2 * count * width * columns * len(places),
             bytes_accessed=2 * width * columns * len(places) + 4 * count * width,
@@ -847,7 +847,7 @@
             ),
         ),
         out_shape=jax.ShapeDtypeStruct((len(HOPS), 2, rows, width), LOW),
-        compiler_params=pltpu.CompilerParams(vmem_limit_bytes=SOME),
+        compiler_params=pltpu.CompilerParams(vmem_limit_bytes=VMEM),
         cost_estimate=pl.CostEstimate(
             flops=4 * count * columns * width,
             bytes_accessed=2 * (count * (2 * columns + width) + 2 * columns * width),
@@ -1050,8 +1050,10 @@
             normed_two_b, back_rows, weight, mats, hidden_state
         )
         expert_in, h0, h1, g0, g1, u0, u1 = held
-        down_got = swap_tensor(low_tn(h1, back_rows))
         late = {}
+
+        def down_stage(gated):
+            late["down"] = swap_tensor(low_tn(gated(h1), back_rows))
 
         def gate_stage(gated):
             late["gate"] = low_tn(gated(expert_in), g1)
@@ -1062,9 +1064,10 @@
         def mixed_stage(gated):
             late["mixed"] = mixed_pass(gated(h0), h1, down_mats, chips, core[None])
 
-        fillers = Fillers(gate_stage, up_stage, mixed_stage)
+        fillers = Fillers(down_stage, gate_stage, up_stage, mixed_stage)
         normed_two_grad = ring_sum(same, cross, fillers)
         gate_sent, up_sent, mixed_rows = late["gate"], late["up"], late["mixed"]
+        down_got = late["down"]
     else:
         hidden_other = swap_tensor(hidden_state)
         expert_in = lax.all_gather(normed_two_b, "dp", axis=0, tiled=True)
@@ -1111,7 +1114,9 @@
         key_grad, value_grad, key_flat, gain_key_local[None], key_scale, cosine, sine, returned
     )
     query_inner, *soon = together(query_inner, *soon)
-    query_inner, key_inner = lax.psum((query_inner[:, 0], key_inner[:, 0]), "tensor")
+    query_inner, key_inner = lax.psum(
+        jnp.stack([query_inner[:, 0], key_inner[:, 0]], axis=0), "tensor"
+    )
     query_pre_grad, key_pre_grad, pre_sent = pre_grads_pass(
         core[None],
         (
@@ -1150,9 +1155,12 @@
         grads = jnp.stack(
             [gain_one_grad, gain_two_grad, wide(query_gain_part[0]), wide(key_gain_part[0])]
         ).reshape(4, dp_count, block)
-        grads = jnp.swapaxes(grads, 0, 1).reshape(dp_count, 4 * block)
-        sums = jnp.sum(lax.all_to_all(grads, "dp", 0, 0, tiled=True), axis=0)
-        return (sums + swap_tensor(sums)).reshape(4, block)
+        grads = jnp.swapaxes(grads, 0, 1).reshape(dp_count, 1, 4 * block)
+        sides = lax.axis_size("tensor")
+        grads = jnp.broadcast_to(grads, (dp_count, sides, 4 * block))
+        grads = grads.reshape(dp_count * sides, 4 * block)
+        sums = lax.all_to_all(grads, ("dp", "tensor"), 0, 0, tiled=True)
+        return jnp.sum(sums, axis=0).reshape(4, block)
 
     if ring:
         pre_got = swap_bit(pre_sent, "dp", 0)
@@ -1176,15 +1184,15 @@
         def normed_stage(gated):
             late["normed"] = share(back_all(*[gated(grad) for grad in pre_grads]))
 
-        def expert_stage(gated):
-            late["down"] = grad_sum(gated(h0), back_rows, down_got)
-            late["gate"] = grad_sum(gated(expert_in), g0, gate_got)
-
         def input_stage(gated):
             late["input"] = input_side(late["normed"][0], gated(late["normed"][1]))
+            late["down"] = grad_sum(gated(h0), back_rows, down_got)
+
+        def expert_stage(gated):
             late["gains"] = gain_side(gated(late["normed"][2]))
-
-        fillers = Fillers(normed_stage, expert_stage, input_stage)
+            late["gate"] = grad_sum(gated(expert_in), g0, gate_got)
+
+        fillers = Fillers(normed_stage, input_stage, expert_stage)
         w_half, token = ring_weights(w_blocks, *far, fillers)
         input_half, input_other = late["input"]
         gain_sums = late["gains"]

time: 715 us -> 706 us (0.987)
  local copies, waits for them, and re-layouts: 69.5 us -> 34.9 us
  Pallas kernels: 198 us -> 216 us
  waiting for transfers between devices: 226 us -> 241 us
  blocking collectives: 18.4 us -> 9.88 us
    unnamed x208 -> x137, local copies, waits for them, and re-layouts: 47.7 us -> 7.22 us
    ppermute x19 -> x18, waiting for transfers between devices: 115 us -> 131 us  [swap_tensor(): return lax.ppermute(block, 'tensor', [(0, 1), (1, 0)])]
    ppermute x12, waiting for transfers between devices: 36.7 us -> 26.7 us  [behind(): return lax.ppermute(block, 'dp', BEHIND)]
    psum x1, blocking collectives: 13 us -> 4.94 us  [body(): lax.psum(jnp.stack([query_inner[:, 0], key_inner[:, 0]], axis=0), 'tensor')]
    ppermute x41, waiting for transfers between devices: 72.5 us -> 80.2 us  [swap_bit(): return lax.ppermute(block, axis, [(i, i ^ 1 << bit) for i in range(count)])]
    ppermute x19 -> x18, starting transfers between devices: 22.5 us -> 24.7 us  [swap_tensor(): return lax.ppermute(block, 'tensor', [(0, 1), (1, 0)])]
  transfers between devices with their start and end apart: 88 -> 87, of which waited for: 29 -> 31; matrix products, arithmetic and copies ran while one was open for 17% -> 18% of each run, Pallas kernels for 28% -> 31%
where the time goes in v10:
time: 706 us; the launch traced here: 696 us
  waiting for transfers between devices  241 us (34%)
  Pallas kernels  216 us (31%)
  starting transfers between devices  70.3 us (10%)
  other arithmetic  55.4 us (8%)
  matrix products  53.9 us (8%)
  local copies, waits for them, and re-layouts  34.9 us (5%)
  between operations  15.5 us (2%)
  blocking collectives  9.88 us (1%)
    ppermute x18, waiting for transfers between devices, swap_tensor(): return lax.ppermute(block, 'tensor', [(0, 1), (1, 0)])  131 us
    pallas_call x5, Pallas kernels, expert_chunk(): pl.pallas_call(lambda *refs: chunk_kernel(len(pieces), len(held), at, spl...  92.2 us
    ppermute x41, waiting for transfers between devices, swap_bit(): return lax.ppermute(block, axis, [(i, i ^ 1 << bit) for i in range(count)])  80.2 us
    dot_general x6, matrix products, dot_tn(): lax.dot_general(left, right, (((0,), (0,)), ((), ())), preferred_element_...  53.8 us
    ppermute x12, waiting for transfers between devices, behind(): return lax.ppermute(block, 'dp', BEHIND)  26.7 us
    ppermute x18, starting transfers between devices, swap_tensor(): return lax.ppermute(block, 'tensor', [(0, 1), (1, 0)])  24.7 us
    pallas_call x1, Pallas kernels, attend_back(): pl.pallas_call(attend_back_kernel, grid=(width // HEAD // PAIR,), in_spec...  19.8 us
    pallas_call x1, Pallas kernels, mixed_pass(): pl.pallas_call(mixed_kernel, grid_spec=pltpu.PrefetchScalarGridSpec(num_s...  17.6 us
  transfers between devices with their start and end apart: 87, of which 31 were waited for; matrix products, arithmetic and copies ran while one was open for 18% of the time, Pallas kernels for 31%

profile of v10, /device:TPU:0, one launch (start us, length us, event | category | flops | bytes accessed | tf_op | source)
XLA Modules:
  0.0 696.3 jit_solution(16398918543795403364)
XLA Ops:
  10.1 2.4 shard_map.309
  12.7 2.3 dynamic-slice_convert_fusion.2
  15.1 3.0 collective-permute-start
  22.1 42.6 %collective-permute-done.refs_5_.refs_7_.refs_9_ = bf16[2048,512]{1,0:T(8,128)(2,1)} collective-permute-done((bf16[2048,512]{1,0:T(8,128)(2,1)S(1)}, bf16[2048,512]{1,0:T(8,128)(2,1)}, u32[]{:S(2)}, u32[]{:S(2)}) %collective-permute-start) | collective-permute-done | bytes 2097184 | tf_op jit(solution)/shard_map/ppermute | solution.py:26
  64.7 44.1 %collective-permute-done.1.refs_7_.refs_9_.refs_11_ = bf16[2048,512]{1,0:T(8,128)(2,1)} collective-permute-done((bf16[2048,512]{1,0:T(8,128)(2,1)}, bf16[2048,512]{1,0:T(8,128)(2,1)}, u32[]{:S(2)}, u32[]{:S(2)}) %collective-permute-start.1) | collective-permute-done | bytes 2097184 | tf_op jit(solution)/shard_map/ppermute | solution.py:26
  111.9 11.7 %shard_map.310 = (f32[320,1024]{1,0:T(8,128)}, f32[320,1024]{1,0:T(8,128)}, bf16[320,1024]{1,0:T(8,128)(2,1)}) custom-call(bf16[320,2048]{1,0:T(8,128)(2,1)} %multiply_convert_fusion.refs_0_, bf16[16,528,1024]{2,1,0:T(8,128)(2,1)} %bitcast.91, bf16[16,528,1024]{2,1,0:T(8,128)(2,1)} %bitcast.92, bf16[16,528,1024]{2,1,0:T(8,128)(2,1)} %bitcast.93), custom_call_target="tpu_custom_call" | custom-call | flops 4026531840 | bytes 15204352 | tf_op jit(solution)/shard_map/pallas_call | solution.py:502
  128.4 4.9 all-reduce.3
  136.4 2.6 shard_map.311.k_ref
  144.4 3.7 collective-permute-done.5.refs_3_
  149.1 3.7 collective-permute-done.3.refs_1_
  154.6 2.5 collective-permute-start.7
  157.1 5.2 collective-permute-done.10.refs_8_
  162.4 8.6 %collective-permute-done.12.refs_10_ = bf16[128,1024]{1,0:T(8,128)(2,1)} collective-permute-done((bf16[128,1024]{1,0:T(8,128)(2,1)}, bf16[128,1024]{1,0:T(8,128)(2,1)}, u32[]{:S(2)}, u32[]{:S(2)}) %collective-permute-start.12) | collective-permute-done | bytes 262176 | tf_op jit(solution)/shard_map/ppermute | solution.py:22
  173.2 13.6 %collective-permute-done.14.refs_12_ = bf16[128,1024]{1,0:T(8,128)(2,1)} collective-permute-done((bf16[128,1024]{1,0:T(8,128)(2,1)}, bf16[128,1024]{1,0:T(8,128)(2,1)}, u32[]{:S(2)}, u32[]{:S(2)}) %collective-permute-start.14) | collective-permute-done | bytes 262176 | tf_op jit(solution)/shard_map/ppermute | solution.py:22
  189.0 12.1 %shard_map.312.refs_0_.refs_8_ = bf16[320,1024]{1,0:T(8,128)(2,1)} custom-call(f32[320,1024]{1,0:T(8,128)} %get-tuple-element.163.flat_ref.refs_0_, f32[1,1024]{1,0:T(1,128)} %bitcast.133, f32[320,1]{1,0:T(8,128)} %broadcast_in_dim.138.scale_ref.refs_3_, f32[320,128]{1,0:T(8,128)} %get-tuple-element.165.cos_ref.refs_5_, ...), custom_call_target="tpu_custom_call" | custom-call | tf_op jit(solution)/shard_map/pallas_call | solution.py:271
  201.1 5.9 shard_map.313
  207.0 2.2 dynamic-slice_convert_fusion.1
  209.3 3.0 collective-permute-start.17
  214.1 8.9 %shard_map.314.refs_3_.refs_5_.refs_7_ = bf16[2560,2048]{1,0:T(8,128)(2,1)} custom-call(s32[16]{0:T(128)} %get-tuple-element.377.refs_0_, bf16[16,160,2048]{2,1,0:T(8,128)(2,1)} %bitcast.125), custom_call_target="tpu_custom_call" | custom-call | tf_op jit(solution)/shard_map/pallas_call | solution.py:454
  223.0 5.1 collective-permute-done.17
  230.3 2.1 collective-permute-done.18.refs_2_
  232.3 2.2 collective-permute-start.20
  238.9 13.7 %shard_map.315 = (bf16[160,2048]{1,0:T(8,128)(2,1)}, bf16[160,2048]{1,0:T(8,128)(2,1)}, bf16[2560,2048]{1,0:T(8,128)(2,1)}, bf16[2560,512]{1,0:T(8,128)(2,1)}, b...) custom-call(f32[2560,1]{1,0:T(8,128)} %copy.94.refs_0_, ...), custom_call_target="tpu_custom_call" | custom-call | flops 6710886400 | bytes 19791872 | tf_op jit(solution)/shard_map/pallas_call | solution.py:787
  253.5 2.0 collective-permute-start.23
  256.3 13.7 %shard_map.316 = (bf16[320,2048]{1,0:T(8,128)(2,1)}, bf16[2560,2048]{1,0:T(8,128)(2,1)}, bf16[2560,512]{1,0:T(8,128)(2,1)}, bf16[2560,512]{1,0:T(8,128)(2,1)}, b...) custom-call(f32[2560,1]{1,0:T(8,128)} %copy.94.refs_0_, ...), custom_call_target="tpu_custom_call", output_to_operand_aliasing={{1}: (10, {}), {2}: (11, {}), {3}: (12, {}), {4}: (13, {}),... | custom-call | flops 6710886400 | bytes 19791872 | tf_op jit(solution)/shard_map/pallas_call | solution.py:787
  271.2 2.0 collective-permute-start.30
  275.2 21.5 %shard_map.317 = (bf16[320,2048]{1,0:T(8,128)(2,1)}, bf16[320,2048]{1,0:T(8,128)(2,1)}, bf16[2560,2048]{1,0:T(8,128)(2,1)}, bf16[2560,512]{1,0:T(8,128)(2,1)}, b...) custom-call(f32[2560,1]{1,0:T(8,128)} %copy.94.refs_0_, ...), custom_call_target="tpu_custom_call", output_to_operand_aliasing={{2}: (12, {}), {3}: (13, {}), {4}: (14, {}), {5}: (15, {}),... | custom-call | flops 13421772800 | bytes 27000832 | tf_op jit(solution)/shard_map/pallas_call | solution.py:787
  301.3 21.8 %shard_map.318 = (bf16[320,2048]{1,0:T(8,128)(2,1)}, bf16[320,2048]{1,0:T(8,128)(2,1)}, bf16[2560,2048]{1,0:T(8,128)(2,1)}, bf16[2560,512]{1,0:T(8,128)(2,1)}, b...) custom-call(f32[2560,1]{1,0:T(8,128)} %copy.94.refs_0_, ...), custom_call_target="tpu_custom_call", output_to_operand_aliasing={{2}: (12, {}), {3}: (13, {}), {4}: (14, {}), {5}: (15, {}),... | custom-call | flops 13421772800 | bytes 27000832 | tf_op jit(solution)/shard_map/pallas_call | solution.py:787
  326.2 21.6 %shard_map.319 = (bf16[160,2048]{1,0:T(8,128)(2,1)}, bf16[160,2048]{1,0:T(8,128)(2,1)}, bf16[320,2048]{1,0:T(8,128)(2,1)}, bf16[2560,2048]{1,0:T(8,128)(2,1)}, b...) custom-call(f32[2560,1]{1,0:T(8,128)} %copy.94.refs_0_, ...), custom_call_target="tpu_custom_call", output_to_operand_aliasing={{3}: (14, {}), {4}: (15, {}), {5}: (16, {}), {6}: (17, {}),... | custom-call | flops 13421772800 | bytes 27000832 | tf_op jit(solution)/shard_map/pallas_call | solution.py:787
  352.5 11.4 %convolution_convert_fusion.2 = bf16[512,2048]{1,0:T(8,128)(2,1)} fusion(bf16[2560,512]{1,0:T(8,128)(2,1)S(1)} %copy-done.3, bf16[2560,2048]{1,0:T(8,128)(2,1)} %shard_map.314.refs_3_.refs_5_.refs_7_), kind=kOutput, calls=%fused_computation.6 | convolution fusion | flops 5369757696 | bytes 15204352 | tf_op jit(solution)/shard_map/dot_general | solution.py:150
  369.3 5.8 convolution_convert_fusion.1
  377.0 6.2 collective-permute-done.49
  386.7 6.8 convolution_convert_fusion
  393.5 6.0 collective-permute-done.50
  403.2 17.6 %shard_map.320 = bf16[8,2,160,2048]{3,2,1,0:T(8,128)(2,1)} custom-call(s32[8]{0:T(128)} %compare_select_fusion.6.chip_ref, s32[8]{0:T(128)} %constant.192.clone.same_ref, s32[8]{0:T(128)} %constant.193.clone.cross_ref, s32[1]{0:T(128)} %bitcast.15.core_ref, bf16[2560,512]{1,0:T(8,128)(2,1)} %get-tuple-element.309.refs_0_.refs_1_, ...), custom_call_target="tpu_custom_call" | custom-call | flops 10737418240 | bytes 19922944 | tf_op jit(solution)/shard_map/pallas_call | solution.py:839
  421.6 1.9 convert_add_fusion.6
  423.5 10.4 %collective-permute-done.53 = bf16[1024,512]{1,0:T(8,128)(2,1)} collective-permute-done((bf16[1024,512]{1,0:T(8,128)(2,1)}, bf16[1024,512]{1,0:T(8,128)(2,1)}, u32[]{:S(2)}, u32[]{:S(2)}) %collective-permute-start.53) | collective-permute-done | bytes 1048608 | tf_op jit(solution)/shard_map/ppermute | solution.py:26
  438.9 13.6 %collective-permute-done.54 = bf16[160,2048]{1,0:T(8,128)(2,1)S(1)} collective-permute-done((bf16[160,2048]{1,0:T(8,128)(2,1)S(1)}, bf16[160,2048]{1,0:T(8,128)(2,1)S(1)}, u32[]{:S(2)}, u32[]{:S(2)}) %collective-permute-start.54) | collective-permute-done | bytes 655392 | tf_op jit(solution)/shard_map/ppermute | solution.py:26
  454.8 5.8 shard_map.321.refs_14_
  462.2 19.8 %shard_map.322 = (f32[320,1024]{1,0:T(8,128)}, f32[320,1]{1,0:T(8,128)}, f32[1,1024]{1,0:T(1,128)}, f32[320,1024]{1,0:T(8,128)}, f32[320,1024]{1,0:T(8,128)}, /*...) custom-call(f32[320,1024]{1,0:T(8,128)} %get-tuple-element.163.flat_, ...), custom_call_target="tpu_custom_call" | custom-call | flops 20000000000 | bytes 40000000 | tf_op jit(solution)/shard_map/pallas_call | solution.py:330
  485.7 2.2 collective-permute-done.63.refs_2_
  488.8 3.2 shard_map.323
  493.5 2.3 slice.214
  497.0 25.1 %collective-permute-done.65.refs_9_ = bf16[2,128,1024]{2,1,0:T(8,128)(2,1)} collective-permute-done((bf16[2,128,1024]{2,1,0:T(8,128)(2,1)}, bf16[2,128,1024]{2,1,0:T(8,128)(2,1)}, u32[]{:S(2)}, u32[]{:S(2)}) %collective-permute-start.65) | collective-permute-done | bytes 524320 | tf_op jit(solution)/shard_map/ppermute | solution.py:22
  526.4 6.8 collective-permute-done.67.refs_11_
  534.6 5.3 shard_map.324
  541.2 4.9 psum.23
  547.7 4.8 shard_map.325
  555.5 14.2 %shard_map.326 = (bf16[8,256,2048]{2,1,0:T(8,128)(2,1)}, bf16[256,1024]{1,0:T(8,128)(2,1)}, bf16[256,1024]{1,0:T(8,128)(2,1)}) custom-call(s32[8]{0:T(128)} %compare_select_fusion.6.chip_ref, s32[1]{0:T(128)} %bitcast.15.core_ref, bf16[320,2048]{1,0:T(8,128)(2,1)} %multiply_convert_fusion.refs_0_, bf16[320,2048]{1,0:T(8,128)(2,1)} %collective-permute-done.56.refs_1_, ...), custom_call_target="tpu_custom_call" | custom-call | flops 5368709120 | bytes 16252928 | tf_op jit(solution)/shard_map/pallas_call | solution.py:616
  573.7 10.2 %collective-permute-done.70 = bf16[256,1024]{1,0:T(8,128)(2,1)S(1)} collective-permute-done((bf16[256,1024]{1,0:T(8,128)(2,1)}, bf16[256,1024]{1,0:T(8,128)(2,1)S(1)}, u32[]{:S(2)}, u32[]{:S(2)}) %collective-permute-start.70) | collective-permute-done | bytes 524320 | tf_op jit(solution)/shard_map/ppermute | solution.py:49
  589.7 9.4 %shard_map.327 = f32[320,2048]{1,0:T(8,128)} custom-call(bf16[320,1024]{1,0:T(8,128)(2,1)} %get-tuple-element.293.refs_4_.refs_0_, bf16[320,1024]{1,0:T(8,128)(2,1)} %get-tuple-element.294.refs_5_.refs_1_, bf16[320,1024]{1,0:T(8,128)(2,1)} %get-tuple-element.295.refs_10_.refs_6_.refs_2_, bf16[16,528,1024]{2,1,0:T(8,128)(2,1)} %bitcast.97, ...), custom_call_target="tpu_custom_call" | custom-call | flops 4026531840 | bytes 15204352 | tf_op jit(solution)/shard_map/pallas_call | solution.py:533
  602.2 2.2 multiply_reduce_fusion
  605.0 4.3 collective-permute-done.71
  610.7 3.0 fusion.1
  615.8 15.1 %collective-permute-done.73 = bf16[160,2048]{1,0:T(8,128)(2,1)S(1)} collective-permute-done((bf16[160,2048]{1,0:T(8,128)(2,1)S(1)}, bf16[160,2048]{1,0:T(8,128)(2,1)S(1)}, u32[]{:S(2)}, u32[]{:S(2)}) %collective-permute-start.73) | collective-permute-done | bytes 655392 | tf_op jit(solution)/shard_map/ppermute | solution.py:26
  634.3 8.4 %add_bitcast_fusion = f32[1,512,2048]{2,1,0:T(8,128)} fusion(bf16[512,2048]{1,0:T(8,128)(2,1)} %collective-permute-done.52, bf16[2560,512]{1,0:T(8,128)(2,1)S(1)} %copy-done.2, bf16[2560,2048]{1,0:T(8,128)(2,1)S(1)} %bitcast.101), kind=kOutput, calls=%fused_computation.1 | convolution fusion | flops 5370806272 | bytes 19398656 | tf_op jit(solution)/shard_map/dot_general | solution.py:150
  642.7 3.8 fusion.2
  646.5 1.9 collective-permute-start.78
  649.3 3.9 all-to-all-start
  653.2 12.5 %add_bitcast_fusion.2 = f32[1,2048,512]{2,1,0:T(8,128)} fusion(bf16[2560,2048]{1,0:T(8,128)(2,1)} %get-tuple-element.301, bf16[2560,512]{1,0:T(8,128)(2,1)} %get-tuple-element.302, bf16[1024,512]{1,0:T(8,128)(2,1)} %collective-permute-done.58, bf16[1024,512]{1,0:T(8,128)(2,1)} %collective-permute-done.53), kind=kOutput, calls=%fused_computation.3 | convolution fusion | flops 5373952000 | bytes 19398656 | tf_op jit(solution)/shard_map/dot_general | solution.py:150
  665.8 8.9 %add_bitcast_fusion.1 = f32[1,2048,512]{2,1,0:T(8,128)} fusion(bf16[2560,2048]{1,0:T(8,128)(2,1)S(1)} %bitcast.105, bf16[2560,512]{1,0:T(8,128)(2,1)S(1)} %copy-done.5, bf16[512,512]{1,0:T(8,128)(2,1)} %collective-permute-done.82, bf16[512,512]{1,0:T(8,128)(2,1)} %collective-permute-done.81, bf16[1024,512]{1,0:T(8,128)(2,1)} %collective-permute-done.59), kind=kOutput, calls=%fused_computation.2 | convolution fusion | flops 5376049152 | bytes 19398656 | tf_op jit(solution)/shard_map/dot_general | solution.py:150
  674.7 1.9 fusion.8
  678.3 2.4 fusion.3
  681.8 1.9 broadcast_select_fusion.1
  (403 shorter events, 128.1 us)
Async XLA Ops:
  7.2 101.6 %all-gather.5.cloned.1.call-start = ((), (), s32[]{:S(2)}) async-start(), calls=%async_computation.3 | async-start | bytes 18382848 | tf_op jit(solution)/shard_map/all_gather | solution.py:958
  12.6 201.5 %all-gather.7.cloned.1.call-start = ((), (), s32[]{:S(2)}) async-start(), calls=%async_computation.4 | async-start | bytes 11141120 | tf_op jit(solution)/shard_map/all_gather | solution.py:960
  15.0 554.6 %reduce-scatter.2.cloned.1.call-start = ((), (), s32[]{:S(2)}) async-start(), calls=%async_computation.2 | async-start | bytes 11141120 | tf_op jit(solution)/shard_map/reduce_scatter | solution.py:1088
  15.1 49.6 %collective-permute-start = (bf16[2048,512]{1,0:T(8,128)(2,1)S(1)}, bf16[2048,512]{1,0:T(8,128)(2,1)}, u32[]{:S(2)}, u32[]{:S(2)}) collective-permute-start(bf16[2048,512]{1,0:T(8,128)(2,1)S(1)} %bitcast.111), channel_id=1, source_target_pairs={{0,1},{1,0},{2,3},{3,2},{4,5},{5,4},{6,7},{7,6},{8,9},{9,8},{10,11... | collective-permute-start | bytes 6291464 | tf_op jit(solution)/shard_map/ppermute | solution.py:26
  18.1 90.7 %collective-permute-start.1 = (bf16[2048,512]{1,0:T(8,128)(2,1)}, bf16[2048,512]{1,0:T(8,128)(2,1)}, u32[]{:S(2)}, u32[]{:S(2)}) collective-permute-start(bf16[2048,512]{1,0:T(8,128)(2,1)} %bitcast.112), channel_id=1, source_target_pairs={{0,1},{1,0},{2,3},{3,2},{4,5},{5,4},{6,7},{7,6},{8,9},{9,8},{10,11... | collective-permute-start | bytes 6291464 | tf_op jit(solution)/shard_map/ppermute | solution.py:26
  133.4 73.7 %collective-permute-start.16 = (bf16[512,2048]{1,0:T(8,128)(2,1)S(1)}, bf16[512,2048]{1,0:T(8,128)(2,1)}, u32[]{:S(2)}, u32[]{:S(2)}) collective-permute-start(bf16[512,2048]{1,0:T(8,128)(2,1)S(1)} %bitcast.124), channel_id=1, source_target_pairs={{0,1},{1,0},{2,3},{3,2},{4,5},{5,4},{6,7},{7,6},{8,9},{9,8},{10,11... | collective-permute-start | bytes 6291464 | tf_op jit(solution)/shard_map/ppermute | solution.py:26
  143.9 18.5 %collective-permute-start.10 = (bf16[128,1024]{1,0:T(8,128)(2,1)}, bf16[128,1024]{1,0:T(8,128)(2,1)}, u32[]{:S(2)}, u32[]{:S(2)}) collective-permute-start(bf16[128,1024]{1,0:T(8,128)(2,1)} %slice.190), channel_id=1, source_target_pairs={{0,4},{2,6},{4,0},{6,2},{8,12},{10,14},{12,8},{14,10},{16,20},{18,... | collective-permute-start | bytes 786440 | tf_op jit(solution)/shard_map/ppermute | solution.py:22
  148.1 22.9 %collective-permute-start.12 = (bf16[128,1024]{1,0:T(8,128)(2,1)}, bf16[128,1024]{1,0:T(8,128)(2,1)}, u32[]{:S(2)}, u32[]{:S(2)}) collective-permute-start(bf16[128,1024]{1,0:T(8,128)(2,1)} %slice.190), channel_id=1, source_target_pairs={{0,8},{2,10},{4,12},{6,14},{8,0},{10,2},{12,4},{14,6},{16,24},{18,... | collective-permute-start | bytes 786440 | tf_op jit(solution)/shard_map/ppermute | solution.py:22
  152.8 18.2 %collective-permute-start.9 = (bf16[128,1024]{1,0:T(8,128)(2,1)}, bf16[128,1024]{1,0:T(8,128)(2,1)}, u32[]{:S(2)}, u32[]{:S(2)}) collective-permute-start(bf16[128,1024]{1,0:T(8,128)(2,1)} %slice.190), channel_id=1, source_target_pairs={{0,2},{2,0},{4,6},{6,4},{8,10},{10,8},{12,14},{14,12},{16,18},{18,... | collective-permute-start | bytes 786440 | tf_op jit(solution)/shard_map/ppermute | solution.py:22
  154.6 17.9 %collective-permute-start.7 = (bf16[128,1024]{1,0:T(8,128)(2,1)}, bf16[128,1024]{1,0:T(8,128)(2,1)}, u32[]{:S(2)}, u32[]{:S(2)}) collective-permute-start(bf16[128,1024]{1,0:T(8,128)(2,1)} %collective-permute-done.5.refs_3_), channel_id=1, source_target_pairs={{0,4},{2,6},{4,0},{6,2},{8,12},{10,14},{12,8},{14,10},{16,20},{18,... | collective-permute-start | bytes 786440 | tf_op jit(solution)/shard_map/ppermute | solution.py:22
  171.0 15.8 %collective-permute-start.14 = (bf16[128,1024]{1,0:T(8,128)(2,1)}, bf16[128,1024]{1,0:T(8,128)(2,1)}, u32[]{:S(2)}, u32[]{:S(2)}) collective-permute-start(bf16[128,1024]{1,0:T(8,128)(2,1)} %collective-permute-done.10.refs_8_), channel_id=1, source_target_pairs={{0,8},{2,10},{4,12},{6,14},{8,0},{10,2},{12,4},{14,6},{16,24},{18,... | collective-permute-start | bytes 786440 | tf_op jit(solution)/shard_map/ppermute | solution.py:22
  172.5 16.5 %collective-permute-start.11 = (bf16[128,1024]{1,0:T(8,128)(2,1)}, bf16[128,1024]{1,0:T(8,128)(2,1)}, u32[]{:S(2)}, u32[]{:S(2)}) collective-permute-start(bf16[128,1024]{1,0:T(8,128)(2,1)} %collective-permute-done.10.refs_8_), channel_id=1, source_target_pairs={{0,2},{2,0},{4,6},{6,4},{8,10},{10,8},{12,14},{14,12},{16,18},{18,... | collective-permute-start | bytes 786440 | tf_op jit(solution)/shard_map/ppermute | solution.py:22
  172.7 16.3 %collective-permute-start.13 = (bf16[128,1024]{1,0:T(8,128)(2,1)}, bf16[128,1024]{1,0:T(8,128)(2,1)}, u32[]{:S(2)}, u32[]{:S(2)}) collective-permute-start(bf16[128,1024]{1,0:T(8,128)(2,1)} %collective-permute-done.12.refs_10_), channel_id=1, source_target_pairs={{0,2},{2,0},{4,6},{6,4},{8,10},{10,8},{12,14},{14,12},{16,18},{18,... | collective-permute-start | bytes 786440 | tf_op jit(solution)/shard_map/ppermute | solution.py:22
  173.0 16.0 %collective-permute-start.8 = (bf16[128,1024]{1,0:T(8,128)(2,1)}, bf16[128,1024]{1,0:T(8,128)(2,1)}, u32[]{:S(2)}, u32[]{:S(2)}) collective-permute-start(bf16[128,1024]{1,0:T(8,128)(2,1)} %collective-permute-done.7.refs_5_), channel_id=1, source_target_pairs={{0,2},{2,0},{4,6},{6,4},{8,10},{10,8},{12,14},{14,12},{16,18},{18,... | collective-permute-start | bytes 786440 | tf_op jit(solution)/shard_map/ppermute | solution.py:22
  209.3 18.9 %collective-permute-start.17 = (bf16[160,2048]{1,0:T(8,128)(2,1)}, bf16[160,2048]{1,0:T(8,128)(2,1)}, u32[]{:S(2)}, u32[]{:S(2)}) collective-permute-start(bf16[160,2048]{1,0:T(8,128)(2,1)} %dynamic-slice_convert_fusion.1), channel_id=1, source_target_pairs={{0,1},{1,0},{2,3},{3,2},{4,5},{5,4},{6,7},{7,6},{8,9},{9,8},{10,11... | collective-permute-start | bytes 1966088 | tf_op jit(solution)/shard_map/ppermute | solution.py:26
  232.3 20.2 %collective-permute-start.19 = (bf16[160,2048]{1,0:T(8,128)(2,1)S(1)}, bf16[160,2048]{1,0:T(8,128)(2,1)}, u32[]{:S(2)}, u32[]{:S(2)}) collective-permute-start(bf16[160,2048]{1,0:T(8,128)(2,1)S(1)} %multiply_convert_fusion.1.refs_1_), channel_id=1, source_target_pairs={{0,8},{2,10},{8,16},{10,18},{16,24},{18,26},{24,28},{26,30},{28,20... | collective-permute-start | bytes 1966088 | tf_op jit(solution)/shard_map/ppermute | solution.py:45
  232.3 20.2 %collective-permute-start.20 = (bf16[160,2048]{1,0:T(8,128)(2,1)S(1)}, bf16[160,2048]{1,0:T(8,128)(2,1)S(1)}, u32[]{:S(2)}, u32[]{:S(2)}) collective-permute-start(bf16[160,2048]{1,0:T(8,128)(2,1)S(1)} %multiply_convert_fusion.1.refs_1_), channel_id=1, source_target_pairs={{8,0},{10,2},{16,8},{18,10},{24,16},{26,18},{28,24},{30,26},{20,28... | collective-permute-start | bytes 1966088 | tf_op jit(solution)/shard_map/ppermute | solution.py:49
  237.1 18.9 %collective-permute-start.24 = (f32[40,2048]{1,0:T(8,128)}, f32[40,2048]{1,0:T(8,128)S(1)}, u32[]{:S(2)}, u32[]{:S(2)}) collective-permute-start(f32[40,2048]{1,0:T(8,128)} %get-tuple-element.189), channel_id=1, source_target_pairs={{0,1},{1,0},{2,3},{3,2},{4,5},{5,4},{6,7},{7,6},{8,9},{9,8},{10,11... | collective-permute-start | bytes 983048 | tf_op jit(solution)/shard_map/ppermute | solution.py:26
  253.5 16.5 %collective-permute-start.22 = (bf16[160,2048]{1,0:T(8,128)(2,1)}, bf16[160,2048]{1,0:T(8,128)(2,1)S(1)}, u32[]{:S(2)}, u32[]{:S(2)}) collective-permute-start(bf16[160,2048]{1,0:T(8,128)(2,1)} %collective-permute-done.19.refs_1_), channel_id=1, source_target_pairs={{0,8},{2,10},{8,16},{10,18},{16,24},{18,26},{24,28},{26,30},{28,20... | collective-permute-start | bytes 1966088 | tf_op jit(solution)/shard_map/ppermute | solution.py:45
  253.5 16.6 %collective-permute-start.23 = (bf16[160,2048]{1,0:T(8,128)(2,1)}, bf16[160,2048]{1,0:T(8,128)(2,1)S(1)}, u32[]{:S(2)}, u32[]{:S(2)}) collective-permute-start(bf16[160,2048]{1,0:T(8,128)(2,1)} %copy-done.31), channel_id=1, source_target_pairs={{8,0},{10,2},{16,8},{18,10},{24,16},{26,18},{28,24},{30,26},{20,28... | collective-permute-start | bytes 1966088 | tf_op jit(solution)/shard_map/ppermute | solution.py:49
  255.5 17.7 %collective-permute-start.26 = (bf16[160,2048]{1,0:T(8,128)(2,1)}, bf16[160,2048]{1,0:T(8,128)(2,1)}, u32[]{:S(2)}, u32[]{:S(2)}) collective-permute-start(bf16[160,2048]{1,0:T(8,128)(2,1)} %collective-permute-done.19.refs_1_), channel_id=1, source_target_pairs={{0,2},{2,0},{4,6},{6,4},{8,10},{10,8},{12,14},{14,12},{16,18},{18,... | collective-permute-start | bytes 1966088 | tf_op jit(solution)/shard_map/ppermute | solution.py:22
  255.5 18.0 %collective-permute-start.27 = (bf16[160,2048]{1,0:T(8,128)(2,1)}, bf16[160,2048]{1,0:T(8,128)(2,1)}, u32[]{:S(2)}, u32[]{:S(2)}) collective-permute-start(bf16[160,2048]{1,0:T(8,128)(2,1)} %copy-done.31), channel_id=1, source_target_pairs={{0,2},{2,0},{4,6},{6,4},{8,10},{10,8},{12,14},{14,12},{16,18},{18,... | collective-permute-start | bytes 1966088 | tf_op jit(solution)/shard_map/ppermute | solution.py:22
  270.0 26.6 %collective-permute-start.29 = (bf16[160,2048]{1,0:T(8,128)(2,1)S(1)}, bf16[160,2048]{1,0:T(8,128)(2,1)S(1)}, u32[]{:S(2)}, u32[]{:S(2)}) collective-permute-start(bf16[160,2048]{1,0:T(8,128)(2,1)S(1)} %collective-permute-done.22.refs_1_), channel_id=1, source_target_pairs={{0,8},{2,10},{8,16},{10,18},{16,24},{18,26},{24,28},{26,30},{28,20... | collective-permute-start | bytes 1966088 | tf_op jit(solution)/shard_map/ppermute | solution.py:45
  270.4 28.7 %collective-permute-start.32 = (bf16[160,2048]{1,0:T(8,128)(2,1)S(1)}, bf16[160,2048]{1,0:T(8,128)(2,1)}, u32[]{:S(2)}, u32[]{:S(2)}) collective-permute-start(bf16[160,2048]{1,0:T(8,128)(2,1)S(1)} %collective-permute-done.22.refs_1_), channel_id=1, source_target_pairs={{0,2},{2,0},{4,6},{6,4},{8,10},{10,8},{12,14},{14,12},{16,18},{18,... | collective-permute-start | bytes 1966088 | tf_op jit(solution)/shard_map/ppermute | solution.py:22
  271.2 25.5 %collective-permute-start.30 = (bf16[160,2048]{1,0:T(8,128)(2,1)S(1)}, bf16[160,2048]{1,0:T(8,128)(2,1)S(1)}, u32[]{:S(2)}, u32[]{:S(2)}) collective-permute-start(bf16[160,2048]{1,0:T(8,128)(2,1)S(1)} %collective-permute-done.23.refs_2_), channel_id=1, source_target_pairs={{8,0},{10,2},{16,8},{18,10},{24,16},{26,18},{28,24},{30,26},{20,28... | collective-permute-start | bytes 1966088 | tf_op jit(solution)/shard_map/ppermute | solution.py:49
  273.2 26.2 %collective-permute-start.33 = (bf16[160,2048]{1,0:T(8,128)(2,1)S(1)}, bf16[160,2048]{1,0:T(8,128)(2,1)}, u32[]{:S(2)}, u32[]{:S(2)}) collective-permute-start(bf16[160,2048]{1,0:T(8,128)(2,1)S(1)} %collective-permute-done.23.refs_2_), channel_id=1, source_target_pairs={{0,2},{2,0},{4,6},{6,4},{8,10},{10,8},{12,14},{14,12},{16,18},{18,... | collective-permute-start | bytes 1966088 | tf_op jit(solution)/shard_map/ppermute | solution.py:22
  273.5 25.3 %collective-permute-start.31 = (f32[40,2048]{1,0:T(8,128)}, f32[40,2048]{1,0:T(8,128)}, u32[]{:S(2)}, u32[]{:S(2)}) collective-permute-start(f32[40,2048]{1,0:T(8,128)} %get-tuple-element.215), channel_id=1, source_target_pairs={{0,1},{1,0},{2,3},{3,2},{4,5},{5,4},{6,7},{7,6},{8,9},{9,8},{10,11... | collective-permute-start | bytes 983048 | tf_op jit(solution)/shard_map/ppermute | solution.py:26
  297.5 27.9 %collective-permute-start.40 = (bf16[160,2048]{1,0:T(8,128)(2,1)S(1)}, bf16[160,2048]{1,0:T(8,128)(2,1)}, u32[]{:S(2)}, u32[]{:S(2)}) collective-permute-start(bf16[160,2048]{1,0:T(8,128)(2,1)S(1)} %collective-permute-done.29.refs_1_), channel_id=1, source_target_pairs={{0,2},{2,0},{4,6},{6,4},{8,10},{10,8},{12,14},{14,12},{16,18},{18,... | collective-permute-start | bytes 1966088 | tf_op jit(solution)/shard_map/ppermute | solution.py:22
  298.3 27.2 %collective-permute-start.41 = (bf16[160,2048]{1,0:T(8,128)(2,1)S(1)}, bf16[160,2048]{1,0:T(8,128)(2,1)}, u32[]{:S(2)}, u32[]{:S(2)}) collective-permute-start(bf16[160,2048]{1,0:T(8,128)(2,1)S(1)} %collective-permute-done.30.refs_2_), channel_id=1, source_target_pairs={{0,2},{2,0},{4,6},{6,4},{8,10},{10,8},{12,14},{14,12},{16,18},{18,... | collective-permute-start | bytes 1966088 | tf_op jit(solution)/shard_map/ppermute | solution.py:22
  298.8 24.2 %collective-permute-start.37 = (f32[40,2048]{1,0:T(8,128)}, f32[40,2048]{1,0:T(8,128)}, u32[]{:S(2)}, u32[]{:S(2)}) collective-permute-start(f32[40,2048]{1,0:T(8,128)} %get-tuple-element.226), channel_id=1, source_target_pairs={{0,1},{1,0},{2,3},{3,2},{4,5},{5,4},{6,7},{7,6},{8,9},{9,8},{10,11... | collective-permute-start | bytes 983048 | tf_op jit(solution)/shard_map/ppermute | solution.py:26
  299.1 24.0 %collective-permute-start.35 = (bf16[80,2048]{1,0:T(8,128)(2,1)}, bf16[80,2048]{1,0:T(8,128)(2,1)}, u32[]{:S(2)}, u32[]{:S(2)}) collective-permute-start(bf16[80,2048]{1,0:T(8,128)(2,1)} %slice.201), channel_id=1, source_target_pairs={{0,8},{2,10},{8,16},{10,18},{16,24},{18,26},{24,28},{26,30},{28,20... | collective-permute-start | bytes 983048 | tf_op jit(solution)/shard_map/ppermute | solution.py:45
  299.5 23.6 %collective-permute-start.36 = (bf16[80,2048]{1,0:T(8,128)(2,1)}, bf16[80,2048]{1,0:T(8,128)(2,1)}, u32[]{:S(2)}, u32[]{:S(2)}) collective-permute-start(bf16[80,2048]{1,0:T(8,128)(2,1)} %slice.202), channel_id=1, source_target_pairs={{8,0},{10,2},{16,8},{18,10},{24,16},{26,18},{28,24},{30,26},{20,28... | collective-permute-start | bytes 983048 | tf_op jit(solution)/shard_map/ppermute | solution.py:49
  323.6 25.7 %collective-permute-start.28 = (bf16[320,2048]{1,0:T(8,128)(2,1)}, bf16[320,2048]{1,0:T(8,128)(2,1)S(1)}, u32[]{:S(2)}, u32[]{:S(2)}) collective-permute-start(bf16[320,2048]{1,0:T(8,128)(2,1)} %get-tuple-element.211), channel_id=1, source_target_pairs={{0,2},{2,0},{4,6},{6,4},{8,10},{10,8},{12,14},{14,12},{16,18},{18,... | collective-permute-start | bytes 3932168 | tf_op jit(solution)/shard_map/ppermute | solution.py:22
  348.5 72.2 %collective-permute-start.21 = (bf16[160,2048]{1,0:T(8,128)(2,1)}, bf16[160,2048]{1,0:T(8,128)(2,1)}, u32[]{:S(2)}, u32[]{:S(2)}) collective-permute-start(bf16[160,2048]{1,0:T(8,128)(2,1)} %get-tuple-element.186), channel_id=1, source_target_pairs={{0,2},{2,0},{4,6},{6,4},{8,10},{10,8},{12,14},{14,12},{16,18},{18,... | collective-permute-start | bytes 1966088 | tf_op jit(solution)/shard_map/ppermute | solution.py:22
  348.8 15.1 %collective-permute-start.34 = (bf16[320,2048]{1,0:T(8,128)(2,1)}, bf16[320,2048]{1,0:T(8,128)(2,1)S(1)}, u32[]{:S(2)}, u32[]{:S(2)}) collective-permute-start(bf16[320,2048]{1,0:T(8,128)(2,1)} %get-tuple-element.225), channel_id=1, source_target_pairs={{0,2},{2,0},{4,6},{6,4},{8,10},{10,8},{12,14},{14,12},{16,18},{18,... | collective-permute-start | bytes 3932168 | tf_op jit(solution)/shard_map/ppermute | solution.py:22
  349.0 17.3 %collective-permute-start.42 = (bf16[320,2048]{1,0:T(8,128)(2,1)}, bf16[320,2048]{1,0:T(8,128)(2,1)S(1)}, u32[]{:S(2)}, u32[]{:S(2)}) collective-permute-start(bf16[320,2048]{1,0:T(8,128)(2,1)} %get-tuple-element.238), channel_id=1, source_target_pairs={{0,2},{2,0},{4,6},{6,4},{8,10},{10,8},{12,14},{14,12},{16,18},{18,... | collective-permute-start | bytes 3932168 | tf_op jit(solution)/shard_map/ppermute | solution.py:22
  350.4 16.5 %collective-permute-start.44 = (bf16[80,2048]{1,0:T(8,128)(2,1)S(1)}, bf16[80,2048]{1,0:T(8,128)(2,1)S(1)}, u32[]{:S(2)}, u32[]{:S(2)}) collective-permute-start(bf16[80,2048]{1,0:T(8,128)(2,1)S(1)} %get-tuple-element.414), channel_id=1, source_target_pairs={{0,8},{2,10},{8,16},{10,18},{16,24},{18,26},{24,28},{26,30},{28,20... | collective-permute-start | bytes 983048 | tf_op jit(solution)/shard_map/ppermute | solution.py:45
  350.8 15.5 %collective-permute-start.48 = (bf16[80,2048]{1,0:T(8,128)(2,1)S(1)}, bf16[80,2048]{1,0:T(8,128)(2,1)S(1)}, u32[]{:S(2)}, u32[]{:S(2)}) collective-permute-start(bf16[80,2048]{1,0:T(8,128)(2,1)S(1)} %get-tuple-element.415), channel_id=1, source_target_pairs={{8,0},{10,2},{16,8},{18,10},{24,16},{26,18},{28,24},{30,26},{20,28... | collective-permute-start | bytes 983048 | tf_op jit(solution)/shard_map/ppermute | solution.py:49
  363.9 70.0 %collective-permute-start.52 = (bf16[512,2048]{1,0:T(8,128)(2,1)}, bf16[512,2048]{1,0:T(8,128)(2,1)}, u32[]{:S(2)}, u32[]{:S(2)}) collective-permute-start(bf16[512,2048]{1,0:T(8,128)(2,1)} %convolution_convert_fusion.2), channel_id=1, source_target_pairs={{0,1},{1,0},{2,3},{3,2},{4,5},{5,4},{6,7},{7,6},{8,9},{9,8},{10,11... | collective-permute-start | bytes 6291464 | tf_op jit(solution)/shard_map/ppermute | solution.py:26
  367.1 16.0 %collective-permute-start.49 = (bf16[160,2048]{1,0:T(8,128)(2,1)S(1)}, bf16[160,2048]{1,0:T(8,128)(2,1)S(1)}, u32[]{:S(2)}, u32[]{:S(2)}) collective-permute-start(bf16[160,2048]{1,0:T(8,128)(2,1)S(1)} %pad_maximum_fusion.6), channel_id=1, source_target_pairs={{8,0},{10,2},{16,8},{18,10},{24,16},{26,18},{28,24},{30,26},{20,28... | collective-permute-start | bytes 1966088 | tf_op jit(solution)/shard_map/ppermute | solution.py:49
  368.4 15.7 %collective-permute-start.45 = (bf16[160,2048]{1,0:T(8,128)(2,1)S(1)}, bf16[160,2048]{1,0:T(8,128)(2,1)S(1)}, u32[]{:S(2)}, u32[]{:S(2)}) collective-permute-start(bf16[160,2048]{1,0:T(8,128)(2,1)S(1)} %pad_maximum_fusion.5), channel_id=1, source_target_pairs={{0,8},{2,10},{8,16},{10,18},{16,24},{18,26},{24,28},{26,30},{28,20... | collective-permute-start | bytes 1966088 | tf_op jit(solution)/shard_map/ppermute | solution.py:45
  376.3 57.6 %collective-permute-start.53 = (bf16[1024,512]{1,0:T(8,128)(2,1)}, bf16[1024,512]{1,0:T(8,128)(2,1)}, u32[]{:S(2)}, u32[]{:S(2)}) collective-permute-start(bf16[1024,512]{1,0:T(8,128)(2,1)} %slice.263), channel_id=1, source_target_pairs={{0,1},{1,0},{2,3},{3,2},{4,5},{5,4},{6,7},{7,6},{8,9},{9,8},{10,11... | collective-permute-start | bytes 3145736 | tf_op jit(solution)/shard_map/ppermute | solution.py:26
  384.6 14.9 %collective-permute-start.50 = (bf16[160,2048]{1,0:T(8,128)(2,1)S(1)}, bf16[160,2048]{1,0:T(8,128)(2,1)S(1)}, u32[]{:S(2)}, u32[]{:S(2)}) collective-permute-start(bf16[160,2048]{1,0:T(8,128)(2,1)S(1)} %get-tuple-element.397), channel_id=1, source_target_pairs={{8,0},{10,2},{16,8},{18,10},{24,16},{26,18},{28,24},{30,26},{20,28... | collective-permute-start | bytes 1966088 | tf_op jit(solution)/shard_map/ppermute | solution.py:49
  401.1 19.6 %collective-permute-start.47 = (bf16[160,2048]{1,0:T(8,128)(2,1)}, bf16[160,2048]{1,0:T(8,128)(2,1)S(1)}, u32[]{:S(2)}, u32[]{:S(2)}) collective-permute-start(bf16[160,2048]{1,0:T(8,128)(2,1)} %get-tuple-element.394), channel_id=1, source_target_pairs={{0,8},{2,10},{8,16},{10,18},{16,24},{18,26},{24,28},{26,30},{28,20... | collective-permute-start | bytes 1966088 | tf_op jit(solution)/shard_map/ppermute | solution.py:45
  402.6 18.9 %collective-permute-start.51 = (bf16[160,2048]{1,0:T(8,128)(2,1)S(1)}, bf16[160,2048]{1,0:T(8,128)(2,1)}, u32[]{:S(2)}, u32[]{:S(2)}) collective-permute-start(bf16[160,2048]{1,0:T(8,128)(2,1)S(1)} %get-tuple-element.395), channel_id=1, source_target_pairs={{8,0},{10,2},{16,8},{18,10},{24,16},{26,18},{28,24},{30,26},{20,28... | collective-permute-start | bytes 1966088 | tf_op jit(solution)/shard_map/ppermute | solution.py:49
  437.2 15.3 %collective-permute-start.54 = (bf16[160,2048]{1,0:T(8,128)(2,1)S(1)}, bf16[160,2048]{1,0:T(8,128)(2,1)S(1)}, u32[]{:S(2)}, u32[]{:S(2)}) collective-permute-start(bf16[160,2048]{1,0:T(8,128)(2,1)S(1)} %get-tuple-element.372), channel_id=1, source_target_pairs={{0,1},{1,0},{2,3},{3,2},{4,5},{5,4},{6,7},{7,6},{8,9},{9,8},{10,11... | collective-permute-start | bytes 1966088 | tf_op jit(solution)/shard_map/ppermute | solution.py:26
  460.5 35.3 %collective-permute-start.58 = (bf16[1024,512]{1,0:T(8,128)(2,1)}, bf16[1024,512]{1,0:T(8,128)(2,1)}, u32[]{:S(2)}, u32[]{:S(2)}) collective-permute-start(bf16[1024,512]{1,0:T(8,128)(2,1)} %slice.213), channel_id=1, source_target_pairs={{0,1},{1,0},{2,3},{3,2},{4,5},{5,4},{6,7},{7,6},{8,9},{9,8},{10,11... | collective-permute-start | bytes 3145736 | tf_op jit(solution)/shard_map/ppermute | solution.py:26
  482.7 43.7 %collective-permute-start.56 = (bf16[320,2048]{1,0:T(8,128)(2,1)}, bf16[320,2048]{1,0:T(8,128)(2,1)}, u32[]{:S(2)}, u32[]{:S(2)}) collective-permute-start(bf16[320,2048]{1,0:T(8,128)(2,1)} %multiply_convert_fusion.refs_0_), channel_id=1, source_target_pairs={{0,2},{2,0},{4,6},{6,4},{8,10},{10,8},{12,14},{14,12},{16,18},{18,... | collective-permute-start | bytes 3932168 | tf_op jit(solution)/shard_map/ppermute | solution.py:22
  484.2 42.2 %collective-permute-start.57 = (bf16[320,2048]{1,0:T(8,128)(2,1)S(1)}, bf16[320,2048]{1,0:T(8,128)(2,1)}, u32[]{:S(2)}, u32[]{:S(2)}) collective-permute-start(bf16[320,2048]{1,0:T(8,128)(2,1)S(1)} %copy-done.12), channel_id=1, source_target_pairs={{0,2},{2,0},{4,6},{6,4},{8,10},{10,8},{12,14},{14,12},{16,18},{18,... | collective-permute-start | bytes 3932168 | tf_op jit(solution)/shard_map/ppermute | solution.py:22
  492.0 30.1 %collective-permute-start.65 = (bf16[2,128,1024]{2,1,0:T(8,128)(2,1)}, bf16[2,128,1024]{2,1,0:T(8,128)(2,1)}, u32[]{:S(2)}, u32[]{:S(2)}) collective-permute-start(bf16[2,128,1024]{2,1,0:T(8,128)(2,1)} %get-tuple-element.271), channel_id=1, source_target_pairs={{0,8},{2,10},{4,12},{6,14},{8,0},{10,2},{12,4},{14,6},{16,24},{18,... | collective-permute-start | bytes 1572872 | tf_op jit(solution)/shard_map/ppermute | solution.py:22
  492.6 29.6 %collective-permute-start.64 = (bf16[2,128,1024]{2,1,0:T(8,128)(2,1)}, bf16[2,128,1024]{2,1,0:T(8,128)(2,1)}, u32[]{:S(2)}, u32[]{:S(2)}) collective-permute-start(bf16[2,128,1024]{2,1,0:T(8,128)(2,1)} %get-tuple-element.270), channel_id=1, source_target_pairs={{0,4},{2,6},{4,0},{6,2},{8,12},{10,14},{12,8},{14,10},{16,20},{18,... | collective-permute-start | bytes 1572872 | tf_op jit(solution)/shard_map/ppermute | solution.py:22
  495.8 45.1 %collective-permute-start.59 = (bf16[1024,512]{1,0:T(8,128)(2,1)}, bf16[1024,512]{1,0:T(8,128)(2,1)}, u32[]{:S(2)}, u32[]{:S(2)}) collective-permute-start(bf16[1024,512]{1,0:T(8,128)(2,1)} %slice.214), channel_id=1, source_target_pairs={{0,1},{1,0},{2,3},{3,2},{4,5},{5,4},{6,7},{7,6},{8,9},{9,8},{10,11... | collective-permute-start | bytes 3145736 | tf_op jit(solution)/shard_map/ppermute | solution.py:26
  584.2 25.1 %collective-permute-start.71 = (bf16[256,2048]{1,0:T(8,128)(2,1)S(1)}, bf16[256,2048]{1,0:T(8,128)(2,1)}, u32[]{:S(2)}, u32[]{:S(2)}) collective-permute-start(bf16[256,2048]{1,0:T(8,128)(2,1)S(1)} %pad_maximum_fusion.3), channel_id=1, source_target_pairs={{8,0},{10,2},{16,8},{18,10},{24,16},{26,18},{28,24},{30,26},{20,28... | collective-permute-start | bytes 3145736 | tf_op jit(solution)/shard_map/ppermute | solution.py:49
  586.3 24.4 %collective-permute-start.76 = (bf16[256,2048]{1,0:T(8,128)(2,1)}, bf16[256,2048]{1,0:T(8,128)(2,1)}, u32[]{:S(2)}, u32[]{:S(2)}) collective-permute-start(bf16[256,2048]{1,0:T(8,128)(2,1)} %pad_maximum_fusion.4), channel_id=1, source_target_pairs={{0,8},{2,10},{8,16},{10,18},{16,24},{18,26},{24,28},{26,30},{28,20... | collective-permute-start | bytes 3145736 | tf_op jit(solution)/shard_map/ppermute | solution.py:45
  587.6 16.7 %collective-permute-start.81 = (bf16[512,512]{1,0:T(8,128)(2,1)}, bf16[512,512]{1,0:T(8,128)(2,1)}, u32[]{:S(2)}, u32[]{:S(2)}) collective-permute-start(bf16[512,512]{1,0:T(8,128)(2,1)} %get-tuple-element.307), channel_id=1, source_target_pairs={{0,1},{1,0},{2,3},{3,2},{4,5},{5,4},{6,7},{7,6},{8,9},{9,8},{10,11... | collective-permute-start | bytes 1572872 | tf_op jit(solution)/shard_map/ppermute | solution.py:26
  589.2 85.5 %collective-permute-start.69 = (bf16[160,2048]{1,0:T(8,128)(2,1)}, bf16[160,2048]{1,0:T(8,128)(2,1)}, u32[]{:S(2)}, u32[]{:S(2)}) collective-permute-start(bf16[160,2048]{1,0:T(8,128)(2,1)} %reduce-scatter.2.cloned.1.call-done), channel_id=1, source_target_pairs={{0,1},{1,0},{2,3},{3,2},{4,5},{5,4},{6,7},{7,6},{8,9},{9,8},{10,11... | collective-permute-start | bytes 1966088 | tf_op jit(solution)/shard_map/ppermute | solution.py:26
  600.6 30.2 %collective-permute-start.73 = (bf16[160,2048]{1,0:T(8,128)(2,1)S(1)}, bf16[160,2048]{1,0:T(8,128)(2,1)S(1)}, u32[]{:S(2)}, u32[]{:S(2)}) collective-permute-start(bf16[160,2048]{1,0:T(8,128)(2,1)S(1)} %dynamic-slice_convert_fusion), channel_id=1, source_target_pairs={{0,1},{1,0},{2,3},{3,2},{4,5},{5,4},{6,7},{7,6},{8,9},{9,8},{10,11... | collective-permute-start | bytes 1966088 | tf_op jit(solution)/shard_map/ppermute | solution.py:26
  604.4 61.3 %collective-permute-start.82 = (bf16[512,512]{1,0:T(8,128)(2,1)}, bf16[512,512]{1,0:T(8,128)(2,1)}, u32[]{:S(2)}, u32[]{:S(2)}) collective-permute-start(bf16[512,512]{1,0:T(8,128)(2,1)} %get-tuple-element.308), channel_id=1, source_target_pairs={{0,1},{1,0},{2,3},{3,2},{4,5},{5,4},{6,7},{7,6},{8,9},{9,8},{10,11... | collective-permute-start | bytes 1572872 | tf_op jit(solution)/shard_map/ppermute | solution.py:26
  613.7 29.0 %collective-permute-start.72 = (bf16[256,2048]{1,0:T(8,128)(2,1)S(1)}, bf16[256,2048]{1,0:T(8,128)(2,1)S(1)}, u32[]{:S(2)}, u32[]{:S(2)}) collective-permute-start(bf16[256,2048]{1,0:T(8,128)(2,1)S(1)} %get-tuple-element.381), channel_id=1, source_target_pairs={{8,0},{10,2},{16,8},{18,10},{24,16},{26,18},{28,24},{30,26},{20,28... | collective-permute-start | bytes 3145736 | tf_op jit(solution)/shard_map/ppermute | solution.py:49
  615.4 27.3 %collective-permute-start.77 = (bf16[256,2048]{1,0:T(8,128)(2,1)S(1)}, bf16[256,2048]{1,0:T(8,128)(2,1)S(1)}, u32[]{:S(2)}, u32[]{:S(2)}) collective-permute-start(bf16[256,2048]{1,0:T(8,128)(2,1)S(1)} %get-tuple-element.380), channel_id=1, source_target_pairs={{0,8},{2,10},{8,16},{10,18},{16,24},{18,26},{24,28},{26,30},{28,20... | collective-permute-start | bytes 3145736 | tf_op jit(solution)/shard_map/ppermute | solution.py:45
  632.8 49.0 %collective-permute-start.74 = (f32[160,2048]{1,0:T(8,128)}, f32[160,2048]{1,0:T(8,128)}, u32[]{:S(2)}, u32[]{:S(2)}) collective-permute-start(f32[160,2048]{1,0:T(8,128)} %fusion.6), channel_id=1, source_target_pairs={{0,1},{1,0},{2,3},{3,2},{4,5},{5,4},{6,7},{7,6},{8,9},{9,8},{10,11... | collective-permute-start | bytes 3932168 | tf_op jit(solution)/shard_map/ppermute | solution.py:26
  646.5 31.8 %collective-permute-start.78 = (bf16[256,2048]{1,0:T(8,128)(2,1)}, bf16[256,2048]{1,0:T(8,128)(2,1)}, u32[]{:S(2)}, u32[]{:S(2)}) collective-permute-start(bf16[256,2048]{1,0:T(8,128)(2,1)} %get-tuple-element.378), channel_id=1, source_target_pairs={{0,8},{2,10},{8,16},{10,18},{16,24},{18,26},{24,28},{26,30},{28,20... | collective-permute-start | bytes 3145736 | tf_op jit(solution)/shard_map/ppermute | solution.py:45
  648.5 29.9 %collective-permute-start.79 = (bf16[256,2048]{1,0:T(8,128)(2,1)}, bf16[256,2048]{1,0:T(8,128)(2,1)}, u32[]{:S(2)}, u32[]{:S(2)}) collective-permute-start(bf16[256,2048]{1,0:T(8,128)(2,1)} %get-tuple-element.379), channel_id=1, source_target_pairs={{8,0},{10,2},{16,8},{18,10},{24,16},{26,18},{28,24},{30,26},{20,28... | collective-permute-start | bytes 3145736 | tf_op jit(solution)/shard_map/ppermute | solution.py:49
  649.3 28.9 %all-to-all-start = ((f32[32,1,512]{2,1,0:T(1,128)}), f32[32,1,512]{2,1,0:T(1,128)S(1)}, u32[]{:S(2)}, u32[]{:S(2)}) async-start(f32[32,1,512]{2,1,0:T(1,128)} %all_to_all.6), calls=%async_computation.1 | async-start | bytes 131072 | tf_op jit(solution)/shard_map/all_to_all | solution.py:1162
  (90 other events, 960.5 us)
Sparse Core Ops, SparseCore 0:
  12.7 94.2 all-gather.4
  109.9 98.4 all-gather.6
  434.1 132.8 reduce-scatter.1

commit v11 on v10

--- a/solution.py
+++ b/solution.py
@@ -192,12 +192,13 @@
     return pltpu.roll(values, HEAD // 2, 1)
 
 
-def rope_kernel(pre_ref, gain_ref, scale_ref, cos_ref, sin_ref, out_ref):
+def rope_kernel(pre_ref, gain_ref, scale_ref, cos_ref, sin_ref, out_ref, first_ref):
     scale, cosine, sine = scale_ref[...], cos_ref[...], sin_ref[...]
     for at in range(0, pre_ref.shape[1], HEAD):
         span = slice(at, at + HEAD)
         normed = pre_ref[:, span] * scale * gain_ref[:, span]
         out_ref[:, span] = (normed * cosine + turn(normed) * sine).astype(LOW)
+    first_ref[...] = out_ref[: first_ref.shape[0]]
 
 
 def rope_pass(flat, gain, scale, cosine, sine):
@@ -208,8 +209,8 @@
         rope_kernel,
         grid=(2,),
         in_specs=[wide(rows), wide(1)] + [kept_spec(a) for a in (scale, cosine, sine)],
-        out_specs=wide(rows),
-        out_shape=jax.ShapeDtypeStruct((rows, width), LOW),
+        out_specs=[wide(rows), wide(PR_DEV)],
+        out_shape=[jax.ShapeDtypeStruct((count, width), LOW) for count in (rows, PR_DEV)],
     )(flat, gain, scale, cosine, sine)
 
 
@@ -464,6 +465,59 @@
     )(blocks, packed)
 
 
+def load_packed(gathered, places, block, held, sems):
+    copies = [
+        pltpu.make_async_copy(
+            gathered.at[:, pl.ds(place * block, block)], held.at[k], sems.at[k]
+        )
+        for k, place in enumerate(places)
+    ]
+    for one in copies:
+        one.start()
+    return copies
+
+
+def held_pack(gathered, places, block):
+    count, columns = gathered.shape[0], gathered.shape[2]
+    return [
+        pltpu.VMEM((len(places), count, block, columns), LOW),
+        pltpu.SemaphoreType.DMA((len(places),)),
+    ]
+
+
+def project_kernel(places, block, heads, rows_ref, gathered, *refs):
+    outs, firsts, (held, sems) = refs[: len(places)], refs[len(places) : -2], refs[-2:]
+    copies = load_packed(gathered, places, block, held, sems)
+    rows = rows_ref[...]
+    for k, (one, out) in enumerate(zip(copies, outs)):
+        one.wait()
+        out[...] = dot_nn(rows, held[k].reshape(-1, out.shape[1])).astype(out.dtype)
+    for first, k in zip(firsts, heads):
+        first[...] = outs[k][: first.shape[0]]
+
+
+def project(rows, gathered, block, places, roundings, heads=()):
+    count, width = rows.shape
+    columns = gathered.shape[2]
+    outs = [jax.ShapeDtypeStruct((count, columns), rounding) for rounding in roundings]
+    outs += [jax.ShapeDtypeStruct((PR_DEV, columns), roundings[k]) for k in heads]
+    fixed = lambda a: pl.BlockSpec(a.shape, lambda i: (0, 0))
+    return pl.pallas_call(
+        lambda *refs: project_kernel(places, block, heads, *refs),
+        grid=(1,),
+        in_specs=[fixed(rows), pl.BlockSpec(memory_space=pl.ANY)],
+        out_specs=[fixed(out) for out in outs],
+        out_shape=outs,
+        scratch_shapes=held_pack(gathered, places, block),
+        compiler_params=pltpu.CompilerParams(vmem_limit_bytes=VMEM),
+        cost_estimate=pl.CostEstimate(
+            flops=2 * count * width * columns * len(places),
+            bytes_accessed=2 * width * columns * len(places) + 8 * count * columns,
+            transcendentals=0,
+        ),
+    )(rows, gathered)
+
+
 def pack_specs(gathered, places, steps, at):
     count, width = gathered.shape[0] // steps, gathered.shape[2]
     block = at
@@ -473,49 +527,6 @@
     ]
 
 
-def project_kernel(mats, roundings, rows_ref, *refs):
-    mat_refs, out_refs, totals = refs[:mats], refs[mats : 2 * mats], refs[2 * mats :]
-    step = pl.program_id(0)
-    rows = rows_ref[...]
-    for mat, out, total, rounding in zip(mat_refs, out_refs, totals, roundings):
-        flat = mat[...].reshape(-1, mat.shape[2])
-        part = dot_nn(rows, flat)
-
-        @pl.when(step == 0)
-        def _():
-            total[...] = part
-
-        @pl.when(step > 0)
-        def _():
-            total[...] += part
-
-        @pl.when(step == pl.num_programs(0) - 1)
-        def _():
-            out[...] = total[...].astype(rounding)
-
-
-def project(rows, gathered, block, places, roundings):
-    count, width = rows.shape
-    columns = gathered.shape[2]
-    steps = 4
-    outs = [jax.ShapeDtypeStruct((count, columns), rounding) for rounding in roundings]
-    return pl.pallas_call(
-        lambda *refs: project_kernel(len(places), roundings, *refs),
-        grid=(steps,),
-        in_specs=[pl.BlockSpec((count, width // steps), lambda i: (0, i))]
-        + pack_specs(gathered, places, steps, block),
-        out_specs=[pl.BlockSpec((count, columns), lambda i: (0, 0)) for _ in outs],
-        out_shape=outs,
-        scratch_shapes=[pltpu.VMEM((count, columns), FULL)] * len(outs),
-        compiler_params=pltpu.CompilerParams(vmem_limit_bytes=VMEM),
-        cost_estimate=pl.CostEstimate(
-            flops=2 * count * width * columns * len(places),
-            bytes_accessed=2 * width * columns * len(places) + 8 * count * columns,
-            transcendentals=0,
-        ),
-    )(rows, *[gathered] * len(places))
-
-
 def project_back_kernel(mats, *refs):
     out = refs[-1]
     total = None
@@ -528,7 +539,7 @@
 def project_back(rows, gathered, block, places):
     count, columns = rows[0].shape
     width = gathered.shape[0] * block
-    steps = 4
+    steps = 4 if len(places) > 1 else 2
     fixed = pl.BlockSpec((count, columns), lambda i: (0, 0), pipeline_mode=pl.Buffered(1))
     return pl.pallas_call(
         lambda *refs: project_back_kernel(len(places), *refs),
@@ -645,14 +656,73 @@
     outward, inward = part(3), part(-3)
     right = jnp.concatenate([add_low(outward[:, :cut], right), outward[:, cut:]], axis=1)
     left = jnp.concatenate([inward[:, :cut], add_low(inward[:, cut:], left)], axis=1)
+    right, left = together(right, left)
     right, left = ahead(right), behind(left)
     fillers.next(left)
     token = left
     for hop in (2, 1):
-        right, left = ahead(add_low(part(hop), right)), behind(add_low(part(-hop), left))
+        right, left = together(add_low(part(hop), right), add_low(part(-hop), left))
+        right, left = ahead(right), behind(left)
         fillers.next(left)
         token = left if hop == 2 else token
-    return part(0).astype(FULL) + right.astype(FULL) + left.astype(FULL), token
+    return (blocks, right, left), token
+
+
+def sum_kernel(core_ref, blocks_ref, right_ref, left_ref, own_ref, sent_ref):
+    rows = own_ref.shape[0]
+    for k, out in enumerate((own_ref, sent_ref)):
+        side = core_ref[0] if k == 0 else 1 - core_ref[0]
+        span = pl.ds(pl.multiple_of(side * rows, rows), rows)
+        out[...] = (
+            blocks_ref[0, span].astype(FULL)
+            + right_ref[span].astype(FULL)
+            + left_ref[span].astype(FULL)
+        )
+
+
+def sum_weights(core, blocks, right, left):
+    rows, width = right.shape
+    whole = pl.BlockSpec((rows, width), lambda i: (0, 0))
+    half = pl.BlockSpec((rows // 2, width), lambda i: (0, 0))
+    return pl.pallas_call(
+        sum_kernel,
+        grid=(1,),
+        in_specs=[
+            pl.BlockSpec(memory_space=pltpu.SMEM),
+            pl.BlockSpec((1, rows, width), lambda i: (HOPS.index(0), 0, 0)),
+            whole,
+            whole,
+        ],
+        out_specs=[half, half],
+        out_shape=[jax.ShapeDtypeStruct((rows // 2, width), FULL)] * 2,
+    )(core, blocks, right, left)
+
+
+def place_kernel(core_ref, own_ref, got_ref, *outs):
+    columns = own_ref.shape[1] // 4
+    first = core_ref[0] == 0
+    for k, out in enumerate(outs):
+        span = slice(k * columns, (k + 1) * columns)
+        own, got = own_ref[:, span], got_ref[:, span]
+        left, right = jnp.where(first, own, got), jnp.where(first, got, own)
+        if k < 3:
+            out[:, :columns], out[:, columns:] = left, right
+        else:
+            out[:columns], out[columns:] = left.T, right.T
+
+
+def place_weights(core, own, got):
+    rows, width = own.shape
+    columns = width // 2
+    shapes = [(rows, columns)] * 3 + [(columns, rows)]
+    return pl.pallas_call(
+        place_kernel,
+        grid=(1,),
+        in_specs=[pl.BlockSpec(memory_space=pltpu.SMEM)]
+        + [pl.BlockSpec((rows, width), lambda i: (0, 0))] * 2,
+        out_specs=[pl.BlockSpec(shape, lambda i: (0, 0)) for shape in shapes],
+        out_shape=[jax.ShapeDtypeStruct(shape, FULL) for shape in shapes],
+    )(core, own, got)
 
 
 def expert_kernel(
@@ -1011,11 +1081,11 @@
     weight = weight.reshape(-1, 1)
 
     normed_b = rms_norm(tokens_f, gain_one).astype(LOW)
-    query_flat, key_flat, values_b = project(
-        normed_b, gathered, block, (0, 1, 2), (FULL, FULL, LOW)
+    query_flat, key_flat, values_b, value_prompt = project(
+        normed_b, gathered, block, (0, 1, 2), (FULL, FULL, LOW), (2,)
     )
     key_sq = jnp.sum(key_flat * key_flat, axis=1)
-    key_sq, value_prompt = together(key_sq, values_b[:PR_DEV])
+    key_sq, value_prompt = together(key_sq, value_prompt)
     value_pieces = collect_prompt(value_prompt, 1, 2)
     query_sq, key_sq = lax.psum(
         (jnp.sum(query_flat * query_flat, axis=1), key_sq), "tensor"
@@ -1024,8 +1094,8 @@
     down_mats = (down_mat, swap_tensor(down_mat))
     query_scale = lax.rsqrt(query_sq / column_total + EPSILON)[:, None]
     key_scale = lax.rsqrt(key_sq / column_total + EPSILON)[:, None]
-    keys_b = rope_pass(key_flat, gain_key_local[None], key_scale, cosine, sine)
-    pieces = (*collect_prompt(keys_b[:PR_DEV], 2, 1), *value_pieces)
+    keys_b, key_prompt = rope_pass(key_flat, gain_key_local[None], key_scale, cosine, sine)
+    pieces = (*collect_prompt(key_prompt, 2, 1), *value_pieces)
     turned_by = (gain_query_local[None], query_scale, cosine, sine, bias)
     context_b = attend(query_flat, *turned_by, keys_b, values_b, pieces)
     attn_part = project_back([context_b], gathered, block, (3,))
@@ -1081,7 +1151,8 @@
         down_got = swap_tensor(low_tn(h1, back_rows))
         gate_sent = low_tn(expert_in, g1)
         up_sent = low_tn(expert_in, u1)
-    gate_first = swap_tensor(upper(gate_sent))
+    quarter = gate_sent.shape[0] // 4
+    gate_first = swap_tensor(gate_sent[:quarter])
     normed_two_grad, down_got, gate_first, mixed_rows, up_sent = together(
         normed_two_grad, down_got, gate_first, mixed_rows, up_sent
     )
@@ -1094,7 +1165,11 @@
     attn_grad_b = both_halves(attn_grad_half, swap_tensor(attn_grad_half))
     attn_grad_b, gate_sent, up_sent = together(attn_grad_b, gate_sent, up_sent)
     (context_grad_b,) = project(attn_grad_b, gathered, block, (3,), (LOW,))
-    soon = swap_in_turn([lower(gate_sent), upper(up_sent)], context_grad_b)
+    (gate_middle,) = swap_in_turn([gate_sent[quarter : 3 * quarter]], context_grad_b)
+    soon = [
+        swap_tensor(after(piece, gate_middle))
+        for piece in (gate_sent[3 * quarter :], upper(up_sent))
+    ]
     if ring:
         pair = lambda own: (own, swap_bit(own, "dp", 0))
         columns = local_width // 2
@@ -1129,7 +1204,7 @@
         (key_flat, key_normed_grad, gain_key_local[None], key_scale, key_inner[:, None]),
         value_pre_grad,
     )
-    gate_got = jnp.concatenate([gate_first, soon[0]], axis=0)
+    gate_got = jnp.concatenate([gate_first, gate_middle, soon[0]], axis=0)
     pre_grads = (query_pre_grad, key_pre_grad, value_pre_grad)
     grad_sum = lambda left, right, got: dot_tn(left, right) + got.astype(FULL)
     back_all = lambda *grads: project_back(grads, gathered, block, (0, 1, 2))
@@ -1175,10 +1250,8 @@
             context_got,
         )
         w_blocks, mixed, *far = together(w_blocks, mixed, *far)
-        up_got = jnp.concatenate(
-            [soon[1], *swap_in_turn(cut_rows(lower(up_sent), 2), far[0])], axis=0
-        )
-        mixed_other = swap_tensor(mixed)
+        up_third, up_last = cut_rows(lower(up_sent), 2)
+        up_third = swap_tensor(after(up_third, far[0]))
         late = {}
 
         def normed_stage(gated):
@@ -1186,34 +1259,31 @@
 
         def input_stage(gated):
             late["input"] = input_side(late["normed"][0], gated(late["normed"][1]))
+            late["up"] = swap_tensor(after(up_last, late["input"][0]))
             late["down"] = grad_sum(gated(h0), back_rows, down_got)
 
         def expert_stage(gated):
             late["gains"] = gain_side(gated(late["normed"][2]))
+            late["mixed"] = swap_tensor(gated(mixed))
             late["gate"] = grad_sum(gated(expert_in), g0, gate_got)
 
         fillers = Fillers(normed_stage, input_stage, expert_stage)
-        w_half, token = ring_weights(w_blocks, *far, fillers)
+        w_parts, token = ring_weights(w_blocks, *far, fillers)
         input_half, input_other = late["input"]
         gain_sums = late["gains"]
         down_grad, gate_w_grad = late["down"], late["gate"]
+        up_got = jnp.concatenate([soon[1], up_third, late["up"]], axis=0)
         up_w_grad = grad_sum(after(expert_in, token), u0, up_got)
-        own_w = lax.dynamic_slice_in_dim(w_half, core * block, block, axis=0)
-        got_w = swap_bit(
-            lax.dynamic_slice_in_dim(w_half, (1 - core) * block, block, axis=0), "dp", 0
-        )
-        left_w, right_w = jnp.where(core == 0, own_w, got_w), jnp.where(core == 0, got_w, own_w)
-        w_sums = [
-            jnp.concatenate([w[:, j * columns : (j + 1) * columns] for w in (left_w, right_w)], axis=1)
-            for j in range(4)
-        ]
-        mixed_other = after(mixed_other, token)
+        own_w, sent_w = sum_weights(core[None], *w_parts)
+        w_sums = place_weights(core[None], own_w, swap_bit(sent_w, "dp", 0))
+        mixed_other = late["mixed"]
     else:
         w_grads = jnp.concatenate(
             [low_tn(normed_b, g) for g in pre_grads] + [low_tn(attn_grad_b, context_b)], axis=1
         )
         w_sum = lax.psum_scatter(w_grads, "dp", scatter_dimension=0, tiled=True).astype(FULL)
         w_sums = [w_sum[:, j * local_width : (j + 1) * local_width] for j in range(4)]
+        w_sums[3] = w_sums[3].T
         down_grad = grad_sum(h0, back_rows, down_got)
         gate_w_grad = grad_sum(expert_in, g0, gate_got)
         up_got = jnp.concatenate([soon[1], swap_tensor(lower(up_sent))], axis=0)
@@ -1235,7 +1305,7 @@
         w_sums[2],
         gain_sums[2],
         gain_sums[3],
-        w_sums[3].T,
+        w_sums[3],
         gain_sums[1],
         gate_w_grad[None],
         up_w_grad[None],

time: 706 us -> 702 us (level)
    ppermute x18 -> x19, waiting for transfers between devices: 131 us -> 109 us  [swap_tensor(): return lax.ppermute(block, 'tensor', [(0, 1), (1, 0)])]
    ppermute x12, waiting for transfers between devices: 26.7 us -> 43.3 us  [behind(): return lax.ppermute(block, 'dp', BEHIND)]
    pallas_call x2 -> x4, Pallas kernels: 17.5 us -> 21.7 us  [the longest x2 15.3 us: project(): pl.pallas_call(lambda *refs: project_kernel(places, block, heads, *refs),...]
    ppermute x18 -> x19, starting transfers between devices: 24.7 us -> 24 us  [swap_tensor(): return lax.ppermute(block, 'tensor', [(0, 1), (1, 0)])]
  transfers between devices with their start and end apart: 87 -> 88, of which waited for: 31 -> 29; matrix products, arithmetic and copies ran while one was open for 18% -> 18% of each run, Pallas kernels for 31% -> 31%
where the time goes in v11:
time: 702 us; the launch traced here: 695 us
  waiting for transfers between devices  243 us (35%)
  Pallas kernels  219 us (31%)
  starting transfers between devices  69.7 us (10%)
  matrix products  53.9 us (8%)
  other arithmetic  49.8 us (7%)
  local copies, waits for them, and re-layouts  34.5 us (5%)
  between operations  15.4 us (2%)
  blocking collectives  10.1 us (1%)
    ppermute x19, waiting for transfers between devices, swap_tensor(): return lax.ppermute(block, 'tensor', [(0, 1), (1, 0)])  109 us
    pallas_call x5, Pallas kernels, expert_chunk(): pl.pallas_call(lambda *refs: chunk_kernel(len(pieces), len(held), at, spl...  92.2 us
    ppermute x41, waiting for transfers between devices, swap_bit(): return lax.ppermute(block, axis, [(i, i ^ 1 << bit) for i in range(count)])  81.1 us
    dot_general x6, matrix products, dot_tn(): lax.dot_general(left, right, (((0,), (0,)), ((), ())), preferred_element_...  53.7 us
    ppermute x12, waiting for transfers between devices, behind(): return lax.ppermute(block, 'dp', BEHIND)  43.3 us
    ppermute x19, starting transfers between devices, swap_tensor(): return lax.ppermute(block, 'tensor', [(0, 1), (1, 0)])  24 us
    pallas_call x1, Pallas kernels, attend_back(): pl.pallas_call(attend_back_kernel, grid=(width // HEAD // PAIR,), in_spec...  19.8 us
    pallas_call x1, Pallas kernels, mixed_pass(): pl.pallas_call(mixed_kernel, grid_spec=pltpu.PrefetchScalarGridSpec(num_s...  17.6 us
  transfers between devices with their start and end apart: 88, of which 29 were waited for; matrix products, arithmetic and copies ran while one was open for 18% of the time, Pallas kernels for 31%

profile of v11, /device:TPU:0, one launch (start us, length us, event | category | flops | bytes accessed | tf_op | source)
XLA Modules:
  0.0 694.9 jit_solution(4634561854778129194)
XLA Ops:
  10.1 2.4 shard_map.309
  12.7 2.3 dynamic-slice_convert_fusion.2
  15.1 3.0 collective-permute-start
  22.0 42.7 %collective-permute-done.refs_5_.refs_7_.refs_9_ = bf16[2048,512]{1,0:T(8,128)(2,1)} collective-permute-done((bf16[2048,512]{1,0:T(8,128)(2,1)S(1)}, bf16[2048,512]{1,0:T(8,128)(2,1)}, u32[]{:S(2)}, u32[]{:S(2)}) %collective-permute-start) | collective-permute-done | bytes 2097184 | tf_op jit(solution)/shard_map/ppermute | solution.py:26
  64.7 44.1 %collective-permute-done.1.refs_7_.refs_9_.refs_11_ = bf16[2048,512]{1,0:T(8,128)(2,1)} collective-permute-done((bf16[2048,512]{1,0:T(8,128)(2,1)}, bf16[2048,512]{1,0:T(8,128)(2,1)}, u32[]{:S(2)}, u32[]{:S(2)}) %collective-permute-start.1) | collective-permute-done | bytes 2097184 | tf_op jit(solution)/shard_map/ppermute | solution.py:26
  111.9 9.0 %shard_map.310 = (f32[320,1024]{1,0:T(8,128)}, f32[320,1024]{1,0:T(8,128)}, bf16[320,1024]{1,0:T(8,128)(2,1)}, bf16[128,1024]{1,0:T(8,128)(2,1)}) custom-call(bf16[320,2048]{1,0:T(8,128)(2,1)} %multiply_convert_fusion.refs_0_, bf16[16,528,1024]{2,1,0:T(8,128)(2,1)} %bitcast.86), custom_call_target="tpu_custom_call" | custom-call | flops 4026531840 | bytes 15204352 | tf_op jit(solution)/shard_map/pallas_call | solution.py:505
  124.1 5.1 all-reduce.3
  132.4 2.7 shard_map.311
  138.7 9.2 %collective-permute-done.5.refs_3_ = bf16[128,1024]{1,0:T(8,128)(2,1)} collective-permute-done((bf16[128,1024]{1,0:T(8,128)(2,1)}, bf16[128,1024]{1,0:T(8,128)(2,1)}, u32[]{:S(2)}, u32[]{:S(2)}) %collective-permute-start.5) | collective-permute-done | bytes 262176 | tf_op jit(solution)/shard_map/ppermute | solution.py:22
  152.0 6.2 collective-permute-done.12.refs_10_
  158.4 5.3 collective-permute-done.7.refs_5_
  164.3 18.2 %collective-permute-done.14.refs_12_ = bf16[128,1024]{1,0:T(8,128)(2,1)} collective-permute-done((bf16[128,1024]{1,0:T(8,128)(2,1)}, bf16[128,1024]{1,0:T(8,128)(2,1)}, u32[]{:S(2)}, u32[]{:S(2)}) %collective-permute-start.14) | collective-permute-done | bytes 262176 | tf_op jit(solution)/shard_map/ppermute | solution.py:22
  184.7 11.9 %shard_map.312.refs_0_.refs_8_ = bf16[320,1024]{1,0:T(8,128)(2,1)} custom-call(f32[320,1024]{1,0:T(8,128)} %get-tuple-element.179.flat_ref.refs_0_, f32[1,1024]{1,0:T(1,128)} %bitcast.126, f32[320,1]{1,0:T(8,128)} %broadcast_in_dim.140.scale_ref.refs_3_, f32[320,128]{1,0:T(8,128)} %get-tuple-element.181.cos_ref.refs_5_, ...), custom_call_target="tpu_custom_call" | custom-call | tf_op jit(solution)/shard_map/pallas_call | solution.py:272
  196.6 4.6 shard_map.313
  201.2 2.2 dynamic-slice_convert_fusion.1
  207.4 8.9 %shard_map.314.refs_3_.refs_5_.refs_7_ = bf16[2560,2048]{1,0:T(8,128)(2,1)} custom-call(s32[16]{0:T(128)} %get-tuple-element.357.refs_0_, bf16[16,160,2048]{2,1,0:T(8,128)(2,1)} %bitcast.118), custom_call_target="tpu_custom_call" | custom-call | tf_op jit(solution)/shard_map/pallas_call | solution.py:455
  216.3 4.7 collective-permute-done.17
  223.1 2.1 collective-permute-done.18.refs_2_
  225.2 2.0 collective-permute-start.20
  231.2 13.7 %shard_map.315 = (bf16[160,2048]{1,0:T(8,128)(2,1)}, bf16[160,2048]{1,0:T(8,128)(2,1)}, bf16[2560,2048]{1,0:T(8,128)(2,1)}, bf16[2560,512]{1,0:T(8,128)(2,1)}, b...) custom-call(f32[2560,1]{1,0:T(8,128)} %copy.91.refs_0_, ...), custom_call_target="tpu_custom_call" | custom-call | flops 6710886400 | bytes 19791872 | tf_op jit(solution)/shard_map/pallas_call | solution.py:857
  245.8 2.4 collective-permute-start.23
  249.3 13.7 %shard_map.316 = (bf16[320,2048]{1,0:T(8,128)(2,1)}, bf16[2560,2048]{1,0:T(8,128)(2,1)}, bf16[2560,512]{1,0:T(8,128)(2,1)}, bf16[2560,512]{1,0:T(8,128)(2,1)}, b...) custom-call(f32[2560,1]{1,0:T(8,128)} %copy.91.refs_0_, ...), custom_call_target="tpu_custom_call", output_to_operand_aliasing={{1}: (10, {}), {2}: (11, {}), {3}: (12, {}), {4}: (13, {}),... | custom-call | flops 6710886400 | bytes 19791872 | tf_op jit(solution)/shard_map/pallas_call | solution.py:857
  267.6 21.5 %shard_map.317 = (bf16[320,2048]{1,0:T(8,128)(2,1)}, bf16[320,2048]{1,0:T(8,128)(2,1)}, bf16[2560,2048]{1,0:T(8,128)(2,1)}, bf16[2560,512]{1,0:T(8,128)(2,1)}, b...) custom-call(f32[2560,1]{1,0:T(8,128)} %copy.91.refs_0_, ...), custom_call_target="tpu_custom_call", output_to_operand_aliasing={{2}: (12, {}), {3}: (13, {}), {4}: (14, {}), {5}: (15, {}),... | custom-call | flops 13421772800 | bytes 27000832 | tf_op jit(solution)/shard_map/pallas_call | solution.py:857
  294.0 21.7 %shard_map.318 = (bf16[320,2048]{1,0:T(8,128)(2,1)}, bf16[320,2048]{1,0:T(8,128)(2,1)}, bf16[2560,2048]{1,0:T(8,128)(2,1)}, bf16[2560,512]{1,0:T(8,128)(2,1)}, b...) custom-call(f32[2560,1]{1,0:T(8,128)} %copy.91.refs_0_, ...), custom_call_target="tpu_custom_call", output_to_operand_aliasing={{2}: (12, {}), {3}: (13, {}), {4}: (14, {}), {5}: (15, {}),... | custom-call | flops 13421772800 | bytes 27000832 | tf_op jit(solution)/shard_map/pallas_call | solution.py:857
  318.8 21.6 %shard_map.319 = (bf16[160,2048]{1,0:T(8,128)(2,1)}, bf16[160,2048]{1,0:T(8,128)(2,1)}, bf16[320,2048]{1,0:T(8,128)(2,1)}, bf16[2560,2048]{1,0:T(8,128)(2,1)}, b...) custom-call(f32[2560,1]{1,0:T(8,128)} %copy.91.refs_0_, ...), custom_call_target="tpu_custom_call", output_to_operand_aliasing={{3}: (14, {}), {4}: (15, {}), {5}: (16, {}), {6}: (17, {}),... | custom-call | flops 13421772800 | bytes 27000832 | tf_op jit(solution)/shard_map/pallas_call | solution.py:857
  345.2 11.4 %convolution_convert_fusion.2 = bf16[512,2048]{1,0:T(8,128)(2,1)} fusion(bf16[2560,512]{1,0:T(8,128)(2,1)S(1)} %copy-done.3, bf16[2560,2048]{1,0:T(8,128)(2,1)} %shard_map.314.refs_3_.refs_5_.refs_7_), kind=kOutput, calls=%fused_computation.6 | convolution fusion | flops 5369757696 | bytes 15204352 | tf_op jit(solution)/shard_map/dot_general | solution.py:150
  361.8 5.8 convolution_convert_fusion.1
  369.2 6.4 collective-permute-done.49
  379.1 6.8 convolution_convert_fusion
  385.9 6.0 collective-permute-done.50
  395.7 17.6 %shard_map.320 = bf16[8,2,160,2048]{3,2,1,0:T(8,128)(2,1)} custom-call(s32[8]{0:T(128)} %compare_select_fusion.6.chip_ref, s32[8]{0:T(128)} %constant.190.clone.same_ref, s32[8]{0:T(128)} %constant.191.clone.cross_ref, s32[1]{0:T(128)} %bitcast.15.core_ref, bf16[2560,512]{1,0:T(8,128)(2,1)} %get-tuple-element.341.refs_0_.refs_1_, ...), custom_call_target="tpu_custom_call" | custom-call | flops 10737418240 | bytes 19922944 | tf_op jit(solution)/shard_map/pallas_call | solution.py:909
  414.1 1.9 convert_add_fusion.5
  420.5 13.4 %collective-permute-done.54 = bf16[160,2048]{1,0:T(8,128)(2,1)S(1)} collective-permute-done((bf16[160,2048]{1,0:T(8,128)(2,1)S(1)}, bf16[160,2048]{1,0:T(8,128)(2,1)S(1)}, u32[]{:S(2)}, u32[]{:S(2)}) %collective-permute-start.54) | collective-permute-done | bytes 655392 | tf_op jit(solution)/shard_map/ppermute | solution.py:26
  436.2 6.3 shard_map.321.refs_14_
  444.1 19.8 %shard_map.322 = (f32[320,1024]{1,0:T(8,128)}, f32[320,1]{1,0:T(8,128)}, f32[1,1024]{1,0:T(1,128)}, f32[320,1024]{1,0:T(8,128)}, f32[320,1024]{1,0:T(8,128)}, /*...) custom-call(f32[320,1024]{1,0:T(8,128)} %get-tuple-element.179.flat_, ...), custom_call_target="tpu_custom_call" | custom-call | flops 20000000000 | bytes 40000000 | tf_op jit(solution)/shard_map/pallas_call | solution.py:331
  467.7 3.1 shard_map.323
  472.8 2.3 slice.183
  476.1 1.9 slice.181
  477.9 26.0 %collective-permute-done.66.refs_9_ = bf16[2,128,1024]{2,1,0:T(8,128)(2,1)S(1)} collective-permute-done((bf16[2,128,1024]{2,1,0:T(8,128)(2,1)}, bf16[2,128,1024]{2,1,0:T(8,128)(2,1)S(1)}, u32[]{:S(2)}, u32[]{:S(2)}) %collective-permute-start.66) | collective-permute-done | bytes 524320 | tf_op jit(solution)/shard_map/ppermute | solution.py:22
  507.4 7.4 %collective-permute-done.68.refs_11_ = bf16[128,1024]{1,0:T(8,128)(2,1)S(1)} collective-permute-done((bf16[128,1024]{1,0:T(8,128)(2,1)S(1)}, bf16[128,1024]{1,0:T(8,128)(2,1)S(1)}, u32[]{:S(2)}, u32[]{:S(2)}) %collective-permute-start.68) | collective-permute-done | bytes 262176 | tf_op jit(solution)/shard_map/ppermute | solution.py:22
  516.0 5.3 shard_map.324
  522.6 4.9 psum.23
  529.2 4.9 shard_map.325
  534.2 2.8 collective-permute-done.69.refs_7_
  537.9 14.2 %shard_map.326 = (bf16[8,256,2048]{2,1,0:T(8,128)(2,1)}, bf16[256,1024]{1,0:T(8,128)(2,1)}, bf16[256,1024]{1,0:T(8,128)(2,1)}) custom-call(s32[8]{0:T(128)} %compare_select_fusion.6.chip_ref, s32[1]{0:T(128)} %bitcast.15.core_ref, bf16[320,2048]{1,0:T(8,128)(2,1)} %multiply_convert_fusion.refs_0_, bf16[320,2048]{1,0:T(8,128)(2,1)} %collective-permute-done.56.refs_1_, ...), custom_call_target="tpu_custom_call" | custom-call | flops 5368709120 | bytes 16252928 | tf_op jit(solution)/shard_map/pallas_call | solution.py:627
  555.9 10.6 %collective-permute-done.71 = bf16[256,1024]{1,0:T(8,128)(2,1)S(1)} collective-permute-done((bf16[256,1024]{1,0:T(8,128)(2,1)}, bf16[256,1024]{1,0:T(8,128)(2,1)S(1)}, u32[]{:S(2)}, u32[]{:S(2)}) %collective-permute-start.71) | collective-permute-done | bytes 524320 | tf_op jit(solution)/shard_map/ppermute | solution.py:49
  570.3 9.4 %shard_map.327 = f32[320,2048]{1,0:T(8,128)} custom-call(bf16[320,1024]{1,0:T(8,128)(2,1)} %get-tuple-element.317.refs_4_.refs_0_, bf16[320,1024]{1,0:T(8,128)(2,1)} %get-tuple-element.318.refs_5_.refs_1_, bf16[320,1024]{1,0:T(8,128)(2,1)} %get-tuple-element.319.refs_10_.refs_6_.refs_2_, bf16[16,528,1024]{2,1,0:T(8,128)(2,1)} %bitcast.90, ...), custom_call_target="tpu_custom_call" | custom-call | flops 4026531840 | bytes 15204352 | tf_op jit(solution)/shard_map/pallas_call | solution.py:544
  582.9 2.2 fusion.45
  587.3 7.4 %collective-permute-done.73 = bf16[256,2048]{1,0:T(8,128)(2,1)} collective-permute-done((bf16[256,2048]{1,0:T(8,128)(2,1)}, bf16[256,2048]{1,0:T(8,128)(2,1)}, u32[]{:S(2)}, u32[]{:S(2)}) %collective-permute-start.73) | collective-permute-done | bytes 1048608 | tf_op jit(solution)/shard_map/ppermute | solution.py:49
  594.7 4.3 collective-permute-done.76
  603.0 6.5 collective-permute-done.72
  609.5 2.6 fusion.2
  614.2 8.4 %add_bitcast_fusion = f32[1,512,2048]{2,1,0:T(8,128)} fusion(bf16[512,2048]{1,0:T(8,128)(2,1)} %collective-permute-done.52, bf16[2560,512]{1,0:T(8,128)(2,1)S(1)} %copy-done.2, bf16[2560,2048]{1,0:T(8,128)(2,1)S(1)} %bitcast.94), kind=kOutput, calls=%fused_computation.1 | convolution fusion | flops 5370806272 | bytes 19398656 | tf_op jit(solution)/shard_map/dot_general | solution.py:150
  622.6 12.9 %collective-permute-done.74 = bf16[256,2048]{1,0:T(8,128)(2,1)S(1)} collective-permute-done((bf16[256,2048]{1,0:T(8,128)(2,1)S(1)}, bf16[256,2048]{1,0:T(8,128)(2,1)S(1)}, u32[]{:S(2)}, u32[]{:S(2)}) %collective-permute-start.74) | collective-permute-done | bytes 1048608 | tf_op jit(solution)/shard_map/ppermute | solution.py:49
  636.1 3.8 fusion
  642.8 5.2 all-to-all-start
  648.0 12.5 %add_bitcast_fusion.2 = f32[1,2048,512]{2,1,0:T(8,128)} fusion(bf16[2560,2048]{1,0:T(8,128)(2,1)} %get-tuple-element.333, bf16[2560,512]{1,0:T(8,128)(2,1)} %get-tuple-element.334, bf16[512,512]{1,0:T(8,128)(2,1)} %collective-permute-done.59, bf16[1024,512]{1,0:T(8,128)(2,1)} %collective-permute-done.58, bf16[512,512]{1,0:T(8,128)(2,1)} %collective-permute-done.53), kind=kOutput, calls=%fused_computation.3 | convolution fusion | flops 5376049152 | bytes 19398656 | tf_op jit(solution)/shard_map/dot_general | solution.py:150
  660.5 1.9 collective-permute-start.75
  662.4 8.8 %add_bitcast_fusion.1 = f32[1,2048,512]{2,1,0:T(8,128)} fusion(bf16[2560,2048]{1,0:T(8,128)(2,1)S(1)} %bitcast.98, bf16[2560,512]{1,0:T(8,128)(2,1)S(1)} %copy-done.5, bf16[512,512]{1,0:T(8,128)(2,1)} %collective-permute-done.83, bf16[512,512]{1,0:T(8,128)(2,1)} %collective-permute-done.82, bf16[1024,512]{1,0:T(8,128)(2,1)} %collective-permute-done.60), kind=kOutput, calls=%fused_computation.2 | convolution fusion | flops 5376049152 | bytes 19398656 | tf_op jit(solution)/shard_map/dot_general | solution.py:150
  671.8 3.0 broadcast_select_fusion.1
  674.8 3.4 shard_map.328
  678.2 3.1 pad_maximum_fusion.1
  681.3 1.9 fusion.7
  684.9 3.0 shard_map.329
  (398 shorter events, 119.2 us)
Async XLA Ops:
  7.2 101.6 %all-gather.5.cloned.1.call-start = ((), (), s32[]{:S(2)}) async-start(), calls=%async_computation.3 | async-start | bytes 18382848 | tf_op jit(solution)/shard_map/all_gather | solution.py:1028
  12.6 194.7 %all-gather.7.cloned.1.call-start = ((), (), s32[]{:S(2)}) async-start(), calls=%async_computation.4 | async-start | bytes 11141120 | tf_op jit(solution)/shard_map/all_gather | solution.py:1030
  15.0 537.0 %reduce-scatter.2.cloned.1.call-start = ((), (), s32[]{:S(2)}) async-start(), calls=%async_computation.2 | async-start | bytes 11141120 | tf_op jit(solution)/shard_map/reduce_scatter | solution.py:1159
  15.1 49.6 %collective-permute-start = (bf16[2048,512]{1,0:T(8,128)(2,1)S(1)}, bf16[2048,512]{1,0:T(8,128)(2,1)}, u32[]{:S(2)}, u32[]{:S(2)}) collective-permute-start(bf16[2048,512]{1,0:T(8,128)(2,1)S(1)} %bitcast.104), channel_id=1, source_target_pairs={{0,1},{1,0},{2,3},{3,2},{4,5},{5,4},{6,7},{7,6},{8,9},{9,8},{10,11... | collective-permute-start | bytes 6291464 | tf_op jit(solution)/shard_map/ppermute | solution.py:26
  18.1 90.7 %collective-permute-start.1 = (bf16[2048,512]{1,0:T(8,128)(2,1)}, bf16[2048,512]{1,0:T(8,128)(2,1)}, u32[]{:S(2)}, u32[]{:S(2)}) collective-permute-start(bf16[2048,512]{1,0:T(8,128)(2,1)} %bitcast.105), channel_id=1, source_target_pairs={{0,1},{1,0},{2,3},{3,2},{4,5},{5,4},{6,7},{7,6},{8,9},{9,8},{10,11... | collective-permute-start | bytes 6291464 | tf_op jit(solution)/shard_map/ppermute | solution.py:26
  129.2 71.9 %collective-permute-start.16 = (bf16[512,2048]{1,0:T(8,128)(2,1)S(1)}, bf16[512,2048]{1,0:T(8,128)(2,1)}, u32[]{:S(2)}, u32[]{:S(2)}) collective-permute-start(bf16[512,2048]{1,0:T(8,128)(2,1)S(1)} %bitcast.117), channel_id=1, source_target_pairs={{0,1},{1,0},{2,3},{3,2},{4,5},{5,4},{6,7},{7,6},{8,9},{9,8},{10,11... | collective-permute-start | bytes 6291464 | tf_op jit(solution)/shard_map/ppermute | solution.py:26
  158.1 24.4 %collective-permute-start.14 = (bf16[128,1024]{1,0:T(8,128)(2,1)}, bf16[128,1024]{1,0:T(8,128)(2,1)}, u32[]{:S(2)}, u32[]{:S(2)}) collective-permute-start(bf16[128,1024]{1,0:T(8,128)(2,1)} %collective-permute-done.10.refs_8_), channel_id=1, source_target_pairs={{0,8},{2,10},{4,12},{6,14},{8,0},{10,2},{12,4},{14,6},{16,24},{18,... | collective-permute-start | bytes 786440 | tf_op jit(solution)/shard_map/ppermute | solution.py:22
  163.7 21.0 %collective-permute-start.11 = (bf16[128,1024]{1,0:T(8,128)(2,1)}, bf16[128,1024]{1,0:T(8,128)(2,1)}, u32[]{:S(2)}, u32[]{:S(2)}) collective-permute-start(bf16[128,1024]{1,0:T(8,128)(2,1)} %collective-permute-done.10.refs_8_), channel_id=1, source_target_pairs={{0,2},{2,0},{4,6},{6,4},{8,10},{10,8},{12,14},{14,12},{16,18},{18,... | collective-permute-start | bytes 786440 | tf_op jit(solution)/shard_map/ppermute | solution.py:22
  163.7 21.0 %collective-permute-start.13 = (bf16[128,1024]{1,0:T(8,128)(2,1)}, bf16[128,1024]{1,0:T(8,128)(2,1)}, u32[]{:S(2)}, u32[]{:S(2)}) collective-permute-start(bf16[128,1024]{1,0:T(8,128)(2,1)} %collective-permute-done.12.refs_10_), channel_id=1, source_target_pairs={{0,2},{2,0},{4,6},{6,4},{8,10},{10,8},{12,14},{14,12},{16,18},{18,... | collective-permute-start | bytes 786440 | tf_op jit(solution)/shard_map/ppermute | solution.py:22
  164.2 20.5 %collective-permute-start.8 = (bf16[128,1024]{1,0:T(8,128)(2,1)}, bf16[128,1024]{1,0:T(8,128)(2,1)}, u32[]{:S(2)}, u32[]{:S(2)}) collective-permute-start(bf16[128,1024]{1,0:T(8,128)(2,1)} %collective-permute-done.7.refs_5_), channel_id=1, source_target_pairs={{0,2},{2,0},{4,6},{6,4},{8,10},{10,8},{12,14},{14,12},{16,18},{18,... | collective-permute-start | bytes 786440 | tf_op jit(solution)/shard_map/ppermute | solution.py:22
  203.4 17.6 %collective-permute-start.17 = (bf16[160,2048]{1,0:T(8,128)(2,1)}, bf16[160,2048]{1,0:T(8,128)(2,1)}, u32[]{:S(2)}, u32[]{:S(2)}) collective-permute-start(bf16[160,2048]{1,0:T(8,128)(2,1)} %dynamic-slice_convert_fusion.1), channel_id=1, source_target_pairs={{0,1},{1,0},{2,3},{3,2},{4,5},{5,4},{6,7},{7,6},{8,9},{9,8},{10,11... | collective-permute-start | bytes 1966088 | tf_op jit(solution)/shard_map/ppermute | solution.py:26
  225.2 19.8 %collective-permute-start.19 = (bf16[160,2048]{1,0:T(8,128)(2,1)S(1)}, bf16[160,2048]{1,0:T(8,128)(2,1)}, u32[]{:S(2)}, u32[]{:S(2)}) collective-permute-start(bf16[160,2048]{1,0:T(8,128)(2,1)S(1)} %multiply_convert_fusion.1.refs_1_), channel_id=1, source_target_pairs={{0,8},{2,10},{8,16},{10,18},{16,24},{18,26},{24,28},{26,30},{28,20... | collective-permute-start | bytes 1966088 | tf_op jit(solution)/shard_map/ppermute | solution.py:45
  225.2 19.8 %collective-permute-start.20 = (bf16[160,2048]{1,0:T(8,128)(2,1)S(1)}, bf16[160,2048]{1,0:T(8,128)(2,1)S(1)}, u32[]{:S(2)}, u32[]{:S(2)}) collective-permute-start(bf16[160,2048]{1,0:T(8,128)(2,1)S(1)} %multiply_convert_fusion.1.refs_1_), channel_id=1, source_target_pairs={{8,0},{10,2},{16,8},{18,10},{24,16},{26,18},{28,24},{30,26},{20,28... | collective-permute-start | bytes 1966088 | tf_op jit(solution)/shard_map/ppermute | solution.py:49
  229.8 18.9 %collective-permute-start.24 = (f32[40,2048]{1,0:T(8,128)}, f32[40,2048]{1,0:T(8,128)S(1)}, u32[]{:S(2)}, u32[]{:S(2)}) collective-permute-start(f32[40,2048]{1,0:T(8,128)} %get-tuple-element.208), channel_id=1, source_target_pairs={{0,1},{1,0},{2,3},{3,2},{4,5},{5,4},{6,7},{7,6},{8,9},{9,8},{10,11... | collective-permute-start | bytes 983048 | tf_op jit(solution)/shard_map/ppermute | solution.py:26
  245.8 17.2 %collective-permute-start.22 = (bf16[160,2048]{1,0:T(8,128)(2,1)}, bf16[160,2048]{1,0:T(8,128)(2,1)S(1)}, u32[]{:S(2)}, u32[]{:S(2)}) collective-permute-start(bf16[160,2048]{1,0:T(8,128)(2,1)} %collective-permute-done.19.refs_1_), channel_id=1, source_target_pairs={{0,8},{2,10},{8,16},{10,18},{16,24},{18,26},{24,28},{26,30},{28,20... | collective-permute-start | bytes 1966088 | tf_op jit(solution)/shard_map/ppermute | solution.py:45
  245.8 17.2 %collective-permute-start.23 = (bf16[160,2048]{1,0:T(8,128)(2,1)}, bf16[160,2048]{1,0:T(8,128)(2,1)S(1)}, u32[]{:S(2)}, u32[]{:S(2)}) collective-permute-start(bf16[160,2048]{1,0:T(8,128)(2,1)} %copy-done.32), channel_id=1, source_target_pairs={{8,0},{10,2},{16,8},{18,10},{24,16},{26,18},{28,24},{30,26},{20,28... | collective-permute-start | bytes 1966088 | tf_op jit(solution)/shard_map/ppermute | solution.py:49
  248.2 17.7 %collective-permute-start.26 = (bf16[160,2048]{1,0:T(8,128)(2,1)}, bf16[160,2048]{1,0:T(8,128)(2,1)}, u32[]{:S(2)}, u32[]{:S(2)}) collective-permute-start(bf16[160,2048]{1,0:T(8,128)(2,1)} %collective-permute-done.19.refs_1_), channel_id=1, source_target_pairs={{0,2},{2,0},{4,6},{6,4},{8,10},{10,8},{12,14},{14,12},{16,18},{18,... | collective-permute-start | bytes 1966088 | tf_op jit(solution)/shard_map/ppermute | solution.py:22
  248.2 17.9 %collective-permute-start.27 = (bf16[160,2048]{1,0:T(8,128)(2,1)}, bf16[160,2048]{1,0:T(8,128)(2,1)}, u32[]{:S(2)}, u32[]{:S(2)}) collective-permute-start(bf16[160,2048]{1,0:T(8,128)(2,1)} %copy-done.32), channel_id=1, source_target_pairs={{0,2},{2,0},{4,6},{6,4},{8,10},{10,8},{12,14},{14,12},{16,18},{18,... | collective-permute-start | bytes 1966088 | tf_op jit(solution)/shard_map/ppermute | solution.py:22
  248.7 15.1 %collective-permute-start.25 = (f32[40,2048]{1,0:T(8,128)}, f32[40,2048]{1,0:T(8,128)S(1)}, u32[]{:S(2)}, u32[]{:S(2)}) collective-permute-start(f32[40,2048]{1,0:T(8,128)} %get-tuple-element.220), channel_id=1, source_target_pairs={{0,1},{1,0},{2,3},{3,2},{4,5},{5,4},{6,7},{7,6},{8,9},{9,8},{10,11... | collective-permute-start | bytes 983048 | tf_op jit(solution)/shard_map/ppermute | solution.py:26
  263.1 26.0 %collective-permute-start.29 = (bf16[160,2048]{1,0:T(8,128)(2,1)S(1)}, bf16[160,2048]{1,0:T(8,128)(2,1)S(1)}, u32[]{:S(2)}, u32[]{:S(2)}) collective-permute-start(bf16[160,2048]{1,0:T(8,128)(2,1)S(1)} %collective-permute-done.22.refs_1_), channel_id=1, source_target_pairs={{0,8},{2,10},{8,16},{10,18},{16,24},{18,26},{24,28},{26,30},{28,20... | collective-permute-start | bytes 1966088 | tf_op jit(solution)/shard_map/ppermute | solution.py:45
  263.8 28.0 %collective-permute-start.32 = (bf16[160,2048]{1,0:T(8,128)(2,1)S(1)}, bf16[160,2048]{1,0:T(8,128)(2,1)}, u32[]{:S(2)}, u32[]{:S(2)}) collective-permute-start(bf16[160,2048]{1,0:T(8,128)(2,1)S(1)} %collective-permute-done.22.refs_1_), channel_id=1, source_target_pairs={{0,2},{2,0},{4,6},{6,4},{8,10},{10,8},{12,14},{14,12},{16,18},{18,... | collective-permute-start | bytes 1966088 | tf_op jit(solution)/shard_map/ppermute | solution.py:22
  264.5 24.6 %collective-permute-start.30 = (bf16[160,2048]{1,0:T(8,128)(2,1)S(1)}, bf16[160,2048]{1,0:T(8,128)(2,1)S(1)}, u32[]{:S(2)}, u32[]{:S(2)}) collective-permute-start(bf16[160,2048]{1,0:T(8,128)(2,1)S(1)} %collective-permute-done.23.refs_2_), channel_id=1, source_target_pairs={{8,0},{10,2},{16,8},{18,10},{24,16},{26,18},{28,24},{30,26},{20,28... | collective-permute-start | bytes 1966088 | tf_op jit(solution)/shard_map/ppermute | solution.py:49
  265.9 26.6 %collective-permute-start.33 = (bf16[160,2048]{1,0:T(8,128)(2,1)S(1)}, bf16[160,2048]{1,0:T(8,128)(2,1)}, u32[]{:S(2)}, u32[]{:S(2)}) collective-permute-start(bf16[160,2048]{1,0:T(8,128)(2,1)S(1)} %collective-permute-done.23.refs_2_), channel_id=1, source_target_pairs={{0,2},{2,0},{4,6},{6,4},{8,10},{10,8},{12,14},{14,12},{16,18},{18,... | collective-permute-start | bytes 1966088 | tf_op jit(solution)/shard_map/ppermute | solution.py:22
  266.1 25.1 %collective-permute-start.31 = (f32[40,2048]{1,0:T(8,128)}, f32[40,2048]{1,0:T(8,128)}, u32[]{:S(2)}, u32[]{:S(2)}) collective-permute-start(f32[40,2048]{1,0:T(8,128)} %get-tuple-element.234), channel_id=1, source_target_pairs={{0,1},{1,0},{2,3},{3,2},{4,5},{5,4},{6,7},{7,6},{8,9},{9,8},{10,11... | collective-permute-start | bytes 983048 | tf_op jit(solution)/shard_map/ppermute | solution.py:26
  289.9 28.1 %collective-permute-start.40 = (bf16[160,2048]{1,0:T(8,128)(2,1)S(1)}, bf16[160,2048]{1,0:T(8,128)(2,1)}, u32[]{:S(2)}, u32[]{:S(2)}) collective-permute-start(bf16[160,2048]{1,0:T(8,128)(2,1)S(1)} %collective-permute-done.29.refs_1_), channel_id=1, source_target_pairs={{0,2},{2,0},{4,6},{6,4},{8,10},{10,8},{12,14},{14,12},{16,18},{18,... | collective-permute-start | bytes 1966088 | tf_op jit(solution)/shard_map/ppermute | solution.py:22
  290.7 27.4 %collective-permute-start.41 = (bf16[160,2048]{1,0:T(8,128)(2,1)S(1)}, bf16[160,2048]{1,0:T(8,128)(2,1)}, u32[]{:S(2)}, u32[]{:S(2)}) collective-permute-start(bf16[160,2048]{1,0:T(8,128)(2,1)S(1)} %collective-permute-done.30.refs_2_), channel_id=1, source_target_pairs={{0,2},{2,0},{4,6},{6,4},{8,10},{10,8},{12,14},{14,12},{16,18},{18,... | collective-permute-start | bytes 1966088 | tf_op jit(solution)/shard_map/ppermute | solution.py:22
  291.2 24.5 %collective-permute-start.37 = (f32[40,2048]{1,0:T(8,128)}, f32[40,2048]{1,0:T(8,128)}, u32[]{:S(2)}, u32[]{:S(2)}) collective-permute-start(f32[40,2048]{1,0:T(8,128)} %get-tuple-element.245), channel_id=1, source_target_pairs={{0,1},{1,0},{2,3},{3,2},{4,5},{5,4},{6,7},{7,6},{8,9},{9,8},{10,11... | collective-permute-start | bytes 983048 | tf_op jit(solution)/shard_map/ppermute | solution.py:26
  291.8 23.9 %collective-permute-start.35 = (bf16[80,2048]{1,0:T(8,128)(2,1)}, bf16[80,2048]{1,0:T(8,128)(2,1)}, u32[]{:S(2)}, u32[]{:S(2)}) collective-permute-start(bf16[80,2048]{1,0:T(8,128)(2,1)} %slice.169), channel_id=1, source_target_pairs={{0,8},{2,10},{8,16},{10,18},{16,24},{18,26},{24,28},{26,30},{28,20... | collective-permute-start | bytes 983048 | tf_op jit(solution)/shard_map/ppermute | solution.py:45
  292.4 23.2 %collective-permute-start.36 = (bf16[80,2048]{1,0:T(8,128)(2,1)}, bf16[80,2048]{1,0:T(8,128)(2,1)}, u32[]{:S(2)}, u32[]{:S(2)}) collective-permute-start(bf16[80,2048]{1,0:T(8,128)(2,1)} %slice.170), channel_id=1, source_target_pairs={{8,0},{10,2},{16,8},{18,10},{24,16},{26,18},{28,24},{30,26},{20,28... | collective-permute-start | bytes 983048 | tf_op jit(solution)/shard_map/ppermute | solution.py:49
  316.3 25.8 %collective-permute-start.28 = (bf16[320,2048]{1,0:T(8,128)(2,1)}, bf16[320,2048]{1,0:T(8,128)(2,1)S(1)}, u32[]{:S(2)}, u32[]{:S(2)}) collective-permute-start(bf16[320,2048]{1,0:T(8,128)(2,1)} %get-tuple-element.230), channel_id=1, source_target_pairs={{0,2},{2,0},{4,6},{6,4},{8,10},{10,8},{12,14},{14,12},{16,18},{18,... | collective-permute-start | bytes 3932168 | tf_op jit(solution)/shard_map/ppermute | solution.py:22
  341.2 72.1 %collective-permute-start.21 = (bf16[160,2048]{1,0:T(8,128)(2,1)}, bf16[160,2048]{1,0:T(8,128)(2,1)}, u32[]{:S(2)}, u32[]{:S(2)}) collective-permute-start(bf16[160,2048]{1,0:T(8,128)(2,1)} %get-tuple-element.205), channel_id=1, source_target_pairs={{0,2},{2,0},{4,6},{6,4},{8,10},{10,8},{12,14},{14,12},{16,18},{18,... | collective-permute-start | bytes 1966088 | tf_op jit(solution)/shard_map/ppermute | solution.py:22
  341.6 15.1 %collective-permute-start.34 = (bf16[320,2048]{1,0:T(8,128)(2,1)}, bf16[320,2048]{1,0:T(8,128)(2,1)S(1)}, u32[]{:S(2)}, u32[]{:S(2)}) collective-permute-start(bf16[320,2048]{1,0:T(8,128)(2,1)} %get-tuple-element.244), channel_id=1, source_target_pairs={{0,2},{2,0},{4,6},{6,4},{8,10},{10,8},{12,14},{14,12},{16,18},{18,... | collective-permute-start | bytes 3932168 | tf_op jit(solution)/shard_map/ppermute | solution.py:22
  341.7 17.0 %collective-permute-start.42 = (bf16[320,2048]{1,0:T(8,128)(2,1)}, bf16[320,2048]{1,0:T(8,128)(2,1)S(1)}, u32[]{:S(2)}, u32[]{:S(2)}) collective-permute-start(bf16[320,2048]{1,0:T(8,128)(2,1)} %get-tuple-element.257), channel_id=1, source_target_pairs={{0,2},{2,0},{4,6},{6,4},{8,10},{10,8},{12,14},{14,12},{16,18},{18,... | collective-permute-start | bytes 3932168 | tf_op jit(solution)/shard_map/ppermute | solution.py:22
  343.1 16.2 %collective-permute-start.44 = (bf16[80,2048]{1,0:T(8,128)(2,1)S(1)}, bf16[80,2048]{1,0:T(8,128)(2,1)S(1)}, u32[]{:S(2)}, u32[]{:S(2)}) collective-permute-start(bf16[80,2048]{1,0:T(8,128)(2,1)S(1)} %get-tuple-element.384), channel_id=1, source_target_pairs={{0,8},{2,10},{8,16},{10,18},{16,24},{18,26},{24,28},{26,30},{28,20... | collective-permute-start | bytes 983048 | tf_op jit(solution)/shard_map/ppermute | solution.py:45
  343.8 14.9 %collective-permute-start.48 = (bf16[80,2048]{1,0:T(8,128)(2,1)S(1)}, bf16[80,2048]{1,0:T(8,128)(2,1)S(1)}, u32[]{:S(2)}, u32[]{:S(2)}) collective-permute-start(bf16[80,2048]{1,0:T(8,128)(2,1)S(1)} %get-tuple-element.385), channel_id=1, source_target_pairs={{8,0},{10,2},{16,8},{18,10},{24,16},{26,18},{28,24},{30,26},{20,28... | collective-permute-start | bytes 983048 | tf_op jit(solution)/shard_map/ppermute | solution.py:49
  356.6 59.4 %collective-permute-start.52 = (bf16[512,2048]{1,0:T(8,128)(2,1)}, bf16[512,2048]{1,0:T(8,128)(2,1)}, u32[]{:S(2)}, u32[]{:S(2)}) collective-permute-start(bf16[512,2048]{1,0:T(8,128)(2,1)} %convolution_convert_fusion.2), channel_id=1, source_target_pairs={{0,1},{1,0},{2,3},{3,2},{4,5},{5,4},{6,7},{7,6},{8,9},{9,8},{10,11... | collective-permute-start | bytes 6291464 | tf_op jit(solution)/shard_map/ppermute | solution.py:26
  359.6 16.0 %collective-permute-start.49 = (bf16[160,2048]{1,0:T(8,128)(2,1)S(1)}, bf16[160,2048]{1,0:T(8,128)(2,1)S(1)}, u32[]{:S(2)}, u32[]{:S(2)}) collective-permute-start(bf16[160,2048]{1,0:T(8,128)(2,1)S(1)} %pad_maximum_fusion.6), channel_id=1, source_target_pairs={{8,0},{10,2},{16,8},{18,10},{24,16},{26,18},{28,24},{30,26},{20,28... | collective-permute-start | bytes 1966088 | tf_op jit(solution)/shard_map/ppermute | solution.py:49
  360.8 15.7 %collective-permute-start.45 = (bf16[160,2048]{1,0:T(8,128)(2,1)S(1)}, bf16[160,2048]{1,0:T(8,128)(2,1)S(1)}, u32[]{:S(2)}, u32[]{:S(2)}) collective-permute-start(bf16[160,2048]{1,0:T(8,128)(2,1)S(1)} %pad_maximum_fusion.5), channel_id=1, source_target_pairs={{0,8},{2,10},{8,16},{10,18},{16,24},{18,26},{24,28},{26,30},{28,20... | collective-permute-start | bytes 1966088 | tf_op jit(solution)/shard_map/ppermute | solution.py:45
  368.5 47.5 %collective-permute-start.53 = (bf16[512,512]{1,0:T(8,128)(2,1)}, bf16[512,512]{1,0:T(8,128)(2,1)}, u32[]{:S(2)}, u32[]{:S(2)}) collective-permute-start(bf16[512,512]{1,0:T(8,128)(2,1)} %slice.222), channel_id=1, source_target_pairs={{0,1},{1,0},{2,3},{3,2},{4,5},{5,4},{6,7},{7,6},{8,9},{9,8},{10,11... | collective-permute-start | bytes 1572872 | tf_op jit(solution)/shard_map/ppermute | solution.py:26
  377.0 14.9 %collective-permute-start.50 = (bf16[160,2048]{1,0:T(8,128)(2,1)S(1)}, bf16[160,2048]{1,0:T(8,128)(2,1)S(1)}, u32[]{:S(2)}, u32[]{:S(2)}) collective-permute-start(bf16[160,2048]{1,0:T(8,128)(2,1)S(1)} %get-tuple-element.375), channel_id=1, source_target_pairs={{8,0},{10,2},{16,8},{18,10},{24,16},{26,18},{28,24},{30,26},{20,28... | collective-permute-start | bytes 1966088 | tf_op jit(solution)/shard_map/ppermute | solution.py:49
  377.6 14.7 %collective-permute-start.46 = (bf16[160,2048]{1,0:T(8,128)(2,1)S(1)}, bf16[160,2048]{1,0:T(8,128)(2,1)S(1)}, u32[]{:S(2)}, u32[]{:S(2)}) collective-permute-start(bf16[160,2048]{1,0:T(8,128)(2,1)S(1)} %get-tuple-element.374), channel_id=1, source_target_pairs={{0,8},{2,10},{8,16},{10,18},{16,24},{18,26},{24,28},{26,30},{28,20... | collective-permute-start | bytes 1966088 | tf_op jit(solution)/shard_map/ppermute | solution.py:45
  393.6 19.6 %collective-permute-start.47 = (bf16[160,2048]{1,0:T(8,128)(2,1)}, bf16[160,2048]{1,0:T(8,128)(2,1)S(1)}, u32[]{:S(2)}, u32[]{:S(2)}) collective-permute-start(bf16[160,2048]{1,0:T(8,128)(2,1)} %get-tuple-element.372), channel_id=1, source_target_pairs={{0,8},{2,10},{8,16},{10,18},{16,24},{18,26},{24,28},{26,30},{28,20... | collective-permute-start | bytes 1966088 | tf_op jit(solution)/shard_map/ppermute | solution.py:45
  395.0 19.0 %collective-permute-start.51 = (bf16[160,2048]{1,0:T(8,128)(2,1)S(1)}, bf16[160,2048]{1,0:T(8,128)(2,1)}, u32[]{:S(2)}, u32[]{:S(2)}) collective-permute-start(bf16[160,2048]{1,0:T(8,128)(2,1)S(1)} %get-tuple-element.373), channel_id=1, source_target_pairs={{8,0},{10,2},{16,8},{18,10},{24,16},{26,18},{28,24},{30,26},{20,28... | collective-permute-start | bytes 1966088 | tf_op jit(solution)/shard_map/ppermute | solution.py:49
  419.3 14.7 %collective-permute-start.54 = (bf16[160,2048]{1,0:T(8,128)(2,1)S(1)}, bf16[160,2048]{1,0:T(8,128)(2,1)S(1)}, u32[]{:S(2)}, u32[]{:S(2)}) collective-permute-start(bf16[160,2048]{1,0:T(8,128)(2,1)S(1)} %get-tuple-element.352), channel_id=1, source_target_pairs={{0,1},{1,0},{2,3},{3,2},{4,5},{5,4},{6,7},{7,6},{8,9},{9,8},{10,11... | collective-permute-start | bytes 1966088 | tf_op jit(solution)/shard_map/ppermute | solution.py:26
  442.5 29.2 %collective-permute-start.58 = (bf16[1024,512]{1,0:T(8,128)(2,1)}, bf16[1024,512]{1,0:T(8,128)(2,1)}, u32[]{:S(2)}, u32[]{:S(2)}) collective-permute-start(bf16[1024,512]{1,0:T(8,128)(2,1)} %slice.182), channel_id=1, source_target_pairs={{0,1},{1,0},{2,3},{3,2},{4,5},{5,4},{6,7},{7,6},{8,9},{9,8},{10,11... | collective-permute-start | bytes 3145736 | tf_op jit(solution)/shard_map/ppermute | solution.py:26
  464.5 41.3 %collective-permute-start.56 = (bf16[320,2048]{1,0:T(8,128)(2,1)}, bf16[320,2048]{1,0:T(8,128)(2,1)}, u32[]{:S(2)}, u32[]{:S(2)}) collective-permute-start(bf16[320,2048]{1,0:T(8,128)(2,1)} %multiply_convert_fusion.refs_0_), channel_id=1, source_target_pairs={{0,2},{2,0},{4,6},{6,4},{8,10},{10,8},{12,14},{14,12},{16,18},{18,... | collective-permute-start | bytes 3932168 | tf_op jit(solution)/shard_map/ppermute | solution.py:22
  466.2 41.2 %collective-permute-start.57 = (bf16[320,2048]{1,0:T(8,128)(2,1)S(1)}, bf16[320,2048]{1,0:T(8,128)(2,1)}, u32[]{:S(2)}, u32[]{:S(2)}) collective-permute-start(bf16[320,2048]{1,0:T(8,128)(2,1)S(1)} %copy-done.12), channel_id=1, source_target_pairs={{0,2},{2,0},{4,6},{6,4},{8,10},{10,8},{12,14},{14,12},{16,18},{18,... | collective-permute-start | bytes 3932168 | tf_op jit(solution)/shard_map/ppermute | solution.py:22
  470.8 33.1 %collective-permute-start.66 = (bf16[2,128,1024]{2,1,0:T(8,128)(2,1)}, bf16[2,128,1024]{2,1,0:T(8,128)(2,1)S(1)}, u32[]{:S(2)}, u32[]{:S(2)}) collective-permute-start(bf16[2,128,1024]{2,1,0:T(8,128)(2,1)} %get-tuple-element.291), channel_id=1, source_target_pairs={{0,8},{2,10},{4,12},{6,14},{8,0},{10,2},{12,4},{14,6},{16,24},{18,... | collective-permute-start | bytes 1572872 | tf_op jit(solution)/shard_map/ppermute | solution.py:22
  471.7 32.3 %collective-permute-start.65 = (bf16[2,128,1024]{2,1,0:T(8,128)(2,1)}, bf16[2,128,1024]{2,1,0:T(8,128)(2,1)S(1)}, u32[]{:S(2)}, u32[]{:S(2)}) collective-permute-start(bf16[2,128,1024]{2,1,0:T(8,128)(2,1)} %get-tuple-element.290), channel_id=1, source_target_pairs={{0,4},{2,6},{4,0},{6,2},{8,12},{10,14},{12,8},{14,10},{16,20},{18,... | collective-permute-start | bytes 1572872 | tf_op jit(solution)/shard_map/ppermute | solution.py:22
  475.1 47.3 %collective-permute-start.60 = (bf16[1024,512]{1,0:T(8,128)(2,1)}, bf16[1024,512]{1,0:T(8,128)(2,1)}, u32[]{:S(2)}, u32[]{:S(2)}) collective-permute-start(bf16[1024,512]{1,0:T(8,128)(2,1)} %slice.183), channel_id=1, source_target_pairs={{0,1},{1,0},{2,3},{3,2},{4,5},{5,4},{6,7},{7,6},{8,9},{9,8},{10,11... | collective-permute-start | bytes 3145736 | tf_op jit(solution)/shard_map/ppermute | solution.py:26
  504.0 18.4 %collective-permute-start.59 = (bf16[512,512]{1,0:T(8,128)(2,1)}, bf16[512,512]{1,0:T(8,128)(2,1)}, u32[]{:S(2)}, u32[]{:S(2)}) collective-permute-start(bf16[512,512]{1,0:T(8,128)(2,1)} %slice.181), channel_id=1, source_target_pairs={{0,1},{1,0},{2,3},{3,2},{4,5},{5,4},{6,7},{7,6},{8,9},{9,8},{10,11... | collective-permute-start | bytes 1572872 | tf_op jit(solution)/shard_map/ppermute | solution.py:26
  552.6 15.1 %collective-permute-start.70 = (bf16[256,1024]{1,0:T(8,128)(2,1)}, bf16[256,1024]{1,0:T(8,128)(2,1)S(1)}, u32[]{:S(2)}, u32[]{:S(2)}) collective-permute-start(bf16[256,1024]{1,0:T(8,128)(2,1)} %get-tuple-element.311), channel_id=1, source_target_pairs={{0,8},{2,10},{8,16},{10,18},{16,24},{18,26},{24,28},{26,30},{28,20... | collective-permute-start | bytes 1572872 | tf_op jit(solution)/shard_map/ppermute | solution.py:45
  569.0 25.7 %collective-permute-start.73 = (bf16[256,2048]{1,0:T(8,128)(2,1)}, bf16[256,2048]{1,0:T(8,128)(2,1)}, u32[]{:S(2)}, u32[]{:S(2)}) collective-permute-start(bf16[256,2048]{1,0:T(8,128)(2,1)} %pad_maximum_fusion.4), channel_id=1, source_target_pairs={{8,0},{10,2},{16,8},{18,10},{24,16},{26,18},{28,24},{30,26},{20,28... | collective-permute-start | bytes 3145736 | tf_op jit(solution)/shard_map/ppermute | solution.py:49
  581.3 17.7 %collective-permute-start.76 = (bf16[160,2048]{1,0:T(8,128)(2,1)S(1)}, bf16[160,2048]{1,0:T(8,128)(2,1)S(1)}, u32[]{:S(2)}, u32[]{:S(2)}) collective-permute-start(bf16[160,2048]{1,0:T(8,128)(2,1)S(1)} %dynamic-slice_convert_fusion), channel_id=1, source_target_pairs={{0,1},{1,0},{2,3},{3,2},{4,5},{5,4},{6,7},{7,6},{8,9},{9,8},{10,11... | collective-permute-start | bytes 1966088 | tf_op jit(solution)/shard_map/ppermute | solution.py:26
  585.2 75.3 %collective-permute-start.82 = (bf16[512,512]{1,0:T(8,128)(2,1)}, bf16[512,512]{1,0:T(8,128)(2,1)}, u32[]{:S(2)}, u32[]{:S(2)}) collective-permute-start(bf16[512,512]{1,0:T(8,128)(2,1)} %get-tuple-element.339), channel_id=1, source_target_pairs={{0,1},{1,0},{2,3},{3,2},{4,5},{5,4},{6,7},{7,6},{8,9},{9,8},{10,11... | collective-permute-start | bytes 1572872 | tf_op jit(solution)/shard_map/ppermute | solution.py:26
  585.7 23.7 %collective-permute-start.72 = (bf16[256,2048]{1,0:T(8,128)(2,1)}, bf16[256,2048]{1,0:T(8,128)(2,1)S(1)}, u32[]{:S(2)}, u32[]{:S(2)}) collective-permute-start(bf16[256,2048]{1,0:T(8,128)(2,1)} %pad_maximum_fusion.3), channel_id=1, source_target_pairs={{0,8},{2,10},{8,16},{10,18},{16,24},{18,26},{24,28},{26,30},{28,20... | collective-permute-start | bytes 3145736 | tf_op jit(solution)/shard_map/ppermute | solution.py:45
  600.9 70.9 %collective-permute-start.77 = (f32[160,2048]{1,0:T(8,128)}, f32[160,2048]{1,0:T(8,128)}, u32[]{:S(2)}, u32[]{:S(2)}) collective-permute-start(f32[160,2048]{1,0:T(8,128)} %fusion.5), channel_id=1, source_target_pairs={{0,1},{1,0},{2,3},{3,2},{4,5},{5,4},{6,7},{7,6},{8,9},{9,8},{10,11... | collective-permute-start | bytes 3932168 | tf_op jit(solution)/shard_map/ppermute | solution.py:26
  602.5 59.9 %collective-permute-start.83 = (bf16[512,512]{1,0:T(8,128)(2,1)}, bf16[512,512]{1,0:T(8,128)(2,1)}, u32[]{:S(2)}, u32[]{:S(2)}) collective-permute-start(bf16[512,512]{1,0:T(8,128)(2,1)} %get-tuple-element.340), channel_id=1, source_target_pairs={{0,1},{1,0},{2,3},{3,2},{4,5},{5,4},{6,7},{7,6},{8,9},{9,8},{10,11... | collective-permute-start | bytes 1572872 | tf_op jit(solution)/shard_map/ppermute | solution.py:26
  612.1 23.4 %collective-permute-start.74 = (bf16[256,2048]{1,0:T(8,128)(2,1)S(1)}, bf16[256,2048]{1,0:T(8,128)(2,1)S(1)}, u32[]{:S(2)}, u32[]{:S(2)}) collective-permute-start(bf16[256,2048]{1,0:T(8,128)(2,1)S(1)} %get-tuple-element.315), channel_id=1, source_target_pairs={{8,0},{10,2},{16,8},{18,10},{24,16},{26,18},{28,24},{30,26},{20,28... | collective-permute-start | bytes 3145736 | tf_op jit(solution)/shard_map/ppermute | solution.py:49
  613.7 22.4 %collective-permute-start.78 = (bf16[256,2048]{1,0:T(8,128)(2,1)S(1)}, bf16[256,2048]{1,0:T(8,128)(2,1)S(1)}, u32[]{:S(2)}, u32[]{:S(2)}) collective-permute-start(bf16[256,2048]{1,0:T(8,128)(2,1)S(1)} %get-tuple-element.324), channel_id=1, source_target_pairs={{0,8},{2,10},{8,16},{10,18},{16,24},{18,26},{24,28},{26,30},{28,20... | collective-permute-start | bytes 3145736 | tf_op jit(solution)/shard_map/ppermute | solution.py:45
  639.9 34.9 %collective-permute-start.79 = (bf16[256,2048]{1,0:T(8,128)(2,1)}, bf16[256,2048]{1,0:T(8,128)(2,1)}, u32[]{:S(2)}, u32[]{:S(2)}) collective-permute-start(bf16[256,2048]{1,0:T(8,128)(2,1)} %get-tuple-element.325), channel_id=1, source_target_pairs={{0,8},{2,10},{8,16},{10,18},{16,24},{18,26},{24,28},{26,30},{28,20... | collective-permute-start | bytes 3145736 | tf_op jit(solution)/shard_map/ppermute | solution.py:45
  641.1 33.7 %collective-permute-start.80 = (bf16[256,2048]{1,0:T(8,128)(2,1)}, bf16[256,2048]{1,0:T(8,128)(2,1)}, u32[]{:S(2)}, u32[]{:S(2)}) collective-permute-start(bf16[256,2048]{1,0:T(8,128)(2,1)} %get-tuple-element.326), channel_id=1, source_target_pairs={{8,0},{10,2},{16,8},{18,10},{24,16},{26,18},{28,24},{30,26},{20,28... | collective-permute-start | bytes 3145736 | tf_op jit(solution)/shard_map/ppermute | solution.py:49
  642.8 28.4 %all-to-all-start = ((f32[32,1,512]{2,1,0:T(1,128)}), f32[32,1,512]{2,1,0:T(1,128)S(1)}, u32[]{:S(2)}, u32[]{:S(2)}) async-start(f32[32,1,512]{2,1,0:T(1,128)} %all_to_all.6), calls=%async_computation.1 | async-start | bytes 131072 | tf_op jit(solution)/shard_map/all_to_all | solution.py:1237
  660.5 20.9 %collective-permute-start.75 = (bf16[160,2048]{1,0:T(8,128)(2,1)}, bf16[160,2048]{1,0:T(8,128)(2,1)}, u32[]{:S(2)}, u32[]{:S(2)}) collective-permute-start(bf16[160,2048]{1,0:T(8,128)(2,1)} %reduce-scatter.2.cloned.1.call-done), channel_id=1, source_target_pairs={{0,1},{1,0},{2,3},{3,2},{4,5},{5,4},{6,7},{7,6},{8,9},{9,8},{10,11... | collective-permute-start | bytes 1966088 | tf_op jit(solution)/shard_map/ppermute | solution.py:26
  (92 other events, 1036.8 us)
Sparse Core Ops, SparseCore 0:
  12.7 94.2 all-gather.4
  109.9 97.4 all-gather.6
  416.1 134.4 reduce-scatter.1

commit v12 on v11

--- a/solution.py
+++ b/solution.py
@@ -723,6 +723,29 @@
         out_specs=[pl.BlockSpec(shape, lambda i: (0, 0)) for shape in shapes],
         out_shape=[jax.ShapeDtypeStruct(shape, FULL) for shape in shapes],
     )(core, own, got)
+
+
+def join_kernel(parts, side_ref, *refs):
+    out_ref = refs[-1]
+    rows = out_ref.shape[0] // 2
+    for k, side in ((0, side_ref[0]), (1, 1 - side_ref[0])):
+        total = refs[k * parts][...].astype(FULL)
+        for j in range(1, parts):
+            total = total + refs[k * parts + j][...].astype(FULL)
+        out_ref[pl.ds(pl.multiple_of(side * rows, rows), rows)] = total
+
+
+def join_halves(side, own, other):
+    rows, width = own[0].shape
+    columns = width // 2
+    half = pl.BlockSpec((rows, columns), lambda i: (0, i))
+    return pl.pallas_call(
+        lambda *refs: join_kernel(len(own), *refs),
+        grid=(2,),
+        in_specs=[pl.BlockSpec(memory_space=pltpu.SMEM)] + [half] * (2 * len(own)),
+        out_specs=pl.BlockSpec((2 * rows, columns), lambda i: (0, i)),
+        out_shape=jax.ShapeDtypeStruct((2 * rows, width), FULL),
+    )(side, *own, *other)
 
 
 def expert_kernel(
@@ -1239,6 +1262,8 @@
 
     if ring:
         pre_got = swap_bit(pre_sent, "dp", 0)
+        normed_own, normed_other, gain_one_grad = share(back_all(*pre_grads))
+        pre_got, normed_own = together(pre_got, normed_own)
         w_blocks, *far = weight_grads(
             chips,
             core[None],
@@ -1254,20 +1279,19 @@
         up_third = swap_tensor(after(up_third, far[0]))
         late = {}
 
-        def normed_stage(gated):
-            late["normed"] = share(back_all(*[gated(grad) for grad in pre_grads]))
-
         def input_stage(gated):
-            late["input"] = input_side(late["normed"][0], gated(late["normed"][1]))
+            late["input"] = input_side(normed_own, gated(normed_other))
             late["up"] = swap_tensor(after(up_last, late["input"][0]))
             late["down"] = grad_sum(gated(h0), back_rows, down_got)
 
         def expert_stage(gated):
-            late["gains"] = gain_side(gated(late["normed"][2]))
+            late["gate"] = grad_sum(gated(expert_in), g0, gate_got)
             late["mixed"] = swap_tensor(gated(mixed))
-            late["gate"] = grad_sum(gated(expert_in), g0, gate_got)
-
-        fillers = Fillers(normed_stage, input_stage, expert_stage)
+
+        def gain_stage(gated):
+            late["gains"] = gain_side(gated(gain_one_grad))
+
+        fillers = Fillers(input_stage, expert_stage, gain_stage)
         w_parts, token = ring_weights(w_blocks, *far, fillers)
         input_half, input_other = late["input"]
         gain_sums = late["gains"]
@@ -1292,10 +1316,8 @@
         *normed_parts, gain_one_grad = share(back_all(*pre_grads))
         gain_sums = gain_side(gain_one_grad)
         input_half, input_other = input_side(*normed_parts)
-    input_grad = both_halves(input_half, input_other)
-    output = both_halves(
-        hidden_state + mixed.astype(FULL), hidden_other + mixed_other.astype(FULL)
-    )
+    input_grad = join_halves(side[None], [input_half], [input_other])
+    output = join_halves(side[None], [hidden_state, mixed], [hidden_other, mixed_other])
     return (
         output,
         input_grad,

time: 702 us -> 692 us (0.986)
  other arithmetic: 49.8 us -> 40.3 us
    ppermute x12, waiting for transfers between devices: 43.3 us -> 56.9 us  [behind(): return lax.ppermute(block, 'dp', BEHIND)]
  transfers between devices with their start and end apart: 88 -> 88, of which waited for: 29 -> 28; matrix products, arithmetic and copies ran while one was open for 18% -> 17% of each run, Pallas kernels for 31% -> 32%
where the time goes in v12:
time: 692 us; the launch traced here: 685 us
  waiting for transfers between devices  241 us (35%)
  Pallas kernels  225 us (33%)
  starting transfers between devices  65.7 us (9%)
  matrix products  53.7 us (8%)
  other arithmetic  40.3 us (6%)
  local copies, waits for them, and re-layouts  34.1 us (5%)
  between operations  15.3 us (2%)
  blocking collectives  10.4 us (2%)
    ppermute x19, waiting for transfers between devices, swap_tensor(): return lax.ppermute(block, 'tensor', [(0, 1), (1, 0)])  105 us
    pallas_call x5, Pallas kernels, expert_chunk(): pl.pallas_call(lambda *refs: chunk_kernel(len(pieces), len(held), at, spl...  92.5 us
    ppermute x41, waiting for transfers between devices, swap_bit(): return lax.ppermute(block, axis, [(i, i ^ 1 << bit) for i in range(count)])  74.8 us
    ppermute x12, waiting for transfers between devices, behind(): return lax.ppermute(block, 'dp', BEHIND)  56.9 us
    dot_general x6, matrix products, dot_tn(): lax.dot_general(left, right, (((0,), (0,)), ((), ())), preferred_element_...  53.5 us
    ppermute x19, starting transfers between devices, swap_tensor(): return lax.ppermute(block, 'tensor', [(0, 1), (1, 0)])  21.2 us
    pallas_call x1, Pallas kernels, attend_back(): pl.pallas_call(attend_back_kernel, grid=(width // HEAD // PAIR,), in_spec...  19.8 us
    pallas_call x1, Pallas kernels, mixed_pass(): pl.pallas_call(mixed_kernel, grid_spec=pltpu.PrefetchScalarGridSpec(num_s...  17.6 us
  transfers between devices with their start and end apart: 88, of which 28 were waited for; matrix products, arithmetic and copies ran while one was open for 17% of the time, Pallas kernels for 32%

profile of v12, /device:TPU:0, one launch (start us, length us, event | category | flops | bytes accessed | tf_op | source)
XLA Modules:
  0.0 685.2 jit_solution(4708062186481216666)
XLA Ops:
  10.1 2.4 shard_map.309
  12.7 2.3 dynamic-slice_convert_fusion.2
  15.1 3.0 collective-permute-start
  22.1 42.6 %collective-permute-done.refs_5_.refs_7_.refs_9_ = bf16[2048,512]{1,0:T(8,128)(2,1)} collective-permute-done((bf16[2048,512]{1,0:T(8,128)(2,1)S(1)}, bf16[2048,512]{1,0:T(8,128)(2,1)}, u32[]{:S(2)}, u32[]{:S(2)}) %collective-permute-start) | collective-permute-done | bytes 2097184 | tf_op jit(solution)/shard_map/ppermute | solution.py:26
  64.7 44.1 %collective-permute-done.1.refs_7_.refs_9_.refs_11_ = bf16[2048,512]{1,0:T(8,128)(2,1)} collective-permute-done((bf16[2048,512]{1,0:T(8,128)(2,1)}, bf16[2048,512]{1,0:T(8,128)(2,1)}, u32[]{:S(2)}, u32[]{:S(2)}) %collective-permute-start.1) | collective-permute-done | bytes 2097184 | tf_op jit(solution)/shard_map/ppermute | solution.py:26
  111.9 9.0 %shard_map.310 = (f32[320,1024]{1,0:T(8,128)}, f32[320,1024]{1,0:T(8,128)}, bf16[320,1024]{1,0:T(8,128)(2,1)}, bf16[128,1024]{1,0:T(8,128)(2,1)}) custom-call(bf16[320,2048]{1,0:T(8,128)(2,1)} %multiply_convert_fusion.refs_0_, bf16[16,528,1024]{2,1,0:T(8,128)(2,1)} %bitcast.87), custom_call_target="tpu_custom_call" | custom-call | flops 4026531840 | bytes 15204352 | tf_op jit(solution)/shard_map/pallas_call | solution.py:505
  124.1 5.5 all-reduce.3
  132.7 2.7 shard_map.311
  139.0 8.9 %collective-permute-done.5.refs_3_ = bf16[128,1024]{1,0:T(8,128)(2,1)} collective-permute-done((bf16[128,1024]{1,0:T(8,128)(2,1)}, bf16[128,1024]{1,0:T(8,128)(2,1)}, u32[]{:S(2)}, u32[]{:S(2)}) %collective-permute-start.5) | collective-permute-done | bytes 262176 | tf_op jit(solution)/shard_map/ppermute | solution.py:22
  152.0 6.5 collective-permute-done.12.refs_10_
  158.8 5.1 collective-permute-done.7.refs_5_
  164.5 18.5 %collective-permute-done.14.refs_12_ = bf16[128,1024]{1,0:T(8,128)(2,1)} collective-permute-done((bf16[128,1024]{1,0:T(8,128)(2,1)}, bf16[128,1024]{1,0:T(8,128)(2,1)}, u32[]{:S(2)}, u32[]{:S(2)}) %collective-permute-start.14) | collective-permute-done | bytes 262176 | tf_op jit(solution)/shard_map/ppermute | solution.py:22
  185.1 11.9 %shard_map.312.refs_0_.refs_8_ = bf16[320,1024]{1,0:T(8,128)(2,1)} custom-call(f32[320,1024]{1,0:T(8,128)} %get-tuple-element.179.flat_ref.refs_0_, f32[1,1024]{1,0:T(1,128)} %bitcast.129, f32[320,1]{1,0:T(8,128)} %broadcast_in_dim.145.scale_ref.refs_3_, f32[320,128]{1,0:T(8,128)} %get-tuple-element.181.cos_ref.refs_5_, ...), custom_call_target="tpu_custom_call" | custom-call | tf_op jit(solution)/shard_map/pallas_call | solution.py:272
  197.0 4.6 shard_map.313
  207.4 8.7 %shard_map.314.refs_3_.refs_5_.refs_7_ = bf16[2560,2048]{1,0:T(8,128)(2,1)} custom-call(s32[16]{0:T(128)} %get-tuple-element.357.refs_0_, bf16[16,160,2048]{2,1,0:T(8,128)(2,1)} %bitcast.121), custom_call_target="tpu_custom_call" | custom-call | tf_op jit(solution)/shard_map/pallas_call | solution.py:455
  216.1 4.1 collective-permute-done.17
  220.2 2.0 multiply_reduce_fusion.6
  222.5 2.1 collective-permute-done.18.refs_2_
  224.6 2.0 collective-permute-start.20
  230.4 13.7 %shard_map.315 = (bf16[160,2048]{1,0:T(8,128)(2,1)}, bf16[160,2048]{1,0:T(8,128)(2,1)}, bf16[2560,2048]{1,0:T(8,128)(2,1)}, bf16[2560,512]{1,0:T(8,128)(2,1)}, b...) custom-call(f32[2560,1]{1,0:T(8,128)} %copy.91.refs_0_, ...), custom_call_target="tpu_custom_call" | custom-call | flops 6710886400 | bytes 19791872 | tf_op jit(solution)/shard_map/pallas_call | solution.py:880
  245.1 2.2 collective-permute-start.23
  248.5 13.7 %shard_map.316 = (bf16[320,2048]{1,0:T(8,128)(2,1)}, bf16[2560,2048]{1,0:T(8,128)(2,1)}, bf16[2560,512]{1,0:T(8,128)(2,1)}, bf16[2560,512]{1,0:T(8,128)(2,1)}, b...) custom-call(f32[2560,1]{1,0:T(8,128)} %copy.91.refs_0_, ...), custom_call_target="tpu_custom_call", output_to_operand_aliasing={{1}: (10, {}), {2}: (11, {}), {3}: (12, {}), {4}: (13, {}),... | custom-call | flops 6710886400 | bytes 19791872 | tf_op jit(solution)/shard_map/pallas_call | solution.py:880
  266.6 21.5 %shard_map.317 = (bf16[320,2048]{1,0:T(8,128)(2,1)}, bf16[320,2048]{1,0:T(8,128)(2,1)}, bf16[2560,2048]{1,0:T(8,128)(2,1)}, bf16[2560,512]{1,0:T(8,128)(2,1)}, b...) custom-call(f32[2560,1]{1,0:T(8,128)} %copy.91.refs_0_, ...), custom_call_target="tpu_custom_call", output_to_operand_aliasing={{2}: (12, {}), {3}: (13, {}), {4}: (14, {}), {5}: (15, {}),... | custom-call | flops 13421772800 | bytes 27000832 | tf_op jit(solution)/shard_map/pallas_call | solution.py:880
  291.4 1.9 collective-permute-start.36
  293.3 21.9 %shard_map.318 = (bf16[320,2048]{1,0:T(8,128)(2,1)}, bf16[320,2048]{1,0:T(8,128)(2,1)}, bf16[2560,2048]{1,0:T(8,128)(2,1)}, bf16[2560,512]{1,0:T(8,128)(2,1)}, b...) custom-call(f32[2560,1]{1,0:T(8,128)} %copy.91.refs_0_, ...), custom_call_target="tpu_custom_call", output_to_operand_aliasing={{2}: (12, {}), {3}: (13, {}), {4}: (14, {}), {5}: (15, {}),... | custom-call | flops 13421772800 | bytes 27000832 | tf_op jit(solution)/shard_map/pallas_call | solution.py:880
  318.2 21.7 %shard_map.319 = (bf16[160,2048]{1,0:T(8,128)(2,1)}, bf16[160,2048]{1,0:T(8,128)(2,1)}, bf16[320,2048]{1,0:T(8,128)(2,1)}, bf16[2560,2048]{1,0:T(8,128)(2,1)}, b...) custom-call(f32[2560,1]{1,0:T(8,128)} %copy.91.refs_0_, ...), custom_call_target="tpu_custom_call", output_to_operand_aliasing={{3}: (14, {}), {4}: (15, {}), {5}: (16, {}), {6}: (17, {}),... | custom-call | flops 13421772800 | bytes 27000832 | tf_op jit(solution)/shard_map/pallas_call | solution.py:880
  345.6 11.2 %convolution_convert_fusion.2 = bf16[512,2048]{1,0:T(8,128)(2,1)} fusion(bf16[2560,512]{1,0:T(8,128)(2,1)S(1)} %copy-done.4, bf16[2560,2048]{1,0:T(8,128)(2,1)} %shard_map.314.refs_3_.refs_5_.refs_7_), kind=kOutput, calls=%fused_computation.6 | convolution fusion | flops 5369757696 | bytes 15204352 | tf_op jit(solution)/shard_map/dot_general | solution.py:150
  361.7 5.8 convolution_convert_fusion.1
  368.5 7.0 %collective-permute-done.49 = bf16[160,2048]{1,0:T(8,128)(2,1)S(1)} collective-permute-done((bf16[160,2048]{1,0:T(8,128)(2,1)S(1)}, bf16[160,2048]{1,0:T(8,128)(2,1)S(1)}, u32[]{:S(2)}, u32[]{:S(2)}) %collective-permute-start.49) | collective-permute-done | bytes 655392 | tf_op jit(solution)/shard_map/ppermute | solution.py:49
  379.3 6.8 convolution_convert_fusion
  386.1 6.0 collective-permute-done.50
  395.7 17.6 %shard_map.320 = bf16[8,2,160,2048]{3,2,1,0:T(8,128)(2,1)} custom-call(s32[8]{0:T(128)} %compare_select_fusion.6.chip_ref, s32[8]{0:T(128)} %constant.190.clone.same_ref, s32[8]{0:T(128)} %constant.191.clone.cross_ref, s32[1]{0:T(128)} %bitcast.16.core_ref, bf16[2560,512]{1,0:T(8,128)(2,1)} %get-tuple-element.341.refs_0_.refs_1_, ...), custom_call_target="tpu_custom_call" | custom-call | flops 10737418240 | bytes 19922944 | tf_op jit(solution)/shard_map/pallas_call | solution.py:932
  414.1 1.9 convert_add_fusion.4
  420.4 13.7 %collective-permute-done.54 = bf16[160,2048]{1,0:T(8,128)(2,1)S(1)} collective-permute-done((bf16[160,2048]{1,0:T(8,128)(2,1)S(1)}, bf16[160,2048]{1,0:T(8,128)(2,1)S(1)}, u32[]{:S(2)}, u32[]{:S(2)}) %collective-permute-start.54) | collective-permute-done | bytes 655392 | tf_op jit(solution)/shard_map/ppermute | solution.py:26
  436.4 6.2 shard_map.321.refs_14_
  444.0 19.8 %shard_map.322 = (f32[320,1024]{1,0:T(8,128)}, f32[320,1]{1,0:T(8,128)}, f32[1,1024]{1,0:T(1,128)}, f32[320,1024]{1,0:T(8,128)}, f32[320,1024]{1,0:T(8,128)}, /*...) custom-call(f32[320,1024]{1,0:T(8,128)} %get-tuple-element.179.flat_, ...), custom_call_target="tpu_custom_call" | custom-call | flops 20000000000 | bytes 40000000 | tf_op jit(solution)/shard_map/pallas_call | solution.py:331
  469.1 3.1 shard_map.323
  474.3 2.3 slice.183
  477.8 2.2 pad_maximum_fusion.1.refs_3_
  479.9 1.9 slice.181
  481.8 21.9 %collective-permute-done.66.refs_9_ = bf16[2,128,1024]{2,1,0:T(8,128)(2,1)S(1)} collective-permute-done((bf16[2,128,1024]{2,1,0:T(8,128)(2,1)}, bf16[2,128,1024]{2,1,0:T(8,128)(2,1)S(1)}, u32[]{:S(2)}, u32[]{:S(2)}) %collective-permute-start.66) | collective-permute-done | bytes 524320 | tf_op jit(solution)/shard_map/ppermute | solution.py:22
  508.1 6.4 collective-permute-done.68.refs_11_
  515.8 5.3 shard_map.324
  522.4 4.9 psum.23
  529.0 5.0 shard_map.325
  534.1 9.3 %shard_map.326 = f32[320,2048]{1,0:T(8,128)} custom-call(bf16[320,1024]{1,0:T(8,128)(2,1)} %get-tuple-element.297.refs_0_.refs_4_, bf16[320,1024]{1,0:T(8,128)(2,1)} %get-tuple-element.298.refs_1_.refs_5_, bf16[320,1024]{1,0:T(8,128)(2,1)} %get-tuple-element.296.refs_10_.refs_2_.refs_6_, bf16[16,528,1024]{2,1,0:T(8,128)(2,1)} %bitcast.91, ...), custom_call_target="tpu_custom_call" | custom-call | flops 4026531840 | bytes 15204352 | tf_op jit(solution)/shard_map/pallas_call | solution.py:544
  543.4 2.3 dynamic-slice_convert_fusion
  549.0 14.1 %shard_map.327 = (bf16[8,256,2048]{2,1,0:T(8,128)(2,1)}, bf16[256,1024]{1,0:T(8,128)(2,1)}, bf16[256,1024]{1,0:T(8,128)(2,1)}) custom-call(s32[8]{0:T(128)} %compare_select_fusion.6.chip_ref, s32[1]{0:T(128)} %bitcast.16.core_ref, bf16[320,2048]{1,0:T(8,128)(2,1)} %multiply_convert_fusion.refs_0_, bf16[320,2048]{1,0:T(8,128)(2,1)} %collective-permute-done.56.refs_1_, ...), custom_call_target="tpu_custom_call" | custom-call | flops 5368709120 | bytes 16252928 | tf_op jit(solution)/shard_map/pallas_call | solution.py:627
  563.9 2.1 collective-permute-start.70
  566.0 1.8 slice_bitcast_fusion
  567.9 10.6 %collective-permute-done.71 = bf16[256,1024]{1,0:T(8,128)(2,1)S(1)} collective-permute-done((bf16[256,1024]{1,0:T(8,128)(2,1)}, bf16[256,1024]{1,0:T(8,128)(2,1)S(1)}, u32[]{:S(2)}, u32[]{:S(2)}) %collective-permute-start.71) | collective-permute-done | bytes 524320 | tf_op jit(solution)/shard_map/ppermute | solution.py:49
  579.1 2.3 collective-permute-start.72
  585.6 18.7 %collective-permute-done.72 = bf16[256,2048]{1,0:T(8,128)(2,1)S(1)} collective-permute-done((bf16[256,2048]{1,0:T(8,128)(2,1)S(1)}, bf16[256,2048]{1,0:T(8,128)(2,1)S(1)}, u32[]{:S(2)}, u32[]{:S(2)}) %collective-permute-start.72) | collective-permute-done | bytes 1048608 | tf_op jit(solution)/shard_map/ppermute | solution.py:49
  605.7 2.1 fusion.2
  610.0 8.4 %add_bitcast_fusion = f32[1,512,2048]{2,1,0:T(8,128)} fusion(bf16[512,2048]{1,0:T(8,128)(2,1)} %collective-permute-done.52, bf16[2560,512]{1,0:T(8,128)(2,1)S(1)} %copy-done.3, bf16[2560,2048]{1,0:T(8,128)(2,1)S(1)} %bitcast.95), kind=kOutput, calls=%fused_computation.1 | convolution fusion | flops 5370806272 | bytes 19398656 | tf_op jit(solution)/shard_map/dot_general | solution.py:150
  618.3 13.2 %collective-permute-done.77 = bf16[256,2048]{1,0:T(8,128)(2,1)} collective-permute-done((bf16[256,2048]{1,0:T(8,128)(2,1)}, bf16[256,2048]{1,0:T(8,128)(2,1)}, u32[]{:S(2)}, u32[]{:S(2)}) %collective-permute-start.77) | collective-permute-done | bytes 1048608 | tf_op jit(solution)/shard_map/ppermute | solution.py:49
  632.4 3.6 fusion
  638.1 9.4 %add_bitcast_fusion.2 = f32[1,2048,512]{2,1,0:T(8,128)} fusion(bf16[2560,2048]{1,0:T(8,128)(2,1)S(1)} %bitcast.99, bf16[2560,512]{1,0:T(8,128)(2,1)S(1)} %copy-done.5, bf16[512,512]{1,0:T(8,128)(2,1)} %collective-permute-done.59, bf16[1024,512]{1,0:T(8,128)(2,1)} %collective-permute-done.58, bf16[512,512]{1,0:T(8,128)(2,1)} %collective-permute-done.53), kind=kOutput, calls=%fused_computation.3 | convolution fusion | flops 5376049152 | bytes 19398656 | tf_op jit(solution)/shard_map/dot_general | solution.py:150
  647.5 2.9 shard_map.329
  650.4 3.2 shard_map.328
  654.4 3.7 all-to-all-start
  659.5 3.4 shard_map.330
  662.8 11.9 %add_bitcast_fusion.1 = f32[1,2048,512]{2,1,0:T(8,128)} fusion(bf16[2560,2048]{1,0:T(8,128)(2,1)} %get-tuple-element.336, bf16[2560,512]{1,0:T(8,128)(2,1)S(1)} %copy-done.7, bf16[512,512]{1,0:T(8,128)(2,1)} %collective-permute-done.83, bf16[512,512]{1,0:T(8,128)(2,1)} %collective-permute-done.82, bf16[1024,512]{1,0:T(8,128)(2,1)} %collective-permute-done.60), kind=kOutput, calls=%fused_computation.2 | convolution fusion | flops 5376049152 | bytes 19398656 | tf_op jit(solution)/shard_map/dot_general | solution.py:150
  675.4 3.0 shard_map.331
  (421 shorter events, 112.2 us)
Async XLA Ops:
  7.2 101.6 %all-gather.5.cloned.1.call-start = ((), (), s32[]{:S(2)}) async-start(), calls=%async_computation.3 | async-start | bytes 18382848 | tf_op jit(solution)/shard_map/all_gather | solution.py:1051
  12.6 194.7 %all-gather.7.cloned.1.call-start = ((), (), s32[]{:S(2)}) async-start(), calls=%async_computation.4 | async-start | bytes 11141120 | tf_op jit(solution)/shard_map/all_gather | solution.py:1053
  15.0 548.2 %reduce-scatter.2.cloned.1.call-start = ((), (), s32[]{:S(2)}) async-start(), calls=%async_computation.2 | async-start | bytes 11141120 | tf_op jit(solution)/shard_map/reduce_scatter | solution.py:1182
  15.1 49.6 %collective-permute-start = (bf16[2048,512]{1,0:T(8,128)(2,1)S(1)}, bf16[2048,512]{1,0:T(8,128)(2,1)}, u32[]{:S(2)}, u32[]{:S(2)}) collective-permute-start(bf16[2048,512]{1,0:T(8,128)(2,1)S(1)} %bitcast.105), channel_id=1, source_target_pairs={{0,1},{1,0},{2,3},{3,2},{4,5},{5,4},{6,7},{7,6},{8,9},{9,8},{10,11... | collective-permute-start | bytes 6291464 | tf_op jit(solution)/shard_map/ppermute | solution.py:26
  18.1 90.7 %collective-permute-start.1 = (bf16[2048,512]{1,0:T(8,128)(2,1)}, bf16[2048,512]{1,0:T(8,128)(2,1)}, u32[]{:S(2)}, u32[]{:S(2)}) collective-permute-start(bf16[2048,512]{1,0:T(8,128)(2,1)} %bitcast.106), channel_id=1, source_target_pairs={{0,1},{1,0},{2,3},{3,2},{4,5},{5,4},{6,7},{7,6},{8,9},{9,8},{10,11... | collective-permute-start | bytes 6291464 | tf_op jit(solution)/shard_map/ppermute | solution.py:26
  129.5 72.1 %collective-permute-start.16 = (bf16[512,2048]{1,0:T(8,128)(2,1)S(1)}, bf16[512,2048]{1,0:T(8,128)(2,1)}, u32[]{:S(2)}, u32[]{:S(2)}) collective-permute-start(bf16[512,2048]{1,0:T(8,128)(2,1)S(1)} %bitcast.118), channel_id=1, source_target_pairs={{0,1},{1,0},{2,3},{3,2},{4,5},{5,4},{6,7},{7,6},{8,9},{9,8},{10,11... | collective-permute-start | bytes 6291464 | tf_op jit(solution)/shard_map/ppermute | solution.py:26
  158.5 24.4 %collective-permute-start.14 = (bf16[128,1024]{1,0:T(8,128)(2,1)}, bf16[128,1024]{1,0:T(8,128)(2,1)}, u32[]{:S(2)}, u32[]{:S(2)}) collective-permute-start(bf16[128,1024]{1,0:T(8,128)(2,1)} %collective-permute-done.10.refs_8_), channel_id=1, source_target_pairs={{0,8},{2,10},{4,12},{6,14},{8,0},{10,2},{12,4},{14,6},{16,24},{18,... | collective-permute-start | bytes 786440 | tf_op jit(solution)/shard_map/ppermute | solution.py:22
  163.9 21.2 %collective-permute-start.11 = (bf16[128,1024]{1,0:T(8,128)(2,1)}, bf16[128,1024]{1,0:T(8,128)(2,1)}, u32[]{:S(2)}, u32[]{:S(2)}) collective-permute-start(bf16[128,1024]{1,0:T(8,128)(2,1)} %collective-permute-done.10.refs_8_), channel_id=1, source_target_pairs={{0,2},{2,0},{4,6},{6,4},{8,10},{10,8},{12,14},{14,12},{16,18},{18,... | collective-permute-start | bytes 786440 | tf_op jit(solution)/shard_map/ppermute | solution.py:22
  163.9 21.2 %collective-permute-start.13 = (bf16[128,1024]{1,0:T(8,128)(2,1)}, bf16[128,1024]{1,0:T(8,128)(2,1)}, u32[]{:S(2)}, u32[]{:S(2)}) collective-permute-start(bf16[128,1024]{1,0:T(8,128)(2,1)} %collective-permute-done.12.refs_10_), channel_id=1, source_target_pairs={{0,2},{2,0},{4,6},{6,4},{8,10},{10,8},{12,14},{14,12},{16,18},{18,... | collective-permute-start | bytes 786440 | tf_op jit(solution)/shard_map/ppermute | solution.py:22
  164.4 20.7 %collective-permute-start.8 = (bf16[128,1024]{1,0:T(8,128)(2,1)}, bf16[128,1024]{1,0:T(8,128)(2,1)}, u32[]{:S(2)}, u32[]{:S(2)}) collective-permute-start(bf16[128,1024]{1,0:T(8,128)(2,1)} %collective-permute-done.7.refs_5_), channel_id=1, source_target_pairs={{0,2},{2,0},{4,6},{6,4},{8,10},{10,8},{12,14},{14,12},{16,18},{18,... | collective-permute-start | bytes 786440 | tf_op jit(solution)/shard_map/ppermute | solution.py:22
  203.0 17.2 %collective-permute-start.17 = (bf16[160,2048]{1,0:T(8,128)(2,1)S(1)}, bf16[160,2048]{1,0:T(8,128)(2,1)S(1)}, u32[]{:S(2)}, u32[]{:S(2)}) collective-permute-start(bf16[160,2048]{1,0:T(8,128)(2,1)S(1)} %dynamic-slice_convert_fusion.1), channel_id=1, source_target_pairs={{0,1},{1,0},{2,3},{3,2},{4,5},{5,4},{6,7},{7,6},{8,9},{9,8},{10,11... | collective-permute-start | bytes 1966088 | tf_op jit(solution)/shard_map/ppermute | solution.py:26
  224.6 19.6 %collective-permute-start.19 = (bf16[160,2048]{1,0:T(8,128)(2,1)S(1)}, bf16[160,2048]{1,0:T(8,128)(2,1)}, u32[]{:S(2)}, u32[]{:S(2)}) collective-permute-start(bf16[160,2048]{1,0:T(8,128)(2,1)S(1)} %multiply_convert_fusion.1.refs_1_), channel_id=1, source_target_pairs={{0,8},{2,10},{8,16},{10,18},{16,24},{18,26},{24,28},{26,30},{28,20... | collective-permute-start | bytes 1966088 | tf_op jit(solution)/shard_map/ppermute | solution.py:45
  224.6 19.6 %collective-permute-start.20 = (bf16[160,2048]{1,0:T(8,128)(2,1)S(1)}, bf16[160,2048]{1,0:T(8,128)(2,1)S(1)}, u32[]{:S(2)}, u32[]{:S(2)}) collective-permute-start(bf16[160,2048]{1,0:T(8,128)(2,1)S(1)} %multiply_convert_fusion.1.refs_1_), channel_id=1, source_target_pairs={{8,0},{10,2},{16,8},{18,10},{24,16},{26,18},{28,24},{30,26},{20,28... | collective-permute-start | bytes 1966088 | tf_op jit(solution)/shard_map/ppermute | solution.py:49
  229.2 18.6 %collective-permute-start.24 = (f32[40,2048]{1,0:T(8,128)}, f32[40,2048]{1,0:T(8,128)S(1)}, u32[]{:S(2)}, u32[]{:S(2)}) collective-permute-start(f32[40,2048]{1,0:T(8,128)} %get-tuple-element.208), channel_id=1, source_target_pairs={{0,1},{1,0},{2,3},{3,2},{4,5},{5,4},{6,7},{7,6},{8,9},{9,8},{10,11... | collective-permute-start | bytes 983048 | tf_op jit(solution)/shard_map/ppermute | solution.py:26
  245.1 17.2 %collective-permute-start.22 = (bf16[160,2048]{1,0:T(8,128)(2,1)}, bf16[160,2048]{1,0:T(8,128)(2,1)}, u32[]{:S(2)}, u32[]{:S(2)}) collective-permute-start(bf16[160,2048]{1,0:T(8,128)(2,1)} %collective-permute-done.19.refs_1_), channel_id=1, source_target_pairs={{0,8},{2,10},{8,16},{10,18},{16,24},{18,26},{24,28},{26,30},{28,20... | collective-permute-start | bytes 1966088 | tf_op jit(solution)/shard_map/ppermute | solution.py:45
  245.1 17.2 %collective-permute-start.23 = (bf16[160,2048]{1,0:T(8,128)(2,1)}, bf16[160,2048]{1,0:T(8,128)(2,1)S(1)}, u32[]{:S(2)}, u32[]{:S(2)}) collective-permute-start(bf16[160,2048]{1,0:T(8,128)(2,1)} %copy-done.37), channel_id=1, source_target_pairs={{8,0},{10,2},{16,8},{18,10},{24,16},{26,18},{28,24},{30,26},{20,28... | collective-permute-start | bytes 1966088 | tf_op jit(solution)/shard_map/ppermute | solution.py:49
  247.2 17.9 %collective-permute-start.26 = (bf16[160,2048]{1,0:T(8,128)(2,1)}, bf16[160,2048]{1,0:T(8,128)(2,1)}, u32[]{:S(2)}, u32[]{:S(2)}) collective-permute-start(bf16[160,2048]{1,0:T(8,128)(2,1)} %collective-permute-done.19.refs_1_), channel_id=1, source_target_pairs={{0,2},{2,0},{4,6},{6,4},{8,10},{10,8},{12,14},{14,12},{16,18},{18,... | collective-permute-start | bytes 1966088 | tf_op jit(solution)/shard_map/ppermute | solution.py:22
  247.2 18.1 %collective-permute-start.27 = (bf16[160,2048]{1,0:T(8,128)(2,1)}, bf16[160,2048]{1,0:T(8,128)(2,1)}, u32[]{:S(2)}, u32[]{:S(2)}) collective-permute-start(bf16[160,2048]{1,0:T(8,128)(2,1)} %copy-done.37), channel_id=1, source_target_pairs={{0,2},{2,0},{4,6},{6,4},{8,10},{10,8},{12,14},{14,12},{16,18},{18,... | collective-permute-start | bytes 1966088 | tf_op jit(solution)/shard_map/ppermute | solution.py:22
  247.7 14.9 %collective-permute-start.25 = (f32[40,2048]{1,0:T(8,128)}, f32[40,2048]{1,0:T(8,128)S(1)}, u32[]{:S(2)}, u32[]{:S(2)}) collective-permute-start(f32[40,2048]{1,0:T(8,128)} %get-tuple-element.220), channel_id=1, source_target_pairs={{0,1},{1,0},{2,3},{3,2},{4,5},{5,4},{6,7},{7,6},{8,9},{9,8},{10,11... | collective-permute-start | bytes 983048 | tf_op jit(solution)/shard_map/ppermute | solution.py:26
  262.3 25.9 %collective-permute-start.29 = (bf16[160,2048]{1,0:T(8,128)(2,1)}, bf16[160,2048]{1,0:T(8,128)(2,1)S(1)}, u32[]{:S(2)}, u32[]{:S(2)}) collective-permute-start(bf16[160,2048]{1,0:T(8,128)(2,1)} %collective-permute-done.22.refs_1_), channel_id=1, source_target_pairs={{0,8},{2,10},{8,16},{10,18},{16,24},{18,26},{24,28},{26,30},{28,20... | collective-permute-start | bytes 1966088 | tf_op jit(solution)/shard_map/ppermute | solution.py:45
  262.7 28.4 %collective-permute-start.32 = (bf16[160,2048]{1,0:T(8,128)(2,1)}, bf16[160,2048]{1,0:T(8,128)(2,1)}, u32[]{:S(2)}, u32[]{:S(2)}) collective-permute-start(bf16[160,2048]{1,0:T(8,128)(2,1)} %collective-permute-done.22.refs_1_), channel_id=1, source_target_pairs={{0,2},{2,0},{4,6},{6,4},{8,10},{10,8},{12,14},{14,12},{16,18},{18,... | collective-permute-start | bytes 1966088 | tf_op jit(solution)/shard_map/ppermute | solution.py:22
  263.4 24.7 %collective-permute-start.30 = (bf16[160,2048]{1,0:T(8,128)(2,1)S(1)}, bf16[160,2048]{1,0:T(8,128)(2,1)S(1)}, u32[]{:S(2)}, u32[]{:S(2)}) collective-permute-start(bf16[160,2048]{1,0:T(8,128)(2,1)S(1)} %collective-permute-done.23.refs_2_), channel_id=1, source_target_pairs={{8,0},{10,2},{16,8},{18,10},{24,16},{26,18},{28,24},{30,26},{20,28... | collective-permute-start | bytes 1966088 | tf_op jit(solution)/shard_map/ppermute | solution.py:49
  265.1 26.3 %collective-permute-start.33 = (bf16[160,2048]{1,0:T(8,128)(2,1)S(1)}, bf16[160,2048]{1,0:T(8,128)(2,1)}, u32[]{:S(2)}, u32[]{:S(2)}) collective-permute-start(bf16[160,2048]{1,0:T(8,128)(2,1)S(1)} %collective-permute-done.23.refs_2_), channel_id=1, source_target_pairs={{0,2},{2,0},{4,6},{6,4},{8,10},{10,8},{12,14},{14,12},{16,18},{18,... | collective-permute-start | bytes 1966088 | tf_op jit(solution)/shard_map/ppermute | solution.py:22
  265.4 24.9 %collective-permute-start.31 = (f32[40,2048]{1,0:T(8,128)}, f32[40,2048]{1,0:T(8,128)S(1)}, u32[]{:S(2)}, u32[]{:S(2)}) collective-permute-start(f32[40,2048]{1,0:T(8,128)} %get-tuple-element.234), channel_id=1, source_target_pairs={{0,1},{1,0},{2,3},{3,2},{4,5},{5,4},{6,7},{7,6},{8,9},{9,8},{10,11... | collective-permute-start | bytes 983048 | tf_op jit(solution)/shard_map/ppermute | solution.py:26
  289.0 28.4 %collective-permute-start.40 = (bf16[160,2048]{1,0:T(8,128)(2,1)S(1)}, bf16[160,2048]{1,0:T(8,128)(2,1)}, u32[]{:S(2)}, u32[]{:S(2)}) collective-permute-start(bf16[160,2048]{1,0:T(8,128)(2,1)S(1)} %collective-permute-done.29.refs_1_), channel_id=1, source_target_pairs={{0,2},{2,0},{4,6},{6,4},{8,10},{10,8},{12,14},{14,12},{16,18},{18,... | collective-permute-start | bytes 1966088 | tf_op jit(solution)/shard_map/ppermute | solution.py:22
  289.8 27.6 %collective-permute-start.41 = (bf16[160,2048]{1,0:T(8,128)(2,1)S(1)}, bf16[160,2048]{1,0:T(8,128)(2,1)}, u32[]{:S(2)}, u32[]{:S(2)}) collective-permute-start(bf16[160,2048]{1,0:T(8,128)(2,1)S(1)} %collective-permute-done.30.refs_2_), channel_id=1, source_target_pairs={{0,2},{2,0},{4,6},{6,4},{8,10},{10,8},{12,14},{14,12},{16,18},{18,... | collective-permute-start | bytes 1966088 | tf_op jit(solution)/shard_map/ppermute | solution.py:22
  290.3 24.9 %collective-permute-start.37 = (f32[40,2048]{1,0:T(8,128)}, f32[40,2048]{1,0:T(8,128)}, u32[]{:S(2)}, u32[]{:S(2)}) collective-permute-start(f32[40,2048]{1,0:T(8,128)} %get-tuple-element.245), channel_id=1, source_target_pairs={{0,1},{1,0},{2,3},{3,2},{4,5},{5,4},{6,7},{7,6},{8,9},{9,8},{10,11... | collective-permute-start | bytes 983048 | tf_op jit(solution)/shard_map/ppermute | solution.py:26
  291.1 24.1 %collective-permute-start.35 = (bf16[80,2048]{1,0:T(8,128)(2,1)}, bf16[80,2048]{1,0:T(8,128)(2,1)S(1)}, u32[]{:S(2)}, u32[]{:S(2)}) collective-permute-start(bf16[80,2048]{1,0:T(8,128)(2,1)} %slice.169), channel_id=1, source_target_pairs={{0,8},{2,10},{8,16},{10,18},{16,24},{18,26},{24,28},{26,30},{28,20... | collective-permute-start | bytes 983048 | tf_op jit(solution)/shard_map/ppermute | solution.py:45
  291.4 23.8 %collective-permute-start.36 = (bf16[80,2048]{1,0:T(8,128)(2,1)}, bf16[80,2048]{1,0:T(8,128)(2,1)S(1)}, u32[]{:S(2)}, u32[]{:S(2)}) collective-permute-start(bf16[80,2048]{1,0:T(8,128)(2,1)} %slice.170), channel_id=1, source_target_pairs={{8,0},{10,2},{16,8},{18,10},{24,16},{26,18},{28,24},{30,26},{20,28... | collective-permute-start | bytes 983048 | tf_op jit(solution)/shard_map/ppermute | solution.py:49
  315.8 25.6 %collective-permute-start.28 = (bf16[320,2048]{1,0:T(8,128)(2,1)}, bf16[320,2048]{1,0:T(8,128)(2,1)}, u32[]{:S(2)}, u32[]{:S(2)}) collective-permute-start(bf16[320,2048]{1,0:T(8,128)(2,1)} %get-tuple-element.230), channel_id=1, source_target_pairs={{0,2},{2,0},{4,6},{6,4},{8,10},{10,8},{12,14},{14,12},{16,18},{18,... | collective-permute-start | bytes 3932168 | tf_op jit(solution)/shard_map/ppermute | solution.py:22
  340.6 72.7 %collective-permute-start.21 = (bf16[160,2048]{1,0:T(8,128)(2,1)}, bf16[160,2048]{1,0:T(8,128)(2,1)}, u32[]{:S(2)}, u32[]{:S(2)}) collective-permute-start(bf16[160,2048]{1,0:T(8,128)(2,1)} %get-tuple-element.205), channel_id=1, source_target_pairs={{0,2},{2,0},{4,6},{6,4},{8,10},{10,8},{12,14},{14,12},{16,18},{18,... | collective-permute-start | bytes 1966088 | tf_op jit(solution)/shard_map/ppermute | solution.py:22
  340.9 15.9 %collective-permute-start.34 = (bf16[320,2048]{1,0:T(8,128)(2,1)}, bf16[320,2048]{1,0:T(8,128)(2,1)S(1)}, u32[]{:S(2)}, u32[]{:S(2)}) collective-permute-start(bf16[320,2048]{1,0:T(8,128)(2,1)} %get-tuple-element.244), channel_id=1, source_target_pairs={{0,2},{2,0},{4,6},{6,4},{8,10},{10,8},{12,14},{14,12},{16,18},{18,... | collective-permute-start | bytes 3932168 | tf_op jit(solution)/shard_map/ppermute | solution.py:22
  341.1 17.6 %collective-permute-start.42 = (bf16[320,2048]{1,0:T(8,128)(2,1)}, bf16[320,2048]{1,0:T(8,128)(2,1)S(1)}, u32[]{:S(2)}, u32[]{:S(2)}) collective-permute-start(bf16[320,2048]{1,0:T(8,128)(2,1)} %get-tuple-element.257), channel_id=1, source_target_pairs={{0,2},{2,0},{4,6},{6,4},{8,10},{10,8},{12,14},{14,12},{16,18},{18,... | collective-permute-start | bytes 3932168 | tf_op jit(solution)/shard_map/ppermute | solution.py:22
  343.5 15.7 %collective-permute-start.44 = (bf16[80,2048]{1,0:T(8,128)(2,1)S(1)}, bf16[80,2048]{1,0:T(8,128)(2,1)S(1)}, u32[]{:S(2)}, u32[]{:S(2)}) collective-permute-start(bf16[80,2048]{1,0:T(8,128)(2,1)S(1)} %get-tuple-element.380), channel_id=1, source_target_pairs={{0,8},{2,10},{8,16},{10,18},{16,24},{18,26},{24,28},{26,30},{28,20... | collective-permute-start | bytes 983048 | tf_op jit(solution)/shard_map/ppermute | solution.py:45
  343.9 14.7 %collective-permute-start.48 = (bf16[80,2048]{1,0:T(8,128)(2,1)S(1)}, bf16[80,2048]{1,0:T(8,128)(2,1)S(1)}, u32[]{:S(2)}, u32[]{:S(2)}) collective-permute-start(bf16[80,2048]{1,0:T(8,128)(2,1)S(1)} %get-tuple-element.381), channel_id=1, source_target_pairs={{8,0},{10,2},{16,8},{18,10},{24,16},{26,18},{28,24},{30,26},{20,28... | collective-permute-start | bytes 983048 | tf_op jit(solution)/shard_map/ppermute | solution.py:49
  356.8 59.2 %collective-permute-start.52 = (bf16[512,2048]{1,0:T(8,128)(2,1)}, bf16[512,2048]{1,0:T(8,128)(2,1)}, u32[]{:S(2)}, u32[]{:S(2)}) collective-permute-start(bf16[512,2048]{1,0:T(8,128)(2,1)} %convolution_convert_fusion.2), channel_id=1, source_target_pairs={{0,1},{1,0},{2,3},{3,2},{4,5},{5,4},{6,7},{7,6},{8,9},{9,8},{10,11... | collective-permute-start | bytes 6291464 | tf_op jit(solution)/shard_map/ppermute | solution.py:26
  359.5 16.0 %collective-permute-start.49 = (bf16[160,2048]{1,0:T(8,128)(2,1)S(1)}, bf16[160,2048]{1,0:T(8,128)(2,1)S(1)}, u32[]{:S(2)}, u32[]{:S(2)}) collective-permute-start(bf16[160,2048]{1,0:T(8,128)(2,1)S(1)} %pad_maximum_fusion.5), channel_id=1, source_target_pairs={{8,0},{10,2},{16,8},{18,10},{24,16},{26,18},{28,24},{30,26},{20,28... | collective-permute-start | bytes 1966088 | tf_op jit(solution)/shard_map/ppermute | solution.py:49
  360.9 15.7 %collective-permute-start.45 = (bf16[160,2048]{1,0:T(8,128)(2,1)S(1)}, bf16[160,2048]{1,0:T(8,128)(2,1)S(1)}, u32[]{:S(2)}, u32[]{:S(2)}) collective-permute-start(bf16[160,2048]{1,0:T(8,128)(2,1)S(1)} %pad_maximum_fusion.4), channel_id=1, source_target_pairs={{0,8},{2,10},{8,16},{10,18},{16,24},{18,26},{24,28},{26,30},{28,20... | collective-permute-start | bytes 1966088 | tf_op jit(solution)/shard_map/ppermute | solution.py:45
  367.6 48.4 %collective-permute-start.53 = (bf16[512,512]{1,0:T(8,128)(2,1)S(1)}, bf16[512,512]{1,0:T(8,128)(2,1)}, u32[]{:S(2)}, u32[]{:S(2)}) collective-permute-start(bf16[512,512]{1,0:T(8,128)(2,1)S(1)} %slice.222), channel_id=1, source_target_pairs={{0,1},{1,0},{2,3},{3,2},{4,5},{5,4},{6,7},{7,6},{8,9},{9,8},{10,11... | collective-permute-start | bytes 1572872 | tf_op jit(solution)/shard_map/ppermute | solution.py:26
  377.2 14.9 %collective-permute-start.50 = (bf16[160,2048]{1,0:T(8,128)(2,1)S(1)}, bf16[160,2048]{1,0:T(8,128)(2,1)S(1)}, u32[]{:S(2)}, u32[]{:S(2)}) collective-permute-start(bf16[160,2048]{1,0:T(8,128)(2,1)S(1)} %get-tuple-element.371), channel_id=1, source_target_pairs={{8,0},{10,2},{16,8},{18,10},{24,16},{26,18},{28,24},{30,26},{20,28... | collective-permute-start | bytes 1966088 | tf_op jit(solution)/shard_map/ppermute | solution.py:49
  393.7 19.6 %collective-permute-start.47 = (bf16[160,2048]{1,0:T(8,128)(2,1)}, bf16[160,2048]{1,0:T(8,128)(2,1)S(1)}, u32[]{:S(2)}, u32[]{:S(2)}) collective-permute-start(bf16[160,2048]{1,0:T(8,128)(2,1)} %get-tuple-element.368), channel_id=1, source_target_pairs={{0,8},{2,10},{8,16},{10,18},{16,24},{18,26},{24,28},{26,30},{28,20... | collective-permute-start | bytes 1966088 | tf_op jit(solution)/shard_map/ppermute | solution.py:45
  395.2 18.9 %collective-permute-start.51 = (bf16[160,2048]{1,0:T(8,128)(2,1)S(1)}, bf16[160,2048]{1,0:T(8,128)(2,1)}, u32[]{:S(2)}, u32[]{:S(2)}) collective-permute-start(bf16[160,2048]{1,0:T(8,128)(2,1)S(1)} %get-tuple-element.369), channel_id=1, source_target_pairs={{8,0},{10,2},{16,8},{18,10},{24,16},{26,18},{28,24},{30,26},{20,28... | collective-permute-start | bytes 1966088 | tf_op jit(solution)/shard_map/ppermute | solution.py:49
  419.3 14.8 %collective-permute-start.54 = (bf16[160,2048]{1,0:T(8,128)(2,1)S(1)}, bf16[160,2048]{1,0:T(8,128)(2,1)S(1)}, u32[]{:S(2)}, u32[]{:S(2)}) collective-permute-start(bf16[160,2048]{1,0:T(8,128)(2,1)S(1)} %get-tuple-element.352), channel_id=1, source_target_pairs={{0,1},{1,0},{2,3},{3,2},{4,5},{5,4},{6,7},{7,6},{8,9},{9,8},{10,11... | collective-permute-start | bytes 1966088 | tf_op jit(solution)/shard_map/ppermute | solution.py:26
  442.6 30.5 %collective-permute-start.58 = (bf16[1024,512]{1,0:T(8,128)(2,1)}, bf16[1024,512]{1,0:T(8,128)(2,1)}, u32[]{:S(2)}, u32[]{:S(2)}) collective-permute-start(bf16[1024,512]{1,0:T(8,128)(2,1)} %slice.182), channel_id=1, source_target_pairs={{0,1},{1,0},{2,3},{3,2},{4,5},{5,4},{6,7},{7,6},{8,9},{9,8},{10,11... | collective-permute-start | bytes 3145736 | tf_op jit(solution)/shard_map/ppermute | solution.py:26
  464.4 41.0 %collective-permute-start.56 = (bf16[320,2048]{1,0:T(8,128)(2,1)S(1)}, bf16[320,2048]{1,0:T(8,128)(2,1)}, u32[]{:S(2)}, u32[]{:S(2)}) collective-permute-start(bf16[320,2048]{1,0:T(8,128)(2,1)S(1)} %copy-done.14), channel_id=1, source_target_pairs={{0,2},{2,0},{4,6},{6,4},{8,10},{10,8},{12,14},{14,12},{16,18},{18,... | collective-permute-start | bytes 3932168 | tf_op jit(solution)/shard_map/ppermute | solution.py:22
  466.1 40.9 %collective-permute-start.57 = (bf16[320,2048]{1,0:T(8,128)(2,1)S(1)}, bf16[320,2048]{1,0:T(8,128)(2,1)}, u32[]{:S(2)}, u32[]{:S(2)}) collective-permute-start(bf16[320,2048]{1,0:T(8,128)(2,1)S(1)} %copy-done.13), channel_id=1, source_target_pairs={{0,2},{2,0},{4,6},{6,4},{8,10},{10,8},{12,14},{14,12},{16,18},{18,... | collective-permute-start | bytes 3932168 | tf_op jit(solution)/shard_map/ppermute | solution.py:22
  472.3 31.5 %collective-permute-start.66 = (bf16[2,128,1024]{2,1,0:T(8,128)(2,1)}, bf16[2,128,1024]{2,1,0:T(8,128)(2,1)S(1)}, u32[]{:S(2)}, u32[]{:S(2)}) collective-permute-start(bf16[2,128,1024]{2,1,0:T(8,128)(2,1)} %get-tuple-element.291), channel_id=1, source_target_pairs={{0,8},{2,10},{4,12},{6,14},{8,0},{10,2},{12,4},{14,6},{16,24},{18,... | collective-permute-start | bytes 1572872 | tf_op jit(solution)/shard_map/ppermute | solution.py:22
  473.1 30.8 %collective-permute-start.65 = (bf16[2,128,1024]{2,1,0:T(8,128)(2,1)}, bf16[2,128,1024]{2,1,0:T(8,128)(2,1)S(1)}, u32[]{:S(2)}, u32[]{:S(2)}) collective-permute-start(bf16[2,128,1024]{2,1,0:T(8,128)(2,1)} %get-tuple-element.290), channel_id=1, source_target_pairs={{0,4},{2,6},{4,0},{6,2},{8,12},{10,14},{12,8},{14,10},{16,20},{18,... | collective-permute-start | bytes 1572872 | tf_op jit(solution)/shard_map/ppermute | solution.py:22
  476.6 45.6 %collective-permute-start.60 = (bf16[1024,512]{1,0:T(8,128)(2,1)}, bf16[1024,512]{1,0:T(8,128)(2,1)}, u32[]{:S(2)}, u32[]{:S(2)}) collective-permute-start(bf16[1024,512]{1,0:T(8,128)(2,1)} %slice.183), channel_id=1, source_target_pairs={{0,1},{1,0},{2,3},{3,2},{4,5},{5,4},{6,7},{7,6},{8,9},{9,8},{10,11... | collective-permute-start | bytes 3145736 | tf_op jit(solution)/shard_map/ppermute | solution.py:26
  504.0 18.2 %collective-permute-start.59 = (bf16[512,512]{1,0:T(8,128)(2,1)}, bf16[512,512]{1,0:T(8,128)(2,1)}, u32[]{:S(2)}, u32[]{:S(2)}) collective-permute-start(bf16[512,512]{1,0:T(8,128)(2,1)} %slice.181), channel_id=1, source_target_pairs={{0,1},{1,0},{2,3},{3,2},{4,5},{5,4},{6,7},{7,6},{8,9},{9,8},{10,11... | collective-permute-start | bytes 1572872 | tf_op jit(solution)/shard_map/ppermute | solution.py:26
  545.7 36.8 %collective-permute-start.74 = (bf16[160,2048]{1,0:T(8,128)(2,1)}, bf16[160,2048]{1,0:T(8,128)(2,1)S(1)}, u32[]{:S(2)}, u32[]{:S(2)}) collective-permute-start(bf16[160,2048]{1,0:T(8,128)(2,1)} %dynamic-slice_convert_fusion), channel_id=1, source_target_pairs={{0,1},{1,0},{2,3},{3,2},{4,5},{5,4},{6,7},{7,6},{8,9},{9,8},{10,11... | collective-permute-start | bytes 1966088 | tf_op jit(solution)/shard_map/ppermute | solution.py:26
  563.2 15.3 %collective-permute-start.71 = (bf16[256,1024]{1,0:T(8,128)(2,1)}, bf16[256,1024]{1,0:T(8,128)(2,1)S(1)}, u32[]{:S(2)}, u32[]{:S(2)}) collective-permute-start(bf16[256,1024]{1,0:T(8,128)(2,1)} %get-tuple-element.313), channel_id=1, source_target_pairs={{8,0},{10,2},{16,8},{18,10},{24,16},{26,18},{28,24},{30,26},{20,28... | collective-permute-start | bytes 1572872 | tf_op jit(solution)/shard_map/ppermute | solution.py:49
  563.9 14.8 %collective-permute-start.70 = (bf16[256,1024]{1,0:T(8,128)(2,1)}, bf16[256,1024]{1,0:T(8,128)(2,1)S(1)}, u32[]{:S(2)}, u32[]{:S(2)}) collective-permute-start(bf16[256,1024]{1,0:T(8,128)(2,1)} %get-tuple-element.312), channel_id=1, source_target_pairs={{0,8},{2,10},{8,16},{10,18},{16,24},{18,26},{24,28},{26,30},{28,20... | collective-permute-start | bytes 1572872 | tf_op jit(solution)/shard_map/ppermute | solution.py:45
  579.1 25.2 %collective-permute-start.72 = (bf16[256,2048]{1,0:T(8,128)(2,1)S(1)}, bf16[256,2048]{1,0:T(8,128)(2,1)S(1)}, u32[]{:S(2)}, u32[]{:S(2)}) collective-permute-start(bf16[256,2048]{1,0:T(8,128)(2,1)S(1)} %pad_maximum_fusion.3), channel_id=1, source_target_pairs={{8,0},{10,2},{16,8},{18,10},{24,16},{26,18},{28,24},{30,26},{20,28... | collective-permute-start | bytes 3145736 | tf_op jit(solution)/shard_map/ppermute | solution.py:49
  581.4 24.2 %collective-permute-start.76 = (bf16[256,2048]{1,0:T(8,128)(2,1)S(1)}, bf16[256,2048]{1,0:T(8,128)(2,1)S(1)}, u32[]{:S(2)}, u32[]{:S(2)}) collective-permute-start(bf16[256,2048]{1,0:T(8,128)(2,1)S(1)} %pad_maximum_fusion.2), channel_id=1, source_target_pairs={{0,8},{2,10},{8,16},{10,18},{16,24},{18,26},{24,28},{26,30},{28,20... | collective-permute-start | bytes 3145736 | tf_op jit(solution)/shard_map/ppermute | solution.py:45
  581.9 80.9 %collective-permute-start.82 = (bf16[512,512]{1,0:T(8,128)(2,1)}, bf16[512,512]{1,0:T(8,128)(2,1)}, u32[]{:S(2)}, u32[]{:S(2)}) collective-permute-start(bf16[512,512]{1,0:T(8,128)(2,1)} %get-tuple-element.339), channel_id=1, source_target_pairs={{0,1},{1,0},{2,3},{3,2},{4,5},{5,4},{6,7},{7,6},{8,9},{9,8},{10,11... | collective-permute-start | bytes 1572872 | tf_op jit(solution)/shard_map/ppermute | solution.py:26
  583.5 53.4 %collective-permute-start.75 = (f32[160,2048]{1,0:T(8,128)S(1)}, f32[160,2048]{1,0:T(8,128)S(1)}, u32[]{:S(2)}, u32[]{:S(2)}) collective-permute-start(f32[160,2048]{1,0:T(8,128)S(1)} %fusion.5.refs_1_), channel_id=1, source_target_pairs={{0,1},{1,0},{2,3},{3,2},{4,5},{5,4},{6,7},{7,6},{8,9},{9,8},{10,11... | collective-permute-start | bytes 3932168 | tf_op jit(solution)/shard_map/ppermute | solution.py:26
  585.0 77.8 %collective-permute-start.83 = (bf16[512,512]{1,0:T(8,128)(2,1)}, bf16[512,512]{1,0:T(8,128)(2,1)}, u32[]{:S(2)}, u32[]{:S(2)}) collective-permute-start(bf16[512,512]{1,0:T(8,128)(2,1)} %get-tuple-element.340), channel_id=1, source_target_pairs={{0,1},{1,0},{2,3},{3,2},{4,5},{5,4},{6,7},{7,6},{8,9},{9,8},{10,11... | collective-permute-start | bytes 1572872 | tf_op jit(solution)/shard_map/ppermute | solution.py:26
  607.9 23.7 %collective-permute-start.77 = (bf16[256,2048]{1,0:T(8,128)(2,1)}, bf16[256,2048]{1,0:T(8,128)(2,1)}, u32[]{:S(2)}, u32[]{:S(2)}) collective-permute-start(bf16[256,2048]{1,0:T(8,128)(2,1)} %get-tuple-element.319), channel_id=1, source_target_pairs={{8,0},{10,2},{16,8},{18,10},{24,16},{26,18},{28,24},{30,26},{20,28... | collective-permute-start | bytes 3145736 | tf_op jit(solution)/shard_map/ppermute | solution.py:49
  609.3 23.0 %collective-permute-start.78 = (bf16[256,2048]{1,0:T(8,128)(2,1)}, bf16[256,2048]{1,0:T(8,128)(2,1)}, u32[]{:S(2)}, u32[]{:S(2)}) collective-permute-start(bf16[256,2048]{1,0:T(8,128)(2,1)} %get-tuple-element.323), channel_id=1, source_target_pairs={{0,8},{2,10},{8,16},{10,18},{16,24},{18,26},{24,28},{26,30},{28,20... | collective-permute-start | bytes 3145736 | tf_op jit(solution)/shard_map/ppermute | solution.py:45
  631.5 18.8 %collective-permute-start.73 = (bf16[160,2048]{1,0:T(8,128)(2,1)S(1)}, bf16[160,2048]{1,0:T(8,128)(2,1)}, u32[]{:S(2)}, u32[]{:S(2)}) collective-permute-start(bf16[160,2048]{1,0:T(8,128)(2,1)S(1)} %copy-done.33), channel_id=1, source_target_pairs={{0,1},{1,0},{2,3},{3,2},{4,5},{5,4},{6,7},{7,6},{8,9},{9,8},{10,11... | collective-permute-start | bytes 1966088 | tf_op jit(solution)/shard_map/ppermute | solution.py:26
  636.0 22.1 %collective-permute-start.79 = (bf16[256,2048]{1,0:T(8,128)(2,1)}, bf16[256,2048]{1,0:T(8,128)(2,1)}, u32[]{:S(2)}, u32[]{:S(2)}) collective-permute-start(bf16[256,2048]{1,0:T(8,128)(2,1)} %get-tuple-element.324), channel_id=1, source_target_pairs={{0,8},{2,10},{8,16},{10,18},{16,24},{18,26},{24,28},{26,30},{28,20... | collective-permute-start | bytes 3145736 | tf_op jit(solution)/shard_map/ppermute | solution.py:45
  636.9 22.5 %collective-permute-start.80 = (bf16[256,2048]{1,0:T(8,128)(2,1)}, bf16[256,2048]{1,0:T(8,128)(2,1)}, u32[]{:S(2)}, u32[]{:S(2)}) collective-permute-start(bf16[256,2048]{1,0:T(8,128)(2,1)} %get-tuple-element.325), channel_id=1, source_target_pairs={{8,0},{10,2},{16,8},{18,10},{24,16},{26,18},{28,24},{30,26},{20,28... | collective-permute-start | bytes 3145736 | tf_op jit(solution)/shard_map/ppermute | solution.py:49
  654.4 20.4 %all-to-all-start = ((f32[32,1,512]{2,1,0:T(1,128)}), f32[32,1,512]{2,1,0:T(1,128)S(1)}, u32[]{:S(2)}, u32[]{:S(2)}) async-start(f32[32,1,512]{2,1,0:T(1,128)} %all_to_all.6), calls=%async_computation.1 | async-start | bytes 131072 | tf_op jit(solution)/shard_map/all_to_all | solution.py:1260
  (103 other events, 1424.2 us)
Sparse Core Ops, SparseCore 0:
  12.7 94.2 all-gather.4
  109.9 97.4 all-gather.6
  416.2 134.3 reduce-scatter.1

commit v13 on v12

--- a/solution.py
+++ b/solution.py
@@ -77,12 +77,19 @@
 
 
 class Fillers:
-    def __init__(self, *stages):
-        self.stages = list(stages)
+    def __init__(self, late, *stages):
+        self.late, self.stages, self.seen = late, list(stages), set(late)
 
     def next(self, token):
         if self.stages:
             self.stages.pop(0)(lambda value: after(value, token))
+
+    def settle(self, *blocks):
+        due = {key: value for key, value in self.late.items() if key not in self.seen}
+        self.seen.update(due)
+        *blocks, due = lax.optimization_barrier((*blocks, due))
+        self.late.update(due)
+        return blocks
 
 
 def ring_sum(same, cross, fillers):
@@ -651,21 +658,22 @@
 def ring_weights(blocks, right, left, fillers):
     part = lambda hop: blocks[HOPS.index(hop)]
     cut = blocks.shape[2] // 2
+    fillers.next(right)
     right, left = ahead(right), behind(left)
+    right, left = fillers.settle(right, left)
     fillers.next(left)
     outward, inward = part(3), part(-3)
     right = jnp.concatenate([add_low(outward[:, :cut], right), outward[:, cut:]], axis=1)
     left = jnp.concatenate([inward[:, :cut], add_low(inward[:, cut:], left)], axis=1)
     right, left = together(right, left)
     right, left = ahead(right), behind(left)
-    fillers.next(left)
-    token = left
     for hop in (2, 1):
+        right, left = fillers.settle(right, left)
+        fillers.next(left)
         right, left = together(add_low(part(hop), right), add_low(part(-hop), left))
         right, left = ahead(right), behind(left)
-        fillers.next(left)
-        token = left if hop == 2 else token
-    return (blocks, right, left), token
+    right, left = fillers.settle(right, left)
+    return blocks, right, left
 
 
 def sum_kernel(core_ref, blocks_ref, right_ref, left_ref, own_ref, sent_ref):
@@ -1157,7 +1165,7 @@
         def mixed_stage(gated):
             late["mixed"] = mixed_pass(gated(h0), h1, down_mats, chips, core[None])
 
-        fillers = Fillers(down_stage, gate_stage, up_stage, mixed_stage)
+        fillers = Fillers(late, down_stage, gate_stage, up_stage, mixed_stage)
         normed_two_grad = ring_sum(same, cross, fillers)
         gate_sent, up_sent, mixed_rows = late["gate"], late["up"], late["mixed"]
         down_got = late["down"]
@@ -1236,15 +1244,15 @@
         jnp.zeros((column_total,), FULL), part, side * local_width, 0
     )
 
-    def share(part):
-        return own_half(part), swap_tensor(other_half(part).astype(LOW)), gain_part(part)
+    def back_shares(*grads):
+        part = back_all(*grads)
+        return own_half(part), other_half(part).astype(LOW), gain_part(part)
 
     def input_side(own, other):
         unused_one, norm_one_back = jax.vjp(
             lambda values: rms_norm(values, gain_one), own_half(tokens_f)
         )
-        input_half = state_half + norm_one_back(own + other.astype(FULL))[0]
-        return input_half, swap_tensor(input_half)
+        return state_half + norm_one_back(own + other.astype(FULL))[0]
 
     def gain_part(part):
         return jnp.sum(part * rms_norm(tokens_f, 1.0), axis=0)
@@ -1262,8 +1270,6 @@
 
     if ring:
         pre_got = swap_bit(pre_sent, "dp", 0)
-        normed_own, normed_other, gain_one_grad = share(back_all(*pre_grads))
-        pre_got, normed_own = together(pre_got, normed_own)
         w_blocks, *far = weight_grads(
             chips,
             core[None],
@@ -1275,32 +1281,40 @@
             context_got,
         )
         w_blocks, mixed, *far = together(w_blocks, mixed, *far)
-        up_third, up_last = cut_rows(lower(up_sent), 2)
-        up_third = swap_tensor(after(up_third, far[0]))
-        late = {}
+        up_pieces = swap_in_turn(cut_rows(lower(up_sent), 2), far[0])
+        late, later = {}, {}
+
+        def normed_stage(gated):
+            late["own"], late["sent"], late["gain"] = back_shares(*map(gated, pre_grads))
+
+        def gate_product_stage(gated):
+            other = swap_tensor(late["sent"])
+            late["gate"] = grad_sum(gated(expert_in), g0, gate_got)
+            late["mixed"], late["pieces"] = gated(mixed), up_pieces
+            later["other"] = other
 
         def input_stage(gated):
-            late["input"] = input_side(normed_own, gated(normed_other))
-            late["up"] = swap_tensor(after(up_last, late["input"][0]))
+            later["mixed"] = swap_tensor(late["mixed"])
+            late["half"] = input_side(late["own"], gated(later["other"]))
+            later["half"] = swap_tensor(late["half"])
             late["down"] = grad_sum(gated(h0), back_rows, down_got)
-
-        def expert_stage(gated):
-            late["gate"] = grad_sum(gated(expert_in), g0, gate_got)
-            late["mixed"] = swap_tensor(gated(mixed))
-
-        def gain_stage(gated):
-            late["gains"] = gain_side(gated(gain_one_grad))
-
-        fillers = Fillers(input_stage, expert_stage, gain_stage)
-        w_parts, token = ring_weights(w_blocks, *far, fillers)
-        input_half, input_other = late["input"]
+            late["gains"] = gain_side(gated(late["gain"]))
+
+        def up_product_stage(gated):
+            up_got = jnp.concatenate([soon[1], *late["pieces"]], axis=0)
+            late["up"] = grad_sum(gated(expert_in), u0, up_got)
+            late["mixed_other"] = later["mixed"]
+
+        fillers = Fillers(
+            late, normed_stage, gate_product_stage, input_stage, up_product_stage
+        )
+        w_parts = ring_weights(w_blocks, *far, fillers)
+        input_half, input_other = late["half"], later["half"]
         gain_sums = late["gains"]
-        down_grad, gate_w_grad = late["down"], late["gate"]
-        up_got = jnp.concatenate([soon[1], up_third, late["up"]], axis=0)
-        up_w_grad = grad_sum(after(expert_in, token), u0, up_got)
+        down_grad, gate_w_grad, up_w_grad = late["down"], late["gate"], late["up"]
         own_w, sent_w = sum_weights(core[None], *w_parts)
         w_sums = place_weights(core[None], own_w, swap_bit(sent_w, "dp", 0))
-        mixed_other = late["mixed"]
+        mixed_other = late["mixed_other"]
     else:
         w_grads = jnp.concatenate(
             [low_tn(normed_b, g) for g in pre_grads] + [low_tn(attn_grad_b, context_b)], axis=1
@@ -1313,9 +1327,10 @@
         up_got = jnp.concatenate([soon[1], swap_tensor(lower(up_sent))], axis=0)
         up_w_grad = grad_sum(expert_in, u0, up_got)
         mixed_other = swap_tensor(mixed)
-        *normed_parts, gain_one_grad = share(back_all(*pre_grads))
+        normed_own, normed_sent, gain_one_grad = back_shares(*pre_grads)
         gain_sums = gain_side(gain_one_grad)
-        input_half, input_other = input_side(*normed_parts)
+        input_half = input_side(normed_own, swap_tensor(normed_sent))
+        input_other = swap_tensor(input_half)
     input_grad = join_halves(side[None], [input_half], [input_other])
     output = join_halves(side[None], [hidden_state, mixed], [hidden_other, mixed_other])
     return (

time: 692 us -> 695 us (level)
  waiting for transfers between devices: 241 us -> 229 us
    ppermute x12, waiting for transfers between devices: 56.9 us -> 17.1 us  [behind(): return lax.ppermute(block, 'dp', BEHIND)]
    ppermute x12, waiting for transfers between devices: 3.29 us -> 27.5 us  [ahead(): return lax.ppermute(block, 'dp', AHEAD)]
  transfers between devices with their start and end apart: 88 -> 88, of which waited for: 28 -> 30; matrix products, arithmetic and copies ran while one was open for 17% -> 18% of each run, Pallas kernels for 32% -> 32%
where the time goes in v13:
time: 695 us; the launch traced here: 688 us
  waiting for transfers between devices  229 us (33%)
  Pallas kernels  225 us (32%)
  starting transfers between devices  67.5 us (10%)
  matrix products  59.4 us (9%)
  other arithmetic  46.1 us (7%)
  local copies, waits for them, and re-layouts  35.5 us (5%)
  between operations  15.3 us (2%)
  blocking collectives  10 us (1%)
    ppermute x19, waiting for transfers between devices, swap_tensor(): return lax.ppermute(block, 'tensor', [(0, 1), (1, 0)])  104 us
    pallas_call x5, Pallas kernels, expert_chunk(): pl.pallas_call(lambda *refs: chunk_kernel(len(pieces), len(held), at, spl...  92.2 us
    ppermute x41, waiting for transfers between devices, swap_bit(): return lax.ppermute(block, axis, [(i, i ^ 1 << bit) for i in range(count)])  79.6 us
    dot_general x6, matrix products, dot_tn(): lax.dot_general(left, right, (((0,), (0,)), ((), ())), preferred_element_...  59.3 us
    ppermute x12, waiting for transfers between devices, ahead(): return lax.ppermute(block, 'dp', AHEAD)  27.5 us
    ppermute x19, starting transfers between devices, swap_tensor(): return lax.ppermute(block, 'tensor', [(0, 1), (1, 0)])  23.4 us
    pallas_call x1, Pallas kernels, attend_back(): pl.pallas_call(attend_back_kernel, grid=(width // HEAD // PAIR,), in_spec...  19.8 us
    pallas_call x1, Pallas kernels, mixed_pass(): pl.pallas_call(mixed_kernel, grid_spec=pltpu.PrefetchScalarGridSpec(num_s...  17.8 us
  transfers between devices with their start and end apart: 88, of which 30 were waited for; matrix products, arithmetic and copies ran while one was open for 18% of the time, Pallas kernels for 32%

profile of v13, /device:TPU:0, one launch (start us, length us, event | category | flops | bytes accessed | tf_op | source)
XLA Modules:
  0.0 688.1 jit_solution(15106452388637227840)
XLA Ops:
  10.1 2.4 shard_map.309
  12.7 2.3 dynamic-slice_convert_fusion.2
  15.1 3.0 collective-permute-start
  22.0 42.7 %collective-permute-done.refs_5_.refs_7_.refs_9_ = bf16[2048,512]{1,0:T(8,128)(2,1)} collective-permute-done((bf16[2048,512]{1,0:T(8,128)(2,1)S(1)}, bf16[2048,512]{1,0:T(8,128)(2,1)}, u32[]{:S(2)}, u32[]{:S(2)}) %collective-permute-start) | collective-permute-done | bytes 2097184 | tf_op jit(solution)/shard_map/ppermute | solution.py:26
  64.7 44.1 %collective-permute-done.1.refs_7_.refs_9_.refs_11_ = bf16[2048,512]{1,0:T(8,128)(2,1)} collective-permute-done((bf16[2048,512]{1,0:T(8,128)(2,1)}, bf16[2048,512]{1,0:T(8,128)(2,1)}, u32[]{:S(2)}, u32[]{:S(2)}) %collective-permute-start.1) | collective-permute-done | bytes 2097184 | tf_op jit(solution)/shard_map/ppermute | solution.py:26
  111.9 9.0 %shard_map.310 = (f32[320,1024]{1,0:T(8,128)}, f32[320,1024]{1,0:T(8,128)}, bf16[320,1024]{1,0:T(8,128)(2,1)}, bf16[128,1024]{1,0:T(8,128)(2,1)}) custom-call(bf16[320,2048]{1,0:T(8,128)(2,1)} %multiply_convert_fusion.refs_0_, bf16[16,528,1024]{2,1,0:T(8,128)(2,1)} %bitcast.93), custom_call_target="tpu_custom_call" | custom-call | flops 4026531840 | bytes 15204352 | tf_op jit(solution)/shard_map/pallas_call | solution.py:512
  124.1 5.1 all-reduce.3
  132.3 2.7 shard_map.311
  138.6 9.3 %collective-permute-done.5.refs_3_ = bf16[128,1024]{1,0:T(8,128)(2,1)} collective-permute-done((bf16[128,1024]{1,0:T(8,128)(2,1)}, bf16[128,1024]{1,0:T(8,128)(2,1)}, u32[]{:S(2)}, u32[]{:S(2)}) %collective-permute-start.5) | collective-permute-done | bytes 262176 | tf_op jit(solution)/shard_map/ppermute | solution.py:22
  152.0 6.0 collective-permute-done.12.refs_10_
  158.2 5.4 collective-permute-done.7.refs_5_
  164.2 18.1 %collective-permute-done.14.refs_12_ = bf16[128,1024]{1,0:T(8,128)(2,1)} collective-permute-done((bf16[128,1024]{1,0:T(8,128)(2,1)}, bf16[128,1024]{1,0:T(8,128)(2,1)}, u32[]{:S(2)}, u32[]{:S(2)}) %collective-permute-start.14) | collective-permute-done | bytes 262176 | tf_op jit(solution)/shard_map/ppermute | solution.py:22
  184.5 11.9 %shard_map.312.refs_0_.refs_8_ = bf16[320,1024]{1,0:T(8,128)(2,1)} custom-call(f32[320,1024]{1,0:T(8,128)} %get-tuple-element.200.flat_ref.refs_0_, f32[1,1024]{1,0:T(1,128)} %bitcast.129, f32[320,1]{1,0:T(8,128)} %broadcast_in_dim.145.scale_ref.refs_3_, f32[320,128]{1,0:T(8,128)} %get-tuple-element.202.cos_ref.refs_5_, ...), custom_call_target="tpu_custom_call" | custom-call | tf_op jit(solution)/shard_map/pallas_call | solution.py:279
  196.4 4.6 shard_map.313
  204.1 1.8 convert_element_type.294
  207.4 8.8 %shard_map.314.refs_3_.refs_5_.refs_7_ = bf16[2560,2048]{1,0:T(8,128)(2,1)} custom-call(s32[16]{0:T(128)} %get-tuple-element.399.refs_0_, bf16[16,160,2048]{2,1,0:T(8,128)(2,1)} %bitcast.121), custom_call_target="tpu_custom_call" | custom-call | tf_op jit(solution)/shard_map/pallas_call | solution.py:462
  216.2 3.4 collective-permute-done.17
  219.6 2.0 multiply_reduce_fusion.6
  221.9 2.1 collective-permute-done.18.refs_2_
  224.0 2.0 collective-permute-start.20
  230.3 13.7 %shard_map.315 = (bf16[160,2048]{1,0:T(8,128)(2,1)}, bf16[160,2048]{1,0:T(8,128)(2,1)}, bf16[2560,2048]{1,0:T(8,128)(2,1)}, bf16[2560,512]{1,0:T(8,128)(2,1)}, b...) custom-call(f32[2560,1]{1,0:T(8,128)} %copy.91.refs_0_, ...), custom_call_target="tpu_custom_call" | custom-call | flops 6710886400 | bytes 19791872 | tf_op jit(solution)/shard_map/pallas_call | solution.py:888
  245.0 2.2 collective-permute-start.23
  248.0 13.7 %shard_map.316 = (bf16[320,2048]{1,0:T(8,128)(2,1)}, bf16[2560,2048]{1,0:T(8,128)(2,1)}, bf16[2560,512]{1,0:T(8,128)(2,1)}, bf16[2560,512]{1,0:T(8,128)(2,1)}, b...) custom-call(f32[2560,1]{1,0:T(8,128)} %copy.91.refs_0_, ...), custom_call_target="tpu_custom_call", output_to_operand_aliasing={{1}: (10, {}), {2}: (11, {}), {3}: (12, {}), {4}: (13, {}),... | custom-call | flops 6710886400 | bytes 19791872 | tf_op jit(solution)/shard_map/pallas_call | solution.py:888
  266.5 21.5 %shard_map.317 = (bf16[320,2048]{1,0:T(8,128)(2,1)}, bf16[320,2048]{1,0:T(8,128)(2,1)}, bf16[2560,2048]{1,0:T(8,128)(2,1)}, bf16[2560,512]{1,0:T(8,128)(2,1)}, b...) custom-call(f32[2560,1]{1,0:T(8,128)} %copy.91.refs_0_, ...), custom_call_target="tpu_custom_call", output_to_operand_aliasing={{2}: (12, {}), {3}: (13, {}), {4}: (14, {}), {5}: (15, {}),... | custom-call | flops 13421772800 | bytes 27000832 | tf_op jit(solution)/shard_map/pallas_call | solution.py:888
  293.3 21.7 %shard_map.318 = (bf16[320,2048]{1,0:T(8,128)(2,1)}, bf16[320,2048]{1,0:T(8,128)(2,1)}, bf16[2560,2048]{1,0:T(8,128)(2,1)}, bf16[2560,512]{1,0:T(8,128)(2,1)}, b...) custom-call(f32[2560,1]{1,0:T(8,128)} %copy.91.refs_0_, ...), custom_call_target="tpu_custom_call", output_to_operand_aliasing={{2}: (12, {}), {3}: (13, {}), {4}: (14, {}), {5}: (15, {}),... | custom-call | flops 13421772800 | bytes 27000832 | tf_op jit(solution)/shard_map/pallas_call | solution.py:888
  318.0 21.6 %shard_map.319 = (bf16[160,2048]{1,0:T(8,128)(2,1)}, bf16[160,2048]{1,0:T(8,128)(2,1)}, bf16[320,2048]{1,0:T(8,128)(2,1)}, bf16[2560,2048]{1,0:T(8,128)(2,1)}, b...) custom-call(f32[2560,1]{1,0:T(8,128)} %copy.91.refs_0_, ...), custom_call_target="tpu_custom_call", output_to_operand_aliasing={{3}: (14, {}), {4}: (15, {}), {5}: (16, {}), {6}: (17, {}),... | custom-call | flops 13421772800 | bytes 27000832 | tf_op jit(solution)/shard_map/pallas_call | solution.py:888
  345.4 11.2 %convolution_convert_fusion.2 = bf16[512,2048]{1,0:T(8,128)(2,1)} fusion(bf16[2560,512]{1,0:T(8,128)(2,1)S(1)} %copy-done.4, bf16[2560,2048]{1,0:T(8,128)(2,1)} %shard_map.314.refs_3_.refs_5_.refs_7_), kind=kOutput, calls=%fused_computation.6 | convolution fusion | flops 5369757696 | bytes 15204352 | tf_op jit(solution)/shard_map/dot_general | solution.py:157
  361.6 5.8 convolution_convert_fusion.1
  368.3 7.1 %collective-permute-done.49 = bf16[160,2048]{1,0:T(8,128)(2,1)S(1)} collective-permute-done((bf16[160,2048]{1,0:T(8,128)(2,1)S(1)}, bf16[160,2048]{1,0:T(8,128)(2,1)S(1)}, u32[]{:S(2)}, u32[]{:S(2)}) %collective-permute-start.49) | collective-permute-done | bytes 655392 | tf_op jit(solution)/shard_map/ppermute | solution.py:49
  379.0 6.8 convolution_convert_fusion
  385.8 6.0 collective-permute-done.50
  395.6 17.8 %shard_map.320 = bf16[8,2,160,2048]{3,2,1,0:T(8,128)(2,1)} custom-call(s32[8]{0:T(128)} %compare_select_fusion.6.chip_ref, s32[8]{0:T(128)} %constant.190.clone.same_ref, s32[8]{0:T(128)} %constant.191.clone.cross_ref, s32[1]{0:T(128)} %bitcast.16.core_ref, bf16[2560,512]{1,0:T(8,128)(2,1)} %get-tuple-element.352.refs_0_.refs_1_, ...), custom_call_target="tpu_custom_call" | custom-call | flops 10737418240 | bytes 19922944 | tf_op jit(solution)/shard_map/pallas_call | solution.py:940
  414.2 1.9 convert_add_fusion.7
  420.5 13.4 %collective-permute-done.54 = bf16[160,2048]{1,0:T(8,128)(2,1)S(1)} collective-permute-done((bf16[160,2048]{1,0:T(8,128)(2,1)S(1)}, bf16[160,2048]{1,0:T(8,128)(2,1)S(1)}, u32[]{:S(2)}, u32[]{:S(2)}) %collective-permute-start.54) | collective-permute-done | bytes 655392 | tf_op jit(solution)/shard_map/ppermute | solution.py:26
  436.3 6.2 shard_map.321.refs_14_
  443.9 19.8 %shard_map.322 = (f32[320,1024]{1,0:T(8,128)}, f32[320,1]{1,0:T(8,128)}, f32[1,1024]{1,0:T(1,128)}, f32[320,1024]{1,0:T(8,128)}, f32[320,1024]{1,0:T(8,128)}, /*...) custom-call(f32[320,1024]{1,0:T(8,128)} %get-tuple-element.200.flat_, ...), custom_call_target="tpu_custom_call" | custom-call | flops 20000000000 | bytes 40000000 | tf_op jit(solution)/shard_map/pallas_call | solution.py:338
  469.1 3.1 shard_map.323
  474.3 2.3 slice.179
  477.6 1.9 slice.177
  479.4 24.3 %collective-permute-done.66.refs_9_ = bf16[2,128,1024]{2,1,0:T(8,128)(2,1)S(1)} collective-permute-done((bf16[2,128,1024]{2,1,0:T(8,128)(2,1)}, bf16[2,128,1024]{2,1,0:T(8,128)(2,1)S(1)}, u32[]{:S(2)}, u32[]{:S(2)}) %collective-permute-start.66) | collective-permute-done | bytes 524320 | tf_op jit(solution)/shard_map/ppermute | solution.py:22
  507.1 7.5 %collective-permute-done.68.refs_11_ = bf16[128,1024]{1,0:T(8,128)(2,1)S(1)} collective-permute-done((bf16[128,1024]{1,0:T(8,128)(2,1)S(1)}, bf16[128,1024]{1,0:T(8,128)(2,1)S(1)}, u32[]{:S(2)}, u32[]{:S(2)}) %collective-permute-start.68) | collective-permute-done | bytes 262176 | tf_op jit(solution)/shard_map/ppermute | solution.py:22
  515.8 5.3 shard_map.324
  522.4 4.9 psum.23
  529.0 4.8 shard_map.325
  537.7 14.2 %shard_map.326 = (bf16[8,256,2048]{2,1,0:T(8,128)(2,1)}, bf16[256,1024]{1,0:T(8,128)(2,1)}, bf16[256,1024]{1,0:T(8,128)(2,1)}) custom-call(s32[8]{0:T(128)} %compare_select_fusion.6.chip_ref, s32[1]{0:T(128)} %bitcast.16.core_ref, bf16[320,2048]{1,0:T(8,128)(2,1)} %multiply_convert_fusion.refs_0_, bf16[320,2048]{1,0:T(8,128)(2,1)} %collective-permute-done.56.refs_1_, ...), custom_call_target="tpu_custom_call" | custom-call | flops 5368709120 | bytes 16252928 | tf_op jit(solution)/shard_map/pallas_call | solution.py:634
  551.9 2.0 collective-permute-start.70
  557.3 9.4 %shard_map.327 = f32[320,2048]{1,0:T(8,128)} custom-call(bf16[320,1024]{1,0:T(8,128)(2,1)} %get-tuple-element.334.refs_4_.refs_0_, bf16[320,1024]{1,0:T(8,128)(2,1)} %get-tuple-element.335.refs_5_.refs_1_, bf16[320,1024]{1,0:T(8,128)(2,1)} %get-tuple-element.336.refs_10_.refs_6_.refs_2_, bf16[16,528,1024]{2,1,0:T(8,128)(2,1)} %bitcast.97, ...), custom_call_target="tpu_custom_call" | custom-call | flops 4026531840 | bytes 15204352 | tf_op jit(solution)/shard_map/pallas_call | solution.py:551
  566.7 2.3 multiply_reduce_fusion
  573.0 2.0 collective-permute-start.72
  576.5 11.9 %convert_add_fusion.2 = f32[2048,512]{1,0:T(8,128)} fusion(bf16[2560,2048]{1,0:T(8,128)(2,1)} %get-tuple-element.366, bf16[2560,512]{1,0:T(8,128)(2,1)S(1)} %copy-done.5, bf16[512,512]{1,0:T(8,128)(2,1)} %collective-permute-done.59, bf16[1024,512]{1,0:T(8,128)(2,1)} %collective-permute-done.58, bf16[512,512]{1,0:T(8,128)(2,1)} %collective-permute-done.53), kind=kOutput, calls=%fused_computation.3 | convolution fusion | flops 5376049152 | bytes 19398656 | tf_op jit(solution)/shard_map/dot_general | solution.py:157
  588.5 8.6 %collective-permute-done.72 = bf16[256,2048]{1,0:T(8,128)(2,1)S(1)} collective-permute-done((bf16[256,2048]{1,0:T(8,128)(2,1)S(1)}, bf16[256,2048]{1,0:T(8,128)(2,1)S(1)}, u32[]{:S(2)}, u32[]{:S(2)}) %collective-permute-start.72) | collective-permute-done | bytes 1048608 | tf_op jit(solution)/shard_map/ppermute | solution.py:45
  597.1 2.1 collective-permute-done.73
  600.9 3.9 all-to-all-start
  604.9 4.5 fusion.1
  615.9 11.7 %convert_add_fusion.1 = f32[512,2048]{1,0:T(8,128)} fusion(bf16[512,2048]{1,0:T(8,128)(2,1)} %collective-permute-done.52, bf16[2560,512]{1,0:T(8,128)(2,1)S(1)} %copy-done.3, bf16[2560,2048]{1,0:T(8,128)(2,1)} %shard_map.314.refs_3_.refs_5_.refs_7_), kind=kOutput, calls=%fused_computation.2 | convolution fusion | flops 5370806272 | bytes 19398656 | tf_op jit(solution)/shard_map/dot_general | solution.py:157
  627.6 7.4 %collective-permute-done.76 = bf16[256,2048]{1,0:T(8,128)(2,1)} collective-permute-done((bf16[256,2048]{1,0:T(8,128)(2,1)}, bf16[256,2048]{1,0:T(8,128)(2,1)}, u32[]{:S(2)}, u32[]{:S(2)}) %collective-permute-start.76) | collective-permute-done | bytes 1048608 | tf_op jit(solution)/shard_map/ppermute | solution.py:45
  636.4 3.1 fusion
  641.6 11.9 %convert_add_fusion = f32[2048,512]{1,0:T(8,128)} fusion(bf16[2560,2048]{1,0:T(8,128)(2,1)} %get-tuple-element.366, bf16[2560,512]{1,0:T(8,128)(2,1)S(1)} %copy-done.7, bf16[512,512]{1,0:T(8,128)(2,1)S(1)} %copy-done.70, bf16[512,512]{1,0:T(8,128)(2,1)} %collective-permute-done.74, bf16[1024,512]{1,0:T(8,128)(2,1)} %collective-permute-done.60), kind=kOutput, calls=%fused_computation.1 | convolution fusion | flops 5376049152 | bytes 19398656 | tf_op jit(solution)/shard_map/dot_general | solution.py:157
  653.5 10.2 %collective-permute-done.79.right_ref = bf16[256,2048]{1,0:T(8,128)(2,1)S(1)} collective-permute-done((bf16[256,2048]{1,0:T(8,128)(2,1)S(1)}, bf16[256,2048]{1,0:T(8,128)(2,1)S(1)}, u32[]{:S(2)}, u32[]{:S(2)}) %collective-permute-start.79) | collective-permute-done | bytes 1048608 | tf_op jit(solution)/shard_map/ppermute | solution.py:45
  665.0 3.4 shard_map.330
  668.4 2.3 pad_maximum_fusion.1.refs_3_
  672.2 2.9 shard_map.329
  675.1 3.2 shard_map.328
  678.3 3.0 shard_map.331
  (410 shorter events, 121.5 us)
Async XLA Ops:
  7.2 101.6 %all-gather.5.cloned.1.call-start = ((), (), s32[]{:S(2)}) async-start(), calls=%async_computation.3 | async-start | bytes 18382848 | tf_op jit(solution)/shard_map/all_gather | solution.py:1059
  12.6 194.7 %all-gather.7.cloned.1.call-start = ((), (), s32[]{:S(2)}) async-start(), calls=%async_computation.4 | async-start | bytes 11141120 | tf_op jit(solution)/shard_map/all_gather | solution.py:1061
  15.0 536.9 %reduce-scatter.2.cloned.1.call-start = ((), (), s32[]{:S(2)}) async-start(), calls=%async_computation.2 | async-start | bytes 11141120 | tf_op jit(solution)/shard_map/reduce_scatter | solution.py:1190
  15.1 49.6 %collective-permute-start = (bf16[2048,512]{1,0:T(8,128)(2,1)S(1)}, bf16[2048,512]{1,0:T(8,128)(2,1)}, u32[]{:S(2)}, u32[]{:S(2)}) collective-permute-start(bf16[2048,512]{1,0:T(8,128)(2,1)S(1)} %bitcast.107), channel_id=1, source_target_pairs={{0,1},{1,0},{2,3},{3,2},{4,5},{5,4},{6,7},{7,6},{8,9},{9,8},{10,11... | collective-permute-start | bytes 6291464 | tf_op jit(solution)/shard_map/ppermute | solution.py:26
  18.1 90.7 %collective-permute-start.1 = (bf16[2048,512]{1,0:T(8,128)(2,1)}, bf16[2048,512]{1,0:T(8,128)(2,1)}, u32[]{:S(2)}, u32[]{:S(2)}) collective-permute-start(bf16[2048,512]{1,0:T(8,128)(2,1)} %bitcast.108), channel_id=1, source_target_pairs={{0,1},{1,0},{2,3},{3,2},{4,5},{5,4},{6,7},{7,6},{8,9},{9,8},{10,11... | collective-permute-start | bytes 6291464 | tf_op jit(solution)/shard_map/ppermute | solution.py:26
  129.2 71.8 %collective-permute-start.16 = (bf16[512,2048]{1,0:T(8,128)(2,1)S(1)}, bf16[512,2048]{1,0:T(8,128)(2,1)}, u32[]{:S(2)}, u32[]{:S(2)}) collective-permute-start(bf16[512,2048]{1,0:T(8,128)(2,1)S(1)} %bitcast.120), channel_id=1, source_target_pairs={{0,1},{1,0},{2,3},{3,2},{4,5},{5,4},{6,7},{7,6},{8,9},{9,8},{10,11... | collective-permute-start | bytes 6291464 | tf_op jit(solution)/shard_map/ppermute | solution.py:26
  158.0 24.4 %collective-permute-start.14 = (bf16[128,1024]{1,0:T(8,128)(2,1)}, bf16[128,1024]{1,0:T(8,128)(2,1)}, u32[]{:S(2)}, u32[]{:S(2)}) collective-permute-start(bf16[128,1024]{1,0:T(8,128)(2,1)} %collective-permute-done.10.refs_8_), channel_id=1, source_target_pairs={{0,8},{2,10},{4,12},{6,14},{8,0},{10,2},{12,4},{14,6},{16,24},{18,... | collective-permute-start | bytes 786440 | tf_op jit(solution)/shard_map/ppermute | solution.py:22
  163.6 20.9 %collective-permute-start.11 = (bf16[128,1024]{1,0:T(8,128)(2,1)}, bf16[128,1024]{1,0:T(8,128)(2,1)}, u32[]{:S(2)}, u32[]{:S(2)}) collective-permute-start(bf16[128,1024]{1,0:T(8,128)(2,1)} %collective-permute-done.10.refs_8_), channel_id=1, source_target_pairs={{0,2},{2,0},{4,6},{6,4},{8,10},{10,8},{12,14},{14,12},{16,18},{18,... | collective-permute-start | bytes 786440 | tf_op jit(solution)/shard_map/ppermute | solution.py:22
  163.6 20.9 %collective-permute-start.13 = (bf16[128,1024]{1,0:T(8,128)(2,1)}, bf16[128,1024]{1,0:T(8,128)(2,1)}, u32[]{:S(2)}, u32[]{:S(2)}) collective-permute-start(bf16[128,1024]{1,0:T(8,128)(2,1)} %collective-permute-done.12.refs_10_), channel_id=1, source_target_pairs={{0,2},{2,0},{4,6},{6,4},{8,10},{10,8},{12,14},{14,12},{16,18},{18,... | collective-permute-start | bytes 786440 | tf_op jit(solution)/shard_map/ppermute | solution.py:22
  164.2 20.3 %collective-permute-start.8 = (bf16[128,1024]{1,0:T(8,128)(2,1)}, bf16[128,1024]{1,0:T(8,128)(2,1)}, u32[]{:S(2)}, u32[]{:S(2)}) collective-permute-start(bf16[128,1024]{1,0:T(8,128)(2,1)} %collective-permute-done.7.refs_5_), channel_id=1, source_target_pairs={{0,2},{2,0},{4,6},{6,4},{8,10},{10,8},{12,14},{14,12},{16,18},{18,... | collective-permute-start | bytes 786440 | tf_op jit(solution)/shard_map/ppermute | solution.py:22
  202.4 17.2 %collective-permute-start.17 = (bf16[160,2048]{1,0:T(8,128)(2,1)S(1)}, bf16[160,2048]{1,0:T(8,128)(2,1)S(1)}, u32[]{:S(2)}, u32[]{:S(2)}) collective-permute-start(bf16[160,2048]{1,0:T(8,128)(2,1)S(1)} %dynamic-slice_convert_fusion.1), channel_id=1, source_target_pairs={{0,1},{1,0},{2,3},{3,2},{4,5},{5,4},{6,7},{7,6},{8,9},{9,8},{10,11... | collective-permute-start | bytes 1966088 | tf_op jit(solution)/shard_map/ppermute | solution.py:26
  224.0 20.1 %collective-permute-start.19 = (bf16[160,2048]{1,0:T(8,128)(2,1)S(1)}, bf16[160,2048]{1,0:T(8,128)(2,1)}, u32[]{:S(2)}, u32[]{:S(2)}) collective-permute-start(bf16[160,2048]{1,0:T(8,128)(2,1)S(1)} %multiply_convert_fusion.1.refs_1_), channel_id=1, source_target_pairs={{0,8},{2,10},{8,16},{10,18},{16,24},{18,26},{24,28},{26,30},{28,20... | collective-permute-start | bytes 1966088 | tf_op jit(solution)/shard_map/ppermute | solution.py:45
  224.0 20.1 %collective-permute-start.20 = (bf16[160,2048]{1,0:T(8,128)(2,1)S(1)}, bf16[160,2048]{1,0:T(8,128)(2,1)S(1)}, u32[]{:S(2)}, u32[]{:S(2)}) collective-permute-start(bf16[160,2048]{1,0:T(8,128)(2,1)S(1)} %multiply_convert_fusion.1.refs_1_), channel_id=1, source_target_pairs={{8,0},{10,2},{16,8},{18,10},{24,16},{26,18},{28,24},{30,26},{20,28... | collective-permute-start | bytes 1966088 | tf_op jit(solution)/shard_map/ppermute | solution.py:49
  228.6 19.1 %collective-permute-start.24 = (f32[40,2048]{1,0:T(8,128)}, f32[40,2048]{1,0:T(8,128)S(1)}, u32[]{:S(2)}, u32[]{:S(2)}) collective-permute-start(f32[40,2048]{1,0:T(8,128)} %get-tuple-element.229), channel_id=1, source_target_pairs={{0,1},{1,0},{2,3},{3,2},{4,5},{5,4},{6,7},{7,6},{8,9},{9,8},{10,11... | collective-permute-start | bytes 983048 | tf_op jit(solution)/shard_map/ppermute | solution.py:26
  245.0 16.7 %collective-permute-start.22 = (bf16[160,2048]{1,0:T(8,128)(2,1)}, bf16[160,2048]{1,0:T(8,128)(2,1)}, u32[]{:S(2)}, u32[]{:S(2)}) collective-permute-start(bf16[160,2048]{1,0:T(8,128)(2,1)} %collective-permute-done.19.refs_1_), channel_id=1, source_target_pairs={{0,8},{2,10},{8,16},{10,18},{16,24},{18,26},{24,28},{26,30},{28,20... | collective-permute-start | bytes 1966088 | tf_op jit(solution)/shard_map/ppermute | solution.py:45
  245.0 16.7 %collective-permute-start.23 = (bf16[160,2048]{1,0:T(8,128)(2,1)}, bf16[160,2048]{1,0:T(8,128)(2,1)S(1)}, u32[]{:S(2)}, u32[]{:S(2)}) collective-permute-start(bf16[160,2048]{1,0:T(8,128)(2,1)} %copy-done.39), channel_id=1, source_target_pairs={{8,0},{10,2},{16,8},{18,10},{24,16},{26,18},{28,24},{30,26},{20,28... | collective-permute-start | bytes 1966088 | tf_op jit(solution)/shard_map/ppermute | solution.py:49
  247.2 17.4 %collective-permute-start.26 = (bf16[160,2048]{1,0:T(8,128)(2,1)}, bf16[160,2048]{1,0:T(8,128)(2,1)}, u32[]{:S(2)}, u32[]{:S(2)}) collective-permute-start(bf16[160,2048]{1,0:T(8,128)(2,1)} %collective-permute-done.19.refs_1_), channel_id=1, source_target_pairs={{0,2},{2,0},{4,6},{6,4},{8,10},{10,8},{12,14},{14,12},{16,18},{18,... | collective-permute-start | bytes 1966088 | tf_op jit(solution)/shard_map/ppermute | solution.py:22
  247.2 17.6 %collective-permute-start.27 = (bf16[160,2048]{1,0:T(8,128)(2,1)}, bf16[160,2048]{1,0:T(8,128)(2,1)}, u32[]{:S(2)}, u32[]{:S(2)}) collective-permute-start(bf16[160,2048]{1,0:T(8,128)(2,1)} %copy-done.39), channel_id=1, source_target_pairs={{0,2},{2,0},{4,6},{6,4},{8,10},{10,8},{12,14},{14,12},{16,18},{18,... | collective-permute-start | bytes 1966088 | tf_op jit(solution)/shard_map/ppermute | solution.py:22
  247.7 15.2 %collective-permute-start.25 = (f32[40,2048]{1,0:T(8,128)}, f32[40,2048]{1,0:T(8,128)S(1)}, u32[]{:S(2)}, u32[]{:S(2)}) collective-permute-start(f32[40,2048]{1,0:T(8,128)} %get-tuple-element.241), channel_id=1, source_target_pairs={{0,1},{1,0},{2,3},{3,2},{4,5},{5,4},{6,7},{7,6},{8,9},{9,8},{10,11... | collective-permute-start | bytes 983048 | tf_op jit(solution)/shard_map/ppermute | solution.py:26
  261.7 26.3 %collective-permute-start.29 = (bf16[160,2048]{1,0:T(8,128)(2,1)}, bf16[160,2048]{1,0:T(8,128)(2,1)S(1)}, u32[]{:S(2)}, u32[]{:S(2)}) collective-permute-start(bf16[160,2048]{1,0:T(8,128)(2,1)} %collective-permute-done.22.refs_1_), channel_id=1, source_target_pairs={{0,8},{2,10},{8,16},{10,18},{16,24},{18,26},{24,28},{26,30},{28,20... | collective-permute-start | bytes 1966088 | tf_op jit(solution)/shard_map/ppermute | solution.py:45
  262.9 28.0 %collective-permute-start.32 = (bf16[160,2048]{1,0:T(8,128)(2,1)}, bf16[160,2048]{1,0:T(8,128)(2,1)}, u32[]{:S(2)}, u32[]{:S(2)}) collective-permute-start(bf16[160,2048]{1,0:T(8,128)(2,1)} %collective-permute-done.22.refs_1_), channel_id=1, source_target_pairs={{0,2},{2,0},{4,6},{6,4},{8,10},{10,8},{12,14},{14,12},{16,18},{18,... | collective-permute-start | bytes 1966088 | tf_op jit(solution)/shard_map/ppermute | solution.py:22
  263.6 24.4 %collective-permute-start.30 = (bf16[160,2048]{1,0:T(8,128)(2,1)S(1)}, bf16[160,2048]{1,0:T(8,128)(2,1)S(1)}, u32[]{:S(2)}, u32[]{:S(2)}) collective-permute-start(bf16[160,2048]{1,0:T(8,128)(2,1)S(1)} %collective-permute-done.23.refs_2_), channel_id=1, source_target_pairs={{8,0},{10,2},{16,8},{18,10},{24,16},{26,18},{28,24},{30,26},{20,28... | collective-permute-start | bytes 1966088 | tf_op jit(solution)/shard_map/ppermute | solution.py:49
  264.6 26.9 %collective-permute-start.33 = (bf16[160,2048]{1,0:T(8,128)(2,1)S(1)}, bf16[160,2048]{1,0:T(8,128)(2,1)}, u32[]{:S(2)}, u32[]{:S(2)}) collective-permute-start(bf16[160,2048]{1,0:T(8,128)(2,1)S(1)} %collective-permute-done.23.refs_2_), channel_id=1, source_target_pairs={{0,2},{2,0},{4,6},{6,4},{8,10},{10,8},{12,14},{14,12},{16,18},{18,... | collective-permute-start | bytes 1966088 | tf_op jit(solution)/shard_map/ppermute | solution.py:22
  264.8 25.3 %collective-permute-start.31 = (f32[40,2048]{1,0:T(8,128)}, f32[40,2048]{1,0:T(8,128)S(1)}, u32[]{:S(2)}, u32[]{:S(2)}) collective-permute-start(f32[40,2048]{1,0:T(8,128)} %get-tuple-element.255), channel_id=1, source_target_pairs={{0,1},{1,0},{2,3},{3,2},{4,5},{5,4},{6,7},{7,6},{8,9},{9,8},{10,11... | collective-permute-start | bytes 983048 | tf_op jit(solution)/shard_map/ppermute | solution.py:26
  288.8 28.4 %collective-permute-start.40 = (bf16[160,2048]{1,0:T(8,128)(2,1)S(1)}, bf16[160,2048]{1,0:T(8,128)(2,1)}, u32[]{:S(2)}, u32[]{:S(2)}) collective-permute-start(bf16[160,2048]{1,0:T(8,128)(2,1)S(1)} %collective-permute-done.29.refs_1_), channel_id=1, source_target_pairs={{0,2},{2,0},{4,6},{6,4},{8,10},{10,8},{12,14},{14,12},{16,18},{18,... | collective-permute-start | bytes 1966088 | tf_op jit(solution)/shard_map/ppermute | solution.py:22
  289.6 27.6 %collective-permute-start.41 = (bf16[160,2048]{1,0:T(8,128)(2,1)S(1)}, bf16[160,2048]{1,0:T(8,128)(2,1)}, u32[]{:S(2)}, u32[]{:S(2)}) collective-permute-start(bf16[160,2048]{1,0:T(8,128)(2,1)S(1)} %collective-permute-done.30.refs_2_), channel_id=1, source_target_pairs={{0,2},{2,0},{4,6},{6,4},{8,10},{10,8},{12,14},{14,12},{16,18},{18,... | collective-permute-start | bytes 1966088 | tf_op jit(solution)/shard_map/ppermute | solution.py:22
  290.1 24.9 %collective-permute-start.37 = (f32[40,2048]{1,0:T(8,128)}, f32[40,2048]{1,0:T(8,128)}, u32[]{:S(2)}, u32[]{:S(2)}) collective-permute-start(f32[40,2048]{1,0:T(8,128)} %get-tuple-element.266), channel_id=1, source_target_pairs={{0,1},{1,0},{2,3},{3,2},{4,5},{5,4},{6,7},{7,6},{8,9},{9,8},{10,11... | collective-permute-start | bytes 983048 | tf_op jit(solution)/shard_map/ppermute | solution.py:26
  290.8 24.2 %collective-permute-start.35 = (bf16[80,2048]{1,0:T(8,128)(2,1)}, bf16[80,2048]{1,0:T(8,128)(2,1)S(1)}, u32[]{:S(2)}, u32[]{:S(2)}) collective-permute-start(bf16[80,2048]{1,0:T(8,128)(2,1)} %slice.165), channel_id=1, source_target_pairs={{0,8},{2,10},{8,16},{10,18},{16,24},{18,26},{24,28},{26,30},{28,20... | collective-permute-start | bytes 983048 | tf_op jit(solution)/shard_map/ppermute | solution.py:45
  291.5 23.5 %collective-permute-start.36 = (bf16[80,2048]{1,0:T(8,128)(2,1)}, bf16[80,2048]{1,0:T(8,128)(2,1)S(1)}, u32[]{:S(2)}, u32[]{:S(2)}) collective-permute-start(bf16[80,2048]{1,0:T(8,128)(2,1)} %slice.166), channel_id=1, source_target_pairs={{8,0},{10,2},{16,8},{18,10},{24,16},{26,18},{28,24},{30,26},{20,28... | collective-permute-start | bytes 983048 | tf_op jit(solution)/shard_map/ppermute | solution.py:49
  315.6 25.6 %collective-permute-start.28 = (bf16[320,2048]{1,0:T(8,128)(2,1)}, bf16[320,2048]{1,0:T(8,128)(2,1)}, u32[]{:S(2)}, u32[]{:S(2)}) collective-permute-start(bf16[320,2048]{1,0:T(8,128)(2,1)} %get-tuple-element.251), channel_id=1, source_target_pairs={{0,2},{2,0},{4,6},{6,4},{8,10},{10,8},{12,14},{14,12},{16,18},{18,... | collective-permute-start | bytes 3932168 | tf_op jit(solution)/shard_map/ppermute | solution.py:22
  340.3 73.0 %collective-permute-start.21 = (bf16[160,2048]{1,0:T(8,128)(2,1)}, bf16[160,2048]{1,0:T(8,128)(2,1)}, u32[]{:S(2)}, u32[]{:S(2)}) collective-permute-start(bf16[160,2048]{1,0:T(8,128)(2,1)} %get-tuple-element.226), channel_id=1, source_target_pairs={{0,2},{2,0},{4,6},{6,4},{8,10},{10,8},{12,14},{14,12},{16,18},{18,... | collective-permute-start | bytes 1966088 | tf_op jit(solution)/shard_map/ppermute | solution.py:22
  340.7 15.9 %collective-permute-start.34 = (bf16[320,2048]{1,0:T(8,128)(2,1)}, bf16[320,2048]{1,0:T(8,128)(2,1)S(1)}, u32[]{:S(2)}, u32[]{:S(2)}) collective-permute-start(bf16[320,2048]{1,0:T(8,128)(2,1)} %get-tuple-element.265), channel_id=1, source_target_pairs={{0,2},{2,0},{4,6},{6,4},{8,10},{10,8},{12,14},{14,12},{16,18},{18,... | collective-permute-start | bytes 3932168 | tf_op jit(solution)/shard_map/ppermute | solution.py:22
  340.8 17.7 %collective-permute-start.42 = (bf16[320,2048]{1,0:T(8,128)(2,1)}, bf16[320,2048]{1,0:T(8,128)(2,1)S(1)}, u32[]{:S(2)}, u32[]{:S(2)}) collective-permute-start(bf16[320,2048]{1,0:T(8,128)(2,1)} %get-tuple-element.278), channel_id=1, source_target_pairs={{0,2},{2,0},{4,6},{6,4},{8,10},{10,8},{12,14},{14,12},{16,18},{18,... | collective-permute-start | bytes 3932168 | tf_op jit(solution)/shard_map/ppermute | solution.py:22
  343.3 15.8 %collective-permute-start.44 = (bf16[80,2048]{1,0:T(8,128)(2,1)S(1)}, bf16[80,2048]{1,0:T(8,128)(2,1)S(1)}, u32[]{:S(2)}, u32[]{:S(2)}) collective-permute-start(bf16[80,2048]{1,0:T(8,128)(2,1)S(1)} %get-tuple-element.422), channel_id=1, source_target_pairs={{0,8},{2,10},{8,16},{10,18},{16,24},{18,26},{24,28},{26,30},{28,20... | collective-permute-start | bytes 983048 | tf_op jit(solution)/shard_map/ppermute | solution.py:45
  344.0 14.5 %collective-permute-start.48 = (bf16[80,2048]{1,0:T(8,128)(2,1)S(1)}, bf16[80,2048]{1,0:T(8,128)(2,1)S(1)}, u32[]{:S(2)}, u32[]{:S(2)}) collective-permute-start(bf16[80,2048]{1,0:T(8,128)(2,1)S(1)} %get-tuple-element.423), channel_id=1, source_target_pairs={{8,0},{10,2},{16,8},{18,10},{24,16},{26,18},{28,24},{30,26},{20,28... | collective-permute-start | bytes 983048 | tf_op jit(solution)/shard_map/ppermute | solution.py:49
  356.6 59.5 %collective-permute-start.52 = (bf16[512,2048]{1,0:T(8,128)(2,1)}, bf16[512,2048]{1,0:T(8,128)(2,1)}, u32[]{:S(2)}, u32[]{:S(2)}) collective-permute-start(bf16[512,2048]{1,0:T(8,128)(2,1)} %convolution_convert_fusion.2), channel_id=1, source_target_pairs={{0,1},{1,0},{2,3},{3,2},{4,5},{5,4},{6,7},{7,6},{8,9},{9,8},{10,11... | collective-permute-start | bytes 6291464 | tf_op jit(solution)/shard_map/ppermute | solution.py:26
  359.4 16.0 %collective-permute-start.49 = (bf16[160,2048]{1,0:T(8,128)(2,1)S(1)}, bf16[160,2048]{1,0:T(8,128)(2,1)S(1)}, u32[]{:S(2)}, u32[]{:S(2)}) collective-permute-start(bf16[160,2048]{1,0:T(8,128)(2,1)S(1)} %pad_maximum_fusion.5), channel_id=1, source_target_pairs={{8,0},{10,2},{16,8},{18,10},{24,16},{26,18},{28,24},{30,26},{20,28... | collective-permute-start | bytes 1966088 | tf_op jit(solution)/shard_map/ppermute | solution.py:49
  360.6 15.7 %collective-permute-start.45 = (bf16[160,2048]{1,0:T(8,128)(2,1)S(1)}, bf16[160,2048]{1,0:T(8,128)(2,1)S(1)}, u32[]{:S(2)}, u32[]{:S(2)}) collective-permute-start(bf16[160,2048]{1,0:T(8,128)(2,1)S(1)} %pad_maximum_fusion.4), channel_id=1, source_target_pairs={{0,8},{2,10},{8,16},{10,18},{16,24},{18,26},{24,28},{26,30},{28,20... | collective-permute-start | bytes 1966088 | tf_op jit(solution)/shard_map/ppermute | solution.py:45
  367.5 48.6 %collective-permute-start.53 = (bf16[512,512]{1,0:T(8,128)(2,1)S(1)}, bf16[512,512]{1,0:T(8,128)(2,1)}, u32[]{:S(2)}, u32[]{:S(2)}) collective-permute-start(bf16[512,512]{1,0:T(8,128)(2,1)S(1)} %slice.218), channel_id=1, source_target_pairs={{0,1},{1,0},{2,3},{3,2},{4,5},{5,4},{6,7},{7,6},{8,9},{9,8},{10,11... | collective-permute-start | bytes 1572872 | tf_op jit(solution)/shard_map/ppermute | solution.py:26
  376.9 14.9 %collective-permute-start.50 = (bf16[160,2048]{1,0:T(8,128)(2,1)S(1)}, bf16[160,2048]{1,0:T(8,128)(2,1)S(1)}, u32[]{:S(2)}, u32[]{:S(2)}) collective-permute-start(bf16[160,2048]{1,0:T(8,128)(2,1)S(1)} %get-tuple-element.413), channel_id=1, source_target_pairs={{8,0},{10,2},{16,8},{18,10},{24,16},{26,18},{28,24},{30,26},{20,28... | collective-permute-start | bytes 1966088 | tf_op jit(solution)/shard_map/ppermute | solution.py:49
  377.4 14.7 %collective-permute-start.46 = (bf16[160,2048]{1,0:T(8,128)(2,1)S(1)}, bf16[160,2048]{1,0:T(8,128)(2,1)S(1)}, u32[]{:S(2)}, u32[]{:S(2)}) collective-permute-start(bf16[160,2048]{1,0:T(8,128)(2,1)S(1)} %get-tuple-element.412), channel_id=1, source_target_pairs={{0,8},{2,10},{8,16},{10,18},{16,24},{18,26},{24,28},{26,30},{28,20... | collective-permute-start | bytes 1966088 | tf_op jit(solution)/shard_map/ppermute | solution.py:45
  393.5 19.8 %collective-permute-start.47 = (bf16[160,2048]{1,0:T(8,128)(2,1)}, bf16[160,2048]{1,0:T(8,128)(2,1)S(1)}, u32[]{:S(2)}, u32[]{:S(2)}) collective-permute-start(bf16[160,2048]{1,0:T(8,128)(2,1)} %get-tuple-element.410), channel_id=1, source_target_pairs={{0,8},{2,10},{8,16},{10,18},{16,24},{18,26},{24,28},{26,30},{28,20... | collective-permute-start | bytes 1966088 | tf_op jit(solution)/shard_map/ppermute | solution.py:45
  394.9 19.3 %collective-permute-start.51 = (bf16[160,2048]{1,0:T(8,128)(2,1)S(1)}, bf16[160,2048]{1,0:T(8,128)(2,1)}, u32[]{:S(2)}, u32[]{:S(2)}) collective-permute-start(bf16[160,2048]{1,0:T(8,128)(2,1)S(1)} %get-tuple-element.411), channel_id=1, source_target_pairs={{8,0},{10,2},{16,8},{18,10},{24,16},{26,18},{28,24},{30,26},{20,28... | collective-permute-start | bytes 1966088 | tf_op jit(solution)/shard_map/ppermute | solution.py:49
  419.4 14.5 %collective-permute-start.54 = (bf16[160,2048]{1,0:T(8,128)(2,1)S(1)}, bf16[160,2048]{1,0:T(8,128)(2,1)S(1)}, u32[]{:S(2)}, u32[]{:S(2)}) collective-permute-start(bf16[160,2048]{1,0:T(8,128)(2,1)S(1)} %get-tuple-element.394), channel_id=1, source_target_pairs={{0,1},{1,0},{2,3},{3,2},{4,5},{5,4},{6,7},{7,6},{8,9},{9,8},{10,11... | collective-permute-start | bytes 1966088 | tf_op jit(solution)/shard_map/ppermute | solution.py:26
  442.5 30.6 %collective-permute-start.58 = (bf16[1024,512]{1,0:T(8,128)(2,1)}, bf16[1024,512]{1,0:T(8,128)(2,1)}, u32[]{:S(2)}, u32[]{:S(2)}) collective-permute-start(bf16[1024,512]{1,0:T(8,128)(2,1)} %slice.178), channel_id=1, source_target_pairs={{0,1},{1,0},{2,3},{3,2},{4,5},{5,4},{6,7},{7,6},{8,9},{9,8},{10,11... | collective-permute-start | bytes 3145736 | tf_op jit(solution)/shard_map/ppermute | solution.py:26
  464.4 41.1 %collective-permute-start.56 = (bf16[320,2048]{1,0:T(8,128)(2,1)S(1)}, bf16[320,2048]{1,0:T(8,128)(2,1)}, u32[]{:S(2)}, u32[]{:S(2)}) collective-permute-start(bf16[320,2048]{1,0:T(8,128)(2,1)S(1)} %copy-done.14), channel_id=1, source_target_pairs={{0,2},{2,0},{4,6},{6,4},{8,10},{10,8},{12,14},{14,12},{16,18},{18,... | collective-permute-start | bytes 3932168 | tf_op jit(solution)/shard_map/ppermute | solution.py:22
  466.1 41.0 %collective-permute-start.57 = (bf16[320,2048]{1,0:T(8,128)(2,1)S(1)}, bf16[320,2048]{1,0:T(8,128)(2,1)}, u32[]{:S(2)}, u32[]{:S(2)}) collective-permute-start(bf16[320,2048]{1,0:T(8,128)(2,1)S(1)} %copy-done.13), channel_id=1, source_target_pairs={{0,2},{2,0},{4,6},{6,4},{8,10},{10,8},{12,14},{14,12},{16,18},{18,... | collective-permute-start | bytes 3932168 | tf_op jit(solution)/shard_map/ppermute | solution.py:22
  472.2 31.5 %collective-permute-start.66 = (bf16[2,128,1024]{2,1,0:T(8,128)(2,1)}, bf16[2,128,1024]{2,1,0:T(8,128)(2,1)S(1)}, u32[]{:S(2)}, u32[]{:S(2)}) collective-permute-start(bf16[2,128,1024]{2,1,0:T(8,128)(2,1)} %get-tuple-element.312), channel_id=1, source_target_pairs={{0,8},{2,10},{4,12},{6,14},{8,0},{10,2},{12,4},{14,6},{16,24},{18,... | collective-permute-start | bytes 1572872 | tf_op jit(solution)/shard_map/ppermute | solution.py:22
  473.1 30.9 %collective-permute-start.65 = (bf16[2,128,1024]{2,1,0:T(8,128)(2,1)}, bf16[2,128,1024]{2,1,0:T(8,128)(2,1)S(1)}, u32[]{:S(2)}, u32[]{:S(2)}) collective-permute-start(bf16[2,128,1024]{2,1,0:T(8,128)(2,1)} %get-tuple-element.311), channel_id=1, source_target_pairs={{0,4},{2,6},{4,0},{6,2},{8,12},{10,14},{12,8},{14,10},{16,20},{18,... | collective-permute-start | bytes 1572872 | tf_op jit(solution)/shard_map/ppermute | solution.py:22
  476.6 45.6 %collective-permute-start.60 = (bf16[1024,512]{1,0:T(8,128)(2,1)}, bf16[1024,512]{1,0:T(8,128)(2,1)}, u32[]{:S(2)}, u32[]{:S(2)}) collective-permute-start(bf16[1024,512]{1,0:T(8,128)(2,1)} %slice.179), channel_id=1, source_target_pairs={{0,1},{1,0},{2,3},{3,2},{4,5},{5,4},{6,7},{7,6},{8,9},{9,8},{10,11... | collective-permute-start | bytes 3145736 | tf_op jit(solution)/shard_map/ppermute | solution.py:26
  504.0 18.3 %collective-permute-start.59 = (bf16[512,512]{1,0:T(8,128)(2,1)}, bf16[512,512]{1,0:T(8,128)(2,1)}, u32[]{:S(2)}, u32[]{:S(2)}) collective-permute-start(bf16[512,512]{1,0:T(8,128)(2,1)} %slice.177), channel_id=1, source_target_pairs={{0,1},{1,0},{2,3},{3,2},{4,5},{5,4},{6,7},{7,6},{8,9},{9,8},{10,11... | collective-permute-start | bytes 1572872 | tf_op jit(solution)/shard_map/ppermute | solution.py:26
  551.9 17.6 %collective-permute-start.70 = (bf16[256,1024]{1,0:T(8,128)(2,1)}, bf16[256,1024]{1,0:T(8,128)(2,1)}, u32[]{:S(2)}, u32[]{:S(2)}) collective-permute-start(bf16[256,1024]{1,0:T(8,128)(2,1)} %get-tuple-element.332), channel_id=1, source_target_pairs={{0,8},{2,10},{8,16},{10,18},{16,24},{18,26},{24,28},{26,30},{28,20... | collective-permute-start | bytes 1572872 | tf_op jit(solution)/shard_map/ppermute | solution.py:45
  553.9 17.0 %collective-permute-start.74 = (bf16[512,512]{1,0:T(8,128)(2,1)}, bf16[512,512]{1,0:T(8,128)(2,1)}, u32[]{:S(2)}, u32[]{:S(2)}) collective-permute-start(bf16[512,512]{1,0:T(8,128)(2,1)} %get-tuple-element.346), channel_id=1, source_target_pairs={{0,1},{1,0},{2,3},{3,2},{4,5},{5,4},{6,7},{7,6},{8,9},{9,8},{10,11... | collective-permute-start | bytes 1572872 | tf_op jit(solution)/shard_map/ppermute | solution.py:26
  570.9 17.5 %collective-permute-start.75 = (bf16[512,512]{1,0:T(8,128)(2,1)S(1)}, bf16[512,512]{1,0:T(8,128)(2,1)S(1)}, u32[]{:S(2)}, u32[]{:S(2)}) collective-permute-start(bf16[512,512]{1,0:T(8,128)(2,1)S(1)} %copy-done.40), channel_id=1, source_target_pairs={{0,1},{1,0},{2,3},{3,2},{4,5},{5,4},{6,7},{7,6},{8,9},{9,8},{10,11... | collective-permute-start | bytes 1572872 | tf_op jit(solution)/shard_map/ppermute | solution.py:26
  573.0 24.1 %collective-permute-start.72 = (bf16[256,2048]{1,0:T(8,128)(2,1)S(1)}, bf16[256,2048]{1,0:T(8,128)(2,1)S(1)}, u32[]{:S(2)}, u32[]{:S(2)}) collective-permute-start(bf16[256,2048]{1,0:T(8,128)(2,1)S(1)} %pad_maximum_fusion.2), channel_id=1, source_target_pairs={{0,8},{2,10},{8,16},{10,18},{16,24},{18,26},{24,28},{26,30},{28,20... | collective-permute-start | bytes 3145736 | tf_op jit(solution)/shard_map/ppermute | solution.py:45
  575.0 24.1 %collective-permute-start.73 = (bf16[256,2048]{1,0:T(8,128)(2,1)S(1)}, bf16[256,2048]{1,0:T(8,128)(2,1)S(1)}, u32[]{:S(2)}, u32[]{:S(2)}) collective-permute-start(bf16[256,2048]{1,0:T(8,128)(2,1)S(1)} %pad_maximum_fusion.3), channel_id=1, source_target_pairs={{8,0},{10,2},{16,8},{18,10},{24,16},{26,18},{28,24},{30,26},{20,28... | collective-permute-start | bytes 3145736 | tf_op jit(solution)/shard_map/ppermute | solution.py:49
  575.1 24.1 %collective-permute-start.78 = (bf16[160,2048]{1,0:T(8,128)(2,1)S(1)}, bf16[160,2048]{1,0:T(8,128)(2,1)S(1)}, u32[]{:S(2)}, u32[]{:S(2)}) collective-permute-start(bf16[160,2048]{1,0:T(8,128)(2,1)S(1)} %dynamic-slice_convert_fusion), channel_id=1, source_target_pairs={{0,1},{1,0},{2,3},{3,2},{4,5},{5,4},{6,7},{7,6},{8,9},{9,8},{10,11... | collective-permute-start | bytes 1966088 | tf_op jit(solution)/shard_map/ppermute | solution.py:26
  600.9 26.6 %all-to-all-start = ((f32[32,1,512]{2,1,0:T(1,128)}), f32[32,1,512]{2,1,0:T(1,128)S(1)}, u32[]{:S(2)}, u32[]{:S(2)}) async-start(f32[32,1,512]{2,1,0:T(1,128)} %all_to_all.6), calls=%async_computation.1 | async-start | bytes 131072 | tf_op jit(solution)/shard_map/all_to_all | solution.py:1268
  609.4 25.6 %collective-permute-start.76 = (bf16[256,2048]{1,0:T(8,128)(2,1)}, bf16[256,2048]{1,0:T(8,128)(2,1)}, u32[]{:S(2)}, u32[]{:S(2)}) collective-permute-start(bf16[256,2048]{1,0:T(8,128)(2,1)} %get-tuple-element.350), channel_id=1, source_target_pairs={{0,8},{2,10},{8,16},{10,18},{16,24},{18,26},{24,28},{26,30},{28,20... | collective-permute-start | bytes 3145736 | tf_op jit(solution)/shard_map/ppermute | solution.py:45
  611.2 25.2 %collective-permute-start.77 = (bf16[256,2048]{1,0:T(8,128)(2,1)}, bf16[256,2048]{1,0:T(8,128)(2,1)}, u32[]{:S(2)}, u32[]{:S(2)}) collective-permute-start(bf16[256,2048]{1,0:T(8,128)(2,1)} %get-tuple-element.351), channel_id=1, source_target_pairs={{8,0},{10,2},{16,8},{18,10},{24,16},{26,18},{28,24},{30,26},{20,28... | collective-permute-start | bytes 3145736 | tf_op jit(solution)/shard_map/ppermute | solution.py:49
  611.4 42.1 %collective-permute-start.81 = (bf16[160,2048]{1,0:T(8,128)(2,1)}, bf16[160,2048]{1,0:T(8,128)(2,1)}, u32[]{:S(2)}, u32[]{:S(2)}) collective-permute-start(bf16[160,2048]{1,0:T(8,128)(2,1)} %reduce-scatter.2.cloned.1.call-done.refs_2_), channel_id=1, source_target_pairs={{0,1},{1,0},{2,3},{3,2},{4,5},{5,4},{6,7},{7,6},{8,9},{9,8},{10,11... | collective-permute-start | bytes 1966088 | tf_op jit(solution)/shard_map/ppermute | solution.py:26
  614.1 57.0 %collective-permute-start.82 = (f32[160,2048]{1,0:T(8,128)S(1)}, f32[160,2048]{1,0:T(8,128)S(1)}, u32[]{:S(2)}, u32[]{:S(2)}) collective-permute-start(f32[160,2048]{1,0:T(8,128)S(1)} %fusion.5.refs_1_), channel_id=1, source_target_pairs={{0,1},{1,0},{2,3},{3,2},{4,5},{5,4},{6,7},{7,6},{8,9},{9,8},{10,11... | collective-permute-start | bytes 3932168 | tf_op jit(solution)/shard_map/ppermute | solution.py:26
  639.5 24.1 %collective-permute-start.79 = (bf16[256,2048]{1,0:T(8,128)(2,1)S(1)}, bf16[256,2048]{1,0:T(8,128)(2,1)S(1)}, u32[]{:S(2)}, u32[]{:S(2)}) collective-permute-start(bf16[256,2048]{1,0:T(8,128)(2,1)S(1)} %get-tuple-element.363), channel_id=1, source_target_pairs={{0,8},{2,10},{8,16},{10,18},{16,24},{18,26},{24,28},{26,30},{28,20... | collective-permute-start | bytes 3145736 | tf_op jit(solution)/shard_map/ppermute | solution.py:45
  641.1 23.9 %collective-permute-start.80 = (bf16[256,2048]{1,0:T(8,128)(2,1)S(1)}, bf16[256,2048]{1,0:T(8,128)(2,1)}, u32[]{:S(2)}, u32[]{:S(2)}) collective-permute-start(bf16[256,2048]{1,0:T(8,128)(2,1)S(1)} %get-tuple-element.364), channel_id=1, source_target_pairs={{8,0},{10,2},{16,8},{18,10},{24,16},{26,18},{28,24},{30,26},{20,28... | collective-permute-start | bytes 3145736 | tf_op jit(solution)/shard_map/ppermute | solution.py:49
  (99 other events, 1128.9 us)
Sparse Core Ops, SparseCore 0:
  12.7 94.2 all-gather.4
  109.9 97.4 all-gather.6
  416.3 134.2 reduce-scatter.1

commit v14 on v13

--- a/solution.py
+++ b/solution.py
@@ -1246,7 +1246,7 @@
 
     def back_shares(*grads):
         part = back_all(*grads)
-        return own_half(part), other_half(part).astype(LOW), gain_part(part)
+        return own_half(part), other_half(part).astype(LOW), part
 
     def input_side(own, other):
         unused_one, norm_one_back = jax.vjp(
@@ -1298,23 +1298,24 @@
             late["half"] = input_side(late["own"], gated(later["other"]))
             later["half"] = swap_tensor(late["half"])
             late["down"] = grad_sum(gated(h0), back_rows, down_got)
-            late["gains"] = gain_side(gated(late["gain"]))
 
         def up_product_stage(gated):
             up_got = jnp.concatenate([soon[1], *late["pieces"]], axis=0)
             late["up"] = grad_sum(gated(expert_in), u0, up_got)
-            late["mixed_other"] = later["mixed"]
+            late["gains"] = gain_side(gain_part(after(late["gain"], late["up"])))
+            late["output"] = join_halves(
+                side[None], [gated(hidden_state), mixed], [hidden_other, later["mixed"]]
+            )
+            late["input"] = join_halves(side[None], [gated(late["half"])], [later["half"]])
 
         fillers = Fillers(
             late, normed_stage, gate_product_stage, input_stage, up_product_stage
         )
         w_parts = ring_weights(w_blocks, *far, fillers)
-        input_half, input_other = late["half"], later["half"]
-        gain_sums = late["gains"]
+        gain_sums, output, input_grad = late["gains"], late["output"], late["input"]
         down_grad, gate_w_grad, up_w_grad = late["down"], late["gate"], late["up"]
         own_w, sent_w = sum_weights(core[None], *w_parts)
         w_sums = place_weights(core[None], own_w, swap_bit(sent_w, "dp", 0))
-        mixed_other = late["mixed_other"]
     else:
         w_grads = jnp.concatenate(
             [low_tn(normed_b, g) for g in pre_grads] + [low_tn(attn_grad_b, context_b)], axis=1
@@ -1327,12 +1328,12 @@
         up_got = jnp.concatenate([soon[1], swap_tensor(lower(up_sent))], axis=0)
         up_w_grad = grad_sum(expert_in, u0, up_got)
         mixed_other = swap_tensor(mixed)
-        normed_own, normed_sent, gain_one_grad = back_shares(*pre_grads)
-        gain_sums = gain_side(gain_one_grad)
+        normed_own, normed_sent, part = back_shares(*pre_grads)
+        gain_sums = gain_side(gain_part(part))
         input_half = input_side(normed_own, swap_tensor(normed_sent))
         input_other = swap_tensor(input_half)
-    input_grad = join_halves(side[None], [input_half], [input_other])
-    output = join_halves(side[None], [hidden_state, mixed], [hidden_other, mixed_other])
+        input_grad = join_halves(side[None], [input_half], [input_other])
+        output = join_halves(side[None], [hidden_state, mixed], [hidden_other, mixed_other])
     return (
         output,
         input_grad,

time: 695 us -> 686 us (0.987)
    ppermute x12, waiting for transfers between devices: 27.5 us -> 17.8 us  [ahead(): return lax.ppermute(block, 'dp', AHEAD)]
  transfers between devices with their start and end apart: 88 -> 88, of which waited for: 30 -> 29; matrix products, arithmetic and copies ran while one was open for 18% -> 18% of each run, Pallas kernels for 32% -> 32%
where the time goes in v14:
time: 686 us; the launch traced here: 680 us
  Pallas kernels  225 us (33%)
  waiting for transfers between devices  225 us (33%)
  starting transfers between devices  66.3 us (10%)
  matrix products  54.9 us (8%)
  other arithmetic  45.6 us (7%)
  local copies, waits for them, and re-layouts  37.2 us (5%)
  between operations  15.3 us (2%)
  blocking collectives  10 us (1%)
    ppermute x19, waiting for transfers between devices, swap_tensor(): return lax.ppermute(block, 'tensor', [(0, 1), (1, 0)])  104 us
    pallas_call x5, Pallas kernels, expert_chunk(): pl.pallas_call(lambda *refs: chunk_kernel(len(pieces), len(held), at, spl...  92.3 us
    ppermute x41, waiting for transfers between devices, swap_bit(): return lax.ppermute(block, axis, [(i, i ^ 1 << bit) for i in range(count)])  81.9 us
    dot_general x6, matrix products, dot_tn(): lax.dot_general(left, right, (((0,), (0,)), ((), ())), preferred_element_...  54.7 us
    ppermute x19, starting transfers between devices, swap_tensor(): return lax.ppermute(block, 'tensor', [(0, 1), (1, 0)])  23.2 us
    pallas_call x1, Pallas kernels, attend_back(): pl.pallas_call(attend_back_kernel, grid=(width // HEAD // PAIR,), in_spec...  19.8 us
    ppermute x12, waiting for transfers between devices, ahead(): return lax.ppermute(block, 'dp', AHEAD)  17.8 us
    pallas_call x1, Pallas kernels, mixed_pass(): pl.pallas_call(mixed_kernel, grid_spec=pltpu.PrefetchScalarGridSpec(num_s...  17.8 us
  transfers between devices with their start and end apart: 88, of which 29 were waited for; matrix products, arithmetic and copies ran while one was open for 18% of the time, Pallas kernels for 32%

profile of v14, /device:TPU:0, one launch (start us, length us, event | category | flops | bytes accessed | tf_op | source)
XLA Modules:
  0.0 679.6 jit_solution(2502722716052346732)
XLA Ops:
  10.1 2.4 shard_map.309
  12.7 2.3 dynamic-slice_convert_fusion.2
  15.1 3.0 collective-permute-start
  22.0 42.7 %collective-permute-done.refs_5_.refs_7_.refs_9_ = bf16[2048,512]{1,0:T(8,128)(2,1)} collective-permute-done((bf16[2048,512]{1,0:T(8,128)(2,1)S(1)}, bf16[2048,512]{1,0:T(8,128)(2,1)}, u32[]{:S(2)}, u32[]{:S(2)}) %collective-permute-start) | collective-permute-done | bytes 2097184 | tf_op jit(solution)/shard_map/ppermute | solution.py:26
  64.7 44.1 %collective-permute-done.1.refs_7_.refs_9_.refs_11_ = bf16[2048,512]{1,0:T(8,128)(2,1)} collective-permute-done((bf16[2048,512]{1,0:T(8,128)(2,1)}, bf16[2048,512]{1,0:T(8,128)(2,1)}, u32[]{:S(2)}, u32[]{:S(2)}) %collective-permute-start.1) | collective-permute-done | bytes 2097184 | tf_op jit(solution)/shard_map/ppermute | solution.py:26
  111.9 9.0 %shard_map.310 = (f32[320,1024]{1,0:T(8,128)}, f32[320,1024]{1,0:T(8,128)}, bf16[320,1024]{1,0:T(8,128)(2,1)}, bf16[128,1024]{1,0:T(8,128)(2,1)}) custom-call(bf16[320,2048]{1,0:T(8,128)(2,1)} %multiply_convert_fusion.refs_0_, bf16[16,528,1024]{2,1,0:T(8,128)(2,1)} %bitcast.93), custom_call_target="tpu_custom_call" | custom-call | flops 4026531840 | bytes 15204352 | tf_op jit(solution)/shard_map/pallas_call | solution.py:512
  124.1 5.1 all-reduce.3
  132.3 2.7 shard_map.311
  138.6 9.2 %collective-permute-done.5.refs_3_ = bf16[128,1024]{1,0:T(8,128)(2,1)} collective-permute-done((bf16[128,1024]{1,0:T(8,128)(2,1)}, bf16[128,1024]{1,0:T(8,128)(2,1)}, u32[]{:S(2)}, u32[]{:S(2)}) %collective-permute-start.5) | collective-permute-done | bytes 262176 | tf_op jit(solution)/shard_map/ppermute | solution.py:22
  152.0 6.0 collective-permute-done.12.refs_10_
  158.3 5.4 collective-permute-done.7.refs_5_
  164.3 18.1 %collective-permute-done.14.refs_12_ = bf16[128,1024]{1,0:T(8,128)(2,1)} collective-permute-done((bf16[128,1024]{1,0:T(8,128)(2,1)}, bf16[128,1024]{1,0:T(8,128)(2,1)}, u32[]{:S(2)}, u32[]{:S(2)}) %collective-permute-start.14) | collective-permute-done | bytes 262176 | tf_op jit(solution)/shard_map/ppermute | solution.py:22
  184.6 11.9 %shard_map.312.refs_0_.refs_8_ = bf16[320,1024]{1,0:T(8,128)(2,1)} custom-call(f32[320,1024]{1,0:T(8,128)} %get-tuple-element.203.flat_ref.refs_0_, f32[1,1024]{1,0:T(1,128)} %bitcast.135, f32[320,1]{1,0:T(8,128)} %broadcast_in_dim.145.scale_ref.refs_3_, f32[320,128]{1,0:T(8,128)} %get-tuple-element.205.cos_ref.refs_5_, ...), custom_call_target="tpu_custom_call" | custom-call | tf_op jit(solution)/shard_map/pallas_call | solution.py:279
  196.5 4.6 shard_map.313
  207.4 8.8 %shard_map.314.refs_3_.refs_5_.refs_7_ = bf16[2560,2048]{1,0:T(8,128)(2,1)} custom-call(s32[16]{0:T(128)} %get-tuple-element.405.refs_0_, bf16[16,160,2048]{2,1,0:T(8,128)(2,1)} %bitcast.127), custom_call_target="tpu_custom_call" | custom-call | tf_op jit(solution)/shard_map/pallas_call | solution.py:462
  216.2 3.5 collective-permute-done.17
  219.7 2.0 multiply_reduce_fusion.6
  222.0 2.1 collective-permute-done.18.refs_2_
  224.1 2.0 collective-permute-start.20
  230.3 13.7 %shard_map.315 = (bf16[160,2048]{1,0:T(8,128)(2,1)}, bf16[160,2048]{1,0:T(8,128)(2,1)}, bf16[2560,2048]{1,0:T(8,128)(2,1)}, bf16[2560,512]{1,0:T(8,128)(2,1)}, b...) custom-call(f32[2560,1]{1,0:T(8,128)} %copy.91.refs_0_, ...), custom_call_target="tpu_custom_call" | custom-call | flops 6710886400 | bytes 19791872 | tf_op jit(solution)/shard_map/pallas_call | solution.py:888
  245.0 2.2 collective-permute-start.23
  248.1 13.7 %shard_map.316 = (bf16[320,2048]{1,0:T(8,128)(2,1)}, bf16[2560,2048]{1,0:T(8,128)(2,1)}, bf16[2560,512]{1,0:T(8,128)(2,1)}, bf16[2560,512]{1,0:T(8,128)(2,1)}, b...) custom-call(f32[2560,1]{1,0:T(8,128)} %copy.91.refs_0_, ...), custom_call_target="tpu_custom_call", output_to_operand_aliasing={{1}: (10, {}), {2}: (11, {}), {3}: (12, {}), {4}: (13, {}),... | custom-call | flops 6710886400 | bytes 19791872 | tf_op jit(solution)/shard_map/pallas_call | solution.py:888
  266.5 21.5 %shard_map.317 = (bf16[320,2048]{1,0:T(8,128)(2,1)}, bf16[320,2048]{1,0:T(8,128)(2,1)}, bf16[2560,2048]{1,0:T(8,128)(2,1)}, bf16[2560,512]{1,0:T(8,128)(2,1)}, b...) custom-call(f32[2560,1]{1,0:T(8,128)} %copy.91.refs_0_, ...), custom_call_target="tpu_custom_call", output_to_operand_aliasing={{2}: (12, {}), {3}: (13, {}), {4}: (14, {}), {5}: (15, {}),... | custom-call | flops 13421772800 | bytes 27000832 | tf_op jit(solution)/shard_map/pallas_call | solution.py:888
  293.3 21.7 %shard_map.318 = (bf16[320,2048]{1,0:T(8,128)(2,1)}, bf16[320,2048]{1,0:T(8,128)(2,1)}, bf16[2560,2048]{1,0:T(8,128)(2,1)}, bf16[2560,512]{1,0:T(8,128)(2,1)}, b...) custom-call(f32[2560,1]{1,0:T(8,128)} %copy.91.refs_0_, ...), custom_call_target="tpu_custom_call", output_to_operand_aliasing={{2}: (12, {}), {3}: (13, {}), {4}: (14, {}), {5}: (15, {}),... | custom-call | flops 13421772800 | bytes 27000832 | tf_op jit(solution)/shard_map/pallas_call | solution.py:888
  318.0 21.6 %shard_map.319 = (bf16[160,2048]{1,0:T(8,128)(2,1)}, bf16[160,2048]{1,0:T(8,128)(2,1)}, bf16[320,2048]{1,0:T(8,128)(2,1)}, bf16[2560,2048]{1,0:T(8,128)(2,1)}, b...) custom-call(f32[2560,1]{1,0:T(8,128)} %copy.91.refs_0_, ...), custom_call_target="tpu_custom_call", output_to_operand_aliasing={{3}: (14, {}), {4}: (15, {}), {5}: (16, {}), {6}: (17, {}),... | custom-call | flops 13421772800 | bytes 27000832 | tf_op jit(solution)/shard_map/pallas_call | solution.py:888
  345.4 11.2 %convolution_convert_fusion.2 = bf16[512,2048]{1,0:T(8,128)(2,1)} fusion(bf16[2560,512]{1,0:T(8,128)(2,1)S(1)} %copy-done.4, bf16[2560,2048]{1,0:T(8,128)(2,1)} %shard_map.314.refs_3_.refs_5_.refs_7_), kind=kOutput, calls=%fused_computation.6 | convolution fusion | flops 5369757696 | bytes 15204352 | tf_op jit(solution)/shard_map/dot_general | solution.py:157
  361.5 5.8 convolution_convert_fusion.1
  368.2 7.1 %collective-permute-done.49 = bf16[160,2048]{1,0:T(8,128)(2,1)S(1)} collective-permute-done((bf16[160,2048]{1,0:T(8,128)(2,1)S(1)}, bf16[160,2048]{1,0:T(8,128)(2,1)S(1)}, u32[]{:S(2)}, u32[]{:S(2)}) %collective-permute-start.49) | collective-permute-done | bytes 655392 | tf_op jit(solution)/shard_map/ppermute | solution.py:49
  378.9 6.8 %convolution_convert_fusion = bf16[2048,512]{1,0:T(8,128)(2,1)} fusion(bf16[2560,2048]{1,0:T(8,128)(2,1)S(1)} %bitcast.103, bf16[2560,512]{1,0:T(8,128)(2,1)S(1)} %copy-done.8), kind=kOutput, calls=%fused_computation.4 | convolution fusion | flops 5369757696 | bytes 15204352 | tf_op jit(solution)/shard_map/dot_general | solution.py:157
  385.7 6.0 collective-permute-done.50
  395.5 17.8 %shard_map.320 = bf16[8,2,160,2048]{3,2,1,0:T(8,128)(2,1)} custom-call(s32[8]{0:T(128)} %compare_select_fusion.7.chip_ref, s32[8]{0:T(128)} %constant.190.clone.same_ref, s32[8]{0:T(128)} %constant.191.clone.cross_ref, s32[1]{0:T(128)} %bitcast.core_ref, bf16[2560,512]{1,0:T(8,128)(2,1)} %get-tuple-element.351.refs_0_.refs_1_, ...), custom_call_target="tpu_custom_call" | custom-call | flops 10737418240 | bytes 19922944 | tf_op jit(solution)/shard_map/pallas_call | solution.py:940
  414.2 1.9 convert_add_fusion.7
  420.5 13.4 %collective-permute-done.54 = bf16[160,2048]{1,0:T(8,128)(2,1)S(1)} collective-permute-done((bf16[160,2048]{1,0:T(8,128)(2,1)S(1)}, bf16[160,2048]{1,0:T(8,128)(2,1)S(1)}, u32[]{:S(2)}, u32[]{:S(2)}) %collective-permute-start.54) | collective-permute-done | bytes 655392 | tf_op jit(solution)/shard_map/ppermute | solution.py:26
  436.2 6.2 shard_map.321.refs_14_
  443.9 19.8 %shard_map.322 = (f32[320,1024]{1,0:T(8,128)}, f32[320,1]{1,0:T(8,128)}, f32[1,1024]{1,0:T(1,128)}, f32[320,1024]{1,0:T(8,128)}, f32[320,1024]{1,0:T(8,128)}, /*...) custom-call(f32[320,1024]{1,0:T(8,128)} %get-tuple-element.203.flat_, ...), custom_call_target="tpu_custom_call" | custom-call | flops 20000000000 | bytes 40000000 | tf_op jit(solution)/shard_map/pallas_call | solution.py:338
  469.1 3.2 shard_map.323
  474.3 2.3 slice.179
  479.5 24.2 %collective-permute-done.66.refs_9_ = bf16[2,128,1024]{2,1,0:T(8,128)(2,1)S(1)} collective-permute-done((bf16[2,128,1024]{2,1,0:T(8,128)(2,1)}, bf16[2,128,1024]{2,1,0:T(8,128)(2,1)S(1)}, u32[]{:S(2)}, u32[]{:S(2)}) %collective-permute-start.66) | collective-permute-done | bytes 524320 | tf_op jit(solution)/shard_map/ppermute | solution.py:22
  507.0 7.4 %collective-permute-done.68.refs_11_ = bf16[128,1024]{1,0:T(8,128)(2,1)S(1)} collective-permute-done((bf16[128,1024]{1,0:T(8,128)(2,1)S(1)}, bf16[128,1024]{1,0:T(8,128)(2,1)S(1)}, u32[]{:S(2)}, u32[]{:S(2)}) %collective-permute-start.68) | collective-permute-done | bytes 262176 | tf_op jit(solution)/shard_map/ppermute | solution.py:22
  515.8 5.4 shard_map.324
  522.4 4.9 psum.23
  529.0 4.8 shard_map.325
  537.7 14.2 %shard_map.326 = (bf16[8,256,2048]{2,1,0:T(8,128)(2,1)}, bf16[256,1024]{1,0:T(8,128)(2,1)}, bf16[256,1024]{1,0:T(8,128)(2,1)}) custom-call(s32[8]{0:T(128)} %compare_select_fusion.7.chip_ref, s32[1]{0:T(128)} %bitcast.core_ref, bf16[320,2048]{1,0:T(8,128)(2,1)} %multiply_convert_fusion.refs_0_, bf16[320,2048]{1,0:T(8,128)(2,1)} %collective-permute-done.56.refs_1_, ...), custom_call_target="tpu_custom_call" | custom-call | flops 5368709120 | bytes 16252928 | tf_op jit(solution)/shard_map/pallas_call | solution.py:634
  551.9 2.0 collective-permute-start.70
  555.5 2.8 slice_bitcast_fusion
  558.3 9.3 %shard_map.327 = f32[320,2048]{1,0:T(8,128)} custom-call(bf16[320,1024]{1,0:T(8,128)(2,1)} %get-tuple-element.332.refs_4_.refs_0_, bf16[320,1024]{1,0:T(8,128)(2,1)} %get-tuple-element.333.refs_5_.refs_1_, bf16[320,1024]{1,0:T(8,128)(2,1)} %get-tuple-element.334.refs_10_.refs_6_.refs_2_, bf16[16,528,1024]{2,1,0:T(8,128)(2,1)} %bitcast.97, ...), custom_call_target="tpu_custom_call" | custom-call | flops 4026531840 | bytes 15204352 | tf_op jit(solution)/shard_map/pallas_call | solution.py:551
  567.6 2.4 dynamic-slice_convert_fusion
  576.5 2.3 collective-permute-start.72
  580.3 12.1 %convert_add_fusion.2 = f32[2048,512]{1,0:T(8,128)} fusion(bf16[2560,2048]{1,0:T(8,128)(2,1)} %get-tuple-element.361, bf16[2560,512]{1,0:T(8,128)(2,1)S(1)} %copy-done.5, bf16[512,512]{1,0:T(8,128)(2,1)} %collective-permute-done.59, bf16[1024,512]{1,0:T(8,128)(2,1)} %collective-permute-done.58, bf16[512,512]{1,0:T(8,128)(2,1)} %collective-permute-done.53), kind=kOutput, calls=%fused_computation.3 | convolution fusion | flops 5376049152 | bytes 19398656 | tf_op jit(solution)/shard_map/dot_general | solution.py:157
  592.4 8.5 %collective-permute-done.72 = bf16[256,2048]{1,0:T(8,128)(2,1)S(1)} collective-permute-done((bf16[256,2048]{1,0:T(8,128)(2,1)S(1)}, bf16[256,2048]{1,0:T(8,128)(2,1)S(1)}, u32[]{:S(2)}, u32[]{:S(2)}) %collective-permute-start.72) | collective-permute-done | bytes 1048608 | tf_op jit(solution)/shard_map/ppermute | solution.py:45
  600.9 2.4 collective-permute-done.73
  603.3 3.3 fusion.1
  612.6 9.5 %convert_add_fusion.1 = f32[512,2048]{1,0:T(8,128)} fusion(bf16[512,2048]{1,0:T(8,128)(2,1)} %collective-permute-done.52, bf16[2560,512]{1,0:T(8,128)(2,1)S(1)} %copy-done.3, bf16[2560,2048]{1,0:T(8,128)(2,1)S(1)} %bitcast.101), kind=kOutput, calls=%fused_computation.2 | convolution fusion | flops 5370806272 | bytes 19398656 | tf_op jit(solution)/shard_map/dot_general | solution.py:157
  622.1 8.0 %collective-permute-done.76 = bf16[256,2048]{1,0:T(8,128)(2,1)} collective-permute-done((bf16[256,2048]{1,0:T(8,128)(2,1)}, bf16[256,2048]{1,0:T(8,128)(2,1)}, u32[]{:S(2)}, u32[]{:S(2)}) %collective-permute-start.76) | collective-permute-done | bytes 1048608 | tf_op jit(solution)/shard_map/ppermute | solution.py:45
  631.3 3.6 fusion
  637.0 9.3 %convert_add_fusion = f32[2048,512]{1,0:T(8,128)} fusion(bf16[2560,2048]{1,0:T(8,128)(2,1)S(1)} %bitcast.105, bf16[2560,512]{1,0:T(8,128)(2,1)S(1)} %copy-done.7, bf16[512,512]{1,0:T(8,128)(2,1)} %collective-permute-done.75, bf16[512,512]{1,0:T(8,128)(2,1)} %collective-permute-done.74, bf16[1024,512]{1,0:T(8,128)(2,1)} %collective-permute-done.60), kind=kOutput, calls=%fused_computation.1 | convolution fusion | flops 5376049152 | bytes 19398656 | tf_op jit(solution)/shard_map/dot_general | solution.py:157
  647.6 2.8 all-to-all-start
  650.4 2.2 pad_maximum_fusion.1.refs_3_
  652.6 3.2 shard_map.329
  655.9 3.8 all-to-all-done
  659.7 2.9 shard_map.328
  662.6 3.4 shard_map.330
  666.5 2.3 collective-permute-done.83.got_ref
  669.9 3.0 shard_map.331
  (417 shorter events, 123.2 us)
Async XLA Ops:
  7.2 101.6 %all-gather.5.cloned.1.call-start = ((), (), s32[]{:S(2)}) async-start(), calls=%async_computation.3 | async-start | bytes 18382848 | tf_op jit(solution)/shard_map/all_gather | solution.py:1059
  12.6 194.7 %all-gather.7.cloned.1.call-start = ((), (), s32[]{:S(2)}) async-start(), calls=%async_computation.4 | async-start | bytes 11141120 | tf_op jit(solution)/shard_map/all_gather | solution.py:1061
  15.0 536.8 %reduce-scatter.2.cloned.1.call-start = ((), (), s32[]{:S(2)}) async-start(), calls=%async_computation.2 | async-start | bytes 11141120 | tf_op jit(solution)/shard_map/reduce_scatter | solution.py:1190
  15.1 49.6 %collective-permute-start = (bf16[2048,512]{1,0:T(8,128)(2,1)S(1)}, bf16[2048,512]{1,0:T(8,128)(2,1)}, u32[]{:S(2)}, u32[]{:S(2)}) collective-permute-start(bf16[2048,512]{1,0:T(8,128)(2,1)S(1)} %bitcast.111), channel_id=1, source_target_pairs={{0,1},{1,0},{2,3},{3,2},{4,5},{5,4},{6,7},{7,6},{8,9},{9,8},{10,11... | collective-permute-start | bytes 6291464 | tf_op jit(solution)/shard_map/ppermute | solution.py:26
  18.1 90.7 %collective-permute-start.1 = (bf16[2048,512]{1,0:T(8,128)(2,1)}, bf16[2048,512]{1,0:T(8,128)(2,1)}, u32[]{:S(2)}, u32[]{:S(2)}) collective-permute-start(bf16[2048,512]{1,0:T(8,128)(2,1)} %bitcast.112), channel_id=1, source_target_pairs={{0,1},{1,0},{2,3},{3,2},{4,5},{5,4},{6,7},{7,6},{8,9},{9,8},{10,11... | collective-permute-start | bytes 6291464 | tf_op jit(solution)/shard_map/ppermute | solution.py:26
  129.2 71.9 %collective-permute-start.16 = (bf16[512,2048]{1,0:T(8,128)(2,1)S(1)}, bf16[512,2048]{1,0:T(8,128)(2,1)}, u32[]{:S(2)}, u32[]{:S(2)}) collective-permute-start(bf16[512,2048]{1,0:T(8,128)(2,1)S(1)} %bitcast.124), channel_id=1, source_target_pairs={{0,1},{1,0},{2,3},{3,2},{4,5},{5,4},{6,7},{7,6},{8,9},{9,8},{10,11... | collective-permute-start | bytes 6291464 | tf_op jit(solution)/shard_map/ppermute | solution.py:26
  158.0 24.4 %collective-permute-start.14 = (bf16[128,1024]{1,0:T(8,128)(2,1)}, bf16[128,1024]{1,0:T(8,128)(2,1)}, u32[]{:S(2)}, u32[]{:S(2)}) collective-permute-start(bf16[128,1024]{1,0:T(8,128)(2,1)} %collective-permute-done.10.refs_8_), channel_id=1, source_target_pairs={{0,8},{2,10},{4,12},{6,14},{8,0},{10,2},{12,4},{14,6},{16,24},{18,... | collective-permute-start | bytes 786440 | tf_op jit(solution)/shard_map/ppermute | solution.py:22
  163.7 20.9 %collective-permute-start.11 = (bf16[128,1024]{1,0:T(8,128)(2,1)}, bf16[128,1024]{1,0:T(8,128)(2,1)}, u32[]{:S(2)}, u32[]{:S(2)}) collective-permute-start(bf16[128,1024]{1,0:T(8,128)(2,1)} %collective-permute-done.10.refs_8_), channel_id=1, source_target_pairs={{0,2},{2,0},{4,6},{6,4},{8,10},{10,8},{12,14},{14,12},{16,18},{18,... | collective-permute-start | bytes 786440 | tf_op jit(solution)/shard_map/ppermute | solution.py:22
  163.7 20.9 %collective-permute-start.13 = (bf16[128,1024]{1,0:T(8,128)(2,1)}, bf16[128,1024]{1,0:T(8,128)(2,1)}, u32[]{:S(2)}, u32[]{:S(2)}) collective-permute-start(bf16[128,1024]{1,0:T(8,128)(2,1)} %collective-permute-done.12.refs_10_), channel_id=1, source_target_pairs={{0,2},{2,0},{4,6},{6,4},{8,10},{10,8},{12,14},{14,12},{16,18},{18,... | collective-permute-start | bytes 786440 | tf_op jit(solution)/shard_map/ppermute | solution.py:22
  164.2 20.4 %collective-permute-start.8 = (bf16[128,1024]{1,0:T(8,128)(2,1)}, bf16[128,1024]{1,0:T(8,128)(2,1)}, u32[]{:S(2)}, u32[]{:S(2)}) collective-permute-start(bf16[128,1024]{1,0:T(8,128)(2,1)} %collective-permute-done.7.refs_5_), channel_id=1, source_target_pairs={{0,2},{2,0},{4,6},{6,4},{8,10},{10,8},{12,14},{14,12},{16,18},{18,... | collective-permute-start | bytes 786440 | tf_op jit(solution)/shard_map/ppermute | solution.py:22
  202.5 17.2 %collective-permute-start.17 = (bf16[160,2048]{1,0:T(8,128)(2,1)S(1)}, bf16[160,2048]{1,0:T(8,128)(2,1)S(1)}, u32[]{:S(2)}, u32[]{:S(2)}) collective-permute-start(bf16[160,2048]{1,0:T(8,128)(2,1)S(1)} %dynamic-slice_convert_fusion.1), channel_id=1, source_target_pairs={{0,1},{1,0},{2,3},{3,2},{4,5},{5,4},{6,7},{7,6},{8,9},{9,8},{10,11... | collective-permute-start | bytes 1966088 | tf_op jit(solution)/shard_map/ppermute | solution.py:26
  224.1 20.0 %collective-permute-start.19 = (bf16[160,2048]{1,0:T(8,128)(2,1)S(1)}, bf16[160,2048]{1,0:T(8,128)(2,1)}, u32[]{:S(2)}, u32[]{:S(2)}) collective-permute-start(bf16[160,2048]{1,0:T(8,128)(2,1)S(1)} %multiply_convert_fusion.1.refs_1_), channel_id=1, source_target_pairs={{0,8},{2,10},{8,16},{10,18},{16,24},{18,26},{24,28},{26,30},{28,20... | collective-permute-start | bytes 1966088 | tf_op jit(solution)/shard_map/ppermute | solution.py:45
  224.1 20.0 %collective-permute-start.20 = (bf16[160,2048]{1,0:T(8,128)(2,1)S(1)}, bf16[160,2048]{1,0:T(8,128)(2,1)S(1)}, u32[]{:S(2)}, u32[]{:S(2)}) collective-permute-start(bf16[160,2048]{1,0:T(8,128)(2,1)S(1)} %multiply_convert_fusion.1.refs_1_), channel_id=1, source_target_pairs={{8,0},{10,2},{16,8},{18,10},{24,16},{26,18},{28,24},{30,26},{20,28... | collective-permute-start | bytes 1966088 | tf_op jit(solution)/shard_map/ppermute | solution.py:49
  228.7 19.0 %collective-permute-start.24 = (f32[40,2048]{1,0:T(8,128)}, f32[40,2048]{1,0:T(8,128)S(1)}, u32[]{:S(2)}, u32[]{:S(2)}) collective-permute-start(f32[40,2048]{1,0:T(8,128)} %get-tuple-element.232), channel_id=1, source_target_pairs={{0,1},{1,0},{2,3},{3,2},{4,5},{5,4},{6,7},{7,6},{8,9},{9,8},{10,11... | collective-permute-start | bytes 983048 | tf_op jit(solution)/shard_map/ppermute | solution.py:26
  244.9 16.8 %collective-permute-start.22 = (bf16[160,2048]{1,0:T(8,128)(2,1)}, bf16[160,2048]{1,0:T(8,128)(2,1)}, u32[]{:S(2)}, u32[]{:S(2)}) collective-permute-start(bf16[160,2048]{1,0:T(8,128)(2,1)} %collective-permute-done.19.refs_1_), channel_id=1, source_target_pairs={{0,8},{2,10},{8,16},{10,18},{16,24},{18,26},{24,28},{26,30},{28,20... | collective-permute-start | bytes 1966088 | tf_op jit(solution)/shard_map/ppermute | solution.py:45
  245.0 16.9 %collective-permute-start.23 = (bf16[160,2048]{1,0:T(8,128)(2,1)}, bf16[160,2048]{1,0:T(8,128)(2,1)S(1)}, u32[]{:S(2)}, u32[]{:S(2)}) collective-permute-start(bf16[160,2048]{1,0:T(8,128)(2,1)} %copy-done.36), channel_id=1, source_target_pairs={{8,0},{10,2},{16,8},{18,10},{24,16},{26,18},{28,24},{30,26},{20,28... | collective-permute-start | bytes 1966088 | tf_op jit(solution)/shard_map/ppermute | solution.py:49
  247.2 17.5 %collective-permute-start.26 = (bf16[160,2048]{1,0:T(8,128)(2,1)}, bf16[160,2048]{1,0:T(8,128)(2,1)}, u32[]{:S(2)}, u32[]{:S(2)}) collective-permute-start(bf16[160,2048]{1,0:T(8,128)(2,1)} %collective-permute-done.19.refs_1_), channel_id=1, source_target_pairs={{0,2},{2,0},{4,6},{6,4},{8,10},{10,8},{12,14},{14,12},{16,18},{18,... | collective-permute-start | bytes 1966088 | tf_op jit(solution)/shard_map/ppermute | solution.py:22
  247.2 17.7 %collective-permute-start.27 = (bf16[160,2048]{1,0:T(8,128)(2,1)}, bf16[160,2048]{1,0:T(8,128)(2,1)}, u32[]{:S(2)}, u32[]{:S(2)}) collective-permute-start(bf16[160,2048]{1,0:T(8,128)(2,1)} %copy-done.36), channel_id=1, source_target_pairs={{0,2},{2,0},{4,6},{6,4},{8,10},{10,8},{12,14},{14,12},{16,18},{18,... | collective-permute-start | bytes 1966088 | tf_op jit(solution)/shard_map/ppermute | solution.py:22
  247.7 15.1 %collective-permute-start.25 = (f32[40,2048]{1,0:T(8,128)}, f32[40,2048]{1,0:T(8,128)S(1)}, u32[]{:S(2)}, u32[]{:S(2)}) collective-permute-start(f32[40,2048]{1,0:T(8,128)} %get-tuple-element.244), channel_id=1, source_target_pairs={{0,1},{1,0},{2,3},{3,2},{4,5},{5,4},{6,7},{7,6},{8,9},{9,8},{10,11... | collective-permute-start | bytes 983048 | tf_op jit(solution)/shard_map/ppermute | solution.py:26
  261.8 26.2 %collective-permute-start.29 = (bf16[160,2048]{1,0:T(8,128)(2,1)}, bf16[160,2048]{1,0:T(8,128)(2,1)S(1)}, u32[]{:S(2)}, u32[]{:S(2)}) collective-permute-start(bf16[160,2048]{1,0:T(8,128)(2,1)} %collective-permute-done.22.refs_1_), channel_id=1, source_target_pairs={{0,8},{2,10},{8,16},{10,18},{16,24},{18,26},{24,28},{26,30},{28,20... | collective-permute-start | bytes 1966088 | tf_op jit(solution)/shard_map/ppermute | solution.py:45
  262.8 28.1 %collective-permute-start.32 = (bf16[160,2048]{1,0:T(8,128)(2,1)}, bf16[160,2048]{1,0:T(8,128)(2,1)}, u32[]{:S(2)}, u32[]{:S(2)}) collective-permute-start(bf16[160,2048]{1,0:T(8,128)(2,1)} %collective-permute-done.22.refs_1_), channel_id=1, source_target_pairs={{0,2},{2,0},{4,6},{6,4},{8,10},{10,8},{12,14},{14,12},{16,18},{18,... | collective-permute-start | bytes 1966088 | tf_op jit(solution)/shard_map/ppermute | solution.py:22
  263.5 24.5 %collective-permute-start.30 = (bf16[160,2048]{1,0:T(8,128)(2,1)S(1)}, bf16[160,2048]{1,0:T(8,128)(2,1)S(1)}, u32[]{:S(2)}, u32[]{:S(2)}) collective-permute-start(bf16[160,2048]{1,0:T(8,128)(2,1)S(1)} %collective-permute-done.23.refs_2_), channel_id=1, source_target_pairs={{8,0},{10,2},{16,8},{18,10},{24,16},{26,18},{28,24},{30,26},{20,28... | collective-permute-start | bytes 1966088 | tf_op jit(solution)/shard_map/ppermute | solution.py:49
  264.6 26.8 %collective-permute-start.33 = (bf16[160,2048]{1,0:T(8,128)(2,1)S(1)}, bf16[160,2048]{1,0:T(8,128)(2,1)}, u32[]{:S(2)}, u32[]{:S(2)}) collective-permute-start(bf16[160,2048]{1,0:T(8,128)(2,1)S(1)} %collective-permute-done.23.refs_2_), channel_id=1, source_target_pairs={{0,2},{2,0},{4,6},{6,4},{8,10},{10,8},{12,14},{14,12},{16,18},{18,... | collective-permute-start | bytes 1966088 | tf_op jit(solution)/shard_map/ppermute | solution.py:22
  264.9 25.3 %collective-permute-start.31 = (f32[40,2048]{1,0:T(8,128)}, f32[40,2048]{1,0:T(8,128)S(1)}, u32[]{:S(2)}, u32[]{:S(2)}) collective-permute-start(f32[40,2048]{1,0:T(8,128)} %get-tuple-element.258), channel_id=1, source_target_pairs={{0,1},{1,0},{2,3},{3,2},{4,5},{5,4},{6,7},{7,6},{8,9},{9,8},{10,11... | collective-permute-start | bytes 983048 | tf_op jit(solution)/shard_map/ppermute | solution.py:26
  288.8 28.4 %collective-permute-start.40 = (bf16[160,2048]{1,0:T(8,128)(2,1)S(1)}, bf16[160,2048]{1,0:T(8,128)(2,1)}, u32[]{:S(2)}, u32[]{:S(2)}) collective-permute-start(bf16[160,2048]{1,0:T(8,128)(2,1)S(1)} %collective-permute-done.29.refs_1_), channel_id=1, source_target_pairs={{0,2},{2,0},{4,6},{6,4},{8,10},{10,8},{12,14},{14,12},{16,18},{18,... | collective-permute-start | bytes 1966088 | tf_op jit(solution)/shard_map/ppermute | solution.py:22
  289.6 27.6 %collective-permute-start.41 = (bf16[160,2048]{1,0:T(8,128)(2,1)S(1)}, bf16[160,2048]{1,0:T(8,128)(2,1)}, u32[]{:S(2)}, u32[]{:S(2)}) collective-permute-start(bf16[160,2048]{1,0:T(8,128)(2,1)S(1)} %collective-permute-done.30.refs_2_), channel_id=1, source_target_pairs={{0,2},{2,0},{4,6},{6,4},{8,10},{10,8},{12,14},{14,12},{16,18},{18,... | collective-permute-start | bytes 1966088 | tf_op jit(solution)/shard_map/ppermute | solution.py:22
  290.1 24.9 %collective-permute-start.37 = (f32[40,2048]{1,0:T(8,128)}, f32[40,2048]{1,0:T(8,128)}, u32[]{:S(2)}, u32[]{:S(2)}) collective-permute-start(f32[40,2048]{1,0:T(8,128)} %get-tuple-element.269), channel_id=1, source_target_pairs={{0,1},{1,0},{2,3},{3,2},{4,5},{5,4},{6,7},{7,6},{8,9},{9,8},{10,11... | collective-permute-start | bytes 983048 | tf_op jit(solution)/shard_map/ppermute | solution.py:26
  290.8 24.2 %collective-permute-start.35 = (bf16[80,2048]{1,0:T(8,128)(2,1)}, bf16[80,2048]{1,0:T(8,128)(2,1)S(1)}, u32[]{:S(2)}, u32[]{:S(2)}) collective-permute-start(bf16[80,2048]{1,0:T(8,128)(2,1)} %slice.165), channel_id=1, source_target_pairs={{0,8},{2,10},{8,16},{10,18},{16,24},{18,26},{24,28},{26,30},{28,20... | collective-permute-start | bytes 983048 | tf_op jit(solution)/shard_map/ppermute | solution.py:45
  291.4 23.6 %collective-permute-start.36 = (bf16[80,2048]{1,0:T(8,128)(2,1)}, bf16[80,2048]{1,0:T(8,128)(2,1)S(1)}, u32[]{:S(2)}, u32[]{:S(2)}) collective-permute-start(bf16[80,2048]{1,0:T(8,128)(2,1)} %slice.166), channel_id=1, source_target_pairs={{8,0},{10,2},{16,8},{18,10},{24,16},{26,18},{28,24},{30,26},{20,28... | collective-permute-start | bytes 983048 | tf_op jit(solution)/shard_map/ppermute | solution.py:49
  315.6 25.6 %collective-permute-start.28 = (bf16[320,2048]{1,0:T(8,128)(2,1)}, bf16[320,2048]{1,0:T(8,128)(2,1)}, u32[]{:S(2)}, u32[]{:S(2)}) collective-permute-start(bf16[320,2048]{1,0:T(8,128)(2,1)} %get-tuple-element.254), channel_id=1, source_target_pairs={{0,2},{2,0},{4,6},{6,4},{8,10},{10,8},{12,14},{14,12},{16,18},{18,... | collective-permute-start | bytes 3932168 | tf_op jit(solution)/shard_map/ppermute | solution.py:22
  340.3 73.0 %collective-permute-start.21 = (bf16[160,2048]{1,0:T(8,128)(2,1)}, bf16[160,2048]{1,0:T(8,128)(2,1)}, u32[]{:S(2)}, u32[]{:S(2)}) collective-permute-start(bf16[160,2048]{1,0:T(8,128)(2,1)} %get-tuple-element.229), channel_id=1, source_target_pairs={{0,2},{2,0},{4,6},{6,4},{8,10},{10,8},{12,14},{14,12},{16,18},{18,... | collective-permute-start | bytes 1966088 | tf_op jit(solution)/shard_map/ppermute | solution.py:22
  340.7 15.9 %collective-permute-start.34 = (bf16[320,2048]{1,0:T(8,128)(2,1)}, bf16[320,2048]{1,0:T(8,128)(2,1)S(1)}, u32[]{:S(2)}, u32[]{:S(2)}) collective-permute-start(bf16[320,2048]{1,0:T(8,128)(2,1)} %get-tuple-element.268), channel_id=1, source_target_pairs={{0,2},{2,0},{4,6},{6,4},{8,10},{10,8},{12,14},{14,12},{16,18},{18,... | collective-permute-start | bytes 3932168 | tf_op jit(solution)/shard_map/ppermute | solution.py:22
  340.8 17.7 %collective-permute-start.42 = (bf16[320,2048]{1,0:T(8,128)(2,1)}, bf16[320,2048]{1,0:T(8,128)(2,1)S(1)}, u32[]{:S(2)}, u32[]{:S(2)}) collective-permute-start(bf16[320,2048]{1,0:T(8,128)(2,1)} %get-tuple-element.281), channel_id=1, source_target_pairs={{0,2},{2,0},{4,6},{6,4},{8,10},{10,8},{12,14},{14,12},{16,18},{18,... | collective-permute-start | bytes 3932168 | tf_op jit(solution)/shard_map/ppermute | solution.py:22
  343.3 15.8 %collective-permute-start.44 = (bf16[80,2048]{1,0:T(8,128)(2,1)S(1)}, bf16[80,2048]{1,0:T(8,128)(2,1)S(1)}, u32[]{:S(2)}, u32[]{:S(2)}) collective-permute-start(bf16[80,2048]{1,0:T(8,128)(2,1)S(1)} %get-tuple-element.428), channel_id=1, source_target_pairs={{0,8},{2,10},{8,16},{10,18},{16,24},{18,26},{24,28},{26,30},{28,20... | collective-permute-start | bytes 983048 | tf_op jit(solution)/shard_map/ppermute | solution.py:45
  343.9 14.6 %collective-permute-start.48 = (bf16[80,2048]{1,0:T(8,128)(2,1)S(1)}, bf16[80,2048]{1,0:T(8,128)(2,1)S(1)}, u32[]{:S(2)}, u32[]{:S(2)}) collective-permute-start(bf16[80,2048]{1,0:T(8,128)(2,1)S(1)} %get-tuple-element.429), channel_id=1, source_target_pairs={{8,0},{10,2},{16,8},{18,10},{24,16},{26,18},{28,24},{30,26},{20,28... | collective-permute-start | bytes 983048 | tf_op jit(solution)/shard_map/ppermute | solution.py:49
  356.6 59.5 %collective-permute-start.52 = (bf16[512,2048]{1,0:T(8,128)(2,1)}, bf16[512,2048]{1,0:T(8,128)(2,1)}, u32[]{:S(2)}, u32[]{:S(2)}) collective-permute-start(bf16[512,2048]{1,0:T(8,128)(2,1)} %convolution_convert_fusion.2), channel_id=1, source_target_pairs={{0,1},{1,0},{2,3},{3,2},{4,5},{5,4},{6,7},{7,6},{8,9},{9,8},{10,11... | collective-permute-start | bytes 6291464 | tf_op jit(solution)/shard_map/ppermute | solution.py:26
  359.3 16.0 %collective-permute-start.49 = (bf16[160,2048]{1,0:T(8,128)(2,1)S(1)}, bf16[160,2048]{1,0:T(8,128)(2,1)S(1)}, u32[]{:S(2)}, u32[]{:S(2)}) collective-permute-start(bf16[160,2048]{1,0:T(8,128)(2,1)S(1)} %pad_maximum_fusion.5), channel_id=1, source_target_pairs={{8,0},{10,2},{16,8},{18,10},{24,16},{26,18},{28,24},{30,26},{20,28... | collective-permute-start | bytes 1966088 | tf_op jit(solution)/shard_map/ppermute | solution.py:49
  360.6 15.7 %collective-permute-start.45 = (bf16[160,2048]{1,0:T(8,128)(2,1)S(1)}, bf16[160,2048]{1,0:T(8,128)(2,1)S(1)}, u32[]{:S(2)}, u32[]{:S(2)}) collective-permute-start(bf16[160,2048]{1,0:T(8,128)(2,1)S(1)} %pad_maximum_fusion.4), channel_id=1, source_target_pairs={{0,8},{2,10},{8,16},{10,18},{16,24},{18,26},{24,28},{26,30},{28,20... | collective-permute-start | bytes 1966088 | tf_op jit(solution)/shard_map/ppermute | solution.py:45
  367.4 48.6 %collective-permute-start.53 = (bf16[512,512]{1,0:T(8,128)(2,1)S(1)}, bf16[512,512]{1,0:T(8,128)(2,1)}, u32[]{:S(2)}, u32[]{:S(2)}) collective-permute-start(bf16[512,512]{1,0:T(8,128)(2,1)S(1)} %slice.218), channel_id=1, source_target_pairs={{0,1},{1,0},{2,3},{3,2},{4,5},{5,4},{6,7},{7,6},{8,9},{9,8},{10,11... | collective-permute-start | bytes 1572872 | tf_op jit(solution)/shard_map/ppermute | solution.py:26
  376.9 14.9 %collective-permute-start.50 = (bf16[160,2048]{1,0:T(8,128)(2,1)S(1)}, bf16[160,2048]{1,0:T(8,128)(2,1)S(1)}, u32[]{:S(2)}, u32[]{:S(2)}) collective-permute-start(bf16[160,2048]{1,0:T(8,128)(2,1)S(1)} %get-tuple-element.419), channel_id=1, source_target_pairs={{8,0},{10,2},{16,8},{18,10},{24,16},{26,18},{28,24},{30,26},{20,28... | collective-permute-start | bytes 1966088 | tf_op jit(solution)/shard_map/ppermute | solution.py:49
  377.4 14.7 %collective-permute-start.46 = (bf16[160,2048]{1,0:T(8,128)(2,1)S(1)}, bf16[160,2048]{1,0:T(8,128)(2,1)S(1)}, u32[]{:S(2)}, u32[]{:S(2)}) collective-permute-start(bf16[160,2048]{1,0:T(8,128)(2,1)S(1)} %get-tuple-element.418), channel_id=1, source_target_pairs={{0,8},{2,10},{8,16},{10,18},{16,24},{18,26},{24,28},{26,30},{28,20... | collective-permute-start | bytes 1966088 | tf_op jit(solution)/shard_map/ppermute | solution.py:45
  393.5 19.8 %collective-permute-start.47 = (bf16[160,2048]{1,0:T(8,128)(2,1)}, bf16[160,2048]{1,0:T(8,128)(2,1)S(1)}, u32[]{:S(2)}, u32[]{:S(2)}) collective-permute-start(bf16[160,2048]{1,0:T(8,128)(2,1)} %get-tuple-element.416), channel_id=1, source_target_pairs={{0,8},{2,10},{8,16},{10,18},{16,24},{18,26},{24,28},{26,30},{28,20... | collective-permute-start | bytes 1966088 | tf_op jit(solution)/shard_map/ppermute | solution.py:45
  394.9 19.3 %collective-permute-start.51 = (bf16[160,2048]{1,0:T(8,128)(2,1)S(1)}, bf16[160,2048]{1,0:T(8,128)(2,1)}, u32[]{:S(2)}, u32[]{:S(2)}) collective-permute-start(bf16[160,2048]{1,0:T(8,128)(2,1)S(1)} %get-tuple-element.417), channel_id=1, source_target_pairs={{8,0},{10,2},{16,8},{18,10},{24,16},{26,18},{28,24},{30,26},{20,28... | collective-permute-start | bytes 1966088 | tf_op jit(solution)/shard_map/ppermute | solution.py:49
  419.4 14.5 %collective-permute-start.54 = (bf16[160,2048]{1,0:T(8,128)(2,1)S(1)}, bf16[160,2048]{1,0:T(8,128)(2,1)S(1)}, u32[]{:S(2)}, u32[]{:S(2)}) collective-permute-start(bf16[160,2048]{1,0:T(8,128)(2,1)S(1)} %get-tuple-element.400), channel_id=1, source_target_pairs={{0,1},{1,0},{2,3},{3,2},{4,5},{5,4},{6,7},{7,6},{8,9},{9,8},{10,11... | collective-permute-start | bytes 1966088 | tf_op jit(solution)/shard_map/ppermute | solution.py:26
  442.5 30.6 %collective-permute-start.58 = (bf16[1024,512]{1,0:T(8,128)(2,1)}, bf16[1024,512]{1,0:T(8,128)(2,1)}, u32[]{:S(2)}, u32[]{:S(2)}) collective-permute-start(bf16[1024,512]{1,0:T(8,128)(2,1)} %slice.178), channel_id=1, source_target_pairs={{0,1},{1,0},{2,3},{3,2},{4,5},{5,4},{6,7},{7,6},{8,9},{9,8},{10,11... | collective-permute-start | bytes 3145736 | tf_op jit(solution)/shard_map/ppermute | solution.py:26
  464.4 41.0 %collective-permute-start.56 = (bf16[320,2048]{1,0:T(8,128)(2,1)S(1)}, bf16[320,2048]{1,0:T(8,128)(2,1)}, u32[]{:S(2)}, u32[]{:S(2)}) collective-permute-start(bf16[320,2048]{1,0:T(8,128)(2,1)S(1)} %copy-done.14), channel_id=1, source_target_pairs={{0,2},{2,0},{4,6},{6,4},{8,10},{10,8},{12,14},{14,12},{16,18},{18,... | collective-permute-start | bytes 3932168 | tf_op jit(solution)/shard_map/ppermute | solution.py:22
  466.1 40.9 %collective-permute-start.57 = (bf16[320,2048]{1,0:T(8,128)(2,1)S(1)}, bf16[320,2048]{1,0:T(8,128)(2,1)}, u32[]{:S(2)}, u32[]{:S(2)}) collective-permute-start(bf16[320,2048]{1,0:T(8,128)(2,1)S(1)} %copy-done.13), channel_id=1, source_target_pairs={{0,2},{2,0},{4,6},{6,4},{8,10},{10,8},{12,14},{14,12},{16,18},{18,... | collective-permute-start | bytes 3932168 | tf_op jit(solution)/shard_map/ppermute | solution.py:22
  472.3 31.4 %collective-permute-start.66 = (bf16[2,128,1024]{2,1,0:T(8,128)(2,1)}, bf16[2,128,1024]{2,1,0:T(8,128)(2,1)S(1)}, u32[]{:S(2)}, u32[]{:S(2)}) collective-permute-start(bf16[2,128,1024]{2,1,0:T(8,128)(2,1)} %get-tuple-element.315), channel_id=1, source_target_pairs={{0,8},{2,10},{4,12},{6,14},{8,0},{10,2},{12,4},{14,6},{16,24},{18,... | collective-permute-start | bytes 1572872 | tf_op jit(solution)/shard_map/ppermute | solution.py:22
  473.1 30.9 %collective-permute-start.65 = (bf16[2,128,1024]{2,1,0:T(8,128)(2,1)}, bf16[2,128,1024]{2,1,0:T(8,128)(2,1)S(1)}, u32[]{:S(2)}, u32[]{:S(2)}) collective-permute-start(bf16[2,128,1024]{2,1,0:T(8,128)(2,1)} %get-tuple-element.314), channel_id=1, source_target_pairs={{0,4},{2,6},{4,0},{6,2},{8,12},{10,14},{12,8},{14,10},{16,20},{18,... | collective-permute-start | bytes 1572872 | tf_op jit(solution)/shard_map/ppermute | solution.py:22
  476.7 45.6 %collective-permute-start.60 = (bf16[1024,512]{1,0:T(8,128)(2,1)}, bf16[1024,512]{1,0:T(8,128)(2,1)}, u32[]{:S(2)}, u32[]{:S(2)}) collective-permute-start(bf16[1024,512]{1,0:T(8,128)(2,1)} %slice.179), channel_id=1, source_target_pairs={{0,1},{1,0},{2,3},{3,2},{4,5},{5,4},{6,7},{7,6},{8,9},{9,8},{10,11... | collective-permute-start | bytes 3145736 | tf_op jit(solution)/shard_map/ppermute | solution.py:26
  503.9 18.3 %collective-permute-start.59 = (bf16[512,512]{1,0:T(8,128)(2,1)}, bf16[512,512]{1,0:T(8,128)(2,1)}, u32[]{:S(2)}, u32[]{:S(2)}) collective-permute-start(bf16[512,512]{1,0:T(8,128)(2,1)} %slice.177), channel_id=1, source_target_pairs={{0,1},{1,0},{2,3},{3,2},{4,5},{5,4},{6,7},{7,6},{8,9},{9,8},{10,11... | collective-permute-start | bytes 1572872 | tf_op jit(solution)/shard_map/ppermute | solution.py:26
  551.9 19.4 %collective-permute-start.70 = (bf16[256,1024]{1,0:T(8,128)(2,1)}, bf16[256,1024]{1,0:T(8,128)(2,1)}, u32[]{:S(2)}, u32[]{:S(2)}) collective-permute-start(bf16[256,1024]{1,0:T(8,128)(2,1)} %get-tuple-element.330), channel_id=1, source_target_pairs={{0,8},{2,10},{8,16},{10,18},{16,24},{18,26},{24,28},{26,30},{28,20... | collective-permute-start | bytes 1572872 | tf_op jit(solution)/shard_map/ppermute | solution.py:45
  553.9 19.6 %collective-permute-start.74 = (bf16[512,512]{1,0:T(8,128)(2,1)}, bf16[512,512]{1,0:T(8,128)(2,1)}, u32[]{:S(2)}, u32[]{:S(2)}) collective-permute-start(bf16[512,512]{1,0:T(8,128)(2,1)} %get-tuple-element.345), channel_id=1, source_target_pairs={{0,1},{1,0},{2,3},{3,2},{4,5},{5,4},{6,7},{7,6},{8,9},{9,8},{10,11... | collective-permute-start | bytes 1572872 | tf_op jit(solution)/shard_map/ppermute | solution.py:26
  555.5 15.7 %collective-permute-start.71 = (bf16[256,1024]{1,0:T(8,128)(2,1)}, bf16[256,1024]{1,0:T(8,128)(2,1)}, u32[]{:S(2)}, u32[]{:S(2)}) collective-permute-start(bf16[256,1024]{1,0:T(8,128)(2,1)} %get-tuple-element.331), channel_id=1, source_target_pairs={{8,0},{10,2},{16,8},{18,10},{24,16},{26,18},{28,24},{30,26},{20,28... | collective-permute-start | bytes 1572872 | tf_op jit(solution)/shard_map/ppermute | solution.py:49
  573.5 18.9 %collective-permute-start.75 = (bf16[512,512]{1,0:T(8,128)(2,1)}, bf16[512,512]{1,0:T(8,128)(2,1)}, u32[]{:S(2)}, u32[]{:S(2)}) collective-permute-start(bf16[512,512]{1,0:T(8,128)(2,1)} %get-tuple-element.346), channel_id=1, source_target_pairs={{0,1},{1,0},{2,3},{3,2},{4,5},{5,4},{6,7},{7,6},{8,9},{9,8},{10,11... | collective-permute-start | bytes 1572872 | tf_op jit(solution)/shard_map/ppermute | solution.py:26
  576.5 24.3 %collective-permute-start.72 = (bf16[256,2048]{1,0:T(8,128)(2,1)S(1)}, bf16[256,2048]{1,0:T(8,128)(2,1)S(1)}, u32[]{:S(2)}, u32[]{:S(2)}) collective-permute-start(bf16[256,2048]{1,0:T(8,128)(2,1)S(1)} %pad_maximum_fusion.2), channel_id=1, source_target_pairs={{0,8},{2,10},{8,16},{10,18},{16,24},{18,26},{24,28},{26,30},{28,20... | collective-permute-start | bytes 3145736 | tf_op jit(solution)/shard_map/ppermute | solution.py:45
  578.8 24.4 %collective-permute-start.73 = (bf16[256,2048]{1,0:T(8,128)(2,1)}, bf16[256,2048]{1,0:T(8,128)(2,1)}, u32[]{:S(2)}, u32[]{:S(2)}) collective-permute-start(bf16[256,2048]{1,0:T(8,128)(2,1)} %pad_maximum_fusion.3), channel_id=1, source_target_pairs={{8,0},{10,2},{16,8},{18,10},{24,16},{26,18},{28,24},{30,26},{20,28... | collective-permute-start | bytes 3145736 | tf_op jit(solution)/shard_map/ppermute | solution.py:49
  578.8 24.4 %collective-permute-start.78 = (bf16[160,2048]{1,0:T(8,128)(2,1)}, bf16[160,2048]{1,0:T(8,128)(2,1)S(1)}, u32[]{:S(2)}, u32[]{:S(2)}) collective-permute-start(bf16[160,2048]{1,0:T(8,128)(2,1)} %dynamic-slice_convert_fusion), channel_id=1, source_target_pairs={{0,1},{1,0},{2,3},{3,2},{4,5},{5,4},{6,7},{7,6},{8,9},{9,8},{10,11... | collective-permute-start | bytes 1966088 | tf_op jit(solution)/shard_map/ppermute | solution.py:26
  606.6 23.5 %collective-permute-start.76 = (bf16[256,2048]{1,0:T(8,128)(2,1)}, bf16[256,2048]{1,0:T(8,128)(2,1)}, u32[]{:S(2)}, u32[]{:S(2)}) collective-permute-start(bf16[256,2048]{1,0:T(8,128)(2,1)} %get-tuple-element.349), channel_id=1, source_target_pairs={{0,8},{2,10},{8,16},{10,18},{16,24},{18,26},{24,28},{26,30},{28,20... | collective-permute-start | bytes 3145736 | tf_op jit(solution)/shard_map/ppermute | solution.py:45
  608.3 22.9 %collective-permute-start.77 = (bf16[256,2048]{1,0:T(8,128)(2,1)}, bf16[256,2048]{1,0:T(8,128)(2,1)}, u32[]{:S(2)}, u32[]{:S(2)}) collective-permute-start(bf16[256,2048]{1,0:T(8,128)(2,1)} %get-tuple-element.350), channel_id=1, source_target_pairs={{8,0},{10,2},{16,8},{18,10},{24,16},{26,18},{28,24},{30,26},{20,28... | collective-permute-start | bytes 3145736 | tf_op jit(solution)/shard_map/ppermute | solution.py:49
  608.6 44.0 %collective-permute-start.82 = (bf16[160,2048]{1,0:T(8,128)(2,1)}, bf16[160,2048]{1,0:T(8,128)(2,1)}, u32[]{:S(2)}, u32[]{:S(2)}) collective-permute-start(bf16[160,2048]{1,0:T(8,128)(2,1)} %reduce-scatter.2.cloned.1.call-done.refs_2_), channel_id=1, source_target_pairs={{0,1},{1,0},{2,3},{3,2},{4,5},{5,4},{6,7},{7,6},{8,9},{9,8},{10,11... | collective-permute-start | bytes 1966088 | tf_op jit(solution)/shard_map/ppermute | solution.py:26
  612.0 47.7 %collective-permute-start.81 = (f32[160,2048]{1,0:T(8,128)}, f32[160,2048]{1,0:T(8,128)}, u32[]{:S(2)}, u32[]{:S(2)}) collective-permute-start(f32[160,2048]{1,0:T(8,128)} %fusion.5.refs_1_), channel_id=1, source_target_pairs={{0,1},{1,0},{2,3},{3,2},{4,5},{5,4},{6,7},{7,6},{8,9},{9,8},{10,11... | collective-permute-start | bytes 3932168 | tf_op jit(solution)/shard_map/ppermute | solution.py:26
  634.9 27.7 %collective-permute-start.79 = (bf16[256,2048]{1,0:T(8,128)(2,1)}, bf16[256,2048]{1,0:T(8,128)(2,1)}, u32[]{:S(2)}, u32[]{:S(2)}) collective-permute-start(bf16[256,2048]{1,0:T(8,128)(2,1)} %get-tuple-element.358), channel_id=1, source_target_pairs={{0,8},{2,10},{8,16},{10,18},{16,24},{18,26},{24,28},{26,30},{28,20... | collective-permute-start | bytes 3145736 | tf_op jit(solution)/shard_map/ppermute | solution.py:45
  635.7 26.9 %collective-permute-start.80 = (bf16[256,2048]{1,0:T(8,128)(2,1)}, bf16[256,2048]{1,0:T(8,128)(2,1)}, u32[]{:S(2)}, u32[]{:S(2)}) collective-permute-start(bf16[256,2048]{1,0:T(8,128)(2,1)} %get-tuple-element.359), channel_id=1, source_target_pairs={{8,0},{10,2},{16,8},{18,10},{24,16},{26,18},{28,24},{30,26},{20,28... | collective-permute-start | bytes 3145736 | tf_op jit(solution)/shard_map/ppermute | solution.py:49
  (101 other events, 1326.6 us)
Sparse Core Ops, SparseCore 0:
  12.7 94.2 all-gather.4
  109.9 97.4 all-gather.6
  416.2 134.1 reduce-scatter.1

commit v15 on v14

--- a/solution.py
+++ b/solution.py
@@ -1285,26 +1285,26 @@
         late, later = {}, {}
 
         def normed_stage(gated):
-            late["own"], late["sent"], late["gain"] = back_shares(*map(gated, pre_grads))
+            late["part"] = back_all(*map(gated, pre_grads))
 
         def gate_product_stage(gated):
-            other = swap_tensor(late["sent"])
+            later["other"] = swap_tensor(gated(other_half(late["part"]).astype(LOW)))
+            late["hidden"] = gated(hidden_other)
             late["gate"] = grad_sum(gated(expert_in), g0, gate_got)
             late["mixed"], late["pieces"] = gated(mixed), up_pieces
-            later["other"] = other
 
         def input_stage(gated):
             later["mixed"] = swap_tensor(late["mixed"])
-            late["half"] = input_side(late["own"], gated(later["other"]))
+            late["half"] = input_side(own_half(late["part"]), gated(later["other"]))
             later["half"] = swap_tensor(late["half"])
             late["down"] = grad_sum(gated(h0), back_rows, down_got)
 
         def up_product_stage(gated):
             up_got = jnp.concatenate([soon[1], *late["pieces"]], axis=0)
             late["up"] = grad_sum(gated(expert_in), u0, up_got)
-            late["gains"] = gain_side(gain_part(after(late["gain"], late["up"])))
+            late["gains"] = gain_side(gain_part(after(late["part"], late["up"])))
             late["output"] = join_halves(
-                side[None], [gated(hidden_state), mixed], [hidden_other, later["mixed"]]
+                side[None], [gated(hidden_state), mixed], [late["hidden"], later["mixed"]]
             )
             late["input"] = join_halves(side[None], [gated(late["half"])], [later["half"]])
 

time: 686 us -> 685 us (level)
    ppermute x19, waiting for transfers between devices: 104 us -> 114 us  [swap_tensor(): return lax.ppermute(block, 'tensor', [(0, 1), (1, 0)])]
    ppermute x12, waiting for transfers between devices: 17.8 us -> 9.82 us  [ahead(): return lax.ppermute(block, 'dp', AHEAD)]
  transfers between devices with their start and end apart: 88 -> 88, of which waited for: 29 -> 29; matrix products, arithmetic and copies ran while one was open for 18% -> 17% of each run, Pallas kernels for 32% -> 32%
where the time goes in v15:
time: 685 us; the launch traced here: 678 us
  waiting for transfers between devices  229 us (33%)
  Pallas kernels  225 us (33%)
  starting transfers between devices  66.6 us (10%)
  matrix products  54.7 us (8%)
  other arithmetic  42.7 us (6%)
  local copies, waits for them, and re-layouts  34.4 us (5%)
  between operations  15.4 us (2%)
  blocking collectives  10 us (1%)
    ppermute x19, waiting for transfers between devices, swap_tensor(): return lax.ppermute(block, 'tensor', [(0, 1), (1, 0)])  114 us
    pallas_call x5, Pallas kernels, expert_chunk(): pl.pallas_call(lambda *refs: chunk_kernel(len(pieces), len(held), at, spl...  92.2 us
    ppermute x41, waiting for transfers between devices, swap_bit(): return lax.ppermute(block, axis, [(i, i ^ 1 << bit) for i in range(count)])  80.3 us
    dot_general x6, matrix products, dot_tn(): lax.dot_general(left, right, (((0,), (0,)), ((), ())), preferred_element_...  54.6 us
    ppermute x19, starting transfers between devices, swap_tensor(): return lax.ppermute(block, 'tensor', [(0, 1), (1, 0)])  23.4 us
    pallas_call x1, Pallas kernels, attend_back(): pl.pallas_call(attend_back_kernel, grid=(width // HEAD // PAIR,), in_spec...  19.8 us
    pallas_call x1, Pallas kernels, mixed_pass(): pl.pallas_call(mixed_kernel, grid_spec=pltpu.PrefetchScalarGridSpec(num_s...  17.8 us
    ppermute x12, waiting for transfers between devices, behind(): return lax.ppermute(block, 'dp', BEHIND)  16.7 us
  transfers between devices with their start and end apart: 88, of which 29 were waited for; matrix products, arithmetic and copies ran while one was open for 17% of the time, Pallas kernels for 32%

profile of v15, /device:TPU:0, one launch (start us, length us, event | category | flops | bytes accessed | tf_op | source)
XLA Modules:
  0.0 678.1 jit_solution(15790774537768924239)
XLA Ops:
  10.1 2.4 shard_map.309
  12.7 2.3 dynamic-slice_convert_fusion.2
  15.1 3.0 collective-permute-start
  22.1 42.6 %collective-permute-done.refs_5_.refs_7_.refs_9_ = bf16[2048,512]{1,0:T(8,128)(2,1)} collective-permute-done((bf16[2048,512]{1,0:T(8,128)(2,1)S(1)}, bf16[2048,512]{1,0:T(8,128)(2,1)}, u32[]{:S(2)}, u32[]{:S(2)}) %collective-permute-start) | collective-permute-done | bytes 2097184 | tf_op jit(solution)/shard_map/ppermute | solution.py:26
  64.7 44.1 %collective-permute-done.1.refs_7_.refs_9_.refs_11_ = bf16[2048,512]{1,0:T(8,128)(2,1)} collective-permute-done((bf16[2048,512]{1,0:T(8,128)(2,1)}, bf16[2048,512]{1,0:T(8,128)(2,1)}, u32[]{:S(2)}, u32[]{:S(2)}) %collective-permute-start.1) | collective-permute-done | bytes 2097184 | tf_op jit(solution)/shard_map/ppermute | solution.py:26
  111.9 9.0 %shard_map.310 = (f32[320,1024]{1,0:T(8,128)}, f32[320,1024]{1,0:T(8,128)}, bf16[320,1024]{1,0:T(8,128)(2,1)}, bf16[128,1024]{1,0:T(8,128)(2,1)}) custom-call(bf16[320,2048]{1,0:T(8,128)(2,1)} %multiply_convert_fusion.refs_0_, bf16[16,528,1024]{2,1,0:T(8,128)(2,1)} %bitcast.93), custom_call_target="tpu_custom_call" | custom-call | flops 4026531840 | bytes 15204352 | tf_op jit(solution)/shard_map/pallas_call | solution.py:512
  124.1 5.1 all-reduce.3
  132.3 2.7 shard_map.311
  138.7 9.2 %collective-permute-done.5.refs_3_ = bf16[128,1024]{1,0:T(8,128)(2,1)} collective-permute-done((bf16[128,1024]{1,0:T(8,128)(2,1)}, bf16[128,1024]{1,0:T(8,128)(2,1)}, u32[]{:S(2)}, u32[]{:S(2)}) %collective-permute-start.5) | collective-permute-done | bytes 262176 | tf_op jit(solution)/shard_map/ppermute | solution.py:22
  152.0 6.0 collective-permute-done.12.refs_10_
  158.3 5.4 collective-permute-done.7.refs_5_
  164.3 18.1 %collective-permute-done.14.refs_12_ = bf16[128,1024]{1,0:T(8,128)(2,1)} collective-permute-done((bf16[128,1024]{1,0:T(8,128)(2,1)}, bf16[128,1024]{1,0:T(8,128)(2,1)}, u32[]{:S(2)}, u32[]{:S(2)}) %collective-permute-start.14) | collective-permute-done | bytes 262176 | tf_op jit(solution)/shard_map/ppermute | solution.py:22
  184.6 11.9 %shard_map.312.refs_0_.refs_8_ = bf16[320,1024]{1,0:T(8,128)(2,1)} custom-call(f32[320,1024]{1,0:T(8,128)} %get-tuple-element.204.flat_ref.refs_0_, f32[1,1024]{1,0:T(1,128)} %bitcast.135, f32[320,1]{1,0:T(8,128)} %broadcast_in_dim.145.scale_ref.refs_3_, f32[320,128]{1,0:T(8,128)} %get-tuple-element.206.cos_ref.refs_5_, ...), custom_call_target="tpu_custom_call" | custom-call | tf_op jit(solution)/shard_map/pallas_call | solution.py:279
  196.5 4.6 shard_map.313
  204.1 1.8 convert_element_type.294
  207.4 8.8 %shard_map.314.refs_3_.refs_5_.refs_7_ = bf16[2560,2048]{1,0:T(8,128)(2,1)} custom-call(s32[16]{0:T(128)} %get-tuple-element.407.refs_0_, bf16[16,160,2048]{2,1,0:T(8,128)(2,1)} %bitcast.127), custom_call_target="tpu_custom_call" | custom-call | tf_op jit(solution)/shard_map/pallas_call | solution.py:462
  216.2 3.6 collective-permute-done.17
  219.7 2.0 multiply_reduce_fusion.6
  222.0 2.1 collective-permute-done.18.refs_2_
  224.1 2.0 collective-permute-start.20
  230.3 13.7 %shard_map.315 = (bf16[160,2048]{1,0:T(8,128)(2,1)}, bf16[160,2048]{1,0:T(8,128)(2,1)}, bf16[2560,2048]{1,0:T(8,128)(2,1)}, bf16[2560,512]{1,0:T(8,128)(2,1)}, b...) custom-call(f32[2560,1]{1,0:T(8,128)} %copy.91.refs_0_, ...), custom_call_target="tpu_custom_call" | custom-call | flops 6710886400 | bytes 19791872 | tf_op jit(solution)/shard_map/pallas_call | solution.py:888
  245.0 2.2 collective-permute-start.23
  248.1 13.7 %shard_map.316 = (bf16[320,2048]{1,0:T(8,128)(2,1)}, bf16[2560,2048]{1,0:T(8,128)(2,1)}, bf16[2560,512]{1,0:T(8,128)(2,1)}, bf16[2560,512]{1,0:T(8,128)(2,1)}, b...) custom-call(f32[2560,1]{1,0:T(8,128)} %copy.91.refs_0_, ...), custom_call_target="tpu_custom_call", output_to_operand_aliasing={{1}: (10, {}), {2}: (11, {}), {3}: (12, {}), {4}: (13, {}),... | custom-call | flops 6710886400 | bytes 19791872 | tf_op jit(solution)/shard_map/pallas_call | solution.py:888
  266.5 21.5 %shard_map.317 = (bf16[320,2048]{1,0:T(8,128)(2,1)}, bf16[320,2048]{1,0:T(8,128)(2,1)}, bf16[2560,2048]{1,0:T(8,128)(2,1)}, bf16[2560,512]{1,0:T(8,128)(2,1)}, b...) custom-call(f32[2560,1]{1,0:T(8,128)} %copy.91.refs_0_, ...), custom_call_target="tpu_custom_call", output_to_operand_aliasing={{2}: (12, {}), {3}: (13, {}), {4}: (14, {}), {5}: (15, {}),... | custom-call | flops 13421772800 | bytes 27000832 | tf_op jit(solution)/shard_map/pallas_call | solution.py:888
  291.4 1.9 collective-permute-start.36
  293.3 21.7 %shard_map.318 = (bf16[320,2048]{1,0:T(8,128)(2,1)}, bf16[320,2048]{1,0:T(8,128)(2,1)}, bf16[2560,2048]{1,0:T(8,128)(2,1)}, bf16[2560,512]{1,0:T(8,128)(2,1)}, b...) custom-call(f32[2560,1]{1,0:T(8,128)} %copy.91.refs_0_, ...), custom_call_target="tpu_custom_call", output_to_operand_aliasing={{2}: (12, {}), {3}: (13, {}), {4}: (14, {}), {5}: (15, {}),... | custom-call | flops 13421772800 | bytes 27000832 | tf_op jit(solution)/shard_map/pallas_call | solution.py:888
  317.9 21.6 %shard_map.319 = (bf16[160,2048]{1,0:T(8,128)(2,1)}, bf16[160,2048]{1,0:T(8,128)(2,1)}, bf16[320,2048]{1,0:T(8,128)(2,1)}, bf16[2560,2048]{1,0:T(8,128)(2,1)}, b...) custom-call(f32[2560,1]{1,0:T(8,128)} %copy.91.refs_0_, ...), custom_call_target="tpu_custom_call", output_to_operand_aliasing={{3}: (14, {}), {4}: (15, {}), {5}: (16, {}), {6}: (17, {}),... | custom-call | flops 13421772800 | bytes 27000832 | tf_op jit(solution)/shard_map/pallas_call | solution.py:888
  345.4 11.2 %convolution_convert_fusion.2 = bf16[512,2048]{1,0:T(8,128)(2,1)} fusion(bf16[2560,512]{1,0:T(8,128)(2,1)S(1)} %copy-done.4, bf16[2560,2048]{1,0:T(8,128)(2,1)} %shard_map.314.refs_3_.refs_5_.refs_7_), kind=kOutput, calls=%fused_computation.6 | convolution fusion | flops 5369757696 | bytes 15204352 | tf_op jit(solution)/shard_map/dot_general | solution.py:157
  361.5 5.8 convolution_convert_fusion.1
  368.2 7.1 %collective-permute-done.49 = bf16[160,2048]{1,0:T(8,128)(2,1)S(1)} collective-permute-done((bf16[160,2048]{1,0:T(8,128)(2,1)S(1)}, bf16[160,2048]{1,0:T(8,128)(2,1)S(1)}, u32[]{:S(2)}, u32[]{:S(2)}) %collective-permute-start.49) | collective-permute-done | bytes 655392 | tf_op jit(solution)/shard_map/ppermute | solution.py:49
  378.9 6.8 %convolution_convert_fusion = bf16[2048,512]{1,0:T(8,128)(2,1)} fusion(bf16[2560,2048]{1,0:T(8,128)(2,1)S(1)} %bitcast.103, bf16[2560,512]{1,0:T(8,128)(2,1)S(1)} %copy-done.8), kind=kOutput, calls=%fused_computation.4 | convolution fusion | flops 5369757696 | bytes 15204352 | tf_op jit(solution)/shard_map/dot_general | solution.py:157
  385.7 6.0 collective-permute-done.50
  395.5 17.8 %shard_map.320 = bf16[8,2,160,2048]{3,2,1,0:T(8,128)(2,1)} custom-call(s32[8]{0:T(128)} %compare_select_fusion.7.chip_ref, s32[8]{0:T(128)} %constant.190.clone.same_ref, s32[8]{0:T(128)} %constant.191.clone.cross_ref, s32[1]{0:T(128)} %bitcast.core_ref, bf16[2560,512]{1,0:T(8,128)(2,1)} %get-tuple-element.357.refs_0_.refs_1_, ...), custom_call_target="tpu_custom_call" | custom-call | flops 10737418240 | bytes 19922944 | tf_op jit(solution)/shard_map/pallas_call | solution.py:940
  414.1 1.9 convert_add_fusion.7
  420.5 13.4 %collective-permute-done.54 = bf16[160,2048]{1,0:T(8,128)(2,1)S(1)} collective-permute-done((bf16[160,2048]{1,0:T(8,128)(2,1)S(1)}, bf16[160,2048]{1,0:T(8,128)(2,1)S(1)}, u32[]{:S(2)}, u32[]{:S(2)}) %collective-permute-start.54) | collective-permute-done | bytes 655392 | tf_op jit(solution)/shard_map/ppermute | solution.py:26
  436.2 6.2 shard_map.321.refs_14_
  443.9 19.8 %shard_map.322 = (f32[320,1024]{1,0:T(8,128)}, f32[320,1]{1,0:T(8,128)}, f32[1,1024]{1,0:T(1,128)}, f32[320,1024]{1,0:T(8,128)}, f32[320,1024]{1,0:T(8,128)}, /*...) custom-call(f32[320,1024]{1,0:T(8,128)} %get-tuple-element.204.flat_, ...), custom_call_target="tpu_custom_call" | custom-call | flops 20000000000 | bytes 40000000 | tf_op jit(solution)/shard_map/pallas_call | solution.py:338
  469.1 3.1 shard_map.323
  474.3 2.3 slice.179
  477.5 1.9 slice.177
  479.4 24.3 %collective-permute-done.66.refs_9_ = bf16[2,128,1024]{2,1,0:T(8,128)(2,1)S(1)} collective-permute-done((bf16[2,128,1024]{2,1,0:T(8,128)(2,1)}, bf16[2,128,1024]{2,1,0:T(8,128)(2,1)S(1)}, u32[]{:S(2)}, u32[]{:S(2)}) %collective-permute-start.66) | collective-permute-done | bytes 524320 | tf_op jit(solution)/shard_map/ppermute | solution.py:22
  507.0 7.5 %collective-permute-done.68.refs_11_ = bf16[128,1024]{1,0:T(8,128)(2,1)S(1)} collective-permute-done((bf16[128,1024]{1,0:T(8,128)(2,1)S(1)}, bf16[128,1024]{1,0:T(8,128)(2,1)S(1)}, u32[]{:S(2)}, u32[]{:S(2)}) %collective-permute-start.68) | collective-permute-done | bytes 262176 | tf_op jit(solution)/shard_map/ppermute | solution.py:22
  515.8 5.4 shard_map.324
  522.4 4.9 psum.23
  529.0 4.8 shard_map.325
  533.9 2.3 pad_maximum_fusion.1.refs_3_
  538.1 14.1 %shard_map.326 = (bf16[8,256,2048]{2,1,0:T(8,128)(2,1)}, bf16[256,1024]{1,0:T(8,128)(2,1)}, bf16[256,1024]{1,0:T(8,128)(2,1)}) custom-call(s32[8]{0:T(128)} %compare_select_fusion.7.chip_ref, s32[1]{0:T(128)} %bitcast.core_ref, bf16[320,2048]{1,0:T(8,128)(2,1)} %multiply_convert_fusion.refs_0_, bf16[320,2048]{1,0:T(8,128)(2,1)} %collective-permute-done.56.refs_1_, ...), custom_call_target="tpu_custom_call" | custom-call | flops 5368709120 | bytes 16252928 | tf_op jit(solution)/shard_map/pallas_call | solution.py:634
  552.3 2.1 collective-permute-start.70
  557.7 9.3 %shard_map.327 = f32[320,2048]{1,0:T(8,128)} custom-call(bf16[320,1024]{1,0:T(8,128)(2,1)} %get-tuple-element.333.refs_4_.refs_0_, bf16[320,1024]{1,0:T(8,128)(2,1)} %get-tuple-element.334.refs_5_.refs_1_, bf16[320,1024]{1,0:T(8,128)(2,1)} %get-tuple-element.335.refs_10_.refs_6_.refs_2_, bf16[16,528,1024]{2,1,0:T(8,128)(2,1)} %bitcast.97, ...), custom_call_target="tpu_custom_call" | custom-call | flops 4026531840 | bytes 15204352 | tf_op jit(solution)/shard_map/pallas_call | solution.py:551
  567.1 1.9 collective-permute-done.71
  575.5 12.1 %convert_add_fusion.2 = f32[2048,512]{1,0:T(8,128)} fusion(bf16[2560,2048]{1,0:T(8,128)(2,1)} %get-tuple-element.366, bf16[2560,512]{1,0:T(8,128)(2,1)S(1)} %copy-done.5, bf16[512,512]{1,0:T(8,128)(2,1)} %collective-permute-done.59, bf16[1024,512]{1,0:T(8,128)(2,1)} %collective-permute-done.58, bf16[512,512]{1,0:T(8,128)(2,1)} %collective-permute-done.53), kind=kOutput, calls=%fused_computation.3 | convolution fusion | flops 5376049152 | bytes 19398656 | tf_op jit(solution)/shard_map/dot_general | solution.py:157
  587.6 10.6 %collective-permute-done.75 = bf16[512,512]{1,0:T(8,128)(2,1)} collective-permute-done((bf16[512,512]{1,0:T(8,128)(2,1)}, bf16[512,512]{1,0:T(8,128)(2,1)}, u32[]{:S(2)}, u32[]{:S(2)}) %collective-permute-start.75) | collective-permute-done | bytes 524320 | tf_op jit(solution)/shard_map/ppermute | solution.py:26
  599.3 3.5 fusion.1
  608.4 9.3 %convert_add_fusion.1 = f32[512,2048]{1,0:T(8,128)} fusion(bf16[512,2048]{1,0:T(8,128)(2,1)} %collective-permute-done.52, bf16[2560,512]{1,0:T(8,128)(2,1)S(1)} %copy-done.3, bf16[2560,2048]{1,0:T(8,128)(2,1)S(1)} %bitcast.101), kind=kOutput, calls=%fused_computation.2 | convolution fusion | flops 5370806272 | bytes 19398656 | tf_op jit(solution)/shard_map/dot_general | solution.py:157
  617.8 8.5 %collective-permute-done.76 = bf16[256,2048]{1,0:T(8,128)(2,1)} collective-permute-done((bf16[256,2048]{1,0:T(8,128)(2,1)}, bf16[256,2048]{1,0:T(8,128)(2,1)}, u32[]{:S(2)}, u32[]{:S(2)}) %collective-permute-start.76) | collective-permute-done | bytes 1048608 | tf_op jit(solution)/shard_map/ppermute | solution.py:45
  627.3 3.7 fusion
  633.1 9.3 %convert_add_fusion = f32[2048,512]{1,0:T(8,128)} fusion(bf16[2560,2048]{1,0:T(8,128)(2,1)S(1)} %bitcast.105, bf16[2560,512]{1,0:T(8,128)(2,1)S(1)} %copy-done.7, bf16[512,512]{1,0:T(8,128)(2,1)} %collective-permute-done.75, bf16[512,512]{1,0:T(8,128)(2,1)} %collective-permute-done.74, bf16[1024,512]{1,0:T(8,128)(2,1)} %collective-permute-done.60), kind=kOutput, calls=%fused_computation.1 | convolution fusion | flops 5376049152 | bytes 19398656 | tf_op jit(solution)/shard_map/dot_general | solution.py:157
  643.7 3.0 all-to-all-start
  646.7 3.3 shard_map.329
  650.0 6.8 all-to-all-done
  656.8 2.9 shard_map.328
  661.1 3.4 shard_map.330
  665.0 2.3 collective-permute-done.83.got_ref
  668.3 3.0 shard_map.331
  (420 shorter events, 117.8 us)
Async XLA Ops:
  7.2 101.6 %all-gather.5.cloned.1.call-start = ((), (), s32[]{:S(2)}) async-start(), calls=%async_computation.3 | async-start | bytes 18382848 | tf_op jit(solution)/shard_map/all_gather | solution.py:1059
  12.6 194.7 %all-gather.7.cloned.1.call-start = ((), (), s32[]{:S(2)}) async-start(), calls=%async_computation.4 | async-start | bytes 11141120 | tf_op jit(solution)/shard_map/all_gather | solution.py:1061
  15.0 537.2 %reduce-scatter.2.cloned.1.call-start = ((), (), s32[]{:S(2)}) async-start(), calls=%async_computation.2 | async-start | bytes 11141120 | tf_op jit(solution)/shard_map/reduce_scatter | solution.py:1190
  15.1 49.6 %collective-permute-start = (bf16[2048,512]{1,0:T(8,128)(2,1)S(1)}, bf16[2048,512]{1,0:T(8,128)(2,1)}, u32[]{:S(2)}, u32[]{:S(2)}) collective-permute-start(bf16[2048,512]{1,0:T(8,128)(2,1)S(1)} %bitcast.111), channel_id=1, source_target_pairs={{0,1},{1,0},{2,3},{3,2},{4,5},{5,4},{6,7},{7,6},{8,9},{9,8},{10,11... | collective-permute-start | bytes 6291464 | tf_op jit(solution)/shard_map/ppermute | solution.py:26
  18.1 90.7 %collective-permute-start.1 = (bf16[2048,512]{1,0:T(8,128)(2,1)}, bf16[2048,512]{1,0:T(8,128)(2,1)}, u32[]{:S(2)}, u32[]{:S(2)}) collective-permute-start(bf16[2048,512]{1,0:T(8,128)(2,1)} %bitcast.112), channel_id=1, source_target_pairs={{0,1},{1,0},{2,3},{3,2},{4,5},{5,4},{6,7},{7,6},{8,9},{9,8},{10,11... | collective-permute-start | bytes 6291464 | tf_op jit(solution)/shard_map/ppermute | solution.py:26
  129.2 71.9 %collective-permute-start.16 = (bf16[512,2048]{1,0:T(8,128)(2,1)S(1)}, bf16[512,2048]{1,0:T(8,128)(2,1)}, u32[]{:S(2)}, u32[]{:S(2)}) collective-permute-start(bf16[512,2048]{1,0:T(8,128)(2,1)S(1)} %bitcast.124), channel_id=1, source_target_pairs={{0,1},{1,0},{2,3},{3,2},{4,5},{5,4},{6,7},{7,6},{8,9},{9,8},{10,11... | collective-permute-start | bytes 6291464 | tf_op jit(solution)/shard_map/ppermute | solution.py:26
  158.0 24.4 %collective-permute-start.14 = (bf16[128,1024]{1,0:T(8,128)(2,1)}, bf16[128,1024]{1,0:T(8,128)(2,1)}, u32[]{:S(2)}, u32[]{:S(2)}) collective-permute-start(bf16[128,1024]{1,0:T(8,128)(2,1)} %collective-permute-done.10.refs_8_), channel_id=1, source_target_pairs={{0,8},{2,10},{4,12},{6,14},{8,0},{10,2},{12,4},{14,6},{16,24},{18,... | collective-permute-start | bytes 786440 | tf_op jit(solution)/shard_map/ppermute | solution.py:22
  163.7 20.9 %collective-permute-start.11 = (bf16[128,1024]{1,0:T(8,128)(2,1)}, bf16[128,1024]{1,0:T(8,128)(2,1)}, u32[]{:S(2)}, u32[]{:S(2)}) collective-permute-start(bf16[128,1024]{1,0:T(8,128)(2,1)} %collective-permute-done.10.refs_8_), channel_id=1, source_target_pairs={{0,2},{2,0},{4,6},{6,4},{8,10},{10,8},{12,14},{14,12},{16,18},{18,... | collective-permute-start | bytes 786440 | tf_op jit(solution)/shard_map/ppermute | solution.py:22
  163.7 20.9 %collective-permute-start.13 = (bf16[128,1024]{1,0:T(8,128)(2,1)}, bf16[128,1024]{1,0:T(8,128)(2,1)}, u32[]{:S(2)}, u32[]{:S(2)}) collective-permute-start(bf16[128,1024]{1,0:T(8,128)(2,1)} %collective-permute-done.12.refs_10_), channel_id=1, source_target_pairs={{0,2},{2,0},{4,6},{6,4},{8,10},{10,8},{12,14},{14,12},{16,18},{18,... | collective-permute-start | bytes 786440 | tf_op jit(solution)/shard_map/ppermute | solution.py:22
  164.2 20.4 %collective-permute-start.8 = (bf16[128,1024]{1,0:T(8,128)(2,1)}, bf16[128,1024]{1,0:T(8,128)(2,1)}, u32[]{:S(2)}, u32[]{:S(2)}) collective-permute-start(bf16[128,1024]{1,0:T(8,128)(2,1)} %collective-permute-done.7.refs_5_), channel_id=1, source_target_pairs={{0,2},{2,0},{4,6},{6,4},{8,10},{10,8},{12,14},{14,12},{16,18},{18,... | collective-permute-start | bytes 786440 | tf_op jit(solution)/shard_map/ppermute | solution.py:22
  202.5 17.2 %collective-permute-start.17 = (bf16[160,2048]{1,0:T(8,128)(2,1)S(1)}, bf16[160,2048]{1,0:T(8,128)(2,1)S(1)}, u32[]{:S(2)}, u32[]{:S(2)}) collective-permute-start(bf16[160,2048]{1,0:T(8,128)(2,1)S(1)} %dynamic-slice_convert_fusion.1), channel_id=1, source_target_pairs={{0,1},{1,0},{2,3},{3,2},{4,5},{5,4},{6,7},{7,6},{8,9},{9,8},{10,11... | collective-permute-start | bytes 1966088 | tf_op jit(solution)/shard_map/ppermute | solution.py:26
  224.1 20.0 %collective-permute-start.19 = (bf16[160,2048]{1,0:T(8,128)(2,1)S(1)}, bf16[160,2048]{1,0:T(8,128)(2,1)}, u32[]{:S(2)}, u32[]{:S(2)}) collective-permute-start(bf16[160,2048]{1,0:T(8,128)(2,1)S(1)} %multiply_convert_fusion.1.refs_1_), channel_id=1, source_target_pairs={{0,8},{2,10},{8,16},{10,18},{16,24},{18,26},{24,28},{26,30},{28,20... | collective-permute-start | bytes 1966088 | tf_op jit(solution)/shard_map/ppermute | solution.py:45
  224.1 20.0 %collective-permute-start.20 = (bf16[160,2048]{1,0:T(8,128)(2,1)S(1)}, bf16[160,2048]{1,0:T(8,128)(2,1)S(1)}, u32[]{:S(2)}, u32[]{:S(2)}) collective-permute-start(bf16[160,2048]{1,0:T(8,128)(2,1)S(1)} %multiply_convert_fusion.1.refs_1_), channel_id=1, source_target_pairs={{8,0},{10,2},{16,8},{18,10},{24,16},{26,18},{28,24},{30,26},{20,28... | collective-permute-start | bytes 1966088 | tf_op jit(solution)/shard_map/ppermute | solution.py:49
  228.7 19.0 %collective-permute-start.24 = (f32[40,2048]{1,0:T(8,128)}, f32[40,2048]{1,0:T(8,128)S(1)}, u32[]{:S(2)}, u32[]{:S(2)}) collective-permute-start(f32[40,2048]{1,0:T(8,128)} %get-tuple-element.233), channel_id=1, source_target_pairs={{0,1},{1,0},{2,3},{3,2},{4,5},{5,4},{6,7},{7,6},{8,9},{9,8},{10,11... | collective-permute-start | bytes 983048 | tf_op jit(solution)/shard_map/ppermute | solution.py:26
  245.0 16.8 %collective-permute-start.22 = (bf16[160,2048]{1,0:T(8,128)(2,1)}, bf16[160,2048]{1,0:T(8,128)(2,1)}, u32[]{:S(2)}, u32[]{:S(2)}) collective-permute-start(bf16[160,2048]{1,0:T(8,128)(2,1)} %collective-permute-done.19.refs_1_), channel_id=1, source_target_pairs={{0,8},{2,10},{8,16},{10,18},{16,24},{18,26},{24,28},{26,30},{28,20... | collective-permute-start | bytes 1966088 | tf_op jit(solution)/shard_map/ppermute | solution.py:45
  245.0 16.8 %collective-permute-start.23 = (bf16[160,2048]{1,0:T(8,128)(2,1)}, bf16[160,2048]{1,0:T(8,128)(2,1)S(1)}, u32[]{:S(2)}, u32[]{:S(2)}) collective-permute-start(bf16[160,2048]{1,0:T(8,128)(2,1)} %copy-done.37), channel_id=1, source_target_pairs={{8,0},{10,2},{16,8},{18,10},{24,16},{26,18},{28,24},{30,26},{20,28... | collective-permute-start | bytes 1966088 | tf_op jit(solution)/shard_map/ppermute | solution.py:49
  247.2 17.4 %collective-permute-start.26 = (bf16[160,2048]{1,0:T(8,128)(2,1)}, bf16[160,2048]{1,0:T(8,128)(2,1)}, u32[]{:S(2)}, u32[]{:S(2)}) collective-permute-start(bf16[160,2048]{1,0:T(8,128)(2,1)} %collective-permute-done.19.refs_1_), channel_id=1, source_target_pairs={{0,2},{2,0},{4,6},{6,4},{8,10},{10,8},{12,14},{14,12},{16,18},{18,... | collective-permute-start | bytes 1966088 | tf_op jit(solution)/shard_map/ppermute | solution.py:22
  247.2 17.7 %collective-permute-start.27 = (bf16[160,2048]{1,0:T(8,128)(2,1)}, bf16[160,2048]{1,0:T(8,128)(2,1)}, u32[]{:S(2)}, u32[]{:S(2)}) collective-permute-start(bf16[160,2048]{1,0:T(8,128)(2,1)} %copy-done.37), channel_id=1, source_target_pairs={{0,2},{2,0},{4,6},{6,4},{8,10},{10,8},{12,14},{14,12},{16,18},{18,... | collective-permute-start | bytes 1966088 | tf_op jit(solution)/shard_map/ppermute | solution.py:22
  247.7 15.1 %collective-permute-start.25 = (f32[40,2048]{1,0:T(8,128)}, f32[40,2048]{1,0:T(8,128)S(1)}, u32[]{:S(2)}, u32[]{:S(2)}) collective-permute-start(f32[40,2048]{1,0:T(8,128)} %get-tuple-element.245), channel_id=1, source_target_pairs={{0,1},{1,0},{2,3},{3,2},{4,5},{5,4},{6,7},{7,6},{8,9},{9,8},{10,11... | collective-permute-start | bytes 983048 | tf_op jit(solution)/shard_map/ppermute | solution.py:26
  261.8 26.2 %collective-permute-start.29 = (bf16[160,2048]{1,0:T(8,128)(2,1)}, bf16[160,2048]{1,0:T(8,128)(2,1)S(1)}, u32[]{:S(2)}, u32[]{:S(2)}) collective-permute-start(bf16[160,2048]{1,0:T(8,128)(2,1)} %collective-permute-done.22.refs_1_), channel_id=1, source_target_pairs={{0,8},{2,10},{8,16},{10,18},{16,24},{18,26},{24,28},{26,30},{28,20... | collective-permute-start | bytes 1966088 | tf_op jit(solution)/shard_map/ppermute | solution.py:45
  262.7 28.1 %collective-permute-start.32 = (bf16[160,2048]{1,0:T(8,128)(2,1)}, bf16[160,2048]{1,0:T(8,128)(2,1)}, u32[]{:S(2)}, u32[]{:S(2)}) collective-permute-start(bf16[160,2048]{1,0:T(8,128)(2,1)} %collective-permute-done.22.refs_1_), channel_id=1, source_target_pairs={{0,2},{2,0},{4,6},{6,4},{8,10},{10,8},{12,14},{14,12},{16,18},{18,... | collective-permute-start | bytes 1966088 | tf_op jit(solution)/shard_map/ppermute | solution.py:22
  263.5 24.6 %collective-permute-start.30 = (bf16[160,2048]{1,0:T(8,128)(2,1)S(1)}, bf16[160,2048]{1,0:T(8,128)(2,1)S(1)}, u32[]{:S(2)}, u32[]{:S(2)}) collective-permute-start(bf16[160,2048]{1,0:T(8,128)(2,1)S(1)} %collective-permute-done.23.refs_2_), channel_id=1, source_target_pairs={{8,0},{10,2},{16,8},{18,10},{24,16},{26,18},{28,24},{30,26},{20,28... | collective-permute-start | bytes 1966088 | tf_op jit(solution)/shard_map/ppermute | solution.py:49
  264.6 26.7 %collective-permute-start.33 = (bf16[160,2048]{1,0:T(8,128)(2,1)S(1)}, bf16[160,2048]{1,0:T(8,128)(2,1)}, u32[]{:S(2)}, u32[]{:S(2)}) collective-permute-start(bf16[160,2048]{1,0:T(8,128)(2,1)S(1)} %collective-permute-done.23.refs_2_), channel_id=1, source_target_pairs={{0,2},{2,0},{4,6},{6,4},{8,10},{10,8},{12,14},{14,12},{16,18},{18,... | collective-permute-start | bytes 1966088 | tf_op jit(solution)/shard_map/ppermute | solution.py:22
  264.9 25.3 %collective-permute-start.31 = (f32[40,2048]{1,0:T(8,128)}, f32[40,2048]{1,0:T(8,128)S(1)}, u32[]{:S(2)}, u32[]{:S(2)}) collective-permute-start(f32[40,2048]{1,0:T(8,128)} %get-tuple-element.259), channel_id=1, source_target_pairs={{0,1},{1,0},{2,3},{3,2},{4,5},{5,4},{6,7},{7,6},{8,9},{9,8},{10,11... | collective-permute-start | bytes 983048 | tf_op jit(solution)/shard_map/ppermute | solution.py:26
  288.9 28.3 %collective-permute-start.40 = (bf16[160,2048]{1,0:T(8,128)(2,1)S(1)}, bf16[160,2048]{1,0:T(8,128)(2,1)}, u32[]{:S(2)}, u32[]{:S(2)}) collective-permute-start(bf16[160,2048]{1,0:T(8,128)(2,1)S(1)} %collective-permute-done.29.refs_1_), channel_id=1, source_target_pairs={{0,2},{2,0},{4,6},{6,4},{8,10},{10,8},{12,14},{14,12},{16,18},{18,... | collective-permute-start | bytes 1966088 | tf_op jit(solution)/shard_map/ppermute | solution.py:22
  289.6 27.6 %collective-permute-start.41 = (bf16[160,2048]{1,0:T(8,128)(2,1)S(1)}, bf16[160,2048]{1,0:T(8,128)(2,1)}, u32[]{:S(2)}, u32[]{:S(2)}) collective-permute-start(bf16[160,2048]{1,0:T(8,128)(2,1)S(1)} %collective-permute-done.30.refs_2_), channel_id=1, source_target_pairs={{0,2},{2,0},{4,6},{6,4},{8,10},{10,8},{12,14},{14,12},{16,18},{18,... | collective-permute-start | bytes 1966088 | tf_op jit(solution)/shard_map/ppermute | solution.py:22
  290.1 24.9 %collective-permute-start.37 = (f32[40,2048]{1,0:T(8,128)}, f32[40,2048]{1,0:T(8,128)}, u32[]{:S(2)}, u32[]{:S(2)}) collective-permute-start(f32[40,2048]{1,0:T(8,128)} %get-tuple-element.270), channel_id=1, source_target_pairs={{0,1},{1,0},{2,3},{3,2},{4,5},{5,4},{6,7},{7,6},{8,9},{9,8},{10,11... | collective-permute-start | bytes 983048 | tf_op jit(solution)/shard_map/ppermute | solution.py:26
  290.8 24.2 %collective-permute-start.35 = (bf16[80,2048]{1,0:T(8,128)(2,1)}, bf16[80,2048]{1,0:T(8,128)(2,1)S(1)}, u32[]{:S(2)}, u32[]{:S(2)}) collective-permute-start(bf16[80,2048]{1,0:T(8,128)(2,1)} %slice.165), channel_id=1, source_target_pairs={{0,8},{2,10},{8,16},{10,18},{16,24},{18,26},{24,28},{26,30},{28,20... | collective-permute-start | bytes 983048 | tf_op jit(solution)/shard_map/ppermute | solution.py:45
  291.4 23.6 %collective-permute-start.36 = (bf16[80,2048]{1,0:T(8,128)(2,1)}, bf16[80,2048]{1,0:T(8,128)(2,1)S(1)}, u32[]{:S(2)}, u32[]{:S(2)}) collective-permute-start(bf16[80,2048]{1,0:T(8,128)(2,1)} %slice.166), channel_id=1, source_target_pairs={{8,0},{10,2},{16,8},{18,10},{24,16},{26,18},{28,24},{30,26},{20,28... | collective-permute-start | bytes 983048 | tf_op jit(solution)/shard_map/ppermute | solution.py:49
  315.6 25.6 %collective-permute-start.28 = (bf16[320,2048]{1,0:T(8,128)(2,1)}, bf16[320,2048]{1,0:T(8,128)(2,1)}, u32[]{:S(2)}, u32[]{:S(2)}) collective-permute-start(bf16[320,2048]{1,0:T(8,128)(2,1)} %get-tuple-element.255), channel_id=1, source_target_pairs={{0,2},{2,0},{4,6},{6,4},{8,10},{10,8},{12,14},{14,12},{16,18},{18,... | collective-permute-start | bytes 3932168 | tf_op jit(solution)/shard_map/ppermute | solution.py:22
  340.3 72.9 %collective-permute-start.21 = (bf16[160,2048]{1,0:T(8,128)(2,1)}, bf16[160,2048]{1,0:T(8,128)(2,1)}, u32[]{:S(2)}, u32[]{:S(2)}) collective-permute-start(bf16[160,2048]{1,0:T(8,128)(2,1)} %get-tuple-element.230), channel_id=1, source_target_pairs={{0,2},{2,0},{4,6},{6,4},{8,10},{10,8},{12,14},{14,12},{16,18},{18,... | collective-permute-start | bytes 1966088 | tf_op jit(solution)/shard_map/ppermute | solution.py:22
  340.7 15.9 %collective-permute-start.34 = (bf16[320,2048]{1,0:T(8,128)(2,1)}, bf16[320,2048]{1,0:T(8,128)(2,1)S(1)}, u32[]{:S(2)}, u32[]{:S(2)}) collective-permute-start(bf16[320,2048]{1,0:T(8,128)(2,1)} %get-tuple-element.269), channel_id=1, source_target_pairs={{0,2},{2,0},{4,6},{6,4},{8,10},{10,8},{12,14},{14,12},{16,18},{18,... | collective-permute-start | bytes 3932168 | tf_op jit(solution)/shard_map/ppermute | solution.py:22
  340.8 17.7 %collective-permute-start.42 = (bf16[320,2048]{1,0:T(8,128)(2,1)}, bf16[320,2048]{1,0:T(8,128)(2,1)S(1)}, u32[]{:S(2)}, u32[]{:S(2)}) collective-permute-start(bf16[320,2048]{1,0:T(8,128)(2,1)} %get-tuple-element.282), channel_id=1, source_target_pairs={{0,2},{2,0},{4,6},{6,4},{8,10},{10,8},{12,14},{14,12},{16,18},{18,... | collective-permute-start | bytes 3932168 | tf_op jit(solution)/shard_map/ppermute | solution.py:22
  343.3 15.8 %collective-permute-start.44 = (bf16[80,2048]{1,0:T(8,128)(2,1)S(1)}, bf16[80,2048]{1,0:T(8,128)(2,1)S(1)}, u32[]{:S(2)}, u32[]{:S(2)}) collective-permute-start(bf16[80,2048]{1,0:T(8,128)(2,1)S(1)} %get-tuple-element.430), channel_id=1, source_target_pairs={{0,8},{2,10},{8,16},{10,18},{16,24},{18,26},{24,28},{26,30},{28,20... | collective-permute-start | bytes 983048 | tf_op jit(solution)/shard_map/ppermute | solution.py:45
  343.9 14.6 %collective-permute-start.48 = (bf16[80,2048]{1,0:T(8,128)(2,1)S(1)}, bf16[80,2048]{1,0:T(8,128)(2,1)S(1)}, u32[]{:S(2)}, u32[]{:S(2)}) collective-permute-start(bf16[80,2048]{1,0:T(8,128)(2,1)S(1)} %get-tuple-element.431), channel_id=1, source_target_pairs={{8,0},{10,2},{16,8},{18,10},{24,16},{26,18},{28,24},{30,26},{20,28... | collective-permute-start | bytes 983048 | tf_op jit(solution)/shard_map/ppermute | solution.py:49
  356.5 59.5 %collective-permute-start.52 = (bf16[512,2048]{1,0:T(8,128)(2,1)}, bf16[512,2048]{1,0:T(8,128)(2,1)}, u32[]{:S(2)}, u32[]{:S(2)}) collective-permute-start(bf16[512,2048]{1,0:T(8,128)(2,1)} %convolution_convert_fusion.2), channel_id=1, source_target_pairs={{0,1},{1,0},{2,3},{3,2},{4,5},{5,4},{6,7},{7,6},{8,9},{9,8},{10,11... | collective-permute-start | bytes 6291464 | tf_op jit(solution)/shard_map/ppermute | solution.py:26
  359.3 16.0 %collective-permute-start.49 = (bf16[160,2048]{1,0:T(8,128)(2,1)S(1)}, bf16[160,2048]{1,0:T(8,128)(2,1)S(1)}, u32[]{:S(2)}, u32[]{:S(2)}) collective-permute-start(bf16[160,2048]{1,0:T(8,128)(2,1)S(1)} %pad_maximum_fusion.5), channel_id=1, source_target_pairs={{8,0},{10,2},{16,8},{18,10},{24,16},{26,18},{28,24},{30,26},{20,28... | collective-permute-start | bytes 1966088 | tf_op jit(solution)/shard_map/ppermute | solution.py:49
  360.6 15.7 %collective-permute-start.45 = (bf16[160,2048]{1,0:T(8,128)(2,1)S(1)}, bf16[160,2048]{1,0:T(8,128)(2,1)S(1)}, u32[]{:S(2)}, u32[]{:S(2)}) collective-permute-start(bf16[160,2048]{1,0:T(8,128)(2,1)S(1)} %pad_maximum_fusion.4), channel_id=1, source_target_pairs={{0,8},{2,10},{8,16},{10,18},{16,24},{18,26},{24,28},{26,30},{28,20... | collective-permute-start | bytes 1966088 | tf_op jit(solution)/shard_map/ppermute | solution.py:45
  367.4 48.6 %collective-permute-start.53 = (bf16[512,512]{1,0:T(8,128)(2,1)S(1)}, bf16[512,512]{1,0:T(8,128)(2,1)}, u32[]{:S(2)}, u32[]{:S(2)}) collective-permute-start(bf16[512,512]{1,0:T(8,128)(2,1)S(1)} %slice.218), channel_id=1, source_target_pairs={{0,1},{1,0},{2,3},{3,2},{4,5},{5,4},{6,7},{7,6},{8,9},{9,8},{10,11... | collective-permute-start | bytes 1572872 | tf_op jit(solution)/shard_map/ppermute | solution.py:26
  376.8 14.9 %collective-permute-start.50 = (bf16[160,2048]{1,0:T(8,128)(2,1)S(1)}, bf16[160,2048]{1,0:T(8,128)(2,1)S(1)}, u32[]{:S(2)}, u32[]{:S(2)}) collective-permute-start(bf16[160,2048]{1,0:T(8,128)(2,1)S(1)} %get-tuple-element.421), channel_id=1, source_target_pairs={{8,0},{10,2},{16,8},{18,10},{24,16},{26,18},{28,24},{30,26},{20,28... | collective-permute-start | bytes 1966088 | tf_op jit(solution)/shard_map/ppermute | solution.py:49
  377.3 14.7 %collective-permute-start.46 = (bf16[160,2048]{1,0:T(8,128)(2,1)S(1)}, bf16[160,2048]{1,0:T(8,128)(2,1)S(1)}, u32[]{:S(2)}, u32[]{:S(2)}) collective-permute-start(bf16[160,2048]{1,0:T(8,128)(2,1)S(1)} %get-tuple-element.420), channel_id=1, source_target_pairs={{0,8},{2,10},{8,16},{10,18},{16,24},{18,26},{24,28},{26,30},{28,20... | collective-permute-start | bytes 1966088 | tf_op jit(solution)/shard_map/ppermute | solution.py:45
  393.4 19.8 %collective-permute-start.47 = (bf16[160,2048]{1,0:T(8,128)(2,1)}, bf16[160,2048]{1,0:T(8,128)(2,1)S(1)}, u32[]{:S(2)}, u32[]{:S(2)}) collective-permute-start(bf16[160,2048]{1,0:T(8,128)(2,1)} %get-tuple-element.418), channel_id=1, source_target_pairs={{0,8},{2,10},{8,16},{10,18},{16,24},{18,26},{24,28},{26,30},{28,20... | collective-permute-start | bytes 1966088 | tf_op jit(solution)/shard_map/ppermute | solution.py:45
  394.9 19.2 %collective-permute-start.51 = (bf16[160,2048]{1,0:T(8,128)(2,1)S(1)}, bf16[160,2048]{1,0:T(8,128)(2,1)}, u32[]{:S(2)}, u32[]{:S(2)}) collective-permute-start(bf16[160,2048]{1,0:T(8,128)(2,1)S(1)} %get-tuple-element.419), channel_id=1, source_target_pairs={{8,0},{10,2},{16,8},{18,10},{24,16},{26,18},{28,24},{30,26},{20,28... | collective-permute-start | bytes 1966088 | tf_op jit(solution)/shard_map/ppermute | solution.py:49
  419.3 14.6 %collective-permute-start.54 = (bf16[160,2048]{1,0:T(8,128)(2,1)S(1)}, bf16[160,2048]{1,0:T(8,128)(2,1)S(1)}, u32[]{:S(2)}, u32[]{:S(2)}) collective-permute-start(bf16[160,2048]{1,0:T(8,128)(2,1)S(1)} %get-tuple-element.402), channel_id=1, source_target_pairs={{0,1},{1,0},{2,3},{3,2},{4,5},{5,4},{6,7},{7,6},{8,9},{9,8},{10,11... | collective-permute-start | bytes 1966088 | tf_op jit(solution)/shard_map/ppermute | solution.py:26
  442.5 30.6 %collective-permute-start.58 = (bf16[1024,512]{1,0:T(8,128)(2,1)}, bf16[1024,512]{1,0:T(8,128)(2,1)}, u32[]{:S(2)}, u32[]{:S(2)}) collective-permute-start(bf16[1024,512]{1,0:T(8,128)(2,1)} %slice.178), channel_id=1, source_target_pairs={{0,1},{1,0},{2,3},{3,2},{4,5},{5,4},{6,7},{7,6},{8,9},{9,8},{10,11... | collective-permute-start | bytes 3145736 | tf_op jit(solution)/shard_map/ppermute | solution.py:26
  464.4 41.0 %collective-permute-start.56 = (bf16[320,2048]{1,0:T(8,128)(2,1)S(1)}, bf16[320,2048]{1,0:T(8,128)(2,1)}, u32[]{:S(2)}, u32[]{:S(2)}) collective-permute-start(bf16[320,2048]{1,0:T(8,128)(2,1)S(1)} %copy-done.14), channel_id=1, source_target_pairs={{0,2},{2,0},{4,6},{6,4},{8,10},{10,8},{12,14},{14,12},{16,18},{18,... | collective-permute-start | bytes 3932168 | tf_op jit(solution)/shard_map/ppermute | solution.py:22
  466.1 40.9 %collective-permute-start.57 = (bf16[320,2048]{1,0:T(8,128)(2,1)S(1)}, bf16[320,2048]{1,0:T(8,128)(2,1)}, u32[]{:S(2)}, u32[]{:S(2)}) collective-permute-start(bf16[320,2048]{1,0:T(8,128)(2,1)S(1)} %copy-done.13), channel_id=1, source_target_pairs={{0,2},{2,0},{4,6},{6,4},{8,10},{10,8},{12,14},{14,12},{16,18},{18,... | collective-permute-start | bytes 3932168 | tf_op jit(solution)/shard_map/ppermute | solution.py:22
  472.2 31.5 %collective-permute-start.66 = (bf16[2,128,1024]{2,1,0:T(8,128)(2,1)}, bf16[2,128,1024]{2,1,0:T(8,128)(2,1)S(1)}, u32[]{:S(2)}, u32[]{:S(2)}) collective-permute-start(bf16[2,128,1024]{2,1,0:T(8,128)(2,1)} %get-tuple-element.316), channel_id=1, source_target_pairs={{0,8},{2,10},{4,12},{6,14},{8,0},{10,2},{12,4},{14,6},{16,24},{18,... | collective-permute-start | bytes 1572872 | tf_op jit(solution)/shard_map/ppermute | solution.py:22
  473.1 30.8 %collective-permute-start.65 = (bf16[2,128,1024]{2,1,0:T(8,128)(2,1)}, bf16[2,128,1024]{2,1,0:T(8,128)(2,1)S(1)}, u32[]{:S(2)}, u32[]{:S(2)}) collective-permute-start(bf16[2,128,1024]{2,1,0:T(8,128)(2,1)} %get-tuple-element.315), channel_id=1, source_target_pairs={{0,4},{2,6},{4,0},{6,2},{8,12},{10,14},{12,8},{14,10},{16,20},{18,... | collective-permute-start | bytes 1572872 | tf_op jit(solution)/shard_map/ppermute | solution.py:22
  476.6 45.6 %collective-permute-start.60 = (bf16[1024,512]{1,0:T(8,128)(2,1)}, bf16[1024,512]{1,0:T(8,128)(2,1)}, u32[]{:S(2)}, u32[]{:S(2)}) collective-permute-start(bf16[1024,512]{1,0:T(8,128)(2,1)} %slice.179), channel_id=1, source_target_pairs={{0,1},{1,0},{2,3},{3,2},{4,5},{5,4},{6,7},{7,6},{8,9},{9,8},{10,11... | collective-permute-start | bytes 3145736 | tf_op jit(solution)/shard_map/ppermute | solution.py:26
  503.9 18.3 %collective-permute-start.59 = (bf16[512,512]{1,0:T(8,128)(2,1)}, bf16[512,512]{1,0:T(8,128)(2,1)}, u32[]{:S(2)}, u32[]{:S(2)}) collective-permute-start(bf16[512,512]{1,0:T(8,128)(2,1)} %slice.177), channel_id=1, source_target_pairs={{0,1},{1,0},{2,3},{3,2},{4,5},{5,4},{6,7},{7,6},{8,9},{9,8},{10,11... | collective-permute-start | bytes 1572872 | tf_op jit(solution)/shard_map/ppermute | solution.py:26
  552.3 14.9 %collective-permute-start.70 = (bf16[256,1024]{1,0:T(8,128)(2,1)}, bf16[256,1024]{1,0:T(8,128)(2,1)S(1)}, u32[]{:S(2)}, u32[]{:S(2)}) collective-permute-start(bf16[256,1024]{1,0:T(8,128)(2,1)} %get-tuple-element.331), channel_id=1, source_target_pairs={{0,8},{2,10},{8,16},{10,18},{16,24},{18,26},{24,28},{26,30},{28,20... | collective-permute-start | bytes 1572872 | tf_op jit(solution)/shard_map/ppermute | solution.py:45
  554.3 14.8 %collective-permute-start.71 = (bf16[256,1024]{1,0:T(8,128)(2,1)}, bf16[256,1024]{1,0:T(8,128)(2,1)S(1)}, u32[]{:S(2)}, u32[]{:S(2)}) collective-permute-start(bf16[256,1024]{1,0:T(8,128)(2,1)} %get-tuple-element.332), channel_id=1, source_target_pairs={{8,0},{10,2},{16,8},{18,10},{24,16},{26,18},{28,24},{30,26},{20,28... | collective-permute-start | bytes 1572872 | tf_op jit(solution)/shard_map/ppermute | solution.py:49
  554.3 18.0 %collective-permute-start.74 = (bf16[512,512]{1,0:T(8,128)(2,1)S(1)}, bf16[512,512]{1,0:T(8,128)(2,1)}, u32[]{:S(2)}, u32[]{:S(2)}) collective-permute-start(bf16[512,512]{1,0:T(8,128)(2,1)S(1)} %get-tuple-element.351), channel_id=1, source_target_pairs={{0,1},{1,0},{2,3},{3,2},{4,5},{5,4},{6,7},{7,6},{8,9},{9,8},{10,11... | collective-permute-start | bytes 1572872 | tf_op jit(solution)/shard_map/ppermute | solution.py:26
  570.6 28.2 %collective-permute-start.78 = (bf16[160,2048]{1,0:T(8,128)(2,1)S(1)}, bf16[160,2048]{1,0:T(8,128)(2,1)S(1)}, u32[]{:S(2)}, u32[]{:S(2)}) collective-permute-start(bf16[160,2048]{1,0:T(8,128)(2,1)S(1)} %dynamic-slice_convert_fusion), channel_id=1, source_target_pairs={{0,1},{1,0},{2,3},{3,2},{4,5},{5,4},{6,7},{7,6},{8,9},{9,8},{10,11... | collective-permute-start | bytes 1966088 | tf_op jit(solution)/shard_map/ppermute | solution.py:26
  572.3 25.9 %collective-permute-start.75 = (bf16[512,512]{1,0:T(8,128)(2,1)}, bf16[512,512]{1,0:T(8,128)(2,1)}, u32[]{:S(2)}, u32[]{:S(2)}) collective-permute-start(bf16[512,512]{1,0:T(8,128)(2,1)} %get-tuple-element.352), channel_id=1, source_target_pairs={{0,1},{1,0},{2,3},{3,2},{4,5},{5,4},{6,7},{7,6},{8,9},{9,8},{10,11... | collective-permute-start | bytes 1572872 | tf_op jit(solution)/shard_map/ppermute | solution.py:26
  573.4 24.9 %collective-permute-start.72 = (bf16[256,2048]{1,0:T(8,128)(2,1)S(1)}, bf16[256,2048]{1,0:T(8,128)(2,1)S(1)}, u32[]{:S(2)}, u32[]{:S(2)}) collective-permute-start(bf16[256,2048]{1,0:T(8,128)(2,1)S(1)} %pad_maximum_fusion.2), channel_id=1, source_target_pairs={{0,8},{2,10},{8,16},{10,18},{16,24},{18,26},{24,28},{26,30},{28,20... | collective-permute-start | bytes 3145736 | tf_op jit(solution)/shard_map/ppermute | solution.py:45
  575.2 23.7 %collective-permute-start.73 = (bf16[256,2048]{1,0:T(8,128)(2,1)S(1)}, bf16[256,2048]{1,0:T(8,128)(2,1)}, u32[]{:S(2)}, u32[]{:S(2)}) collective-permute-start(bf16[256,2048]{1,0:T(8,128)(2,1)S(1)} %pad_maximum_fusion.3), channel_id=1, source_target_pairs={{8,0},{10,2},{16,8},{18,10},{24,16},{26,18},{28,24},{30,26},{20,28... | collective-permute-start | bytes 3145736 | tf_op jit(solution)/shard_map/ppermute | solution.py:49
  602.8 23.4 %collective-permute-start.76 = (bf16[256,2048]{1,0:T(8,128)(2,1)}, bf16[256,2048]{1,0:T(8,128)(2,1)}, u32[]{:S(2)}, u32[]{:S(2)}) collective-permute-start(bf16[256,2048]{1,0:T(8,128)(2,1)} %get-tuple-element.355), channel_id=1, source_target_pairs={{0,8},{2,10},{8,16},{10,18},{16,24},{18,26},{24,28},{26,30},{28,20... | collective-permute-start | bytes 3145736 | tf_op jit(solution)/shard_map/ppermute | solution.py:45
  603.8 23.5 %collective-permute-start.77 = (bf16[256,2048]{1,0:T(8,128)(2,1)}, bf16[256,2048]{1,0:T(8,128)(2,1)}, u32[]{:S(2)}, u32[]{:S(2)}) collective-permute-start(bf16[256,2048]{1,0:T(8,128)(2,1)} %get-tuple-element.356), channel_id=1, source_target_pairs={{8,0},{10,2},{16,8},{18,10},{24,16},{26,18},{28,24},{30,26},{20,28... | collective-permute-start | bytes 3145736 | tf_op jit(solution)/shard_map/ppermute | solution.py:49
  604.8 41.9 %collective-permute-start.82 = (bf16[160,2048]{1,0:T(8,128)(2,1)}, bf16[160,2048]{1,0:T(8,128)(2,1)}, u32[]{:S(2)}, u32[]{:S(2)}) collective-permute-start(bf16[160,2048]{1,0:T(8,128)(2,1)} %reduce-scatter.2.cloned.1.call-done.refs_2_), channel_id=1, source_target_pairs={{0,1},{1,0},{2,3},{3,2},{4,5},{5,4},{6,7},{7,6},{8,9},{9,8},{10,11... | collective-permute-start | bytes 1966088 | tf_op jit(solution)/shard_map/ppermute | solution.py:26
  607.8 49.0 %collective-permute-start.81 = (f32[160,2048]{1,0:T(8,128)}, f32[160,2048]{1,0:T(8,128)}, u32[]{:S(2)}, u32[]{:S(2)}) collective-permute-start(f32[160,2048]{1,0:T(8,128)} %fusion.5.refs_1_), channel_id=1, source_target_pairs={{0,1},{1,0},{2,3},{3,2},{4,5},{5,4},{6,7},{7,6},{8,9},{9,8},{10,11... | collective-permute-start | bytes 3932168 | tf_op jit(solution)/shard_map/ppermute | solution.py:26
  631.0 28.7 %collective-permute-start.79 = (bf16[256,2048]{1,0:T(8,128)(2,1)}, bf16[256,2048]{1,0:T(8,128)(2,1)S(1)}, u32[]{:S(2)}, u32[]{:S(2)}) collective-permute-start(bf16[256,2048]{1,0:T(8,128)(2,1)} %get-tuple-element.364), channel_id=1, source_target_pairs={{0,8},{2,10},{8,16},{10,18},{16,24},{18,26},{24,28},{26,30},{28,20... | collective-permute-start | bytes 3145736 | tf_op jit(solution)/shard_map/ppermute | solution.py:45
  631.9 27.8 %collective-permute-start.80 = (bf16[256,2048]{1,0:T(8,128)(2,1)}, bf16[256,2048]{1,0:T(8,128)(2,1)S(1)}, u32[]{:S(2)}, u32[]{:S(2)}) collective-permute-start(bf16[256,2048]{1,0:T(8,128)(2,1)} %get-tuple-element.365), channel_id=1, source_target_pairs={{8,0},{10,2},{16,8},{18,10},{24,16},{26,18},{28,24},{30,26},{20,28... | collective-permute-start | bytes 3145736 | tf_op jit(solution)/shard_map/ppermute | solution.py:49
  (103 other events, 1368.2 us)
Sparse Core Ops, SparseCore 0:
  12.7 94.2 all-gather.4
  109.9 97.4 all-gather.6
  416.2 134.2 reduce-scatter.1
